TPU v7x, 32 devices: a whole 2x2x4 slice. The times are simulated.
32 devices in a mesh: dp: 8 (over z, y), tensor: 4 (over x, core).
Axes of the slice: x: 2, y: 2, z: 4, core: 2. Of those that a mesh axis runs over, the one named last changes fastest.
Arguments:
- tokens: bfloat16 [16384, 768], P(('dp', 'tensor')), may hold values from -6 to 6
- cotangent: bfloat16 [16384, 768], P(('dp', 'tensor')), may hold values from -6 to 6
- qkv_weight: float32 [3, 768, 768], P(None, 'dp', 'tensor'), may hold values from -0.21875 to 0.21875
- qv_bias: float32 [2, 768], P(None, 'tensor'), may hold values from -1.8 to 1.8
- out_weight: float32 [768, 768], P('tensor', 'dp'), may hold values from -1 to 1
- out_bias: float32 [768], replicated, may hold values from -1.8 to 1.8
- first_gain: float32 [768], replicated, may hold values from 0.5 to 1.5
- first_shift: float32 [768], replicated, may hold values from -1.2 to 1.2
- up_weight: float32 [768, 3072], P('dp', 'tensor'), may hold values from -0.21875 to 0.21875
- up_bias: float32 [3072], P('tensor'), may hold values from -1.8 to 1.8
- down_weight: float32 [3072, 768], P('tensor', 'dp'), may hold values from -0.109375 to 0.109375
- down_bias: float32 [768], replicated, may hold values from -1.8 to 1.8
- second_gain: float32 [768], replicated, may hold values from 0.5 to 1.5
- second_shift: float32 [768], replicated, may hold values from -1.2 to 1.2
- act_ranges: float32 [4], replicated, may hold values from 0.5 to 3.5, as said below
- long_lengths: int32 [8], P('dp'), may hold values from 128 to 512, as said below
- short_lengths: int32 [96], P('dp'), may hold values from 32 to 128, as said below
Outputs:
- layer_out: bfloat16 [16384, 768], P(('dp', 'tensor'))
- tokens_grad: bfloat16 [16384, 768], P(('dp', 'tensor'))
- qkv_grad: float32 [3, 768, 768], P(None, 'dp', 'tensor')
- qv_bias_grad: float32 [2, 768], P(None, 'tensor')
- out_grad: float32 [768, 768], P('tensor', 'dp')
- out_bias_grad: float32 [768], replicated
- first_gain_grad: float32 [768], replicated
- first_shift_grad: float32 [768], replicated
- up_grad: float32 [768, 3072], P('dp', 'tensor')
- up_bias_grad: float32 [3072], P('tensor')
- down_grad: float32 [3072, 768], P('tensor', 'dp')
- down_bias_grad: float32 [768], replicated
- second_gain_grad: float32 [768], replicated
- second_shift_grad: float32 [768], replicated
- new_ranges: float32 [4], replicated
Inputs may be any that keep to these rules, and one draw needn't show every extreme that they name: Each long sequence uses its first long_lengths slots; at least a quarter of 512, and some sequence uses all 512. Each short sequence uses its first short_lengths slots; at least a quarter of 128, and some sequence uses all 128. `act_ranges`: entry 1 lies in 0.5 to 0.8, the others in 2.5 to 3.5.
All inputs are finite; a program needn't handle non-finite values.
Results may differ from a plain program's by a relative error of at most 0.018.
The roundings to bfloat16 on the way count: a program that leaves them out, or rounds other values in their place, can miss the bound.
Values may be sent and summed in bfloat16 or wider, within the bound.
No kernel may reach another device: no remote copies, remote signals or barrier semaphores. Data moves between devices by JAX's collectives and lax.ppermute only.
A program may use at most 128 MiB of HBM per device.

v0:
```python
import jax
import jax.numpy as jnp
from jax import lax
from jax.sharding import PartitionSpec as P

HEAD_DIM = 64
LONG_LEN = 512
SHORT_LEN = 128


ema_decay = 0.9
epsilon = 1e-06
root_half = 0.7071067811865476
density_scale = 0.3989422804014327


def matmul_plain(left, right):
    return jnp.dot(left, right, preferred_element_type=jnp.float32)


def matmul_left_t(left, right):
    return lax.dot_general(
        left, right, (((0,), (0,)), ((), ())), preferred_element_type=jnp.float32
    )


def matmul_right_t(left, right):
    return lax.dot_general(
        left, right, (((1,), (1,)), ((), ())), preferred_element_type=jnp.float32
    )


def saturate(values, limit):
    return limit * jnp.tanh(values / limit)


def saturate_slope(values, limit):
    bent = jnp.tanh(values / limit)
    return 1.0 - bent * bent


def block_masks(long_part, short_part):
    per_block = LONG_LEN // SHORT_LEN
    position = jnp.arange(LONG_LEN, dtype=jnp.int32)
    long_segment = jnp.zeros((long_part.shape[0], LONG_LEN), jnp.int32)
    long_valid = position[None, :] < long_part[:, None]
    short_rows = short_part.reshape(-1, per_block)
    short_segment = jnp.broadcast_to(position // SHORT_LEN, (short_rows.shape[0], LONG_LEN))
    short_limit = jnp.repeat(short_rows, SHORT_LEN, axis=1)
    short_valid = (position % SHORT_LEN)[None, :] < short_limit
    return (
        jnp.concatenate([long_segment, short_segment], 0),
        jnp.concatenate([long_valid, short_valid], 0),
    )


def layer_norm_fwd(summed, gain, shift):
    average = jnp.mean(summed, axis=-1, keepdims=True)
    centered = summed - average
    inv_scale = lax.rsqrt(jnp.mean(centered * centered, axis=-1, keepdims=True) + epsilon)
    normed = centered * inv_scale
    return (normed * gain + shift, normed, inv_scale)


def norm_backward(incoming, normed, inv_scale, gain):
    scaled = incoming * gain
    row_mean = jnp.mean(scaled, axis=-1, keepdims=True)
    row_cross = jnp.mean(scaled * normed, axis=-1, keepdims=True)
    grad_in = inv_scale * (scaled - row_mean - normed * row_cross)
    return (grad_in, jnp.sum(incoming * normed, axis=0), jnp.sum(incoming, axis=0))


def gelu_slope(values):
    return (
        0.5 * (1.0 + lax.erf(values * root_half))
        + values * jnp.exp(-0.5 * values * values) * density_scale
    )


def score_block(queries, key_rows, segment, key_valid):
    scores = jnp.einsum(
        "qhd,khd->hqk", queries, key_rows, preferred_element_type=jnp.float32
    ) * HEAD_DIM ** (-0.5)
    allowed = (segment[:, None] == segment[None, :]) & key_valid[None, :]
    return jnp.where(allowed[None, :, :], scores, -1000000000.0)


def block_forward(pieces):
    queries, key_rows, values, segment, key_valid = pieces
    scores = score_block(queries, key_rows, segment, key_valid)
    row_max = jnp.max(scores, axis=-1, keepdims=True)
    expanded = jnp.exp(scores - row_max)
    row_total = jnp.sum(expanded, axis=-1, keepdims=True)
    shares = (expanded / row_total).astype(jnp.bfloat16)
    context = jnp.einsum("hqk,khd->qhd", shares, values, preferred_element_type=jnp.float32)
    return (context, (row_max + jnp.log(row_total))[:, :, 0])


def block_backward(pieces):
    queries, key_rows, values, segment, key_valid, log_total, grad_ctx = pieces
    score_scale = HEAD_DIM ** (-0.5)
    scores = score_block(queries, key_rows, segment, key_valid)
    shares = jnp.exp(scores - log_total[:, :, None])
    grad_shares = jnp.einsum("qhd,khd->hqk", grad_ctx, values, preferred_element_type=jnp.float32)
    row_inner = jnp.sum(shares * grad_shares, axis=-1, keepdims=True)
    grad_scores = (shares * (grad_shares - row_inner)).astype(jnp.bfloat16)
    grad_values = jnp.einsum(
        "hqk,qhd->khd", shares.astype(jnp.bfloat16), grad_ctx, preferred_element_type=jnp.float32
    )
    grad_queries = (
        jnp.einsum("hqk,khd->qhd", grad_scores, key_rows, preferred_element_type=jnp.float32)
        * score_scale
    )
    grad_keys = (
        jnp.einsum("hqk,qhd->khd", grad_scores, queries, preferred_element_type=jnp.float32)
        * score_scale
    )
    return (
        grad_queries.astype(jnp.bfloat16),
        grad_keys.astype(jnp.bfloat16),
        grad_values.astype(jnp.bfloat16),
    )


def body(
    tokens,
    cotangent,
    qkv_weight,
    qv_bias,
    out_weight,
    out_bias,
    first_gain,
    first_shift,
    up_weight,
    up_bias,
    down_weight,
    down_bias,
    second_gain,
    second_shift,
    act_ranges,
    long_lengths,
    short_lengths,
):
    tensor_lanes = lax.axis_size("tensor")
    column = lax.axis_index("tensor")
    shard_rows = tokens.shape[0]
    group_rows = shard_rows * tensor_lanes
    head_cols = qkv_weight.shape[2]
    up_cols = up_weight.shape[1]
    blocked = (group_rows // LONG_LEN, LONG_LEN, head_cols // HEAD_DIM, HEAD_DIM)
    masters = (
        qkv_weight.astype(jnp.bfloat16),
        out_weight.astype(jnp.bfloat16),
        up_weight.astype(jnp.bfloat16),
        down_weight.astype(jnp.bfloat16),
    )
    qkv_full, out_full, up_full, down_full = (
        lax.all_gather(masters[0], "dp", axis=1, tiled=True),
        lax.all_gather(masters[1], "dp", axis=1, tiled=True),
        lax.all_gather(masters[2], "dp", axis=0, tiled=True),
        lax.all_gather(masters[3], "dp", axis=1, tiled=True),
    )
    inputs = tokens.astype(jnp.float32)
    in_clip = jnp.clip(inputs, -act_ranges[0], act_ranges[0]).astype(jnp.bfloat16)
    in_rows = lax.all_gather(in_clip, "tensor", axis=0, tiled=True)
    projected = jnp.einsum("td,jde->jte", in_rows, qkv_full, preferred_element_type=jnp.float32)
    queries = (projected[0] + qv_bias[0]).astype(jnp.bfloat16).reshape(blocked)
    key_rows = projected[1].astype(jnp.bfloat16).reshape(blocked)
    values = (projected[2] + qv_bias[1]).astype(jnp.bfloat16).reshape(blocked)
    segment, key_valid = block_masks(long_lengths, short_lengths)
    context, log_total = lax.map(block_forward, (queries, key_rows, values, segment, key_valid))
    context = context.reshape(group_rows, head_cols)
    ctx_clip = saturate(context, act_ranges[1]).astype(jnp.bfloat16)
    attn_sum = lax.psum_scatter(
        matmul_plain(ctx_clip, out_full).astype(jnp.bfloat16),
        "tensor",
        scatter_dimension=0,
        tiled=True,
    ).astype(jnp.float32)
    first_sum = inputs + attn_sum + out_bias
    middle, first_normed, first_inv = layer_norm_fwd(first_sum, first_gain, first_shift)
    mid_clip = saturate(middle, act_ranges[2]).astype(jnp.bfloat16)
    mid_rows = lax.all_gather(mid_clip, "tensor", axis=0, tiled=True)
    up_out = matmul_plain(mid_rows, up_full) + up_bias
    hidden = jax.nn.gelu(up_out, approximate=False)
    act_clip = saturate(hidden, act_ranges[3]).astype(jnp.bfloat16)
    ffn_sum = lax.psum_scatter(
        matmul_plain(act_clip, down_full).astype(jnp.bfloat16),
        "tensor",
        scatter_dimension=0,
        tiled=True,
    ).astype(jnp.float32)
    second_sum = middle + ffn_sum + down_bias
    layer_out, second_normed, second_inv = layer_norm_fwd(second_sum, second_gain, second_shift)
    maxima = lax.pmax(
        (
            jnp.max(jnp.abs(inputs)),
            jnp.max(jnp.abs(context)),
            jnp.max(jnp.abs(middle)),
            jnp.max(jnp.abs(hidden)),
        ),
        ("dp", "tensor"),
    )
    new_ranges = ema_decay * act_ranges + (1.0 - ema_decay) * jnp.stack(maxima)
    grad_second, second_gain_part, second_shift_part = norm_backward(
        cotangent.astype(jnp.float32), second_normed, second_inv, second_gain
    )
    down_rows = lax.all_gather(grad_second.astype(jnp.bfloat16), "tensor", axis=0, tiled=True)
    qkv_back, out_back, up_back, down_back = (
        lax.all_gather(masters[0], "dp", axis=1, tiled=True),
        lax.all_gather(masters[1], "dp", axis=1, tiled=True),
        lax.all_gather(masters[2], "dp", axis=0, tiled=True),
        lax.all_gather(masters[3], "dp", axis=1, tiled=True),
    )
    down_grad = matmul_left_t(act_clip, down_rows)
    grad_act = matmul_right_t(down_rows, down_back) * saturate_slope(hidden, act_ranges[3])
    grad_up = (grad_act * gelu_slope(up_out)).astype(jnp.bfloat16)
    up_grad = matmul_left_t(mid_rows, grad_up)
    mid_sum = lax.psum_scatter(
        matmul_right_t(grad_up, up_back).astype(jnp.bfloat16),
        "tensor",
        scatter_dimension=0,
        tiled=True,
    ).astype(jnp.float32)
    grad_middle = grad_second + mid_sum * saturate_slope(middle, act_ranges[2])
    grad_first, first_gain_part, first_shift_part = norm_backward(
        grad_middle, first_normed, first_inv, first_gain
    )
    attn_rows = lax.all_gather(grad_first.astype(jnp.bfloat16), "tensor", axis=0, tiled=True)
    out_grad = matmul_left_t(ctx_clip, attn_rows)
    grad_ctx = (
        matmul_right_t(attn_rows, out_back) * saturate_slope(context, act_ranges[1])
    ).astype(jnp.bfloat16)
    grad_queries, grad_keys, grad_values = lax.map(
        block_backward,
        (queries, key_rows, values, segment, key_valid, log_total, grad_ctx.reshape(blocked)),
    )
    stacked = jnp.stack(
        [
            grad_queries.reshape(group_rows, head_cols),
            grad_keys.reshape(group_rows, head_cols),
            grad_values.reshape(group_rows, head_cols),
        ]
    )
    qkv_grad = jnp.einsum("td,jte->jde", in_rows, stacked, preferred_element_type=jnp.float32)
    input_sum = lax.psum_scatter(
        jnp.einsum("jte,jde->td", stacked, qkv_back, preferred_element_type=jnp.float32).astype(
            jnp.bfloat16
        ),
        "tensor",
        scatter_dimension=0,
        tiled=True,
    ).astype(jnp.float32)
    tokens_grad = (grad_first + jnp.where(jnp.abs(inputs) <= act_ranges[0], input_sum, 0.0)).astype(
        jnp.bfloat16
    )
    qkv_grad, out_grad, up_grad, down_grad = (
        lax.psum_scatter(qkv_grad, "dp", scatter_dimension=1, tiled=True),
        lax.psum_scatter(out_grad, "dp", scatter_dimension=1, tiled=True),
        lax.psum_scatter(up_grad, "dp", scatter_dimension=0, tiled=True),
        lax.psum_scatter(down_grad, "dp", scatter_dimension=1, tiled=True),
    )
    lane_hot = (jnp.arange(tensor_lanes) == column).astype(jnp.float32)

    def spread(vector_piece):
        return (lane_hot[:, None] * vector_piece[None, :]).reshape(-1)

    query_bias_part = jnp.sum(stacked[0].astype(jnp.float32), axis=0)
    value_bias_part = jnp.sum(stacked[2].astype(jnp.float32), axis=0)
    up_bias_part = jnp.sum(grad_up.astype(jnp.float32), axis=0)
    shared = jnp.stack(
        [
            jnp.sum(grad_first, axis=0),
            first_gain_part,
            first_shift_part,
            jnp.sum(grad_second, axis=0),
            second_gain_part,
            second_shift_part,
        ]
    )
    query_total, value_total, up_total, shared_total = lax.psum(
        (spread(query_bias_part), spread(value_bias_part), spread(up_bias_part), shared),
        ("dp", "tensor"),
    )
    qv_bias_grad = jnp.stack(
        [
            lax.dynamic_slice_in_dim(query_total, column * head_cols, head_cols),
            lax.dynamic_slice_in_dim(value_total, column * head_cols, head_cols),
        ]
    )
    up_bias_grad = lax.dynamic_slice_in_dim(up_total, column * up_cols, up_cols)
    return (
        layer_out.astype(jnp.bfloat16),
        tokens_grad,
        qkv_grad,
        qv_bias_grad,
        out_grad,
        shared_total[0],
        shared_total[1],
        shared_total[2],
        up_grad,
        up_bias_grad,
        down_grad,
        shared_total[3],
        shared_total[4],
        shared_total[5],
        new_ranges,
    )


def solution(mesh):
    in_specs = (
        P(("dp", "tensor"), None),
        P(("dp", "tensor"), None),
        P(None, "dp", "tensor"),
        P(None, "tensor"),
        P("tensor", "dp"),
        P(),
        P(),
        P(),
        P("dp", "tensor"),
        P("tensor"),
        P("tensor", "dp"),
        P(),
        P(),
        P(),
        P(),
        P("dp"),
        P("dp"),
    )
    out_specs = (
        P(("dp", "tensor"), None),
        P(("dp", "tensor"), None),
        P(None, "dp", "tensor"),
        P(None, "tensor"),
        P("tensor", "dp"),
        P(),
        P(),
        P(),
        P("dp", "tensor"),
        P("tensor"),
        P("tensor", "dp"),
        P(),
        P(),
        P(),
        P(),
    )
    return jax.shard_map(body, mesh=mesh, in_specs=in_specs, out_specs=out_specs, check_vma=False)
```

profile of v0, /device:TPU:0, one launch (start us, length us, event | category | flops | bytes accessed | tf_op | source)
XLA Modules:
  0.0 788.6 jit_solution(17839399608265176750)
XLA Ops:
  10.0 2.8 fusion.80
  14.0 38.9 %all_gather.29 = bf16[3,768,192]{2,0,1:T(4,128)(2,1)S(1)} all-gather(bf16[3,96,192]{2,0,1:T(4,128)(2,1)S(1)} %copy.88), channel_id=1, replica_groups=mesh['dp'=8,'tensor'=4] {'dp'}, dimensions={1}, use_global_device_ids=true | all-gather | bytes 995328 | tf_op jit(solution)/shard_map/all_gather | solution.py:158
  52.9 2.0 copy.89
  56.7 31.1 %all_gather.30 = bf16[192,768]{0,1:T(8,128)(2,1)S(1)} all-gather(bf16[192,96]{0,1:T(8,128)(2,1)S(1)} %copy.94), channel_id=1, replica_groups=mesh['dp'=8,'tensor'=4] {'dp'}, dimensions={1}, use_global_device_ids=true | all-gather | bytes 331776 | tf_op jit(solution)/shard_map/all_gather | solution.py:159
  87.7 4.1 fusion.104
  93.3 3.2 squeeze.75
  96.5 2.2 squeeze.76
  99.4 2.9 fusion.83
  102.4 16.9 %while.26 = (s32[]{:T(128)}, f32[4,512,3,64]{1,3,2,0:T(8,128)}, f32[4,3,512]{2,1,0:T(4,128)}, bf16[4,512,3,64]{1,3,2,0:T(8,128)(2,1)S(1)}, s32[4,512]{1,0:T(4,12...) while((s32[]{:T(128)}, f32[4,512,3,64]{1,3,2,0:T(8,128)}, ...), condition=%wide.region_3.4_spmd, body=%wide.region_0.3_spmd.sunk | while | flops 211286528 | bytes 11534437 | solution.py:171
  104.8 1.8 fusion.151
  113.2 1.8 fusion.151
  119.3 4.2 abs_reduce_fusion.2
  125.2 2.7 convolution_convert_fusion.2
  128.9 36.0 %reduce-scatter.13.cloned.1.call-done = bf16[512,768]{1,0:T(8,128)(2,1)} async-done(((bf16[2048,768]{1,0:T(8,128)(2,1)}), bf16[512,768]{1,0:T(8,128)(2,1)}) %reduce-scatter.13.cloned.1.call-update) | async-done | bytes 786448 | tf_op jit(solution)/shard_map/reduce_scatter | solution.py:174
  168.7 2.9 multiply_convert_fusion.2
  173.4 27.0 %all-gather.9.cloned.1.call-done = bf16[2048,768]{1,0:T(8,128)(2,1)} async-done(((bf16[512,768]{1,0:T(8,128)(2,1)}), bf16[2048,768]{1,0:T(8,128)(2,1)}) %all-gather.9.cloned.1.call-update) | async-done | bytes 3145744 | tf_op jit(solution)/shard_map/all_gather | solution.py:183
  200.4 17.9 %abs_reduce_fusion = (f32[]{:T(128)}, f32[2048,768]{1,0:T(8,128)S(1)}, f32[2048,768]{1,0:T(8,128)}) fusion(f32[768]{0:T(1024)} %param.30, bf16[2048,768]{1,0:T(8,128)(2,1)} %all-gather.9.cloned.1.call-done, bf16[768,768]{1,0:T(8,128)(2,1)} %all-gather.11.cloned.1.call-done), kind=kOutput, calls=%fused_computation.74 | convolution fusion | flops 2521300992 | bytes 16911364 | tf_op jit(solution)/shard_map/dot_general | solution.py:18
  218.3 2.7 copy-done.5
  221.0 3.6 multiply_convert_fusion.1
  224.6 19.9 %all-gather.13.cloned.1.call-done = bf16[768,768]{0,1:T(8,128)(2,1)} async-done(((bf16[768,96]{0,1:T(8,128)(2,1)}), bf16[768,768]{0,1:T(8,128)(2,1)}) %all-gather.13.cloned.1.call-update) | async-done | bytes 1179664 | tf_op jit(solution)/shard_map/all_gather | solution.py:161
  244.5 6.5 convolution_convert_fusion.1
  251.5 35.7 %reduce-scatter.15.cloned.1.call-done = bf16[512,768]{1,0:T(8,128)(2,1)} async-done(((bf16[2048,768]{1,0:T(8,128)(2,1)}), bf16[512,768]{1,0:T(8,128)(2,1)}) %reduce-scatter.15.cloned.1.call-update) | async-done | bytes 786448 | tf_op jit(solution)/shard_map/reduce_scatter | solution.py:187
  287.2 2.0 fusion.101
  290.9 2.1 fusion.98
  295.3 28.6 %all-gather.15.cloned.1.call-done = bf16[2048,768]{1,0:T(8,128)(2,1)} async-done(((bf16[512,768]{1,0:T(8,128)(2,1)}), bf16[2048,768]{1,0:T(8,128)(2,1)}) %all-gather.15.cloned.1.call-update) | async-done | bytes 3145744 | tf_op jit(solution)/shard_map/all_gather | solution.py:208
  323.9 11.1 %convert_reduce_fusion = (f32[768]{0:T(1024)}, bf16[2048,768]{1,0:T(8,128)(2,1)S(1)}) fusion(f32[2048,768]{1,0:T(8,128)} %get-tuple-element.347, f32[768]{0:T(1024)} %param.30, f32[2048,768]{1,0:T(8,128)} %copy-done.5, f32[]{:T(128)} %bitcast.27, bf16[2048,768]{1,0:T(8,128)(2,1)} %all-gather.15.cloned.1.call-done, ...), kind=kOutput, calls=%fused_computation.75 | convolution fusion | flops 2442657024 | bytes 20060164 | tf_op jit(solution)/shard_map/dot_general | solution.py:28
  336.7 4.0 convolution_convert_fusion
  340.8 37.8 %reduce-scatter.17.cloned.1.call-done = bf16[512,768]{1,0:T(8,128)(2,1)} async-done(((bf16[2048,768]{1,0:T(8,128)(2,1)}), bf16[512,768]{1,0:T(8,128)(2,1)}) %reduce-scatter.17.cloned.1.call-update) | async-done | bytes 786448 | tf_op jit(solution)/shard_map/reduce_scatter | solution.py:219
  378.5 4.9 multiply_reduce_fusion.1
  383.5 2.0 fusion.100
  388.0 2.4 copy.95
  392.1 24.2 %all-gather.17.cloned.1.call-done = bf16[2048,768]{1,0:T(8,128)(2,1)} async-done(((bf16[512,768]{1,0:T(8,128)(2,1)}), bf16[2048,768]{1,0:T(8,128)(2,1)}) %all-gather.17.cloned.1.call-update) | async-done | bytes 3145744 | tf_op jit(solution)/shard_map/all_gather | solution.py:229
  416.4 3.5 fusion.70
  422.7 32.6 %while.27 = (s32[]{:T(128)}, bf16[4,512,3,64]{1,3,2,0:T(8,128)(2,1)}, bf16[4,512,3,64]{1,3,2,0:T(8,128)(2,1)}, bf16[4,512,3,64]{1,3,2,0:T(8,128)(2,1)}, bf16[4,5...) while((s32[]{:T(128)}, ...), condition=%wide.region_17.18_spmd, body=%wide.region_15.17_spmd.sunk | while | flops 511408640 | bytes 26129024 | solution.py:234
  457.8 4.1 convolution_bitcast_fusion
  469.8 5.9 fusion.85
  475.6 4.3 copy.107
  479.9 4.8 reshape.286
  484.8 6.0 bitcast_convert_fusion
  490.9 7.0 fusion.106
  498.3 7.0 fusion.105
  505.5 39.8 %all-reduce.2 = (f32[1]{0:T(128)}, f32[1]{0:T(128)}, f32[1]{0:T(128)}, f32[1]{0:T(128)}) all-reduce(f32[1]{0:T(128)} %bitcast.37, f32[1]{0:T(128)} %bitcast.36, f32[1]{0:T(128)} %bitcast.35, f32[1]{0:T(128)} %bitcast.34), channel_id=1, replica_groups=mesh['dp'=8,'tensor'=4] {'dp','tensor'}, use_global_device_ids=true, to_apply=%region_43.44 | all-reduce | flops 4 | bytes 32 | tf_op jit(solution)/shard_map/pmax | solution.py:195
  545.4 3.2 fusion.96
  550.5 41.6 %all-reduce.1 = (f32[768]{0:T(1024)S(1)}, f32[768]{0:T(1024)S(1)}, f32[6,768]{1,0:T(8,128)S(1)}, f32[3072]{0:T(1024)S(1)}) all-reduce(f32[768]{0:T(1024)S(1)} %mul.303, f32[768]{0:T(1024)S(1)} %mul.298, f32[6,768]{1,0:T(8,128)S(1)} %stack.58, f32[3072]{0:T(1024)S(1)} %mul.309), channel_id=1, replica_groups=mesh['dp'=8,'tensor'=4] {'dp','tensor'}, use_global_device_ids=true, to_apply=%region_23.24 | all-reduce | flops 9216 | bytes 73728 | tf_op jit(solution)/shard_map/psum | solution.py:281
  597.7 36.6 %reduce-scatter.19.cloned.1.call-done = bf16[512,768]{1,0:T(8,128)(2,1)} async-done(((bf16[2048,768]{1,0:T(8,128)(2,1)}), bf16[512,768]{1,0:T(8,128)(2,1)}) %reduce-scatter.19.cloned.1.call-update) | async-done | bytes 786448 | tf_op jit(solution)/shard_map/reduce_scatter | solution.py:246
  634.3 2.9 add_convert_fusion
  637.2 70.8 %reduce-scatter.23.cloned.1.call-done = f32[768,96]{0,1:T(8,128)} async-done(((f32[768,768]{0,1:T(8,128)}), f32[768,96]{0,1:T(8,128)}) %reduce-scatter.23.cloned.1.call-update) | async-done | bytes 294928 | tf_op jit(solution)/shard_map/reduce_scatter | solution.py:261
  708.0 73.0 %reduce-scatter.21.cloned.1.call-done = f32[96,768]{1,0:T(8,128)} async-done(((f32[768,768]{1,0:T(8,128)}), f32[96,768]{1,0:T(8,128)}) %reduce-scatter.21.cloned.1.call-update) | async-done | bytes 294928 | tf_op jit(solution)/shard_map/reduce_scatter | solution.py:260
  (241 shorter events, 91.3 us)
Async XLA Ops:
  8.0 79.7 %all-gather.7.cloned.1.call-start = ((), (), s32[]{:S(2)}) async-start(), calls=%async_computation.8 | async-start | bytes 3932160 | tf_op jit(solution)/shard_map/all_gather | solution.py:165
  12.8 42.1 %copy-start.28 = (f32[2,192]{1,0:T(2,128)S(1)}, f32[2,192]{1,0:T(2,128)}, u32[]{:S(2)}) copy-start(f32[2,192]{1,0:T(2,128)} %param.24) | copy-start | bytes 4612
  12.8 42.9 %copy-start.29 = (s32[12]{0:T(128)S(1)}, s32[12]{0:T(128)}, u32[]{:S(2)}) copy-start(s32[12]{0:T(128)} %param.37) | copy-start | bytes 148
  12.8 43.7 %copy-start.14 = (f32[192,96]{1,0:T(8,128)S(1)}, f32[192,96]{1,0:T(8,128)}, u32[]{:S(2)}) copy-start(f32[192,96]{1,0:T(8,128)} %param.25) | copy-start | bytes 221188
  12.8 152.2 %reduce-scatter.13.cloned.1.call-start = ((), (), s32[]{:S(2)}) async-start(), calls=%async_computation.9 | async-start | bytes 3932160 | tf_op jit(solution)/shard_map/reduce_scatter | solution.py:174
  119.3 5.0 copy-start.6
  124.3 0.9 copy-start.8
  125.2 2.8 copy-start.12
  125.2 39.8 %copy-start = (bf16[512,768]{1,0:T(8,128)(2,1)S(1)}, bf16[512,768]{1,0:T(8,128)(2,1)}, u32[]{:S(2)}) copy-start(bf16[512,768]{1,0:T(8,128)(2,1)} %param.21) | copy-start | bytes 2359300
  125.2 39.8 %copy-start.13 = (f32[768]{0:T(1024)S(1)}, f32[768]{0:T(1024)}, u32[]{:S(2)}) copy-start(f32[768]{0:T(1024)} %param.26) | copy-start | bytes 9220
  127.9 45.5 %all-gather.11.cloned.1.call-start = ((), (), s32[]{:S(2)}) async-start(), calls=%async_computation.11 | async-start | bytes 1327104 | tf_op jit(solution)/shard_map/all_gather | solution.py:160
  128.7 71.7 %all-gather.9.cloned.1.call-start = ((), (), s32[]{:S(2)}) async-start(), calls=%async_computation.10 | async-start | bytes 3932160 | tf_op jit(solution)/shard_map/all_gather | solution.py:183
  165.0 3.7 copy-start.1
  166.5 1.6 copy-start.15
  168.1 0.6 copy-start.17
  171.6 72.9 %all-gather.13.cloned.1.call-start = ((), (), s32[]{:S(2)}) async-start(), calls=%async_computation.12 | async-start | bytes 1327104 | tf_op jit(solution)/shard_map/all_gather | solution.py:161
  173.3 113.9 %reduce-scatter.15.cloned.1.call-start = ((), (), s32[]{:S(2)}) async-start(), calls=%async_computation.13 | async-start | bytes 3932160 | tf_op jit(solution)/shard_map/reduce_scatter | solution.py:187
  218.3 2.7 copy-start.5
  251.0 72.9 %all-gather.15.cloned.1.call-start = ((), (), s32[]{:S(2)}) async-start(), calls=%async_computation.14 | async-start | bytes 3932160 | tf_op jit(solution)/shard_map/all_gather | solution.py:208
  287.2 2.3 copy-start.10
  287.2 2.3 copy-start.20
  287.2 3.7 copy-start.27
  293.0 1.2 copy-start.4
  295.2 83.3 %reduce-scatter.17.cloned.1.call-start = ((), (), s32[]{:S(2)}) async-start(), calls=%async_computation.15 | async-start | bytes 3932160 | tf_op jit(solution)/shard_map/reduce_scatter | solution.py:219
  323.9 12.7 %copy-start.30 = (bf16[768,768]{1,0:T(8,128)(2,1)S(1)}, bf16[768,768]{1,0:T(8,128)(2,1)}, u32[]{:S(2)}) copy-start(bf16[768,768]{1,0:T(8,128)(2,1)} %all-gather.11.cloned.1.call-done) | copy-start | bytes 3538948
  335.0 1.7 copy-start.31
  340.7 75.6 %all-gather.17.cloned.1.call-start = ((), (), s32[]{:S(2)}) async-start(), calls=%async_computation.16 | async-start | bytes 3932160 | tf_op jit(solution)/shard_map/all_gather | solution.py:229
  378.5 4.9 copy-start.16
  385.4 1.2 copy-start.2
  387.7 206.5 %reduce-scatter.27.cloned.1.call-start = ((), (), s32[]{:S(2)}) async-start(), calls=%async_computation.21 | async-start | bytes 884736
  455.4 2.4 copy-start.9
  461.9 133.9 %reduce-scatter.25.cloned.1.call-start = ((), (), s32[]{:S(2)}) async-start(), calls=%async_computation.20 | async-start | bytes 2211840
  479.9 4.9 copy-start.11
  484.7 149.6 %reduce-scatter.19.cloned.1.call-start = ((), (), s32[]{:S(2)}) async-start(), calls=%async_computation.17 | async-start | bytes 3932160 | tf_op jit(solution)/shard_map/reduce_scatter | solution.py:246
  490.8 217.2 %reduce-scatter.23.cloned.1.call-start = ((), (), s32[]{:S(2)}) async-start(), calls=%async_computation.19 | async-start | bytes 2654208 | tf_op jit(solution)/shard_map/reduce_scatter | solution.py:261
  497.9 7.5 copy-start.21
  497.9 7.5 copy-start.19
  497.9 7.5 copy-start.18
  497.9 7.5 copy-start.26
  497.9 47.4 %copy-start.24 = (f32[768]{0:T(1024)S(1)}, f32[768]{0:T(1024)}, u32[]{:S(2)}) copy-start(f32[768]{0:T(1024)} %get-tuple-element.326) | copy-start | bytes 9220
  497.9 47.4 %copy-start.23 = (f32[768]{0:T(1024)S(1)}, f32[768]{0:T(1024)}, u32[]{:S(2)}) copy-start(f32[768]{0:T(1024)} %get-tuple-element.258) | copy-start | bytes 9220
  497.9 47.4 %copy-start.22 = (f32[768]{0:T(1024)S(1)}, f32[768]{0:T(1024)}, u32[]{:S(2)}) copy-start(f32[768]{0:T(1024)} %get-tuple-element.264) | copy-start | bytes 9220
  498.0 47.4 %copy-start.25 = (f32[4]{0:T(128)S(1)}, f32[4]{0:T(128)}, u32[]{:S(2)}) copy-start(f32[4]{0:T(128)} %param.35) | copy-start | bytes 52
  498.0 50.6 %copy-start.7 = (bf16[4,512,3,64]{1,3,2,0:T(8,128)(2,1)S(1)}, bf16[4,512,3,64]{1,3,2,0:T(8,128)(2,1)}, u32[]{:S(2)}) copy-start(bf16[4,512,3,64]{1,3,2,0:T(8,128)(2,1)} %get-tuple-element.119) | copy-start | bytes 2359300
  498.0 283.1 %reduce-scatter.21.cloned.1.call-start = ((), (), s32[]{:S(2)}) async-start(), calls=%async_computation.18 | async-start | bytes 2654208 | tf_op jit(solution)/shard_map/reduce_scatter | solution.py:260
  505.3 129.0 %copy-start.3 = (f32[512,768]{1,0:T(8,128)S(1)}, f32[512,768]{1,0:T(8,128)}, u32[]{:S(2)}) copy-start(f32[512,768]{1,0:T(8,128)} %copy-done.2) | copy-start | bytes 4718596
Sparse Core Ops, SparseCore 0:
  12.9 31.2 all-gather.6
  128.0 36.8 reduce-scatter.12
  295.4 28.5 all-gather.14
  387.8 28.4 all-gather.16
Sparse Core Ops, SparseCore 1:
  131.2 40.4 all-gather.10
  173.6 26.7 all-gather.8
  203.0 41.4 all-gather.12
  251.1 36.1 reduce-scatter.14
  340.8 37.7 reduce-scatter.16
  462.0 63.3 reduce-scatter.26
  528.7 66.4 reduce-scatter.24
  597.6 36.7 reduce-scatter.18
  638.3 69.7 reduce-scatter.22
  712.1 68.9 reduce-scatter.20
where the time goes:
time: 799 us; the launch traced here: 789 us
  waiting for transfers between devices  390 us (49%)
  blocking collectives  151 us (19%)
  matrix products  116 us (15%)
  other arithmetic  56.4 us (7%)
  local copies, waits for them, and re-layouts  55.7 us (7%)
  between operations  17.5 us (2%)
    reduce_scatter x1, waiting for transfers between devices, body(): lax.psum_scatter(up_grad, 'dp', scatter_dimension=0, tiled=True)  73 us
    reduce_scatter x1, waiting for transfers between devices, body(): lax.psum_scatter(down_grad, 'dp', scatter_dimension=1, tiled=True)  70.8 us
    psum x1, blocking collectives, body(): lax.psum((spread(query_bias_part), spread(value_bias_part), spread(up_bia...  41.6 us
    pmax x1, blocking collectives, body(): lax.pmax((jnp.max(jnp.abs(inputs)), jnp.max(jnp.abs(context)), jnp.max(jn...  39.8 us
    all_gather x1, blocking collectives, body(): lax.all_gather(masters[0], 'dp', axis=1, tiled=True)  38.9 us
    reduce_scatter x1, waiting for transfers between devices, body(): lax.psum_scatter(matmul_right_t(grad_up, up_back).astype(jnp.bfloat16), '...  37.8 us
    reduce_scatter x1, waiting for transfers between devices, body(): lax.psum_scatter(jnp.einsum('jte,jde->td', stacked, qkv_back, preferred_e...  36.6 us
    reduce_scatter x1, waiting for transfers between devices, body(): lax.psum_scatter(matmul_plain(ctx_clip, out_full).astype(jnp.bfloat16), '...  36 us
  transfers between devices with their start and end apart: 14, of which 10 were waited for; matrix products, arithmetic and copies ran while one was open for 12% of the time, Pallas kernels for 0%

commit v1 on v0

v1 whole, which is shorter than its diff:
```python
import itertools

import jax
import jax.numpy as jnp
from jax import lax
from jax.sharding import PartitionSpec as P

HEAD_DIM = 64
LONG_LEN = 512
SHORT_LEN = 128
ALL = ("dp", "tensor")

ema_decay = 0.9
epsilon = 1e-06
root_half = 0.7071067811865476
density_scale = 0.3989422804014327
NEG = -1000000000.0

f32 = jnp.float32
bf16 = jnp.bfloat16


def mm(left, right):
    return jnp.dot(left, right, preferred_element_type=f32)


def mm_tn(left, right):
    return lax.dot_general(left, right, (((0,), (0,)), ((), ())), preferred_element_type=f32)


def mm_nt(left, right):
    return lax.dot_general(left, right, (((1,), (1,)), ((), ())), preferred_element_type=f32)


def _lin(z, y, x, c):
    return (z * 2 + y) * 4 + x * 2 + c


def _perm(fn):
    out = []
    for z, y, x, c in itertools.product(range(4), range(2), range(2), range(2)):
        out.append((_lin(z, y, x, c), _lin(*fn(z, y, x, c))))
    return out


PC = _perm(lambda z, y, x, c: (z, y, x, 1 - c))
PX = _perm(lambda z, y, x, c: (z, y, 1 - x, c))
PY = _perm(lambda z, y, x, c: (z, 1 - y, x, c))
PZ = [_perm(lambda z, y, x, c, k=k: ((z + k) % 4, y, x, c)) for k in range(4)]
PZX = [_perm(lambda z, y, x, c, k=k: (z ^ k, y, x, c)) for k in range(4)]


def send(value, perm):
    return lax.ppermute(value, ALL, perm)


class Grid:
    blocks = 4

    def __init__(self):
        dp = lax.axis_index("dp")
        lane = lax.axis_index("tensor")
        self.z, self.y = dp // 2, dp % 2
        self.x, self.c = lane // 2, lane % 2

    def absolute(self, near, far_y):
        both = jnp.stack([near, far_y], 1)
        by_z = jnp.flip(both, 0)
        twice = jnp.concatenate([by_z, by_z], 0)
        placed = lax.dynamic_slice_in_dim(twice, (3 - self.z) % 4, 4, 0)
        placed = jnp.where(self.y == 0, placed, jnp.flip(placed, 1))
        return placed.reshape(-1, near.shape[-1])

    def gather(self, shard):
        own = shard[None]
        far = jnp.stack([send(shard, PZ[k]) for k in (1, 2, 3)])
        line = jnp.concatenate([own, far], 0)
        over_x = jnp.concatenate([send(own, PX), send(far, PX)], 0)
        over_y = jnp.concatenate([send(own, PY), send(far, PY)], 0)
        diag = jnp.concatenate([send(over_y[:2], PX), send(over_x[2:], PY)], 0)
        mine = jnp.stack([self.absolute(line, over_y), self.absolute(over_x, diag)])
        theirs = send(mine, PC)
        return jnp.concatenate([mine, theirs], 0)

    def relative(self, grads):
        n, rows, cols = grads.shape
        split = grads.reshape(n, 4, 2, rows // 8, cols)
        split = jnp.where(self.y == 0, split, jnp.flip(split, 2))
        twice = jnp.concatenate([split, split], 1)
        return lax.dynamic_slice_in_dim(twice, self.z, 4, 1).swapaxes(1, 2)

    def scatter_sum(self, grads):
        got = send(grads[2:].astype(bf16), PC)
        both = self.relative((grads[:2] + got.astype(f32)).astype(bf16))
        from_x = send(both[1, 1, :2], PX)
        from_y = send(both[1, 1, 2:], PY)
        y_out = jnp.concatenate([both[0, 1, :2] + from_x, both[0, 1, 2:]], 0)
        x_out = jnp.concatenate([both[1, 0, :2], both[1, 0, 2:] + from_y], 0)
        in_x = send(x_out, PX)
        in_y = send(y_out, PY)
        line = both[0, 0].astype(f32) + in_x.astype(f32) + in_y.astype(f32)
        low = line.astype(bf16)
        parts = [send(low[k], PZ[k]) for k in (1, 2, 3)]
        return line[0] + parts[0].astype(f32) + parts[1].astype(f32) + parts[2].astype(f32)

    def gather_lane(self, vec):
        over_x = send(vec, PX)
        pair = jnp.stack([vec, over_x])
        return jnp.concatenate([pair, send(pair, PC)], 0)

    def order_lane(self, rel):
        grid = rel.reshape((2, 2) + rel.shape[1:])
        grid = jnp.where(self.x == 0, grid, jnp.flip(grid, 1))
        grid = jnp.where(self.c == 0, grid, jnp.flip(grid, 0))
        return grid.swapaxes(0, 1).reshape(rel.shape)

    def sum_max(self, sums, tops):
        for perm in (PC, PX, PY, PZX[1], PZX[2]):
            sums = sums + send(sums, perm)
            tops = jnp.maximum(tops, send(tops, perm))
        return sums, tops


class Plain:
    def __init__(self):
        self.blocks = lax.axis_size("tensor")

    def gather(self, shard):
        rows = lax.all_gather(shard, "dp", axis=0, tiled=True)
        return lax.all_gather(rows, "tensor", axis=0)

    def scatter_sum(self, grads):
        own = lax.psum_scatter(grads, "tensor", scatter_dimension=0, tiled=False)
        return lax.psum_scatter(own, "dp", scatter_dimension=0, tiled=True)

    def gather_lane(self, vec):
        return lax.all_gather(vec, "tensor", axis=0)

    def order_lane(self, rel):
        return rel

    def sum_max(self, sums, tops):
        return lax.psum(sums, ALL), lax.pmax(tops, ALL)


def saturate(values, limit):
    return limit * jnp.tanh(values / limit)


def saturate_slope(values, limit):
    bent = jnp.tanh(values / limit)
    return 1.0 - bent * bent


def gelu_slope(values):
    return (
        0.5 * (1.0 + lax.erf(values * root_half))
        + values * jnp.exp(-0.5 * values * values) * density_scale
    )


def block_masks(long_part, short_part):
    per_block = LONG_LEN // SHORT_LEN
    position = jnp.arange(LONG_LEN, dtype=jnp.int32)
    long_segment = jnp.zeros((long_part.shape[0], LONG_LEN), jnp.int32)
    long_valid = position[None, :] < long_part[:, None]
    short_rows = short_part.reshape(-1, per_block)
    short_segment = jnp.broadcast_to(position // SHORT_LEN, (short_rows.shape[0], LONG_LEN))
    short_limit = jnp.repeat(short_rows, SHORT_LEN, axis=1)
    short_valid = (position % SHORT_LEN)[None, :] < short_limit
    return (
        jnp.concatenate([long_segment, short_segment], 0),
        jnp.concatenate([long_valid, short_valid], 0),
    )


def norm_forward(summed):
    centered = summed - jnp.mean(summed, axis=-1, keepdims=True)
    inv_scale = lax.rsqrt(jnp.mean(centered * centered, axis=-1, keepdims=True) + epsilon)
    return centered * inv_scale, inv_scale


def norm_backward(incoming, normed, inv_scale, gain):
    scaled = incoming * gain
    row_mean = jnp.mean(scaled, axis=-1, keepdims=True)
    row_cross = jnp.mean(scaled * normed, axis=-1, keepdims=True)
    grad_in = inv_scale * (scaled - row_mean - normed * row_cross)
    return grad_in, jnp.sum(incoming * normed, axis=0), jnp.sum(incoming, axis=0)


def make_body(special):
    def body(
        tokens,
        cotangent,
        qkv_weight,
        qv_bias,
        out_weight,
        out_bias,
        first_gain,
        first_shift,
        up_weight,
        up_bias,
        down_weight,
        down_bias,
        second_gain,
        second_shift,
        act_ranges,
        long_lengths,
        short_lengths,
    ):
        net = Grid() if special else Plain()
        lane = lax.axis_index("tensor")
        rows = tokens.shape[0]
        assert rows == LONG_LEN
        cols = qkv_weight.shape[2]
        heads = cols // HEAD_DIM
        blocks = net.blocks

        shard_a = jnp.concatenate(
            [qkv_weight[0], qkv_weight[1], qkv_weight[2], out_weight.T], 1
        ).astype(bf16)
        biases = net.gather_lane(jnp.concatenate([qv_bias[0], qv_bias[1], up_bias]))
        full_a = net.gather(shard_a)
        full_u = net.gather(up_weight.astype(bf16))
        full_d = net.gather(down_weight.T.astype(bf16))

        inputs = tokens.astype(f32)
        in_clip = jnp.clip(inputs, -act_ranges[0], act_ranges[0]).astype(bf16)

        def part(j):
            return full_a[:, :, j * cols : (j + 1) * cols]

        def project(j):
            return jnp.einsum("td,ade->tae", in_clip, part(j), preferred_element_type=f32)

        shape = (rows, blocks * heads, HEAD_DIM)
        queries = (project(0) + biases[:, :cols]).astype(bf16).reshape(shape)
        key_rows = project(1).astype(bf16).reshape(shape)
        values = (project(2) + biases[:, cols : 2 * cols]).astype(bf16).reshape(shape)
        segments, valids = block_masks(long_lengths, short_lengths)
        segment = lax.dynamic_index_in_dim(segments, lane, 0, False)
        key_valid = lax.dynamic_index_in_dim(valids, lane, 0, False)
        allowed = (segment[:, None] == segment[None, :]) & key_valid[None, :]
        score_scale = HEAD_DIM ** (-0.5)
        scores = (
            jnp.einsum("qhd,khd->hqk", queries, key_rows, preferred_element_type=f32) * score_scale
        )
        scores = jnp.where(allowed[None], scores, NEG)
        expanded = jnp.exp(scores - jnp.max(scores, axis=-1, keepdims=True))
        shares = expanded / jnp.sum(expanded, axis=-1, keepdims=True)
        low_shares = shares.astype(bf16)
        context = jnp.einsum("hqk,khd->qhd", low_shares, values, preferred_element_type=f32)
        context = context.reshape(rows, blocks, cols)
        ctx_clip = saturate(context, act_ranges[1]).astype(bf16)
        attn_out = jnp.einsum("tae,ade->td", ctx_clip, part(3), preferred_element_type=f32)
        first_normed, first_inv = norm_forward(inputs + attn_out + out_bias)
        middle = first_normed * first_gain + first_shift
        mid_clip = saturate(middle, act_ranges[2]).astype(bf16)
        up_out = jnp.einsum("td,ade->tae", mid_clip, full_u, preferred_element_type=f32)
        up_out = up_out + biases[:, 2 * cols :]
        hidden = jax.nn.gelu(up_out, approximate=False)
        act_clip = saturate(hidden, act_ranges[3]).astype(bf16)
        ffn_out = jnp.einsum("tae,ade->td", act_clip, full_d, preferred_element_type=f32)
        second_normed, second_inv = norm_forward(middle + ffn_out + down_bias)
        layer_out = (second_normed * second_gain + second_shift).astype(bf16)
        tops = jnp.stack([jnp.max(jnp.abs(v)) for v in (inputs, context, middle, hidden)])

        grad_second, second_gain_part, second_shift_part = norm_backward(
            cotangent.astype(f32), second_normed, second_inv, second_gain
        )
        ffn_grad = grad_second.astype(bf16)
        down_grad = jnp.einsum("td,tae->ade", ffn_grad, act_clip, preferred_element_type=f32)
        down_grad = net.scatter_sum(down_grad).T
        grad_act = jnp.einsum("td,ade->tae", ffn_grad, full_d, preferred_element_type=f32)
        grad_act = grad_act * saturate_slope(hidden, act_ranges[3])
        grad_up = (grad_act * gelu_slope(up_out)).astype(bf16)
        up_grad = jnp.einsum("td,tae->ade", mid_clip, grad_up, preferred_element_type=f32)
        up_grad = net.scatter_sum(up_grad)
        mid_sum = jnp.einsum("tae,ade->td", grad_up, full_u, preferred_element_type=f32)
        grad_middle = grad_second + mid_sum * saturate_slope(middle, act_ranges[2])
        grad_first, first_gain_part, first_shift_part = norm_backward(
            grad_middle, first_normed, first_inv, first_gain
        )
        attn_grad = grad_first.astype(bf16)
        out_grad = jnp.einsum("td,tae->ade", attn_grad, ctx_clip, preferred_element_type=f32)
        grad_ctx = jnp.einsum("td,ade->tae", attn_grad, part(3), preferred_element_type=f32)
        grad_ctx = (grad_ctx * saturate_slope(context, act_ranges[1])).astype(bf16).reshape(shape)
        grad_shares = jnp.einsum("qhd,khd->hqk", grad_ctx, values, preferred_element_type=f32)
        row_inner = jnp.sum(shares * grad_shares, axis=-1, keepdims=True)
        grad_scores = (shares * (grad_shares - row_inner)).astype(bf16)
        grad_values = jnp.einsum("hqk,qhd->khd", low_shares, grad_ctx, preferred_element_type=f32)
        grad_queries = jnp.einsum("hqk,khd->qhd", grad_scores, key_rows, preferred_element_type=f32)
        grad_keys = jnp.einsum("hqk,qhd->khd", grad_scores, queries, preferred_element_type=f32)
        flat = (rows, blocks, cols)
        grad_queries = (grad_queries * score_scale).astype(bf16).reshape(flat)
        grad_keys = (grad_keys * score_scale).astype(bf16).reshape(flat)
        grad_values = grad_values.astype(bf16).reshape(flat)
        stacked = jnp.concatenate([grad_queries, grad_keys, grad_values], -1)
        qkv_grad = jnp.einsum("td,tae->ade", in_clip, stacked, preferred_element_type=f32)
        a_grad = net.scatter_sum(jnp.concatenate([qkv_grad, out_grad], -1))
        qkv_grad = jnp.stack([a_grad[:, j * cols : (j + 1) * cols] for j in range(3)])
        out_grad = a_grad[:, 3 * cols :].T
        input_sum = jnp.einsum(
            "tae,ade->td", stacked, full_a[:, :, : 3 * cols], preferred_element_type=f32
        )
        tokens_grad = grad_first + jnp.where(jnp.abs(inputs) <= act_ranges[0], input_sum, 0.0)

        laned = jnp.concatenate(
            [
                jnp.sum(grad_queries.astype(f32), axis=0),
                jnp.sum(grad_values.astype(f32), axis=0),
                jnp.sum(grad_up.astype(f32), axis=0),
            ],
            -1,
        )
        shared = jnp.stack(
            [
                jnp.sum(grad_first, axis=0),
                first_gain_part,
                first_shift_part,
                jnp.sum(grad_second, axis=0),
                second_gain_part,
                second_shift_part,
            ]
        )
        wide = laned.shape[1]
        sums = jnp.concatenate([net.order_lane(laned).reshape(-1), shared.reshape(-1)])
        sums, tops = net.sum_max(sums, tops)
        own = lax.dynamic_slice_in_dim(sums, lane * wide, wide)
        shared = sums[blocks * wide :].reshape(shared.shape)
        qv_bias_grad = own[: 2 * cols].reshape(2, cols)
        new_ranges = ema_decay * act_ranges + (1.0 - ema_decay) * tops
        return (
            layer_out,
            tokens_grad.astype(bf16),
            qkv_grad,
            qv_bias_grad,
            out_grad,
            shared[0],
            shared[1],
            shared[2],
            up_grad,
            own[2 * cols :],
            down_grad,
            shared[3],
            shared[4],
            shared[5],
            new_ranges,
        )

    return body


def solution(mesh):
    in_specs = (
        P(ALL, None),
        P(ALL, None),
        P(None, "dp", "tensor"),
        P(None, "tensor"),
        P("tensor", "dp"),
        P(),
        P(),
        P(),
        P("dp", "tensor"),
        P("tensor"),
        P("tensor", "dp"),
        P(),
        P(),
        P(),
        P(),
        P("dp"),
        P("dp"),
    )
    out_specs = (
        P(ALL, None),
        P(ALL, None),
        P(None, "dp", "tensor"),
        P(None, "tensor"),
        P("tensor", "dp"),
        P(),
        P(),
        P(),
        P("dp", "tensor"),
        P("tensor"),
        P("tensor", "dp"),
        P(),
        P(),
        P(),
        P(),
    )
    special = mesh.shape["dp"] == 8 and mesh.shape["tensor"] == 4
    return jax.shard_map(
        make_body(special), mesh=mesh, in_specs=in_specs, out_specs=out_specs, check_vma=False
    )
```

time: 799 us -> 401 us (0.50)
  waiting for transfers between devices: 390 us -> 68.3 us
  blocking collectives: 151 us -> 0 us
  starting transfers between devices: 1.86 us -> 81.9 us
  other arithmetic: 56.4 us -> 99.1 us
  matrix products: 116 us -> 91 us
  between operations: 17.5 us -> 3.65 us
    reduce_scatter x6 -> x0, waiting for transfers between devices: 290 us -> none  [the longest x1 73 us: body(): lax.psum_scatter(up_grad, 'dp', scatter_dimension=0, tiled=True)]
    all_gather x6 -> x0, waiting for transfers between devices: 99.8 us -> none  [the longest x1 28.6 us: body(): lax.all_gather(grad_second.astype(jnp.bfloat16), 'tensor', axis=0, tiled=...]
    ppermute x0 -> x66, starting transfers between devices: none -> 81.9 us  [send(): return lax.ppermute(value, ALL, perm)]
    all_gather x2 -> x0, blocking collectives: 70 us -> none  [the longest x1 38.9 us: body(): lax.all_gather(masters[0], 'dp', axis=1, tiled=True)]
    ppermute x0 -> x66, waiting for transfers between devices: none -> 68.3 us  [send(): return lax.ppermute(value, ALL, perm)]
    psum x1 -> x0, blocking collectives: 41.6 us -> none  [body(): lax.psum((spread(query_bias_part), spread(value_bias_part), spread(up_bia...]
    pmax x1 -> x0, blocking collectives: 39.8 us -> none  [body(): lax.pmax((jnp.max(jnp.abs(inputs)), jnp.max(jnp.abs(context)), jnp.max(jn...]
    another operation x4 -> x25, other arithmetic: 0.59 us -> 31.2 us  [the longest x15 18.7 us: absolute(): both = jnp.stack([near, far_y], 1)]
  transfers between devices with their start and end apart: 14 -> 66, of which waited for: 10 -> 17; matrix products, arithmetic and copies ran while one was open for 12% -> 42% of each run, Pallas kernels for 0% -> 0%
where the time goes in v1:
time: 401 us; the launch traced here: 393 us
  other arithmetic  99.1 us (25%)
  matrix products  91 us (23%)
  starting transfers between devices  81.9 us (20%)
  waiting for transfers between devices  68.3 us (17%)
  local copies, waits for them, and re-layouts  49.5 us (12%)
    ppermute x66, starting transfers between devices, send(): return lax.ppermute(value, ALL, perm)  81.9 us
    ppermute x66, waiting for transfers between devices, send(): return lax.ppermute(value, ALL, perm)  68.3 us
    another operation x15, other arithmetic, absolute(): both = jnp.stack([near, far_y], 1)  18.7 us
    reduce_max x2, other arithmetic, body(): jnp.max(jnp.abs(v))  15.9 us
    unnamed x127, local copies, waits for them, and re-layouts  10 us
    convert_element_type x3, other arithmetic, scatter_sum(): both = self.relative((grads[:2] + got.astype(f32)).astype(bf16))  9.92 us
    dot_general x1, matrix products, body(): jnp.einsum('td,ade->tae', ffn_grad, full_d, preferred_element_type=f32)  8.72 us
    dot_general x1, matrix products, body(): jnp.einsum('td,tae->ade', mid_clip, grad_up, preferred_element_type=f32)  8.56 us
  transfers between devices with their start and end apart: 66, of which 17 were waited for; matrix products, arithmetic and copies ran while one was open for 42% of the time, Pallas kernels for 0%

profile of v1, /device:TPU:0, one launch (start us, length us, event | category | flops | bytes accessed | tf_op | source)
XLA Modules:
  0.0 393.5 jit_solution(1148401739987814469)
XLA Ops:
  2.8 3.1 collective-permute-start
  6.0 2.6 collective-permute-start.1
  23.7 2.9 collective-permute-start.14
  30.8 3.4 collective-permute-done.13
  36.7 3.9 collective-permute-start.24
  42.8 3.5 collective-permute-done.23
  46.9 2.8 collective-permute-done.24
  59.4 7.2 %collective-permute-done.16 = bf16[3,96,768]{2,1,0:T(8,128)(2,1)S(1)} collective-permute-done((bf16[3,96,768]{2,1,0:T(8,128)(2,1)}, bf16[3,96,768]{2,1,0:T(8,128)(2,1)S(1)}, u32[]{:S(2)}, u32[]{:S(2)}) %collective-permute-start.16) | collective-permute-done | bytes 442400 | tf_op jit(solution)/shard_map/ppermute | solution.py:54
  69.2 5.4 %collective-permute-done.26 = bf16[3,96,768]{2,1,0:T(8,128)(2,1)} collective-permute-done((bf16[3,96,768]{2,1,0:T(8,128)(2,1)}, bf16[3,96,768]{2,1,0:T(8,128)(2,1)}, u32[]{:S(2)}, u32[]{:S(2)}) %collective-permute-start.26) | collective-permute-done | bytes 442400 | tf_op jit(solution)/shard_map/ppermute | solution.py:54
  110.6 2.4 rev.62
  113.0 2.5 fusion.67
  121.0 2.4 rev.66
  123.4 2.1 fusion.65
  138.3 7.5 %fusion.142 = (f32[12,512]{1,0:T(8,128)S(1)}, f32[12,512,512]{1,2,0:T(8,128)}) fusion(pred[512,512]{0,1:T(8,128)(4,1)S(1)} %copy-done.39, bf16[512,12,64]{0,2,1:T(8,128)(2,1)S(1)} %bitcast.368, bf16[512,12,64]{0,2,1:T(8,128)(2,1)S(1)} %bitcast.348), kind=kOutput, calls=%fused_computation.336 | convolution fusion | flops 415236608 | bytes 14442496 | tf_op jit(solution)/shard_map/sub | solution.py:249
  145.8 7.2 %abs_reduce_fusion.2 = (f32[]{:T(128)}, f32[12,64,512]{2,1,0:T(8,128)S(1)}, bf16[12,64,512]{2,1,0:T(8,128)(2,1)S(1)}) fusion(f32[]{:T(128)} %bitcast, bf16[512,12,64]{0,2,1:T(8,128)(2,1)} %bitcast.382, f32[12,512,512]{1,2,0:T(8,128)} %get-tuple-element.143, f32[12,512]{1,0:T(8,128)S(1)} %get-tuple-element.142), kind=kOutput, calls=%fused_computation.134 | convolution fusion | flops 411697152 | bytes 15753224 | tf_op jit(solution)/shard_map/hqk,khd->qhd/dot_general | solution.py:252
  153.0 2.5 fusion.143
  155.9 6.5 %fusion.57 = (u8[512,768]{1,0:T(8,128)(4,1)S(1)}, u8[512,768]{1,0:T(8,128)(4,1)S(1)}, f32[512,4,768]{2,0,1:T(8,128)S(1)}) fusion(f32[4,768]{1,0:T(4,128)S(1)} %pad_maximum_fusion.36, bf16[2,768,768]{2,1,0:T(8,128)(2,1)} %collective-permute-done.21, bf16[1,768,768]{2,1,0:T(8,128)(2,1)S(1)} %bitcast.360, bf16[1,768,768]{2,1,0:T(8,128)(2,1)S(1)} %bitcast.357, ...), kind=kOutput, calls=%fused_computation.155 | convolution fusion | flops 2454061056 | bytes 13391876 | tf_op jit(solution)/shard_map/td,ade->tae/dot_general | solution.py:259
  162.4 15.2 %abs_reduce_fusion = (f32[]{:T(128)}, f32[512,4,768]{2,0,1:T(8,128)S(1)}) fusion(u8[512,768]{1,0:T(8,128)(4,1)S(1)} %get-tuple-element.61, u8[512,768]{1,0:T(8,128)(4,1)S(1)} %get-tuple-element.60, f32[512,4,768]{2,0,1:T(8,128)S(1)} %get-tuple-element.146, f32[4,768]{1,0:T(4,128)S(1)} %pad_maximum_fusion.36), kind=kLoop, calls=%fused_computation.23 | loop fusion | flops 113246208 | bytes 13381636 | tf_op jit(solution)/shard_map/reduce_max | solution.py:266
  177.6 5.2 %fusion.144 = (f32[512]{0:T(512)S(1)}, f32[512,768]{1,0:T(8,128)S(1)}) fusion(f32[768]{0:T(1024)S(1)} %copy-done.48, bf16[2,768,768]{2,1,0:T(8,128)(2,1)} %collective-permute-done.31, bf16[1,768,768]{2,1,0:T(8,128)(2,1)S(1)} %bitcast.366, bf16[1,768,768]{2,1,0:T(8,128)(2,1)S(1)} %bitcast.363, f32[768]{0:T(1024)S(1)} %copy-done.49, f32[768]{0:T(1024)S(1)} %copy-done.45, ...), kind=kOutput, calls=%fused_computation.338 | convolution fusion | flops 2428108288 | bytes 14171140 | tf_op jit(solution)/shard_map/tae,ade->td/dot_general | solution.py:263
  185.5 6.0 %convolution_bitcast_fusion = f32[4,768,768]{2,1,0:T(8,128)} fusion(f32[512,768]{1,0:T(8,128)S(1)} %get-tuple-element.78, f32[]{:T(128)} %bitcast.36, f32[512,4,768]{2,0,1:T(8,128)S(1)} %get-tuple-element.72), kind=kOutput, calls=%fused_computation.69 | convolution fusion | flops 2421030912 | bytes 17301508 | tf_op jit(solution)/shard_map/td,tae->ade/dot_general | solution.py:272
  191.6 8.7 %convert_reduce_fusion = (f32[4,768]{1,0:T(4,128)S(1)}, bf16[512,4,768]{2,0,1:T(8,128)(2,1)}) fusion(f32[512,4,768]{2,0,1:T(8,128)S(1)} %get-tuple-element.146, f32[4,768]{1,0:T(4,128)S(1)} %pad_maximum_fusion.36, f32[512,4,768]{2,0,1:T(8,128)S(1)} %get-tuple-element.72, f32[]{:T(128)} %bitcast.36, bf16[2,768,768]{2,1,0:T(8,128)(2,1)} %collective-permute-done.31, ...), kind=kOutput, calls=%fused_computation.24 | convolution fusion | flops 2457203712 | bytes 22044676 | tf_op jit(solution)/shard_map/td,ade->tae/dot_general | solution.py:274
  200.3 8.6 %convolution_bitcast_fusion.1 = f32[4,768,768]{2,1,0:T(8,128)} fusion(bf16[512,4,768]{2,0,1:T(8,128)(2,1)} %get-tuple-element.157, f32[]{:T(128)} %bitcast.37, f32[768]{0:T(1024)S(1)} %copy-done.49, f32[768]{0:T(1024)S(1)} %copy-done.45, f32[512,768]{1,0:T(8,128)S(1)} %get-tuple-element.145, f32[512]{0:T(512)S(1)} %add_rsqrt_fusion.1, ...), kind=kOutput, calls=%fused_computation.70 | convolution fusion | flops 2418671616 | bytes 14166020 | tf_op jit(solution)/shard_map/td,tae->ade/dot_general | solution.py:277
  208.9 6.8 %multiply_reduce_fusion.1 = (f32[768]{0:T(1024)S(1)}, f32[512]{0:T(512)S(1)}, f32[]{:T(128)}, f32[512]{0:T(512)S(1)}, f32[768]{0:T(1024)S(1)}, /*index=5*/f32[512,768]{1,0:T(8,128)S(1)}) fusion(f32[512]{0:T(512)S(1)} %add_rsqrt_fusion.1, f32[512,768]{1,0:T(8,128)S(1)} %get-tuple-element.145, f32[512]{0:T(512)S(1)} %broadcast_multiply_fusion.5, ...), kind=kOutput, calls=%fused_computation.135 | convolution fusion | flops 2427713024 | bytes 12603400 | tf_op jit(solution)/shard_map/tae,ade->td/dot_general | solution.py:279
  218.2 5.8 %multiply_reduce_fusion = (f32[12,512]{1,0:T(8,128)S(1)}, f32[12,512,512]{1,2,0:T(8,128)}) fusion(f32[12,512,512]{1,2,0:T(8,128)S(1)} %bitcast.344, f32[12,512]{1,0:T(8,128)S(1)} %get-tuple-element.142, bf16[512,12,64]{0,2,1:T(8,128)(2,1)S(1)} %bitcast.392, bf16[512,12,64]{0,2,1:T(8,128)(2,1)S(1)} %bitcast.383), kind=kOutput, calls=%fused_computation.2 | convolution fusion | flops 412084224 | bytes 26787840 | tf_op jit(solution)/shard_map/qhd,khd->hqk/dot_general | solution.py:288
  224.0 2.9 convert_reduce_fusion.2
  227.7 6.7 %multiply_convert_fusion = bf16[12,512,512]{1,2,0:T(8,128)(2,1)S(1)} fusion(f32[12,512,512]{1,2,0:T(8,128)} %get-tuple-element.151, f32[12,512]{1,0:T(8,128)S(1)} %get-tuple-element.150, f32[12,512,512]{1,2,0:T(8,128)S(1)} %bitcast.344, f32[12,512]{1,0:T(8,128)S(1)} %get-tuple-element.142), kind=kLoop, calls=%fused_computation.1 | loop fusion | flops 12582912 | bytes 31506432 | tf_op jit(solution)/shard_map/convert_element_type | solution.py:290
  236.4 2.9 multiply_convert_fusion.2
  239.3 4.0 %slice.488 = bf16[2,768,768]{2,1,0:T(8,128)(2,1)} slice(f32[4,768,768]{2,1,0:T(8,128)} %convolution_bitcast_fusion), slice={[2:4], [0:768], [0:768]} | slice | bytes 4718592 | tf_op jit(solution)/shard_map/slice | solution.py:93
  243.9 3.9 %slice.489 = bf16[2,768,768]{2,1,0:T(8,128)(2,1)} slice(f32[4,768,768]{2,1,0:T(8,128)} %convolution_bitcast_fusion.1), slice={[2:4], [0:768], [0:768]} | slice | bytes 4718592 | tf_op jit(solution)/shard_map/slice | solution.py:93
  249.3 4.9 %convolution_bitcast_fusion.2 = f32[4,768,576]{1,2,0:T(8,128)S(1)} fusion(bf16[512,4,192]{0,2,1:T(8,128)(2,1)} %bitcast.417, bf16[512,4,192]{0,2,1:T(8,128)(2,1)} %bitcast.394, bf16[512,4,192]{0,2,1:T(8,128)(2,1)S(1)} %bitcast.370, bf16[512,768]{1,0:T(8,128)(2,1)} %param.17, bf16[]{:T(256)S(6)} %neg.6, f32[]{:T(128)} %bitcast.1), kind=kOutput, calls=%fused_computation.75 | convolution fusion | flops 1821376512 | bytes 10223622 | tf_op jit(solution)/shard_map/td,tae->ade/dot_general | solution.py:299
  254.3 7.5 %fusion.53 = bf16[512,768]{1,0:T(8,128)(2,1)} fusion(f32[512,768]{1,0:T(8,128)S(1)} %copy-done.3, bf16[512,768]{1,0:T(8,128)(2,1)S(1)} %copy-done.37, bf16[4,768,768]{1,2,0:T(8,128)(2,1)} %copy-done.1, bf16[512,4,192]{0,2,1:T(8,128)(2,1)S(1)} %bitcast.418, bf16[512,4,192]{0,2,1:T(8,128)(2,1)S(1)} %bitcast.395, bf16[512,4,192]{0,2,1:T(8,128)(2,1)S(1)} %bitcast.371, ...), kind=kOutput, calls=%fused_computation.128 | convolution fusion | flops 1821376512 | bytes 9044480 | tf_op jit(solution)/shard_map/tae,ade->td/dot_general | solution.py:303
  261.8 2.7 pad_maximum_fusion.41
  270.1 2.7 fusion.165
  274.3 7.5 %collective-permute-start.43 = (f32[9216]{0:T(1024)S(1)}, f32[9216]{0:T(1024)S(1)}, u32[]{:S(2)}, u32[]{:S(2)}) collective-permute-start(f32[9216]{0:T(1024)S(1)} %add.271), channel_id=1, source_target_pairs={{0,8},{1,9},{2,10},{3,11},{4,12},{5,13},{6,14},{7,15},{8,0},{9,1},... | collective-permute-start | bytes 110600 | tf_op jit(solution)/shard_map/ppermute | solution.py:54
  281.8 2.7 fusion.166
  286.0 2.1 collective-permute-done.63
  288.1 2.0 collective-permute-start.64
  299.1 4.0 %fusion.22 = bf16[2,768,768]{2,1,0:T(8,128)(2,1)S(1)} fusion(f32[4,768,768]{2,1,0:T(8,128)} %convolution_bitcast_fusion, bf16[2,768,768]{2,1,0:T(8,128)(2,1)} %collective-permute-done.53), kind=kLoop, calls=%fused_computation.49 | loop fusion | flops 3538944 | bytes 9437184 | tf_op jit(solution)/shard_map/convert_element_type | solution.py:94
  308.6 2.3 fusion.23
  315.7 3.6 fusion.21
  319.3 3.1 copy.106
  337.0 10.9 %collective-permute-done.55 = bf16[4,96,768]{2,1,0:T(8,128)(2,1)S(1)} collective-permute-done((bf16[4,96,768]{2,1,0:T(8,128)(2,1)S(1)}, bf16[4,96,768]{2,1,0:T(8,128)(2,1)S(1)}, u32[]{:S(2)}, u32[]{:S(2)}) %collective-permute-start.55) | collective-permute-done | bytes 589856 | tf_op jit(solution)/shard_map/ppermute | solution.py:54
  349.7 10.3 %collective-permute-done.47 = bf16[4,96,768]{2,1,0:T(8,128)(2,1)S(1)} collective-permute-done((bf16[4,96,768]{2,1,0:T(8,128)(2,1)S(1)}, bf16[4,96,768]{2,1,0:T(8,128)(2,1)S(1)}, u32[]{:S(2)}, u32[]{:S(2)}) %collective-permute-start.47) | collective-permute-done | bytes 589856 | tf_op jit(solution)/shard_map/ppermute | solution.py:54
  363.5 2.7 collective-permute-done.34
  367.2 2.8 collective-permute-start.51
  371.0 8.8 %collective-permute-done.59 = bf16[96,768]{1,0:T(8,128)(2,1)S(1)} collective-permute-done((bf16[96,768]{1,0:T(8,128)(2,1)S(1)}, bf16[96,768]{1,0:T(8,128)(2,1)S(1)}, u32[]{:S(2)}, u32[]{:S(2)}) %collective-permute-start.59) | collective-permute-done | bytes 147488 | tf_op jit(solution)/shard_map/ppermute | solution.py:54
  380.6 5.7 %collective-permute-start.52 = (bf16[96,768]{1,0:T(8,128)(2,1)S(1)}, bf16[96,768]{1,0:T(8,128)(2,1)S(1)}, u32[]{:S(2)}, u32[]{:S(2)}) collective-permute-start(bf16[96,768]{1,0:T(8,128)(2,1)S(1)} %get-tuple-element.113), channel_id=1, source_target_pairs={{0,24},{1,25},{2,26},{3,27},{4,28},{5,29},{6,30},{7,31},{8,0},{9,1... | collective-permute-start | bytes 442376 | tf_op jit(solution)/shard_map/ppermute | solution.py:54
  386.3 4.4 %collective-permute-done.38 = bf16[96,768]{1,0:T(8,128)(2,1)S(1)} collective-permute-done((bf16[96,768]{1,0:T(8,128)(2,1)S(1)}, bf16[96,768]{1,0:T(8,128)(2,1)S(1)}, u32[]{:S(2)}, u32[]{:S(2)}) %collective-permute-start.38) | collective-permute-done | bytes 147488 | tf_op jit(solution)/shard_map/ppermute | solution.py:54
  (399 shorter events, 154.5 us)
Async XLA Ops:
  2.8 20.9 %collective-permute-start = (bf16[96,768]{1,0:T(8,128)(2,1)S(1)}, bf16[96,768]{1,0:T(8,128)(2,1)S(1)}, u32[]{:S(2)}, u32[]{:S(2)}) collective-permute-start(bf16[96,768]{1,0:T(8,128)(2,1)S(1)} %pad_maximum_fusion.35), channel_id=1, source_target_pairs={{0,8},{1,9},{2,10},{3,11},{4,12},{5,13},{6,14},{7,15},{8,16},{9,17... | collective-permute-start | bytes 442376 | tf_op jit(solution)/shard_map/ppermute | solution.py:54
  6.0 21.3 %collective-permute-start.1 = (bf16[96,768]{1,0:T(8,128)(2,1)S(1)}, bf16[96,768]{1,0:T(8,128)(2,1)S(1)}, u32[]{:S(2)}, u32[]{:S(2)}) collective-permute-start(bf16[96,768]{1,0:T(8,128)(2,1)S(1)} %pad_maximum_fusion.35), channel_id=1, source_target_pairs={{0,16},{1,17},{2,18},{3,19},{4,20},{5,21},{6,22},{7,23},{8,24},{9,... | collective-permute-start | bytes 442376 | tf_op jit(solution)/shard_map/ppermute | solution.py:54
  8.5 20.3 %collective-permute-start.2 = (bf16[96,768]{1,0:T(8,128)(2,1)S(1)}, bf16[96,768]{1,0:T(8,128)(2,1)S(1)}, u32[]{:S(2)}, u32[]{:S(2)}) collective-permute-start(bf16[96,768]{1,0:T(8,128)(2,1)S(1)} %pad_maximum_fusion.35), channel_id=1, source_target_pairs={{0,24},{1,25},{2,26},{3,27},{4,28},{5,29},{6,30},{7,31},{8,0},{9,1... | collective-permute-start | bytes 442376 | tf_op jit(solution)/shard_map/ppermute | solution.py:54
  13.9 16.3 %collective-permute-start.12 = (bf16[96,768]{1,0:T(8,128)(2,1)S(1)}, bf16[96,768]{1,0:T(8,128)(2,1)S(1)}, u32[]{:S(2)}, u32[]{:S(2)}) collective-permute-start(bf16[96,768]{1,0:T(8,128)(2,1)S(1)} %convert_element_type.199), channel_id=1, source_target_pairs={{0,8},{1,9},{2,10},{3,11},{4,12},{5,13},{6,14},{7,15},{8,16},{9,17... | collective-permute-start | bytes 442376 | tf_op jit(solution)/shard_map/ppermute | solution.py:54
  28.8 52.5 %collective-permute-start.5 = (bf16[1,96,768]{2,1,0:T(8,128)(2,1)}, bf16[1,96,768]{2,1,0:T(8,128)(2,1)}, u32[]{:S(2)}, u32[]{:S(2)}) collective-permute-start(bf16[1,96,768]{2,1,0:T(8,128)(2,1)} %pad_maximum_fusion.34), channel_id=1, source_target_pairs={{0,2},{1,3},{2,0},{3,1},{4,6},{5,7},{6,4},{7,5},{8,10},{9,11},{10,... | collective-permute-start | bytes 442376 | tf_op jit(solution)/shard_map/ppermute | solution.py:54
  30.2 11.1 %collective-permute-start.22 = (bf16[96,768]{1,0:T(8,128)(2,1)S(1)}, bf16[96,768]{1,0:T(8,128)(2,1)S(1)}, u32[]{:S(2)}, u32[]{:S(2)}) collective-permute-start(bf16[96,768]{1,0:T(8,128)(2,1)S(1)} %get-tuple-element.123), channel_id=1, source_target_pairs={{0,8},{1,9},{2,10},{3,11},{4,12},{5,13},{6,14},{7,15},{8,16},{9,17... | collective-permute-start | bytes 442376 | tf_op jit(solution)/shard_map/ppermute | solution.py:54
  34.2 12.2 %collective-permute-start.23 = (bf16[96,768]{1,0:T(8,128)(2,1)S(1)}, bf16[96,768]{1,0:T(8,128)(2,1)S(1)}, u32[]{:S(2)}, u32[]{:S(2)}) collective-permute-start(bf16[96,768]{1,0:T(8,128)(2,1)S(1)} %get-tuple-element.123), channel_id=1, source_target_pairs={{0,16},{1,17},{2,18},{3,19},{4,20},{5,21},{6,22},{7,23},{8,24},{9,... | collective-permute-start | bytes 442376 | tf_op jit(solution)/shard_map/ppermute | solution.py:54
  36.7 13.0 %collective-permute-start.24 = (bf16[96,768]{1,0:T(8,128)(2,1)S(1)}, bf16[96,768]{1,0:T(8,128)(2,1)S(1)}, u32[]{:S(2)}, u32[]{:S(2)}) collective-permute-start(bf16[96,768]{1,0:T(8,128)(2,1)S(1)} %get-tuple-element.123), channel_id=1, source_target_pairs={{0,24},{1,25},{2,26},{3,27},{4,28},{5,29},{6,30},{7,31},{8,0},{9,1... | collective-permute-start | bytes 442376 | tf_op jit(solution)/shard_map/ppermute | solution.py:54
  40.6 11.2 %collective-permute-start.25 = (bf16[1,96,768]{2,1,0:T(8,128)(2,1)}, bf16[1,96,768]{2,1,0:T(8,128)(2,1)S(1)}, u32[]{:S(2)}, u32[]{:S(2)}) collective-permute-start(bf16[1,96,768]{2,1,0:T(8,128)(2,1)} %get-tuple-element.122), channel_id=1, source_target_pairs={{0,4},{1,5},{2,6},{3,7},{4,0},{5,1},{6,2},{7,3},{8,12},{9,13},{10,... | collective-permute-start | bytes 442376 | tf_op jit(solution)/shard_map/ppermute | solution.py:54
  41.3 15.8 %collective-permute-start.4 = (bf16[3,96,768]{2,1,0:T(8,128)(2,1)}, bf16[3,96,768]{2,1,0:T(8,128)(2,1)S(1)}, u32[]{:S(2)}, u32[]{:S(2)}) collective-permute-start(bf16[3,96,768]{2,1,0:T(8,128)(2,1)} %pad_maximum_fusion.30), channel_id=1, source_target_pairs={{0,4},{1,5},{2,6},{3,7},{4,0},{5,1},{6,2},{7,3},{8,12},{9,13},{10,... | collective-permute-start | bytes 1327112 | tf_op jit(solution)/shard_map/ppermute | solution.py:54
  46.4 31.8 %collective-permute-start.6 = (bf16[3,96,768]{2,1,0:T(8,128)(2,1)}, bf16[3,96,768]{2,1,0:T(8,128)(2,1)}, u32[]{:S(2)}, u32[]{:S(2)}) collective-permute-start(bf16[3,96,768]{2,1,0:T(8,128)(2,1)} %pad_maximum_fusion.30), channel_id=1, source_target_pairs={{0,2},{1,3},{2,0},{3,1},{4,6},{5,7},{6,4},{7,5},{8,10},{9,11},{10,... | collective-permute-start | bytes 1327112 | tf_op jit(solution)/shard_map/ppermute | solution.py:54
  49.7 16.9 %collective-permute-start.16 = (bf16[3,96,768]{2,1,0:T(8,128)(2,1)}, bf16[3,96,768]{2,1,0:T(8,128)(2,1)S(1)}, u32[]{:S(2)}, u32[]{:S(2)}) collective-permute-start(bf16[3,96,768]{2,1,0:T(8,128)(2,1)} %pad_maximum_fusion.31), channel_id=1, source_target_pairs={{0,4},{1,5},{2,6},{3,7},{4,0},{5,1},{6,2},{7,3},{8,12},{9,13},{10,... | collective-permute-start | bytes 1327112 | tf_op jit(solution)/shard_map/ppermute | solution.py:54
  51.9 30.0 %collective-permute-start.18 = (bf16[3,96,768]{2,1,0:T(8,128)(2,1)}, bf16[3,96,768]{2,1,0:T(8,128)(2,1)}, u32[]{:S(2)}, u32[]{:S(2)}) collective-permute-start(bf16[3,96,768]{2,1,0:T(8,128)(2,1)} %pad_maximum_fusion.31), channel_id=1, source_target_pairs={{0,2},{1,3},{2,0},{3,1},{4,6},{5,7},{6,4},{7,5},{8,10},{9,11},{10,... | collective-permute-start | bytes 1327112 | tf_op jit(solution)/shard_map/ppermute | solution.py:54
  57.1 17.5 %collective-permute-start.26 = (bf16[3,96,768]{2,1,0:T(8,128)(2,1)}, bf16[3,96,768]{2,1,0:T(8,128)(2,1)}, u32[]{:S(2)}, u32[]{:S(2)}) collective-permute-start(bf16[3,96,768]{2,1,0:T(8,128)(2,1)} %pad_maximum_fusion.32), channel_id=1, source_target_pairs={{0,4},{1,5},{2,6},{3,7},{4,0},{5,1},{6,2},{7,3},{8,12},{9,13},{10,... | collective-permute-start | bytes 1327112 | tf_op jit(solution)/shard_map/ppermute | solution.py:54
  66.6 23.5 %collective-permute-start.28 = (bf16[3,96,768]{2,1,0:T(8,128)(2,1)}, bf16[3,96,768]{2,1,0:T(8,128)(2,1)}, u32[]{:S(2)}, u32[]{:S(2)}) collective-permute-start(bf16[3,96,768]{2,1,0:T(8,128)(2,1)} %pad_maximum_fusion.32), channel_id=1, source_target_pairs={{0,2},{1,3},{2,0},{3,1},{4,6},{5,7},{6,4},{7,5},{8,10},{9,11},{10,... | collective-permute-start | bytes 1327112 | tf_op jit(solution)/shard_map/ppermute | solution.py:54
  74.6 18.7 %collective-permute-start.17 = (bf16[1,96,768]{2,1,0:T(8,128)(2,1)}, bf16[1,96,768]{2,1,0:T(8,128)(2,1)}, u32[]{:S(2)}, u32[]{:S(2)}) collective-permute-start(bf16[1,96,768]{2,1,0:T(8,128)(2,1)} %convert_bitcast_fusion.4), channel_id=1, source_target_pairs={{0,2},{1,3},{2,0},{3,1},{4,6},{5,7},{6,4},{7,5},{8,10},{9,11},{10,... | collective-permute-start | bytes 442376 | tf_op jit(solution)/shard_map/ppermute | solution.py:54
  78.1 18.6 %collective-permute-start.27 = (bf16[1,96,768]{2,1,0:T(8,128)(2,1)}, bf16[1,96,768]{2,1,0:T(8,128)(2,1)}, u32[]{:S(2)}, u32[]{:S(2)}) collective-permute-start(bf16[1,96,768]{2,1,0:T(8,128)(2,1)} %get-tuple-element.122), channel_id=1, source_target_pairs={{0,2},{1,3},{2,0},{3,1},{4,6},{5,7},{6,4},{7,5},{8,10},{9,11},{10,... | collective-permute-start | bytes 442376 | tf_op jit(solution)/shard_map/ppermute | solution.py:54
  81.3 17.9 %collective-permute-start.7 = (bf16[2,96,768]{2,1,0:T(8,128)(2,1)}, bf16[2,96,768]{2,1,0:T(8,128)(2,1)}, u32[]{:S(2)}, u32[]{:S(2)}) collective-permute-start(bf16[2,96,768]{2,1,0:T(8,128)(2,1)} %slice.326), channel_id=1, source_target_pairs={{0,2},{1,3},{2,0},{3,1},{4,6},{5,7},{6,4},{7,5},{8,10},{9,11},{10,... | collective-permute-start | bytes 884744 | tf_op jit(solution)/shard_map/ppermute | solution.py:54
  81.9 17.9 %collective-permute-start.8 = (bf16[2,96,768]{2,1,0:T(8,128)(2,1)}, bf16[2,96,768]{2,1,0:T(8,128)(2,1)}, u32[]{:S(2)}, u32[]{:S(2)}) collective-permute-start(bf16[2,96,768]{2,1,0:T(8,128)(2,1)} %slice.327), channel_id=1, source_target_pairs={{0,4},{1,5},{2,6},{3,7},{4,0},{5,1},{6,2},{7,3},{8,12},{9,13},{10,... | collective-permute-start | bytes 884744 | tf_op jit(solution)/shard_map/ppermute | solution.py:54
  90.1 18.2 %collective-permute-start.19 = (bf16[2,96,768]{2,1,0:T(8,128)(2,1)}, bf16[2,96,768]{2,1,0:T(8,128)(2,1)}, u32[]{:S(2)}, u32[]{:S(2)}) collective-permute-start(bf16[2,96,768]{2,1,0:T(8,128)(2,1)} %slice.332), channel_id=1, source_target_pairs={{0,2},{1,3},{2,0},{3,1},{4,6},{5,7},{6,4},{7,5},{8,10},{9,11},{10,... | collective-permute-start | bytes 884744 | tf_op jit(solution)/shard_map/ppermute | solution.py:54
  93.3 15.0 %collective-permute-start.20 = (bf16[2,96,768]{2,1,0:T(8,128)(2,1)}, bf16[2,96,768]{2,1,0:T(8,128)(2,1)}, u32[]{:S(2)}, u32[]{:S(2)}) collective-permute-start(bf16[2,96,768]{2,1,0:T(8,128)(2,1)} %slice.333), channel_id=1, source_target_pairs={{0,4},{1,5},{2,6},{3,7},{4,0},{5,1},{6,2},{7,3},{8,12},{9,13},{10,... | collective-permute-start | bytes 884744 | tf_op jit(solution)/shard_map/ppermute | solution.py:54
  96.8 22.0 %collective-permute-start.29 = (bf16[2,96,768]{2,1,0:T(8,128)(2,1)}, bf16[2,96,768]{2,1,0:T(8,128)(2,1)}, u32[]{:S(2)}, u32[]{:S(2)}) collective-permute-start(bf16[2,96,768]{2,1,0:T(8,128)(2,1)} %slice.334), channel_id=1, source_target_pairs={{0,2},{1,3},{2,0},{3,1},{4,6},{5,7},{6,4},{7,5},{8,10},{9,11},{10,... | collective-permute-start | bytes 884744 | tf_op jit(solution)/shard_map/ppermute | solution.py:54
  99.2 19.6 %collective-permute-start.30 = (bf16[2,96,768]{2,1,0:T(8,128)(2,1)}, bf16[2,96,768]{2,1,0:T(8,128)(2,1)}, u32[]{:S(2)}, u32[]{:S(2)}) collective-permute-start(bf16[2,96,768]{2,1,0:T(8,128)(2,1)} %slice.335), channel_id=1, source_target_pairs={{0,4},{1,5},{2,6},{3,7},{4,0},{5,1},{6,2},{7,3},{8,12},{9,13},{10,... | collective-permute-start | bytes 884744 | tf_op jit(solution)/shard_map/ppermute | solution.py:54
  108.3 20.1 %collective-permute-start.9 = (bf16[2,768,768]{1,2,0:T(8,128)(2,1)}, bf16[2,768,768]{1,2,0:T(8,128)(2,1)}, u32[]{:S(2)}, u32[]{:S(2)}) collective-permute-start(bf16[2,768,768]{1,2,0:T(8,128)(2,1)} %pad_maximum_fusion.4), channel_id=1, source_target_pairs={{0,1},{1,0},{2,3},{3,2},{4,5},{5,4},{6,7},{7,6},{8,9},{9,8},{10,11... | collective-permute-start | bytes 7077896 | tf_op jit(solution)/shard_map/ppermute | solution.py:54
  118.3 37.5 %collective-permute-start.21 = (bf16[2,768,768]{2,1,0:T(8,128)(2,1)}, bf16[2,768,768]{2,1,0:T(8,128)(2,1)}, u32[]{:S(2)}, u32[]{:S(2)}) collective-permute-start(bf16[2,768,768]{2,1,0:T(8,128)(2,1)} %pad_maximum_fusion.5), channel_id=1, source_target_pairs={{0,1},{1,0},{2,3},{3,2},{4,5},{5,4},{6,7},{7,6},{8,9},{9,8},{10,11... | collective-permute-start | bytes 7077896 | tf_op jit(solution)/shard_map/ppermute | solution.py:54
  128.5 49.1 %collective-permute-start.31 = (bf16[2,768,768]{2,1,0:T(8,128)(2,1)}, bf16[2,768,768]{2,1,0:T(8,128)(2,1)}, u32[]{:S(2)}, u32[]{:S(2)}) collective-permute-start(bf16[2,768,768]{2,1,0:T(8,128)(2,1)} %pad_maximum_fusion.6), channel_id=1, source_target_pairs={{0,1},{1,0},{2,3},{3,2},{4,5},{5,4},{6,7},{7,6},{8,9},{9,8},{10,11... | collective-permute-start | bytes 7077896 | tf_op jit(solution)/shard_map/ppermute | solution.py:54
  243.4 55.8 %collective-permute-start.53 = (bf16[2,768,768]{2,1,0:T(8,128)(2,1)}, bf16[2,768,768]{2,1,0:T(8,128)(2,1)}, u32[]{:S(2)}, u32[]{:S(2)}) collective-permute-start(bf16[2,768,768]{2,1,0:T(8,128)(2,1)} %slice.488), channel_id=1, source_target_pairs={{0,1},{1,0},{2,3},{3,2},{4,5},{5,4},{6,7},{7,6},{8,9},{9,8},{10,11... | collective-permute-start | bytes 7077896 | tf_op jit(solution)/shard_map/ppermute | solution.py:54
  247.8 60.7 %collective-permute-start.45 = (bf16[2,768,768]{2,1,0:T(8,128)(2,1)}, bf16[2,768,768]{2,1,0:T(8,128)(2,1)}, u32[]{:S(2)}, u32[]{:S(2)}) collective-permute-start(bf16[2,768,768]{2,1,0:T(8,128)(2,1)} %slice.489), channel_id=1, source_target_pairs={{0,1},{1,0},{2,3},{3,2},{4,5},{5,4},{6,7},{7,6},{8,9},{9,8},{10,11... | collective-permute-start | bytes 7077896 | tf_op jit(solution)/shard_map/ppermute | solution.py:54
  248.8 15.7 %collective-permute-start.40 = (f32[9216]{0:T(1024)S(1)}, f32[9216]{0:T(1024)S(1)}, u32[]{:S(2)}, u32[]{:S(2)}) collective-permute-start(f32[9216]{0:T(1024)S(1)} %constant_dynamic-update-slice_fusion.7), channel_id=1, source_target_pairs={{0,1},{1,0},{2,3},{3,2},{4,5},{5,4},{6,7},{7,6},{8,9},{9,8},{10,11... | collective-permute-start | bytes 110600 | tf_op jit(solution)/shard_map/ppermute | solution.py:54
  267.8 47.8 %collective-permute-start.32 = (bf16[2,768,768]{1,2,0:T(8,128)(2,1)}, bf16[2,768,768]{1,2,0:T(8,128)(2,1)}, u32[]{:S(2)}, u32[]{:S(2)}) collective-permute-start(bf16[2,768,768]{1,2,0:T(8,128)(2,1)} %fusion.24), channel_id=1, source_target_pairs={{0,1},{1,0},{2,3},{3,2},{4,5},{5,4},{6,7},{7,6},{8,9},{9,8},{10,11... | collective-permute-start | bytes 7077896 | tf_op jit(solution)/shard_map/ppermute | solution.py:54
  274.3 18.4 %collective-permute-start.43 = (f32[9216]{0:T(1024)S(1)}, f32[9216]{0:T(1024)S(1)}, u32[]{:S(2)}, u32[]{:S(2)}) collective-permute-start(f32[9216]{0:T(1024)S(1)} %add.271), channel_id=1, source_target_pairs={{0,8},{1,9},{2,10},{3,11},{4,12},{5,13},{6,14},{7,15},{8,0},{9,1},... | collective-permute-start | bytes 110600 | tf_op jit(solution)/shard_map/ppermute | solution.py:54
  305.5 19.9 %collective-permute-start.54 = (bf16[2,96,768]{2,1,0:T(8,128)(2,1)}, bf16[2,96,768]{2,1,0:T(8,128)(2,1)}, u32[]{:S(2)}, u32[]{:S(2)}) collective-permute-start(bf16[2,96,768]{2,1,0:T(8,128)(2,1)} %get-tuple-element.88), channel_id=1, source_target_pairs={{0,4},{1,5},{2,6},{3,7},{4,0},{5,1},{6,2},{7,3},{8,12},{9,13},{10,... | collective-permute-start | bytes 884744 | tf_op jit(solution)/shard_map/ppermute | solution.py:54
  307.0 19.9 %collective-permute-start.56 = (bf16[2,96,768]{2,1,0:T(8,128)(2,1)}, bf16[2,96,768]{2,1,0:T(8,128)(2,1)}, u32[]{:S(2)}, u32[]{:S(2)}) collective-permute-start(bf16[2,96,768]{2,1,0:T(8,128)(2,1)} %get-tuple-element.90), channel_id=1, source_target_pairs={{0,2},{1,3},{2,0},{3,1},{4,6},{5,7},{6,4},{7,5},{8,10},{9,11},{10,... | collective-permute-start | bytes 884744 | tf_op jit(solution)/shard_map/ppermute | solution.py:54
  314.6 14.2 %collective-permute-start.46 = (bf16[2,96,768]{2,1,0:T(8,128)(2,1)}, bf16[2,96,768]{2,1,0:T(8,128)(2,1)}, u32[]{:S(2)}, u32[]{:S(2)}) collective-permute-start(bf16[2,96,768]{2,1,0:T(8,128)(2,1)} %get-tuple-element.94), channel_id=1, source_target_pairs={{0,4},{1,5},{2,6},{3,7},{4,0},{5,1},{6,2},{7,3},{8,12},{9,13},{10,... | collective-permute-start | bytes 884744 | tf_op jit(solution)/shard_map/ppermute | solution.py:54
  315.1 14.7 %collective-permute-start.48 = (bf16[2,96,768]{2,1,0:T(8,128)(2,1)}, bf16[2,96,768]{2,1,0:T(8,128)(2,1)}, u32[]{:S(2)}, u32[]{:S(2)}) collective-permute-start(bf16[2,96,768]{2,1,0:T(8,128)(2,1)} %get-tuple-element.96), channel_id=1, source_target_pairs={{0,2},{1,3},{2,0},{3,1},{4,6},{5,7},{6,4},{7,5},{8,10},{9,11},{10,... | collective-permute-start | bytes 884744 | tf_op jit(solution)/shard_map/ppermute | solution.py:54
  328.1 19.8 %collective-permute-start.55 = (bf16[4,96,768]{2,1,0:T(8,128)(2,1)S(1)}, bf16[4,96,768]{2,1,0:T(8,128)(2,1)S(1)}, u32[]{:S(2)}, u32[]{:S(2)}) collective-permute-start(bf16[4,96,768]{2,1,0:T(8,128)(2,1)S(1)} %pad_maximum_fusion.28), channel_id=1, source_target_pairs={{0,2},{1,3},{2,0},{3,1},{4,6},{5,7},{6,4},{7,5},{8,10},{9,11},{10,... | collective-permute-start | bytes 1769480 | tf_op jit(solution)/shard_map/ppermute | solution.py:54
  328.8 19.7 %collective-permute-start.57 = (bf16[4,96,768]{2,1,0:T(8,128)(2,1)S(1)}, bf16[4,96,768]{2,1,0:T(8,128)(2,1)S(1)}, u32[]{:S(2)}, u32[]{:S(2)}) collective-permute-start(bf16[4,96,768]{2,1,0:T(8,128)(2,1)S(1)} %pad_maximum_fusion.29), channel_id=1, source_target_pairs={{0,4},{1,5},{2,6},{3,7},{4,0},{5,1},{6,2},{7,3},{8,12},{9,13},{10,... | collective-permute-start | bytes 1769480 | tf_op jit(solution)/shard_map/ppermute | solution.py:54
  331.0 29.0 %collective-permute-start.47 = (bf16[4,96,768]{2,1,0:T(8,128)(2,1)S(1)}, bf16[4,96,768]{2,1,0:T(8,128)(2,1)S(1)}, u32[]{:S(2)}, u32[]{:S(2)}) collective-permute-start(bf16[4,96,768]{2,1,0:T(8,128)(2,1)S(1)} %pad_maximum_fusion.26), channel_id=1, source_target_pairs={{0,2},{1,3},{2,0},{3,1},{4,6},{5,7},{6,4},{7,5},{8,10},{9,11},{10,... | collective-permute-start | bytes 1769480 | tf_op jit(solution)/shard_map/ppermute | solution.py:54
  333.8 28.0 %collective-permute-start.49 = (bf16[4,96,768]{2,1,0:T(8,128)(2,1)S(1)}, bf16[4,96,768]{2,1,0:T(8,128)(2,1)S(1)}, u32[]{:S(2)}, u32[]{:S(2)}) collective-permute-start(bf16[4,96,768]{2,1,0:T(8,128)(2,1)S(1)} %pad_maximum_fusion.27), channel_id=1, source_target_pairs={{0,4},{1,5},{2,6},{3,7},{4,0},{5,1},{6,2},{7,3},{8,12},{9,13},{10,... | collective-permute-start | bytes 1769480 | tf_op jit(solution)/shard_map/ppermute | solution.py:54
  335.4 30.9 %collective-permute-start.34 = (bf16[4,96,768]{2,1,0:T(8,128)(2,1)S(1)}, bf16[4,96,768]{2,1,0:T(8,128)(2,1)S(1)}, u32[]{:S(2)}, u32[]{:S(2)}) collective-permute-start(bf16[4,96,768]{2,1,0:T(8,128)(2,1)S(1)} %pad_maximum_fusion.24), channel_id=1, source_target_pairs={{0,2},{1,3},{2,0},{3,1},{4,6},{5,7},{6,4},{7,5},{8,10},{9,11},{10,... | collective-permute-start | bytes 1769480 | tf_op jit(solution)/shard_map/ppermute | solution.py:54
  347.9 19.3 %collective-permute-start.36 = (bf16[4,96,768]{2,1,0:T(8,128)(2,1)S(1)}, bf16[4,96,768]{2,1,0:T(8,128)(2,1)S(1)}, u32[]{:S(2)}, u32[]{:S(2)}) collective-permute-start(bf16[4,96,768]{2,1,0:T(8,128)(2,1)S(1)} %pad_maximum_fusion.25), channel_id=1, source_target_pairs={{0,4},{1,5},{2,6},{3,7},{4,0},{5,1},{6,2},{7,3},{8,12},{9,13},{10,... | collective-permute-start | bytes 1769480 | tf_op jit(solution)/shard_map/ppermute | solution.py:54
  348.7 21.6 %collective-permute-start.58 = (bf16[96,768]{1,0:T(8,128)(2,1)S(1)}, bf16[96,768]{1,0:T(8,128)(2,1)S(1)}, u32[]{:S(2)}, u32[]{:S(2)}) collective-permute-start(bf16[96,768]{1,0:T(8,128)(2,1)S(1)} %get-tuple-element.109), channel_id=1, source_target_pairs={{0,8},{1,9},{2,10},{3,11},{4,12},{5,13},{6,14},{7,15},{8,16},{9,17... | collective-permute-start | bytes 442376 | tf_op jit(solution)/shard_map/ppermute | solution.py:54
  360.0 19.9 %collective-permute-start.59 = (bf16[96,768]{1,0:T(8,128)(2,1)S(1)}, bf16[96,768]{1,0:T(8,128)(2,1)S(1)}, u32[]{:S(2)}, u32[]{:S(2)}) collective-permute-start(bf16[96,768]{1,0:T(8,128)(2,1)S(1)} %get-tuple-element.111), channel_id=1, source_target_pairs={{0,16},{1,17},{2,18},{3,19},{4,20},{5,21},{6,22},{7,23},{8,24},{9,... | collective-permute-start | bytes 442376 | tf_op jit(solution)/shard_map/ppermute | solution.py:54
  361.8 18.0 %collective-permute-start.60 = (bf16[96,768]{1,0:T(8,128)(2,1)S(1)}, bf16[96,768]{1,0:T(8,128)(2,1)S(1)}, u32[]{:S(2)}, u32[]{:S(2)}) collective-permute-start(bf16[96,768]{1,0:T(8,128)(2,1)S(1)} %get-tuple-element.110), channel_id=1, source_target_pairs={{0,24},{1,25},{2,26},{3,27},{4,28},{5,29},{6,30},{7,31},{8,0},{9,1... | collective-permute-start | bytes 442376 | tf_op jit(solution)/shard_map/ppermute | solution.py:54
  366.3 26.1 %collective-permute-start.50 = (bf16[96,768]{1,0:T(8,128)(2,1)S(1)}, bf16[96,768]{1,0:T(8,128)(2,1)S(1)}, u32[]{:S(2)}, u32[]{:S(2)}) collective-permute-start(bf16[96,768]{1,0:T(8,128)(2,1)S(1)} %get-tuple-element.112), channel_id=1, source_target_pairs={{0,8},{1,9},{2,10},{3,11},{4,12},{5,13},{6,14},{7,15},{8,16},{9,17... | collective-permute-start | bytes 442376 | tf_op jit(solution)/shard_map/ppermute | solution.py:54
  367.2 25.2 %collective-permute-start.51 = (bf16[96,768]{1,0:T(8,128)(2,1)S(1)}, bf16[96,768]{1,0:T(8,128)(2,1)S(1)}, u32[]{:S(2)}, u32[]{:S(2)}) collective-permute-start(bf16[96,768]{1,0:T(8,128)(2,1)S(1)} %get-tuple-element.114), channel_id=1, source_target_pairs={{0,16},{1,17},{2,18},{3,19},{4,20},{5,21},{6,22},{7,23},{8,24},{9,... | collective-permute-start | bytes 442376 | tf_op jit(solution)/shard_map/ppermute | solution.py:54
  379.8 10.9 %collective-permute-start.38 = (bf16[96,768]{1,0:T(8,128)(2,1)S(1)}, bf16[96,768]{1,0:T(8,128)(2,1)S(1)}, u32[]{:S(2)}, u32[]{:S(2)}) collective-permute-start(bf16[96,768]{1,0:T(8,128)(2,1)S(1)} %get-tuple-element.117), channel_id=1, source_target_pairs={{0,16},{1,17},{2,18},{3,19},{4,20},{5,21},{6,22},{7,23},{8,24},{9,... | collective-permute-start | bytes 442376 | tf_op jit(solution)/shard_map/ppermute | solution.py:54
  380.6 11.8 %collective-permute-start.52 = (bf16[96,768]{1,0:T(8,128)(2,1)S(1)}, bf16[96,768]{1,0:T(8,128)(2,1)S(1)}, u32[]{:S(2)}, u32[]{:S(2)}) collective-permute-start(bf16[96,768]{1,0:T(8,128)(2,1)S(1)} %get-tuple-element.113), channel_id=1, source_target_pairs={{0,24},{1,25},{2,26},{3,27},{4,28},{5,29},{6,30},{7,31},{8,0},{9,1... | collective-permute-start | bytes 442376 | tf_op jit(solution)/shard_map/ppermute | solution.py:54
  (78 other events, 547.2 us)

commit v2 on v1

v2 whole, which is shorter than its diff:
```python
import functools
import itertools

import jax
import jax.numpy as jnp
from jax import lax
from jax.experimental import pallas as pl
from jax.experimental.pallas import tpu as pltpu
from jax.sharding import PartitionSpec as P

HEAD_DIM = 64
LONG_LEN = 512
SHORT_LEN = 128
ALL = ("dp", "tensor")

ema_decay = 0.9
epsilon = 1e-06
root_half = 0.7071067811865476
density_scale = 0.3989422804014327
score_scale = HEAD_DIM ** (-0.5)
NEG = -1000000000.0

f32 = jnp.float32
bf16 = jnp.bfloat16


def mm(left, right):
    return jnp.dot(left, right, preferred_element_type=f32)


def mm_tn(left, right):
    return lax.dot_general(left, right, (((0,), (0,)), ((), ())), preferred_element_type=f32)


def mm_nt(left, right):
    return lax.dot_general(left, right, (((1,), (1,)), ((), ())), preferred_element_type=f32)


def _lin(z, y, x, c):
    return (z * 2 + y) * 4 + x * 2 + c


def _perm(fn):
    out = []
    for z, y, x, c in itertools.product(range(4), range(2), range(2), range(2)):
        out.append((_lin(z, y, x, c), _lin(*fn(z, y, x, c))))
    return out


PC = _perm(lambda z, y, x, c: (z, y, x, 1 - c))
PX = _perm(lambda z, y, x, c: (z, y, 1 - x, c))
PY = _perm(lambda z, y, x, c: (z, 1 - y, x, c))
PZ1 = _perm(lambda z, y, x, c: (z ^ 1, y, x, c))
PZ2 = _perm(lambda z, y, x, c: (z ^ 2, y, x, c))


def send(value, perm):
    return lax.ppermute(value, ALL, perm)


class Pieces:
    def __init__(self, bufs, plan):
        self.bufs, self.plan = list(bufs), plan


class Grid:
    parts = 8

    def gather(self, shard):
        own = shard[None]
        pair = jnp.concatenate([own, send(own, PZ1)], 0)
        line = jnp.concatenate([pair, send(pair, PZ2)], 0)
        over_x = send(line, PX)
        over_y = send(line, PY)
        diag_x = send(over_y[:2], PX)
        diag_y = send(over_x[2:], PY)
        near = [line, over_x, over_y, diag_x, diag_y]
        far = [send(b, PC) for b in near]
        rows = shard.shape[0]
        plan = []
        for base, lane in ((0, 0), (5, 2)):
            for k in range(4):
                plan.append((base, k, lane, rows, 2 * k))
                plan.append((base + 1, k, lane + 1, rows, 2 * k))
                plan.append((base + 2, k, lane, rows, 2 * k + 1))
                plan.append((base + 3 + k // 2, k % 2, lane + 1, rows, 2 * k + 1))
        return Pieces(near + far, plan)

    @staticmethod
    def slot(block, dp):
        place = block ^ dp
        return (place & 1) * 4 + (place >> 1)

    def scatter_sum(self, near, far):
        got = send(far, PC)
        shape = (2, 2, 4) + near.shape[2:]
        near, got = near.reshape(shape), got.reshape(shape)

        def both(i, j, ks=slice(None)):
            return near[i, j, ks].astype(f32) + got[i, j, ks].astype(f32)

        lo, hi = slice(0, 2), slice(2, 4)
        from_x = send(both(1, 1, lo).astype(bf16), PX).astype(f32)
        from_y = send(both(1, 1, hi).astype(bf16), PY).astype(f32)
        x_out = jnp.concatenate([both(1, 0, lo), both(1, 0, hi) + from_y], 0).astype(bf16)
        y_out = jnp.concatenate([both(0, 1, lo) + from_x, both(0, 1, hi)], 0).astype(bf16)
        in_x, in_y = send(x_out, PX).astype(f32), send(y_out, PY).astype(f32)
        far_z = (both(0, 0, hi) + in_x[2:] + in_y[2:]).astype(bf16)
        from_z = send(far_z, PZ2).astype(f32)
        near_z = both(0, 0, lo) + in_x[:2] + in_y[:2] + from_z
        return near_z[0] + send(near_z[1].astype(bf16), PZ1).astype(f32)

    def gather_lane(self, vec):
        pair = jnp.stack([vec, send(vec, PX)])
        return jnp.concatenate([pair, send(pair, PC)], 0)

    def order_lane(self, rel):
        lane = lax.axis_index("tensor")
        grid = rel.reshape((2, 2) + rel.shape[1:])
        grid = jnp.where(lane // 2 == 0, grid, jnp.flip(grid, 1))
        grid = jnp.where(lane % 2 == 0, grid, jnp.flip(grid, 0))
        return grid.swapaxes(0, 1).reshape(rel.shape)

    def sum_max(self, both, is_top):
        for perm in (PC, PX, PY, PZ1, PZ2):
            other = send(both, perm)
            both = jnp.where(is_top, jnp.maximum(both, other), both + other)
        return both


class Plain:
    parts = 1

    def gather(self, shard):
        rows = lax.all_gather(shard, "dp", axis=0, tiled=True)
        full = lax.all_gather(rows, "tensor", axis=0)
        return Pieces([full], [(0, k, k, full.shape[1], 0) for k in range(full.shape[0])])

    @staticmethod
    def slot(block, dp):
        return block

    def scatter_sum(self, near, far):
        grads = jnp.concatenate([near, far], 0)
        grads = grads.reshape((grads.shape[0], -1, grads.shape[-1])).astype(f32)
        own = lax.psum_scatter(grads, "tensor", scatter_dimension=0, tiled=False)
        return lax.psum_scatter(own, "dp", scatter_dimension=0, tiled=True)

    def gather_lane(self, vec):
        return lax.all_gather(vec, "tensor", axis=0)

    def order_lane(self, rel):
        return rel

    def sum_max(self, both, is_top):
        return jnp.where(is_top, lax.pmax(both, ALL), lax.psum(both, ALL))


VM = pl.BlockSpec(memory_space=pltpu.VMEM)
SM = pl.BlockSpec(memory_space=pltpu.SMEM)
HB = pl.BlockSpec(memory_space=pl.ANY)


def like(shape, dtype=f32):
    return jax.ShapeDtypeStruct(shape, dtype)


def call(kernel, name, ins, specs, outs, scratch=(), flops=0, moved=0):
    return pl.pallas_call(
        kernel,
        name=name,
        out_shape=outs,
        in_specs=specs,
        out_specs=[VM] * len(outs),
        scratch_shapes=list(scratch),
        compiler_params=pltpu.CompilerParams(vmem_limit_bytes=60 * 2**20),
        cost_estimate=pl.CostEstimate(flops=flops, bytes_accessed=moved, transcendentals=0),
    )(*ins)


def start_loads(plan, refs, dst, sems, dp, cols=None):
    copies = []
    for n, (buf, sub, lane, rows, place) in enumerate(plan):
        at = pl.multiple_of((dp ^ place) * rows, rows) if rows < dst.shape[1] else 0
        src = refs[buf].at[sub] if cols is None else refs[buf].at[sub, :, pl.ds(*cols)]
        copy = pltpu.make_async_copy(src, dst.at[lane, pl.ds(at, rows)], sems.at[n])
        copy.start()
        copies.append(copy)
    return copies


def wait_all(copies):
    for copy in copies:
        copy.wait()


def row_stats(summed):
    centered = summed - jnp.mean(summed, axis=-1, keepdims=True)
    inv = lax.rsqrt(jnp.mean(centered * centered, axis=-1, keepdims=True) + epsilon)
    return centered * inv, inv


def norm_backward(scaled, normed, inv):
    row_mean = jnp.mean(scaled, axis=-1, keepdims=True)
    row_cross = jnp.mean(scaled * normed, axis=-1, keepdims=True)
    return inv * (scaled - row_mean - normed * row_cross)


def col_sum(values):
    return jnp.sum(values, axis=0, keepdims=True)


def top_of(values):
    return jnp.full((1, 128), jnp.max(jnp.abs(values)), f32)


def attn_forward(plan, nb, dims, dp_ref, lim, tokens, qkv_bias, q_seg, k_seg, vecs, *rest):
    blocks, cols, width = dims
    bufs, rest = rest[:nb], rest[nb:]
    qkv_out, lse_out, in_t, ctx_low, ctx_slope, normed_out, inv_out, middle_out, mid_slope, mid_low, mid_t, top_out = rest[:12]
    weight, in_low, mask, ctx_t, acc, top_ctx, sems = rest[12:]
    heads = cols // HEAD_DIM
    low_q = 3 * cols + HEAD_DIM
    loads = start_loads(plan, bufs, weight, sems, dp_ref[0])
    inputs = tokens[...].astype(f32)
    in_low[...] = jnp.clip(inputs, -lim[0], lim[0]).astype(bf16)
    in_t[...] = in_low[...].T
    top_out[0:1, :] = top_of(inputs)
    mask[...] = jnp.where(k_seg[...] == q_seg[...], 0.0, NEG)
    acc[...] = jnp.zeros_like(acc)
    ctx_t[0:HEAD_DIM, :] = jnp.zeros((HEAD_DIM, ctx_t.shape[1]), f32)
    top_ctx[...] = jnp.zeros_like(top_ctx)
    wait_all(loads)

    def step(lane, carry):
        qkv = (mm(in_low[...], weight[lane, :, :low_q]) + qkv_bias[lane]).astype(bf16)
        qkv_out[lane] = qkv
        for h in range(heads):
            at = h * HEAD_DIM
            q = qkv[:, at : at + HEAD_DIM]
            k = qkv[:, cols + at : cols + at + HEAD_DIM]
            v = qkv[:, 2 * cols + at : 2 * cols + at + HEAD_DIM]
            scores = mm_nt(k, q) * score_scale + mask[...]
            peak = jnp.max(scores, axis=0, keepdims=True)
            grown = jnp.exp(scores - peak)
            total = jnp.sum(grown, axis=0, keepdims=True)
            lse_out[lane, h : h + 1, :] = peak + jnp.log(total)
            shares = (grown * (1.0 / total)).astype(bf16)
            ctx_t[HEAD_DIM + at : 2 * HEAD_DIM + at, :] = mm_tn(v, shares)
        context = ctx_t[...].T
        bent = jnp.tanh(context * lim[5])
        low = (lim[1] * bent).astype(bf16)
        ctx_low[lane] = low
        ctx_slope[lane] = 1.0 - bent * bent
        top_ctx[...] = jnp.maximum(top_ctx[...], jnp.max(jnp.abs(context).reshape(-1, 8, context.shape[1]), axis=0))
        acc[...] += mm_nt(low, weight[lane, :, low_q - 2 * HEAD_DIM :])
        return carry

    lax.fori_loop(0, blocks, step, 0)
    top_out[1:2, :] = top_of(top_ctx[...])
    normed, inv = row_stats(tokens[...].astype(f32) + acc[...] + vecs[0:1, :])
    normed_out[...] = normed
    inv_out[...] = inv
    middle = normed * vecs[1:2, :] + vecs[2:3, :]
    middle_out[...] = middle
    bent = jnp.tanh(middle * lim[6])
    low = (lim[2] * bent).astype(bf16)
    mid_low[...] = low
    mid_slope[...] = 1.0 - bent * bent
    mid_t[...] = low.T
    top_out[2:3, :] = top_of(middle)


def up_forward(plan, nb, dims, dp_ref, lim, mid_low, up_bias, *rest):
    blocks, cols, width = dims
    bufs, rest = rest[:nb], rest[nb:]
    act_out, slope_out, top_out, weight, top_hid, sems = rest
    loads = start_loads(plan, bufs, weight, sems, dp_ref[0])
    top_hid[...] = jnp.zeros_like(top_hid)
    wait_all(loads)

    def step(lane, carry):
        up = mm(mid_low[...], weight[lane]) + up_bias[lane]
        half = 0.5 * (1.0 + lax.erf(up * root_half))
        hidden = up * half
        top_hid[...] = jnp.maximum(top_hid[...], jnp.max(jnp.abs(hidden).reshape(-1, 8, hidden.shape[1]), axis=0))
        bent = jnp.tanh(hidden * lim[7])
        act_out[lane] = (lim[3] * bent).astype(bf16)
        slope_out[lane] = (1.0 - bent * bent) * (half + up * jnp.exp(-0.5 * up * up) * density_scale)
        return carry

    lax.fori_loop(0, blocks, step, 0)
    top_out[...] = jnp.broadcast_to(top_of(top_hid[...]), top_out.shape)


def down_forward(plan, nb, dims, dp_ref, act, middle, cotangent, vecs, *rest):
    blocks, cols, width = dims
    bufs, rest = rest[:nb], rest[nb:]
    layer_out, grad_out, ffn_low, ffn_t, sums, weight, acc, sems = rest
    loads = start_loads(plan, bufs, weight, sems, dp_ref[0])
    acc[...] = middle[...] + vecs[3:4, :]
    wait_all(loads)

    def step(lane, carry):
        acc[...] += mm_nt(act[lane], weight[lane])
        return carry

    lax.fori_loop(0, blocks, step, 0)
    normed, inv = row_stats(acc[...])
    layer_out[...] = (normed * vecs[4:5, :] + vecs[5:6, :]).astype(bf16)
    incoming = cotangent[...].astype(f32)
    grad = norm_backward(incoming * vecs[4:5, :], normed, inv)
    grad_out[...] = grad
    low = grad.astype(bf16)
    ffn_low[...] = low
    ffn_t[...] = low.T
    sums[...] = jnp.zeros_like(sums)
    sums[0:1, :] = col_sum(grad)
    sums[1:2, :] = col_sum(incoming * normed)
    sums[2:3, :] = col_sum(incoming)


def weight_grad(first, slot, parts, dp_ref, left_t, right, out):
    rows = left_t.shape[0] // parts

    def step(i, carry):
        grad = mm(left_t[...], right[first + i]).astype(bf16)
        for block in range(parts):
            out[i, slot(block, dp_ref[0])] = grad[block * rows : (block + 1) * rows]
        return carry

    lax.fori_loop(0, out.shape[0], step, 0)


def act_backward(plan, nb, dims, dp_ref, ffn_low, slope, *rest):
    blocks, cols, width = dims
    bufs, rest = rest[:nb], rest[nb:]
    grad_up, sums, weight, sems = rest
    wait_all(start_loads(plan, bufs, weight, sems, dp_ref[0]))

    def step(lane, carry):
        low = (mm(ffn_low[...], weight[lane]) * slope[lane]).astype(bf16)
        grad_up[lane] = low
        sums[lane] = col_sum(low.astype(f32))
        return carry

    lax.fori_loop(0, blocks, step, 0)


def mid_backward(plans, nbs, dims, dp_ref, grad_up, grad_second, mid_slope, normed, inv, vecs, ctx_slope, *rest):
    blocks, cols, width = dims
    up_bufs, rest = rest[: nbs[0]], rest[nbs[0] :]
    a_bufs, rest = rest[: nbs[1]], rest[nbs[1] :]
    grad_out, attn_t, grad_ctx, sums, weight, out_weight, acc, attn_low, up_sems, a_sems = rest
    at = 3 * cols - HEAD_DIM
    up_loads = start_loads(plans[0], up_bufs, weight, up_sems, dp_ref[0])
    a_loads = start_loads(plans[1], a_bufs, out_weight, a_sems, dp_ref[0], (at, cols + HEAD_DIM))
    acc[...] = jnp.zeros_like(acc)
    wait_all(up_loads)

    def step(lane, carry):
        acc[...] += mm_nt(grad_up[lane], weight[lane])
        return carry

    lax.fori_loop(0, blocks, step, 0)
    incoming = grad_second[...] + acc[...] * mid_slope[...]
    grad = norm_backward(incoming * vecs[1:2, :], normed[...], inv[...])
    grad_out[...] = grad
    attn_low[...] = grad.astype(bf16)
    attn_t[...] = attn_low[...].T
    sums[...] = jnp.zeros_like(sums)
    sums[0:1, :] = col_sum(grad)
    sums[1:2, :] = col_sum(incoming * normed[...])
    sums[2:3, :] = col_sum(incoming)
    wait_all(a_loads)

    def spread(lane, carry):
        grad_ctx[lane] = (mm(attn_low[...], out_weight[lane]) * ctx_slope[lane]).astype(bf16)
        return carry

    lax.fori_loop(0, blocks, spread, 0)


def attn_backward(dims, qkv, lse, grad_ctx, q_seg, k_seg, out, sums, mask):
    blocks, cols, width = dims
    heads = cols // HEAD_DIM
    mask[...] = jnp.where(k_seg[...] == q_seg[...], 0.0, NEG)

    def step(lane, carry):
        for h in range(heads):
            at = h * HEAD_DIM
            q = qkv[lane, :, at : at + HEAD_DIM]
            k = qkv[lane, :, cols + at : cols + at + HEAD_DIM]
            v = qkv[lane, :, 2 * cols + at : 2 * cols + at + HEAD_DIM]
            grad = grad_ctx[lane, :, HEAD_DIM + at : 2 * HEAD_DIM + at]
            shares = jnp.exp(mm_nt(k, q) * score_scale + mask[...] - lse[lane, h : h + 1, :])
            grad_shares = mm_nt(v, grad)
            inner = jnp.sum(shares * grad_shares, axis=0, keepdims=True)
            grad_scores = (shares * (grad_shares - inner)).astype(bf16)
            grad_v = mm(shares.astype(bf16), grad)
            grad_k = mm(grad_scores, q) * score_scale
            grad_q = (mm_tn(k, grad_scores) * score_scale).T
            out[lane, :, at : at + HEAD_DIM] = grad_q.astype(bf16)
            out[lane, :, cols + at : cols + at + HEAD_DIM] = grad_k.astype(bf16)
            out[lane, :, 2 * cols + at : 2 * cols + at + HEAD_DIM] = grad_v.astype(bf16)
        out[lane, :, 3 * cols :] = jnp.zeros((out.shape[1], HEAD_DIM), bf16)
        sums[lane] = col_sum(out[lane].astype(f32))
        return carry

    lax.fori_loop(0, blocks, step, 0)


def in_weight_grad(first, slot, parts, dims, dp_ref, in_t, attn_t, grad_qkv, ctx_low, out):
    blocks, cols, width = dims
    rows = in_t.shape[0] // parts
    at = 3 * cols - HEAD_DIM
    end = 3 * cols + HEAD_DIM

    def step(i, carry):
        left = mm(in_t[...], grad_qkv[first + i])
        right = mm(attn_t[...], ctx_low[first + i])
        mixed = (left[:, at:] + right[:, : end - at]).astype(bf16)
        for block in range(parts):
            rs = slice(block * rows, (block + 1) * rows)
            place = slot(block, dp_ref[0])
            out[i, place, :, :at] = left[rs, :at].astype(bf16)
            out[i, place, :, at:end] = mixed[rs]
            out[i, place, :, end:] = right[rs, end - at :].astype(bf16)
        return carry

    lax.fori_loop(0, out.shape[0], step, 0)


def token_backward(plan, nb, dims, dp_ref, lim, grad_qkv, grad_first, tokens, *rest):
    blocks, cols, width = dims
    bufs, rest = rest[:nb], rest[nb:]
    out, weight, acc, sems = rest
    loads = start_loads(plan, bufs, weight, sems, dp_ref[0], (0, 3 * cols + HEAD_DIM))
    acc[...] = jnp.zeros_like(acc)
    wait_all(loads)

    def step(lane, carry):
        acc[...] += mm_nt(grad_qkv[lane], weight[lane])
        return carry

    lax.fori_loop(0, blocks, step, 0)
    inputs = tokens[...].astype(f32)
    out[...] = (grad_first[...] + jnp.where(jnp.abs(inputs) <= lim[0], acc[...], 0.0)).astype(bf16)


def block_masks(long_part, short_part):
    per_block = LONG_LEN // SHORT_LEN
    position = jnp.arange(LONG_LEN, dtype=jnp.int32)
    long_segment = jnp.zeros((long_part.shape[0], LONG_LEN), jnp.int32)
    long_valid = position[None, :] < long_part[:, None]
    short_rows = short_part.reshape(-1, per_block)
    short_segment = jnp.broadcast_to(position // SHORT_LEN, (short_rows.shape[0], LONG_LEN))
    short_limit = jnp.repeat(short_rows, SHORT_LEN, axis=1)
    short_valid = (position % SHORT_LEN)[None, :] < short_limit
    return (
        jnp.concatenate([long_segment, short_segment], 0),
        jnp.concatenate([long_valid, short_valid], 0),
    )


def make_body(special):
    def body(
        tokens,
        cotangent,
        qkv_weight,
        qv_bias,
        out_weight,
        out_bias,
        first_gain,
        first_shift,
        up_weight,
        up_bias,
        down_weight,
        down_bias,
        second_gain,
        second_shift,
        act_ranges,
        long_lengths,
        short_lengths,
    ):
        net = Grid() if special else Plain()
        lane = lax.axis_index("tensor")
        dp = jnp.full((1,), lax.axis_index("dp"), jnp.int32)
        rows, width = tokens.shape
        assert rows == LONG_LEN
        cols = qkv_weight.shape[2]
        blocks = lax.axis_size("tensor")
        dims = (blocks, cols, width)
        wide = 3 * cols + HEAD_DIM
        out_cols = cols + HEAD_DIM

        shard_a = jnp.concatenate(
            [qkv_weight[0], qkv_weight[1], qkv_weight[2], out_weight.T], 1
        ).astype(bf16)
        biases = net.gather_lane(jnp.concatenate([qv_bias[0], qv_bias[1], up_bias]))
        full_a = net.gather(shard_a)
        full_u = net.gather(up_weight.astype(bf16))
        full_d = net.gather(down_weight.T.astype(bf16))

        def sems(pieces):
            return pltpu.SemaphoreType.DMA((len(pieces.plan),))

        def vmem(*shape, dtype=f32):
            return pltpu.VMEM(shape, dtype)

        qkv_bias = jnp.concatenate(
            [
                biases[:, :cols],
                jnp.zeros((blocks, cols), f32),
                biases[:, cols : 2 * cols],
                jnp.zeros((blocks, HEAD_DIM), f32),
            ],
            1,
        )[:, None]
        up_biases = biases[:, None, 2 * cols :]
        limits = jnp.concatenate([act_ranges, 1.0 / act_ranges])
        vecs = jnp.stack(
            [out_bias, first_gain, first_shift, down_bias, second_gain, second_shift, out_bias, out_bias]
        )
        segments, valids = block_masks(long_lengths, short_lengths)
        q_seg = lax.dynamic_slice_in_dim(segments, lane, 1, 0)
        k_seg = lax.dynamic_slice_in_dim(jnp.where(valids, segments, -1), lane, 1, 0).reshape(rows, 1)

        n_a, n_u, n_d = len(full_a.bufs), len(full_u.bufs), len(full_d.bufs)
        unit = 2 * rows * width * width * blocks
        moved = 2 * width * width * blocks
        qkv, lse, in_t, ctx_low, ctx_slope, normed, inv, middle, mid_slope, mid_low, mid_t, tops = call(
            functools.partial(attn_forward, full_a.plan, n_a, dims),
            "attn_forward",
            [dp, limits, tokens, qkv_bias, q_seg, k_seg, vecs] + full_a.bufs,
            [SM, SM] + [VM] * 5 + [HB] * n_a,
            [
                like((blocks, rows, wide), bf16),
                like((blocks, 8, rows)),
                like((width, rows), bf16),
                like((blocks, rows, out_cols), bf16),
                like((blocks, rows, out_cols)),
                like((rows, width)),
                like((rows, 1)),
                like((rows, width)),
                like((rows, width)),
                like((rows, width), bf16),
                like((width, rows), bf16),
                like((8, 128)),
            ],
            [
                vmem(blocks, width, 4 * cols, dtype=bf16),
                vmem(rows, width, dtype=bf16),
                vmem(rows, rows),
                vmem(out_cols, rows),
                vmem(rows, width),
                vmem(8, out_cols),
                sems(full_a),
            ],
            4 * unit,
            3 * moved,
        )
        up_cols = up_weight.shape[1]
        act, slope, top_hid = call(
            functools.partial(up_forward, full_u.plan, n_u, dims),
            "up_forward",
            [dp, limits, mid_low, up_biases] + full_u.bufs,
            [SM, SM, VM, VM] + [HB] * n_u,
            [like((blocks, rows, up_cols), bf16), like((blocks, rows, up_cols)), like((8, 128))],
            [vmem(blocks, width, up_cols, dtype=bf16), vmem(8, up_cols), sems(full_u)],
            2 * unit,
            3 * moved,
        )
        layer_out, grad_second, ffn_low, ffn_t, sums_b = call(
            functools.partial(down_forward, full_d.plan, n_d, dims),
            "down_forward",
            [dp, act, middle, cotangent, vecs] + full_d.bufs,
            [SM] + [VM] * 4 + [HB] * n_d,
            [
                like((rows, width), bf16),
                like((rows, width)),
                like((rows, width), bf16),
                like((width, rows), bf16),
                like((8, width)),
            ],
            [vmem(blocks, width, up_cols, dtype=bf16), vmem(rows, width), sems(full_d)],
            unit,
            2 * moved,
        )

        half = blocks // 2
        grad_shape = like((half, net.parts, width // net.parts, up_cols), bf16)

        def grad_of(name, left_t, right):
            def side(first, tag):
                return call(
                    functools.partial(weight_grad, first, net.slot, net.parts),
                    name + tag,
                    [dp, left_t, right],
                    [SM, VM, VM],
                    [grad_shape],
                    (),
                    unit // 2,
                    moved,
                )[0]

            far = side(half, "_far")
            return side(0, "_near"), far

        down_near, down_far = grad_of("down_grad", ffn_t, act)
        down_grad = net.scatter_sum(down_near, down_far).T
        grad_up, up_sums = call(
            functools.partial(act_backward, full_d.plan, n_d, dims),
            "act_backward",
            [dp, ffn_low, slope] + full_d.bufs,
            [SM, VM, VM] + [HB] * n_d,
            [like((blocks, rows, up_cols), bf16), like((blocks, 1, up_cols))],
            [vmem(blocks, width, up_cols, dtype=bf16), sems(full_d)],
            unit,
            3 * moved,
        )
        up_near, up_far = grad_of("up_grad", mid_t, grad_up)
        up_grad = net.scatter_sum(up_near, up_far)
        grad_first, attn_t, grad_ctx, sums_a = call(
            functools.partial(mid_backward, (full_u.plan, full_a.plan), (n_u, n_a), dims),
            "mid_backward",
            [dp, grad_up, grad_second, mid_slope, normed, inv, vecs, ctx_slope] + full_u.bufs + full_a.bufs,
            [SM] + [VM] * 7 + [HB] * (n_u + n_a),
            [
                like((rows, width)),
                like((width, rows), bf16),
                like((blocks, rows, out_cols), bf16),
                like((8, width)),
            ],
            [
                vmem(blocks, width, up_cols, dtype=bf16),
                vmem(blocks, width, out_cols, dtype=bf16),
                vmem(rows, width),
                vmem(rows, width, dtype=bf16),
                sems(full_u),
                sems(full_a),
            ],
            unit + unit // 3,
            3 * moved,
        )
        grad_qkv, qkv_sums = call(
            functools.partial(attn_backward, dims),
            "attn_backward",
            [qkv, lse, grad_ctx, q_seg, k_seg],
            [VM] * 5,
            [like((blocks, rows, wide), bf16), like((blocks, 1, wide))],
            [vmem(rows, rows)],
            4 * unit,
            2 * moved,
        )

        def in_side(first, tag):
            return call(
                functools.partial(in_weight_grad, first, net.slot, net.parts, dims),
                "in_grad" + tag,
                [dp, in_t, attn_t, grad_qkv, ctx_low],
                [SM] + [VM] * 4,
                [grad_shape],
                (),
                unit // 2,
                moved,
            )[0]

        a_far = in_side(half, "_far")
        a_near = in_side(0, "_near")
        a_grad = net.scatter_sum(a_near, a_far)
        qkv_grad = jnp.stack([a_grad[:, j * cols : (j + 1) * cols] for j in range(3)])
        out_grad = a_grad[:, 3 * cols :].T
        tokens_grad = call(
            functools.partial(token_backward, full_a.plan, n_a, dims),
            "token_backward",
            [dp, limits, grad_qkv, grad_first, tokens] + full_a.bufs,
            [SM, SM, VM, VM, VM] + [HB] * n_a,
            [like((rows, width), bf16)],
            [vmem(blocks, width, wide, dtype=bf16), vmem(rows, width), sems(full_a)],
            unit,
            2 * moved,
        )[0]

        laned = jnp.concatenate(
            [qkv_sums[:, 0, :cols], qkv_sums[:, 0, 2 * cols : 3 * cols], up_sums[:, 0]], -1
        )
        per_lane = laned.shape[1]
        top_row = jnp.concatenate([tops[:3], top_hid[:1]], 0)
        packed = jnp.concatenate(
            [net.order_lane(laned).reshape(-1, 128), sums_a[:3].reshape(-1, 128), sums_b[:3].reshape(-1, 128), top_row], 0
        )
        is_top = (jnp.arange(packed.shape[0]) >= packed.shape[0] - 4)[:, None]
        packed = net.sum_max(packed, is_top)
        own = lax.dynamic_slice_in_dim(packed, lane * (per_lane // 128), per_lane // 128).reshape(-1)
        shared = packed[blocks * per_lane // 128 : -4].reshape(6, width)
        qv_bias_grad = own[: 2 * cols].reshape(2, cols)
        new_ranges = ema_decay * act_ranges + (1.0 - ema_decay) * packed[-4:, 0]
        return (
            layer_out,
            tokens_grad,
            qkv_grad,
            qv_bias_grad,
            out_grad,
            shared[0],
            shared[1],
            shared[2],
            up_grad,
            own[2 * cols :],
            down_grad,
            shared[3],
            shared[4],
            shared[5],
            new_ranges,
        )

    return body


def solution(mesh):
    in_specs = (
        P(ALL, None),
        P(ALL, None),
        P(None, "dp", "tensor"),
        P(None, "tensor"),
        P("tensor", "dp"),
        P(),
        P(),
        P(),
        P("dp", "tensor"),
        P("tensor"),
        P("tensor", "dp"),
        P(),
        P(),
        P(),
        P(),
        P("dp"),
        P("dp"),
    )
    out_specs = (
        P(ALL, None),
        P(ALL, None),
        P(None, "dp", "tensor"),
        P(None, "tensor"),
        P("tensor", "dp"),
        P(),
        P(),
        P(),
        P("dp", "tensor"),
        P("tensor"),
        P("tensor", "dp"),
        P(),
        P(),
        P(),
        P(),
    )
    special = mesh.shape["dp"] == 8 and mesh.shape["tensor"] == 4
    return jax.shard_map(
        make_body(special), mesh=mesh, in_specs=in_specs, out_specs=out_specs, check_vma=False
    )
```

time: 401 us -> 352 us (0.88); the launches traced: 393 us -> 350 us
  Pallas kernels: 0 us -> 127 us
  matrix products: 91 us -> 0 us
  other arithmetic: 99.1 us -> 39.1 us
  waiting for transfers between devices: 68.3 us -> 108 us
  starting transfers between devices: 81.9 us -> 48.2 us
  local copies, waits for them, and re-layouts: 49.5 us -> 25.8 us
    pallas_call x0 -> x13, Pallas kernels: none -> 127 us  [call(): pl.pallas_call(kernel, name=name, out_shape=outs, in_specs=specs, out_spe...]
    dot_general x15 -> x0, matrix products: 78.3 us -> none  [the longest x1 8.72 us: body(): jnp.einsum('td,ade->tae', ffn_grad, full_d, preferred_element_type=f32)]
    ppermute x66 -> x61, waiting for transfers between devices: 68.3 us -> 108 us  [send(): return lax.ppermute(value, ALL, perm)]
    ppermute x66 -> x61, starting transfers between devices: 81.9 us -> 48.2 us  [send(): return lax.ppermute(value, ALL, perm)]
    another operation x24 -> x5, other arithmetic: 30.4 us -> 5.59 us  [the longest x15 18.7 us: absolute(): both = jnp.stack([near, far_y], 1)]
    reduce_max x2 -> x0, other arithmetic: 15.9 us -> none  [body(): jnp.max(jnp.abs(v))]
    slice x11, local copies, waits for them, and re-layouts: 17 us -> 4.89 us  [the longest x3 1.74 us: gather(): diag_y = send(over_x[2:], PY)]
    convert_element_type x11 -> x9, other arithmetic: 19.9 us -> 8.19 us  [the longest x6 4.79 us: scatter_sum(): in_x, in_y = (send(x_out, PX).astype(f32), send(y_out, PY).astype(f32))]
  transfers between devices with their start and end apart: 66 -> 61, of which waited for: 17 -> 19; matrix products, arithmetic and copies ran while one was open for 42% -> 17% of each run, Pallas kernels for 0% -> 22%
where the time goes in v2:
time: 352 us; the launch traced here: 350 us
  Pallas kernels  127 us (36%)
  waiting for transfers between devices  108 us (31%)
  starting transfers between devices  48.2 us (14%)
  other arithmetic  39.1 us (11%)
  local copies, waits for them, and re-layouts  25.8 us (7%)
    pallas_call x13, Pallas kernels, call(): pl.pallas_call(kernel, name=name, out_shape=outs, in_specs=specs, out_spe...  127 us
    ppermute x61, waiting for transfers between devices, send(): return lax.ppermute(value, ALL, perm)  108 us
    ppermute x61, starting transfers between devices, send(): return lax.ppermute(value, ALL, perm)  48.2 us
    another operation x7, local copies, waits for them, and re-layouts, body(): jnp.stack([out_bias, first_gain, first_shift, down_bias, second_gain, sec...  9.04 us
  transfers between devices with their start and end apart: 61, of which 19 were waited for; matrix products, arithmetic and copies ran while one was open for 17% of the time, Pallas kernels for 22%

profile of v2, /device:TPU:0, one launch (start us, length us, event | category | flops | bytes accessed | tf_op | source)
XLA Modules:
  0.0 350.2 jit_solution(6852371775433503961)
XLA Ops:
  1.7 3.1 collective-permute-start.24
  6.9 2.4 collective-permute-done.24
  9.3 3.0 collective-permute-start.25
  13.7 1.7 collective-permute-start.14
  17.0 19.8 %collective-permute-done.14 = bf16[2,96,768]{2,1,0:T(8,128)(2,1)S(1)} collective-permute-done((bf16[2,96,768]{2,1,0:T(8,128)(2,1)S(1)}, bf16[2,96,768]{2,1,0:T(8,128)(2,1)S(1)}, u32[]{:S(2)}, u32[]{:S(2)}) %collective-permute-start.14) | collective-permute-done | bytes 294944 | tf_op jit(solution)/shard_map/ppermute | solution.py:58
  37.7 1.4 collective-permute-start.16
  39.1 1.5 collective-permute-start.15
  42.2 12.4 %collective-permute-done.3 = bf16[2,96,768]{2,1,0:T(8,128)(2,1)S(1)} collective-permute-done((bf16[2,96,768]{2,1,0:T(8,128)(2,1)S(1)}, bf16[2,96,768]{2,1,0:T(8,128)(2,1)S(1)}, u32[]{:S(2)}, u32[]{:S(2)}) %collective-permute-start.3) | collective-permute-done | bytes 294944 | tf_op jit(solution)/shard_map/ppermute | solution.py:58
  57.1 9.7 %collective-permute-done.27.rest_2_ = bf16[4,96,768]{2,1,0:T(8,128)(2,1)S(1)} collective-permute-done((bf16[4,96,768]{2,1,0:T(8,128)(2,1)S(1)}, bf16[4,96,768]{2,1,0:T(8,128)(2,1)S(1)}, u32[]{:S(2)}, u32[]{:S(2)}) %collective-permute-start.27) | collective-permute-done | bytes 589856 | tf_op jit(solution)/shard_map/ppermute | solution.py:58
  74.7 1.8 collective-permute-done.5.rest_2_.rest_12_
  77.7 1.6 collective-permute-start.18
  80.7 2.9 collective-permute-done.4.rest_1_.rest_11_
  85.3 4.7 %collective-permute-done.17.rest_3_ = bf16[2,96,768]{2,1,0:T(8,128)(2,1)} collective-permute-done((bf16[2,96,768]{2,1,0:T(8,128)(2,1)S(1)}, bf16[2,96,768]{2,1,0:T(8,128)(2,1)}, u32[]{:S(2)}, u32[]{:S(2)}) %collective-permute-start.17) | collective-permute-done | bytes 294944 | tf_op jit(solution)/shard_map/ppermute | solution.py:58
  90.1 1.5 collective-permute-start.7
  91.6 4.7 %collective-permute-done.28.rest_3_ = bf16[2,96,768]{2,1,0:T(8,128)(2,1)S(1)} collective-permute-done((bf16[2,96,768]{2,1,0:T(8,128)(2,1)S(1)}, bf16[2,96,768]{2,1,0:T(8,128)(2,1)S(1)}, u32[]{:S(2)}, u32[]{:S(2)}) %collective-permute-start.28) | collective-permute-done | bytes 294944 | tf_op jit(solution)/shard_map/ppermute | solution.py:58
  97.7 4.5 %collective-permute-done.6.rest_3_.rest_13_ = bf16[2,96,768]{2,1,0:T(8,128)(2,1)} collective-permute-done((bf16[2,96,768]{2,1,0:T(8,128)(2,1)S(1)}, bf16[2,96,768]{2,1,0:T(8,128)(2,1)}, u32[]{:S(2)}, u32[]{:S(2)}) %collective-permute-start.6) | collective-permute-done | bytes 294944 | tf_op jit(solution)/shard_map/ppermute | solution.py:58
  111.8 1.5 copy.106.k_seg
  113.3 1.4 stack.53.vecs
  121.6 20.4 %attn_forward.1 = (bf16[4,512,640]{2,1,0:T(8,128)(2,1)}, f32[4,8,512]{2,1,0:T(8,128)}, bf16[768,512]{1,0:T(8,128)(2,1)}, bf16[4,512,256]{2,1,0:T(8,128)(2,1)}, f...) custom-call(s32[1]{0:T(128)} %bitcast.dp_ref, ...), custom_call_target="tpu_custom_call" | custom-call | flops 9663676416 | bytes 14155776 | tf_op jit(solution)/shard_map/attn_forward/pallas_call | solution.py:169
  143.2 13.6 %up_forward.1 = (bf16[4,512,768]{2,1,0:T(8,128)(2,1)}, f32[4,512,768]{2,1,0:T(8,128)}, f32[8,128]{1,0:T(8,128)}) custom-call(s32[1]{0:T(128)} %bitcast.dp_ref, f32[8]{0:T(128)} %pad_maximum_fusion.17.lim, bf16[512,768]{1,0:T(8,128)(2,1)} %get-tuple-element.43.mid_low, f32[4,1,768]{2,1,0:T(1,128)} %broadcast_in_dim.72.up_bias, ...), custom_call_target="tpu_custom_call" | custom-call | flops 4831838208 | bytes 14155776 | tf_op jit(solution)/shard_map/up_forward/pallas_call | solution.py:169
  158.3 11.5 %down_forward.1 = (bf16[512,768]{1,0:T(8,128)(2,1)}, f32[512,768]{1,0:T(8,128)}, bf16[512,768]{1,0:T(8,128)(2,1)}, bf16[768,512]{1,0:T(8,128)(2,1)}, f32[8,768]{1,0:T(8,128)}) custom-call(s32[1]{0:T(128)} %bitcast.dp_ref, bf16[4,512,768]{2,1,0:T(8,128)(2,1)} %get-tuple-element.44.act.right, f32[512,768]{1,0:T(8,128)} %get-tuple-element.45.middle, ...), custom_call_target="tpu_custom_call" | custom-call | flops 2415919104 | bytes 9437184 | tf_op jit(solution)/shard_map/down_forward/pallas_call | solution.py:169
  169.9 10.7 %act_backward.1 = (bf16[4,512,768]{2,1,0:T(8,128)(2,1)}, f32[4,1,768]{2,1,0:T(1,128)}) custom-call(s32[1]{0:T(128)} %bitcast.dp_ref, bf16[512,768]{1,0:T(8,128)(2,1)} %get-tuple-element.49.ffn_low, f32[4,512,768]{2,1,0:T(8,128)} %get-tuple-element.50.slope, bf16[4,96,768]{2,1,0:T(8,128)(2,1)} %copy-done.2, bf16[4,96,768]{2,1,0:T(8,128)(2,1)} %copy-done.5, ...), custom_call_target="tpu_custom_call" | custom-call | flops 2415919104 | bytes 14155776 | tf_op jit(solution)/shard_map/act_backward/pallas_call | solution.py:169
  181.3 14.9 %mid_backward.1 = (f32[512,768]{1,0:T(8,128)}, bf16[768,512]{1,0:T(8,128)(2,1)}, bf16[4,512,256]{2,1,0:T(8,128)(2,1)}, f32[8,768]{1,0:T(8,128)}) custom-call(s32[1]{0:T(128)} %bitcast.dp_ref, bf16[4,512,768]{2,1,0:T(8,128)(2,1)} %get-tuple-element.51.grad_up.right, f32[512,768]{1,0:T(8,128)} %get-tuple-element.52.grad_second, ...), custom_call_target="tpu_custom_call" | custom-call | flops 3221225472 | bytes 14155776 | tf_op jit(solution)/shard_map/mid_backward/pallas_call | solution.py:169
  196.3 14.4 %attn_backward.1 = (bf16[4,512,640]{2,1,0:T(8,128)(2,1)}, f32[4,1,640]{2,1,0:T(1,128)}) custom-call(bf16[4,512,640]{2,1,0:T(8,128)(2,1)} %get-tuple-element.47.qkv, f32[4,8,512]{2,1,0:T(8,128)} %get-tuple-element.48.lse, bf16[4,512,256]{2,1,0:T(8,128)(2,1)} %get-tuple-element.57.grad_ctx, s32[1,512]{1,0:T(1,128)} %get-tuple-element.166.q_seg, ...), custom_call_target="tpu_custom_call" | custom-call | flops 9663676416 | bytes 9437184 | tf_op jit(solution)/shard_map/attn_backward/pallas_call | solution.py:169
  212.4 5.1 %up_grad_far.1 = bf16[2,8,96,768]{3,2,1,0:T(8,128)(2,1)} custom-call(s32[1]{0:T(128)} %bitcast.dp_ref, bf16[768,512]{1,0:T(8,128)(2,1)} %get-tuple-element.69.left_t, bf16[4,512,768]{2,1,0:T(8,128)(2,1)} %get-tuple-element.51.grad_up.right), custom_call_target="tpu_custom_call" | custom-call | flops 1207959552 | bytes 4718592 | tf_op jit(solution)/shard_map/up_grad_far/pallas_call | solution.py:169
  217.5 5.1 %down_grad_far.1 = bf16[2,8,96,768]{3,2,1,0:T(8,128)(2,1)} custom-call(s32[1]{0:T(128)} %bitcast.dp_ref, bf16[768,512]{1,0:T(8,128)(2,1)} %get-tuple-element.70.left_t, bf16[4,512,768]{2,1,0:T(8,128)(2,1)} %get-tuple-element.44.act.right), custom_call_target="tpu_custom_call" | custom-call | flops 1207959552 | bytes 4718592 | tf_op jit(solution)/shard_map/down_grad_far/pallas_call | solution.py:169
  223.2 5.9 %in_grad_far.1 = bf16[2,8,96,768]{3,2,1,0:T(8,128)(2,1)} custom-call(s32[1]{0:T(128)} %bitcast.dp_ref, bf16[768,512]{1,0:T(8,128)(2,1)} %get-tuple-element.60.in_t, bf16[768,512]{1,0:T(8,128)(2,1)} %get-tuple-element.61.attn_t, bf16[4,512,640]{2,1,0:T(8,128)(2,1)} %get-tuple-element.58.grad_qkv, bf16[4,512,256]{2,1,0:T(8,128)(2,1)} %get-tuple-element.62.ctx_low), custom_call_target="tpu_custom_call" | custom-call | flops 1207959552 | bytes 4718592 | tf_op jit(solution)/shard_map/in_grad_far/pallas_call | solution.py:169
  230.6 9.2 %token_backward.1 = bf16[512,768]{1,0:T(8,128)(2,1)} custom-call(s32[1]{0:T(128)} %bitcast.dp_ref, f32[8]{0:T(128)} %pad_maximum_fusion.17.lim, bf16[4,512,640]{2,1,0:T(8,128)(2,1)} %get-tuple-element.58.grad_qkv, f32[512,768]{1,0:T(8,128)} %get-tuple-element.59.grad_first, bf16[512,768]{1,0:T(8,128)(2,1)} %tokens.3, bf16[4,96,768]{2,1,0:T(8,128)(2,1)} %copy-done.3, ...), custom_call_target="tpu_custom_call" | custom-call | flops 2415919104 | bytes 9437184 | tf_op jit(solution)/shard_map/token_backward/pallas_call | solution.py:169
  241.2 5.9 %in_grad_near.1 = bf16[2,8,96,768]{3,2,1,0:T(8,128)(2,1)} custom-call(s32[1]{0:T(128)} %bitcast.dp_ref, bf16[768,512]{1,0:T(8,128)(2,1)} %get-tuple-element.60.in_t, bf16[768,512]{1,0:T(8,128)(2,1)} %get-tuple-element.61.attn_t, bf16[4,512,640]{2,1,0:T(8,128)(2,1)} %get-tuple-element.58.grad_qkv, bf16[4,512,256]{2,1,0:T(8,128)(2,1)} %get-tuple-element.62.ctx_low), custom_call_target="tpu_custom_call" | custom-call | flops 1207959552 | bytes 4718592 | tf_op jit(solution)/shard_map/in_grad_near/pallas_call | solution.py:169
  247.2 5.2 %up_grad_near.1 = bf16[2,8,96,768]{3,2,1,0:T(8,128)(2,1)} custom-call(s32[1]{0:T(128)} %bitcast.dp_ref, bf16[768,512]{1,0:T(8,128)(2,1)} %get-tuple-element.69.left_t, bf16[4,512,768]{2,1,0:T(8,128)(2,1)} %get-tuple-element.51.grad_up.right), custom_call_target="tpu_custom_call" | custom-call | flops 1207959552 | bytes 4718592 | tf_op jit(solution)/shard_map/up_grad_near/pallas_call | solution.py:169
  252.5 2.3 collective-permute-start.46
  254.8 5.3 %down_grad_near.1 = bf16[2,8,96,768]{3,2,1,0:T(8,128)(2,1)} custom-call(s32[1]{0:T(128)} %bitcast.dp_ref, bf16[768,512]{1,0:T(8,128)(2,1)} %get-tuple-element.70.left_t, bf16[4,512,768]{2,1,0:T(8,128)(2,1)} %get-tuple-element.44.act.right), custom_call_target="tpu_custom_call" | custom-call | flops 1207959552 | bytes 4718592 | tf_op jit(solution)/shard_map/down_grad_near/pallas_call | solution.py:169
  261.5 1.9 fusion.20
  263.4 1.6 collective-permute-start.57
  265.5 1.5 fusion.16
  267.7 1.4 collective-permute-start.48
  269.1 1.5 fusion.12
  270.6 1.6 collective-permute-start.38
  274.8 1.5 fusion.7
  277.8 1.8 collective-permute-done.50
  279.6 1.5 collective-permute-start.56
  286.0 1.5 collective-permute-start.49
  291.0 9.1 %collective-permute-done.58 = bf16[4,96,768]{2,1,0:T(8,128)(2,1)S(1)} collective-permute-done((bf16[4,96,768]{2,1,0:T(8,128)(2,1)S(1)}, bf16[4,96,768]{2,1,0:T(8,128)(2,1)S(1)}, u32[]{:S(2)}, u32[]{:S(2)}) %collective-permute-start.58) | collective-permute-done | bytes 589856 | tf_op jit(solution)/shard_map/ppermute | solution.py:58
  303.4 9.4 %collective-permute-done.51 = bf16[4,96,768]{2,1,0:T(8,128)(2,1)} collective-permute-done((bf16[4,96,768]{2,1,0:T(8,128)(2,1)}, bf16[4,96,768]{2,1,0:T(8,128)(2,1)}, u32[]{:S(2)}, u32[]{:S(2)}) %collective-permute-start.51) | collective-permute-done | bytes 589856 | tf_op jit(solution)/shard_map/ppermute | solution.py:58
  317.0 6.2 %collective-permute-done.39 = bf16[4,96,768]{2,1,0:T(8,128)(2,1)} collective-permute-done((bf16[4,96,768]{2,1,0:T(8,128)(2,1)}, bf16[4,96,768]{2,1,0:T(8,128)(2,1)}, u32[]{:S(2)}, u32[]{:S(2)}) %collective-permute-start.39) | collective-permute-done | bytes 589856 | tf_op jit(solution)/shard_map/ppermute | solution.py:58
  329.0 1.8 collective-permute-start.60
  332.2 8.6 %collective-permute-done.40 = bf16[2,96,768]{2,1,0:T(8,128)(2,1)S(1)} collective-permute-done((bf16[2,96,768]{2,1,0:T(8,128)(2,1)S(1)}, bf16[2,96,768]{2,1,0:T(8,128)(2,1)S(1)}, u32[]{:S(2)}, u32[]{:S(2)}) %collective-permute-start.40) | collective-permute-done | bytes 294944 | tf_op jit(solution)/shard_map/ppermute | solution.py:58
  342.9 4.9 %collective-permute-done.41 = bf16[96,768]{1,0:T(8,128)(2,1)S(1)} collective-permute-done((bf16[96,768]{1,0:T(8,128)(2,1)S(1)}, bf16[96,768]{1,0:T(8,128)(2,1)S(1)}, u32[]{:S(2)}, u32[]{:S(2)}) %collective-permute-start.41) | collective-permute-done | bytes 147488 | tf_op jit(solution)/shard_map/ppermute | solution.py:58
  (255 shorter events, 83.0 us)
Async XLA Ops:
  9.3 31.3 %collective-permute-start.25 = (bf16[2,96,768]{2,1,0:T(8,128)(2,1)S(1)}, bf16[2,96,768]{2,1,0:T(8,128)(2,1)S(1)}, u32[]{:S(2)}, u32[]{:S(2)}) collective-permute-start(bf16[2,96,768]{2,1,0:T(8,128)(2,1)S(1)} %pad_maximum_fusion.11), channel_id=1, source_target_pairs={{0,16},{1,17},{2,18},{3,19},{4,20},{5,21},{6,22},{7,23},{8,24},{9,... | collective-permute-start | bytes 884744 | tf_op jit(solution)/shard_map/ppermute | solution.py:58
  13.7 23.1 %collective-permute-start.14 = (bf16[2,96,768]{2,1,0:T(8,128)(2,1)S(1)}, bf16[2,96,768]{2,1,0:T(8,128)(2,1)S(1)}, u32[]{:S(2)}, u32[]{:S(2)}) collective-permute-start(bf16[2,96,768]{2,1,0:T(8,128)(2,1)S(1)} %pad_maximum_fusion.10), channel_id=1, source_target_pairs={{0,16},{1,17},{2,18},{3,19},{4,20},{5,21},{6,22},{7,23},{8,24},{9,... | collective-permute-start | bytes 884744 | tf_op jit(solution)/shard_map/ppermute | solution.py:58
  15.7 25.6 %collective-permute-start.2 = (bf16[1,96,768]{2,1,0:T(8,128)(2,1)S(1)}, bf16[1,96,768]{2,1,0:T(8,128)(2,1)S(1)}, u32[]{:S(2)}, u32[]{:S(2)}) collective-permute-start(bf16[1,96,768]{2,1,0:T(8,128)(2,1)S(1)} %pad_maximum_fusion.13), channel_id=1, source_target_pairs={{0,8},{1,9},{2,10},{3,11},{4,12},{5,13},{6,14},{7,15},{8,0},{9,1},... | collective-permute-start | bytes 442376 | tf_op jit(solution)/shard_map/ppermute | solution.py:58
  37.7 18.0 %collective-permute-start.16 = (bf16[4,96,768]{2,1,0:T(8,128)(2,1)}, bf16[4,96,768]{2,1,0:T(8,128)(2,1)}, u32[]{:S(2)}, u32[]{:S(2)}) collective-permute-start(bf16[4,96,768]{2,1,0:T(8,128)(2,1)} %pad_maximum_fusion.1.rest_0_), channel_id=1, source_target_pairs={{0,4},{1,5},{2,6},{3,7},{4,0},{5,1},{6,2},{7,3},{8,12},{9,13},{10,... | collective-permute-start | bytes 1769480 | tf_op jit(solution)/shard_map/ppermute | solution.py:58
  39.1 16.8 %collective-permute-start.15 = (bf16[4,96,768]{2,1,0:T(8,128)(2,1)}, bf16[4,96,768]{2,1,0:T(8,128)(2,1)}, u32[]{:S(2)}, u32[]{:S(2)}) collective-permute-start(bf16[4,96,768]{2,1,0:T(8,128)(2,1)} %pad_maximum_fusion.1.rest_0_), channel_id=1, source_target_pairs={{0,2},{1,3},{2,0},{3,1},{4,6},{5,7},{6,4},{7,5},{8,10},{9,11},{10,... | collective-permute-start | bytes 1769480 | tf_op jit(solution)/shard_map/ppermute | solution.py:58
  40.7 26.1 %collective-permute-start.27 = (bf16[4,96,768]{2,1,0:T(8,128)(2,1)S(1)}, bf16[4,96,768]{2,1,0:T(8,128)(2,1)S(1)}, u32[]{:S(2)}, u32[]{:S(2)}) collective-permute-start(bf16[4,96,768]{2,1,0:T(8,128)(2,1)S(1)} %pad_maximum_fusion.2.rest_0_), channel_id=1, source_target_pairs={{0,4},{1,5},{2,6},{3,7},{4,0},{5,1},{6,2},{7,3},{8,12},{9,13},{10,... | collective-permute-start | bytes 1769480 | tf_op jit(solution)/shard_map/ppermute | solution.py:58
  41.4 13.2 %collective-permute-start.3 = (bf16[2,96,768]{2,1,0:T(8,128)(2,1)S(1)}, bf16[2,96,768]{2,1,0:T(8,128)(2,1)S(1)}, u32[]{:S(2)}, u32[]{:S(2)}) collective-permute-start(bf16[2,96,768]{2,1,0:T(8,128)(2,1)S(1)} %pad_maximum_fusion.9), channel_id=1, source_target_pairs={{0,16},{1,17},{2,18},{3,19},{4,20},{5,21},{6,22},{7,23},{8,24},{9,... | collective-permute-start | bytes 884744 | tf_op jit(solution)/shard_map/ppermute | solution.py:58
  41.6 13.1 %collective-permute-start = (f32[1152]{0:T(1024)S(1)}, f32[1152]{0:T(1024)S(1)}, u32[]{:S(2)}, u32[]{:S(2)}) collective-permute-start(f32[1152]{0:T(1024)S(1)} %concatenate.91), channel_id=1, source_target_pairs={{0,2},{1,3},{2,0},{3,1},{4,6},{5,7},{6,4},{7,5},{8,10},{9,11},{10,... | collective-permute-start | bytes 13832 | tf_op jit(solution)/shard_map/ppermute | solution.py:58
  54.6 24.7 %collective-permute-start.19 = (bf16[4,96,768]{2,1,0:T(8,128)(2,1)}, bf16[4,96,768]{2,1,0:T(8,128)(2,1)}, u32[]{:S(2)}, u32[]{:S(2)}) collective-permute-start(bf16[4,96,768]{2,1,0:T(8,128)(2,1)} %pad_maximum_fusion.1.rest_0_), channel_id=1, source_target_pairs={{0,1},{1,0},{2,3},{3,2},{4,5},{5,4},{6,7},{7,6},{8,9},{9,8},{10,11... | collective-permute-start | bytes 1769480 | tf_op jit(solution)/shard_map/ppermute | solution.py:58
  54.7 16.7 %collective-permute-start.26 = (bf16[4,96,768]{2,1,0:T(8,128)(2,1)S(1)}, bf16[4,96,768]{2,1,0:T(8,128)(2,1)S(1)}, u32[]{:S(2)}, u32[]{:S(2)}) collective-permute-start(bf16[4,96,768]{2,1,0:T(8,128)(2,1)S(1)} %pad_maximum_fusion.2.rest_0_), channel_id=1, source_target_pairs={{0,2},{1,3},{2,0},{3,1},{4,6},{5,7},{6,4},{7,5},{8,10},{9,11},{10,... | collective-permute-start | bytes 1769480 | tf_op jit(solution)/shard_map/ppermute | solution.py:58
  55.7 24.1 %collective-permute-start.8 = (bf16[4,96,768]{2,1,0:T(8,128)(2,1)S(1)}, bf16[4,96,768]{2,1,0:T(8,128)(2,1)}, u32[]{:S(2)}, u32[]{:S(2)}) collective-permute-start(bf16[4,96,768]{2,1,0:T(8,128)(2,1)S(1)} %pad_maximum_fusion.rest_0_.rest_10_), channel_id=1, source_target_pairs={{0,1},{1,0},{2,3},{3,2},{4,5},{5,4},{6,7},{7,6},{8,9},{9,8},{10,11... | collective-permute-start | bytes 1769480 | tf_op jit(solution)/shard_map/ppermute | solution.py:58
  56.0 20.6 %collective-permute-start.5 = (bf16[4,96,768]{2,1,0:T(8,128)(2,1)S(1)}, bf16[4,96,768]{2,1,0:T(8,128)(2,1)S(1)}, u32[]{:S(2)}, u32[]{:S(2)}) collective-permute-start(bf16[4,96,768]{2,1,0:T(8,128)(2,1)S(1)} %pad_maximum_fusion.rest_0_.rest_10_), channel_id=1, source_target_pairs={{0,4},{1,5},{2,6},{3,7},{4,0},{5,1},{6,2},{7,3},{8,12},{9,13},{10,... | collective-permute-start | bytes 1769480 | tf_op jit(solution)/shard_map/ppermute | solution.py:58
  66.8 16.9 %collective-permute-start.4 = (bf16[4,96,768]{2,1,0:T(8,128)(2,1)S(1)}, bf16[4,96,768]{2,1,0:T(8,128)(2,1)S(1)}, u32[]{:S(2)}, u32[]{:S(2)}) collective-permute-start(bf16[4,96,768]{2,1,0:T(8,128)(2,1)S(1)} %pad_maximum_fusion.rest_0_.rest_10_), channel_id=1, source_target_pairs={{0,2},{1,3},{2,0},{3,1},{4,6},{5,7},{6,4},{7,5},{8,10},{9,11},{10,... | collective-permute-start | bytes 1769480 | tf_op jit(solution)/shard_map/ppermute | solution.py:58
  76.6 13.5 %collective-permute-start.17 = (bf16[2,96,768]{2,1,0:T(8,128)(2,1)S(1)}, bf16[2,96,768]{2,1,0:T(8,128)(2,1)}, u32[]{:S(2)}, u32[]{:S(2)}) collective-permute-start(bf16[2,96,768]{2,1,0:T(8,128)(2,1)S(1)} %slice.425), channel_id=1, source_target_pairs={{0,2},{1,3},{2,0},{3,1},{4,6},{5,7},{6,4},{7,5},{8,10},{9,11},{10,... | collective-permute-start | bytes 884744 | tf_op jit(solution)/shard_map/ppermute | solution.py:58
  77.7 13.9 %collective-permute-start.18 = (bf16[2,96,768]{2,1,0:T(8,128)(2,1)S(1)}, bf16[2,96,768]{2,1,0:T(8,128)(2,1)S(1)}, u32[]{:S(2)}, u32[]{:S(2)}) collective-permute-start(bf16[2,96,768]{2,1,0:T(8,128)(2,1)S(1)} %slice.426), channel_id=1, source_target_pairs={{0,4},{1,5},{2,6},{3,7},{4,0},{5,1},{6,2},{7,3},{8,12},{9,13},{10,... | collective-permute-start | bytes 884744 | tf_op jit(solution)/shard_map/ppermute | solution.py:58
  79.3 17.0 %collective-permute-start.28 = (bf16[2,96,768]{2,1,0:T(8,128)(2,1)S(1)}, bf16[2,96,768]{2,1,0:T(8,128)(2,1)S(1)}, u32[]{:S(2)}, u32[]{:S(2)}) collective-permute-start(bf16[2,96,768]{2,1,0:T(8,128)(2,1)S(1)} %slice.427), channel_id=1, source_target_pairs={{0,2},{1,3},{2,0},{3,1},{4,6},{5,7},{6,4},{7,5},{8,10},{9,11},{10,... | collective-permute-start | bytes 884744 | tf_op jit(solution)/shard_map/ppermute | solution.py:58
  79.8 17.2 %collective-permute-start.29 = (bf16[2,96,768]{2,1,0:T(8,128)(2,1)S(1)}, bf16[2,96,768]{2,1,0:T(8,128)(2,1)S(1)}, u32[]{:S(2)}, u32[]{:S(2)}) collective-permute-start(bf16[2,96,768]{2,1,0:T(8,128)(2,1)S(1)} %slice.428), channel_id=1, source_target_pairs={{0,4},{1,5},{2,6},{3,7},{4,0},{5,1},{6,2},{7,3},{8,12},{9,13},{10,... | collective-permute-start | bytes 884744 | tf_op jit(solution)/shard_map/ppermute | solution.py:58
  83.6 18.6 %collective-permute-start.6 = (bf16[2,96,768]{2,1,0:T(8,128)(2,1)S(1)}, bf16[2,96,768]{2,1,0:T(8,128)(2,1)}, u32[]{:S(2)}, u32[]{:S(2)}) collective-permute-start(bf16[2,96,768]{2,1,0:T(8,128)(2,1)S(1)} %slice.423), channel_id=1, source_target_pairs={{0,2},{1,3},{2,0},{3,1},{4,6},{5,7},{6,4},{7,5},{8,10},{9,11},{10,... | collective-permute-start | bytes 884744 | tf_op jit(solution)/shard_map/ppermute | solution.py:58
  90.1 26.5 %collective-permute-start.7 = (bf16[2,96,768]{2,1,0:T(8,128)(2,1)}, bf16[2,96,768]{2,1,0:T(8,128)(2,1)}, u32[]{:S(2)}, u32[]{:S(2)}) collective-permute-start(bf16[2,96,768]{2,1,0:T(8,128)(2,1)} %slice.424), channel_id=1, source_target_pairs={{0,4},{1,5},{2,6},{3,7},{4,0},{5,1},{6,2},{7,3},{8,12},{9,13},{10,... | collective-permute-start | bytes 884744 | tf_op jit(solution)/shard_map/ppermute | solution.py:58
  91.6 28.3 %collective-permute-start.21 = (bf16[4,96,768]{2,1,0:T(8,128)(2,1)}, bf16[4,96,768]{2,1,0:T(8,128)(2,1)}, u32[]{:S(2)}, u32[]{:S(2)}) collective-permute-start(bf16[4,96,768]{2,1,0:T(8,128)(2,1)} %collective-permute-done.16.rest_2_), channel_id=1, source_target_pairs={{0,1},{1,0},{2,3},{3,2},{4,5},{5,4},{6,7},{7,6},{8,9},{9,8},{10,11... | collective-permute-start | bytes 1769480 | tf_op jit(solution)/shard_map/ppermute | solution.py:58
  96.3 24.1 %collective-permute-start.10 = (bf16[4,96,768]{2,1,0:T(8,128)(2,1)S(1)}, bf16[4,96,768]{2,1,0:T(8,128)(2,1)}, u32[]{:S(2)}, u32[]{:S(2)}) collective-permute-start(bf16[4,96,768]{2,1,0:T(8,128)(2,1)S(1)} %collective-permute-done.5.rest_2_.rest_12_), channel_id=1, source_target_pairs={{0,1},{1,0},{2,3},{3,2},{4,5},{5,4},{6,7},{7,6},{8,9},{9,8},{10,11... | collective-permute-start | bytes 1769480 | tf_op jit(solution)/shard_map/ppermute | solution.py:58
  97.7 23.2 %collective-permute-start.9 = (bf16[4,96,768]{2,1,0:T(8,128)(2,1)S(1)}, bf16[4,96,768]{2,1,0:T(8,128)(2,1)}, u32[]{:S(2)}, u32[]{:S(2)}) collective-permute-start(bf16[4,96,768]{2,1,0:T(8,128)(2,1)S(1)} %collective-permute-done.4.rest_1_.rest_11_), channel_id=1, source_target_pairs={{0,1},{1,0},{2,3},{3,2},{4,5},{5,4},{6,7},{7,6},{8,9},{9,8},{10,11... | collective-permute-start | bytes 1769480 | tf_op jit(solution)/shard_map/ppermute | solution.py:58
  102.2 14.8 %collective-permute-start.22 = (bf16[2,96,768]{2,1,0:T(8,128)(2,1)}, bf16[2,96,768]{2,1,0:T(8,128)(2,1)}, u32[]{:S(2)}, u32[]{:S(2)}) collective-permute-start(bf16[2,96,768]{2,1,0:T(8,128)(2,1)} %collective-permute-done.17.rest_3_), channel_id=1, source_target_pairs={{0,1},{1,0},{2,3},{3,2},{4,5},{5,4},{6,7},{7,6},{8,9},{9,8},{10,11... | collective-permute-start | bytes 884744 | tf_op jit(solution)/shard_map/ppermute | solution.py:58
  119.9 37.6 %collective-permute-start.30 = (bf16[4,96,768]{2,1,0:T(8,128)(2,1)S(1)}, bf16[4,96,768]{2,1,0:T(8,128)(2,1)}, u32[]{:S(2)}, u32[]{:S(2)}) collective-permute-start(bf16[4,96,768]{2,1,0:T(8,128)(2,1)S(1)} %pad_maximum_fusion.2.rest_0_), channel_id=1, source_target_pairs={{0,1},{1,0},{2,3},{3,2},{4,5},{5,4},{6,7},{7,6},{8,9},{9,8},{10,11... | collective-permute-start | bytes 1769480 | tf_op jit(solution)/shard_map/ppermute | solution.py:58
  120.3 22.4 %collective-permute-start.20 = (bf16[4,96,768]{2,1,0:T(8,128)(2,1)}, bf16[4,96,768]{2,1,0:T(8,128)(2,1)}, u32[]{:S(2)}, u32[]{:S(2)}) collective-permute-start(bf16[4,96,768]{2,1,0:T(8,128)(2,1)} %collective-permute-done.15.rest_1_), channel_id=1, source_target_pairs={{0,1},{1,0},{2,3},{3,2},{4,5},{5,4},{6,7},{7,6},{8,9},{9,8},{10,11... | collective-permute-start | bytes 1769480 | tf_op jit(solution)/shard_map/ppermute | solution.py:58
  120.4 37.1 %collective-permute-start.32 = (bf16[4,96,768]{2,1,0:T(8,128)(2,1)S(1)}, bf16[4,96,768]{2,1,0:T(8,128)(2,1)}, u32[]{:S(2)}, u32[]{:S(2)}) collective-permute-start(bf16[4,96,768]{2,1,0:T(8,128)(2,1)S(1)} %collective-permute-done.27.rest_2_), channel_id=1, source_target_pairs={{0,1},{1,0},{2,3},{3,2},{4,5},{5,4},{6,7},{7,6},{8,9},{9,8},{10,11... | collective-permute-start | bytes 1769480 | tf_op jit(solution)/shard_map/ppermute | solution.py:58
  120.8 36.7 %collective-permute-start.31 = (bf16[4,96,768]{2,1,0:T(8,128)(2,1)S(1)}, bf16[4,96,768]{2,1,0:T(8,128)(2,1)}, u32[]{:S(2)}, u32[]{:S(2)}) collective-permute-start(bf16[4,96,768]{2,1,0:T(8,128)(2,1)S(1)} %collective-permute-done.26.rest_1_), channel_id=1, source_target_pairs={{0,1},{1,0},{2,3},{3,2},{4,5},{5,4},{6,7},{7,6},{8,9},{9,8},{10,11... | collective-permute-start | bytes 1769480 | tf_op jit(solution)/shard_map/ppermute | solution.py:58
  120.9 21.7 %collective-permute-start.23 = (bf16[2,96,768]{2,1,0:T(8,128)(2,1)}, bf16[2,96,768]{2,1,0:T(8,128)(2,1)}, u32[]{:S(2)}, u32[]{:S(2)}) collective-permute-start(bf16[2,96,768]{2,1,0:T(8,128)(2,1)} %copy-done.15), channel_id=1, source_target_pairs={{0,1},{1,0},{2,3},{3,2},{4,5},{5,4},{6,7},{7,6},{8,9},{9,8},{10,11... | collective-permute-start | bytes 884744 | tf_op jit(solution)/shard_map/ppermute | solution.py:58
  142.7 14.8 %collective-permute-start.33 = (bf16[2,96,768]{2,1,0:T(8,128)(2,1)S(1)}, bf16[2,96,768]{2,1,0:T(8,128)(2,1)S(1)}, u32[]{:S(2)}, u32[]{:S(2)}) collective-permute-start(bf16[2,96,768]{2,1,0:T(8,128)(2,1)S(1)} %copy-done.9), channel_id=1, source_target_pairs={{0,1},{1,0},{2,3},{3,2},{4,5},{5,4},{6,7},{7,6},{8,9},{9,8},{10,11... | collective-permute-start | bytes 884744 | tf_op jit(solution)/shard_map/ppermute | solution.py:58
  142.8 14.7 %collective-permute-start.34 = (bf16[2,96,768]{2,1,0:T(8,128)(2,1)}, bf16[2,96,768]{2,1,0:T(8,128)(2,1)S(1)}, u32[]{:S(2)}, u32[]{:S(2)}) collective-permute-start(bf16[2,96,768]{2,1,0:T(8,128)(2,1)} %copy-done.10), channel_id=1, source_target_pairs={{0,1},{1,0},{2,3},{3,2},{4,5},{5,4},{6,7},{7,6},{8,9},{9,8},{10,11... | collective-permute-start | bytes 884744 | tf_op jit(solution)/shard_map/ppermute | solution.py:58
  212.2 17.3 %collective-permute-start.42 = (f32[76,128]{1,0:T(8,128)S(1)}, f32[76,128]{1,0:T(8,128)S(1)}, u32[]{:S(2)}, u32[]{:S(2)}) collective-permute-start(f32[76,128]{1,0:T(8,128)S(1)} %concatenate.110), channel_id=1, source_target_pairs={{0,1},{1,0},{2,3},{3,2},{4,5},{5,4},{6,7},{7,6},{8,9},{9,8},{10,11... | collective-permute-start | bytes 116744 | tf_op jit(solution)/shard_map/ppermute | solution.py:58
  222.7 38.8 %collective-permute-start.54 = (bf16[2,8,96,768]{3,2,1,0:T(8,128)(2,1)}, bf16[2,8,96,768]{3,2,1,0:T(8,128)(2,1)}, u32[]{:S(2)}, u32[]{:S(2)}) collective-permute-start(bf16[2,8,96,768]{3,2,1,0:T(8,128)(2,1)} %down_grad_far.1), channel_id=1, source_target_pairs={{0,1},{1,0},{2,3},{3,2},{4,5},{5,4},{6,7},{7,6},{8,9},{9,8},{10,11... | collective-permute-start | bytes 7077896 | tf_op jit(solution)/shard_map/ppermute | solution.py:58
  223.1 42.4 %collective-permute-start.47 = (bf16[2,8,96,768]{3,2,1,0:T(8,128)(2,1)}, bf16[2,8,96,768]{3,2,1,0:T(8,128)(2,1)}, u32[]{:S(2)}, u32[]{:S(2)}) collective-permute-start(bf16[2,8,96,768]{3,2,1,0:T(8,128)(2,1)} %up_grad_far.1), channel_id=1, source_target_pairs={{0,1},{1,0},{2,3},{3,2},{4,5},{5,4},{6,7},{7,6},{8,9},{9,8},{10,11... | collective-permute-start | bytes 7077896 | tf_op jit(solution)/shard_map/ppermute | solution.py:58
  229.1 40.0 %collective-permute-start.35 = (bf16[2,8,96,768]{3,2,1,0:T(8,128)(2,1)}, bf16[2,8,96,768]{3,2,1,0:T(8,128)(2,1)}, u32[]{:S(2)}, u32[]{:S(2)}) collective-permute-start(bf16[2,8,96,768]{3,2,1,0:T(8,128)(2,1)} %in_grad_far.1), channel_id=1, source_target_pairs={{0,1},{1,0},{2,3},{3,2},{4,5},{5,4},{6,7},{7,6},{8,9},{9,8},{10,11... | collective-permute-start | bytes 7077896 | tf_op jit(solution)/shard_map/ppermute | solution.py:58
  267.7 13.5 %collective-permute-start.48 = (bf16[2,96,768]{2,1,0:T(8,128)(2,1)S(1)}, bf16[2,96,768]{2,1,0:T(8,128)(2,1)S(1)}, u32[]{:S(2)}, u32[]{:S(2)}) collective-permute-start(bf16[2,96,768]{2,1,0:T(8,128)(2,1)S(1)} %get-tuple-element.142), channel_id=1, source_target_pairs={{0,4},{1,5},{2,6},{3,7},{4,0},{5,1},{6,2},{7,3},{8,12},{9,13},{10,... | collective-permute-start | bytes 884744 | tf_op jit(solution)/shard_map/ppermute | solution.py:58
  270.6 15.3 %collective-permute-start.38 = (bf16[2,96,768]{2,1,0:T(8,128)(2,1)S(1)}, bf16[2,96,768]{2,1,0:T(8,128)(2,1)S(1)}, u32[]{:S(2)}, u32[]{:S(2)}) collective-permute-start(bf16[2,96,768]{2,1,0:T(8,128)(2,1)S(1)} %get-tuple-element.147), channel_id=1, source_target_pairs={{0,2},{1,3},{2,0},{3,1},{4,6},{5,7},{6,4},{7,5},{8,10},{9,11},{10,... | collective-permute-start | bytes 884744 | tf_op jit(solution)/shard_map/ppermute | solution.py:58
  273.3 14.1 %collective-permute-start.36 = (bf16[2,96,768]{2,1,0:T(8,128)(2,1)S(1)}, bf16[2,96,768]{2,1,0:T(8,128)(2,1)S(1)}, u32[]{:S(2)}, u32[]{:S(2)}) collective-permute-start(bf16[2,96,768]{2,1,0:T(8,128)(2,1)S(1)} %get-tuple-element.148), channel_id=1, source_target_pairs={{0,4},{1,5},{2,6},{3,7},{4,0},{5,1},{6,2},{7,3},{8,12},{9,13},{10,... | collective-permute-start | bytes 884744 | tf_op jit(solution)/shard_map/ppermute | solution.py:58
  276.3 23.8 %collective-permute-start.58 = (bf16[4,96,768]{2,1,0:T(8,128)(2,1)S(1)}, bf16[4,96,768]{2,1,0:T(8,128)(2,1)S(1)}, u32[]{:S(2)}, u32[]{:S(2)}) collective-permute-start(bf16[4,96,768]{2,1,0:T(8,128)(2,1)S(1)} %pad_maximum_fusion.8), channel_id=1, source_target_pairs={{0,4},{1,5},{2,6},{3,7},{4,0},{5,1},{6,2},{7,3},{8,12},{9,13},{10,... | collective-permute-start | bytes 1769480 | tf_op jit(solution)/shard_map/ppermute | solution.py:58
  279.6 21.8 %collective-permute-start.56 = (bf16[4,96,768]{2,1,0:T(8,128)(2,1)}, bf16[4,96,768]{2,1,0:T(8,128)(2,1)S(1)}, u32[]{:S(2)}, u32[]{:S(2)}) collective-permute-start(bf16[4,96,768]{2,1,0:T(8,128)(2,1)} %pad_maximum_fusion.7), channel_id=1, source_target_pairs={{0,2},{1,3},{2,0},{3,1},{4,6},{5,7},{6,4},{7,5},{8,10},{9,11},{10,... | collective-permute-start | bytes 1769480 | tf_op jit(solution)/shard_map/ppermute | solution.py:58
  283.4 29.5 %collective-permute-start.51 = (bf16[4,96,768]{2,1,0:T(8,128)(2,1)}, bf16[4,96,768]{2,1,0:T(8,128)(2,1)}, u32[]{:S(2)}, u32[]{:S(2)}) collective-permute-start(bf16[4,96,768]{2,1,0:T(8,128)(2,1)} %pad_maximum_fusion.6), channel_id=1, source_target_pairs={{0,4},{1,5},{2,6},{3,7},{4,0},{5,1},{6,2},{7,3},{8,12},{9,13},{10,... | collective-permute-start | bytes 1769480 | tf_op jit(solution)/shard_map/ppermute | solution.py:58
  286.0 28.0 %collective-permute-start.49 = (bf16[4,96,768]{2,1,0:T(8,128)(2,1)}, bf16[4,96,768]{2,1,0:T(8,128)(2,1)}, u32[]{:S(2)}, u32[]{:S(2)}) collective-permute-start(bf16[4,96,768]{2,1,0:T(8,128)(2,1)} %pad_maximum_fusion.5), channel_id=1, source_target_pairs={{0,2},{1,3},{2,0},{3,1},{4,6},{5,7},{6,4},{7,5},{8,10},{9,11},{10,... | collective-permute-start | bytes 1769480 | tf_op jit(solution)/shard_map/ppermute | solution.py:58
  289.6 33.6 %collective-permute-start.39 = (bf16[4,96,768]{2,1,0:T(8,128)(2,1)}, bf16[4,96,768]{2,1,0:T(8,128)(2,1)}, u32[]{:S(2)}, u32[]{:S(2)}) collective-permute-start(bf16[4,96,768]{2,1,0:T(8,128)(2,1)} %pad_maximum_fusion.4), channel_id=1, source_target_pairs={{0,4},{1,5},{2,6},{3,7},{4,0},{5,1},{6,2},{7,3},{8,12},{9,13},{10,... | collective-permute-start | bytes 1769480 | tf_op jit(solution)/shard_map/ppermute | solution.py:58
  300.1 24.3 %collective-permute-start.37 = (bf16[4,96,768]{2,1,0:T(8,128)(2,1)}, bf16[4,96,768]{2,1,0:T(8,128)(2,1)}, u32[]{:S(2)}, u32[]{:S(2)}) collective-permute-start(bf16[4,96,768]{2,1,0:T(8,128)(2,1)} %pad_maximum_fusion.3), channel_id=1, source_target_pairs={{0,2},{1,3},{2,0},{3,1},{4,6},{5,7},{6,4},{7,5},{8,10},{9,11},{10,... | collective-permute-start | bytes 1769480 | tf_op jit(solution)/shard_map/ppermute | solution.py:58
  302.7 25.1 %collective-permute-start.59 = (bf16[2,96,768]{2,1,0:T(8,128)(2,1)S(1)}, bf16[2,96,768]{2,1,0:T(8,128)(2,1)S(1)}, u32[]{:S(2)}, u32[]{:S(2)}) collective-permute-start(bf16[2,96,768]{2,1,0:T(8,128)(2,1)S(1)} %fusion), channel_id=1, source_target_pairs={{0,16},{1,17},{2,18},{3,19},{4,20},{5,21},{6,22},{7,23},{8,24},{9,... | collective-permute-start | bytes 884744 | tf_op jit(solution)/shard_map/ppermute | solution.py:58
  316.3 14.5 %collective-permute-start.52 = (bf16[2,96,768]{2,1,0:T(8,128)(2,1)S(1)}, bf16[2,96,768]{2,1,0:T(8,128)(2,1)S(1)}, u32[]{:S(2)}, u32[]{:S(2)}) collective-permute-start(bf16[2,96,768]{2,1,0:T(8,128)(2,1)S(1)} %fusion.2), channel_id=1, source_target_pairs={{0,16},{1,17},{2,18},{3,19},{4,20},{5,21},{6,22},{7,23},{8,24},{9,... | collective-permute-start | bytes 884744 | tf_op jit(solution)/shard_map/ppermute | solution.py:58
  326.7 14.1 %collective-permute-start.40 = (bf16[2,96,768]{2,1,0:T(8,128)(2,1)S(1)}, bf16[2,96,768]{2,1,0:T(8,128)(2,1)S(1)}, u32[]{:S(2)}, u32[]{:S(2)}) collective-permute-start(bf16[2,96,768]{2,1,0:T(8,128)(2,1)S(1)} %fusion.4), channel_id=1, source_target_pairs={{0,16},{1,17},{2,18},{3,19},{4,20},{5,21},{6,22},{7,23},{8,24},{9,... | collective-permute-start | bytes 884744 | tf_op jit(solution)/shard_map/ppermute | solution.py:58
  329.0 13.2 %collective-permute-start.60 = (bf16[96,768]{1,0:T(8,128)(2,1)S(1)}, bf16[96,768]{1,0:T(8,128)(2,1)S(1)}, u32[]{:S(2)}, u32[]{:S(2)}) collective-permute-start(bf16[96,768]{1,0:T(8,128)(2,1)S(1)} %fusion.30), channel_id=1, source_target_pairs={{0,8},{1,9},{2,10},{3,11},{4,12},{5,13},{6,14},{7,15},{8,0},{9,1},... | collective-permute-start | bytes 442376 | tf_op jit(solution)/shard_map/ppermute | solution.py:58
  331.9 17.6 %collective-permute-start.53 = (bf16[96,768]{1,0:T(8,128)(2,1)S(1)}, bf16[96,768]{1,0:T(8,128)(2,1)S(1)}, u32[]{:S(2)}, u32[]{:S(2)}) collective-permute-start(bf16[96,768]{1,0:T(8,128)(2,1)S(1)} %fusion.29), channel_id=1, source_target_pairs={{0,8},{1,9},{2,10},{3,11},{4,12},{5,13},{6,14},{7,15},{8,0},{9,1},... | collective-permute-start | bytes 442376 | tf_op jit(solution)/shard_map/ppermute | solution.py:58
  (41 other events, 756.3 us)

commit v3 on v1

v3 whole, which is shorter than its diff:
```python
import functools
import itertools

import jax
import jax.numpy as jnp
from jax import lax
from jax.experimental import pallas as pl
from jax.experimental.pallas import tpu as pltpu
from jax.sharding import PartitionSpec as P

HEAD_DIM = 64
LONG_LEN = 512
SHORT_LEN = 128
ALL = ("dp", "tensor")

ema_decay = 0.9
epsilon = 1e-06
root_half = 0.7071067811865476
density_scale = 0.3989422804014327
score_scale = HEAD_DIM ** (-0.5)
NEG = -1000000000.0

f32 = jnp.float32
bf16 = jnp.bfloat16


def mm(left, right):
    return jnp.dot(left, right, preferred_element_type=f32)


def mm_tn(left, right):
    return lax.dot_general(left, right, (((0,), (0,)), ((), ())), preferred_element_type=f32)


def mm_nt(left, right):
    return lax.dot_general(left, right, (((1,), (1,)), ((), ())), preferred_element_type=f32)


def _lin(z, y, x, c):
    return (z * 2 + y) * 4 + x * 2 + c


def _perm(fn):
    out = []
    for z, y, x, c in itertools.product(range(4), range(2), range(2), range(2)):
        out.append((_lin(z, y, x, c), _lin(*fn(z, y, x, c))))
    return out


PC = _perm(lambda z, y, x, c: (z, y, x, 1 - c))
PX = _perm(lambda z, y, x, c: (z, y, 1 - x, c))
PY = _perm(lambda z, y, x, c: (z, 1 - y, x, c))
PZ1 = _perm(lambda z, y, x, c: (z ^ 1, y, x, c))
PZ2 = _perm(lambda z, y, x, c: (z ^ 2, y, x, c))


def tie(*trees):
    leaves, spec = jax.tree.flatten(trees)
    return jax.tree.unflatten(spec, lax.optimization_barrier(leaves))


class Job:
    def __init__(self, stages):
        self.stages, self.value, self.out, self.flight, self.over = stages, None, [], [], False
        self.take(None)

    def take(self, got):
        if not self.over:
            try:
                self.out = self.stages.send(got)
            except StopIteration as stop:
                self.value, self.out, self.over = stop.value, [], True


def step(ins, run=None, start=(), finish=()):
    ins, sends = tie(ins, [[value for value, _ in job.out] for job in start])
    for job, values in zip(start, sends):
        job.flight = [lax.ppermute(v, ALL, perm) for v, (_, perm) in zip(values, job.out)]
    outs = run(*ins) if run else ins
    outs, got = tie(outs, [job.flight for job in finish])
    for job, values in zip(finish, got):
        job.flight = []
        job.take(values)
    return outs


class Pieces:
    def __init__(self, plan):
        self.bufs, self.plan = {}, plan

    def part(self, lanes):
        names = sorted({p[0] for p in self.plan if p[2] in lanes})
        plan = [[(names.index(b), s, r, at) for b, s, lane, r, at in self.plan if lane == want] for want in lanes]
        return [self.bufs[n] for n in names], plan


Z_ORDER = (0, 2, 1, 3)


class Grid:
    parts = 8

    @staticmethod
    def gather(shard, pieces):
        own = shard[None]
        rows = shard.shape[0]
        for base, lane in ((0, 0), (5, 1)):
            for i, k in enumerate(Z_ORDER):
                pieces.plan.append((base, i, lane, rows, 2 * k))
                pieces.plan.append((base + 1, i, lane, rows, 2 * k + 1))
                pieces.plan.append((base + 2, i, lane + 2, rows, 2 * k))
                pieces.plan.append((base + 3 + i // 2, i % 2, lane + 2, rows, 2 * k + 1))
        (far_z,) = yield [(own, PZ2)]
        pair = jnp.concatenate([own, far_z], 0)
        (near_z,) = yield [(pair, PZ1)]
        line = jnp.concatenate([pair, near_z], 0)
        over_x, over_y, line_far = yield [(line, PX), (line, PY), (line, PC)]
        pieces.bufs.update({0: line, 1: over_y, 2: over_x, 5: line_far})
        diag_x, diag_y, over_y_far, over_x_far = yield [
            (over_y[:2], PX),
            (over_x[2:], PY),
            (over_y, PC),
            (over_x, PC),
        ]
        pieces.bufs.update({3: diag_x, 4: diag_y, 6: over_y_far, 7: over_x_far})
        diag_x_far, diag_y_far = yield [(diag_x, PC), (diag_y, PC)]
        pieces.bufs.update({8: diag_x_far, 9: diag_y_far})

    @staticmethod
    def slot(block, dp):
        place = block ^ dp
        return (place & 1) * 4 + (place & 2) + (place >> 2)

    @staticmethod
    def scatter_sum(far, near, late):
        if isinstance(far, list):
            far1, near1 = far[0], near[0]
            (got1,) = yield [(far1, PC)]
            out_x, out_y = add_first(near1, got1)
            from_x, from_y = yield [(out_x, PX), (out_y, PY)]
            (got0,) = yield [(late["far"], PC)]
            near0 = late["near"]
            out_x, out_y = add_second(near1, got1, near0, got0, from_x, from_y)
        else:
            (got,) = yield [(far, PC)]
            out_x, out_y = add_first(near, got)
            from_x, from_y = yield [(out_x, PX), (out_y, PY)]
            near0, got0 = near, got
            out_x, out_y = add_second(near, got, near, got, from_x, from_y)
        in_x, in_y = yield [(out_x, PX), (out_y, PY)]
        return near0, got0, in_x, in_y

    @staticmethod
    def scatter_line(*parts):
        out_z, kept = add_third(*parts)
        (from_z,) = yield [(out_z, PZ1)]
        out_z, kept = add_fourth(kept, from_z)
        (last,) = yield [(out_z, PZ2)]
        return [kept[n] + last[n].astype(f32) for n in range(len(parts))]

    @staticmethod
    def gather_lane(vec):
        (other,) = yield [(vec, PX)]
        pair = jnp.stack([vec, other])
        (more,) = yield [(pair, PC)]
        return jnp.stack([pair, more], 1).reshape((4,) + vec.shape)

    @staticmethod
    def sum_max(both, is_top):
        for perm in (PZ2, PZ1, PX, PY, PC):
            (other,) = yield [(both, perm)]
            both = jnp.where(is_top, jnp.maximum(both, other), both + other)
        return both

    @staticmethod
    def me():
        return lax.axis_index("dp"), lax.axis_index("tensor")


class Plain:
    parts = 1

    @staticmethod
    def gather(shard, pieces):
        rows = lax.all_gather(shard, "dp", axis=0, tiled=True)
        full = lax.all_gather(rows, "tensor", axis=0)
        pieces.plan.extend((0, k, k, full.shape[1], 0) for k in range(full.shape[0]))
        pieces.bufs[0] = full
        return
        yield

    @staticmethod
    def slot(block, dp):
        return block

    @staticmethod
    def scatter_sum(far, near, late):
        if isinstance(far, list):
            while not late:
                yield []
            parts = [late["near"], late["far"], near[0], far[0]]
        else:
            parts = [near[0], far[0], near[1], far[1]]
        grads = jnp.stack(parts).astype(f32)
        return grads.reshape((4, -1, grads.shape[-1]))
        yield

    @staticmethod
    def scatter_line(*parts):
        own = [lax.psum_scatter(p, "tensor", scatter_dimension=0, tiled=False) for p in parts]
        return [lax.psum_scatter(o, "dp", scatter_dimension=0, tiled=True) for o in own]
        yield

    @staticmethod
    def gather_lane(vec):
        return lax.all_gather(vec, "tensor", axis=0)
        yield

    @staticmethod
    def sum_max(both, is_top):
        return jnp.where(is_top, lax.pmax(both, ALL), lax.psum(both, ALL))
        yield

    @staticmethod
    def me():
        return 0, 0


VM = pl.BlockSpec(memory_space=pltpu.VMEM)
SM = pl.BlockSpec(memory_space=pltpu.SMEM)
HB = pl.BlockSpec(memory_space=pl.ANY)
VMEM_MIB = 14


def like(shape, dtype=f32):
    return jax.ShapeDtypeStruct(shape, dtype)


def call(kernel, name, specs, outs, scratch=(), flops=0, moved=0):
    return pl.pallas_call(
        kernel,
        name=name,
        out_shape=outs,
        in_specs=specs,
        out_specs=[VM] * len(outs),
        scratch_shapes=list(scratch),
        compiler_params=pltpu.CompilerParams(vmem_limit_bytes=VMEM_MIB * 2**20),
        cost_estimate=pl.CostEstimate(flops=flops, bytes_accessed=moved, transcendentals=0),
    )


def glue(kernel, outs, *ins):
    return call(kernel, kernel.__name__, [VM] * len(ins), outs)(*ins)


def add_first(near, got):
    part = like((2,) + near.shape[-2:], bf16)
    near, got = near.reshape((-1, 8) + near.shape[-2:]), got.reshape((-1, 8) + got.shape[-2:])

    def first_sums(near, got, out_x, out_y):
        top = near.shape[0] - 1
        for k in range(2):
            out_x[k] = (near[top, 4 + k].astype(f32) + got[top, 4 + k].astype(f32)).astype(bf16)
            out_y[k] = (near[top, 6 + k].astype(f32) + got[top, 6 + k].astype(f32)).astype(bf16)

    return glue(first_sums, [part, part], near, got)


def add_second(near1, got1, near0, got0, from_x, from_y):
    rows = near1.shape[-2:]
    joint = near1 is near0
    ins = [near1, got1] if joint else [near1, got1, near0, got0]
    ins = [value.reshape((-1, 8) + rows) for value in ins]

    def second_sums(*refs):
        *sums, from_x, from_y, out_x, out_y = refs
        near1, got1, near0, got0 = sums * 2 if joint else sums
        top = near1.shape[0] - 1
        for k in range(4):
            over_x = near1[top, k].astype(f32) + got1[top, k].astype(f32)
            over_y = near0[0, 4 + k].astype(f32) + got0[0, 4 + k].astype(f32)
            if k < 2:
                over_y = over_y + from_x[k].astype(f32)
            else:
                over_x = over_x + from_y[k - 2].astype(f32)
            out_x[k] = over_x.astype(bf16)
            out_y[k] = over_y.astype(bf16)

    part = like((4,) + rows, bf16)
    return glue(second_sums, [part, part], *ins, from_x, from_y)


def add_third(*parts):
    rows = parts[0][0].shape[-2:]
    ins = []
    for near, got, in_x, in_y in parts:
        ins += [near.reshape((-1, 8) + rows), got.reshape((-1, 8) + rows), in_x, in_y]

    def third_sums(*refs):
        out, kept = refs[-2:]
        for n in range(len(parts)):
            near, got, in_x, in_y = refs[4 * n : 4 * n + 4]
            for k in range(4):
                total = near[0, k].astype(f32) + got[0, k].astype(f32) + in_x[k].astype(f32) + in_y[k].astype(f32)
                if k < 2:
                    kept[n, k] = total
                else:
                    out[n, k - 2] = total.astype(bf16)

    shape = (len(parts), 2) + rows
    return glue(third_sums, [like(shape, bf16), like(shape)], *ins)


def add_fourth(kept, from_z):
    def fourth_sums(kept, from_z, out, mine):
        for n in range(kept.shape[0]):
            mine[n] = kept[n, 0] + from_z[n, 0].astype(f32)
            out[n] = (kept[n, 1] + from_z[n, 1].astype(f32)).astype(bf16)

    shape = kept.shape[:1] + kept.shape[2:]
    return glue(fourth_sums, [like(shape, bf16), like(shape)], kept, from_z)


class Loads:
    def __init__(self, plan, refs, dst, sems, dp, cols=None):
        self.plan, self.dst, self.sems, self.dp = plan, dst, sems, dp
        for lane, pieces in enumerate(plan):
            for n, (buf, sub, rows, place) in enumerate(pieces):
                src = refs[buf].at[sub] if cols is None else refs[buf].at[sub, :, pl.ds(*cols)]
                pltpu.make_async_copy(src, self.spot(lane, rows, place), sems.at[lane, n]).start()

    def spot(self, lane, rows, place):
        at = pl.multiple_of((self.dp ^ place) * rows, rows) if rows < self.dst.shape[1] else 0
        return self.dst.at[lane, pl.ds(at, rows)]

    def wait(self, lane):
        for n, (_, _, rows, place) in enumerate(self.plan[0]):
            spot = self.spot(lane, rows, place)
            pltpu.make_async_copy(spot, spot, self.sems.at[lane, n]).wait()


def row(vec):
    return vec[...].reshape(1, -1)


def row_stats(summed):
    centered = summed - jnp.mean(summed, axis=-1, keepdims=True)
    inv = lax.rsqrt(jnp.mean(centered * centered, axis=-1, keepdims=True) + epsilon)
    return centered * inv, inv


def norm_backward(scaled, normed, inv):
    row_mean = jnp.mean(scaled, axis=-1, keepdims=True)
    row_cross = jnp.mean(scaled * normed, axis=-1, keepdims=True)
    return inv * (scaled - row_mean - normed * row_cross)


def col_sum(values):
    return jnp.sum(values, axis=0, keepdims=True)


def top_of(values):
    return jnp.full((1, 128), jnp.max(jnp.abs(values)), f32)


def fill_mask(mask, longs, shorts):
    per_block = LONG_LEN // SHORT_LEN
    block = lax.axis_index("tensor")
    n_long = longs.shape[0]
    is_long = block < n_long
    whole = longs[jnp.minimum(block, n_long - 1)]
    first = jnp.maximum(block - n_long, 0) * per_block
    shift = jnp.where(is_long, LONG_LEN.bit_length() - 1, SHORT_LEN.bit_length() - 1)
    size = jnp.where(is_long, LONG_LEN, SHORT_LEN)
    k_pos = lax.broadcasted_iota(jnp.int32, (LONG_LEN, 1), 0)
    q_pos = lax.broadcasted_iota(jnp.int32, (1, LONG_LEN), 1)
    k_seg = lax.shift_right_logical(k_pos, jnp.full_like(k_pos, shift))
    q_seg = lax.shift_right_logical(q_pos, jnp.full_like(q_pos, shift))
    limit = jnp.zeros_like(k_pos)
    for j in range(per_block):
        limit = jnp.where(k_seg == j, jnp.where(is_long, whole, shorts[first + j]), limit)
    k_seg = jnp.where(k_pos - k_seg * size < limit, k_seg, -1)
    mask[...] = jnp.where(k_seg == q_seg, 0.0, NEG)


def attn_forward(net, plan, nb, dims, lim, longs, shorts, tokens, bias, *rest):
    blocks, cols, width = dims
    bufs, rest = rest[:nb], rest[nb:]
    qkv_out, lse_out, in_t, ctx_low, ctx_slope, top_out, weight, in_low, mask, ctx_t, top_ctx, sems = rest
    heads = cols // HEAD_DIM
    low_q = 3 * cols + HEAD_DIM
    loads = Loads(plan, bufs, weight, sems, net.me()[0])
    inputs = tokens[...].astype(f32)
    in_low[...] = jnp.clip(inputs, -lim[0], lim[0]).astype(bf16)
    in_t[...] = in_low[...].T
    top_out[0:1, :] = top_of(inputs)
    fill_mask(mask, longs, shorts)
    ctx_t[0:HEAD_DIM, :] = jnp.zeros((HEAD_DIM, ctx_t.shape[1]), f32)
    top_ctx[...] = jnp.zeros_like(top_ctx)
    inv_limit = 1.0 / jnp.full((1, 1), lim[1], f32)

    def each(lane, carry):
        loads.wait(lane)
        qkv = (mm(in_low[...], weight[lane, :, :low_q]) + bias[lane, :, :low_q]).astype(bf16)
        qkv_out[lane] = qkv
        for h in range(heads):
            at = h * HEAD_DIM
            q = qkv[:, at : at + HEAD_DIM]
            k = qkv[:, cols + at : cols + at + HEAD_DIM]
            v = qkv[:, 2 * cols + at : 2 * cols + at + HEAD_DIM]
            scores = mm_nt(k, q) * score_scale + mask[...]
            peak = jnp.max(scores, axis=0, keepdims=True)
            grown = jnp.exp(scores - peak)
            total = jnp.sum(grown, axis=0, keepdims=True)
            lse_out[lane, h : h + 1, :] = peak + jnp.log(total)
            shares = (grown * (1.0 / total)).astype(bf16)
            ctx_t[HEAD_DIM + at : 2 * HEAD_DIM + at, :] = mm_tn(v, shares)
        context = ctx_t[...].T
        bent = jnp.tanh(context * inv_limit)
        ctx_low[lane] = (lim[1] * bent).astype(bf16)
        ctx_slope[lane] = 1.0 - bent * bent
        top_ctx[...] = jnp.maximum(top_ctx[...], jnp.max(jnp.abs(context).reshape(-1, 8, context.shape[1]), axis=0))
        return carry

    lax.fori_loop(0, blocks, each, 0)
    top_out[1:2, :] = top_of(top_ctx[...])


def attn_finish(dims, lim, ctx_low, tokens, out_bias, gain, shift, weight, *outs):
    blocks, cols, width = dims
    normed_out, inv_out, middle_out, mid_slope, mid_low, mid_t, top_out, acc = outs
    at = 3 * cols - HEAD_DIM
    acc[...] = tokens[...].astype(f32) + row(out_bias)

    def each(lane, carry):
        acc[...] += mm_nt(ctx_low[lane], weight[lane, :, at:])
        return carry

    lax.fori_loop(0, blocks, each, 0)
    normed, inv = row_stats(acc[...])
    normed_out[...] = normed
    inv_out[...] = inv
    middle = normed * row(gain) + row(shift)
    middle_out[...] = middle
    bent = jnp.tanh(middle * (1.0 / jnp.full((1, 1), lim[2], f32)))
    low = (lim[2] * bent).astype(bf16)
    mid_low[...] = low
    mid_slope[...] = 1.0 - bent * bent
    mid_t[...] = low.T
    top_out[...] = jnp.broadcast_to(top_of(middle), top_out.shape)


def up_forward(net, plan, nb, first, low_q, lim, mid_low, bias, *rest):
    bufs, rest = rest[:nb], rest[nb:]
    act_out, slope_out, top_out, weight, top_hid, sems = rest
    loads = Loads(plan, bufs, weight, sems, net.me()[0])
    top_hid[...] = jnp.zeros_like(top_hid)
    inv_limit = 1.0 / jnp.full((1, 1), lim[3], f32)

    def each(lane, carry):
        loads.wait(lane)
        up = mm(mid_low[...], weight[lane]) + bias[first + lane, :, low_q:]
        half = 0.5 * (1.0 + lax.erf(up * root_half))
        hidden = up * half
        top_hid[...] = jnp.maximum(top_hid[...], jnp.max(jnp.abs(hidden).reshape(-1, 8, hidden.shape[1]), axis=0))
        bent = jnp.tanh(hidden * inv_limit)
        act_out[lane] = (lim[3] * bent).astype(bf16)
        slope_out[lane] = (1.0 - bent * bent) * (half + up * jnp.exp(-0.5 * up * up) * density_scale)
        return carry

    lax.fori_loop(0, weight.shape[0], each, 0)
    top_out[...] = jnp.broadcast_to(top_of(top_hid[...]), top_out.shape)


def down_both(net, plan, nb, act0, act1, slope0, slope1, middle, cotangent, down_bias, gain, shift, *rest):
    bufs, rest = rest[:nb], rest[nb:]
    layer_out, grad_out, ffn_t, sums, grad_up, up_sums, weight, acc, ffn_low, sems = rest
    loads = Loads(plan, bufs, weight, sems, net.me()[0])
    acc[...] = middle[...] + row(down_bias)
    half = act0.shape[0]
    for act, first in ((act0, 0), (act1, half)):

        def each(i, carry):
            loads.wait(first + i)
            acc[...] += mm_nt(act[i], weight[first + i])
            return carry

        lax.fori_loop(0, half, each, 0)
    normed, inv = row_stats(acc[...])
    layer_out[...] = (normed * row(gain) + row(shift)).astype(bf16)
    incoming = cotangent[...].astype(f32)
    grad = norm_backward(incoming * row(gain), normed, inv)
    grad_out[...] = grad
    ffn_low[...] = grad.astype(bf16)
    ffn_t[...] = ffn_low[...].T
    sums[...] = jnp.zeros_like(sums)
    sums[0:1, :] = col_sum(grad)
    sums[1:2, :] = col_sum(incoming * normed)
    sums[2:3, :] = col_sum(incoming)
    lane_me = net.me()[1]
    for slope, first in ((slope0, 0), (slope1, half)):

        def back(i, carry):
            low = (mm(ffn_low[...], weight[first + i]) * slope[i]).astype(bf16)
            grad_up[first + i] = low
            up_sums[(first + i) ^ lane_me] = col_sum(low.astype(f32))
            return carry

        lax.fori_loop(0, half, back, 0)


def weight_grad(net, left_t, *rest):
    *rights, far, near = rest
    rows = left_t.shape[0] // net.parts
    dp = net.me()[0]
    half = far.shape[0]
    for x in range(half):
        for out, lane in ((far, 2 * x + 1), (near, 2 * x)):
            right = rights[lane // rights[0].shape[0]]
            grad = mm(left_t[...], right[lane % right.shape[0]]).astype(bf16)
            for block in range(net.parts):
                out[x, net.slot(block, dp)] = grad[block * rows : (block + 1) * rows]


def mid_backward(dims, grad_up, grad_second, mid_slope, normed, inv, gain, ctx_slope, weight0, weight1, out_weight, *outs):
    blocks, cols, width = dims
    grad_out, attn_t, grad_ctx, sums, acc, attn_low = outs
    at = 3 * cols - HEAD_DIM
    acc[...] = jnp.zeros_like(acc)
    half = weight0.shape[0]
    for weight, first in ((weight0, 0), (weight1, half)):

        def each(i, carry):
            acc[...] += mm_nt(grad_up[first + i], weight[i])
            return carry

        lax.fori_loop(0, half, each, 0)
    incoming = grad_second[...] + acc[...] * mid_slope[...]
    grad = norm_backward(incoming * row(gain), normed[...], inv[...])
    grad_out[...] = grad
    attn_low[...] = grad.astype(bf16)
    attn_t[...] = attn_low[...].T
    sums[...] = jnp.zeros_like(sums)
    sums[0:1, :] = col_sum(grad)
    sums[1:2, :] = col_sum(incoming * normed[...])
    sums[2:3, :] = col_sum(incoming)

    def spread(lane, carry):
        grad_ctx[lane] = (mm(attn_low[...], out_weight[lane, :, at:]) * ctx_slope[lane]).astype(bf16)
        return carry

    lax.fori_loop(0, blocks, spread, 0)


def attn_backward(net, first, dims, longs, shorts, qkv, lse, grad_ctx, *rest):
    blocks, cols, width = dims
    extra, (out, sums, mask) = (), rest[-3:]
    if len(rest) > 3:
        *extra, out, packed, sums, mask = rest
    heads = cols // HEAD_DIM
    fill_mask(mask, longs, shorts)
    sums[...] = jnp.zeros_like(sums)
    lane_me = net.me()[1]

    def each(i, carry):
        lane = first + i
        for h in range(heads):
            at = h * HEAD_DIM
            q = qkv[lane, :, at : at + HEAD_DIM]
            k = qkv[lane, :, cols + at : cols + at + HEAD_DIM]
            v = qkv[lane, :, 2 * cols + at : 2 * cols + at + HEAD_DIM]
            grad = grad_ctx[lane, :, HEAD_DIM + at : 2 * HEAD_DIM + at]
            shares = jnp.exp(mm_nt(k, q) * score_scale + mask[...] - lse[lane, h : h + 1, :])
            grad_shares = mm_nt(v, grad)
            inner = jnp.sum(shares * grad_shares, axis=0, keepdims=True)
            grad_scores = (shares * (grad_shares - inner)).astype(bf16)
            grad_v = mm(shares.astype(bf16), grad)
            grad_k = mm(grad_scores, q) * score_scale
            grad_q = (mm_tn(k, grad_scores) * score_scale).T
            out[i, :, at : at + HEAD_DIM] = grad_q.astype(bf16)
            out[i, :, cols + at : cols + at + HEAD_DIM] = grad_k.astype(bf16)
            out[i, :, 2 * cols + at : 2 * cols + at + HEAD_DIM] = grad_v.astype(bf16)
        out[i, :, 3 * cols :] = jnp.zeros((out.shape[1], HEAD_DIM), bf16)
        sums[lane ^ lane_me] = col_sum(out[i].astype(f32))
        return carry

    lax.fori_loop(0, out.shape[0], each, 0)
    if extra:
        more, up_sums, sums_a, sums_b, tops_a, tops_m, top0, top1 = extra
        packed[...] = jnp.zeros_like(packed)
        for j in range(blocks):
            packed[j : j + 1, :] = up_sums[j]
            packed[blocks + j : blocks + j + 1, : sums.shape[2]] = sums[j] + more[j]
        packed[2 * blocks : 2 * blocks + 3, :] = sums_a[0:3, :]
        packed[2 * blocks + 3 : 2 * blocks + 6, :] = sums_b[0:3, :]
        tops = (tops_a[0:1, :], tops_a[1:2, :], tops_m[0:1, :], jnp.maximum(top0[0:1, :], top1[0:1, :]))
        for j, top in enumerate(tops):
            packed[2 * blocks + 6 : 2 * blocks + 7, 128 * j : 128 * j + 128] = top


def in_weight_grad(net, first, dims, in_t, attn_t, grad_qkv, ctx_low, far, near):
    blocks, cols, width = dims
    rows = in_t.shape[0] // net.parts
    at = 3 * cols - HEAD_DIM
    end = 3 * cols + HEAD_DIM
    dp = net.me()[0]
    for i, out in ((1, far), (0, near)):
        left = mm(in_t[...], grad_qkv[i])
        right = mm(attn_t[...], ctx_low[first + i])
        mixed = (left[:, at:] + right[:, : end - at]).astype(bf16)
        for block in range(net.parts):
            rs = slice(block * rows, (block + 1) * rows)
            place = net.slot(block, dp)
            out[place, :, :at] = left[rs, :at].astype(bf16)
            out[place, :, at:end] = mixed[rs]
            out[place, :, end:] = right[rs, end - at :].astype(bf16)


def token_backward(dims, lim, grad_qkv0, grad_qkv1, grad_first, tokens, weight, out, acc):
    blocks, cols, width = dims
    wide = 3 * cols + HEAD_DIM
    acc[...] = jnp.zeros_like(acc)
    half = grad_qkv0.shape[0]
    for grad, first in ((grad_qkv0, 0), (grad_qkv1, half)):

        def each(i, carry):
            acc[...] += mm_nt(grad[i], weight[first + i, :, :wide])
            return carry

        lax.fori_loop(0, half, each, 0)
    inputs = tokens[...].astype(f32)
    out[...] = (grad_first[...] + jnp.where(jnp.abs(inputs) <= lim[0], acc[...], 0.0)).astype(bf16)


def make_body(net):
    def body(
        tokens,
        cotangent,
        qkv_weight,
        qv_bias,
        out_weight,
        out_bias,
        first_gain,
        first_shift,
        up_weight,
        up_bias,
        down_weight,
        down_bias,
        second_gain,
        second_shift,
        act_ranges,
        long_lengths,
        short_lengths,
    ):
        lane = lax.axis_index("tensor")
        rows, width = tokens.shape
        assert rows == LONG_LEN
        cols = qkv_weight.shape[2]
        up_cols = up_weight.shape[1]
        blocks = lax.axis_size("tensor")
        half = blocks // 2
        dims = (blocks, cols, width)
        wide = 3 * cols + HEAD_DIM
        out_cols = cols + HEAD_DIM
        every = tuple(range(blocks))

        pieces_a, pieces_u, pieces_d = Pieces([]), Pieces([]), Pieces([])
        shard_a = jnp.concatenate(
            [qkv_weight[0], qkv_weight[1], qkv_weight[2], out_weight.T], 1
        ).astype(bf16)
        job_a = Job(net.gather(shard_a, pieces_a))
        bias_row = jnp.concatenate(
            [qv_bias[0], jnp.zeros((cols,), f32), qv_bias[1], jnp.zeros((HEAD_DIM,), f32), up_bias]
        )
        job_b = Job(net.gather_lane(bias_row[None]))
        job_u = Job(net.gather(up_weight.astype(bf16), pieces_u))
        job_d = Job(net.gather(down_weight.T.astype(bf16), pieces_d))

        def vmem(*shape, dtype=f32):
            return pltpu.VMEM(shape, dtype)

        def sems(plan):
            return pltpu.SemaphoreType.DMA((len(plan), len(plan[0])))

        unit = 2 * rows * width * width * blocks
        moved = 2 * width * width * blocks

        step((), None, [job_a, job_b], [job_a, job_b])
        step((), None, [job_a, job_b], [job_a, job_b])
        step((), None, [job_a, job_u], [job_a, job_u])
        step((), None, [job_a, job_u, job_d], [job_a])
        step((), None, [job_a], [job_a, job_u, job_d])
        biases = job_b.value

        bufs, plan = pieces_a.part(every)
        qkv, lse, in_t, ctx_low, ctx_slope, tops_a, weight_a = step(
            (act_ranges, long_lengths, short_lengths, tokens, biases, *bufs),
            call(
                functools.partial(attn_forward, net, plan, len(bufs), dims),
                "attn_forward",
                [SM] * 3 + [VM] * 2 + [HB] * len(bufs),
                [
                    like((blocks, rows, wide), bf16),
                    like((blocks, 8, rows)),
                    like((width, rows), bf16),
                    like((blocks, rows, out_cols), bf16),
                    like((blocks, rows, out_cols)),
                    like((8, 128)),
                    like((blocks, width, 4 * cols), bf16),
                ],
                [vmem(rows, width, dtype=bf16), vmem(rows, rows), vmem(out_cols, rows), vmem(8, out_cols), sems(plan)],
                4 * unit,
                3 * moved,
            ),
            [job_u, job_d],
            [job_u, job_d],
        )
        normed, inv, middle, mid_slope, mid_low, mid_t, tops_m = step(
            (act_ranges, ctx_low, tokens, out_bias, first_gain, first_shift, weight_a),
            call(
                functools.partial(attn_finish, dims),
                "attn_finish",
                [SM] + [VM] * 6,
                [
                    like((rows, width)),
                    like((rows, 1)),
                    like((rows, width)),
                    like((rows, width)),
                    like((rows, width), bf16),
                    like((width, rows), bf16),
                    like((8, 128)),
                ],
                [vmem(rows, width)],
                2 * unit,
                2 * moved,
            ),
            [job_u, job_d],
            [job_u],
        )

        def up_part(lanes, start, finish):
            bufs, plan = pieces_u.part(lanes)
            return step(
                (act_ranges, mid_low, biases, *bufs),
                call(
                    functools.partial(up_forward, net, plan, len(bufs), lanes[0], wide),
                    f"up_forward_{lanes[0]}",
                    [SM] + [VM] * 2 + [HB] * len(bufs),
                    [
                        like((half, rows, up_cols), bf16),
                        like((half, rows, up_cols)),
                        like((8, 128)),
                        like((half, width, up_cols), bf16),
                    ],
                    [vmem(8, up_cols), sems(plan)],
                    2 * unit,
                    2 * moved,
                ),
                start,
                finish,
            )

        act0, slope0, top0, weight_u0 = up_part(every[:half], [job_u], [job_u, job_d])
        act1, slope1, top1, weight_u1 = up_part(every[half:], [job_d], [job_d])
        step((), None, [job_d], [job_d])
        bufs_d, plan_d = pieces_d.part(every)
        layer_out, grad_second, ffn_t, sums_b, grad_up, up_sums = step(
            (act0, act1, slope0, slope1, middle, cotangent, down_bias, second_gain, second_shift, *bufs_d),
            call(
                functools.partial(down_both, net, plan_d, len(bufs_d)),
                "down_both",
                [VM] * 9 + [HB] * len(bufs_d),
                [
                    like((rows, width), bf16),
                    like((rows, width)),
                    like((width, rows), bf16),
                    like((8, width)),
                    like((blocks, rows, up_cols), bf16),
                    like((blocks, 1, up_cols)),
                ],
                [
                    vmem(blocks, width, up_cols, dtype=bf16),
                    vmem(rows, width),
                    vmem(rows, width, dtype=bf16),
                    sems(plan_d),
                ],
                2 * unit,
                4 * moved,
            ),
        )

        grad_shape = like((net.parts, width // net.parts, up_cols), bf16)
        both_shape = like((half,) + grad_shape.shape, bf16)

        def grad_of(name, left_t, rights, start=(), finish=()):
            return step(
                (left_t, *rights),
                call(
                    functools.partial(weight_grad, net),
                    name,
                    [VM] * (1 + len(rights)),
                    [both_shape, both_shape],
                    (),
                    unit,
                    moved,
                ),
                start,
                finish,
            )

        late_a = {}
        sum_d = Job(net.scatter_sum(*grad_of("down_grad", ffn_t, (act0, act1)), None))
        sum_u = Job(net.scatter_sum(*grad_of("up_grad", mid_t, (grad_up,), [sum_d], [sum_d]), None))
        grad_first, attn_t, grad_ctx, sums_a = step(
            (grad_up, grad_second, mid_slope, normed, inv, first_gain, ctx_slope, weight_u0, weight_u1, weight_a),
            call(
                functools.partial(mid_backward, dims),
                "mid_backward",
                [VM] * 10,
                [
                    like((rows, width)),
                    like((width, rows), bf16),
                    like((blocks, rows, out_cols), bf16),
                    like((8, width)),
                ],
                [vmem(rows, width), vmem(rows, width, dtype=bf16)],
                unit + unit // 3,
                3 * moved,
            ),
            [sum_d, sum_u],
            [sum_d, sum_u],
        )

        def back_part(first, extra=(), start=(), finish=()):
            return step(
                (long_lengths, short_lengths, qkv, lse, grad_ctx, *extra),
                call(
                    functools.partial(attn_backward, net, first, dims),
                    f"attn_backward_{first}",
                    [SM] * 2 + [VM] * (3 + len(extra)),
                    [like((half, rows, wide), bf16), like((16, width)) if extra else like((blocks, 1, wide))],
                    ([vmem(blocks, 1, wide)] if extra else []) + [vmem(rows, rows)],
                    4 * unit,
                    2 * moved,
                ),
                start,
                finish,
            )

        def in_part(grad_qkv, first, start=(), finish=()):
            return step(
                (in_t, attn_t, grad_qkv, ctx_low),
                call(
                    functools.partial(in_weight_grad, net, first, dims),
                    f"in_grad_{first}",
                    [VM] * 4,
                    [grad_shape, grad_shape],
                    (),
                    unit // 2,
                    moved,
                ),
                start,
                finish,
            )

        grad_qkv1, q_sums1 = back_part(half, (), [sum_u, sum_d], [])
        far, near = in_part(grad_qkv1, half)
        sum_a = Job(net.scatter_sum([far], [near], late_a))
        extra = (q_sums1, up_sums, sums_a, sums_b, tops_a, tops_m, top0, top1)
        grad_qkv0, packed = back_part(0, extra, [sum_a], [sum_u, sum_d, sum_a])
        is_top = (jnp.arange(packed.shape[0]) == 2 * blocks + 6)[:, None]
        sum_s = Job(net.sum_max(packed, is_top))
        far, near = in_part(grad_qkv0, 0, [sum_a, sum_u, sum_s], [])
        late_a.update(far=far, near=near)
        step((), None, [], [sum_a, sum_s])
        tokens_grad = step(
            (act_ranges, grad_qkv0, grad_qkv1, grad_first, tokens, weight_a),
            call(
                functools.partial(token_backward, dims),
                "token_backward",
                [SM] + [VM] * 5,
                [like((rows, width), bf16)],
                [vmem(rows, width)],
                unit,
                2 * moved,
            ),
            [sum_a, sum_s],
            [sum_a, sum_s],
        )[0]
        step((), None, [sum_a, sum_s], [sum_u, sum_s])
        line_du = Job(net.scatter_line(sum_d.value, sum_u.value))
        step((), None, [line_du, sum_s], [sum_a, sum_s])
        line_a = Job(net.scatter_line(sum_a.value))
        step((), None, [line_a, sum_s], [line_du, line_a, sum_s])
        step((), None, [line_a, line_du], [line_du, line_a])

        down_grad, up_grad = line_du.value
        down_grad = down_grad.T
        (a_grad,), packed = line_a.value, sum_s.value
        qkv_grad = jnp.stack([a_grad[:, j * cols : (j + 1) * cols] for j in range(3)])
        out_grad = a_grad[:, 3 * cols :].T
        own = lax.dynamic_slice_in_dim(packed, blocks + lane, 1)
        shared = packed[2 * blocks : 2 * blocks + 6]
        qv_bias_grad = jnp.concatenate([own[:, :cols], own[:, 2 * cols : 3 * cols]], 0)
        up_bias_grad = lax.dynamic_slice_in_dim(packed, lane, 1)[0]
        new_ranges = ema_decay * act_ranges + (1.0 - ema_decay) * packed[2 * blocks + 6, 0:512:128]
        return (
            layer_out,
            tokens_grad,
            qkv_grad,
            qv_bias_grad,
            out_grad,
            shared[0],
            shared[1],
            shared[2],
            up_grad,
            up_bias_grad,
            down_grad,
            shared[3],
            shared[4],
            shared[5],
            new_ranges,
        )

    return body


def solution(mesh):
    in_specs = (
        P(ALL, None),
        P(ALL, None),
        P(None, "dp", "tensor"),
        P(None, "tensor"),
        P("tensor", "dp"),
        P(),
        P(),
        P(),
        P("dp", "tensor"),
        P("tensor"),
        P("tensor", "dp"),
        P(),
        P(),
        P(),
        P(),
        P("dp"),
        P("dp"),
    )
    out_specs = (
        P(ALL, None),
        P(ALL, None),
        P(None, "dp", "tensor"),
        P(None, "tensor"),
        P("tensor", "dp"),
        P(),
        P(),
        P(),
        P("dp", "tensor"),
        P("tensor"),
        P("tensor", "dp"),
        P(),
        P(),
        P(),
        P(),
    )
    net = Grid() if mesh.shape["dp"] == 8 and mesh.shape["tensor"] == 4 else Plain()
    return jax.shard_map(make_body(net), mesh=mesh, in_specs=in_specs, out_specs=out_specs, check_vma=False)
```

time: 401 us -> 278 us (0.69); the launches traced: 393 us -> 275 us
  other arithmetic: 99.1 us -> 6.16 us
  matrix products: 91 us -> 0 us
  Pallas kernels: 0 us -> 85 us
  waiting for transfers between devices: 68.3 us -> 116 us
  local copies, waits for them, and re-layouts: 49.5 us -> 8.88 us
  starting transfers between devices: 81.9 us -> 56.8 us
    pallas_call x0 -> x23, Pallas kernels: none -> 85 us  [the longest x13 82.5 us: step(): outs = run(*ins) if run else ins]
    dot_general x15 -> x0, matrix products: 78.3 us -> none  [the longest x1 8.72 us: body(): jnp.einsum('td,ade->tae', ffn_grad, full_d, preferred_element_type=f32)]
    ppermute x66 -> x60, waiting for transfers between devices: 68.3 us -> 116 us  [step(): lax.ppermute(v, ALL, perm)]
    another operation x24 -> x4, other arithmetic: 30.4 us -> 1.07 us  [the longest x15 18.7 us: absolute(): both = jnp.stack([near, far_y], 1)]
    ppermute x66 -> x60, starting transfers between devices: 81.9 us -> 56.8 us  [step(): lax.ppermute(v, ALL, perm)]
    convert_element_type x11 -> x0, other arithmetic: 19.9 us -> none  [the longest x3 9.92 us: scatter_sum(): both = self.relative((grads[:2] + got.astype(f32)).astype(bf16))]
    slice x12 -> x9, local copies, waits for them, and re-layouts: 17.2 us -> 1.05 us  [the longest x1 0.76 us: body(): qv_bias[1]]
    reduce_max x2 -> x0, other arithmetic: 15.9 us -> none  [body(): jnp.max(jnp.abs(v))]
  transfers between devices with their start and end apart: 66 -> 60, of which waited for: 17 -> 32; matrix products, arithmetic and copies ran while one was open for 42% -> 1% of each run, Pallas kernels for 0% -> 21%
where the time goes in v3:
time: 278 us; the launch traced here: 275 us
  waiting for transfers between devices  116 us (42%)
  Pallas kernels  85 us (31%)
  starting transfers between devices  56.8 us (20%)
  local copies, waits for them, and re-layouts  8.88 us (3%)
  other arithmetic  6.16 us (2%)
    ppermute x60, waiting for transfers between devices, step(): lax.ppermute(v, ALL, perm)  116 us
    pallas_call x13, Pallas kernels, step(): outs = run(*ins) if run else ins  82.5 us
    ppermute x60, starting transfers between devices, step(): lax.ppermute(v, ALL, perm)  56.8 us
    unnamed x38, local copies, waits for them, and re-layouts  6.28 us
  transfers between devices with their start and end apart: 60, of which 32 were waited for; matrix products, arithmetic and copies ran while one was open for 1% of the time, Pallas kernels for 21%

profile of v3, /device:TPU:0, one launch (start us, length us, event | category | flops | bytes accessed | tf_op | source)
XLA Modules:
  0.0 274.9 jit_solution(11655818994635841246)
XLA Ops:
  4.4 4.1 %collective-permute-start = (bf16[1,96,768]{2,1,0:T(8,128)(2,1)S(1)}, bf16[1,96,768]{2,1,0:T(8,128)(2,1)S(1)}, u32[]{:S(2)}, u32[]{:S(2)}) collective-permute-start(bf16[1,96,768]{2,1,0:T(8,128)(2,1)S(1)} %pad_maximum_fusion.7), channel_id=1, source_target_pairs={{0,16},{1,17},{2,18},{3,19},{4,20},{5,21},{6,22},{7,23},{8,24},{9,... | collective-permute-start | bytes 442376 | tf_op jit(solution)/shard_map/ppermute | solution.py:78
  8.5 1.5 collective-permute-start.1
  10.0 2.1 collective-permute-done.1
  12.1 3.4 %collective-permute-done = bf16[1,96,768]{2,1,0:T(8,128)(2,1)S(1)} collective-permute-done((bf16[1,96,768]{2,1,0:T(8,128)(2,1)S(1)}, bf16[1,96,768]{2,1,0:T(8,128)(2,1)S(1)}, u32[]{:S(2)}, u32[]{:S(2)}) %collective-permute-start) | collective-permute-done | bytes 147488 | tf_op jit(solution)/shard_map/ppermute | solution.py:78
  17.6 6.3 %collective-permute-done.2 = bf16[2,96,768]{2,1,0:T(8,128)(2,1)S(1)} collective-permute-done((bf16[2,96,768]{2,1,0:T(8,128)(2,1)S(1)}, bf16[2,96,768]{2,1,0:T(8,128)(2,1)S(1)}, u32[]{:S(2)}, u32[]{:S(2)}) %collective-permute-start.2) | collective-permute-done | bytes 294944 | tf_op jit(solution)/shard_map/ppermute | solution.py:78
  25.4 1.5 collective-permute-start.5
  26.9 3.3 %collective-permute-start.7 = (bf16[1,96,768]{2,1,0:T(8,128)(2,1)S(1)}, bf16[1,96,768]{2,1,0:T(8,128)(2,1)S(1)}, u32[]{:S(2)}, u32[]{:S(2)}) collective-permute-start(bf16[1,96,768]{2,1,0:T(8,128)(2,1)S(1)} %convert_bitcast_fusion.1), channel_id=1, source_target_pairs={{0,16},{1,17},{2,18},{3,19},{4,20},{5,21},{6,22},{7,23},{8,24},{9,... | collective-permute-start | bytes 442376 | tf_op jit(solution)/shard_map/ppermute | solution.py:78
  30.2 7.7 %collective-permute-done.7 = bf16[1,96,768]{2,1,0:T(8,128)(2,1)S(1)} collective-permute-done((bf16[1,96,768]{2,1,0:T(8,128)(2,1)S(1)}, bf16[1,96,768]{2,1,0:T(8,128)(2,1)S(1)}, u32[]{:S(2)}, u32[]{:S(2)}) %collective-permute-start.7) | collective-permute-done | bytes 147488 | tf_op jit(solution)/shard_map/ppermute | solution.py:78
  42.1 2.5 collective-permute-start.14
  44.6 3.7 %collective-permute-done.8.rest_3_ = bf16[2,96,768]{2,1,0:T(8,128)(2,1)S(1)} collective-permute-done((bf16[2,96,768]{2,1,0:T(8,128)(2,1)S(1)}, bf16[2,96,768]{2,1,0:T(8,128)(2,1)S(1)}, u32[]{:S(2)}, u32[]{:S(2)}) %collective-permute-start.8) | collective-permute-done | bytes 294944 | tf_op jit(solution)/shard_map/ppermute | solution.py:78
  49.4 4.2 %collective-permute-start.15 = (bf16[1,96,768]{2,1,0:T(8,128)(2,1)S(1)}, bf16[1,96,768]{2,1,0:T(8,128)(2,1)S(1)}, u32[]{:S(2)}, u32[]{:S(2)}) collective-permute-start(bf16[1,96,768]{2,1,0:T(8,128)(2,1)S(1)} %convert_bitcast_fusion), channel_id=1, source_target_pairs={{0,16},{1,17},{2,18},{3,19},{4,20},{5,21},{6,22},{7,23},{8,24},{9,... | collective-permute-start | bytes 442376 | tf_op jit(solution)/shard_map/ppermute | solution.py:78
  53.7 7.2 %collective-permute-done.15 = bf16[1,96,768]{2,1,0:T(8,128)(2,1)S(1)} collective-permute-done((bf16[1,96,768]{2,1,0:T(8,128)(2,1)S(1)}, bf16[1,96,768]{2,1,0:T(8,128)(2,1)S(1)}, u32[]{:S(2)}, u32[]{:S(2)}) %collective-permute-start.15) | collective-permute-done | bytes 147488 | tf_op jit(solution)/shard_map/ppermute | solution.py:78
  61.0 1.6 collective-permute-start.16
  62.5 1.5 collective-permute-start.17
  64.8 17.7 %attn_forward.1 = (bf16[4,512,640]{2,1,0:T(8,128)(2,1)S(1)}, f32[4,8,512]{2,1,0:T(8,128)S(1)}, bf16[768,512]{1,0:T(8,128)(2,1)S(1)}, bf16[4,512,256]{2,1,0:T(8,1...) custom-call(f32[4]{0:T(128)S(1)} %copy-done.2, ...), custom_call_target="tpu_custom_call" | custom-call | flops 9663676416 | bytes 14155776 | tf_op jit(solution)/shard_map/attn_forward/pallas_call | solution.py:79
  85.8 1.5 collective-permute-start.26
  87.3 6.8 %collective-permute-done.20.rest_1_ = bf16[2,96,768]{2,1,0:T(8,128)(2,1)S(1)} collective-permute-done((bf16[2,96,768]{2,1,0:T(8,128)(2,1)S(1)}, bf16[2,96,768]{2,1,0:T(8,128)(2,1)S(1)}, u32[]{:S(2)}, u32[]{:S(2)}) %collective-permute-start.20) | collective-permute-done | bytes 294944 | tf_op jit(solution)/shard_map/ppermute | solution.py:78
  94.7 3.3 %attn_finish.1 = (f32[512,768]{1,0:T(8,128)S(1)}, f32[512,1]{1,0:T(8,128)S(1)}, f32[512,768]{1,0:T(8,128)S(1)}, f32[512,768]{1,0:T(8,128)S(1)}, bf16[512,768]{1,...) custom-call(f32[4]{0:T(128)S(1)} %copy-done.2, ...), custom_call_target="tpu_custom_call" | custom-call | flops 4831838208 | bytes 9437184 | tf_op jit(solution)/shard_map/attn_finish/pallas_call | solution.py:79
  98.6 6.9 %up_forward_0.1 = (bf16[2,512,768]{2,1,0:T(8,128)(2,1)S(1)}, f32[2,512,768]{2,1,0:T(8,128)S(1)}, f32[8,128]{1,0:T(8,128)S(1)}, bf16[2,768,768]{2,1,0:T(8,128)(2,1)S(1)}) custom-call(f32[4]{0:T(128)S(1)} %copy-done.2, bf16[512,768]{1,0:T(8,128)(2,1)S(1)} %get-tuple-element.443.mid_low, f32[4,1,1408]{2,1,0:T(1,128)S(1)} %bitcast.51, ...), custom_call_target="tpu_custom_call" | custom-call | flops 4831838208 | bytes 9437184 | tf_op jit(solution)/shard_map/up_forward_0/pallas_call | solution.py:79
  106.0 2.0 collective-permute-done.27.rest_1_
  109.7 6.9 %up_forward_2.1 = (bf16[2,512,768]{2,1,0:T(8,128)(2,1)S(1)}, f32[2,512,768]{2,1,0:T(8,128)S(1)}, f32[8,128]{1,0:T(8,128)S(1)}, bf16[2,768,768]{2,1,0:T(8,128)(2,1)S(1)}) custom-call(f32[4]{0:T(128)S(1)} %copy-done.2, bf16[512,768]{1,0:T(8,128)(2,1)S(1)} %get-tuple-element.443.mid_low, f32[4,1,1408]{2,1,0:T(1,128)S(1)} %bitcast.52, ...), custom_call_target="tpu_custom_call" | custom-call | flops 4831838208 | bytes 9437184 | tf_op jit(solution)/shard_map/up_forward_2/pallas_call | solution.py:79
  120.0 14.9 %down_both.1 = (bf16[512,768]{1,0:T(8,128)(2,1)}, f32[512,768]{1,0:T(8,128)S(1)}, bf16[768,512]{1,0:T(8,128)(2,1)S(1)}, f32[8,768]{1,0:T(8,128)S(1)}, bf16[4,512...) custom-call(bf16[2,512,768]{2,1,0:T(8,128)(2,1)S(1)} %get-tuple-element.504.act0.rest_0_, ...), custom_call_target="tpu_custom_call" | custom-call | flops 4831838208 | bytes 18874368 | tf_op jit(solution)/shard_map/down_both/pallas_call | solution.py:79
  136.2 2.7 down_grad.1
  139.1 2.7 up_grad.1
  141.8 1.7 collective-permute-done.35.got.refs_1_
  143.9 1.5 collective-permute-start.36
  145.9 6.3 %mid_backward.1 = (f32[512,768]{1,0:T(8,128)S(1)}, bf16[768,512]{1,0:T(8,128)(2,1)S(1)}, bf16[4,512,256]{2,1,0:T(8,128)(2,1)S(1)}, f32[8,768]{1,0:T(8,128)S(1)}) custom-call(bf16[4,512,768]{2,1,0:T(8,128)(2,1)S(1)} %get-tuple-element.518.rest_0_.grad_up, f32[512,768]{1,0:T(8,128)S(1)} %get-tuple-element.519.grad_second, ...), custom_call_target="tpu_custom_call" | custom-call | flops 3221225472 | bytes 14155776 | tf_op jit(solution)/shard_map/mid_backward/pallas_call | solution.py:79
  154.9 1.6 copy-done.15
  156.5 6.2 %attn_backward_2.1 = (bf16[2,512,640]{2,1,0:T(8,128)(2,1)S(1)}, f32[4,1,640]{2,1,0:T(1,128)S(1)}) custom-call(s32[1]{0:T(128)S(6)} %copy.35.longs, s32[12]{0:T(128)S(1)} %copy-done.9, bf16[4,512,640]{2,1,0:T(8,128)(2,1)S(1)} %copy-done.15, f32[4,8,512]{2,1,0:T(8,128)S(1)} %get-tuple-element.568.lse, bf16[4,512,256]{2,1,0:T(8,128)(2,1)S(1)} %get-tuple-element.569.grad_ctx), custom_call_target="tpu_custom_call" | custom-call | flops 9663676416 | bytes 9437184 | tf_op jit(solution)/shard_map/attn_backward_2/pallas_call | solution.py:79
  162.8 1.8 in_grad_2.1
  165.8 1.5 collective-permute-start.39
  167.3 1.5 collective-permute-start.40
  168.8 6.0 %attn_backward_0.1 = (bf16[2,512,640]{2,1,0:T(8,128)(2,1)S(1)}, f32[16,768]{1,0:T(8,128)S(1)}) custom-call(s32[1]{0:T(128)S(6)} %copy.35.longs, s32[12]{0:T(128)S(1)} %copy-done.9, bf16[4,512,640]{2,1,0:T(8,128)(2,1)S(1)} %copy-done.15, f32[4,8,512]{2,1,0:T(8,128)S(1)} %get-tuple-element.568.lse, bf16[4,512,256]{2,1,0:T(8,128)(2,1)S(1)} %get-tuple-element.569.grad_ctx, ...), custom_call_target="tpu_custom_call" | custom-call | flops 9663676416 | bytes 9437184 | tf_op jit(solution)/shard_map/attn_backward_0/pallas_call | solution.py:79
  174.8 11.9 %collective-permute-done.39.refs_2_ = bf16[2,96,768]{2,1,0:T(8,128)(2,1)S(1)} collective-permute-done((bf16[2,96,768]{2,1,0:T(8,128)(2,1)S(1)}, bf16[2,96,768]{2,1,0:T(8,128)(2,1)S(1)}, u32[]{:S(2)}, u32[]{:S(2)}) %collective-permute-start.39) | collective-permute-done | bytes 294944 | tf_op jit(solution)/shard_map/ppermute | solution.py:78
  187.5 1.5 collective-permute-start.44
  189.5 3.4 %collective-permute-start.46 = (f32[16,768]{1,0:T(8,128)S(1)}, f32[16,768]{1,0:T(8,128)S(1)}, u32[]{:S(2)}, u32[]{:S(2)}) collective-permute-start(f32[16,768]{1,0:T(8,128)S(1)} %get-tuple-element.603), channel_id=1, source_target_pairs={{0,16},{1,17},{2,18},{3,19},{4,20},{5,21},{6,22},{7,23},{8,24},{9,... | collective-permute-start | bytes 147464 | tf_op jit(solution)/shard_map/ppermute | solution.py:78
  192.9 1.8 in_grad_0.1
  199.5 5.2 %token_backward.1 = bf16[512,768]{1,0:T(8,128)(2,1)} custom-call(f32[4]{0:T(128)S(1)} %copy-done.2, bf16[2,512,640]{2,1,0:T(8,128)(2,1)S(1)} %get-tuple-element.606.grad_qkv.grad_qkv0, bf16[2,512,640]{2,1,0:T(8,128)(2,1)S(1)} %get-tuple-element.607.grad_qkv.grad_qkv1, f32[512,768]{1,0:T(8,128)S(1)} %get-tuple-element.608.grad_first, ...), custom_call_target="tpu_custom_call" | custom-call | flops 2415919104 | bytes 9437184 | tf_op jit(solution)/shard_map/token_backward/pallas_call | solution.py:79
  205.2 1.5 collective-permute-start.49
  206.6 1.5 collective-permute-start.50
  208.7 4.6 %collective-permute-done.51.refs_6_ = bf16[4,96,768]{2,1,0:T(8,128)(2,1)S(1)} collective-permute-done((bf16[4,96,768]{2,1,0:T(8,128)(2,1)S(1)}, bf16[4,96,768]{2,1,0:T(8,128)(2,1)S(1)}, u32[]{:S(2)}, u32[]{:S(2)}) %collective-permute-start.51) | collective-permute-done | bytes 589856 | tf_op jit(solution)/shard_map/ppermute | solution.py:78
  213.9 12.6 %collective-permute-done.53 = f32[16,768]{1,0:T(8,128)S(1)} collective-permute-done((f32[16,768]{1,0:T(8,128)S(1)}, f32[16,768]{1,0:T(8,128)S(1)}, u32[]{:S(2)}, u32[]{:S(2)}) %collective-permute-start.53) | collective-permute-done | bytes 49184 | tf_op jit(solution)/shard_map/ppermute | solution.py:78
  229.0 3.6 %collective-permute-done.54 = f32[16,768]{1,0:T(8,128)S(1)} collective-permute-done((f32[16,768]{1,0:T(8,128)S(1)}, f32[16,768]{1,0:T(8,128)S(1)}, u32[]{:S(2)}, u32[]{:S(2)}) %collective-permute-start.54) | collective-permute-done | bytes 49184 | tf_op jit(solution)/shard_map/ppermute | solution.py:78
  234.3 1.6 collective-permute-done.57
  235.8 7.5 %collective-permute-done.55.from_z = bf16[2,2,96,768]{3,2,1,0:T(8,128)(2,1)S(1)} collective-permute-done((bf16[2,2,96,768]{3,2,1,0:T(8,128)(2,1)S(1)}, bf16[2,2,96,768]{3,2,1,0:T(8,128)(2,1)S(1)}, u32[]{:S(2)}, u32[]{:S(2)}) %collective-permute-start.55) | collective-permute-done | bytes 589856 | tf_op jit(solution)/shard_map/ppermute | solution.py:78
  243.4 4.9 %collective-permute-done.56.from_z = bf16[1,2,96,768]{3,2,1,0:T(8,128)(2,1)S(1)} collective-permute-done((bf16[1,2,96,768]{3,2,1,0:T(8,128)(2,1)S(1)}, bf16[1,2,96,768]{3,2,1,0:T(8,128)(2,1)S(1)}, u32[]{:S(2)}, u32[]{:S(2)}) %collective-permute-start.56) | collective-permute-done | bytes 294944 | tf_op jit(solution)/shard_map/ppermute | solution.py:78
  250.0 3.4 %collective-permute-start.58 = (bf16[2,96,768]{2,1,0:T(8,128)(2,1)S(1)}, bf16[2,96,768]{2,1,0:T(8,128)(2,1)S(1)}, u32[]{:S(2)}, u32[]{:S(2)}) collective-permute-start(bf16[2,96,768]{2,1,0:T(8,128)(2,1)S(1)} %get-tuple-element.647), channel_id=1, source_target_pairs={{0,16},{1,17},{2,18},{3,19},{4,20},{5,21},{6,22},{7,23},{8,24},{9,... | collective-permute-start | bytes 884744 | tf_op jit(solution)/shard_map/ppermute | solution.py:78
  254.8 17.1 %collective-permute-done.59 = bf16[1,96,768]{2,1,0:T(8,128)(2,1)S(1)} collective-permute-done((bf16[1,96,768]{2,1,0:T(8,128)(2,1)S(1)}, bf16[1,96,768]{2,1,0:T(8,128)(2,1)S(1)}, u32[]{:S(2)}, u32[]{:S(2)}) %collective-permute-start.59) | collective-permute-done | bytes 147488 | tf_op jit(solution)/shard_map/ppermute | solution.py:78
  (173 shorter events, 46.1 us)
Async XLA Ops:
  4.4 11.1 %collective-permute-start = (bf16[1,96,768]{2,1,0:T(8,128)(2,1)S(1)}, bf16[1,96,768]{2,1,0:T(8,128)(2,1)S(1)}, u32[]{:S(2)}, u32[]{:S(2)}) collective-permute-start(bf16[1,96,768]{2,1,0:T(8,128)(2,1)S(1)} %pad_maximum_fusion.7), channel_id=1, source_target_pairs={{0,16},{1,17},{2,18},{3,19},{4,20},{5,21},{6,22},{7,23},{8,24},{9,... | collective-permute-start | bytes 442376 | tf_op jit(solution)/shard_map/ppermute | solution.py:78
  24.0 13.9 %collective-permute-start.4 = (bf16[4,96,768]{2,1,0:T(8,128)(2,1)S(1)}, bf16[4,96,768]{2,1,0:T(8,128)(2,1)S(1)}, u32[]{:S(2)}, u32[]{:S(2)}) collective-permute-start(bf16[4,96,768]{2,1,0:T(8,128)(2,1)S(1)} %pad_maximum_fusion.rest_0_), channel_id=1, source_target_pairs={{0,2},{1,3},{2,0},{3,1},{4,6},{5,7},{6,4},{7,5},{8,10},{9,11},{10,... | collective-permute-start | bytes 1769480 | tf_op jit(solution)/shard_map/ppermute | solution.py:78
  25.4 13.3 %collective-permute-start.5 = (bf16[4,96,768]{2,1,0:T(8,128)(2,1)S(1)}, bf16[4,96,768]{2,1,0:T(8,128)(2,1)S(1)}, u32[]{:S(2)}, u32[]{:S(2)}) collective-permute-start(bf16[4,96,768]{2,1,0:T(8,128)(2,1)S(1)} %pad_maximum_fusion.rest_0_), channel_id=1, source_target_pairs={{0,4},{1,5},{2,6},{3,7},{4,0},{5,1},{6,2},{7,3},{8,12},{9,13},{10,... | collective-permute-start | bytes 1769480 | tf_op jit(solution)/shard_map/ppermute | solution.py:78
  26.9 11.8 %collective-permute-start.6 = (bf16[4,96,768]{2,1,0:T(8,128)(2,1)S(1)}, bf16[4,96,768]{2,1,0:T(8,128)(2,1)S(1)}, u32[]{:S(2)}, u32[]{:S(2)}) collective-permute-start(bf16[4,96,768]{2,1,0:T(8,128)(2,1)S(1)} %pad_maximum_fusion.rest_0_), channel_id=1, source_target_pairs={{0,1},{1,0},{2,3},{3,2},{4,5},{5,4},{6,7},{7,6},{8,9},{9,8},{10,11... | collective-permute-start | bytes 1769480 | tf_op jit(solution)/shard_map/ppermute | solution.py:78
  26.9 11.0 %collective-permute-start.7 = (bf16[1,96,768]{2,1,0:T(8,128)(2,1)S(1)}, bf16[1,96,768]{2,1,0:T(8,128)(2,1)S(1)}, u32[]{:S(2)}, u32[]{:S(2)}) collective-permute-start(bf16[1,96,768]{2,1,0:T(8,128)(2,1)S(1)} %convert_bitcast_fusion.1), channel_id=1, source_target_pairs={{0,16},{1,17},{2,18},{3,19},{4,20},{5,21},{6,22},{7,23},{8,24},{9,... | collective-permute-start | bytes 442376 | tf_op jit(solution)/shard_map/ppermute | solution.py:78
  38.8 10.1 %collective-permute-start.10 = (bf16[4,96,768]{2,1,0:T(8,128)(2,1)S(1)}, bf16[4,96,768]{2,1,0:T(8,128)(2,1)S(1)}, u32[]{:S(2)}, u32[]{:S(2)}) collective-permute-start(bf16[4,96,768]{2,1,0:T(8,128)(2,1)S(1)} %collective-permute-done.5.rest_1_), channel_id=1, source_target_pairs={{0,1},{1,0},{2,3},{3,2},{4,5},{5,4},{6,7},{7,6},{8,9},{9,8},{10,11... | collective-permute-start | bytes 1769480 | tf_op jit(solution)/shard_map/ppermute | solution.py:78
  38.9 10.0 %collective-permute-start.11 = (bf16[4,96,768]{2,1,0:T(8,128)(2,1)S(1)}, bf16[4,96,768]{2,1,0:T(8,128)(2,1)S(1)}, u32[]{:S(2)}, u32[]{:S(2)}) collective-permute-start(bf16[4,96,768]{2,1,0:T(8,128)(2,1)S(1)} %collective-permute-done.4.rest_2_), channel_id=1, source_target_pairs={{0,1},{1,0},{2,3},{3,2},{4,5},{5,4},{6,7},{7,6},{8,9},{9,8},{10,11... | collective-permute-start | bytes 1769480 | tf_op jit(solution)/shard_map/ppermute | solution.py:78
  39.4 9.0 %collective-permute-start.8 = (bf16[2,96,768]{2,1,0:T(8,128)(2,1)S(1)}, bf16[2,96,768]{2,1,0:T(8,128)(2,1)S(1)}, u32[]{:S(2)}, u32[]{:S(2)}) collective-permute-start(bf16[2,96,768]{2,1,0:T(8,128)(2,1)S(1)} %slice.99), channel_id=1, source_target_pairs={{0,2},{1,3},{2,0},{3,1},{4,6},{5,7},{6,4},{7,5},{8,10},{9,11},{10,... | collective-permute-start | bytes 884744 | tf_op jit(solution)/shard_map/ppermute | solution.py:78
  40.2 8.7 %collective-permute-start.9 = (bf16[2,96,768]{2,1,0:T(8,128)(2,1)S(1)}, bf16[2,96,768]{2,1,0:T(8,128)(2,1)S(1)}, u32[]{:S(2)}, u32[]{:S(2)}) collective-permute-start(bf16[2,96,768]{2,1,0:T(8,128)(2,1)S(1)} %slice.100), channel_id=1, source_target_pairs={{0,4},{1,5},{2,6},{3,7},{4,0},{5,1},{6,2},{7,3},{8,12},{9,13},{10,... | collective-permute-start | bytes 884744 | tf_op jit(solution)/shard_map/ppermute | solution.py:78
  42.1 18.8 %collective-permute-start.14 = (bf16[2,96,768]{2,1,0:T(8,128)(2,1)S(1)}, bf16[2,96,768]{2,1,0:T(8,128)(2,1)S(1)}, u32[]{:S(2)}, u32[]{:S(2)}) collective-permute-start(bf16[2,96,768]{2,1,0:T(8,128)(2,1)S(1)} %pad_maximum_fusion.4), channel_id=1, source_target_pairs={{0,8},{1,9},{2,10},{3,11},{4,12},{5,13},{6,14},{7,15},{8,0},{9,1},... | collective-permute-start | bytes 884744 | tf_op jit(solution)/shard_map/ppermute | solution.py:78
  48.9 12.0 %collective-permute-start.12 = (bf16[2,96,768]{2,1,0:T(8,128)(2,1)S(1)}, bf16[2,96,768]{2,1,0:T(8,128)(2,1)S(1)}, u32[]{:S(2)}, u32[]{:S(2)}) collective-permute-start(bf16[2,96,768]{2,1,0:T(8,128)(2,1)S(1)} %collective-permute-done.8.rest_3_), channel_id=1, source_target_pairs={{0,1},{1,0},{2,3},{3,2},{4,5},{5,4},{6,7},{7,6},{8,9},{9,8},{10,11... | collective-permute-start | bytes 884744 | tf_op jit(solution)/shard_map/ppermute | solution.py:78
  48.9 12.0 %collective-permute-start.13 = (bf16[2,96,768]{2,1,0:T(8,128)(2,1)S(1)}, bf16[2,96,768]{2,1,0:T(8,128)(2,1)S(1)}, u32[]{:S(2)}, u32[]{:S(2)}) collective-permute-start(bf16[2,96,768]{2,1,0:T(8,128)(2,1)S(1)} %collective-permute-done.9.rest_4_), channel_id=1, source_target_pairs={{0,1},{1,0},{2,3},{3,2},{4,5},{5,4},{6,7},{7,6},{8,9},{9,8},{10,11... | collective-permute-start | bytes 884744 | tf_op jit(solution)/shard_map/ppermute | solution.py:78
  49.4 11.5 %collective-permute-start.15 = (bf16[1,96,768]{2,1,0:T(8,128)(2,1)S(1)}, bf16[1,96,768]{2,1,0:T(8,128)(2,1)S(1)}, u32[]{:S(2)}, u32[]{:S(2)}) collective-permute-start(bf16[1,96,768]{2,1,0:T(8,128)(2,1)S(1)} %convert_bitcast_fusion), channel_id=1, source_target_pairs={{0,16},{1,17},{2,18},{3,19},{4,20},{5,21},{6,22},{7,23},{8,24},{9,... | collective-permute-start | bytes 442376 | tf_op jit(solution)/shard_map/ppermute | solution.py:78
  61.0 23.0 %collective-permute-start.16 = (bf16[4,96,768]{2,1,0:T(8,128)(2,1)S(1)}, bf16[4,96,768]{2,1,0:T(8,128)(2,1)S(1)}, u32[]{:S(2)}, u32[]{:S(2)}) collective-permute-start(bf16[4,96,768]{2,1,0:T(8,128)(2,1)S(1)} %pad_maximum_fusion.1.rest_0_), channel_id=1, source_target_pairs={{0,2},{1,3},{2,0},{3,1},{4,6},{5,7},{6,4},{7,5},{8,10},{9,11},{10,... | collective-permute-start | bytes 1769480 | tf_op jit(solution)/shard_map/ppermute | solution.py:78
  62.5 21.5 %collective-permute-start.17 = (bf16[4,96,768]{2,1,0:T(8,128)(2,1)S(1)}, bf16[4,96,768]{2,1,0:T(8,128)(2,1)S(1)}, u32[]{:S(2)}, u32[]{:S(2)}) collective-permute-start(bf16[4,96,768]{2,1,0:T(8,128)(2,1)S(1)} %pad_maximum_fusion.1.rest_0_), channel_id=1, source_target_pairs={{0,4},{1,5},{2,6},{3,7},{4,0},{5,1},{6,2},{7,3},{8,12},{9,13},{10,... | collective-permute-start | bytes 1769480 | tf_op jit(solution)/shard_map/ppermute | solution.py:78
  64.1 20.0 %collective-permute-start.18 = (bf16[4,96,768]{2,1,0:T(8,128)(2,1)S(1)}, bf16[4,96,768]{2,1,0:T(8,128)(2,1)S(1)}, u32[]{:S(2)}, u32[]{:S(2)}) collective-permute-start(bf16[4,96,768]{2,1,0:T(8,128)(2,1)S(1)} %pad_maximum_fusion.1.rest_0_), channel_id=1, source_target_pairs={{0,1},{1,0},{2,3},{3,2},{4,5},{5,4},{6,7},{7,6},{8,9},{9,8},{10,11... | collective-permute-start | bytes 1769480 | tf_op jit(solution)/shard_map/ppermute | solution.py:78
  64.1 19.9 %collective-permute-start.19 = (bf16[2,96,768]{2,1,0:T(8,128)(2,1)S(1)}, bf16[2,96,768]{2,1,0:T(8,128)(2,1)S(1)}, u32[]{:S(2)}, u32[]{:S(2)}) collective-permute-start(bf16[2,96,768]{2,1,0:T(8,128)(2,1)S(1)} %pad_maximum_fusion.5), channel_id=1, source_target_pairs={{0,8},{1,9},{2,10},{3,11},{4,12},{5,13},{6,14},{7,15},{8,0},{9,1},... | collective-permute-start | bytes 884744 | tf_op jit(solution)/shard_map/ppermute | solution.py:78
  84.2 9.9 %collective-permute-start.20 = (bf16[2,96,768]{2,1,0:T(8,128)(2,1)S(1)}, bf16[2,96,768]{2,1,0:T(8,128)(2,1)S(1)}, u32[]{:S(2)}, u32[]{:S(2)}) collective-permute-start(bf16[2,96,768]{2,1,0:T(8,128)(2,1)S(1)} %slice.101), channel_id=1, source_target_pairs={{0,2},{1,3},{2,0},{3,1},{4,6},{5,7},{6,4},{7,5},{8,10},{9,11},{10,... | collective-permute-start | bytes 884744 | tf_op jit(solution)/shard_map/ppermute | solution.py:78
  84.8 9.9 %collective-permute-start.21 = (bf16[2,96,768]{2,1,0:T(8,128)(2,1)S(1)}, bf16[2,96,768]{2,1,0:T(8,128)(2,1)S(1)}, u32[]{:S(2)}, u32[]{:S(2)}) collective-permute-start(bf16[2,96,768]{2,1,0:T(8,128)(2,1)S(1)} %slice.102), channel_id=1, source_target_pairs={{0,4},{1,5},{2,6},{3,7},{4,0},{5,1},{6,2},{7,3},{8,12},{9,13},{10,... | collective-permute-start | bytes 884744 | tf_op jit(solution)/shard_map/ppermute | solution.py:78
  85.3 12.7 %collective-permute-start.22 = (bf16[4,96,768]{2,1,0:T(8,128)(2,1)S(1)}, bf16[4,96,768]{2,1,0:T(8,128)(2,1)S(1)}, u32[]{:S(2)}, u32[]{:S(2)}) collective-permute-start(bf16[4,96,768]{2,1,0:T(8,128)(2,1)S(1)} %collective-permute-done.17.rest_1_), channel_id=1, source_target_pairs={{0,1},{1,0},{2,3},{3,2},{4,5},{5,4},{6,7},{7,6},{8,9},{9,8},{10,11... | collective-permute-start | bytes 1769480 | tf_op jit(solution)/shard_map/ppermute | solution.py:78
  85.3 12.7 %collective-permute-start.23 = (bf16[4,96,768]{2,1,0:T(8,128)(2,1)S(1)}, bf16[4,96,768]{2,1,0:T(8,128)(2,1)S(1)}, u32[]{:S(2)}, u32[]{:S(2)}) collective-permute-start(bf16[4,96,768]{2,1,0:T(8,128)(2,1)S(1)} %collective-permute-done.16.rest_0_), channel_id=1, source_target_pairs={{0,1},{1,0},{2,3},{3,2},{4,5},{5,4},{6,7},{7,6},{8,9},{9,8},{10,11... | collective-permute-start | bytes 1769480 | tf_op jit(solution)/shard_map/ppermute | solution.py:78
  85.8 20.2 %collective-permute-start.26 = (bf16[4,96,768]{2,1,0:T(8,128)(2,1)S(1)}, bf16[4,96,768]{2,1,0:T(8,128)(2,1)S(1)}, u32[]{:S(2)}, u32[]{:S(2)}) collective-permute-start(bf16[4,96,768]{2,1,0:T(8,128)(2,1)S(1)} %pad_maximum_fusion.2.rest_0_), channel_id=1, source_target_pairs={{0,2},{1,3},{2,0},{3,1},{4,6},{5,7},{6,4},{7,5},{8,10},{9,11},{10,... | collective-permute-start | bytes 1769480 | tf_op jit(solution)/shard_map/ppermute | solution.py:78
  94.1 13.9 %collective-permute-start.27 = (bf16[4,96,768]{2,1,0:T(8,128)(2,1)S(1)}, bf16[4,96,768]{2,1,0:T(8,128)(2,1)S(1)}, u32[]{:S(2)}, u32[]{:S(2)}) collective-permute-start(bf16[4,96,768]{2,1,0:T(8,128)(2,1)S(1)} %pad_maximum_fusion.2.rest_0_), channel_id=1, source_target_pairs={{0,4},{1,5},{2,6},{3,7},{4,0},{5,1},{6,2},{7,3},{8,12},{9,13},{10,... | collective-permute-start | bytes 1769480 | tf_op jit(solution)/shard_map/ppermute | solution.py:78
  94.6 13.3 %collective-permute-start.28 = (bf16[4,96,768]{2,1,0:T(8,128)(2,1)S(1)}, bf16[4,96,768]{2,1,0:T(8,128)(2,1)S(1)}, u32[]{:S(2)}, u32[]{:S(2)}) collective-permute-start(bf16[4,96,768]{2,1,0:T(8,128)(2,1)S(1)} %pad_maximum_fusion.2.rest_0_), channel_id=1, source_target_pairs={{0,1},{1,0},{2,3},{3,2},{4,5},{5,4},{6,7},{7,6},{8,9},{9,8},{10,11... | collective-permute-start | bytes 1769480 | tf_op jit(solution)/shard_map/ppermute | solution.py:78
  98.0 10.0 %collective-permute-start.24 = (bf16[2,96,768]{2,1,0:T(8,128)(2,1)S(1)}, bf16[2,96,768]{2,1,0:T(8,128)(2,1)S(1)}, u32[]{:S(2)}, u32[]{:S(2)}) collective-permute-start(bf16[2,96,768]{2,1,0:T(8,128)(2,1)S(1)} %collective-permute-done.20.rest_1_), channel_id=1, source_target_pairs={{0,1},{1,0},{2,3},{3,2},{4,5},{5,4},{6,7},{7,6},{8,9},{9,8},{10,11... | collective-permute-start | bytes 884744 | tf_op jit(solution)/shard_map/ppermute | solution.py:78
  98.5 9.5 %collective-permute-start.25 = (bf16[2,96,768]{2,1,0:T(8,128)(2,1)S(1)}, bf16[2,96,768]{2,1,0:T(8,128)(2,1)S(1)}, u32[]{:S(2)}, u32[]{:S(2)}) collective-permute-start(bf16[2,96,768]{2,1,0:T(8,128)(2,1)S(1)} %collective-permute-done.21.rest_2_), channel_id=1, source_target_pairs={{0,1},{1,0},{2,3},{3,2},{4,5},{5,4},{6,7},{7,6},{8,9},{9,8},{10,11... | collective-permute-start | bytes 884744 | tf_op jit(solution)/shard_map/ppermute | solution.py:78
  108.1 9.8 %collective-permute-start.31 = (bf16[4,96,768]{2,1,0:T(8,128)(2,1)S(1)}, bf16[4,96,768]{2,1,0:T(8,128)(2,1)S(1)}, u32[]{:S(2)}, u32[]{:S(2)}) collective-permute-start(bf16[4,96,768]{2,1,0:T(8,128)(2,1)S(1)} %collective-permute-done.27.rest_1_), channel_id=1, source_target_pairs={{0,1},{1,0},{2,3},{3,2},{4,5},{5,4},{6,7},{7,6},{8,9},{9,8},{10,11... | collective-permute-start | bytes 1769480 | tf_op jit(solution)/shard_map/ppermute | solution.py:78
  108.2 9.8 %collective-permute-start.32 = (bf16[4,96,768]{2,1,0:T(8,128)(2,1)S(1)}, bf16[4,96,768]{2,1,0:T(8,128)(2,1)S(1)}, u32[]{:S(2)}, u32[]{:S(2)}) collective-permute-start(bf16[4,96,768]{2,1,0:T(8,128)(2,1)S(1)} %collective-permute-done.26.rest_2_), channel_id=1, source_target_pairs={{0,1},{1,0},{2,3},{3,2},{4,5},{5,4},{6,7},{7,6},{8,9},{9,8},{10,11... | collective-permute-start | bytes 1769480 | tf_op jit(solution)/shard_map/ppermute | solution.py:78
  108.7 9.0 %collective-permute-start.29 = (bf16[2,96,768]{2,1,0:T(8,128)(2,1)S(1)}, bf16[2,96,768]{2,1,0:T(8,128)(2,1)S(1)}, u32[]{:S(2)}, u32[]{:S(2)}) collective-permute-start(bf16[2,96,768]{2,1,0:T(8,128)(2,1)S(1)} %slice.103), channel_id=1, source_target_pairs={{0,2},{1,3},{2,0},{3,1},{4,6},{5,7},{6,4},{7,5},{8,10},{9,11},{10,... | collective-permute-start | bytes 884744 | tf_op jit(solution)/shard_map/ppermute | solution.py:78
  109.2 8.7 %collective-permute-start.30 = (bf16[2,96,768]{2,1,0:T(8,128)(2,1)S(1)}, bf16[2,96,768]{2,1,0:T(8,128)(2,1)S(1)}, u32[]{:S(2)}, u32[]{:S(2)}) collective-permute-start(bf16[2,96,768]{2,1,0:T(8,128)(2,1)S(1)} %slice.104), channel_id=1, source_target_pairs={{0,4},{1,5},{2,6},{3,7},{4,0},{5,1},{6,2},{7,3},{8,12},{9,13},{10,... | collective-permute-start | bytes 884744 | tf_op jit(solution)/shard_map/ppermute | solution.py:78
  143.7 10.7 %collective-permute-start.38 = (bf16[2,8,96,768]{3,2,1,0:T(8,128)(2,1)S(1)}, bf16[2,8,96,768]{3,2,1,0:T(8,128)(2,1)S(1)}, u32[]{:S(2)}, u32[]{:S(2)}) collective-permute-start(bf16[2,8,96,768]{3,2,1,0:T(8,128)(2,1)S(1)} %get-tuple-element.534), channel_id=1, source_target_pairs={{0,1},{1,0},{2,3},{3,2},{4,5},{5,4},{6,7},{7,6},{8,9},{9,8},{10,11... | collective-permute-start | bytes 7077896 | tf_op jit(solution)/shard_map/ppermute | solution.py:78
  143.9 9.3 %collective-permute-start.36 = (bf16[2,96,768]{2,1,0:T(8,128)(2,1)S(1)}, bf16[2,96,768]{2,1,0:T(8,128)(2,1)S(1)}, u32[]{:S(2)}, u32[]{:S(2)}) collective-permute-start(bf16[2,96,768]{2,1,0:T(8,128)(2,1)S(1)} %get-tuple-element.532), channel_id=1, source_target_pairs={{0,2},{1,3},{2,0},{3,1},{4,6},{5,7},{6,4},{7,5},{8,10},{9,11},{10,... | collective-permute-start | bytes 884744 | tf_op jit(solution)/shard_map/ppermute | solution.py:78
  145.4 9.0 %collective-permute-start.37 = (bf16[2,96,768]{2,1,0:T(8,128)(2,1)S(1)}, bf16[2,96,768]{2,1,0:T(8,128)(2,1)S(1)}, u32[]{:S(2)}, u32[]{:S(2)}) collective-permute-start(bf16[2,96,768]{2,1,0:T(8,128)(2,1)S(1)} %get-tuple-element.533), channel_id=1, source_target_pairs={{0,4},{1,5},{2,6},{3,7},{4,0},{5,1},{6,2},{7,3},{8,12},{9,13},{10,... | collective-permute-start | bytes 884744 | tf_op jit(solution)/shard_map/ppermute | solution.py:78
  164.6 22.4 %collective-permute-start.43 = (bf16[8,96,768]{2,1,0:T(8,128)(2,1)S(1)}, bf16[8,96,768]{2,1,0:T(8,128)(2,1)S(1)}, u32[]{:S(2)}, u32[]{:S(2)}) collective-permute-start(bf16[8,96,768]{2,1,0:T(8,128)(2,1)S(1)} %get-tuple-element.584), channel_id=1, source_target_pairs={{0,1},{1,0},{2,3},{3,2},{4,5},{5,4},{6,7},{7,6},{8,9},{9,8},{10,11... | collective-permute-start | bytes 3538952 | tf_op jit(solution)/shard_map/ppermute | solution.py:78
  164.7 22.3 %collective-permute-start.41 = (bf16[4,96,768]{2,1,0:T(8,128)(2,1)S(1)}, bf16[4,96,768]{2,1,0:T(8,128)(2,1)S(1)}, u32[]{:S(2)}, u32[]{:S(2)}) collective-permute-start(bf16[4,96,768]{2,1,0:T(8,128)(2,1)S(1)} %get-tuple-element.582), channel_id=1, source_target_pairs={{0,2},{1,3},{2,0},{3,1},{4,6},{5,7},{6,4},{7,5},{8,10},{9,11},{10,... | collective-permute-start | bytes 1769480 | tf_op jit(solution)/shard_map/ppermute | solution.py:78
  165.3 21.7 %collective-permute-start.42 = (bf16[4,96,768]{2,1,0:T(8,128)(2,1)S(1)}, bf16[4,96,768]{2,1,0:T(8,128)(2,1)S(1)}, u32[]{:S(2)}, u32[]{:S(2)}) collective-permute-start(bf16[4,96,768]{2,1,0:T(8,128)(2,1)S(1)} %get-tuple-element.583), channel_id=1, source_target_pairs={{0,4},{1,5},{2,6},{3,7},{4,0},{5,1},{6,2},{7,3},{8,12},{9,13},{10,... | collective-permute-start | bytes 1769480 | tf_op jit(solution)/shard_map/ppermute | solution.py:78
  165.8 20.9 %collective-permute-start.39 = (bf16[2,96,768]{2,1,0:T(8,128)(2,1)S(1)}, bf16[2,96,768]{2,1,0:T(8,128)(2,1)S(1)}, u32[]{:S(2)}, u32[]{:S(2)}) collective-permute-start(bf16[2,96,768]{2,1,0:T(8,128)(2,1)S(1)} %get-tuple-element.580), channel_id=1, source_target_pairs={{0,2},{1,3},{2,0},{3,1},{4,6},{5,7},{6,4},{7,5},{8,10},{9,11},{10,... | collective-permute-start | bytes 884744 | tf_op jit(solution)/shard_map/ppermute | solution.py:78
  167.3 19.7 %collective-permute-start.40 = (bf16[2,96,768]{2,1,0:T(8,128)(2,1)S(1)}, bf16[2,96,768]{2,1,0:T(8,128)(2,1)S(1)}, u32[]{:S(2)}, u32[]{:S(2)}) collective-permute-start(bf16[2,96,768]{2,1,0:T(8,128)(2,1)S(1)} %get-tuple-element.581), channel_id=1, source_target_pairs={{0,4},{1,5},{2,6},{3,7},{4,0},{5,1},{6,2},{7,3},{8,12},{9,13},{10,... | collective-permute-start | bytes 884744 | tf_op jit(solution)/shard_map/ppermute | solution.py:78
  187.5 8.3 %collective-permute-start.44 = (bf16[2,96,768]{2,1,0:T(8,128)(2,1)S(1)}, bf16[2,96,768]{2,1,0:T(8,128)(2,1)S(1)}, u32[]{:S(2)}, u32[]{:S(2)}) collective-permute-start(bf16[2,96,768]{2,1,0:T(8,128)(2,1)S(1)} %get-tuple-element.601), channel_id=1, source_target_pairs={{0,2},{1,3},{2,0},{3,1},{4,6},{5,7},{6,4},{7,5},{8,10},{9,11},{10,... | collective-permute-start | bytes 884744 | tf_op jit(solution)/shard_map/ppermute | solution.py:78
  197.0 16.3 %collective-permute-start.51 = (bf16[4,96,768]{2,1,0:T(8,128)(2,1)S(1)}, bf16[4,96,768]{2,1,0:T(8,128)(2,1)S(1)}, u32[]{:S(2)}, u32[]{:S(2)}) collective-permute-start(bf16[4,96,768]{2,1,0:T(8,128)(2,1)S(1)} %get-tuple-element.625), channel_id=1, source_target_pairs={{0,2},{1,3},{2,0},{3,1},{4,6},{5,7},{6,4},{7,5},{8,10},{9,11},{10,... | collective-permute-start | bytes 1769480 | tf_op jit(solution)/shard_map/ppermute | solution.py:78
  197.7 16.2 %collective-permute-start.52 = (bf16[4,96,768]{2,1,0:T(8,128)(2,1)S(1)}, bf16[4,96,768]{2,1,0:T(8,128)(2,1)S(1)}, u32[]{:S(2)}, u32[]{:S(2)}) collective-permute-start(bf16[4,96,768]{2,1,0:T(8,128)(2,1)S(1)} %get-tuple-element.626), channel_id=1, source_target_pairs={{0,4},{1,5},{2,6},{3,7},{4,0},{5,1},{6,2},{7,3},{8,12},{9,13},{10,... | collective-permute-start | bytes 1769480 | tf_op jit(solution)/shard_map/ppermute | solution.py:78
  205.2 27.4 %collective-permute-start.49 = (bf16[4,96,768]{2,1,0:T(8,128)(2,1)S(1)}, bf16[4,96,768]{2,1,0:T(8,128)(2,1)S(1)}, u32[]{:S(2)}, u32[]{:S(2)}) collective-permute-start(bf16[4,96,768]{2,1,0:T(8,128)(2,1)S(1)} %get-tuple-element.621), channel_id=1, source_target_pairs={{0,2},{1,3},{2,0},{3,1},{4,6},{5,7},{6,4},{7,5},{8,10},{9,11},{10,... | collective-permute-start | bytes 1769480 | tf_op jit(solution)/shard_map/ppermute | solution.py:78
  206.6 26.0 %collective-permute-start.50 = (bf16[4,96,768]{2,1,0:T(8,128)(2,1)S(1)}, bf16[4,96,768]{2,1,0:T(8,128)(2,1)S(1)}, u32[]{:S(2)}, u32[]{:S(2)}) collective-permute-start(bf16[4,96,768]{2,1,0:T(8,128)(2,1)S(1)} %get-tuple-element.622), channel_id=1, source_target_pairs={{0,4},{1,5},{2,6},{3,7},{4,0},{5,1},{6,2},{7,3},{8,12},{9,13},{10,... | collective-permute-start | bytes 1769480 | tf_op jit(solution)/shard_map/ppermute | solution.py:78
  208.1 18.3 %collective-permute-start.53 = (f32[16,768]{1,0:T(8,128)S(1)}, f32[16,768]{1,0:T(8,128)S(1)}, u32[]{:S(2)}, u32[]{:S(2)}) collective-permute-start(f32[16,768]{1,0:T(8,128)S(1)} %add_select_fusion.3), channel_id=1, source_target_pairs={{0,2},{1,3},{2,0},{3,1},{4,6},{5,7},{6,4},{7,5},{8,10},{9,11},{10,... | collective-permute-start | bytes 147464 | tf_op jit(solution)/shard_map/ppermute | solution.py:78
  227.2 16.2 %collective-permute-start.55 = (bf16[2,2,96,768]{3,2,1,0:T(8,128)(2,1)S(1)}, bf16[2,2,96,768]{3,2,1,0:T(8,128)(2,1)S(1)}, u32[]{:S(2)}, u32[]{:S(2)}) collective-permute-start(bf16[2,2,96,768]{3,2,1,0:T(8,128)(2,1)S(1)} %get-tuple-element.636), channel_id=1, source_target_pairs={{0,8},{1,9},{2,10},{3,11},{4,12},{5,13},{6,14},{7,15},{8,0},{9,1},... | collective-permute-start | bytes 1769480 | tf_op jit(solution)/shard_map/ppermute | solution.py:78
  233.6 14.7 %collective-permute-start.56 = (bf16[1,2,96,768]{3,2,1,0:T(8,128)(2,1)S(1)}, bf16[1,2,96,768]{3,2,1,0:T(8,128)(2,1)S(1)}, u32[]{:S(2)}, u32[]{:S(2)}) collective-permute-start(bf16[1,2,96,768]{3,2,1,0:T(8,128)(2,1)S(1)} %get-tuple-element.639), channel_id=1, source_target_pairs={{0,8},{1,9},{2,10},{3,11},{4,12},{5,13},{6,14},{7,15},{8,0},{9,1},... | collective-permute-start | bytes 884744 | tf_op jit(solution)/shard_map/ppermute | solution.py:78
  250.0 22.0 %collective-permute-start.58 = (bf16[2,96,768]{2,1,0:T(8,128)(2,1)S(1)}, bf16[2,96,768]{2,1,0:T(8,128)(2,1)S(1)}, u32[]{:S(2)}, u32[]{:S(2)}) collective-permute-start(bf16[2,96,768]{2,1,0:T(8,128)(2,1)S(1)} %get-tuple-element.647), channel_id=1, source_target_pairs={{0,16},{1,17},{2,18},{3,19},{4,20},{5,21},{6,22},{7,23},{8,24},{9,... | collective-permute-start | bytes 884744 | tf_op jit(solution)/shard_map/ppermute | solution.py:78
  253.4 18.5 %collective-permute-start.59 = (bf16[1,96,768]{2,1,0:T(8,128)(2,1)S(1)}, bf16[1,96,768]{2,1,0:T(8,128)(2,1)S(1)}, u32[]{:S(2)}, u32[]{:S(2)}) collective-permute-start(bf16[1,96,768]{2,1,0:T(8,128)(2,1)S(1)} %get-tuple-element.648), channel_id=1, source_target_pairs={{0,16},{1,17},{2,18},{3,19},{4,20},{5,21},{6,22},{7,23},{8,24},{9,... | collective-permute-start | bytes 442376 | tf_op jit(solution)/shard_map/ppermute | solution.py:78
  (30 other events, 296.3 us)

commit v4 on v3

--- a/solution.py
+++ b/solution.py
@@ -89,42 +89,35 @@
         self.bufs, self.plan = {}, plan
 
     def part(self, lanes):
-        names = sorted({p[0] for p in self.plan if p[2] in lanes})
-        plan = [[(names.index(b), s, r, at) for b, s, lane, r, at in self.plan if lane == want] for want in lanes]
-        return [self.bufs[n] for n in names], plan
-
-
-Z_ORDER = (0, 2, 1, 3)
+        plan = [p for p in self.plan if p[1] in lanes]
+        names = sorted({p[0] for p in plan})
+        return [self.bufs[n] for n in names], [(names.index(b), lane, lanes[0], k, y) for b, lane, k, y in plan]
 
 
 class Grid:
     parts = 8
 
     @staticmethod
-    def gather(shard, pieces):
+    def gather(shard, pieces, line_later=False):
         own = shard[None]
-        rows = shard.shape[0]
         for base, lane in ((0, 0), (5, 1)):
-            for i, k in enumerate(Z_ORDER):
-                pieces.plan.append((base, i, lane, rows, 2 * k))
-                pieces.plan.append((base + 1, i, lane, rows, 2 * k + 1))
-                pieces.plan.append((base + 2, i, lane + 2, rows, 2 * k))
-                pieces.plan.append((base + 3 + i // 2, i % 2, lane + 2, rows, 2 * k + 1))
+            pieces.plan.append((base, lane, 0, 0))
+            pieces.plan.append((base + 1, lane, 0, 1))
+            pieces.plan.append((base + 2, lane + 2, 0, 0))
+            pieces.plan.append((base + 3, lane + 2, 0, 1))
+            pieces.plan.append((base + 4, lane + 2, 2, 1))
         (far_z,) = yield [(own, PZ2)]
         pair = jnp.concatenate([own, far_z], 0)
         (near_z,) = yield [(pair, PZ1)]
         line = jnp.concatenate([pair, near_z], 0)
-        over_x, over_y, line_far = yield [(line, PX), (line, PY), (line, PC)]
-        pieces.bufs.update({0: line, 1: over_y, 2: over_x, 5: line_far})
-        diag_x, diag_y, over_y_far, over_x_far = yield [
-            (over_y[:2], PX),
-            (over_x[2:], PY),
-            (over_y, PC),
-            (over_x, PC),
-        ]
-        pieces.bufs.update({3: diag_x, 4: diag_y, 6: over_y_far, 7: over_x_far})
-        diag_x_far, diag_y_far = yield [(diag_x, PC), (diag_y, PC)]
-        pieces.bufs.update({8: diag_x_far, 9: diag_y_far})
+        to_core = [(line, PC)]
+        now, later = ([], to_core) if line_later else (to_core, [])
+        over_x, over_y, *rest = yield [(line, PX), (line, PY)] + now
+        diag_x, diag_y, over_y_far, *more = yield [(over_y[:2], PX), (over_x[2:], PY), (over_y, PC)] + later
+        (line_far,) = rest + more
+        pieces.bufs.update({0: line, 1: over_y, 2: over_x, 3: diag_x, 4: diag_y, 5: line_far, 6: over_y_far})
+        over_x_far, diag_x_far, diag_y_far = yield [(over_x, PC), (diag_x, PC), (diag_y, PC)]
+        pieces.bufs.update({7: over_x_far, 8: diag_x_far, 9: diag_y_far})
 
     @staticmethod
     def slot(block, dp):
@@ -132,23 +125,13 @@
         return (place & 1) * 4 + (place & 2) + (place >> 2)
 
     @staticmethod
-    def scatter_sum(far, near, late):
-        if isinstance(far, list):
-            far1, near1 = far[0], near[0]
-            (got1,) = yield [(far1, PC)]
-            out_x, out_y = add_first(near1, got1)
-            from_x, from_y = yield [(out_x, PX), (out_y, PY)]
-            (got0,) = yield [(late["far"], PC)]
-            near0 = late["near"]
-            out_x, out_y = add_second(near1, got1, near0, got0, from_x, from_y)
-        else:
-            (got,) = yield [(far, PC)]
-            out_x, out_y = add_first(near, got)
-            from_x, from_y = yield [(out_x, PX), (out_y, PY)]
-            near0, got0 = near, got
-            out_x, out_y = add_second(near, got, near, got, from_x, from_y)
+    def scatter_sum(far, near):
+        (got,) = yield [(far, PC)]
+        out_x, out_y = add_first(near, got)
+        from_x, from_y = yield [(out_x, PX), (out_y, PY)]
+        out_x, out_y = add_second(near, got, from_x, from_y)
         in_x, in_y = yield [(out_x, PX), (out_y, PY)]
-        return near0, got0, in_x, in_y
+        return near, got, in_x, in_y
 
     @staticmethod
     def scatter_line(*parts):
@@ -167,7 +150,7 @@
 
     @staticmethod
     def sum_max(both, is_top):
-        for perm in (PZ2, PZ1, PX, PY, PC):
+        for perm in (PZ2, PZ1, PC, PX, PY):
             (other,) = yield [(both, perm)]
             both = jnp.where(is_top, jnp.maximum(both, other), both + other)
         return both
@@ -181,11 +164,12 @@
     parts = 1
 
     @staticmethod
-    def gather(shard, pieces):
+    def gather(shard, pieces, line_later=False):
         rows = lax.all_gather(shard, "dp", axis=0, tiled=True)
         full = lax.all_gather(rows, "tensor", axis=0)
-        pieces.plan.extend((0, k, k, full.shape[1], 0) for k in range(full.shape[0]))
-        pieces.bufs[0] = full
+        for k in range(full.shape[0]):
+            pieces.plan.append((k, k, None, None))
+            pieces.bufs[k] = full[k][None]
         return
         yield
 
@@ -194,14 +178,8 @@
         return block
 
     @staticmethod
-    def scatter_sum(far, near, late):
-        if isinstance(far, list):
-            while not late:
-                yield []
-            parts = [late["near"], late["far"], near[0], far[0]]
-        else:
-            parts = [near[0], far[0], near[1], far[1]]
-        grads = jnp.stack(parts).astype(f32)
+    def scatter_sum(far, near):
+        grads = jnp.stack([near[0], far[0], near[1], far[1]]).astype(f32)
         return grads.reshape((4, -1, grads.shape[-1]))
         yield
 
@@ -228,7 +206,6 @@
 
 VM = pl.BlockSpec(memory_space=pltpu.VMEM)
 SM = pl.BlockSpec(memory_space=pltpu.SMEM)
-HB = pl.BlockSpec(memory_space=pl.ANY)
 VMEM_MIB = 14
 
 
@@ -254,31 +231,20 @@
 
 
 def add_first(near, got):
-    part = like((2,) + near.shape[-2:], bf16)
-    near, got = near.reshape((-1, 8) + near.shape[-2:]), got.reshape((-1, 8) + got.shape[-2:])
-
     def first_sums(near, got, out_x, out_y):
-        top = near.shape[0] - 1
         for k in range(2):
-            out_x[k] = (near[top, 4 + k].astype(f32) + got[top, 4 + k].astype(f32)).astype(bf16)
-            out_y[k] = (near[top, 6 + k].astype(f32) + got[top, 6 + k].astype(f32)).astype(bf16)
-
+            out_x[k] = (near[1, 4 + k].astype(f32) + got[1, 4 + k].astype(f32)).astype(bf16)
+            out_y[k] = (near[1, 6 + k].astype(f32) + got[1, 6 + k].astype(f32)).astype(bf16)
+
+    part = like((2,) + near.shape[2:], bf16)
     return glue(first_sums, [part, part], near, got)
 
 
-def add_second(near1, got1, near0, got0, from_x, from_y):
-    rows = near1.shape[-2:]
-    joint = near1 is near0
-    ins = [near1, got1] if joint else [near1, got1, near0, got0]
-    ins = [value.reshape((-1, 8) + rows) for value in ins]
-
-    def second_sums(*refs):
-        *sums, from_x, from_y, out_x, out_y = refs
-        near1, got1, near0, got0 = sums * 2 if joint else sums
-        top = near1.shape[0] - 1
+def add_second(near, got, from_x, from_y):
+    def second_sums(near, got, from_x, from_y, out_x, out_y):
         for k in range(4):
-            over_x = near1[top, k].astype(f32) + got1[top, k].astype(f32)
-            over_y = near0[0, 4 + k].astype(f32) + got0[0, 4 + k].astype(f32)
+            over_x = near[1, k].astype(f32) + got[1, k].astype(f32)
+            over_y = near[0, 4 + k].astype(f32) + got[0, 4 + k].astype(f32)
             if k < 2:
                 over_y = over_y + from_x[k].astype(f32)
             else:
@@ -286,8 +252,8 @@
             out_x[k] = over_x.astype(bf16)
             out_y[k] = over_y.astype(bf16)
 
-    part = like((4,) + rows, bf16)
-    return glue(second_sums, [part, part], *ins, from_x, from_y)
+    part = like((4,) + near.shape[2:], bf16)
+    return glue(second_sums, [part, part], near, got, from_x, from_y)
 
 
 def add_third(*parts):
@@ -321,22 +287,21 @@
     return glue(fourth_sums, [like(shape, bf16), like(shape)], kept, from_z)
 
 
-class Loads:
-    def __init__(self, plan, refs, dst, sems, dp, cols=None):
-        self.plan, self.dst, self.sems, self.dp = plan, dst, sems, dp
-        for lane, pieces in enumerate(plan):
-            for n, (buf, sub, rows, place) in enumerate(pieces):
-                src = refs[buf].at[sub] if cols is None else refs[buf].at[sub, :, pl.ds(*cols)]
-                pltpu.make_async_copy(src, self.spot(lane, rows, place), sems.at[lane, n]).start()
-
-    def spot(self, lane, rows, place):
-        at = pl.multiple_of((self.dp ^ place) * rows, rows) if rows < self.dst.shape[1] else 0
-        return self.dst.at[lane, pl.ds(at, rows)]
-
-    def wait(self, lane):
-        for n, (_, _, rows, place) in enumerate(self.plan[0]):
-            spot = self.spot(lane, rows, place)
-            pltpu.make_async_copy(spot, spot, self.sems.at[lane, n]).wait()
+def assemble(plan, bufs, dst, dp):
+    for buf, lane, first, k, y in plan:
+        src, to = bufs[buf], lane - first
+        if k is None:
+            dst[to] = src[0]
+            continue
+        rows = src.shape[1]
+
+        def move(i, carry):
+            z = k + i
+            place = 4 * (z & 1) + 2 * (z >> 1) + y
+            dst[to, pl.ds(pl.multiple_of((dp ^ place) * rows, rows), rows)] = src[i]
+            return carry
+
+        lax.fori_loop(0, src.shape[0], move, 0)
 
 
 def row(vec):
@@ -386,10 +351,10 @@
 def attn_forward(net, plan, nb, dims, lim, longs, shorts, tokens, bias, *rest):
     blocks, cols, width = dims
     bufs, rest = rest[:nb], rest[nb:]
-    qkv_out, lse_out, in_t, ctx_low, ctx_slope, top_out, weight, in_low, mask, ctx_t, top_ctx, sems = rest
+    qkv_out, lse_out, in_t, ctx_low, ctx_slope, top_out, weight, in_low, mask, ctx_t, top_ctx = rest
     heads = cols // HEAD_DIM
     low_q = 3 * cols + HEAD_DIM
-    loads = Loads(plan, bufs, weight, sems, net.me()[0])
+    assemble(plan, bufs, weight, net.me()[0])
     inputs = tokens[...].astype(f32)
     in_low[...] = jnp.clip(inputs, -lim[0], lim[0]).astype(bf16)
     in_t[...] = in_low[...].T
@@ -400,7 +365,6 @@
     inv_limit = 1.0 / jnp.full((1, 1), lim[1], f32)
 
     def each(lane, carry):
-        loads.wait(lane)
         qkv = (mm(in_low[...], weight[lane, :, :low_q]) + bias[lane, :, :low_q]).astype(bf16)
         qkv_out[lane] = qkv
         for h in range(heads):
@@ -452,13 +416,12 @@
 
 def up_forward(net, plan, nb, first, low_q, lim, mid_low, bias, *rest):
     bufs, rest = rest[:nb], rest[nb:]
-    act_out, slope_out, top_out, weight, top_hid, sems = rest
-    loads = Loads(plan, bufs, weight, sems, net.me()[0])
+    act_out, slope_out, top_out, weight, top_hid = rest
+    assemble(plan, bufs, weight, net.me()[0])
     top_hid[...] = jnp.zeros_like(top_hid)
     inv_limit = 1.0 / jnp.full((1, 1), lim[3], f32)
 
     def each(lane, carry):
-        loads.wait(lane)
         up = mm(mid_low[...], weight[lane]) + bias[first + lane, :, low_q:]
         half = 0.5 * (1.0 + lax.erf(up * root_half))
         hidden = up * half
@@ -474,14 +437,13 @@
 
 def down_both(net, plan, nb, act0, act1, slope0, slope1, middle, cotangent, down_bias, gain, shift, *rest):
     bufs, rest = rest[:nb], rest[nb:]
-    layer_out, grad_out, ffn_t, sums, grad_up, up_sums, weight, acc, ffn_low, sems = rest
-    loads = Loads(plan, bufs, weight, sems, net.me()[0])
+    layer_out, grad_out, ffn_t, sums, grad_up, up_sums, weight, acc, ffn_low = rest
+    assemble(plan, bufs, weight, net.me()[0])
     acc[...] = middle[...] + row(down_bias)
     half = act0.shape[0]
     for act, first in ((act0, 0), (act1, half)):
 
         def each(i, carry):
-            loads.wait(first + i)
             acc[...] += mm_nt(act[i], weight[first + i])
             return carry
 
@@ -552,18 +514,17 @@
     lax.fori_loop(0, blocks, spread, 0)
 
 
-def attn_backward(net, first, dims, longs, shorts, qkv, lse, grad_ctx, *rest):
+def attn_backward(net, dims, longs, shorts, qkv, lse, grad_ctx, in_t, attn_t, ctx_low, *rest):
     blocks, cols, width = dims
-    extra, (out, sums, mask) = (), rest[-3:]
-    if len(rest) > 3:
-        *extra, out, packed, sums, mask = rest
+    up_sums, sums_a, sums_b, tops_a, tops_m, top0, top1, out, far, near, packed, sums, mask = rest
     heads = cols // HEAD_DIM
+    rows = in_t.shape[0] // net.parts
+    start = 3 * cols - HEAD_DIM
+    end = 3 * cols + HEAD_DIM
     fill_mask(mask, longs, shorts)
-    sums[...] = jnp.zeros_like(sums)
-    lane_me = net.me()[1]
-
-    def each(i, carry):
-        lane = first + i
+    dp, lane_me = net.me()
+
+    def each(lane, carry):
         for h in range(heads):
             at = h * HEAD_DIM
             q = qkv[lane, :, at : at + HEAD_DIM]
@@ -577,57 +538,49 @@
             grad_v = mm(shares.astype(bf16), grad)
             grad_k = mm(grad_scores, q) * score_scale
             grad_q = (mm_tn(k, grad_scores) * score_scale).T
-            out[i, :, at : at + HEAD_DIM] = grad_q.astype(bf16)
-            out[i, :, cols + at : cols + at + HEAD_DIM] = grad_k.astype(bf16)
-            out[i, :, 2 * cols + at : 2 * cols + at + HEAD_DIM] = grad_v.astype(bf16)
-        out[i, :, 3 * cols :] = jnp.zeros((out.shape[1], HEAD_DIM), bf16)
-        sums[lane ^ lane_me] = col_sum(out[i].astype(f32))
+            out[lane, :, at : at + HEAD_DIM] = grad_q.astype(bf16)
+            out[lane, :, cols + at : cols + at + HEAD_DIM] = grad_k.astype(bf16)
+            out[lane, :, 2 * cols + at : 2 * cols + at + HEAD_DIM] = grad_v.astype(bf16)
+        out[lane, :, 3 * cols :] = jnp.zeros((out.shape[1], HEAD_DIM), bf16)
+        sums[lane ^ lane_me] = col_sum(out[lane].astype(f32))
         return carry
 
-    lax.fori_loop(0, out.shape[0], each, 0)
-    if extra:
-        more, up_sums, sums_a, sums_b, tops_a, tops_m, top0, top1 = extra
-        packed[...] = jnp.zeros_like(packed)
-        for j in range(blocks):
-            packed[j : j + 1, :] = up_sums[j]
-            packed[blocks + j : blocks + j + 1, : sums.shape[2]] = sums[j] + more[j]
-        packed[2 * blocks : 2 * blocks + 3, :] = sums_a[0:3, :]
-        packed[2 * blocks + 3 : 2 * blocks + 6, :] = sums_b[0:3, :]
-        tops = (tops_a[0:1, :], tops_a[1:2, :], tops_m[0:1, :], jnp.maximum(top0[0:1, :], top1[0:1, :]))
-        for j, top in enumerate(tops):
-            packed[2 * blocks + 6 : 2 * blocks + 7, 128 * j : 128 * j + 128] = top
-
-
-def in_weight_grad(net, first, dims, in_t, attn_t, grad_qkv, ctx_low, far, near):
+    lax.fori_loop(0, blocks, each, 0)
+
+    def weights(x, carry):
+        for core, to in ((1, far), (0, near)):
+            left = mm(in_t[...], out[2 * x + core])
+            right = mm(attn_t[...], ctx_low[2 * x + core])
+            mixed = (left[:, start:] + right[:, : end - start]).astype(bf16)
+            for block in range(net.parts):
+                rs = slice(block * rows, (block + 1) * rows)
+                place = net.slot(block, dp)
+                to[x, place, :, :start] = left[rs, :start].astype(bf16)
+                to[x, place, :, start:end] = mixed[rs]
+                to[x, place, :, end:] = right[rs, end - start :].astype(bf16)
+        return carry
+
+    lax.fori_loop(0, far.shape[0], weights, 0)
+    packed[...] = jnp.zeros_like(packed)
+    for j in range(blocks):
+        packed[j : j + 1, :] = up_sums[j]
+        packed[blocks + j : blocks + j + 1, : sums.shape[2]] = sums[j]
+    packed[2 * blocks : 2 * blocks + 3, :] = sums_a[0:3, :]
+    packed[2 * blocks + 3 : 2 * blocks + 6, :] = sums_b[0:3, :]
+    tops = (tops_a[0:1, :], tops_a[1:2, :], tops_m[0:1, :], jnp.maximum(top0[0:1, :], top1[0:1, :]))
+    for j, top in enumerate(tops):
+        packed[2 * blocks + 6 : 2 * blocks + 7, 128 * j : 128 * j + 128] = top
+
+
+def token_backward(dims, lim, grad_qkv, grad_first, tokens, weight, out, acc):
     blocks, cols, width = dims
-    rows = in_t.shape[0] // net.parts
-    at = 3 * cols - HEAD_DIM
-    end = 3 * cols + HEAD_DIM
-    dp = net.me()[0]
-    for i, out in ((1, far), (0, near)):
-        left = mm(in_t[...], grad_qkv[i])
-        right = mm(attn_t[...], ctx_low[first + i])
-        mixed = (left[:, at:] + right[:, : end - at]).astype(bf16)
-        for block in range(net.parts):
-            rs = slice(block * rows, (block + 1) * rows)
-            place = net.slot(block, dp)
-            out[place, :, :at] = left[rs, :at].astype(bf16)
-            out[place, :, at:end] = mixed[rs]
-            out[place, :, end:] = right[rs, end - at :].astype(bf16)
-
-
-def token_backward(dims, lim, grad_qkv0, grad_qkv1, grad_first, tokens, weight, out, acc):
-    blocks, cols, width = dims
-    wide = 3 * cols + HEAD_DIM
     acc[...] = jnp.zeros_like(acc)
-    half = grad_qkv0.shape[0]
-    for grad, first in ((grad_qkv0, 0), (grad_qkv1, half)):
-
-        def each(i, carry):
-            acc[...] += mm_nt(grad[i], weight[first + i, :, :wide])
-            return carry
-
-        lax.fori_loop(0, half, each, 0)
+
+    def each(lane, carry):
+        acc[...] += mm_nt(grad_qkv[lane], weight[lane, :, : 3 * cols + HEAD_DIM])
+        return carry
+
+    lax.fori_loop(0, blocks, each, 0)
     inputs = tokens[...].astype(f32)
     out[...] = (grad_first[...] + jnp.where(jnp.abs(inputs) <= lim[0], acc[...], 0.0)).astype(bf16)
 
@@ -674,22 +627,19 @@
         )
         job_b = Job(net.gather_lane(bias_row[None]))
         job_u = Job(net.gather(up_weight.astype(bf16), pieces_u))
-        job_d = Job(net.gather(down_weight.T.astype(bf16), pieces_d))
+        job_d = Job(net.gather(down_weight.T.astype(bf16), pieces_d, True))
 
         def vmem(*shape, dtype=f32):
             return pltpu.VMEM(shape, dtype)
 
-        def sems(plan):
-            return pltpu.SemaphoreType.DMA((len(plan), len(plan[0])))
-
         unit = 2 * rows * width * width * blocks
         moved = 2 * width * width * blocks
 
         step((), None, [job_a, job_b], [job_a, job_b])
-        step((), None, [job_a, job_b], [job_a, job_b])
+        step((), None, [job_a, job_u, job_b], [job_a, job_u, job_b])
         step((), None, [job_a, job_u], [job_a, job_u])
-        step((), None, [job_a, job_u, job_d], [job_a])
-        step((), None, [job_a], [job_a, job_u, job_d])
+        step((), None, [job_a, job_d], [job_a, job_d])
+        step((), None, [job_u, job_a], [job_a])
         biases = job_b.value
 
         bufs, plan = pieces_a.part(every)
@@ -698,7 +648,7 @@
             call(
                 functools.partial(attn_forward, net, plan, len(bufs), dims),
                 "attn_forward",
-                [SM] * 3 + [VM] * 2 + [HB] * len(bufs),
+                [SM] * 3 + [VM] * 2 + [VM] * len(bufs),
                 [
                     like((blocks, rows, wide), bf16),
                     like((blocks, 8, rows)),
@@ -708,11 +658,11 @@
                     like((8, 128)),
                     like((blocks, width, 4 * cols), bf16),
                 ],
-                [vmem(rows, width, dtype=bf16), vmem(rows, rows), vmem(out_cols, rows), vmem(8, out_cols), sems(plan)],
+                [vmem(rows, width, dtype=bf16), vmem(rows, rows), vmem(out_cols, rows), vmem(8, out_cols)],
                 4 * unit,
                 3 * moved,
             ),
-            [job_u, job_d],
+            [job_d],
             [job_u, job_d],
         )
         normed, inv, middle, mid_slope, mid_low, mid_t, tops_m = step(
@@ -745,14 +695,14 @@
                 call(
                     functools.partial(up_forward, net, plan, len(bufs), lanes[0], wide),
                     f"up_forward_{lanes[0]}",
-                    [SM] + [VM] * 2 + [HB] * len(bufs),
+                    [SM] + [VM] * 2 + [VM] * len(bufs),
                     [
                         like((half, rows, up_cols), bf16),
                         like((half, rows, up_cols)),
                         like((8, 128)),
                         like((half, width, up_cols), bf16),
                     ],
-                    [vmem(8, up_cols), sems(plan)],
+                    [vmem(8, up_cols)],
                     2 * unit,
                     2 * moved,
                 ),
@@ -760,8 +710,9 @@
                 finish,
             )
 
-        act0, slope0, top0, weight_u0 = up_part(every[:half], [job_u], [job_u, job_d])
-        act1, slope1, top1, weight_u1 = up_part(every[half:], [job_d], [job_d])
+        act0, slope0, top0, weight_u0 = up_part(every[:half], [job_u], [job_u])
+        act1, slope1, top1, weight_u1 = up_part(every[half:], [], [job_d])
+        step((), None, [job_d], [job_d])
         step((), None, [job_d], [job_d])
         bufs_d, plan_d = pieces_d.part(every)
         layer_out, grad_second, ffn_t, sums_b, grad_up, up_sums = step(
@@ -769,7 +720,7 @@
             call(
                 functools.partial(down_both, net, plan_d, len(bufs_d)),
                 "down_both",
-                [VM] * 9 + [HB] * len(bufs_d),
+                [VM] * 9 + [VM] * len(bufs_d),
                 [
                     like((rows, width), bf16),
                     like((rows, width)),
@@ -782,7 +733,6 @@
                     vmem(blocks, width, up_cols, dtype=bf16),
                     vmem(rows, width),
                     vmem(rows, width, dtype=bf16),
-                    sems(plan_d),
                 ],
                 2 * unit,
                 4 * moved,
@@ -808,9 +758,8 @@
                 finish,
             )
 
-        late_a = {}
-        sum_d = Job(net.scatter_sum(*grad_of("down_grad", ffn_t, (act0, act1)), None))
-        sum_u = Job(net.scatter_sum(*grad_of("up_grad", mid_t, (grad_up,), [sum_d], [sum_d]), None))
+        sum_d = Job(net.scatter_sum(*grad_of("down_grad", ffn_t, (act0, act1))))
+        sum_u = Job(net.scatter_sum(*grad_of("up_grad", mid_t, (grad_up,), [sum_d], [sum_d])))
         grad_first, attn_t, grad_ctx, sums_a = step(
             (grad_up, grad_second, mid_slope, normed, inv, first_gain, ctx_slope, weight_u0, weight_u1, weight_a),
             call(
@@ -831,70 +780,48 @@
             [sum_d, sum_u],
         )
 
-        def back_part(first, extra=(), start=(), finish=()):
-            return step(
-                (long_lengths, short_lengths, qkv, lse, grad_ctx, *extra),
-                call(
-                    functools.partial(attn_backward, net, first, dims),
-                    f"attn_backward_{first}",
-                    [SM] * 2 + [VM] * (3 + len(extra)),
-                    [like((half, rows, wide), bf16), like((16, width)) if extra else like((blocks, 1, wide))],
-                    ([vmem(blocks, 1, wide)] if extra else []) + [vmem(rows, rows)],
-                    4 * unit,
-                    2 * moved,
-                ),
-                start,
-                finish,
-            )
-
-        def in_part(grad_qkv, first, start=(), finish=()):
-            return step(
-                (in_t, attn_t, grad_qkv, ctx_low),
-                call(
-                    functools.partial(in_weight_grad, net, first, dims),
-                    f"in_grad_{first}",
-                    [VM] * 4,
-                    [grad_shape, grad_shape],
-                    (),
-                    unit // 2,
-                    moved,
-                ),
-                start,
-                finish,
-            )
-
-        grad_qkv1, q_sums1 = back_part(half, (), [sum_u, sum_d], [])
-        far, near = in_part(grad_qkv1, half)
-        sum_a = Job(net.scatter_sum([far], [near], late_a))
-        extra = (q_sums1, up_sums, sums_a, sums_b, tops_a, tops_m, top0, top1)
-        grad_qkv0, packed = back_part(0, extra, [sum_a], [sum_u, sum_d, sum_a])
+        grad_qkv, far, near, packed = step(
+            (long_lengths, short_lengths, qkv, lse, grad_ctx, in_t, attn_t, ctx_low)
+            + (up_sums, sums_a, sums_b, tops_a, tops_m, top0, top1),
+            call(
+                functools.partial(attn_backward, net, dims),
+                "attn_backward",
+                [SM] * 2 + [VM] * 13,
+                [like((blocks, rows, wide), bf16), both_shape, both_shape, like((16, width))],
+                [vmem(blocks, 1, wide), vmem(rows, rows)],
+                4 * unit,
+                2 * moved,
+            ),
+            [sum_u, sum_d],
+            [sum_u, sum_d],
+        )
+        sum_a = Job(net.scatter_sum(far, near))
         is_top = (jnp.arange(packed.shape[0]) == 2 * blocks + 6)[:, None]
         sum_s = Job(net.sum_max(packed, is_top))
-        far, near = in_part(grad_qkv0, 0, [sum_a, sum_u, sum_s], [])
-        late_a.update(far=far, near=near)
-        step((), None, [], [sum_a, sum_s])
+        line_d = Job(net.scatter_line(sum_d.value))
         tokens_grad = step(
-            (act_ranges, grad_qkv0, grad_qkv1, grad_first, tokens, weight_a),
+            (act_ranges, grad_qkv, grad_first, tokens, weight_a),
             call(
                 functools.partial(token_backward, dims),
                 "token_backward",
-                [SM] + [VM] * 5,
+                [SM] + [VM] * 4,
                 [like((rows, width), bf16)],
                 [vmem(rows, width)],
                 unit,
                 2 * moved,
             ),
-            [sum_a, sum_s],
-            [sum_a, sum_s],
+            [sum_a, sum_u, line_d, sum_s],
+            [sum_a, line_d, sum_s],
         )[0]
-        step((), None, [sum_a, sum_s], [sum_u, sum_s])
-        line_du = Job(net.scatter_line(sum_d.value, sum_u.value))
-        step((), None, [line_du, sum_s], [sum_a, sum_s])
+        step((), None, [sum_a, sum_s], [sum_a, sum_u, sum_s])
+        line_u = Job(net.scatter_line(sum_u.value))
+        step((), None, [sum_a, line_d, line_u, sum_s], [line_d, line_u, sum_s])
+        step((), None, [line_u, sum_s], [sum_a, sum_s])
         line_a = Job(net.scatter_line(sum_a.value))
-        step((), None, [line_a, sum_s], [line_du, line_a, sum_s])
-        step((), None, [line_a, line_du], [line_du, line_a])
-
-        down_grad, up_grad = line_du.value
+        step((), None, [line_a, sum_s], [line_u, line_a, sum_s])
+        step((), None, [line_a], [line_a])
+
+        (down_grad,), (up_grad,) = line_d.value, line_u.value
         down_grad = down_grad.T
         (a_grad,), packed = line_a.value, sum_s.value
         qkv_grad = jnp.stack([a_grad[:, j * cols : (j + 1) * cols] for j in range(3)])

time: 278 us -> 227 us (0.82)
  waiting for transfers between devices: 116 us -> 85.4 us
  Pallas kernels: 85 us -> 65.8 us
  starting transfers between devices: 56.8 us -> 63.2 us
  local copies, waits for them, and re-layouts: 8.88 us -> 4.42 us
    ppermute x60 -> x61, waiting for transfers between devices: 116 us -> 85.4 us  [step(): lax.ppermute(v, ALL, perm)]
    pallas_call x13 -> x10, Pallas kernels: 82.5 us -> 63.3 us  [step(): outs = run(*ins) if run else ins]
    ppermute x60 -> x61, starting transfers between devices: 56.8 us -> 63.2 us  [step(): lax.ppermute(v, ALL, perm)]
    unnamed x38 -> x32, local copies, waits for them, and re-layouts: 6.28 us -> 1.82 us
  transfers between devices with their start and end apart: 60 -> 61, of which waited for: 32 -> 33; matrix products, arithmetic and copies ran while one was open for 1% -> 2% of each run, Pallas kernels for 21% -> 23%
where the time goes in v4:
time: 227 us; the launch traced here: 226 us
  waiting for transfers between devices  85.4 us (38%)
  Pallas kernels  65.8 us (29%)
  starting transfers between devices  63.2 us (28%)
  other arithmetic  5.68 us (3%)
  local copies, waits for them, and re-layouts  4.42 us (2%)
    ppermute x61, waiting for transfers between devices, step(): lax.ppermute(v, ALL, perm)  85.4 us
    pallas_call x10, Pallas kernels, step(): outs = run(*ins) if run else ins  63.3 us
    ppermute x61, starting transfers between devices, step(): lax.ppermute(v, ALL, perm)  63.2 us
  transfers between devices with their start and end apart: 61, of which 33 were waited for; matrix products, arithmetic and copies ran while one was open for 2% of the time, Pallas kernels for 23%

profile of v4, /device:TPU:0, one launch (start us, length us, event | category | flops | bytes accessed | tf_op | source)
XLA Modules:
  0.0 226.4 jit_solution(7145529960436460028)
XLA Ops:
  4.3 4.1 %collective-permute-start = (bf16[1,96,768]{2,1,0:T(8,128)(2,1)S(1)}, bf16[1,96,768]{2,1,0:T(8,128)(2,1)S(1)}, u32[]{:S(2)}, u32[]{:S(2)}) collective-permute-start(bf16[1,96,768]{2,1,0:T(8,128)(2,1)S(1)} %pad_maximum_fusion.7), channel_id=1, source_target_pairs={{0,16},{1,17},{2,18},{3,19},{4,20},{5,21},{6,22},{7,23},{8,24},{9,... | collective-permute-start | bytes 442376 | tf_op jit(solution)/shard_map/ppermute | solution.py:78
  8.5 1.5 collective-permute-start.1
  12.1 3.4 %collective-permute-done = bf16[1,96,768]{2,1,0:T(8,128)(2,1)S(1)} collective-permute-done((bf16[1,96,768]{2,1,0:T(8,128)(2,1)S(1)}, bf16[1,96,768]{2,1,0:T(8,128)(2,1)S(1)}, u32[]{:S(2)}, u32[]{:S(2)}) %collective-permute-start) | collective-permute-done | bytes 147488 | tf_op jit(solution)/shard_map/ppermute | solution.py:78
  16.4 3.4 %collective-permute-start.3 = (bf16[1,96,768]{2,1,0:T(8,128)(2,1)S(1)}, bf16[1,96,768]{2,1,0:T(8,128)(2,1)S(1)}, u32[]{:S(2)}, u32[]{:S(2)}) collective-permute-start(bf16[1,96,768]{2,1,0:T(8,128)(2,1)S(1)} %convert_bitcast_fusion.1), channel_id=1, source_target_pairs={{0,16},{1,17},{2,18},{3,19},{4,20},{5,21},{6,22},{7,23},{8,24},{9,... | collective-permute-start | bytes 442376 | tf_op jit(solution)/shard_map/ppermute | solution.py:78
  20.9 5.1 %collective-permute-done.3 = bf16[1,96,768]{2,1,0:T(8,128)(2,1)S(1)} collective-permute-done((bf16[1,96,768]{2,1,0:T(8,128)(2,1)S(1)}, bf16[1,96,768]{2,1,0:T(8,128)(2,1)S(1)}, u32[]{:S(2)}, u32[]{:S(2)}) %collective-permute-start.3) | collective-permute-done | bytes 147488 | tf_op jit(solution)/shard_map/ppermute | solution.py:78
  27.2 1.3 collective-permute-start.5
  28.5 1.5 collective-permute-start.6
  30.1 3.3 %collective-permute-start.8 = (bf16[2,96,768]{2,1,0:T(8,128)(2,1)S(1)}, bf16[2,96,768]{2,1,0:T(8,128)(2,1)S(1)}, u32[]{:S(2)}, u32[]{:S(2)}) collective-permute-start(bf16[2,96,768]{2,1,0:T(8,128)(2,1)S(1)} %pad_maximum_fusion.4), channel_id=1, source_target_pairs={{0,8},{1,9},{2,10},{3,11},{4,12},{5,13},{6,14},{7,15},{8,0},{9,1},... | collective-permute-start | bytes 884744 | tf_op jit(solution)/shard_map/ppermute | solution.py:78
  33.4 7.7 %collective-permute-done.8 = bf16[2,96,768]{2,1,0:T(8,128)(2,1)S(1)} collective-permute-done((bf16[2,96,768]{2,1,0:T(8,128)(2,1)S(1)}, bf16[2,96,768]{2,1,0:T(8,128)(2,1)S(1)}, u32[]{:S(2)}, u32[]{:S(2)}) %collective-permute-start.8) | collective-permute-done | bytes 294944 | tf_op jit(solution)/shard_map/ppermute | solution.py:78
  42.0 1.6 collective-permute-start.10
  44.1 3.4 %collective-permute-start.12 = (bf16[1,96,768]{2,1,0:T(8,128)(2,1)S(1)}, bf16[1,96,768]{2,1,0:T(8,128)(2,1)S(1)}, u32[]{:S(2)}, u32[]{:S(2)}) collective-permute-start(bf16[1,96,768]{2,1,0:T(8,128)(2,1)S(1)} %convert_bitcast_fusion), channel_id=1, source_target_pairs={{0,16},{1,17},{2,18},{3,19},{4,20},{5,21},{6,22},{7,23},{8,24},{9,... | collective-permute-start | bytes 442376 | tf_op jit(solution)/shard_map/ppermute | solution.py:78
  47.6 3.8 %collective-permute-done.12 = bf16[1,96,768]{2,1,0:T(8,128)(2,1)S(1)} collective-permute-done((bf16[1,96,768]{2,1,0:T(8,128)(2,1)S(1)}, bf16[1,96,768]{2,1,0:T(8,128)(2,1)S(1)}, u32[]{:S(2)}, u32[]{:S(2)}) %collective-permute-start.12) | collective-permute-done | bytes 147488 | tf_op jit(solution)/shard_map/ppermute | solution.py:78
  55.5 4.4 %collective-permute-start.19 = (bf16[2,96,768]{2,1,0:T(8,128)(2,1)S(1)}, bf16[2,96,768]{2,1,0:T(8,128)(2,1)S(1)}, u32[]{:S(2)}, u32[]{:S(2)}) collective-permute-start(bf16[2,96,768]{2,1,0:T(8,128)(2,1)S(1)} %pad_maximum_fusion.5), channel_id=1, source_target_pairs={{0,8},{1,9},{2,10},{3,11},{4,12},{5,13},{6,14},{7,15},{8,0},{9,1},... | collective-permute-start | bytes 884744 | tf_op jit(solution)/shard_map/ppermute | solution.py:78
  59.9 11.5 %attn_forward.1 = (bf16[4,512,640]{2,1,0:T(8,128)(2,1)S(1)}, f32[4,8,512]{2,1,0:T(8,128)S(1)}, bf16[768,512]{1,0:T(8,128)(2,1)S(1)}, bf16[4,512,256]{2,1,0:T(8,1...) custom-call(f32[4]{0:T(128)S(1)} %copy-done.2, ...), custom_call_target="tpu_custom_call" | custom-call | flops 9663676416 | bytes 14155776 | tf_op jit(solution)/shard_map/attn_forward/pallas_call | solution.py:79
  73.1 1.5 collective-permute-start.21
  74.7 3.3 %attn_finish.1 = (f32[512,768]{1,0:T(8,128)S(1)}, f32[512,1]{1,0:T(8,128)S(1)}, f32[512,768]{1,0:T(8,128)S(1)}, f32[512,768]{1,0:T(8,128)S(1)}, bf16[512,768]{1,...) custom-call(f32[4]{0:T(128)S(1)} %copy-done.2, ...), custom_call_target="tpu_custom_call" | custom-call | flops 4831838208 | bytes 9437184 | tf_op jit(solution)/shard_map/attn_finish/pallas_call | solution.py:79
  78.0 3.2 %collective-permute-done.20.rest_1_ = bf16[2,96,768]{2,1,0:T(8,128)(2,1)S(1)} collective-permute-done((bf16[2,96,768]{2,1,0:T(8,128)(2,1)S(1)}, bf16[2,96,768]{2,1,0:T(8,128)(2,1)S(1)}, u32[]{:S(2)}, u32[]{:S(2)}) %collective-permute-start.20) | collective-permute-done | bytes 294944 | tf_op jit(solution)/shard_map/ppermute | solution.py:78
  84.7 3.9 %up_forward_0.1 = (bf16[2,512,768]{2,1,0:T(8,128)(2,1)S(1)}, f32[2,512,768]{2,1,0:T(8,128)S(1)}, f32[8,128]{1,0:T(8,128)S(1)}, bf16[2,768,768]{2,1,0:T(8,128)(2,1)S(1)}) custom-call(f32[4]{0:T(128)S(1)} %copy-done.2, bf16[512,768]{1,0:T(8,128)(2,1)S(1)} %get-tuple-element.428.mid_low, f32[4,1,1408]{2,1,0:T(1,128)S(1)} %bitcast.39, ...), custom_call_target="tpu_custom_call" | custom-call | flops 4831838208 | bytes 9437184 | tf_op jit(solution)/shard_map/up_forward_0/pallas_call | solution.py:79
  88.8 3.9 %up_forward_2.1 = (bf16[2,512,768]{2,1,0:T(8,128)(2,1)S(1)}, f32[2,512,768]{2,1,0:T(8,128)S(1)}, f32[8,128]{1,0:T(8,128)S(1)}, bf16[2,768,768]{2,1,0:T(8,128)(2,1)S(1)}) custom-call(f32[4]{0:T(128)S(1)} %copy-done.2, bf16[512,768]{1,0:T(8,128)(2,1)S(1)} %get-tuple-element.428.mid_low, f32[4,1,1408]{2,1,0:T(1,128)S(1)} %bitcast.40, ...), custom_call_target="tpu_custom_call" | custom-call | flops 4831838208 | bytes 9437184 | tf_op jit(solution)/shard_map/up_forward_2/pallas_call | solution.py:79
  92.7 5.2 %collective-permute-done.26.rest_2_ = bf16[4,96,768]{2,1,0:T(8,128)(2,1)S(1)} collective-permute-done((bf16[4,96,768]{2,1,0:T(8,128)(2,1)S(1)}, bf16[4,96,768]{2,1,0:T(8,128)(2,1)S(1)}, u32[]{:S(2)}, u32[]{:S(2)}) %collective-permute-start.26) | collective-permute-done | bytes 589856 | tf_op jit(solution)/shard_map/ppermute | solution.py:78
  100.3 1.5 collective-permute-start.29
  101.8 6.2 %collective-permute-done.28.rest_3_ = bf16[2,96,768]{2,1,0:T(8,128)(2,1)S(1)} collective-permute-done((bf16[2,96,768]{2,1,0:T(8,128)(2,1)S(1)}, bf16[2,96,768]{2,1,0:T(8,128)(2,1)S(1)}, u32[]{:S(2)}, u32[]{:S(2)}) %collective-permute-start.28) | collective-permute-done | bytes 294944 | tf_op jit(solution)/shard_map/ppermute | solution.py:78
  109.6 1.8 collective-permute-done.33.rest_8_
  111.9 8.8 %down_both.1 = (bf16[512,768]{1,0:T(8,128)(2,1)}, f32[512,768]{1,0:T(8,128)S(1)}, bf16[768,512]{1,0:T(8,128)(2,1)S(1)}, f32[8,768]{1,0:T(8,128)S(1)}, bf16[4,512...) custom-call(bf16[2,512,768]{2,1,0:T(8,128)(2,1)S(1)} %get-tuple-element.494.act0.rest_0_, ...), custom_call_target="tpu_custom_call" | custom-call | flops 4831838208 | bytes 18874368 | tf_op jit(solution)/shard_map/down_both/pallas_call | solution.py:79
  120.7 2.7 %down_grad.1 = (bf16[2,8,96,768]{3,2,1,0:T(8,128)(2,1)S(1)}, bf16[2,8,96,768]{3,2,1,0:T(8,128)(2,1)S(1)}) custom-call(bf16[768,512]{1,0:T(8,128)(2,1)S(1)} %get-tuple-element.493.left_t, bf16[2,512,768]{2,1,0:T(8,128)(2,1)S(1)} %get-tuple-element.494.act0.rest_0_, bf16[2,512,768]{2,1,0:T(8,128)(2,1)S(1)} %get-tuple-element.495.act1.rest_1_), custom_call_target="tpu_custom_call" | custom-call | flops 2415919104 | bytes 4718592 | tf_op jit(solution)/shard_map/down_grad/pallas_call | solution.py:79
  123.6 2.7 %up_grad.1 = (bf16[2,8,96,768]{3,2,1,0:T(8,128)(2,1)S(1)}, bf16[2,8,96,768]{3,2,1,0:T(8,128)(2,1)S(1)}) custom-call(bf16[768,512]{1,0:T(8,128)(2,1)S(1)} %get-tuple-element.499.left_t, bf16[4,512,768]{2,1,0:T(8,128)(2,1)S(1)} %get-tuple-element.508.rest_0_.grad_up), custom_call_target="tpu_custom_call" | custom-call | flops 2415919104 | bytes 4718592 | tf_op jit(solution)/shard_map/up_grad/pallas_call | solution.py:79
  126.3 1.7 collective-permute-done.35.got.refs_1_
  130.4 6.2 %mid_backward.1 = (f32[512,768]{1,0:T(8,128)S(1)}, bf16[768,512]{1,0:T(8,128)(2,1)S(1)}, bf16[4,512,256]{2,1,0:T(8,128)(2,1)S(1)}, f32[8,768]{1,0:T(8,128)S(1)}) custom-call(bf16[4,512,768]{2,1,0:T(8,128)(2,1)S(1)} %get-tuple-element.508.rest_0_.grad_up, f32[512,768]{1,0:T(8,128)S(1)} %get-tuple-element.509.grad_second, ...), custom_call_target="tpu_custom_call" | custom-call | flops 3221225472 | bytes 14155776 | tf_op jit(solution)/shard_map/mid_backward/pallas_call | solution.py:79
  140.0 1.5 collective-permute-start.42
  142.8 15.1 %attn_backward.1 = (bf16[4,512,640]{2,1,0:T(8,128)(2,1)S(1)}, bf16[2,8,96,768]{3,2,1,0:T(8,128)(2,1)S(1)}, bf16[2,8,96,768]{3,2,1,0:T(8,128)(2,1)S(1)}, f32[16,768]{1,0:T(8,128)S(1)}) custom-call(s32[1]{0:T(128)S(6)} %copy.35.longs, s32[12]{0:T(128)S(1)} %copy-done.9, bf16[4,512,640]{2,1,0:T(8,128)(2,1)S(1)} %copy-done.11, ...), custom_call_target="tpu_custom_call" | custom-call | flops 9663676416 | bytes 9437184 | tf_op jit(solution)/shard_map/attn_backward/pallas_call | solution.py:79
  157.9 1.7 collective-permute-done.39.from_x
  161.3 3.1 %collective-permute-start.44 = (bf16[1,2,96,768]{3,2,1,0:T(8,128)(2,1)S(1)}, bf16[1,2,96,768]{3,2,1,0:T(8,128)(2,1)S(1)}, u32[]{:S(2)}, u32[]{:S(2)}) collective-permute-start(bf16[1,2,96,768]{3,2,1,0:T(8,128)(2,1)S(1)} %get-tuple-element.583), channel_id=1, source_target_pairs={{0,8},{1,9},{2,10},{3,11},{4,12},{5,13},{6,14},{7,15},{8,0},{9,1},... | collective-permute-start | bytes 884744 | tf_op jit(solution)/shard_map/ppermute | solution.py:78
  164.4 1.7 collective-permute-start.45
  166.1 1.5 collective-permute-start.48
  168.1 5.1 %token_backward.1 = bf16[512,768]{1,0:T(8,128)(2,1)} custom-call(f32[4]{0:T(128)S(1)} %copy-done.2, bf16[4,512,640]{2,1,0:T(8,128)(2,1)S(1)} %get-tuple-element.578.grad_qkv, f32[512,768]{1,0:T(8,128)S(1)} %get-tuple-element.579.grad_first, bf16[512,768]{1,0:T(8,128)(2,1)S(1)} %copy-done, bf16[4,768,768]{2,1,0:T(8,128)(2,1)S(1)} %get-tuple-element.581.weight.out_weight), custom_call_target="tpu_custom_call" | custom-call | flops 2415919104 | bytes 9437184 | tf_op jit(solution)/shard_map/token_backward/pallas_call | solution.py:79
  174.0 1.5 collective-permute-start.47
  175.5 1.5 collective-permute-start.50
  177.0 5.3 %collective-permute-done.48.refs_2_ = bf16[4,96,768]{2,1,0:T(8,128)(2,1)S(1)} collective-permute-done((bf16[4,96,768]{2,1,0:T(8,128)(2,1)S(1)}, bf16[4,96,768]{2,1,0:T(8,128)(2,1)S(1)}, u32[]{:S(2)}, u32[]{:S(2)}) %collective-permute-start.48) | collective-permute-done | bytes 589856 | tf_op jit(solution)/shard_map/ppermute | solution.py:78
  182.3 1.5 collective-permute-done.49.refs_3_
  183.8 3.8 %collective-permute-done.46.from_x = bf16[2,96,768]{2,1,0:T(8,128)(2,1)S(1)} collective-permute-done((bf16[2,96,768]{2,1,0:T(8,128)(2,1)S(1)}, bf16[2,96,768]{2,1,0:T(8,128)(2,1)S(1)}, u32[]{:S(2)}, u32[]{:S(2)}) %collective-permute-start.46) | collective-permute-done | bytes 294944 | tf_op jit(solution)/shard_map/ppermute | solution.py:78
  193.4 5.5 %collective-permute-done.53 = bf16[1,96,768]{2,1,0:T(8,128)(2,1)S(1)} collective-permute-done((bf16[1,96,768]{2,1,0:T(8,128)(2,1)S(1)}, bf16[1,96,768]{2,1,0:T(8,128)(2,1)S(1)}, u32[]{:S(2)}, u32[]{:S(2)}) %collective-permute-start.53) | collective-permute-done | bytes 147488 | tf_op jit(solution)/shard_map/ppermute | solution.py:78
  198.9 2.0 collective-permute-done.54.from_z
  201.0 1.5 collective-permute-start.56
  202.5 2.6 %collective-permute-done.56 = f32[16,768]{1,0:T(8,128)S(1)} collective-permute-done((f32[16,768]{1,0:T(8,128)S(1)}, f32[16,768]{1,0:T(8,128)S(1)}, u32[]{:S(2)}, u32[]{:S(2)}) %collective-permute-start.56) | collective-permute-done | bytes 49184 | tf_op jit(solution)/shard_map/ppermute | solution.py:78
  207.2 1.5 collective-permute-start.59
  208.8 5.2 %collective-permute-done.57 = bf16[1,96,768]{2,1,0:T(8,128)(2,1)S(1)} collective-permute-done((bf16[1,96,768]{2,1,0:T(8,128)(2,1)S(1)}, bf16[1,96,768]{2,1,0:T(8,128)(2,1)S(1)}, u32[]{:S(2)}, u32[]{:S(2)}) %collective-permute-start.57) | collective-permute-done | bytes 147488 | tf_op jit(solution)/shard_map/ppermute | solution.py:78
  214.0 2.2 collective-permute-done.58.from_z
  220.3 4.4 %collective-permute-done.60 = bf16[1,96,768]{2,1,0:T(8,128)(2,1)S(1)} collective-permute-done((bf16[1,96,768]{2,1,0:T(8,128)(2,1)S(1)}, bf16[1,96,768]{2,1,0:T(8,128)(2,1)S(1)}, u32[]{:S(2)}, u32[]{:S(2)}) %collective-permute-start.60) | collective-permute-done | bytes 147488 | tf_op jit(solution)/shard_map/ppermute | solution.py:78
  (169 shorter events, 47.7 us)
Async XLA Ops:
  4.3 11.1 %collective-permute-start = (bf16[1,96,768]{2,1,0:T(8,128)(2,1)S(1)}, bf16[1,96,768]{2,1,0:T(8,128)(2,1)S(1)}, u32[]{:S(2)}, u32[]{:S(2)}) collective-permute-start(bf16[1,96,768]{2,1,0:T(8,128)(2,1)S(1)} %pad_maximum_fusion.7), channel_id=1, source_target_pairs={{0,16},{1,17},{2,18},{3,19},{4,20},{5,21},{6,22},{7,23},{8,24},{9,... | collective-permute-start | bytes 442376 | tf_op jit(solution)/shard_map/ppermute | solution.py:78
  15.6 11.4 %collective-permute-start.2 = (bf16[2,96,768]{2,1,0:T(8,128)(2,1)S(1)}, bf16[2,96,768]{2,1,0:T(8,128)(2,1)S(1)}, u32[]{:S(2)}, u32[]{:S(2)}) collective-permute-start(bf16[2,96,768]{2,1,0:T(8,128)(2,1)S(1)} %pad_maximum_fusion.3), channel_id=1, source_target_pairs={{0,8},{1,9},{2,10},{3,11},{4,12},{5,13},{6,14},{7,15},{8,0},{9,1},... | collective-permute-start | bytes 884744 | tf_op jit(solution)/shard_map/ppermute | solution.py:78
  16.4 9.6 %collective-permute-start.3 = (bf16[1,96,768]{2,1,0:T(8,128)(2,1)S(1)}, bf16[1,96,768]{2,1,0:T(8,128)(2,1)S(1)}, u32[]{:S(2)}, u32[]{:S(2)}) collective-permute-start(bf16[1,96,768]{2,1,0:T(8,128)(2,1)S(1)} %convert_bitcast_fusion.1), channel_id=1, source_target_pairs={{0,16},{1,17},{2,18},{3,19},{4,20},{5,21},{6,22},{7,23},{8,24},{9,... | collective-permute-start | bytes 442376 | tf_op jit(solution)/shard_map/ppermute | solution.py:78
  27.2 13.9 %collective-permute-start.5 = (bf16[4,96,768]{2,1,0:T(8,128)(2,1)S(1)}, bf16[4,96,768]{2,1,0:T(8,128)(2,1)S(1)}, u32[]{:S(2)}, u32[]{:S(2)}) collective-permute-start(bf16[4,96,768]{2,1,0:T(8,128)(2,1)S(1)} %pad_maximum_fusion.rest_0_), channel_id=1, source_target_pairs={{0,2},{1,3},{2,0},{3,1},{4,6},{5,7},{6,4},{7,5},{8,10},{9,11},{10,... | collective-permute-start | bytes 1769480 | tf_op jit(solution)/shard_map/ppermute | solution.py:78
  28.5 13.3 %collective-permute-start.6 = (bf16[4,96,768]{2,1,0:T(8,128)(2,1)S(1)}, bf16[4,96,768]{2,1,0:T(8,128)(2,1)S(1)}, u32[]{:S(2)}, u32[]{:S(2)}) collective-permute-start(bf16[4,96,768]{2,1,0:T(8,128)(2,1)S(1)} %pad_maximum_fusion.rest_0_), channel_id=1, source_target_pairs={{0,4},{1,5},{2,6},{3,7},{4,0},{5,1},{6,2},{7,3},{8,12},{9,13},{10,... | collective-permute-start | bytes 1769480 | tf_op jit(solution)/shard_map/ppermute | solution.py:78
  30.1 11.8 %collective-permute-start.7 = (bf16[4,96,768]{2,1,0:T(8,128)(2,1)S(1)}, bf16[4,96,768]{2,1,0:T(8,128)(2,1)S(1)}, u32[]{:S(2)}, u32[]{:S(2)}) collective-permute-start(bf16[4,96,768]{2,1,0:T(8,128)(2,1)S(1)} %pad_maximum_fusion.rest_0_), channel_id=1, source_target_pairs={{0,1},{1,0},{2,3},{3,2},{4,5},{5,4},{6,7},{7,6},{8,9},{9,8},{10,11... | collective-permute-start | bytes 1769480 | tf_op jit(solution)/shard_map/ppermute | solution.py:78
  30.1 11.0 %collective-permute-start.8 = (bf16[2,96,768]{2,1,0:T(8,128)(2,1)S(1)}, bf16[2,96,768]{2,1,0:T(8,128)(2,1)S(1)}, u32[]{:S(2)}, u32[]{:S(2)}) collective-permute-start(bf16[2,96,768]{2,1,0:T(8,128)(2,1)S(1)} %pad_maximum_fusion.4), channel_id=1, source_target_pairs={{0,8},{1,9},{2,10},{3,11},{4,12},{5,13},{6,14},{7,15},{8,0},{9,1},... | collective-permute-start | bytes 884744 | tf_op jit(solution)/shard_map/ppermute | solution.py:78
  41.9 10.7 %collective-permute-start.11 = (bf16[4,96,768]{2,1,0:T(8,128)(2,1)S(1)}, bf16[4,96,768]{2,1,0:T(8,128)(2,1)S(1)}, u32[]{:S(2)}, u32[]{:S(2)}) collective-permute-start(bf16[4,96,768]{2,1,0:T(8,128)(2,1)S(1)} %collective-permute-done.6.rest_1_), channel_id=1, source_target_pairs={{0,1},{1,0},{2,3},{3,2},{4,5},{5,4},{6,7},{7,6},{8,9},{9,8},{10,11... | collective-permute-start | bytes 1769480 | tf_op jit(solution)/shard_map/ppermute | solution.py:78
  42.0 9.4 %collective-permute-start.10 = (bf16[2,96,768]{2,1,0:T(8,128)(2,1)S(1)}, bf16[2,96,768]{2,1,0:T(8,128)(2,1)S(1)}, u32[]{:S(2)}, u32[]{:S(2)}) collective-permute-start(bf16[2,96,768]{2,1,0:T(8,128)(2,1)S(1)} %slice.88), channel_id=1, source_target_pairs={{0,4},{1,5},{2,6},{3,7},{4,0},{5,1},{6,2},{7,3},{8,12},{9,13},{10,... | collective-permute-start | bytes 884744 | tf_op jit(solution)/shard_map/ppermute | solution.py:78
  43.6 9.1 %collective-permute-start.9 = (bf16[2,96,768]{2,1,0:T(8,128)(2,1)S(1)}, bf16[2,96,768]{2,1,0:T(8,128)(2,1)S(1)}, u32[]{:S(2)}, u32[]{:S(2)}) collective-permute-start(bf16[2,96,768]{2,1,0:T(8,128)(2,1)S(1)} %slice.87), channel_id=1, source_target_pairs={{0,2},{1,3},{2,0},{3,1},{4,6},{5,7},{6,4},{7,5},{8,10},{9,11},{10,... | collective-permute-start | bytes 884744 | tf_op jit(solution)/shard_map/ppermute | solution.py:78
  44.1 7.3 %collective-permute-start.12 = (bf16[1,96,768]{2,1,0:T(8,128)(2,1)S(1)}, bf16[1,96,768]{2,1,0:T(8,128)(2,1)S(1)}, u32[]{:S(2)}, u32[]{:S(2)}) collective-permute-start(bf16[1,96,768]{2,1,0:T(8,128)(2,1)S(1)} %convert_bitcast_fusion), channel_id=1, source_target_pairs={{0,16},{1,17},{2,18},{3,19},{4,20},{5,21},{6,22},{7,23},{8,24},{9,... | collective-permute-start | bytes 442376 | tf_op jit(solution)/shard_map/ppermute | solution.py:78
  54.0 17.5 %collective-permute-start.16 = (bf16[4,96,768]{2,1,0:T(8,128)(2,1)S(1)}, bf16[4,96,768]{2,1,0:T(8,128)(2,1)S(1)}, u32[]{:S(2)}, u32[]{:S(2)}) collective-permute-start(bf16[4,96,768]{2,1,0:T(8,128)(2,1)S(1)} %pad_maximum_fusion.1.rest_0_), channel_id=1, source_target_pairs={{0,2},{1,3},{2,0},{3,1},{4,6},{5,7},{6,4},{7,5},{8,10},{9,11},{10,... | collective-permute-start | bytes 1769480 | tf_op jit(solution)/shard_map/ppermute | solution.py:78
  54.6 16.9 %collective-permute-start.17 = (bf16[4,96,768]{2,1,0:T(8,128)(2,1)S(1)}, bf16[4,96,768]{2,1,0:T(8,128)(2,1)S(1)}, u32[]{:S(2)}, u32[]{:S(2)}) collective-permute-start(bf16[4,96,768]{2,1,0:T(8,128)(2,1)S(1)} %pad_maximum_fusion.1.rest_0_), channel_id=1, source_target_pairs={{0,4},{1,5},{2,6},{3,7},{4,0},{5,1},{6,2},{7,3},{8,12},{9,13},{10,... | collective-permute-start | bytes 1769480 | tf_op jit(solution)/shard_map/ppermute | solution.py:78
  55.4 16.1 %collective-permute-start.18 = (bf16[4,96,768]{2,1,0:T(8,128)(2,1)S(1)}, bf16[4,96,768]{2,1,0:T(8,128)(2,1)S(1)}, u32[]{:S(2)}, u32[]{:S(2)}) collective-permute-start(bf16[4,96,768]{2,1,0:T(8,128)(2,1)S(1)} %pad_maximum_fusion.1.rest_0_), channel_id=1, source_target_pairs={{0,1},{1,0},{2,3},{3,2},{4,5},{5,4},{6,7},{7,6},{8,9},{9,8},{10,11... | collective-permute-start | bytes 1769480 | tf_op jit(solution)/shard_map/ppermute | solution.py:78
  55.5 16.0 %collective-permute-start.19 = (bf16[2,96,768]{2,1,0:T(8,128)(2,1)S(1)}, bf16[2,96,768]{2,1,0:T(8,128)(2,1)S(1)}, u32[]{:S(2)}, u32[]{:S(2)}) collective-permute-start(bf16[2,96,768]{2,1,0:T(8,128)(2,1)S(1)} %pad_maximum_fusion.5), channel_id=1, source_target_pairs={{0,8},{1,9},{2,10},{3,11},{4,12},{5,13},{6,14},{7,15},{8,0},{9,1},... | collective-permute-start | bytes 884744 | tf_op jit(solution)/shard_map/ppermute | solution.py:78
  71.7 10.5 %collective-permute-start.22 = (bf16[4,96,768]{2,1,0:T(8,128)(2,1)S(1)}, bf16[4,96,768]{2,1,0:T(8,128)(2,1)S(1)}, u32[]{:S(2)}, u32[]{:S(2)}) collective-permute-start(bf16[4,96,768]{2,1,0:T(8,128)(2,1)S(1)} %collective-permute-done.17.rest_1_), channel_id=1, source_target_pairs={{0,1},{1,0},{2,3},{3,2},{4,5},{5,4},{6,7},{7,6},{8,9},{9,8},{10,11... | collective-permute-start | bytes 1769480 | tf_op jit(solution)/shard_map/ppermute | solution.py:78
  71.8 9.3 %collective-permute-start.20 = (bf16[2,96,768]{2,1,0:T(8,128)(2,1)S(1)}, bf16[2,96,768]{2,1,0:T(8,128)(2,1)S(1)}, u32[]{:S(2)}, u32[]{:S(2)}) collective-permute-start(bf16[2,96,768]{2,1,0:T(8,128)(2,1)S(1)} %slice.89), channel_id=1, source_target_pairs={{0,2},{1,3},{2,0},{3,1},{4,6},{5,7},{6,4},{7,5},{8,10},{9,11},{10,... | collective-permute-start | bytes 884744 | tf_op jit(solution)/shard_map/ppermute | solution.py:78
  73.1 9.0 %collective-permute-start.21 = (bf16[2,96,768]{2,1,0:T(8,128)(2,1)S(1)}, bf16[2,96,768]{2,1,0:T(8,128)(2,1)S(1)}, u32[]{:S(2)}, u32[]{:S(2)}) collective-permute-start(bf16[2,96,768]{2,1,0:T(8,128)(2,1)S(1)} %slice.90), channel_id=1, source_target_pairs={{0,4},{1,5},{2,6},{3,7},{4,0},{5,1},{6,2},{7,3},{8,12},{9,13},{10,... | collective-permute-start | bytes 884744 | tf_op jit(solution)/shard_map/ppermute | solution.py:78
  82.2 6.5 %collective-permute-start.23 = (bf16[4,96,768]{2,1,0:T(8,128)(2,1)S(1)}, bf16[4,96,768]{2,1,0:T(8,128)(2,1)S(1)}, u32[]{:S(2)}, u32[]{:S(2)}) collective-permute-start(bf16[4,96,768]{2,1,0:T(8,128)(2,1)S(1)} %collective-permute-done.16.rest_0_), channel_id=1, source_target_pairs={{0,1},{1,0},{2,3},{3,2},{4,5},{5,4},{6,7},{7,6},{8,9},{9,8},{10,11... | collective-permute-start | bytes 1769480 | tf_op jit(solution)/shard_map/ppermute | solution.py:78
  82.2 15.7 %collective-permute-start.26 = (bf16[4,96,768]{2,1,0:T(8,128)(2,1)S(1)}, bf16[4,96,768]{2,1,0:T(8,128)(2,1)S(1)}, u32[]{:S(2)}, u32[]{:S(2)}) collective-permute-start(bf16[4,96,768]{2,1,0:T(8,128)(2,1)S(1)} %pad_maximum_fusion.2.rest_0_), channel_id=1, source_target_pairs={{0,2},{1,3},{2,0},{3,1},{4,6},{5,7},{6,4},{7,5},{8,10},{9,11},{10,... | collective-permute-start | bytes 1769480 | tf_op jit(solution)/shard_map/ppermute | solution.py:78
  82.9 15.5 %collective-permute-start.27 = (bf16[4,96,768]{2,1,0:T(8,128)(2,1)S(1)}, bf16[4,96,768]{2,1,0:T(8,128)(2,1)S(1)}, u32[]{:S(2)}, u32[]{:S(2)}) collective-permute-start(bf16[4,96,768]{2,1,0:T(8,128)(2,1)S(1)} %pad_maximum_fusion.2.rest_0_), channel_id=1, source_target_pairs={{0,4},{1,5},{2,6},{3,7},{4,0},{5,1},{6,2},{7,3},{8,12},{9,13},{10,... | collective-permute-start | bytes 1769480 | tf_op jit(solution)/shard_map/ppermute | solution.py:78
  98.4 10.6 %collective-permute-start.30 = (bf16[4,96,768]{2,1,0:T(8,128)(2,1)S(1)}, bf16[4,96,768]{2,1,0:T(8,128)(2,1)S(1)}, u32[]{:S(2)}, u32[]{:S(2)}) collective-permute-start(bf16[4,96,768]{2,1,0:T(8,128)(2,1)S(1)} %collective-permute-done.27.rest_1_), channel_id=1, source_target_pairs={{0,1},{1,0},{2,3},{3,2},{4,5},{5,4},{6,7},{7,6},{8,9},{9,8},{10,11... | collective-permute-start | bytes 1769480 | tf_op jit(solution)/shard_map/ppermute | solution.py:78
  98.5 10.5 %collective-permute-start.31 = (bf16[4,96,768]{2,1,0:T(8,128)(2,1)S(1)}, bf16[4,96,768]{2,1,0:T(8,128)(2,1)S(1)}, u32[]{:S(2)}, u32[]{:S(2)}) collective-permute-start(bf16[4,96,768]{2,1,0:T(8,128)(2,1)S(1)} %pad_maximum_fusion.2.rest_0_), channel_id=1, source_target_pairs={{0,1},{1,0},{2,3},{3,2},{4,5},{5,4},{6,7},{7,6},{8,9},{9,8},{10,11... | collective-permute-start | bytes 1769480 | tf_op jit(solution)/shard_map/ppermute | solution.py:78
  99.0 9.0 %collective-permute-start.28 = (bf16[2,96,768]{2,1,0:T(8,128)(2,1)S(1)}, bf16[2,96,768]{2,1,0:T(8,128)(2,1)S(1)}, u32[]{:S(2)}, u32[]{:S(2)}) collective-permute-start(bf16[2,96,768]{2,1,0:T(8,128)(2,1)S(1)} %slice.91), channel_id=1, source_target_pairs={{0,2},{1,3},{2,0},{3,1},{4,6},{5,7},{6,4},{7,5},{8,10},{9,11},{10,... | collective-permute-start | bytes 884744 | tf_op jit(solution)/shard_map/ppermute | solution.py:78
  100.3 8.7 %collective-permute-start.29 = (bf16[2,96,768]{2,1,0:T(8,128)(2,1)S(1)}, bf16[2,96,768]{2,1,0:T(8,128)(2,1)S(1)}, u32[]{:S(2)}, u32[]{:S(2)}) collective-permute-start(bf16[2,96,768]{2,1,0:T(8,128)(2,1)S(1)} %slice.92), channel_id=1, source_target_pairs={{0,4},{1,5},{2,6},{3,7},{4,0},{5,1},{6,2},{7,3},{8,12},{9,13},{10,... | collective-permute-start | bytes 884744 | tf_op jit(solution)/shard_map/ppermute | solution.py:78
  128.2 10.0 %collective-permute-start.38 = (bf16[2,8,96,768]{3,2,1,0:T(8,128)(2,1)S(1)}, bf16[2,8,96,768]{3,2,1,0:T(8,128)(2,1)S(1)}, u32[]{:S(2)}, u32[]{:S(2)}) collective-permute-start(bf16[2,8,96,768]{3,2,1,0:T(8,128)(2,1)S(1)} %get-tuple-element.524), channel_id=1, source_target_pairs={{0,1},{1,0},{2,3},{3,2},{4,5},{5,4},{6,7},{7,6},{8,9},{9,8},{10,11... | collective-permute-start | bytes 7077896 | tf_op jit(solution)/shard_map/ppermute | solution.py:78
  128.4 9.3 %collective-permute-start.36 = (bf16[2,96,768]{2,1,0:T(8,128)(2,1)S(1)}, bf16[2,96,768]{2,1,0:T(8,128)(2,1)S(1)}, u32[]{:S(2)}, u32[]{:S(2)}) collective-permute-start(bf16[2,96,768]{2,1,0:T(8,128)(2,1)S(1)} %get-tuple-element.522), channel_id=1, source_target_pairs={{0,2},{1,3},{2,0},{3,1},{4,6},{5,7},{6,4},{7,5},{8,10},{9,11},{10,... | collective-permute-start | bytes 884744 | tf_op jit(solution)/shard_map/ppermute | solution.py:78
  129.1 9.0 %collective-permute-start.37 = (bf16[2,96,768]{2,1,0:T(8,128)(2,1)S(1)}, bf16[2,96,768]{2,1,0:T(8,128)(2,1)S(1)}, u32[]{:S(2)}, u32[]{:S(2)}) collective-permute-start(bf16[2,96,768]{2,1,0:T(8,128)(2,1)S(1)} %get-tuple-element.523), channel_id=1, source_target_pairs={{0,4},{1,5},{2,6},{3,7},{4,0},{5,1},{6,2},{7,3},{8,12},{9,13},{10,... | collective-permute-start | bytes 884744 | tf_op jit(solution)/shard_map/ppermute | solution.py:78
  138.7 21.8 %collective-permute-start.41 = (bf16[4,96,768]{2,1,0:T(8,128)(2,1)S(1)}, bf16[4,96,768]{2,1,0:T(8,128)(2,1)S(1)}, u32[]{:S(2)}, u32[]{:S(2)}) collective-permute-start(bf16[4,96,768]{2,1,0:T(8,128)(2,1)S(1)} %get-tuple-element.564), channel_id=1, source_target_pairs={{0,2},{1,3},{2,0},{3,1},{4,6},{5,7},{6,4},{7,5},{8,10},{9,11},{10,... | collective-permute-start | bytes 1769480 | tf_op jit(solution)/shard_map/ppermute | solution.py:78
  140.0 20.5 %collective-permute-start.42 = (bf16[4,96,768]{2,1,0:T(8,128)(2,1)S(1)}, bf16[4,96,768]{2,1,0:T(8,128)(2,1)S(1)}, u32[]{:S(2)}, u32[]{:S(2)}) collective-permute-start(bf16[4,96,768]{2,1,0:T(8,128)(2,1)S(1)} %get-tuple-element.565), channel_id=1, source_target_pairs={{0,4},{1,5},{2,6},{3,7},{4,0},{5,1},{6,2},{7,3},{8,12},{9,13},{10,... | collective-permute-start | bytes 1769480 | tf_op jit(solution)/shard_map/ppermute | solution.py:78
  141.5 18.0 %collective-permute-start.39 = (bf16[2,96,768]{2,1,0:T(8,128)(2,1)S(1)}, bf16[2,96,768]{2,1,0:T(8,128)(2,1)S(1)}, u32[]{:S(2)}, u32[]{:S(2)}) collective-permute-start(bf16[2,96,768]{2,1,0:T(8,128)(2,1)S(1)} %get-tuple-element.562), channel_id=1, source_target_pairs={{0,2},{1,3},{2,0},{3,1},{4,6},{5,7},{6,4},{7,5},{8,10},{9,11},{10,... | collective-permute-start | bytes 884744 | tf_op jit(solution)/shard_map/ppermute | solution.py:78
  142.1 18.4 %collective-permute-start.40 = (bf16[2,96,768]{2,1,0:T(8,128)(2,1)S(1)}, bf16[2,96,768]{2,1,0:T(8,128)(2,1)S(1)}, u32[]{:S(2)}, u32[]{:S(2)}) collective-permute-start(bf16[2,96,768]{2,1,0:T(8,128)(2,1)S(1)} %get-tuple-element.563), channel_id=1, source_target_pairs={{0,4},{1,5},{2,6},{3,7},{4,0},{5,1},{6,2},{7,3},{8,12},{9,13},{10,... | collective-permute-start | bytes 884744 | tf_op jit(solution)/shard_map/ppermute | solution.py:78
  161.2 12.0 %collective-permute-start.43 = (bf16[2,8,96,768]{3,2,1,0:T(8,128)(2,1)S(1)}, bf16[2,8,96,768]{3,2,1,0:T(8,128)(2,1)S(1)}, u32[]{:S(2)}, u32[]{:S(2)}) collective-permute-start(bf16[2,8,96,768]{3,2,1,0:T(8,128)(2,1)S(1)} %get-tuple-element.582), channel_id=1, source_target_pairs={{0,1},{1,0},{2,3},{3,2},{4,5},{5,4},{6,7},{7,6},{8,9},{9,8},{10,11... | collective-permute-start | bytes 7077896 | tf_op jit(solution)/shard_map/ppermute | solution.py:78
  161.3 11.9 %collective-permute-start.44 = (bf16[1,2,96,768]{3,2,1,0:T(8,128)(2,1)S(1)}, bf16[1,2,96,768]{3,2,1,0:T(8,128)(2,1)S(1)}, u32[]{:S(2)}, u32[]{:S(2)}) collective-permute-start(bf16[1,2,96,768]{3,2,1,0:T(8,128)(2,1)S(1)} %get-tuple-element.583), channel_id=1, source_target_pairs={{0,8},{1,9},{2,10},{3,11},{4,12},{5,13},{6,14},{7,15},{8,0},{9,1},... | collective-permute-start | bytes 884744 | tf_op jit(solution)/shard_map/ppermute | solution.py:78
  164.4 8.7 %collective-permute-start.45 = (f32[16,768]{1,0:T(8,128)S(1)}, f32[16,768]{1,0:T(8,128)S(1)}, u32[]{:S(2)}, u32[]{:S(2)}) collective-permute-start(f32[16,768]{1,0:T(8,128)S(1)} %get-tuple-element.584), channel_id=1, source_target_pairs={{0,16},{1,17},{2,18},{3,19},{4,20},{5,21},{6,22},{7,23},{8,24},{9,... | collective-permute-start | bytes 147464 | tf_op jit(solution)/shard_map/ppermute | solution.py:78
  166.1 16.2 %collective-permute-start.48 = (bf16[4,96,768]{2,1,0:T(8,128)(2,1)S(1)}, bf16[4,96,768]{2,1,0:T(8,128)(2,1)S(1)}, u32[]{:S(2)}, u32[]{:S(2)}) collective-permute-start(bf16[4,96,768]{2,1,0:T(8,128)(2,1)S(1)} %get-tuple-element.593), channel_id=1, source_target_pairs={{0,2},{1,3},{2,0},{3,1},{4,6},{5,7},{6,4},{7,5},{8,10},{9,11},{10,... | collective-permute-start | bytes 1769480 | tf_op jit(solution)/shard_map/ppermute | solution.py:78
  167.6 16.2 %collective-permute-start.49 = (bf16[4,96,768]{2,1,0:T(8,128)(2,1)S(1)}, bf16[4,96,768]{2,1,0:T(8,128)(2,1)S(1)}, u32[]{:S(2)}, u32[]{:S(2)}) collective-permute-start(bf16[4,96,768]{2,1,0:T(8,128)(2,1)S(1)} %get-tuple-element.594), channel_id=1, source_target_pairs={{0,4},{1,5},{2,6},{3,7},{4,0},{5,1},{6,2},{7,3},{8,12},{9,13},{10,... | collective-permute-start | bytes 1769480 | tf_op jit(solution)/shard_map/ppermute | solution.py:78
  173.4 14.1 %collective-permute-start.46 = (bf16[2,96,768]{2,1,0:T(8,128)(2,1)S(1)}, bf16[2,96,768]{2,1,0:T(8,128)(2,1)S(1)}, u32[]{:S(2)}, u32[]{:S(2)}) collective-permute-start(bf16[2,96,768]{2,1,0:T(8,128)(2,1)S(1)} %get-tuple-element.591), channel_id=1, source_target_pairs={{0,2},{1,3},{2,0},{3,1},{4,6},{5,7},{6,4},{7,5},{8,10},{9,11},{10,... | collective-permute-start | bytes 884744 | tf_op jit(solution)/shard_map/ppermute | solution.py:78
  174.0 14.7 %collective-permute-start.47 = (bf16[2,96,768]{2,1,0:T(8,128)(2,1)S(1)}, bf16[2,96,768]{2,1,0:T(8,128)(2,1)S(1)}, u32[]{:S(2)}, u32[]{:S(2)}) collective-permute-start(bf16[2,96,768]{2,1,0:T(8,128)(2,1)S(1)} %get-tuple-element.592), channel_id=1, source_target_pairs={{0,4},{1,5},{2,6},{3,7},{4,0},{5,1},{6,2},{7,3},{8,12},{9,13},{10,... | collective-permute-start | bytes 884744 | tf_op jit(solution)/shard_map/ppermute | solution.py:78
  175.5 8.3 %collective-permute-start.50 = (f32[16,768]{1,0:T(8,128)S(1)}, f32[16,768]{1,0:T(8,128)S(1)}, u32[]{:S(2)}, u32[]{:S(2)}) collective-permute-start(f32[16,768]{1,0:T(8,128)S(1)} %add_select_fusion.4), channel_id=1, source_target_pairs={{0,8},{1,9},{2,10},{3,11},{4,12},{5,13},{6,14},{7,15},{8,0},{9,1},... | collective-permute-start | bytes 147464 | tf_op jit(solution)/shard_map/ppermute | solution.py:78
  189.5 15.6 %collective-permute-start.51 = (bf16[4,96,768]{2,1,0:T(8,128)(2,1)S(1)}, bf16[4,96,768]{2,1,0:T(8,128)(2,1)S(1)}, u32[]{:S(2)}, u32[]{:S(2)}) collective-permute-start(bf16[4,96,768]{2,1,0:T(8,128)(2,1)S(1)} %get-tuple-element.607), channel_id=1, source_target_pairs={{0,2},{1,3},{2,0},{3,1},{4,6},{5,7},{6,4},{7,5},{8,10},{9,11},{10,... | collective-permute-start | bytes 1769480 | tf_op jit(solution)/shard_map/ppermute | solution.py:78
  190.1 15.0 %collective-permute-start.52 = (bf16[4,96,768]{2,1,0:T(8,128)(2,1)S(1)}, bf16[4,96,768]{2,1,0:T(8,128)(2,1)S(1)}, u32[]{:S(2)}, u32[]{:S(2)}) collective-permute-start(bf16[4,96,768]{2,1,0:T(8,128)(2,1)S(1)} %get-tuple-element.608), channel_id=1, source_target_pairs={{0,4},{1,5},{2,6},{3,7},{4,0},{5,1},{6,2},{7,3},{8,12},{9,13},{10,... | collective-permute-start | bytes 1769480 | tf_op jit(solution)/shard_map/ppermute | solution.py:78
  190.6 10.2 %collective-permute-start.54 = (bf16[1,2,96,768]{3,2,1,0:T(8,128)(2,1)S(1)}, bf16[1,2,96,768]{3,2,1,0:T(8,128)(2,1)S(1)}, u32[]{:S(2)}, u32[]{:S(2)}) collective-permute-start(bf16[1,2,96,768]{3,2,1,0:T(8,128)(2,1)S(1)} %get-tuple-element.611), channel_id=1, source_target_pairs={{0,8},{1,9},{2,10},{3,11},{4,12},{5,13},{6,14},{7,15},{8,0},{9,1},... | collective-permute-start | bytes 884744 | tf_op jit(solution)/shard_map/ppermute | solution.py:78
  190.9 8.0 %collective-permute-start.53 = (bf16[1,96,768]{2,1,0:T(8,128)(2,1)S(1)}, bf16[1,96,768]{2,1,0:T(8,128)(2,1)S(1)}, u32[]{:S(2)}, u32[]{:S(2)}) collective-permute-start(bf16[1,96,768]{2,1,0:T(8,128)(2,1)S(1)} %get-tuple-element.610), channel_id=1, source_target_pairs={{0,16},{1,17},{2,18},{3,19},{4,20},{5,21},{6,22},{7,23},{8,24},{9,... | collective-permute-start | bytes 442376 | tf_op jit(solution)/shard_map/ppermute | solution.py:78
  205.5 10.7 %collective-permute-start.58 = (bf16[1,2,96,768]{3,2,1,0:T(8,128)(2,1)S(1)}, bf16[1,2,96,768]{3,2,1,0:T(8,128)(2,1)S(1)}, u32[]{:S(2)}, u32[]{:S(2)}) collective-permute-start(bf16[1,2,96,768]{3,2,1,0:T(8,128)(2,1)S(1)} %get-tuple-element.623), channel_id=1, source_target_pairs={{0,8},{1,9},{2,10},{3,11},{4,12},{5,13},{6,14},{7,15},{8,0},{9,1},... | collective-permute-start | bytes 884744 | tf_op jit(solution)/shard_map/ppermute | solution.py:78
  206.8 7.2 %collective-permute-start.57 = (bf16[1,96,768]{2,1,0:T(8,128)(2,1)S(1)}, bf16[1,96,768]{2,1,0:T(8,128)(2,1)S(1)}, u32[]{:S(2)}, u32[]{:S(2)}) collective-permute-start(bf16[1,96,768]{2,1,0:T(8,128)(2,1)S(1)} %get-tuple-element.620), channel_id=1, source_target_pairs={{0,16},{1,17},{2,18},{3,19},{4,20},{5,21},{6,22},{7,23},{8,24},{9,... | collective-permute-start | bytes 442376 | tf_op jit(solution)/shard_map/ppermute | solution.py:78
  207.2 6.7 %collective-permute-start.59 = (f32[16,768]{1,0:T(8,128)S(1)}, f32[16,768]{1,0:T(8,128)S(1)}, u32[]{:S(2)}, u32[]{:S(2)}) collective-permute-start(f32[16,768]{1,0:T(8,128)S(1)} %add_select_fusion.1), channel_id=1, source_target_pairs={{0,4},{1,5},{2,6},{3,7},{4,0},{5,1},{6,2},{7,3},{8,12},{9,13},{10,... | collective-permute-start | bytes 147464 | tf_op jit(solution)/shard_map/ppermute | solution.py:78
  216.9 7.9 %collective-permute-start.60 = (bf16[1,96,768]{2,1,0:T(8,128)(2,1)S(1)}, bf16[1,96,768]{2,1,0:T(8,128)(2,1)S(1)}, u32[]{:S(2)}, u32[]{:S(2)}) collective-permute-start(bf16[1,96,768]{2,1,0:T(8,128)(2,1)S(1)} %get-tuple-element.627), channel_id=1, source_target_pairs={{0,16},{1,17},{2,18},{3,19},{4,20},{5,21},{6,22},{7,23},{8,24},{9,... | collective-permute-start | bytes 442376 | tf_op jit(solution)/shard_map/ppermute | solution.py:78
  (28 other events, 292.8 us)

commit v5 on v4

--- a/solution.py
+++ b/solution.py
@@ -134,12 +134,24 @@
         return near, got, in_x, in_y
 
     @staticmethod
-    def scatter_line(*parts):
-        out_z, kept = add_third(*parts)
+    def scatter_line(near, got, in_x, in_y):
+        out_z, kept = add_third(near, got, in_x, in_y)
         (from_z,) = yield [(out_z, PZ1)]
         out_z, kept = add_fourth(kept, from_z)
         (last,) = yield [(out_z, PZ2)]
-        return [kept[n] + last[n].astype(f32) for n in range(len(parts))]
+        return kept + last.astype(f32)
+
+    @staticmethod
+    def scatter_z_first(far, near):
+        (got,) = yield [(far, PC)]
+        (from_z,) = yield [(add_near_z(near, got), PZ1)]
+        out_x, out_y = add_corner(near, got, from_z)
+        from_x, from_y = yield [(out_x, PX), (out_y, PY)]
+        out_x, out_y = add_sides(near, got, from_z, from_x, from_y)
+        in_x, in_y = yield [(out_x, PX), (out_y, PY)]
+        out_z, kept = add_own(near, got, from_z, in_x, in_y)
+        (last,) = yield [(out_z, PZ2)]
+        return kept + last.astype(f32)
 
     @staticmethod
     def gather_lane(vec):
@@ -180,14 +192,19 @@
     @staticmethod
     def scatter_sum(far, near):
         grads = jnp.stack([near[0], far[0], near[1], far[1]]).astype(f32)
-        return grads.reshape((4, -1, grads.shape[-1]))
+        return (grads.reshape((4, -1, grads.shape[-1])),)
         yield
 
     @staticmethod
-    def scatter_line(*parts):
-        own = [lax.psum_scatter(p, "tensor", scatter_dimension=0, tiled=False) for p in parts]
-        return [lax.psum_scatter(o, "dp", scatter_dimension=0, tiled=True) for o in own]
+    def scatter_line(grads):
+        own = lax.psum_scatter(grads, "tensor", scatter_dimension=0, tiled=False)
+        return lax.psum_scatter(own, "dp", scatter_dimension=0, tiled=True)
         yield
+
+    @staticmethod
+    def scatter_z_first(far, near):
+        grads = yield from Plain.scatter_sum(far, near)
+        return (yield from Plain.scatter_line(*grads))
 
     @staticmethod
     def gather_lane(vec):
@@ -256,35 +273,79 @@
     return glue(second_sums, [part, part], near, got, from_x, from_y)
 
 
-def add_third(*parts):
-    rows = parts[0][0].shape[-2:]
-    ins = []
-    for near, got, in_x, in_y in parts:
-        ins += [near.reshape((-1, 8) + rows), got.reshape((-1, 8) + rows), in_x, in_y]
-
-    def third_sums(*refs):
-        out, kept = refs[-2:]
-        for n in range(len(parts)):
-            near, got, in_x, in_y = refs[4 * n : 4 * n + 4]
-            for k in range(4):
-                total = near[0, k].astype(f32) + got[0, k].astype(f32) + in_x[k].astype(f32) + in_y[k].astype(f32)
-                if k < 2:
-                    kept[n, k] = total
-                else:
-                    out[n, k - 2] = total.astype(bf16)
-
-    shape = (len(parts), 2) + rows
-    return glue(third_sums, [like(shape, bf16), like(shape)], *ins)
+def add_third(near, got, in_x, in_y):
+    def third_sums(near, got, in_x, in_y, out, kept):
+        for k in range(4):
+            total = near[0, k].astype(f32) + got[0, k].astype(f32) + in_x[k].astype(f32) + in_y[k].astype(f32)
+            if k < 2:
+                kept[k] = total
+            else:
+                out[k - 2] = total.astype(bf16)
+
+    shape = (2,) + near.shape[2:]
+    return glue(third_sums, [like(shape, bf16), like(shape)], near, got, in_x, in_y)
 
 
 def add_fourth(kept, from_z):
     def fourth_sums(kept, from_z, out, mine):
-        for n in range(kept.shape[0]):
-            mine[n] = kept[n, 0] + from_z[n, 0].astype(f32)
-            out[n] = (kept[n, 1] + from_z[n, 1].astype(f32)).astype(bf16)
-
-    shape = kept.shape[:1] + kept.shape[2:]
+        mine[...] = kept[0] + from_z[0].astype(f32)
+        out[...] = (kept[1] + from_z[1].astype(f32)).astype(bf16)
+
+    shape = kept.shape[1:]
     return glue(fourth_sums, [like(shape, bf16), like(shape)], kept, from_z)
+
+
+def add_near_z(near, got):
+    def near_z_sums(near, got, out):
+        for y in range(2):
+            for k in range(2):
+                out[:, 2 * y + k] = (near[:, 4 * y + 2 + k].astype(f32) + got[:, 4 * y + 2 + k].astype(f32)).astype(bf16)
+
+    return glue(near_z_sums, [like((2, 4) + near.shape[2:], bf16)], near, got)[0]
+
+
+def three(near, got, from_z, x, y, k):
+    return near[x, 4 * y + k].astype(f32) + got[x, 4 * y + k].astype(f32) + from_z[x, 2 * y + k].astype(f32)
+
+
+def add_corner(near, got, from_z):
+    def corner_sums(near, got, from_z, out_x, out_y):
+        out_x[...] = three(near, got, from_z, 1, 1, 0).astype(bf16)
+        out_y[...] = three(near, got, from_z, 1, 1, 1).astype(bf16)
+
+    part = like(near.shape[2:], bf16)
+    return glue(corner_sums, [part, part], near, got, from_z)
+
+
+def add_sides(near, got, from_z, from_x, from_y):
+    def side_sums(near, got, from_z, from_x, from_y, out_x, out_y):
+        out_x[0] = three(near, got, from_z, 1, 0, 0).astype(bf16)
+        out_x[1] = (three(near, got, from_z, 1, 0, 1) + from_y[...].astype(f32)).astype(bf16)
+        out_y[0] = (three(near, got, from_z, 0, 1, 0) + from_x[...].astype(f32)).astype(bf16)
+        out_y[1] = three(near, got, from_z, 0, 1, 1).astype(bf16)
+
+    part = like((2,) + near.shape[2:], bf16)
+    return glue(side_sums, [part, part], near, got, from_z, from_x, from_y)
+
+
+def add_own(near, got, from_z, in_x, in_y):
+    def own_sums(near, got, from_z, in_x, in_y, out, kept):
+        kept[...] = three(near, got, from_z, 0, 0, 0) + in_x[0].astype(f32) + in_y[0].astype(f32)
+        out[...] = (three(near, got, from_z, 0, 0, 1) + in_x[1].astype(f32) + in_y[1].astype(f32)).astype(bf16)
+
+    shape = near.shape[2:]
+    return glue(own_sums, [like(shape, bf16), like(shape)], near, got, from_z, in_x, in_y)
+
+
+def attn_shard(qkv_weight, out_weight):
+    _, rows, cols = qkv_weight.shape
+
+    def attn_weights(qkv, out_weight, out):
+        for j in range(3):
+            out[:, j * cols : (j + 1) * cols] = qkv[j].astype(bf16)
+        out[:, 3 * cols :] = out_weight[...].T.astype(bf16)
+
+    return glue(attn_weights, [like((rows, 4 * cols), bf16)], qkv_weight, out_weight)[0]
 
 
 def assemble(plan, bufs, dst, dp):
@@ -618,9 +679,7 @@
         every = tuple(range(blocks))
 
         pieces_a, pieces_u, pieces_d = Pieces([]), Pieces([]), Pieces([])
-        shard_a = jnp.concatenate(
-            [qkv_weight[0], qkv_weight[1], qkv_weight[2], out_weight.T], 1
-        ).astype(bf16)
+        shard_a = attn_shard(qkv_weight, out_weight)
         job_a = Job(net.gather(shard_a, pieces_a))
         bias_row = jnp.concatenate(
             [qv_bias[0], jnp.zeros((cols,), f32), qv_bias[1], jnp.zeros((HEAD_DIM,), f32), up_bias]
@@ -636,9 +695,9 @@
         moved = 2 * width * width * blocks
 
         step((), None, [job_a, job_b], [job_a, job_b])
-        step((), None, [job_a, job_u, job_b], [job_a, job_u, job_b])
+        step((), None, [job_a, job_b], [job_a, job_b])
+        step((), None, [job_a, job_u, job_d], [job_a, job_u, job_d])
         step((), None, [job_a, job_u], [job_a, job_u])
-        step((), None, [job_a, job_d], [job_a, job_d])
         step((), None, [job_u, job_a], [job_a])
         biases = job_b.value
 
@@ -662,8 +721,8 @@
                 4 * unit,
                 3 * moved,
             ),
-            [job_d],
-            [job_u, job_d],
+            [],
+            [job_u],
         )
         normed, inv, middle, mid_slope, mid_low, mid_t, tops_m = step(
             (act_ranges, ctx_low, tokens, out_bias, first_gain, first_shift, weight_a),
@@ -685,7 +744,7 @@
                 2 * moved,
             ),
             [job_u, job_d],
-            [job_u],
+            [job_u, job_d],
         )
 
         def up_part(lanes, start, finish):
@@ -710,7 +769,7 @@
                 finish,
             )
 
-        act0, slope0, top0, weight_u0 = up_part(every[:half], [job_u], [job_u])
+        act0, slope0, top0, weight_u0 = up_part(every[:half], [job_u, job_d], [job_u])
         act1, slope1, top1, weight_u1 = up_part(every[half:], [], [job_d])
         step((), None, [job_d], [job_d])
         step((), None, [job_d], [job_d])
@@ -758,8 +817,9 @@
                 finish,
             )
 
-        sum_d = Job(net.scatter_sum(*grad_of("down_grad", ffn_t, (act0, act1))))
+        sum_d = Job(net.scatter_z_first(*grad_of("down_grad", ffn_t, (act0, act1))))
         sum_u = Job(net.scatter_sum(*grad_of("up_grad", mid_t, (grad_up,), [sum_d], [sum_d])))
+        step((), None, [sum_u, sum_d], [sum_u])
         grad_first, attn_t, grad_ctx, sums_a = step(
             (grad_up, grad_second, mid_slope, normed, inv, first_gain, ctx_slope, weight_u0, weight_u1, weight_a),
             call(
@@ -776,8 +836,8 @@
                 unit + unit // 3,
                 3 * moved,
             ),
-            [sum_d, sum_u],
-            [sum_d, sum_u],
+            [sum_u],
+            [sum_u],
         )
 
         grad_qkv, far, near, packed = step(
@@ -792,13 +852,13 @@
                 4 * unit,
                 2 * moved,
             ),
-            [sum_u, sum_d],
+            [sum_u],
             [sum_u, sum_d],
         )
         sum_a = Job(net.scatter_sum(far, near))
         is_top = (jnp.arange(packed.shape[0]) == 2 * blocks + 6)[:, None]
         sum_s = Job(net.sum_max(packed, is_top))
-        line_d = Job(net.scatter_line(sum_d.value))
+        line_u = Job(net.scatter_line(*sum_u.value))
         tokens_grad = step(
             (act_ranges, grad_qkv, grad_first, tokens, weight_a),
             call(
@@ -810,20 +870,19 @@
                 unit,
                 2 * moved,
             ),
-            [sum_a, sum_u, line_d, sum_s],
-            [sum_a, line_d, sum_s],
+            [sum_a, sum_d, line_u],
+            [sum_a, sum_d],
         )[0]
-        step((), None, [sum_a, sum_s], [sum_a, sum_u, sum_s])
-        line_u = Job(net.scatter_line(sum_u.value))
-        step((), None, [sum_a, line_d, line_u, sum_s], [line_d, line_u, sum_s])
-        step((), None, [line_u, sum_s], [sum_a, sum_s])
-        line_a = Job(net.scatter_line(sum_a.value))
-        step((), None, [line_a, sum_s], [line_u, line_a, sum_s])
-        step((), None, [line_a], [line_a])
-
-        (down_grad,), (up_grad,) = line_d.value, line_u.value
+        step((), None, [sum_a, sum_d], [sum_a, sum_d, line_u])
+        step((), None, [sum_a, line_u, sum_d, sum_s], [line_u, sum_d, sum_s])
+        step((), None, [sum_s], [sum_a, sum_s])
+        line_a = Job(net.scatter_line(*sum_a.value))
+        step((), None, [line_a, sum_s], [sum_s])
+        step((), None, [sum_s], [line_a, sum_s])
+        step((), None, [line_a, sum_s], [line_a, sum_s])
+
+        down_grad, up_grad, a_grad, packed = sum_d.value, line_u.value, line_a.value, sum_s.value
         down_grad = down_grad.T
-        (a_grad,), packed = line_a.value, sum_s.value
         qkv_grad = jnp.stack([a_grad[:, j * cols : (j + 1) * cols] for j in range(3)])
         out_grad = a_grad[:, 3 * cols :].T
         own = lax.dynamic_slice_in_dim(packed, blocks + lane, 1)

time: 227 us -> 234 us (1.031)
  waiting for transfers between devices: 85.4 us -> 102 us
  starting transfers between devices: 63.2 us -> 51.3 us
    ppermute x61, waiting for transfers between devices: 85.4 us -> 102 us  [step(): lax.ppermute(v, ALL, perm)]
    ppermute x61, starting transfers between devices: 63.2 us -> 51.3 us  [step(): lax.ppermute(v, ALL, perm)]
  transfers between devices with their start and end apart: 61 -> 61, of which waited for: 33 -> 35; matrix products, arithmetic and copies ran while one was open for 2% -> 2% of each run, Pallas kernels for 23% -> 22%
where the time goes in v5:
time: 234 us; the launch traced here: 233 us
  waiting for transfers between devices  102 us (44%)
  Pallas kernels  65.7 us (28%)
  starting transfers between devices  51.3 us (22%)
  local copies, waits for them, and re-layouts  6.73 us (3%)
  other arithmetic  5.98 us (3%)
    ppermute x61, waiting for transfers between devices, step(): lax.ppermute(v, ALL, perm)  102 us
    pallas_call x10, Pallas kernels, step(): outs = run(*ins) if run else ins  63 us
    ppermute x61, starting transfers between devices, step(): lax.ppermute(v, ALL, perm)  51.3 us
  transfers between devices with their start and end apart: 61, of which 35 were waited for; matrix products, arithmetic and copies ran while one was open for 2% of the time, Pallas kernels for 22%

profile of v5, /device:TPU:0, one launch (start us, length us, event | category | flops | bytes accessed | tf_op | source)
XLA Modules:
  0.0 233.2 jit_solution(16347950974010124322)
XLA Ops:
  4.2 4.1 %collective-permute-start = (bf16[1,96,768]{2,1,0:T(8,128)(2,1)S(1)}, bf16[1,96,768]{2,1,0:T(8,128)(2,1)S(1)}, u32[]{:S(2)}, u32[]{:S(2)}) collective-permute-start(bf16[1,96,768]{2,1,0:T(8,128)(2,1)S(1)} %bitcast.28), channel_id=1, source_target_pairs={{0,16},{1,17},{2,18},{3,19},{4,20},{5,21},{6,22},{7,23},{8,24},{9,... | collective-permute-start | bytes 442376 | tf_op jit(solution)/shard_map/ppermute | solution.py:78
  8.3 1.5 collective-permute-start.1
  9.8 2.1 collective-permute-done.1
  12.0 3.4 %collective-permute-done = bf16[1,96,768]{2,1,0:T(8,128)(2,1)S(1)} collective-permute-done((bf16[1,96,768]{2,1,0:T(8,128)(2,1)S(1)}, bf16[1,96,768]{2,1,0:T(8,128)(2,1)S(1)}, u32[]{:S(2)}, u32[]{:S(2)}) %collective-permute-start) | collective-permute-done | bytes 147488 | tf_op jit(solution)/shard_map/ppermute | solution.py:78
  18.4 5.2 %collective-permute-done.2 = bf16[2,96,768]{2,1,0:T(8,128)(2,1)S(1)} collective-permute-done((bf16[2,96,768]{2,1,0:T(8,128)(2,1)S(1)}, bf16[2,96,768]{2,1,0:T(8,128)(2,1)S(1)}, u32[]{:S(2)}, u32[]{:S(2)}) %collective-permute-start.2) | collective-permute-done | bytes 294944 | tf_op jit(solution)/shard_map/ppermute | solution.py:78
  23.7 1.3 collective-permute-start.4
  25.0 1.5 collective-permute-start.5
  26.6 3.3 %collective-permute-start.7 = (bf16[1,96,768]{2,1,0:T(8,128)(2,1)S(1)}, bf16[1,96,768]{2,1,0:T(8,128)(2,1)S(1)}, u32[]{:S(2)}, u32[]{:S(2)}) collective-permute-start(bf16[1,96,768]{2,1,0:T(8,128)(2,1)S(1)} %convert_bitcast_fusion.1), channel_id=1, source_target_pairs={{0,16},{1,17},{2,18},{3,19},{4,20},{5,21},{6,22},{7,23},{8,24},{9,... | collective-permute-start | bytes 442376 | tf_op jit(solution)/shard_map/ppermute | solution.py:78
  29.9 11.0 %collective-permute-done.7 = bf16[1,96,768]{2,1,0:T(8,128)(2,1)S(1)} collective-permute-done((bf16[1,96,768]{2,1,0:T(8,128)(2,1)S(1)}, bf16[1,96,768]{2,1,0:T(8,128)(2,1)S(1)}, u32[]{:S(2)}, u32[]{:S(2)}) %collective-permute-start.7) | collective-permute-done | bytes 147488 | tf_op jit(solution)/shard_map/ppermute | solution.py:78
  40.9 3.0 %collective-permute-done.8 = bf16[1,96,768]{2,1,0:T(8,128)(2,1)S(1)} collective-permute-done((bf16[1,96,768]{2,1,0:T(8,128)(2,1)S(1)}, bf16[1,96,768]{2,1,0:T(8,128)(2,1)S(1)}, u32[]{:S(2)}, u32[]{:S(2)}) %collective-permute-start.8) | collective-permute-done | bytes 147488 | tf_op jit(solution)/shard_map/ppermute | solution.py:78
  46.0 7.6 %collective-permute-done.10.rest_4_ = bf16[2,96,768]{2,1,0:T(8,128)(2,1)S(1)} collective-permute-done((bf16[2,96,768]{2,1,0:T(8,128)(2,1)S(1)}, bf16[2,96,768]{2,1,0:T(8,128)(2,1)S(1)}, u32[]{:S(2)}, u32[]{:S(2)}) %collective-permute-start.10) | collective-permute-done | bytes 294944 | tf_op jit(solution)/shard_map/ppermute | solution.py:78
  56.3 1.5 collective-permute-start.17
  57.9 11.3 %attn_forward.1 = (bf16[4,512,640]{2,1,0:T(8,128)(2,1)S(1)}, f32[4,8,512]{2,1,0:T(8,128)S(1)}, bf16[768,512]{1,0:T(8,128)(2,1)S(1)}, bf16[4,512,256]{2,1,0:T(8,1...) custom-call(f32[4]{0:T(128)S(1)} %copy-done.4, ...), custom_call_target="tpu_custom_call" | custom-call | flops 9663676416 | bytes 14155776 | tf_op jit(solution)/shard_map/attn_forward/pallas_call | solution.py:79
  69.2 1.5 copy-done.14
  71.8 1.6 collective-permute-start.19
  73.4 1.5 collective-permute-start.20
  76.2 3.3 %attn_finish.1 = (f32[512,768]{1,0:T(8,128)S(1)}, f32[512,1]{1,0:T(8,128)S(1)}, f32[512,768]{1,0:T(8,128)S(1)}, f32[512,768]{1,0:T(8,128)S(1)}, bf16[512,768]{1,...) custom-call(f32[4]{0:T(128)S(1)} %copy-done.4, ...), custom_call_target="tpu_custom_call" | custom-call | flops 4831838208 | bytes 9437184 | tf_op jit(solution)/shard_map/attn_finish/pallas_call | solution.py:79
  79.4 1.8 collective-permute-done.19.rest_1_
  85.4 3.9 %up_forward_0.1 = (bf16[2,512,768]{2,1,0:T(8,128)(2,1)S(1)}, f32[2,512,768]{2,1,0:T(8,128)S(1)}, f32[8,128]{1,0:T(8,128)S(1)}, bf16[2,768,768]{2,1,0:T(8,128)(2,1)S(1)}) custom-call(f32[4]{0:T(128)S(1)} %copy-done.4, bf16[512,768]{1,0:T(8,128)(2,1)S(1)} %get-tuple-element.424.mid_low, f32[4,1,1408]{2,1,0:T(1,128)S(1)} %bitcast.32, ...), custom_call_target="tpu_custom_call" | custom-call | flops 4831838208 | bytes 9437184 | tf_op jit(solution)/shard_map/up_forward_0/pallas_call | solution.py:79
  89.5 4.0 %up_forward_2.1 = (bf16[2,512,768]{2,1,0:T(8,128)(2,1)S(1)}, f32[2,512,768]{2,1,0:T(8,128)S(1)}, f32[8,128]{1,0:T(8,128)S(1)}, bf16[2,768,768]{2,1,0:T(8,128)(2,1)S(1)}) custom-call(f32[4]{0:T(128)S(1)} %copy-done.4, bf16[512,768]{1,0:T(8,128)(2,1)S(1)} %get-tuple-element.424.mid_low, f32[4,1,1408]{2,1,0:T(1,128)S(1)} %bitcast.33, ...), custom_call_target="tpu_custom_call" | custom-call | flops 4831838208 | bytes 9437184 | tf_op jit(solution)/shard_map/up_forward_2/pallas_call | solution.py:79
  93.4 6.6 %collective-permute-done.26.rest_2_ = bf16[4,96,768]{2,1,0:T(8,128)(2,1)S(1)} collective-permute-done((bf16[4,96,768]{2,1,0:T(8,128)(2,1)S(1)}, bf16[4,96,768]{2,1,0:T(8,128)(2,1)S(1)}, u32[]{:S(2)}, u32[]{:S(2)}) %collective-permute-start.26) | collective-permute-done | bytes 589856 | tf_op jit(solution)/shard_map/ppermute | solution.py:78
  100.9 1.5 collective-permute-start.28
  102.9 7.0 %collective-permute-done.28.rest_3_ = bf16[2,96,768]{2,1,0:T(8,128)(2,1)S(1)} collective-permute-done((bf16[2,96,768]{2,1,0:T(8,128)(2,1)S(1)}, bf16[2,96,768]{2,1,0:T(8,128)(2,1)S(1)}, u32[]{:S(2)}, u32[]{:S(2)}) %collective-permute-start.28) | collective-permute-done | bytes 294944 | tf_op jit(solution)/shard_map/ppermute | solution.py:78
  111.7 1.8 collective-permute-done.33.rest_8_
  114.0 8.8 %down_both.1 = (bf16[512,768]{1,0:T(8,128)(2,1)}, f32[512,768]{1,0:T(8,128)S(1)}, bf16[768,512]{1,0:T(8,128)(2,1)S(1)}, f32[8,768]{1,0:T(8,128)S(1)}, bf16[4,512...) custom-call(bf16[2,512,768]{2,1,0:T(8,128)(2,1)S(1)} %get-tuple-element.491.act0.rest_0_, ...), custom_call_target="tpu_custom_call" | custom-call | flops 4831838208 | bytes 18874368 | tf_op jit(solution)/shard_map/down_both/pallas_call | solution.py:79
  122.8 2.7 %down_grad.1 = (bf16[2,8,96,768]{3,2,1,0:T(8,128)(2,1)S(1)}, bf16[2,8,96,768]{3,2,1,0:T(8,128)(2,1)S(1)}) custom-call(bf16[768,512]{1,0:T(8,128)(2,1)S(1)} %get-tuple-element.490.left_t, bf16[2,512,768]{2,1,0:T(8,128)(2,1)S(1)} %get-tuple-element.491.act0.rest_0_, bf16[2,512,768]{2,1,0:T(8,128)(2,1)S(1)} %get-tuple-element.492.act1.rest_1_), custom_call_target="tpu_custom_call" | custom-call | flops 2415919104 | bytes 4718592 | tf_op jit(solution)/shard_map/down_grad/pallas_call | solution.py:79
  125.7 2.7 %up_grad.1 = (bf16[2,8,96,768]{3,2,1,0:T(8,128)(2,1)S(1)}, bf16[2,8,96,768]{3,2,1,0:T(8,128)(2,1)S(1)}) custom-call(bf16[768,512]{1,0:T(8,128)(2,1)S(1)} %get-tuple-element.494.left_t, bf16[4,512,768]{2,1,0:T(8,128)(2,1)S(1)} %get-tuple-element.506.rest_0_.grad_up), custom_call_target="tpu_custom_call" | custom-call | flops 2415919104 | bytes 4718592 | tf_op jit(solution)/shard_map/up_grad/pallas_call | solution.py:79
  128.4 1.7 collective-permute-done.35.got
  130.6 1.3 collective-permute-start.41
  131.9 3.1 %collective-permute-done.36.got = bf16[2,8,96,768]{3,2,1,0:T(8,128)(2,1)S(1)} collective-permute-done((bf16[2,8,96,768]{3,2,1,0:T(8,128)(2,1)S(1)}, bf16[2,8,96,768]{3,2,1,0:T(8,128)(2,1)S(1)}, u32[]{:S(2)}, u32[]{:S(2)}) %collective-permute-start.36) | collective-permute-done | bytes 2359328 | tf_op jit(solution)/shard_map/ppermute | solution.py:78
  136.3 6.2 %mid_backward.1 = (f32[512,768]{1,0:T(8,128)S(1)}, bf16[768,512]{1,0:T(8,128)(2,1)S(1)}, bf16[4,512,256]{2,1,0:T(8,128)(2,1)S(1)}, f32[8,768]{1,0:T(8,128)S(1)}) custom-call(bf16[4,512,768]{2,1,0:T(8,128)(2,1)S(1)} %get-tuple-element.506.rest_0_.grad_up, f32[512,768]{1,0:T(8,128)S(1)} %get-tuple-element.507.grad_second, ...), custom_call_target="tpu_custom_call" | custom-call | flops 3221225472 | bytes 14155776 | tf_op jit(solution)/shard_map/mid_backward/pallas_call | solution.py:79
  142.5 1.8 collective-permute-done.37.from_x
  144.9 1.6 collective-permute-start.39
  147.0 15.0 %attn_backward.1 = (bf16[4,512,640]{2,1,0:T(8,128)(2,1)S(1)}, bf16[2,8,96,768]{3,2,1,0:T(8,128)(2,1)S(1)}, bf16[2,8,96,768]{3,2,1,0:T(8,128)(2,1)S(1)}, f32[16,768]{1,0:T(8,128)S(1)}) custom-call(s32[1]{0:T(128)S(6)} %copy.34.longs, s32[12]{0:T(128)S(1)} %copy-done.11, bf16[4,512,640]{2,1,0:T(8,128)(2,1)S(1)} %copy-done.15, ...), custom_call_target="tpu_custom_call" | custom-call | flops 9663676416 | bytes 9437184 | tf_op jit(solution)/shard_map/attn_backward/pallas_call | solution.py:79
  165.9 5.1 %token_backward.1 = bf16[512,768]{1,0:T(8,128)(2,1)} custom-call(f32[4]{0:T(128)S(1)} %copy-done.4, bf16[4,512,640]{2,1,0:T(8,128)(2,1)S(1)} %get-tuple-element.568.grad_qkv, f32[512,768]{1,0:T(8,128)S(1)} %get-tuple-element.569.grad_first, bf16[512,768]{1,0:T(8,128)(2,1)S(1)} %copy-done, bf16[4,768,768]{2,1,0:T(8,128)(2,1)S(1)} %get-tuple-element.571.weight.out_weight), custom_call_target="tpu_custom_call" | custom-call | flops 2415919104 | bytes 9437184 | tf_op jit(solution)/shard_map/token_backward/pallas_call | solution.py:79
  171.4 1.6 collective-permute-start.45
  175.6 5.8 %collective-permute-done.45.from_x = bf16[2,96,768]{2,1,0:T(8,128)(2,1)S(1)} collective-permute-done((bf16[2,96,768]{2,1,0:T(8,128)(2,1)S(1)}, bf16[2,96,768]{2,1,0:T(8,128)(2,1)S(1)}, u32[]{:S(2)}, u32[]{:S(2)}) %collective-permute-start.45) | collective-permute-done | bytes 294944 | tf_op jit(solution)/shard_map/ppermute | solution.py:78
  181.4 1.5 collective-permute-done.46.from_y
  182.9 3.4 %collective-permute-done.47.in_x = bf16[2,96,768]{2,1,0:T(8,128)(2,1)S(1)} collective-permute-done((bf16[2,96,768]{2,1,0:T(8,128)(2,1)S(1)}, bf16[2,96,768]{2,1,0:T(8,128)(2,1)S(1)}, u32[]{:S(2)}, u32[]{:S(2)}) %collective-permute-start.47) | collective-permute-done | bytes 294944 | tf_op jit(solution)/shard_map/ppermute | solution.py:78
  189.9 2.4 %collective-permute-start.52 = (bf16[96,768]{1,0:T(8,128)(2,1)S(1)}, bf16[96,768]{1,0:T(8,128)(2,1)S(1)}, u32[]{:S(2)}, u32[]{:S(2)}) collective-permute-start(bf16[96,768]{1,0:T(8,128)(2,1)S(1)} %get-tuple-element.602), channel_id=1, source_target_pairs={{0,16},{1,17},{2,18},{3,19},{4,20},{5,21},{6,22},{7,23},{8,24},{9,... | collective-permute-start | bytes 442376 | tf_op jit(solution)/shard_map/ppermute | solution.py:78
  192.8 2.4 %collective-permute-start.54 = (f32[16,768]{1,0:T(8,128)S(1)}, f32[16,768]{1,0:T(8,128)S(1)}, u32[]{:S(2)}, u32[]{:S(2)}) collective-permute-start(f32[16,768]{1,0:T(8,128)S(1)} %get-tuple-element.604), channel_id=1, source_target_pairs={{0,16},{1,17},{2,18},{3,19},{4,20},{5,21},{6,22},{7,23},{8,24},{9,... | collective-permute-start | bytes 147464 | tf_op jit(solution)/shard_map/ppermute | solution.py:78
  195.2 10.8 %collective-permute-done.54 = f32[16,768]{1,0:T(8,128)S(1)} collective-permute-done((f32[16,768]{1,0:T(8,128)S(1)}, f32[16,768]{1,0:T(8,128)S(1)}, u32[]{:S(2)}, u32[]{:S(2)}) %collective-permute-start.54) | collective-permute-done | bytes 49184 | tf_op jit(solution)/shard_map/ppermute | solution.py:78
  206.6 3.6 %collective-permute-done.55 = f32[16,768]{1,0:T(8,128)S(1)} collective-permute-done((f32[16,768]{1,0:T(8,128)S(1)}, f32[16,768]{1,0:T(8,128)S(1)}, u32[]{:S(2)}, u32[]{:S(2)}) %collective-permute-start.55) | collective-permute-done | bytes 49184 | tf_op jit(solution)/shard_map/ppermute | solution.py:78
  213.6 2.4 %collective-permute-done.58 = f32[16,768]{1,0:T(8,128)S(1)} collective-permute-done((f32[16,768]{1,0:T(8,128)S(1)}, f32[16,768]{1,0:T(8,128)S(1)}, u32[]{:S(2)}, u32[]{:S(2)}) %collective-permute-start.58) | collective-permute-done | bytes 49184 | tf_op jit(solution)/shard_map/ppermute | solution.py:78
  216.0 4.0 %collective-permute-done.56.from_z = bf16[2,96,768]{2,1,0:T(8,128)(2,1)S(1)} collective-permute-done((bf16[2,96,768]{2,1,0:T(8,128)(2,1)S(1)}, bf16[2,96,768]{2,1,0:T(8,128)(2,1)S(1)}, u32[]{:S(2)}, u32[]{:S(2)}) %collective-permute-start.56) | collective-permute-done | bytes 294944 | tf_op jit(solution)/shard_map/ppermute | solution.py:78
  220.2 2.2 collective-permute-start.59
  224.0 2.4 %collective-permute-done.60 = f32[16,768]{1,0:T(8,128)S(1)} collective-permute-done((f32[16,768]{1,0:T(8,128)S(1)}, f32[16,768]{1,0:T(8,128)S(1)}, u32[]{:S(2)}, u32[]{:S(2)}) %collective-permute-start.60) | collective-permute-done | bytes 49184 | tf_op jit(solution)/shard_map/ppermute | solution.py:78
  226.4 3.2 %collective-permute-done.59 = bf16[96,768]{1,0:T(8,128)(2,1)S(1)} collective-permute-done((bf16[96,768]{1,0:T(8,128)(2,1)S(1)}, bf16[96,768]{1,0:T(8,128)(2,1)S(1)}, u32[]{:S(2)}, u32[]{:S(2)}) %collective-permute-start.59) | collective-permute-done | bytes 147488 | tf_op jit(solution)/shard_map/ppermute | solution.py:78
  (168 shorter events, 44.3 us)
Async XLA Ops:
  4.2 11.1 %collective-permute-start = (bf16[1,96,768]{2,1,0:T(8,128)(2,1)S(1)}, bf16[1,96,768]{2,1,0:T(8,128)(2,1)S(1)}, u32[]{:S(2)}, u32[]{:S(2)}) collective-permute-start(bf16[1,96,768]{2,1,0:T(8,128)(2,1)S(1)} %bitcast.28), channel_id=1, source_target_pairs={{0,16},{1,17},{2,18},{3,19},{4,20},{5,21},{6,22},{7,23},{8,24},{9,... | collective-permute-start | bytes 442376 | tf_op jit(solution)/shard_map/ppermute | solution.py:78
  15.4 8.2 %collective-permute-start.2 = (bf16[2,96,768]{2,1,0:T(8,128)(2,1)S(1)}, bf16[2,96,768]{2,1,0:T(8,128)(2,1)S(1)}, u32[]{:S(2)}, u32[]{:S(2)}) collective-permute-start(bf16[2,96,768]{2,1,0:T(8,128)(2,1)S(1)} %pad_maximum_fusion.3), channel_id=1, source_target_pairs={{0,8},{1,9},{2,10},{3,11},{4,12},{5,13},{6,14},{7,15},{8,0},{9,1},... | collective-permute-start | bytes 884744 | tf_op jit(solution)/shard_map/ppermute | solution.py:78
  23.7 20.2 %collective-permute-start.4 = (bf16[4,96,768]{2,1,0:T(8,128)(2,1)S(1)}, bf16[4,96,768]{2,1,0:T(8,128)(2,1)S(1)}, u32[]{:S(2)}, u32[]{:S(2)}) collective-permute-start(bf16[4,96,768]{2,1,0:T(8,128)(2,1)S(1)} %pad_maximum_fusion.rest_0_), channel_id=1, source_target_pairs={{0,2},{1,3},{2,0},{3,1},{4,6},{5,7},{6,4},{7,5},{8,10},{9,11},{10,... | collective-permute-start | bytes 1769480 | tf_op jit(solution)/shard_map/ppermute | solution.py:78
  25.0 18.9 %collective-permute-start.5 = (bf16[4,96,768]{2,1,0:T(8,128)(2,1)S(1)}, bf16[4,96,768]{2,1,0:T(8,128)(2,1)S(1)}, u32[]{:S(2)}, u32[]{:S(2)}) collective-permute-start(bf16[4,96,768]{2,1,0:T(8,128)(2,1)S(1)} %pad_maximum_fusion.rest_0_), channel_id=1, source_target_pairs={{0,4},{1,5},{2,6},{3,7},{4,0},{5,1},{6,2},{7,3},{8,12},{9,13},{10,... | collective-permute-start | bytes 1769480 | tf_op jit(solution)/shard_map/ppermute | solution.py:78
  26.6 17.3 %collective-permute-start.6 = (bf16[4,96,768]{2,1,0:T(8,128)(2,1)S(1)}, bf16[4,96,768]{2,1,0:T(8,128)(2,1)S(1)}, u32[]{:S(2)}, u32[]{:S(2)}) collective-permute-start(bf16[4,96,768]{2,1,0:T(8,128)(2,1)S(1)} %pad_maximum_fusion.rest_0_), channel_id=1, source_target_pairs={{0,1},{1,0},{2,3},{3,2},{4,5},{5,4},{6,7},{7,6},{8,9},{9,8},{10,11... | collective-permute-start | bytes 1769480 | tf_op jit(solution)/shard_map/ppermute | solution.py:78
  26.6 14.3 %collective-permute-start.7 = (bf16[1,96,768]{2,1,0:T(8,128)(2,1)S(1)}, bf16[1,96,768]{2,1,0:T(8,128)(2,1)S(1)}, u32[]{:S(2)}, u32[]{:S(2)}) collective-permute-start(bf16[1,96,768]{2,1,0:T(8,128)(2,1)S(1)} %convert_bitcast_fusion.1), channel_id=1, source_target_pairs={{0,16},{1,17},{2,18},{3,19},{4,20},{5,21},{6,22},{7,23},{8,24},{9,... | collective-permute-start | bytes 442376 | tf_op jit(solution)/shard_map/ppermute | solution.py:78
  29.9 14.0 %collective-permute-start.8 = (bf16[1,96,768]{2,1,0:T(8,128)(2,1)S(1)}, bf16[1,96,768]{2,1,0:T(8,128)(2,1)S(1)}, u32[]{:S(2)}, u32[]{:S(2)}) collective-permute-start(bf16[1,96,768]{2,1,0:T(8,128)(2,1)S(1)} %convert_bitcast_fusion), channel_id=1, source_target_pairs={{0,16},{1,17},{2,18},{3,19},{4,20},{5,21},{6,22},{7,23},{8,24},{9,... | collective-permute-start | bytes 442376 | tf_op jit(solution)/shard_map/ppermute | solution.py:78
  44.0 10.2 %collective-permute-start.11 = (bf16[4,96,768]{2,1,0:T(8,128)(2,1)S(1)}, bf16[4,96,768]{2,1,0:T(8,128)(2,1)S(1)}, u32[]{:S(2)}, u32[]{:S(2)}) collective-permute-start(bf16[4,96,768]{2,1,0:T(8,128)(2,1)S(1)} %collective-permute-done.5.rest_1_), channel_id=1, source_target_pairs={{0,1},{1,0},{2,3},{3,2},{4,5},{5,4},{6,7},{7,6},{8,9},{9,8},{10,11... | collective-permute-start | bytes 1769480 | tf_op jit(solution)/shard_map/ppermute | solution.py:78
  44.1 9.4 %collective-permute-start.10 = (bf16[2,96,768]{2,1,0:T(8,128)(2,1)S(1)}, bf16[2,96,768]{2,1,0:T(8,128)(2,1)S(1)}, u32[]{:S(2)}, u32[]{:S(2)}) collective-permute-start(bf16[2,96,768]{2,1,0:T(8,128)(2,1)S(1)} %slice.73), channel_id=1, source_target_pairs={{0,4},{1,5},{2,6},{3,7},{4,0},{5,1},{6,2},{7,3},{8,12},{9,13},{10,... | collective-permute-start | bytes 884744 | tf_op jit(solution)/shard_map/ppermute | solution.py:78
  44.7 9.1 %collective-permute-start.12 = (bf16[2,96,768]{2,1,0:T(8,128)(2,1)S(1)}, bf16[2,96,768]{2,1,0:T(8,128)(2,1)S(1)}, u32[]{:S(2)}, u32[]{:S(2)}) collective-permute-start(bf16[2,96,768]{2,1,0:T(8,128)(2,1)S(1)} %get-tuple-element.339), channel_id=1, source_target_pairs={{0,8},{1,9},{2,10},{3,11},{4,12},{5,13},{6,14},{7,15},{8,0},{9,1},... | collective-permute-start | bytes 884744 | tf_op jit(solution)/shard_map/ppermute | solution.py:78
  45.4 8.8 %collective-permute-start.9 = (bf16[2,96,768]{2,1,0:T(8,128)(2,1)S(1)}, bf16[2,96,768]{2,1,0:T(8,128)(2,1)S(1)}, u32[]{:S(2)}, u32[]{:S(2)}) collective-permute-start(bf16[2,96,768]{2,1,0:T(8,128)(2,1)S(1)} %slice.72), channel_id=1, source_target_pairs={{0,2},{1,3},{2,0},{3,1},{4,6},{5,7},{6,4},{7,5},{8,10},{9,11},{10,... | collective-permute-start | bytes 884744 | tf_op jit(solution)/shard_map/ppermute | solution.py:78
  55.7 15.7 %collective-permute-start.16 = (bf16[4,96,768]{2,1,0:T(8,128)(2,1)S(1)}, bf16[4,96,768]{2,1,0:T(8,128)(2,1)S(1)}, u32[]{:S(2)}, u32[]{:S(2)}) collective-permute-start(bf16[4,96,768]{2,1,0:T(8,128)(2,1)S(1)} %pad_maximum_fusion.1.rest_0_), channel_id=1, source_target_pairs={{0,2},{1,3},{2,0},{3,1},{4,6},{5,7},{6,4},{7,5},{8,10},{9,11},{10,... | collective-permute-start | bytes 1769480 | tf_op jit(solution)/shard_map/ppermute | solution.py:78
  56.3 15.4 %collective-permute-start.17 = (bf16[4,96,768]{2,1,0:T(8,128)(2,1)S(1)}, bf16[4,96,768]{2,1,0:T(8,128)(2,1)S(1)}, u32[]{:S(2)}, u32[]{:S(2)}) collective-permute-start(bf16[4,96,768]{2,1,0:T(8,128)(2,1)S(1)} %pad_maximum_fusion.1.rest_0_), channel_id=1, source_target_pairs={{0,4},{1,5},{2,6},{3,7},{4,0},{5,1},{6,2},{7,3},{8,12},{9,13},{10,... | collective-permute-start | bytes 1769480 | tf_op jit(solution)/shard_map/ppermute | solution.py:78
  57.8 13.9 %collective-permute-start.18 = (bf16[4,96,768]{2,1,0:T(8,128)(2,1)S(1)}, bf16[4,96,768]{2,1,0:T(8,128)(2,1)S(1)}, u32[]{:S(2)}, u32[]{:S(2)}) collective-permute-start(bf16[4,96,768]{2,1,0:T(8,128)(2,1)S(1)} %pad_maximum_fusion.1.rest_0_), channel_id=1, source_target_pairs={{0,1},{1,0},{2,3},{3,2},{4,5},{5,4},{6,7},{7,6},{8,9},{9,8},{10,11... | collective-permute-start | bytes 1769480 | tf_op jit(solution)/shard_map/ppermute | solution.py:78
  71.7 11.9 %collective-permute-start.21 = (bf16[4,96,768]{2,1,0:T(8,128)(2,1)S(1)}, bf16[4,96,768]{2,1,0:T(8,128)(2,1)S(1)}, u32[]{:S(2)}, u32[]{:S(2)}) collective-permute-start(bf16[4,96,768]{2,1,0:T(8,128)(2,1)S(1)} %collective-permute-done.17.rest_1_), channel_id=1, source_target_pairs={{0,1},{1,0},{2,3},{3,2},{4,5},{5,4},{6,7},{7,6},{8,9},{9,8},{10,11... | collective-permute-start | bytes 1769480 | tf_op jit(solution)/shard_map/ppermute | solution.py:78
  71.8 9.4 %collective-permute-start.19 = (bf16[2,96,768]{2,1,0:T(8,128)(2,1)S(1)}, bf16[2,96,768]{2,1,0:T(8,128)(2,1)S(1)}, u32[]{:S(2)}, u32[]{:S(2)}) collective-permute-start(bf16[2,96,768]{2,1,0:T(8,128)(2,1)S(1)} %slice.74), channel_id=1, source_target_pairs={{0,2},{1,3},{2,0},{3,1},{4,6},{5,7},{6,4},{7,5},{8,10},{9,11},{10,... | collective-permute-start | bytes 884744 | tf_op jit(solution)/shard_map/ppermute | solution.py:78
  73.4 9.1 %collective-permute-start.20 = (bf16[2,96,768]{2,1,0:T(8,128)(2,1)S(1)}, bf16[2,96,768]{2,1,0:T(8,128)(2,1)S(1)}, u32[]{:S(2)}, u32[]{:S(2)}) collective-permute-start(bf16[2,96,768]{2,1,0:T(8,128)(2,1)S(1)} %slice.75), channel_id=1, source_target_pairs={{0,4},{1,5},{2,6},{3,7},{4,0},{5,1},{6,2},{7,3},{8,12},{9,13},{10,... | collective-permute-start | bytes 884744 | tf_op jit(solution)/shard_map/ppermute | solution.py:78
  74.9 8.8 %collective-permute-start.22 = (bf16[2,96,768]{2,1,0:T(8,128)(2,1)S(1)}, bf16[2,96,768]{2,1,0:T(8,128)(2,1)S(1)}, u32[]{:S(2)}, u32[]{:S(2)}) collective-permute-start(bf16[2,96,768]{2,1,0:T(8,128)(2,1)S(1)} %get-tuple-element.398), channel_id=1, source_target_pairs={{0,8},{1,9},{2,10},{3,11},{4,12},{5,13},{6,14},{7,15},{8,0},{9,1},... | collective-permute-start | bytes 884744 | tf_op jit(solution)/shard_map/ppermute | solution.py:78
  83.7 5.7 %collective-permute-start.23 = (bf16[4,96,768]{2,1,0:T(8,128)(2,1)S(1)}, bf16[4,96,768]{2,1,0:T(8,128)(2,1)S(1)}, u32[]{:S(2)}, u32[]{:S(2)}) collective-permute-start(bf16[4,96,768]{2,1,0:T(8,128)(2,1)S(1)} %collective-permute-done.16.rest_0_), channel_id=1, source_target_pairs={{0,1},{1,0},{2,3},{3,2},{4,5},{5,4},{6,7},{7,6},{8,9},{9,8},{10,11... | collective-permute-start | bytes 1769480 | tf_op jit(solution)/shard_map/ppermute | solution.py:78
  83.8 5.6 %collective-permute-start.24 = (bf16[2,96,768]{2,1,0:T(8,128)(2,1)S(1)}, bf16[2,96,768]{2,1,0:T(8,128)(2,1)S(1)}, u32[]{:S(2)}, u32[]{:S(2)}) collective-permute-start(bf16[2,96,768]{2,1,0:T(8,128)(2,1)S(1)} %collective-permute-done.19.rest_1_), channel_id=1, source_target_pairs={{0,1},{1,0},{2,3},{3,2},{4,5},{5,4},{6,7},{7,6},{8,9},{9,8},{10,11... | collective-permute-start | bytes 884744 | tf_op jit(solution)/shard_map/ppermute | solution.py:78
  84.3 5.1 %collective-permute-start.25 = (bf16[2,96,768]{2,1,0:T(8,128)(2,1)S(1)}, bf16[2,96,768]{2,1,0:T(8,128)(2,1)S(1)}, u32[]{:S(2)}, u32[]{:S(2)}) collective-permute-start(bf16[2,96,768]{2,1,0:T(8,128)(2,1)S(1)} %collective-permute-done.20.rest_2_), channel_id=1, source_target_pairs={{0,1},{1,0},{2,3},{3,2},{4,5},{5,4},{6,7},{7,6},{8,9},{9,8},{10,11... | collective-permute-start | bytes 884744 | tf_op jit(solution)/shard_map/ppermute | solution.py:78
  84.4 15.7 %collective-permute-start.26 = (bf16[4,96,768]{2,1,0:T(8,128)(2,1)S(1)}, bf16[4,96,768]{2,1,0:T(8,128)(2,1)S(1)}, u32[]{:S(2)}, u32[]{:S(2)}) collective-permute-start(bf16[4,96,768]{2,1,0:T(8,128)(2,1)S(1)} %pad_maximum_fusion.2.rest_0_), channel_id=1, source_target_pairs={{0,2},{1,3},{2,0},{3,1},{4,6},{5,7},{6,4},{7,5},{8,10},{9,11},{10,... | collective-permute-start | bytes 1769480 | tf_op jit(solution)/shard_map/ppermute | solution.py:78
  84.9 15.4 %collective-permute-start.27 = (bf16[4,96,768]{2,1,0:T(8,128)(2,1)S(1)}, bf16[4,96,768]{2,1,0:T(8,128)(2,1)S(1)}, u32[]{:S(2)}, u32[]{:S(2)}) collective-permute-start(bf16[4,96,768]{2,1,0:T(8,128)(2,1)S(1)} %pad_maximum_fusion.2.rest_0_), channel_id=1, source_target_pairs={{0,4},{1,5},{2,6},{3,7},{4,0},{5,1},{6,2},{7,3},{8,12},{9,13},{10,... | collective-permute-start | bytes 1769480 | tf_op jit(solution)/shard_map/ppermute | solution.py:78
  100.4 10.8 %collective-permute-start.30 = (bf16[4,96,768]{2,1,0:T(8,128)(2,1)S(1)}, bf16[4,96,768]{2,1,0:T(8,128)(2,1)S(1)}, u32[]{:S(2)}, u32[]{:S(2)}) collective-permute-start(bf16[4,96,768]{2,1,0:T(8,128)(2,1)S(1)} %collective-permute-done.27.rest_1_), channel_id=1, source_target_pairs={{0,1},{1,0},{2,3},{3,2},{4,5},{5,4},{6,7},{7,6},{8,9},{9,8},{10,11... | collective-permute-start | bytes 1769480 | tf_op jit(solution)/shard_map/ppermute | solution.py:78
  100.5 10.7 %collective-permute-start.31 = (bf16[4,96,768]{2,1,0:T(8,128)(2,1)S(1)}, bf16[4,96,768]{2,1,0:T(8,128)(2,1)S(1)}, u32[]{:S(2)}, u32[]{:S(2)}) collective-permute-start(bf16[4,96,768]{2,1,0:T(8,128)(2,1)S(1)} %pad_maximum_fusion.2.rest_0_), channel_id=1, source_target_pairs={{0,1},{1,0},{2,3},{3,2},{4,5},{5,4},{6,7},{7,6},{8,9},{9,8},{10,11... | collective-permute-start | bytes 1769480 | tf_op jit(solution)/shard_map/ppermute | solution.py:78
  100.9 9.0 %collective-permute-start.28 = (bf16[2,96,768]{2,1,0:T(8,128)(2,1)S(1)}, bf16[2,96,768]{2,1,0:T(8,128)(2,1)S(1)}, u32[]{:S(2)}, u32[]{:S(2)}) collective-permute-start(bf16[2,96,768]{2,1,0:T(8,128)(2,1)S(1)} %slice.76), channel_id=1, source_target_pairs={{0,2},{1,3},{2,0},{3,1},{4,6},{5,7},{6,4},{7,5},{8,10},{9,11},{10,... | collective-permute-start | bytes 884744 | tf_op jit(solution)/shard_map/ppermute | solution.py:78
  102.4 8.7 %collective-permute-start.29 = (bf16[2,96,768]{2,1,0:T(8,128)(2,1)S(1)}, bf16[2,96,768]{2,1,0:T(8,128)(2,1)S(1)}, u32[]{:S(2)}, u32[]{:S(2)}) collective-permute-start(bf16[2,96,768]{2,1,0:T(8,128)(2,1)S(1)} %slice.77), channel_id=1, source_target_pairs={{0,4},{1,5},{2,6},{3,7},{4,0},{5,1},{6,2},{7,3},{8,12},{9,13},{10,... | collective-permute-start | bytes 884744 | tf_op jit(solution)/shard_map/ppermute | solution.py:78
  125.5 4.6 %collective-permute-start.35 = (bf16[2,8,96,768]{3,2,1,0:T(8,128)(2,1)S(1)}, bf16[2,8,96,768]{3,2,1,0:T(8,128)(2,1)S(1)}, u32[]{:S(2)}, u32[]{:S(2)}) collective-permute-start(bf16[2,8,96,768]{3,2,1,0:T(8,128)(2,1)S(1)} %get-tuple-element.498), channel_id=1, source_target_pairs={{0,1},{1,0},{2,3},{3,2},{4,5},{5,4},{6,7},{7,6},{8,9},{9,8},{10,11... | collective-permute-start | bytes 7077896 | tf_op jit(solution)/shard_map/ppermute | solution.py:78
  130.6 31.4 %collective-permute-start.41 = (bf16[2,4,96,768]{3,2,1,0:T(8,128)(2,1)S(1)}, bf16[2,4,96,768]{3,2,1,0:T(8,128)(2,1)S(1)}, u32[]{:S(2)}, u32[]{:S(2)}) collective-permute-start(bf16[2,4,96,768]{3,2,1,0:T(8,128)(2,1)S(1)} %near_z_sums.1), channel_id=1, source_target_pairs={{0,8},{1,9},{2,10},{3,11},{4,12},{5,13},{6,14},{7,15},{8,0},{9,1},... | collective-permute-start | bytes 3538952 | tf_op jit(solution)/shard_map/ppermute | solution.py:78
  135.2 9.1 %collective-permute-start.37 = (bf16[2,96,768]{2,1,0:T(8,128)(2,1)S(1)}, bf16[2,96,768]{2,1,0:T(8,128)(2,1)S(1)}, u32[]{:S(2)}, u32[]{:S(2)}) collective-permute-start(bf16[2,96,768]{2,1,0:T(8,128)(2,1)S(1)} %get-tuple-element.520), channel_id=1, source_target_pairs={{0,2},{1,3},{2,0},{3,1},{4,6},{5,7},{6,4},{7,5},{8,10},{9,11},{10,... | collective-permute-start | bytes 884744 | tf_op jit(solution)/shard_map/ppermute | solution.py:78
  135.8 8.8 %collective-permute-start.38 = (bf16[2,96,768]{2,1,0:T(8,128)(2,1)S(1)}, bf16[2,96,768]{2,1,0:T(8,128)(2,1)S(1)}, u32[]{:S(2)}, u32[]{:S(2)}) collective-permute-start(bf16[2,96,768]{2,1,0:T(8,128)(2,1)S(1)} %get-tuple-element.521), channel_id=1, source_target_pairs={{0,4},{1,5},{2,6},{3,7},{4,0},{5,1},{6,2},{7,3},{8,12},{9,13},{10,... | collective-permute-start | bytes 884744 | tf_op jit(solution)/shard_map/ppermute | solution.py:78
  144.9 17.1 %collective-permute-start.39 = (bf16[4,96,768]{2,1,0:T(8,128)(2,1)S(1)}, bf16[4,96,768]{2,1,0:T(8,128)(2,1)S(1)}, u32[]{:S(2)}, u32[]{:S(2)}) collective-permute-start(bf16[4,96,768]{2,1,0:T(8,128)(2,1)S(1)} %get-tuple-element.555), channel_id=1, source_target_pairs={{0,2},{1,3},{2,0},{3,1},{4,6},{5,7},{6,4},{7,5},{8,10},{9,11},{10,... | collective-permute-start | bytes 1769480 | tf_op jit(solution)/shard_map/ppermute | solution.py:78
  146.4 15.6 %collective-permute-start.40 = (bf16[4,96,768]{2,1,0:T(8,128)(2,1)S(1)}, bf16[4,96,768]{2,1,0:T(8,128)(2,1)S(1)}, u32[]{:S(2)}, u32[]{:S(2)}) collective-permute-start(bf16[4,96,768]{2,1,0:T(8,128)(2,1)S(1)} %get-tuple-element.556), channel_id=1, source_target_pairs={{0,4},{1,5},{2,6},{3,7},{4,0},{5,1},{6,2},{7,3},{8,12},{9,13},{10,... | collective-permute-start | bytes 1769480 | tf_op jit(solution)/shard_map/ppermute | solution.py:78
  162.5 8.5 %collective-permute-start.42 = (bf16[2,8,96,768]{3,2,1,0:T(8,128)(2,1)S(1)}, bf16[2,8,96,768]{3,2,1,0:T(8,128)(2,1)S(1)}, u32[]{:S(2)}, u32[]{:S(2)}) collective-permute-start(bf16[2,8,96,768]{3,2,1,0:T(8,128)(2,1)S(1)} %get-tuple-element.572), channel_id=1, source_target_pairs={{0,1},{1,0},{2,3},{3,2},{4,5},{5,4},{6,7},{7,6},{8,9},{9,8},{10,11... | collective-permute-start | bytes 7077896 | tf_op jit(solution)/shard_map/ppermute | solution.py:78
  162.6 8.5 %collective-permute-start.43 = (bf16[96,768]{1,0:T(8,128)(2,1)S(1)}, bf16[96,768]{1,0:T(8,128)(2,1)S(1)}, u32[]{:S(2)}, u32[]{:S(2)}) collective-permute-start(bf16[96,768]{1,0:T(8,128)(2,1)S(1)} %get-tuple-element.573), channel_id=1, source_target_pairs={{0,2},{1,3},{2,0},{3,1},{4,6},{5,7},{6,4},{7,5},{8,10},{9,11},{10,... | collective-permute-start | bytes 442376 | tf_op jit(solution)/shard_map/ppermute | solution.py:78
  163.8 7.3 %collective-permute-start.44 = (bf16[96,768]{1,0:T(8,128)(2,1)S(1)}, bf16[96,768]{1,0:T(8,128)(2,1)S(1)}, u32[]{:S(2)}, u32[]{:S(2)}) collective-permute-start(bf16[96,768]{1,0:T(8,128)(2,1)S(1)} %get-tuple-element.574), channel_id=1, source_target_pairs={{0,4},{1,5},{2,6},{3,7},{4,0},{5,1},{6,2},{7,3},{8,12},{9,13},{10,... | collective-permute-start | bytes 442376 | tf_op jit(solution)/shard_map/ppermute | solution.py:78
  164.7 10.9 %collective-permute-start.49 = (bf16[2,96,768]{2,1,0:T(8,128)(2,1)S(1)}, bf16[2,96,768]{2,1,0:T(8,128)(2,1)S(1)}, u32[]{:S(2)}, u32[]{:S(2)}) collective-permute-start(bf16[2,96,768]{2,1,0:T(8,128)(2,1)S(1)} %get-tuple-element.588), channel_id=1, source_target_pairs={{0,8},{1,9},{2,10},{3,11},{4,12},{5,13},{6,14},{7,15},{8,0},{9,1},... | collective-permute-start | bytes 884744 | tf_op jit(solution)/shard_map/ppermute | solution.py:78
  171.4 9.9 %collective-permute-start.45 = (bf16[2,96,768]{2,1,0:T(8,128)(2,1)S(1)}, bf16[2,96,768]{2,1,0:T(8,128)(2,1)S(1)}, u32[]{:S(2)}, u32[]{:S(2)}) collective-permute-start(bf16[2,96,768]{2,1,0:T(8,128)(2,1)S(1)} %get-tuple-element.584), channel_id=1, source_target_pairs={{0,2},{1,3},{2,0},{3,1},{4,6},{5,7},{6,4},{7,5},{8,10},{9,11},{10,... | collective-permute-start | bytes 884744 | tf_op jit(solution)/shard_map/ppermute | solution.py:78
  173.0 9.9 %collective-permute-start.46 = (bf16[2,96,768]{2,1,0:T(8,128)(2,1)S(1)}, bf16[2,96,768]{2,1,0:T(8,128)(2,1)S(1)}, u32[]{:S(2)}, u32[]{:S(2)}) collective-permute-start(bf16[2,96,768]{2,1,0:T(8,128)(2,1)S(1)} %get-tuple-element.585), channel_id=1, source_target_pairs={{0,4},{1,5},{2,6},{3,7},{4,0},{5,1},{6,2},{7,3},{8,12},{9,13},{10,... | collective-permute-start | bytes 884744 | tf_op jit(solution)/shard_map/ppermute | solution.py:78
  173.5 12.8 %collective-permute-start.47 = (bf16[2,96,768]{2,1,0:T(8,128)(2,1)S(1)}, bf16[2,96,768]{2,1,0:T(8,128)(2,1)S(1)}, u32[]{:S(2)}, u32[]{:S(2)}) collective-permute-start(bf16[2,96,768]{2,1,0:T(8,128)(2,1)S(1)} %get-tuple-element.586), channel_id=1, source_target_pairs={{0,2},{1,3},{2,0},{3,1},{4,6},{5,7},{6,4},{7,5},{8,10},{9,11},{10,... | collective-permute-start | bytes 884744 | tf_op jit(solution)/shard_map/ppermute | solution.py:78
  174.6 12.9 %collective-permute-start.48 = (bf16[2,96,768]{2,1,0:T(8,128)(2,1)S(1)}, bf16[2,96,768]{2,1,0:T(8,128)(2,1)S(1)}, u32[]{:S(2)}, u32[]{:S(2)}) collective-permute-start(bf16[2,96,768]{2,1,0:T(8,128)(2,1)S(1)} %get-tuple-element.587), channel_id=1, source_target_pairs={{0,4},{1,5},{2,6},{3,7},{4,0},{5,1},{6,2},{7,3},{8,12},{9,13},{10,... | collective-permute-start | bytes 884744 | tf_op jit(solution)/shard_map/ppermute | solution.py:78
  188.2 22.0 %collective-permute-start.50 = (bf16[4,96,768]{2,1,0:T(8,128)(2,1)S(1)}, bf16[4,96,768]{2,1,0:T(8,128)(2,1)S(1)}, u32[]{:S(2)}, u32[]{:S(2)}) collective-permute-start(bf16[4,96,768]{2,1,0:T(8,128)(2,1)S(1)} %get-tuple-element.600), channel_id=1, source_target_pairs={{0,2},{1,3},{2,0},{3,1},{4,6},{5,7},{6,4},{7,5},{8,10},{9,11},{10,... | collective-permute-start | bytes 1769480 | tf_op jit(solution)/shard_map/ppermute | solution.py:78
  188.8 21.4 %collective-permute-start.51 = (bf16[4,96,768]{2,1,0:T(8,128)(2,1)S(1)}, bf16[4,96,768]{2,1,0:T(8,128)(2,1)S(1)}, u32[]{:S(2)}, u32[]{:S(2)}) collective-permute-start(bf16[4,96,768]{2,1,0:T(8,128)(2,1)S(1)} %get-tuple-element.601), channel_id=1, source_target_pairs={{0,4},{1,5},{2,6},{3,7},{4,0},{5,1},{6,2},{7,3},{8,12},{9,13},{10,... | collective-permute-start | bytes 1769480 | tf_op jit(solution)/shard_map/ppermute | solution.py:78
  189.9 16.1 %collective-permute-start.52 = (bf16[96,768]{1,0:T(8,128)(2,1)S(1)}, bf16[96,768]{1,0:T(8,128)(2,1)S(1)}, u32[]{:S(2)}, u32[]{:S(2)}) collective-permute-start(bf16[96,768]{1,0:T(8,128)(2,1)S(1)} %get-tuple-element.602), channel_id=1, source_target_pairs={{0,16},{1,17},{2,18},{3,19},{4,20},{5,21},{6,22},{7,23},{8,24},{9,... | collective-permute-start | bytes 442376 | tf_op jit(solution)/shard_map/ppermute | solution.py:78
  192.2 13.8 %collective-permute-start.53 = (bf16[96,768]{1,0:T(8,128)(2,1)S(1)}, bf16[96,768]{1,0:T(8,128)(2,1)S(1)}, u32[]{:S(2)}, u32[]{:S(2)}) collective-permute-start(bf16[96,768]{1,0:T(8,128)(2,1)S(1)} %get-tuple-element.603), channel_id=1, source_target_pairs={{0,16},{1,17},{2,18},{3,19},{4,20},{5,21},{6,22},{7,23},{8,24},{9,... | collective-permute-start | bytes 442376 | tf_op jit(solution)/shard_map/ppermute | solution.py:78
  192.8 13.2 %collective-permute-start.54 = (f32[16,768]{1,0:T(8,128)S(1)}, f32[16,768]{1,0:T(8,128)S(1)}, u32[]{:S(2)}, u32[]{:S(2)}) collective-permute-start(f32[16,768]{1,0:T(8,128)S(1)} %get-tuple-element.604), channel_id=1, source_target_pairs={{0,16},{1,17},{2,18},{3,19},{4,20},{5,21},{6,22},{7,23},{8,24},{9,... | collective-permute-start | bytes 147464 | tf_op jit(solution)/shard_map/ppermute | solution.py:78
  210.6 9.4 %collective-permute-start.56 = (bf16[2,96,768]{2,1,0:T(8,128)(2,1)S(1)}, bf16[2,96,768]{2,1,0:T(8,128)(2,1)S(1)}, u32[]{:S(2)}, u32[]{:S(2)}) collective-permute-start(bf16[2,96,768]{2,1,0:T(8,128)(2,1)S(1)} %get-tuple-element.611), channel_id=1, source_target_pairs={{0,8},{1,9},{2,10},{3,11},{4,12},{5,13},{6,14},{7,15},{8,0},{9,1},... | collective-permute-start | bytes 884744 | tf_op jit(solution)/shard_map/ppermute | solution.py:78
  220.2 9.4 %collective-permute-start.59 = (bf16[96,768]{1,0:T(8,128)(2,1)S(1)}, bf16[96,768]{1,0:T(8,128)(2,1)S(1)}, u32[]{:S(2)}, u32[]{:S(2)}) collective-permute-start(bf16[96,768]{1,0:T(8,128)(2,1)S(1)} %get-tuple-element.617), channel_id=1, source_target_pairs={{0,16},{1,17},{2,18},{3,19},{4,20},{5,21},{6,22},{7,23},{8,24},{9,... | collective-permute-start | bytes 442376 | tf_op jit(solution)/shard_map/ppermute | solution.py:78
  (29 other events, 328.2 us)

commit v6 on v5

--- a/solution.py
+++ b/solution.py
@@ -144,12 +144,13 @@
     @staticmethod
     def scatter_z_first(far, near):
         (got,) = yield [(far, PC)]
-        (from_z,) = yield [(add_near_z(near, got), PZ1)]
-        out_x, out_y = add_corner(near, got, from_z)
-        from_x, from_y = yield [(out_x, PX), (out_y, PY)]
-        out_x, out_y = add_sides(near, got, from_z, from_x, from_y)
+        out_1, out_0 = add_near_z(near, got)
+        (from_1,) = yield [(out_1, PZ1)]
+        out_x, out_y = add_corner(near, got, from_1)
+        from_x, from_y, from_0 = yield [(out_x, PX), (out_y, PY), (out_0, PZ1)]
+        out_x, out_y = add_sides(near, got, from_1, from_0, from_x, from_y)
         in_x, in_y = yield [(out_x, PX), (out_y, PY)]
-        out_z, kept = add_own(near, got, from_z, in_x, in_y)
+        out_z, kept = add_own(near, got, from_0, in_x, in_y)
         (last,) = yield [(out_z, PZ2)]
         return kept + last.astype(f32)
 
@@ -296,45 +297,48 @@
 
 
 def add_near_z(near, got):
-    def near_z_sums(near, got, out):
-        for y in range(2):
-            for k in range(2):
-                out[:, 2 * y + k] = (near[:, 4 * y + 2 + k].astype(f32) + got[:, 4 * y + 2 + k].astype(f32)).astype(bf16)
-
-    return glue(near_z_sums, [like((2, 4) + near.shape[2:], bf16)], near, got)[0]
+    def near_z_sums(near, got, out_1, out_0):
+        for x, out in ((1, out_1), (0, out_0)):
+            for y in range(2):
+                for k in range(2):
+                    at = 4 * y + 2 + k
+                    out[2 * y + k] = (near[x, at].astype(f32) + got[x, at].astype(f32)).astype(bf16)
+
+    part = like((4,) + near.shape[2:], bf16)
+    return glue(near_z_sums, [part, part], near, got)
 
 
 def three(near, got, from_z, x, y, k):
-    return near[x, 4 * y + k].astype(f32) + got[x, 4 * y + k].astype(f32) + from_z[x, 2 * y + k].astype(f32)
-
-
-def add_corner(near, got, from_z):
-    def corner_sums(near, got, from_z, out_x, out_y):
-        out_x[...] = three(near, got, from_z, 1, 1, 0).astype(bf16)
-        out_y[...] = three(near, got, from_z, 1, 1, 1).astype(bf16)
+    return near[x, 4 * y + k].astype(f32) + got[x, 4 * y + k].astype(f32) + from_z[2 * y + k].astype(f32)
+
+
+def add_corner(near, got, from_1):
+    def corner_sums(near, got, from_1, out_x, out_y):
+        out_x[...] = three(near, got, from_1, 1, 1, 0).astype(bf16)
+        out_y[...] = three(near, got, from_1, 1, 1, 1).astype(bf16)
 
     part = like(near.shape[2:], bf16)
-    return glue(corner_sums, [part, part], near, got, from_z)
-
-
-def add_sides(near, got, from_z, from_x, from_y):
-    def side_sums(near, got, from_z, from_x, from_y, out_x, out_y):
-        out_x[0] = three(near, got, from_z, 1, 0, 0).astype(bf16)
-        out_x[1] = (three(near, got, from_z, 1, 0, 1) + from_y[...].astype(f32)).astype(bf16)
-        out_y[0] = (three(near, got, from_z, 0, 1, 0) + from_x[...].astype(f32)).astype(bf16)
-        out_y[1] = three(near, got, from_z, 0, 1, 1).astype(bf16)
+    return glue(corner_sums, [part, part], near, got, from_1)
+
+
+def add_sides(near, got, from_1, from_0, from_x, from_y):
+    def side_sums(near, got, from_1, from_0, from_x, from_y, out_x, out_y):
+        out_x[0] = three(near, got, from_1, 1, 0, 0).astype(bf16)
+        out_x[1] = (three(near, got, from_1, 1, 0, 1) + from_y[...].astype(f32)).astype(bf16)
+        out_y[0] = (three(near, got, from_0, 0, 1, 0) + from_x[...].astype(f32)).astype(bf16)
+        out_y[1] = three(near, got, from_0, 0, 1, 1).astype(bf16)
 
     part = like((2,) + near.shape[2:], bf16)
-    return glue(side_sums, [part, part], near, got, from_z, from_x, from_y)
-
-
-def add_own(near, got, from_z, in_x, in_y):
-    def own_sums(near, got, from_z, in_x, in_y, out, kept):
-        kept[...] = three(near, got, from_z, 0, 0, 0) + in_x[0].astype(f32) + in_y[0].astype(f32)
-        out[...] = (three(near, got, from_z, 0, 0, 1) + in_x[1].astype(f32) + in_y[1].astype(f32)).astype(bf16)
+    return glue(side_sums, [part, part], near, got, from_1, from_0, from_x, from_y)
+
+
+def add_own(near, got, from_0, in_x, in_y):
+    def own_sums(near, got, from_0, in_x, in_y, out, kept):
+        kept[...] = three(near, got, from_0, 0, 0, 0) + in_x[0].astype(f32) + in_y[0].astype(f32)
+        out[...] = (three(near, got, from_0, 0, 0, 1) + in_x[1].astype(f32) + in_y[1].astype(f32)).astype(bf16)
 
     shape = near.shape[2:]
-    return glue(own_sums, [like(shape, bf16), like(shape)], near, got, from_z, in_x, in_y)
+    return glue(own_sums, [like(shape, bf16), like(shape)], near, got, from_0, in_x, in_y)
 
 
 def attn_shard(qkv_weight, out_weight):
@@ -694,10 +698,10 @@
         unit = 2 * rows * width * width * blocks
         moved = 2 * width * width * blocks
 
+        step((), None, [job_a], [job_a])
         step((), None, [job_a, job_b], [job_a, job_b])
-        step((), None, [job_a, job_b], [job_a, job_b])
+        step((), None, [job_a, job_u, job_b], [job_a, job_u, job_b])
         step((), None, [job_a, job_u, job_d], [job_a, job_u, job_d])
-        step((), None, [job_a, job_u], [job_a, job_u])
         step((), None, [job_u, job_a], [job_a])
         biases = job_b.value
 
@@ -817,9 +821,8 @@
                 finish,
             )
 
-        sum_d = Job(net.scatter_z_first(*grad_of("down_grad", ffn_t, (act0, act1))))
-        sum_u = Job(net.scatter_sum(*grad_of("up_grad", mid_t, (grad_up,), [sum_d], [sum_d])))
-        step((), None, [sum_u, sum_d], [sum_u])
+        sum_u = Job(net.scatter_sum(*grad_of("up_grad", mid_t, (grad_up,))))
+        sum_d = Job(net.scatter_z_first(*grad_of("down_grad", ffn_t, (act0, act1), [sum_u], [sum_u])))
         grad_first, attn_t, grad_ctx, sums_a = step(
             (grad_up, grad_second, mid_slope, normed, inv, first_gain, ctx_slope, weight_u0, weight_u1, weight_a),
             call(
@@ -836,8 +839,8 @@
                 unit + unit // 3,
                 3 * moved,
             ),
-            [sum_u],
-            [sum_u],
+            [sum_d, sum_u],
+            [sum_d, sum_u],
         )
 
         grad_qkv, far, near, packed = step(
@@ -852,13 +855,14 @@
                 4 * unit,
                 2 * moved,
             ),
-            [sum_u],
+            [sum_u, sum_d],
             [sum_u, sum_d],
         )
         sum_a = Job(net.scatter_sum(far, near))
         is_top = (jnp.arange(packed.shape[0]) == 2 * blocks + 6)[:, None]
         sum_s = Job(net.sum_max(packed, is_top))
         line_u = Job(net.scatter_line(*sum_u.value))
+        step((), None, [sum_a, sum_d, sum_s], [sum_a, sum_s])
         tokens_grad = step(
             (act_ranges, grad_qkv, grad_first, tokens, weight_a),
             call(
@@ -870,16 +874,14 @@
                 unit,
                 2 * moved,
             ),
-            [sum_a, sum_d, line_u],
+            [sum_a],
             [sum_a, sum_d],
         )[0]
-        step((), None, [sum_a, sum_d], [sum_a, sum_d, line_u])
-        step((), None, [sum_a, line_u, sum_d, sum_s], [line_u, sum_d, sum_s])
-        step((), None, [sum_s], [sum_a, sum_s])
+        step((), None, [sum_a, line_u, sum_s], [line_u, sum_s])
+        step((), None, [line_u, sum_s], [sum_a, sum_s])
         line_a = Job(net.scatter_line(*sum_a.value))
-        step((), None, [line_a, sum_s], [sum_s])
-        step((), None, [sum_s], [line_a, sum_s])
-        step((), None, [line_a, sum_s], [line_a, sum_s])
+        step((), None, [line_a, sum_d, sum_s], [line_a, sum_d, sum_s])
+        step((), None, [line_a, sum_d, sum_s], [line_a, sum_d, line_u, sum_s])
 
         down_grad, up_grad, a_grad, packed = sum_d.value, line_u.value, line_a.value, sum_s.value
         down_grad = down_grad.T

time: 234 us -> 228 us (0.974)
  waiting for transfers between devices: 102 us -> 87.2 us
  starting transfers between devices: 51.3 us -> 63.5 us
    ppermute x61 -> x62, waiting for transfers between devices: 102 us -> 87.2 us  [step(): lax.ppermute(v, ALL, perm)]
    ppermute x61 -> x62, starting transfers between devices: 51.3 us -> 63.5 us  [step(): lax.ppermute(v, ALL, perm)]
  transfers between devices with their start and end apart: 61 -> 62, of which waited for: 35 -> 33; matrix products, arithmetic and copies ran while one was open for 2% -> 1% of each run, Pallas kernels for 22% -> 23%
where the time goes in v6:
time: 228 us
  waiting for transfers between devices  87.2 us (38%)
  Pallas kernels  65.7 us (29%)
  starting transfers between devices  63.5 us (28%)
  local copies, waits for them, and re-layouts  5.28 us (2%)
  other arithmetic  4.41 us (2%)
    ppermute x62, waiting for transfers between devices, step(): lax.ppermute(v, ALL, perm)  87.2 us
    ppermute x62, starting transfers between devices, step(): lax.ppermute(v, ALL, perm)  63.5 us
    pallas_call x10, Pallas kernels, step(): outs = run(*ins) if run else ins  63.1 us
  transfers between devices with their start and end apart: 62, of which 33 were waited for; matrix products, arithmetic and copies ran while one was open for 1% of the time, Pallas kernels for 23%

profile of v6, /device:TPU:0, one launch (start us, length us, event | category | flops | bytes accessed | tf_op | source)
XLA Modules:
  0.0 228.0 jit_solution(3275294481021983696)
XLA Ops:
  2.7 4.1 %collective-permute-start = (bf16[1,96,768]{2,1,0:T(8,128)(2,1)S(1)}, bf16[1,96,768]{2,1,0:T(8,128)(2,1)S(1)}, u32[]{:S(2)}, u32[]{:S(2)}) collective-permute-start(bf16[1,96,768]{2,1,0:T(8,128)(2,1)S(1)} %bitcast.28), channel_id=1, source_target_pairs={{0,16},{1,17},{2,18},{3,19},{4,20},{5,21},{6,22},{7,23},{8,24},{9,... | collective-permute-start | bytes 442376 | tf_op jit(solution)/shard_map/ppermute | solution.py:78
  8.3 5.5 %collective-permute-done = bf16[1,96,768]{2,1,0:T(8,128)(2,1)S(1)} collective-permute-done((bf16[1,96,768]{2,1,0:T(8,128)(2,1)S(1)}, bf16[1,96,768]{2,1,0:T(8,128)(2,1)S(1)}, u32[]{:S(2)}, u32[]{:S(2)}) %collective-permute-start) | collective-permute-done | bytes 147488 | tf_op jit(solution)/shard_map/ppermute | solution.py:78
  14.6 1.5 collective-permute-start.2
  18.2 3.8 %collective-permute-done.1 = bf16[2,96,768]{2,1,0:T(8,128)(2,1)S(1)} collective-permute-done((bf16[2,96,768]{2,1,0:T(8,128)(2,1)S(1)}, bf16[2,96,768]{2,1,0:T(8,128)(2,1)S(1)}, u32[]{:S(2)}, u32[]{:S(2)}) %collective-permute-start.1) | collective-permute-done | bytes 294944 | tf_op jit(solution)/shard_map/ppermute | solution.py:78
  22.2 1.3 collective-permute-start.3
  23.5 1.5 collective-permute-start.4
  25.0 3.3 %collective-permute-start.6 = (bf16[1,96,768]{2,1,0:T(8,128)(2,1)S(1)}, bf16[1,96,768]{2,1,0:T(8,128)(2,1)S(1)}, u32[]{:S(2)}, u32[]{:S(2)}) collective-permute-start(bf16[1,96,768]{2,1,0:T(8,128)(2,1)S(1)} %convert_bitcast_fusion.1), channel_id=1, source_target_pairs={{0,16},{1,17},{2,18},{3,19},{4,20},{5,21},{6,22},{7,23},{8,24},{9,... | collective-permute-start | bytes 442376 | tf_op jit(solution)/shard_map/ppermute | solution.py:78
  29.5 6.5 %collective-permute-done.6 = bf16[1,96,768]{2,1,0:T(8,128)(2,1)S(1)} collective-permute-done((bf16[1,96,768]{2,1,0:T(8,128)(2,1)S(1)}, bf16[1,96,768]{2,1,0:T(8,128)(2,1)S(1)}, u32[]{:S(2)}, u32[]{:S(2)}) %collective-permute-start.6) | collective-permute-done | bytes 147488 | tf_op jit(solution)/shard_map/ppermute | solution.py:78
  37.0 2.5 %collective-permute-start.11 = (bf16[2,96,768]{2,1,0:T(8,128)(2,1)S(1)}, bf16[2,96,768]{2,1,0:T(8,128)(2,1)S(1)}, u32[]{:S(2)}, u32[]{:S(2)}) collective-permute-start(bf16[2,96,768]{2,1,0:T(8,128)(2,1)S(1)} %pad_maximum_fusion.4), channel_id=1, source_target_pairs={{0,8},{1,9},{2,10},{3,11},{4,12},{5,13},{6,14},{7,15},{8,0},{9,1},... | collective-permute-start | bytes 884744 | tf_op jit(solution)/shard_map/ppermute | solution.py:78
  40.1 1.5 collective-permute-start.9
  41.6 3.4 %collective-permute-start.12 = (bf16[1,96,768]{2,1,0:T(8,128)(2,1)S(1)}, bf16[1,96,768]{2,1,0:T(8,128)(2,1)S(1)}, u32[]{:S(2)}, u32[]{:S(2)}) collective-permute-start(bf16[1,96,768]{2,1,0:T(8,128)(2,1)S(1)} %convert_bitcast_fusion), channel_id=1, source_target_pairs={{0,16},{1,17},{2,18},{3,19},{4,20},{5,21},{6,22},{7,23},{8,24},{9,... | collective-permute-start | bytes 442376 | tf_op jit(solution)/shard_map/ppermute | solution.py:78
  45.0 4.6 %collective-permute-done.12 = bf16[1,96,768]{2,1,0:T(8,128)(2,1)S(1)} collective-permute-done((bf16[1,96,768]{2,1,0:T(8,128)(2,1)S(1)}, bf16[1,96,768]{2,1,0:T(8,128)(2,1)S(1)}, u32[]{:S(2)}, u32[]{:S(2)}) %collective-permute-start.12) | collective-permute-done | bytes 147488 | tf_op jit(solution)/shard_map/ppermute | solution.py:78
  52.4 1.5 collective-permute-start.17
  54.1 11.3 %attn_forward.1 = (bf16[4,512,640]{2,1,0:T(8,128)(2,1)S(1)}, f32[4,8,512]{2,1,0:T(8,128)S(1)}, bf16[768,512]{1,0:T(8,128)(2,1)S(1)}, bf16[4,512,256]{2,1,0:T(8,1...) custom-call(f32[4]{0:T(128)S(1)} %copy-done.4, ...), custom_call_target="tpu_custom_call" | custom-call | flops 9663676416 | bytes 14155776 | tf_op jit(solution)/shard_map/attn_forward/pallas_call | solution.py:79
  65.5 2.0 collective-permute-done.16.rest_0_
  67.9 1.6 collective-permute-start.19
  69.5 1.5 collective-permute-start.20
  71.0 3.7 %collective-permute-start.22 = (bf16[2,96,768]{2,1,0:T(8,128)(2,1)S(1)}, bf16[2,96,768]{2,1,0:T(8,128)(2,1)S(1)}, u32[]{:S(2)}, u32[]{:S(2)}) collective-permute-start(bf16[2,96,768]{2,1,0:T(8,128)(2,1)S(1)} %pad_maximum_fusion.5), channel_id=1, source_target_pairs={{0,8},{1,9},{2,10},{3,11},{4,12},{5,13},{6,14},{7,15},{8,0},{9,1},... | collective-permute-start | bytes 884744 | tf_op jit(solution)/shard_map/ppermute | solution.py:78
  74.7 3.2 %attn_finish.1 = (f32[512,768]{1,0:T(8,128)S(1)}, f32[512,1]{1,0:T(8,128)S(1)}, f32[512,768]{1,0:T(8,128)S(1)}, f32[512,768]{1,0:T(8,128)S(1)}, bf16[512,768]{1,...) custom-call(f32[4]{0:T(128)S(1)} %copy-done.4, ...), custom_call_target="tpu_custom_call" | custom-call | flops 4831838208 | bytes 9437184 | tf_op jit(solution)/shard_map/attn_finish/pallas_call | solution.py:79
  78.6 3.2 %collective-permute-done.22 = bf16[2,96,768]{2,1,0:T(8,128)(2,1)S(1)} collective-permute-done((bf16[2,96,768]{2,1,0:T(8,128)(2,1)S(1)}, bf16[2,96,768]{2,1,0:T(8,128)(2,1)S(1)}, u32[]{:S(2)}, u32[]{:S(2)}) %collective-permute-start.22) | collective-permute-done | bytes 294944 | tf_op jit(solution)/shard_map/ppermute | solution.py:78
  83.5 3.9 %up_forward_0.1 = (bf16[2,512,768]{2,1,0:T(8,128)(2,1)S(1)}, f32[2,512,768]{2,1,0:T(8,128)S(1)}, f32[8,128]{1,0:T(8,128)S(1)}, bf16[2,768,768]{2,1,0:T(8,128)(2,1)S(1)}) custom-call(f32[4]{0:T(128)S(1)} %copy-done.4, bf16[512,768]{1,0:T(8,128)(2,1)S(1)} %get-tuple-element.428.mid_low, f32[4,1,1408]{2,1,0:T(1,128)S(1)} %bitcast.32, ...), custom_call_target="tpu_custom_call" | custom-call | flops 4831838208 | bytes 9437184 | tf_op jit(solution)/shard_map/up_forward_0/pallas_call | solution.py:79
  87.5 4.0 %up_forward_2.1 = (bf16[2,512,768]{2,1,0:T(8,128)(2,1)S(1)}, f32[2,512,768]{2,1,0:T(8,128)S(1)}, f32[8,128]{1,0:T(8,128)S(1)}, bf16[2,768,768]{2,1,0:T(8,128)(2,1)S(1)}) custom-call(f32[4]{0:T(128)S(1)} %copy-done.4, bf16[512,768]{1,0:T(8,128)(2,1)S(1)} %get-tuple-element.428.mid_low, f32[4,1,1408]{2,1,0:T(1,128)S(1)} %bitcast.33, ...), custom_call_target="tpu_custom_call" | custom-call | flops 4831838208 | bytes 9437184 | tf_op jit(solution)/shard_map/up_forward_2/pallas_call | solution.py:79
  91.5 6.6 %collective-permute-done.26.rest_2_ = bf16[4,96,768]{2,1,0:T(8,128)(2,1)S(1)} collective-permute-done((bf16[4,96,768]{2,1,0:T(8,128)(2,1)S(1)}, bf16[4,96,768]{2,1,0:T(8,128)(2,1)S(1)}, u32[]{:S(2)}, u32[]{:S(2)}) %collective-permute-start.26) | collective-permute-done | bytes 589856 | tf_op jit(solution)/shard_map/ppermute | solution.py:78
  99.0 1.5 collective-permute-start.28
  101.0 7.0 %collective-permute-done.28.rest_3_ = bf16[2,96,768]{2,1,0:T(8,128)(2,1)S(1)} collective-permute-done((bf16[2,96,768]{2,1,0:T(8,128)(2,1)S(1)}, bf16[2,96,768]{2,1,0:T(8,128)(2,1)S(1)}, u32[]{:S(2)}, u32[]{:S(2)}) %collective-permute-start.28) | collective-permute-done | bytes 294944 | tf_op jit(solution)/shard_map/ppermute | solution.py:78
  109.8 1.8 collective-permute-done.33.rest_8_
  112.1 8.8 %down_both.1 = (bf16[512,768]{1,0:T(8,128)(2,1)}, f32[512,768]{1,0:T(8,128)S(1)}, bf16[768,512]{1,0:T(8,128)(2,1)S(1)}, f32[8,768]{1,0:T(8,128)S(1)}, bf16[4,512...) custom-call(bf16[2,512,768]{2,1,0:T(8,128)(2,1)S(1)} %get-tuple-element.498.act0.rest_0_, ...), custom_call_target="tpu_custom_call" | custom-call | flops 4831838208 | bytes 18874368 | tf_op jit(solution)/shard_map/down_both/pallas_call | solution.py:79
  120.9 2.7 %up_grad.1 = (bf16[2,8,96,768]{3,2,1,0:T(8,128)(2,1)S(1)}, bf16[2,8,96,768]{3,2,1,0:T(8,128)(2,1)S(1)}) custom-call(bf16[768,512]{1,0:T(8,128)(2,1)S(1)} %get-tuple-element.494.left_t, bf16[4,512,768]{2,1,0:T(8,128)(2,1)S(1)} %get-tuple-element.508.rest_0_.grad_up), custom_call_target="tpu_custom_call" | custom-call | flops 2415919104 | bytes 4718592 | tf_op jit(solution)/shard_map/up_grad/pallas_call | solution.py:79
  123.8 2.7 %down_grad.1 = (bf16[2,8,96,768]{3,2,1,0:T(8,128)(2,1)S(1)}, bf16[2,8,96,768]{3,2,1,0:T(8,128)(2,1)S(1)}) custom-call(bf16[768,512]{1,0:T(8,128)(2,1)S(1)} %get-tuple-element.497.left_t, bf16[2,512,768]{2,1,0:T(8,128)(2,1)S(1)} %get-tuple-element.498.act0.rest_0_, bf16[2,512,768]{2,1,0:T(8,128)(2,1)S(1)} %get-tuple-element.499.act1.rest_1_), custom_call_target="tpu_custom_call" | custom-call | flops 2415919104 | bytes 4718592 | tf_op jit(solution)/shard_map/down_grad/pallas_call | solution.py:79
  126.5 1.7 collective-permute-done.35.got
  129.6 6.2 %mid_backward.1 = (f32[512,768]{1,0:T(8,128)S(1)}, bf16[768,512]{1,0:T(8,128)(2,1)S(1)}, bf16[4,512,256]{2,1,0:T(8,128)(2,1)S(1)}, f32[8,768]{1,0:T(8,128)S(1)}) custom-call(bf16[4,512,768]{2,1,0:T(8,128)(2,1)S(1)} %get-tuple-element.508.rest_0_.grad_up, f32[512,768]{1,0:T(8,128)S(1)} %get-tuple-element.509.grad_second, ...), custom_call_target="tpu_custom_call" | custom-call | flops 3221225472 | bytes 14155776 | tf_op jit(solution)/shard_map/mid_backward/pallas_call | solution.py:79
  135.8 2.0 collective-permute-done.37.from_x
  138.8 1.5 collective-permute-start.39
  140.8 1.7 collective-permute-start.41
  142.6 15.1 %attn_backward.1 = (bf16[4,512,640]{2,1,0:T(8,128)(2,1)S(1)}, bf16[2,8,96,768]{3,2,1,0:T(8,128)(2,1)S(1)}, bf16[2,8,96,768]{3,2,1,0:T(8,128)(2,1)S(1)}, f32[16,768]{1,0:T(8,128)S(1)}) custom-call(s32[1]{0:T(128)S(6)} %copy.34.longs, s32[12]{0:T(128)S(1)} %copy-done.11, bf16[4,512,640]{2,1,0:T(8,128)(2,1)S(1)} %copy-done.15, ...), custom_call_target="tpu_custom_call" | custom-call | flops 9663676416 | bytes 9437184 | tf_op jit(solution)/shard_map/attn_backward/pallas_call | solution.py:79
  158.2 1.4 collective-permute-start.43
  162.0 10.5 %collective-permute-done.43 = f32[16,768]{1,0:T(8,128)S(1)} collective-permute-done((f32[16,768]{1,0:T(8,128)S(1)}, f32[16,768]{1,0:T(8,128)S(1)}, u32[]{:S(2)}, u32[]{:S(2)}) %collective-permute-start.43) | collective-permute-done | bytes 49184 | tf_op jit(solution)/shard_map/ppermute | solution.py:78
  174.8 5.1 %token_backward.1 = bf16[512,768]{1,0:T(8,128)(2,1)} custom-call(f32[4]{0:T(128)S(1)} %copy-done.4, bf16[4,512,640]{2,1,0:T(8,128)(2,1)S(1)} %get-tuple-element.579.grad_qkv, f32[512,768]{1,0:T(8,128)S(1)} %get-tuple-element.580.grad_first, bf16[512,768]{1,0:T(8,128)(2,1)S(1)} %copy-done, bf16[4,768,768]{2,1,0:T(8,128)(2,1)S(1)} %get-tuple-element.582.weight.out_weight), custom_call_target="tpu_custom_call" | custom-call | flops 2415919104 | bytes 9437184 | tf_op jit(solution)/shard_map/token_backward/pallas_call | solution.py:79
  183.4 1.5 collective-permute-start.50
  184.9 3.3 %collective-permute-start.51 = (bf16[2,96,768]{2,1,0:T(8,128)(2,1)S(1)}, bf16[2,96,768]{2,1,0:T(8,128)(2,1)S(1)}, u32[]{:S(2)}, u32[]{:S(2)}) collective-permute-start(bf16[2,96,768]{2,1,0:T(8,128)(2,1)S(1)} %get-tuple-element.600), channel_id=1, source_target_pairs={{0,8},{1,9},{2,10},{3,11},{4,12},{5,13},{6,14},{7,15},{8,0},{9,1},... | collective-permute-start | bytes 884744 | tf_op jit(solution)/shard_map/ppermute | solution.py:78
  188.2 5.8 %collective-permute-done.52 = f32[16,768]{1,0:T(8,128)S(1)} collective-permute-done((f32[16,768]{1,0:T(8,128)S(1)}, f32[16,768]{1,0:T(8,128)S(1)}, u32[]{:S(2)}, u32[]{:S(2)}) %collective-permute-start.52) | collective-permute-done | bytes 49184 | tf_op jit(solution)/shard_map/ppermute | solution.py:78
  197.1 3.1 %collective-permute-start.54 = (bf16[2,96,768]{2,1,0:T(8,128)(2,1)S(1)}, bf16[2,96,768]{2,1,0:T(8,128)(2,1)S(1)}, u32[]{:S(2)}, u32[]{:S(2)}) collective-permute-start(bf16[2,96,768]{2,1,0:T(8,128)(2,1)S(1)} %get-tuple-element.616), channel_id=1, source_target_pairs={{0,8},{1,9},{2,10},{3,11},{4,12},{5,13},{6,14},{7,15},{8,0},{9,1},... | collective-permute-start | bytes 884744 | tf_op jit(solution)/shard_map/ppermute | solution.py:78
  202.3 1.5 collective-permute-start.57
  203.9 3.6 %collective-permute-done.57 = f32[16,768]{1,0:T(8,128)S(1)} collective-permute-done((f32[16,768]{1,0:T(8,128)S(1)}, f32[16,768]{1,0:T(8,128)S(1)}, u32[]{:S(2)}, u32[]{:S(2)}) %collective-permute-start.57) | collective-permute-done | bytes 49184 | tf_op jit(solution)/shard_map/ppermute | solution.py:78
  208.6 2.7 %collective-permute-start.59 = (bf16[96,768]{1,0:T(8,128)(2,1)S(1)}, bf16[96,768]{1,0:T(8,128)(2,1)S(1)}, u32[]{:S(2)}, u32[]{:S(2)}) collective-permute-start(bf16[96,768]{1,0:T(8,128)(2,1)S(1)} %get-tuple-element.628), channel_id=1, source_target_pairs={{0,16},{1,17},{2,18},{3,19},{4,20},{5,21},{6,22},{7,23},{8,24},{9,... | collective-permute-start | bytes 442376 | tf_op jit(solution)/shard_map/ppermute | solution.py:78
  212.3 6.5 %collective-permute-done.60 = bf16[96,768]{1,0:T(8,128)(2,1)S(1)} collective-permute-done((bf16[96,768]{1,0:T(8,128)(2,1)S(1)}, bf16[96,768]{1,0:T(8,128)(2,1)S(1)}, u32[]{:S(2)}, u32[]{:S(2)}) %collective-permute-start.60) | collective-permute-done | bytes 147488 | tf_op jit(solution)/shard_map/ppermute | solution.py:78
  218.8 3.1 %collective-permute-done.58 = bf16[96,768]{1,0:T(8,128)(2,1)S(1)} collective-permute-done((bf16[96,768]{1,0:T(8,128)(2,1)S(1)}, bf16[96,768]{1,0:T(8,128)(2,1)S(1)}, u32[]{:S(2)}, u32[]{:S(2)}) %collective-permute-start.58) | collective-permute-done | bytes 147488 | tf_op jit(solution)/shard_map/ppermute | solution.py:78
  221.9 1.6 collective-permute-done.59
  (176 shorter events, 41.3 us)
Async XLA Ops:
  2.7 11.1 %collective-permute-start = (bf16[1,96,768]{2,1,0:T(8,128)(2,1)S(1)}, bf16[1,96,768]{2,1,0:T(8,128)(2,1)S(1)}, u32[]{:S(2)}, u32[]{:S(2)}) collective-permute-start(bf16[1,96,768]{2,1,0:T(8,128)(2,1)S(1)} %bitcast.28), channel_id=1, source_target_pairs={{0,16},{1,17},{2,18},{3,19},{4,20},{5,21},{6,22},{7,23},{8,24},{9,... | collective-permute-start | bytes 442376 | tf_op jit(solution)/shard_map/ppermute | solution.py:78
  13.8 8.2 %collective-permute-start.1 = (bf16[2,96,768]{2,1,0:T(8,128)(2,1)S(1)}, bf16[2,96,768]{2,1,0:T(8,128)(2,1)S(1)}, u32[]{:S(2)}, u32[]{:S(2)}) collective-permute-start(bf16[2,96,768]{2,1,0:T(8,128)(2,1)S(1)} %pad_maximum_fusion.3), channel_id=1, source_target_pairs={{0,8},{1,9},{2,10},{3,11},{4,12},{5,13},{6,14},{7,15},{8,0},{9,1},... | collective-permute-start | bytes 884744 | tf_op jit(solution)/shard_map/ppermute | solution.py:78
  22.2 13.9 %collective-permute-start.3 = (bf16[4,96,768]{2,1,0:T(8,128)(2,1)S(1)}, bf16[4,96,768]{2,1,0:T(8,128)(2,1)S(1)}, u32[]{:S(2)}, u32[]{:S(2)}) collective-permute-start(bf16[4,96,768]{2,1,0:T(8,128)(2,1)S(1)} %pad_maximum_fusion.rest_0_), channel_id=1, source_target_pairs={{0,2},{1,3},{2,0},{3,1},{4,6},{5,7},{6,4},{7,5},{8,10},{9,11},{10,... | collective-permute-start | bytes 1769480 | tf_op jit(solution)/shard_map/ppermute | solution.py:78
  23.5 13.3 %collective-permute-start.4 = (bf16[4,96,768]{2,1,0:T(8,128)(2,1)S(1)}, bf16[4,96,768]{2,1,0:T(8,128)(2,1)S(1)}, u32[]{:S(2)}, u32[]{:S(2)}) collective-permute-start(bf16[4,96,768]{2,1,0:T(8,128)(2,1)S(1)} %pad_maximum_fusion.rest_0_), channel_id=1, source_target_pairs={{0,4},{1,5},{2,6},{3,7},{4,0},{5,1},{6,2},{7,3},{8,12},{9,13},{10,... | collective-permute-start | bytes 1769480 | tf_op jit(solution)/shard_map/ppermute | solution.py:78
  25.0 11.8 %collective-permute-start.5 = (bf16[4,96,768]{2,1,0:T(8,128)(2,1)S(1)}, bf16[4,96,768]{2,1,0:T(8,128)(2,1)S(1)}, u32[]{:S(2)}, u32[]{:S(2)}) collective-permute-start(bf16[4,96,768]{2,1,0:T(8,128)(2,1)S(1)} %pad_maximum_fusion.rest_0_), channel_id=1, source_target_pairs={{0,1},{1,0},{2,3},{3,2},{4,5},{5,4},{6,7},{7,6},{8,9},{9,8},{10,11... | collective-permute-start | bytes 1769480 | tf_op jit(solution)/shard_map/ppermute | solution.py:78
  25.0 11.0 %collective-permute-start.6 = (bf16[1,96,768]{2,1,0:T(8,128)(2,1)S(1)}, bf16[1,96,768]{2,1,0:T(8,128)(2,1)S(1)}, u32[]{:S(2)}, u32[]{:S(2)}) collective-permute-start(bf16[1,96,768]{2,1,0:T(8,128)(2,1)S(1)} %convert_bitcast_fusion.1), channel_id=1, source_target_pairs={{0,16},{1,17},{2,18},{3,19},{4,20},{5,21},{6,22},{7,23},{8,24},{9,... | collective-permute-start | bytes 442376 | tf_op jit(solution)/shard_map/ppermute | solution.py:78
  36.9 13.4 %collective-permute-start.10 = (bf16[4,96,768]{2,1,0:T(8,128)(2,1)S(1)}, bf16[4,96,768]{2,1,0:T(8,128)(2,1)S(1)}, u32[]{:S(2)}, u32[]{:S(2)}) collective-permute-start(bf16[4,96,768]{2,1,0:T(8,128)(2,1)S(1)} %collective-permute-done.4.rest_1_), channel_id=1, source_target_pairs={{0,1},{1,0},{2,3},{3,2},{4,5},{5,4},{6,7},{7,6},{8,9},{9,8},{10,11... | collective-permute-start | bytes 1769480 | tf_op jit(solution)/shard_map/ppermute | solution.py:78
  37.0 13.3 %collective-permute-start.11 = (bf16[2,96,768]{2,1,0:T(8,128)(2,1)S(1)}, bf16[2,96,768]{2,1,0:T(8,128)(2,1)S(1)}, u32[]{:S(2)}, u32[]{:S(2)}) collective-permute-start(bf16[2,96,768]{2,1,0:T(8,128)(2,1)S(1)} %pad_maximum_fusion.4), channel_id=1, source_target_pairs={{0,8},{1,9},{2,10},{3,11},{4,12},{5,13},{6,14},{7,15},{8,0},{9,1},... | collective-permute-start | bytes 884744 | tf_op jit(solution)/shard_map/ppermute | solution.py:78
  39.5 10.8 %collective-permute-start.8 = (bf16[2,96,768]{2,1,0:T(8,128)(2,1)S(1)}, bf16[2,96,768]{2,1,0:T(8,128)(2,1)S(1)}, u32[]{:S(2)}, u32[]{:S(2)}) collective-permute-start(bf16[2,96,768]{2,1,0:T(8,128)(2,1)S(1)} %slice.72), channel_id=1, source_target_pairs={{0,2},{1,3},{2,0},{3,1},{4,6},{5,7},{6,4},{7,5},{8,10},{9,11},{10,... | collective-permute-start | bytes 884744 | tf_op jit(solution)/shard_map/ppermute | solution.py:78
  40.1 10.2 %collective-permute-start.9 = (bf16[2,96,768]{2,1,0:T(8,128)(2,1)S(1)}, bf16[2,96,768]{2,1,0:T(8,128)(2,1)S(1)}, u32[]{:S(2)}, u32[]{:S(2)}) collective-permute-start(bf16[2,96,768]{2,1,0:T(8,128)(2,1)S(1)} %slice.73), channel_id=1, source_target_pairs={{0,4},{1,5},{2,6},{3,7},{4,0},{5,1},{6,2},{7,3},{8,12},{9,13},{10,... | collective-permute-start | bytes 884744 | tf_op jit(solution)/shard_map/ppermute | solution.py:78
  41.6 8.0 %collective-permute-start.12 = (bf16[1,96,768]{2,1,0:T(8,128)(2,1)S(1)}, bf16[1,96,768]{2,1,0:T(8,128)(2,1)S(1)}, u32[]{:S(2)}, u32[]{:S(2)}) collective-permute-start(bf16[1,96,768]{2,1,0:T(8,128)(2,1)S(1)} %convert_bitcast_fusion), channel_id=1, source_target_pairs={{0,16},{1,17},{2,18},{3,19},{4,20},{5,21},{6,22},{7,23},{8,24},{9,... | collective-permute-start | bytes 442376 | tf_op jit(solution)/shard_map/ppermute | solution.py:78
  51.8 15.7 %collective-permute-start.16 = (bf16[4,96,768]{2,1,0:T(8,128)(2,1)S(1)}, bf16[4,96,768]{2,1,0:T(8,128)(2,1)S(1)}, u32[]{:S(2)}, u32[]{:S(2)}) collective-permute-start(bf16[4,96,768]{2,1,0:T(8,128)(2,1)S(1)} %pad_maximum_fusion.1.rest_0_), channel_id=1, source_target_pairs={{0,2},{1,3},{2,0},{3,1},{4,6},{5,7},{6,4},{7,5},{8,10},{9,11},{10,... | collective-permute-start | bytes 1769480 | tf_op jit(solution)/shard_map/ppermute | solution.py:78
  52.4 15.4 %collective-permute-start.17 = (bf16[4,96,768]{2,1,0:T(8,128)(2,1)S(1)}, bf16[4,96,768]{2,1,0:T(8,128)(2,1)S(1)}, u32[]{:S(2)}, u32[]{:S(2)}) collective-permute-start(bf16[4,96,768]{2,1,0:T(8,128)(2,1)S(1)} %pad_maximum_fusion.1.rest_0_), channel_id=1, source_target_pairs={{0,4},{1,5},{2,6},{3,7},{4,0},{5,1},{6,2},{7,3},{8,12},{9,13},{10,... | collective-permute-start | bytes 1769480 | tf_op jit(solution)/shard_map/ppermute | solution.py:78
  54.0 13.8 %collective-permute-start.18 = (bf16[4,96,768]{2,1,0:T(8,128)(2,1)S(1)}, bf16[4,96,768]{2,1,0:T(8,128)(2,1)S(1)}, u32[]{:S(2)}, u32[]{:S(2)}) collective-permute-start(bf16[4,96,768]{2,1,0:T(8,128)(2,1)S(1)} %pad_maximum_fusion.1.rest_0_), channel_id=1, source_target_pairs={{0,1},{1,0},{2,3},{3,2},{4,5},{5,4},{6,7},{7,6},{8,9},{9,8},{10,11... | collective-permute-start | bytes 1769480 | tf_op jit(solution)/shard_map/ppermute | solution.py:78
  67.9 13.9 %collective-permute-start.21 = (bf16[4,96,768]{2,1,0:T(8,128)(2,1)S(1)}, bf16[4,96,768]{2,1,0:T(8,128)(2,1)S(1)}, u32[]{:S(2)}, u32[]{:S(2)}) collective-permute-start(bf16[4,96,768]{2,1,0:T(8,128)(2,1)S(1)} %collective-permute-done.17.rest_1_), channel_id=1, source_target_pairs={{0,1},{1,0},{2,3},{3,2},{4,5},{5,4},{6,7},{7,6},{8,9},{9,8},{10,11... | collective-permute-start | bytes 1769480 | tf_op jit(solution)/shard_map/ppermute | solution.py:78
  67.9 10.0 %collective-permute-start.19 = (bf16[2,96,768]{2,1,0:T(8,128)(2,1)S(1)}, bf16[2,96,768]{2,1,0:T(8,128)(2,1)S(1)}, u32[]{:S(2)}, u32[]{:S(2)}) collective-permute-start(bf16[2,96,768]{2,1,0:T(8,128)(2,1)S(1)} %slice.74), channel_id=1, source_target_pairs={{0,2},{1,3},{2,0},{3,1},{4,6},{5,7},{6,4},{7,5},{8,10},{9,11},{10,... | collective-permute-start | bytes 884744 | tf_op jit(solution)/shard_map/ppermute | solution.py:78
  69.5 9.1 %collective-permute-start.20 = (bf16[2,96,768]{2,1,0:T(8,128)(2,1)S(1)}, bf16[2,96,768]{2,1,0:T(8,128)(2,1)S(1)}, u32[]{:S(2)}, u32[]{:S(2)}) collective-permute-start(bf16[2,96,768]{2,1,0:T(8,128)(2,1)S(1)} %slice.75), channel_id=1, source_target_pairs={{0,4},{1,5},{2,6},{3,7},{4,0},{5,1},{6,2},{7,3},{8,12},{9,13},{10,... | collective-permute-start | bytes 884744 | tf_op jit(solution)/shard_map/ppermute | solution.py:78
  71.0 10.7 %collective-permute-start.22 = (bf16[2,96,768]{2,1,0:T(8,128)(2,1)S(1)}, bf16[2,96,768]{2,1,0:T(8,128)(2,1)S(1)}, u32[]{:S(2)}, u32[]{:S(2)}) collective-permute-start(bf16[2,96,768]{2,1,0:T(8,128)(2,1)S(1)} %pad_maximum_fusion.5), channel_id=1, source_target_pairs={{0,8},{1,9},{2,10},{3,11},{4,12},{5,13},{6,14},{7,15},{8,0},{9,1},... | collective-permute-start | bytes 884744 | tf_op jit(solution)/shard_map/ppermute | solution.py:78
  82.4 15.7 %collective-permute-start.26 = (bf16[4,96,768]{2,1,0:T(8,128)(2,1)S(1)}, bf16[4,96,768]{2,1,0:T(8,128)(2,1)S(1)}, u32[]{:S(2)}, u32[]{:S(2)}) collective-permute-start(bf16[4,96,768]{2,1,0:T(8,128)(2,1)S(1)} %pad_maximum_fusion.2.rest_0_), channel_id=1, source_target_pairs={{0,2},{1,3},{2,0},{3,1},{4,6},{5,7},{6,4},{7,5},{8,10},{9,11},{10,... | collective-permute-start | bytes 1769480 | tf_op jit(solution)/shard_map/ppermute | solution.py:78
  83.0 15.4 %collective-permute-start.27 = (bf16[4,96,768]{2,1,0:T(8,128)(2,1)S(1)}, bf16[4,96,768]{2,1,0:T(8,128)(2,1)S(1)}, u32[]{:S(2)}, u32[]{:S(2)}) collective-permute-start(bf16[4,96,768]{2,1,0:T(8,128)(2,1)S(1)} %pad_maximum_fusion.2.rest_0_), channel_id=1, source_target_pairs={{0,4},{1,5},{2,6},{3,7},{4,0},{5,1},{6,2},{7,3},{8,12},{9,13},{10,... | collective-permute-start | bytes 1769480 | tf_op jit(solution)/shard_map/ppermute | solution.py:78
  98.4 10.8 %collective-permute-start.30 = (bf16[4,96,768]{2,1,0:T(8,128)(2,1)S(1)}, bf16[4,96,768]{2,1,0:T(8,128)(2,1)S(1)}, u32[]{:S(2)}, u32[]{:S(2)}) collective-permute-start(bf16[4,96,768]{2,1,0:T(8,128)(2,1)S(1)} %collective-permute-done.27.rest_1_), channel_id=1, source_target_pairs={{0,1},{1,0},{2,3},{3,2},{4,5},{5,4},{6,7},{7,6},{8,9},{9,8},{10,11... | collective-permute-start | bytes 1769480 | tf_op jit(solution)/shard_map/ppermute | solution.py:78
  98.5 10.7 %collective-permute-start.31 = (bf16[4,96,768]{2,1,0:T(8,128)(2,1)S(1)}, bf16[4,96,768]{2,1,0:T(8,128)(2,1)S(1)}, u32[]{:S(2)}, u32[]{:S(2)}) collective-permute-start(bf16[4,96,768]{2,1,0:T(8,128)(2,1)S(1)} %pad_maximum_fusion.2.rest_0_), channel_id=1, source_target_pairs={{0,1},{1,0},{2,3},{3,2},{4,5},{5,4},{6,7},{7,6},{8,9},{9,8},{10,11... | collective-permute-start | bytes 1769480 | tf_op jit(solution)/shard_map/ppermute | solution.py:78
  99.0 9.0 %collective-permute-start.28 = (bf16[2,96,768]{2,1,0:T(8,128)(2,1)S(1)}, bf16[2,96,768]{2,1,0:T(8,128)(2,1)S(1)}, u32[]{:S(2)}, u32[]{:S(2)}) collective-permute-start(bf16[2,96,768]{2,1,0:T(8,128)(2,1)S(1)} %slice.76), channel_id=1, source_target_pairs={{0,2},{1,3},{2,0},{3,1},{4,6},{5,7},{6,4},{7,5},{8,10},{9,11},{10,... | collective-permute-start | bytes 884744 | tf_op jit(solution)/shard_map/ppermute | solution.py:78
  100.5 8.7 %collective-permute-start.29 = (bf16[2,96,768]{2,1,0:T(8,128)(2,1)S(1)}, bf16[2,96,768]{2,1,0:T(8,128)(2,1)S(1)}, u32[]{:S(2)}, u32[]{:S(2)}) collective-permute-start(bf16[2,96,768]{2,1,0:T(8,128)(2,1)S(1)} %slice.77), channel_id=1, source_target_pairs={{0,4},{1,5},{2,6},{3,7},{4,0},{5,1},{6,2},{7,3},{8,12},{9,13},{10,... | collective-permute-start | bytes 884744 | tf_op jit(solution)/shard_map/ppermute | solution.py:78
  128.3 9.8 %collective-permute-start.36 = (bf16[2,8,96,768]{3,2,1,0:T(8,128)(2,1)S(1)}, bf16[2,8,96,768]{3,2,1,0:T(8,128)(2,1)S(1)}, u32[]{:S(2)}, u32[]{:S(2)}) collective-permute-start(bf16[2,8,96,768]{3,2,1,0:T(8,128)(2,1)S(1)} %get-tuple-element.522), channel_id=1, source_target_pairs={{0,1},{1,0},{2,3},{3,2},{4,5},{5,4},{6,7},{7,6},{8,9},{9,8},{10,11... | collective-permute-start | bytes 7077896 | tf_op jit(solution)/shard_map/ppermute | solution.py:78
  128.5 9.3 %collective-permute-start.37 = (bf16[2,96,768]{2,1,0:T(8,128)(2,1)S(1)}, bf16[2,96,768]{2,1,0:T(8,128)(2,1)S(1)}, u32[]{:S(2)}, u32[]{:S(2)}) collective-permute-start(bf16[2,96,768]{2,1,0:T(8,128)(2,1)S(1)} %get-tuple-element.523), channel_id=1, source_target_pairs={{0,2},{1,3},{2,0},{3,1},{4,6},{5,7},{6,4},{7,5},{8,10},{9,11},{10,... | collective-permute-start | bytes 884744 | tf_op jit(solution)/shard_map/ppermute | solution.py:78
  129.1 9.0 %collective-permute-start.38 = (bf16[2,96,768]{2,1,0:T(8,128)(2,1)S(1)}, bf16[2,96,768]{2,1,0:T(8,128)(2,1)S(1)}, u32[]{:S(2)}, u32[]{:S(2)}) collective-permute-start(bf16[2,96,768]{2,1,0:T(8,128)(2,1)S(1)} %get-tuple-element.524), channel_id=1, source_target_pairs={{0,4},{1,5},{2,6},{3,7},{4,0},{5,1},{6,2},{7,3},{8,12},{9,13},{10,... | collective-permute-start | bytes 884744 | tf_op jit(solution)/shard_map/ppermute | solution.py:78
  138.8 18.9 %collective-permute-start.39 = (bf16[4,96,768]{2,1,0:T(8,128)(2,1)S(1)}, bf16[4,96,768]{2,1,0:T(8,128)(2,1)S(1)}, u32[]{:S(2)}, u32[]{:S(2)}) collective-permute-start(bf16[4,96,768]{2,1,0:T(8,128)(2,1)S(1)} %get-tuple-element.561), channel_id=1, source_target_pairs={{0,2},{1,3},{2,0},{3,1},{4,6},{5,7},{6,4},{7,5},{8,10},{9,11},{10,... | collective-permute-start | bytes 1769480 | tf_op jit(solution)/shard_map/ppermute | solution.py:78
  140.3 17.4 %collective-permute-start.40 = (bf16[4,96,768]{2,1,0:T(8,128)(2,1)S(1)}, bf16[4,96,768]{2,1,0:T(8,128)(2,1)S(1)}, u32[]{:S(2)}, u32[]{:S(2)}) collective-permute-start(bf16[4,96,768]{2,1,0:T(8,128)(2,1)S(1)} %get-tuple-element.562), channel_id=1, source_target_pairs={{0,4},{1,5},{2,6},{3,7},{4,0},{5,1},{6,2},{7,3},{8,12},{9,13},{10,... | collective-permute-start | bytes 1769480 | tf_op jit(solution)/shard_map/ppermute | solution.py:78
  140.8 16.9 %collective-permute-start.41 = (bf16[4,96,768]{2,1,0:T(8,128)(2,1)S(1)}, bf16[4,96,768]{2,1,0:T(8,128)(2,1)S(1)}, u32[]{:S(2)}, u32[]{:S(2)}) collective-permute-start(bf16[4,96,768]{2,1,0:T(8,128)(2,1)S(1)} %get-tuple-element.563), channel_id=1, source_target_pairs={{0,8},{1,9},{2,10},{3,11},{4,12},{5,13},{6,14},{7,15},{8,0},{9,1},... | collective-permute-start | bytes 1769480 | tf_op jit(solution)/shard_map/ppermute | solution.py:78
  157.8 14.7 %collective-permute-start.42 = (bf16[2,8,96,768]{3,2,1,0:T(8,128)(2,1)S(1)}, bf16[2,8,96,768]{3,2,1,0:T(8,128)(2,1)S(1)}, u32[]{:S(2)}, u32[]{:S(2)}) collective-permute-start(bf16[2,8,96,768]{3,2,1,0:T(8,128)(2,1)S(1)} %get-tuple-element.573), channel_id=1, source_target_pairs={{0,1},{1,0},{2,3},{3,2},{4,5},{5,4},{6,7},{7,6},{8,9},{9,8},{10,11... | collective-permute-start | bytes 7077896 | tf_op jit(solution)/shard_map/ppermute | solution.py:78
  157.9 22.0 %collective-permute-start.48 = (bf16[4,96,768]{2,1,0:T(8,128)(2,1)S(1)}, bf16[4,96,768]{2,1,0:T(8,128)(2,1)S(1)}, u32[]{:S(2)}, u32[]{:S(2)}) collective-permute-start(bf16[4,96,768]{2,1,0:T(8,128)(2,1)S(1)} %get-tuple-element.587), channel_id=1, source_target_pairs={{0,8},{1,9},{2,10},{3,11},{4,12},{5,13},{6,14},{7,15},{8,0},{9,1},... | collective-permute-start | bytes 1769480 | tf_op jit(solution)/shard_map/ppermute | solution.py:78
  158.2 14.2 %collective-permute-start.43 = (f32[16,768]{1,0:T(8,128)S(1)}, f32[16,768]{1,0:T(8,128)S(1)}, u32[]{:S(2)}, u32[]{:S(2)}) collective-permute-start(f32[16,768]{1,0:T(8,128)S(1)} %get-tuple-element.574), channel_id=1, source_target_pairs={{0,16},{1,17},{2,18},{3,19},{4,20},{5,21},{6,22},{7,23},{8,24},{9,... | collective-permute-start | bytes 147464 | tf_op jit(solution)/shard_map/ppermute | solution.py:78
  159.7 20.2 %collective-permute-start.46 = (bf16[96,768]{1,0:T(8,128)(2,1)S(1)}, bf16[96,768]{1,0:T(8,128)(2,1)S(1)}, u32[]{:S(2)}, u32[]{:S(2)}) collective-permute-start(bf16[96,768]{1,0:T(8,128)(2,1)S(1)} %get-tuple-element.585), channel_id=1, source_target_pairs={{0,2},{1,3},{2,0},{3,1},{4,6},{5,7},{6,4},{7,5},{8,10},{9,11},{10,... | collective-permute-start | bytes 442376 | tf_op jit(solution)/shard_map/ppermute | solution.py:78
  160.8 19.2 %collective-permute-start.47 = (bf16[96,768]{1,0:T(8,128)(2,1)S(1)}, bf16[96,768]{1,0:T(8,128)(2,1)S(1)}, u32[]{:S(2)}, u32[]{:S(2)}) collective-permute-start(bf16[96,768]{1,0:T(8,128)(2,1)S(1)} %get-tuple-element.586), channel_id=1, source_target_pairs={{0,4},{1,5},{2,6},{3,7},{4,0},{5,1},{6,2},{7,3},{8,12},{9,13},{10,... | collective-permute-start | bytes 442376 | tf_op jit(solution)/shard_map/ppermute | solution.py:78
  172.6 8.6 %collective-permute-start.44 = (bf16[2,96,768]{2,1,0:T(8,128)(2,1)S(1)}, bf16[2,96,768]{2,1,0:T(8,128)(2,1)S(1)}, u32[]{:S(2)}, u32[]{:S(2)}) collective-permute-start(bf16[2,96,768]{2,1,0:T(8,128)(2,1)S(1)} %get-tuple-element.583), channel_id=1, source_target_pairs={{0,2},{1,3},{2,0},{3,1},{4,6},{5,7},{6,4},{7,5},{8,10},{9,11},{10,... | collective-permute-start | bytes 884744 | tf_op jit(solution)/shard_map/ppermute | solution.py:78
  173.6 8.2 %collective-permute-start.45 = (bf16[2,96,768]{2,1,0:T(8,128)(2,1)S(1)}, bf16[2,96,768]{2,1,0:T(8,128)(2,1)S(1)}, u32[]{:S(2)}, u32[]{:S(2)}) collective-permute-start(bf16[2,96,768]{2,1,0:T(8,128)(2,1)S(1)} %get-tuple-element.584), channel_id=1, source_target_pairs={{0,4},{1,5},{2,6},{3,7},{4,0},{5,1},{6,2},{7,3},{8,12},{9,13},{10,... | collective-permute-start | bytes 884744 | tf_op jit(solution)/shard_map/ppermute | solution.py:78
  182.2 13.7 %collective-permute-start.49 = (bf16[4,96,768]{2,1,0:T(8,128)(2,1)S(1)}, bf16[4,96,768]{2,1,0:T(8,128)(2,1)S(1)}, u32[]{:S(2)}, u32[]{:S(2)}) collective-permute-start(bf16[4,96,768]{2,1,0:T(8,128)(2,1)S(1)} %get-tuple-element.597), channel_id=1, source_target_pairs={{0,2},{1,3},{2,0},{3,1},{4,6},{5,7},{6,4},{7,5},{8,10},{9,11},{10,... | collective-permute-start | bytes 1769480 | tf_op jit(solution)/shard_map/ppermute | solution.py:78
  183.4 13.4 %collective-permute-start.50 = (bf16[4,96,768]{2,1,0:T(8,128)(2,1)S(1)}, bf16[4,96,768]{2,1,0:T(8,128)(2,1)S(1)}, u32[]{:S(2)}, u32[]{:S(2)}) collective-permute-start(bf16[4,96,768]{2,1,0:T(8,128)(2,1)S(1)} %get-tuple-element.598), channel_id=1, source_target_pairs={{0,4},{1,5},{2,6},{3,7},{4,0},{5,1},{6,2},{7,3},{8,12},{9,13},{10,... | collective-permute-start | bytes 1769480 | tf_op jit(solution)/shard_map/ppermute | solution.py:78
  184.9 9.1 %collective-permute-start.51 = (bf16[2,96,768]{2,1,0:T(8,128)(2,1)S(1)}, bf16[2,96,768]{2,1,0:T(8,128)(2,1)S(1)}, u32[]{:S(2)}, u32[]{:S(2)}) collective-permute-start(bf16[2,96,768]{2,1,0:T(8,128)(2,1)S(1)} %get-tuple-element.600), channel_id=1, source_target_pairs={{0,8},{1,9},{2,10},{3,11},{4,12},{5,13},{6,14},{7,15},{8,0},{9,1},... | collective-permute-start | bytes 884744 | tf_op jit(solution)/shard_map/ppermute | solution.py:78
  188.2 5.8 %collective-permute-start.52 = (f32[16,768]{1,0:T(8,128)S(1)}, f32[16,768]{1,0:T(8,128)S(1)}, u32[]{:S(2)}, u32[]{:S(2)}) collective-permute-start(f32[16,768]{1,0:T(8,128)S(1)} %add_select_fusion.4), channel_id=1, source_target_pairs={{0,8},{1,9},{2,10},{3,11},{4,12},{5,13},{6,14},{7,15},{8,0},{9,1},... | collective-permute-start | bytes 147464 | tf_op jit(solution)/shard_map/ppermute | solution.py:78
  197.1 10.4 %collective-permute-start.54 = (bf16[2,96,768]{2,1,0:T(8,128)(2,1)S(1)}, bf16[2,96,768]{2,1,0:T(8,128)(2,1)S(1)}, u32[]{:S(2)}, u32[]{:S(2)}) collective-permute-start(bf16[2,96,768]{2,1,0:T(8,128)(2,1)S(1)} %get-tuple-element.616), channel_id=1, source_target_pairs={{0,8},{1,9},{2,10},{3,11},{4,12},{5,13},{6,14},{7,15},{8,0},{9,1},... | collective-permute-start | bytes 884744 | tf_op jit(solution)/shard_map/ppermute | solution.py:78
  200.2 7.3 %collective-permute-start.55 = (bf16[2,96,768]{2,1,0:T(8,128)(2,1)S(1)}, bf16[2,96,768]{2,1,0:T(8,128)(2,1)S(1)}, u32[]{:S(2)}, u32[]{:S(2)}) collective-permute-start(bf16[2,96,768]{2,1,0:T(8,128)(2,1)S(1)} %get-tuple-element.617), channel_id=1, source_target_pairs={{0,2},{1,3},{2,0},{3,1},{4,6},{5,7},{6,4},{7,5},{8,10},{9,11},{10,... | collective-permute-start | bytes 884744 | tf_op jit(solution)/shard_map/ppermute | solution.py:78
  201.3 6.7 %collective-permute-start.56 = (bf16[2,96,768]{2,1,0:T(8,128)(2,1)S(1)}, bf16[2,96,768]{2,1,0:T(8,128)(2,1)S(1)}, u32[]{:S(2)}, u32[]{:S(2)}) collective-permute-start(bf16[2,96,768]{2,1,0:T(8,128)(2,1)S(1)} %get-tuple-element.618), channel_id=1, source_target_pairs={{0,4},{1,5},{2,6},{3,7},{4,0},{5,1},{6,2},{7,3},{8,12},{9,13},{10,... | collective-permute-start | bytes 884744 | tf_op jit(solution)/shard_map/ppermute | solution.py:78
  203.8 15.1 %collective-permute-start.60 = (bf16[96,768]{1,0:T(8,128)(2,1)S(1)}, bf16[96,768]{1,0:T(8,128)(2,1)S(1)}, u32[]{:S(2)}, u32[]{:S(2)}) collective-permute-start(bf16[96,768]{1,0:T(8,128)(2,1)S(1)} %get-tuple-element.629), channel_id=1, source_target_pairs={{0,16},{1,17},{2,18},{3,19},{4,20},{5,21},{6,22},{7,23},{8,24},{9,... | collective-permute-start | bytes 442376 | tf_op jit(solution)/shard_map/ppermute | solution.py:78
  208.3 13.6 %collective-permute-start.58 = (bf16[96,768]{1,0:T(8,128)(2,1)S(1)}, bf16[96,768]{1,0:T(8,128)(2,1)S(1)}, u32[]{:S(2)}, u32[]{:S(2)}) collective-permute-start(bf16[96,768]{1,0:T(8,128)(2,1)S(1)} %get-tuple-element.627), channel_id=1, source_target_pairs={{0,16},{1,17},{2,18},{3,19},{4,20},{5,21},{6,22},{7,23},{8,24},{9,... | collective-permute-start | bytes 442376 | tf_op jit(solution)/shard_map/ppermute | solution.py:78
  208.6 14.9 %collective-permute-start.59 = (bf16[96,768]{1,0:T(8,128)(2,1)S(1)}, bf16[96,768]{1,0:T(8,128)(2,1)S(1)}, u32[]{:S(2)}, u32[]{:S(2)}) collective-permute-start(bf16[96,768]{1,0:T(8,128)(2,1)S(1)} %get-tuple-element.628), channel_id=1, source_target_pairs={{0,16},{1,17},{2,18},{3,19},{4,20},{5,21},{6,22},{7,23},{8,24},{9,... | collective-permute-start | bytes 442376 | tf_op jit(solution)/shard_map/ppermute | solution.py:78
  211.3 7.5 %collective-permute-start.61 = (f32[16,768]{1,0:T(8,128)S(1)}, f32[16,768]{1,0:T(8,128)S(1)}, u32[]{:S(2)}, u32[]{:S(2)}) collective-permute-start(f32[16,768]{1,0:T(8,128)S(1)} %add_select_fusion.1), channel_id=1, source_target_pairs={{0,4},{1,5},{2,6},{3,7},{4,0},{5,1},{6,2},{7,3},{8,12},{9,13},{10,... | collective-permute-start | bytes 147464 | tf_op jit(solution)/shard_map/ppermute | solution.py:78
  (33 other events, 397.5 us)

commit v7 on v6

--- a/solution.py
+++ b/solution.py
@@ -91,33 +91,54 @@
     def part(self, lanes):
         plan = [p for p in self.plan if p[1] in lanes]
         names = sorted({p[0] for p in plan})
-        return [self.bufs[n] for n in names], [(names.index(b), lane, lanes[0], k, y) for b, lane, k, y in plan]
+        return [self.bufs[n] for n in names], [(names.index(b), lane - lanes[0], at, col) for b, lane, at, col in plan]
 
 
 class Grid:
     parts = 8
 
     @staticmethod
-    def gather(shard, pieces, line_later=False):
+    def gather(shard, pieces):
         own = shard[None]
         for base, lane in ((0, 0), (5, 1)):
-            pieces.plan.append((base, lane, 0, 0))
-            pieces.plan.append((base + 1, lane, 0, 1))
-            pieces.plan.append((base + 2, lane + 2, 0, 0))
-            pieces.plan.append((base + 3, lane + 2, 0, 1))
-            pieces.plan.append((base + 4, lane + 2, 2, 1))
+            pieces.plan.append((base, lane, (0, 4, 2, 6), 0))
+            pieces.plan.append((base + 1, lane, (1, 5, 3, 7), 0))
+            pieces.plan.append((base + 2, lane + 2, (0, 4, 2, 6), 0))
+            pieces.plan.append((base + 3, lane + 2, (1, 5), 0))
+            pieces.plan.append((base + 4, lane + 2, (3, 7), 0))
         (far_z,) = yield [(own, PZ2)]
         pair = jnp.concatenate([own, far_z], 0)
         (near_z,) = yield [(pair, PZ1)]
         line = jnp.concatenate([pair, near_z], 0)
-        to_core = [(line, PC)]
-        now, later = ([], to_core) if line_later else (to_core, [])
-        over_x, over_y, *rest = yield [(line, PX), (line, PY)] + now
-        diag_x, diag_y, over_y_far, *more = yield [(over_y[:2], PX), (over_x[2:], PY), (over_y, PC)] + later
-        (line_far,) = rest + more
-        pieces.bufs.update({0: line, 1: over_y, 2: over_x, 3: diag_x, 4: diag_y, 5: line_far, 6: over_y_far})
-        over_x_far, diag_x_far, diag_y_far = yield [(over_x, PC), (diag_x, PC), (diag_y, PC)]
-        pieces.bufs.update({7: over_x_far, 8: diag_x_far, 9: diag_y_far})
+        over_x, over_y, line_far = yield [(line, PX), (line, PY), (line, PC)]
+        pieces.bufs.update({0: line, 1: over_y, 2: over_x, 5: line_far})
+        diag_x, diag_y, over_y_far, over_x_far = yield [
+            (over_y[:2], PX),
+            (over_x[2:], PY),
+            (over_y, PC),
+            (over_x, PC),
+        ]
+        pieces.bufs.update({3: diag_x, 4: diag_y, 6: over_y_far, 7: over_x_far})
+        diag_x_far, diag_y_far = yield [(diag_x, PC), (diag_y, PC)]
+        pieces.bufs.update({8: diag_x_far, 9: diag_y_far})
+
+    @staticmethod
+    def gather_plane_first(shard, pieces, first_col):
+        own = shard[None]
+        over_x, over_y = yield [(own, PX), (own, PY)]
+        (diag,) = yield [(over_y, PX)]
+        plane = jnp.concatenate([own, over_y, over_x, diag], 0)
+        (far_z,) = yield [(plane, PZ2)]
+        half = jnp.concatenate([plane, far_z], 0)
+        (near_z,) = yield [(half, PZ1)]
+        half_far, near_z_far = yield [(half, PC), (near_z, PC)]
+        for n, (buf, core) in enumerate(((half, 0), (near_z, 0), (half_far, 1), (near_z_far, 1))):
+            near = 2 * (n % 2)
+            name = 20 + n
+            pieces.bufs[name] = buf
+            for x in range(2):
+                places = tuple(4 * far + near + y for far in range(2) for y in range(2))
+                pieces.plan.append((name, 2 * x + core, (x, places), first_col))
 
     @staticmethod
     def slot(block, dp):
@@ -139,7 +160,7 @@
         (from_z,) = yield [(out_z, PZ1)]
         out_z, kept = add_fourth(kept, from_z)
         (last,) = yield [(out_z, PZ2)]
-        return kept + last.astype(f32)
+        return kept, last
 
     @staticmethod
     def scatter_z_first(far, near):
@@ -152,7 +173,7 @@
         in_x, in_y = yield [(out_x, PX), (out_y, PY)]
         out_z, kept = add_own(near, got, from_0, in_x, in_y)
         (last,) = yield [(out_z, PZ2)]
-        return kept + last.astype(f32)
+        return kept, last
 
     @staticmethod
     def gather_lane(vec):
@@ -163,7 +184,7 @@
 
     @staticmethod
     def sum_max(both, is_top):
-        for perm in (PZ2, PZ1, PC, PX, PY):
+        for perm in (PC, PX, PY, PZ1, PZ2):
             (other,) = yield [(both, perm)]
             both = jnp.where(is_top, jnp.maximum(both, other), both + other)
         return both
@@ -177,14 +198,16 @@
     parts = 1
 
     @staticmethod
-    def gather(shard, pieces, line_later=False):
+    def gather(shard, pieces, first_col=0):
         rows = lax.all_gather(shard, "dp", axis=0, tiled=True)
         full = lax.all_gather(rows, "tensor", axis=0)
         for k in range(full.shape[0]):
-            pieces.plan.append((k, k, None, None))
-            pieces.bufs[k] = full[k][None]
+            pieces.plan.append((first_col + k, k, None, first_col))
+            pieces.bufs[first_col + k] = full[k][None]
         return
         yield
+
+    gather_plane_first = gather
 
     @staticmethod
     def slot(block, dp):
@@ -199,7 +222,8 @@
     @staticmethod
     def scatter_line(grads):
         own = lax.psum_scatter(grads, "tensor", scatter_dimension=0, tiled=False)
-        return lax.psum_scatter(own, "dp", scatter_dimension=0, tiled=True)
+        own = lax.psum_scatter(own, "dp", scatter_dimension=0, tiled=True)
+        return own, jnp.zeros_like(own)
         yield
 
     @staticmethod
@@ -341,6 +365,19 @@
     return glue(own_sums, [like(shape, bf16), like(shape)], near, got, from_0, in_x, in_y)
 
 
+def attn_grads(kept, last):
+    rows, width = kept.shape
+    cols = width // 4
+
+    def attn_sums(kept, last, qkv, out):
+        total = kept[...] + last[...].astype(f32)
+        for j in range(3):
+            qkv[j] = total[:, j * cols : (j + 1) * cols]
+        out[...] = total[:, 3 * cols :].T
+
+    return glue(attn_sums, [like((3, rows, cols)), like((cols, rows))], kept, last)
+
+
 def attn_shard(qkv_weight, out_weight):
     _, rows, cols = qkv_weight.shape
 
@@ -353,20 +390,19 @@
 
 
 def assemble(plan, bufs, dst, dp):
-    for buf, lane, first, k, y in plan:
-        src, to = bufs[buf], lane - first
-        if k is None:
-            dst[to] = src[0]
+    for buf, lane, places, col in plan:
+        src = bufs[buf]
+        _, rows, width = src.shape
+        cols = pl.ds(col, width)
+        if places is None:
+            dst[lane, :, cols] = src[0]
             continue
-        rows = src.shape[1]
-
-        def move(i, carry):
-            z = k + i
-            place = 4 * (z & 1) + 2 * (z >> 1) + y
-            dst[to, pl.ds(pl.multiple_of((dp ^ place) * rows, rows), rows)] = src[i]
-            return carry
-
-        lax.fori_loop(0, src.shape[0], move, 0)
+        index = list(range(len(places)))
+        if isinstance(places[1], tuple):
+            x, places = places
+            index = [4 * (n // 2) + 2 * x + n % 2 for n in range(len(places))]
+        for n, place in zip(index, places):
+            dst[lane, pl.ds(pl.multiple_of((dp ^ place) * rows, rows), rows), cols] = src[n]
 
 
 def row(vec):
@@ -690,7 +726,10 @@
         )
         job_b = Job(net.gather_lane(bias_row[None]))
         job_u = Job(net.gather(up_weight.astype(bf16), pieces_u))
-        job_d = Job(net.gather(down_weight.T.astype(bf16), pieces_d, True))
+        shard_d = down_weight.T.astype(bf16)
+        col = up_cols // 2
+        job_d = Job(net.gather(shard_d[:, :col], pieces_d))
+        job_p = Job(net.gather_plane_first(shard_d[:, col:], pieces_d, col))
 
         def vmem(*shape, dtype=f32):
             return pltpu.VMEM(shape, dtype)
@@ -698,11 +737,11 @@
         unit = 2 * rows * width * width * blocks
         moved = 2 * width * width * blocks
 
-        step((), None, [job_a], [job_a])
-        step((), None, [job_a, job_b], [job_a, job_b])
-        step((), None, [job_a, job_u, job_b], [job_a, job_u, job_b])
+        step((), None, [job_a, job_p, job_b], [job_a, job_p, job_b])
+        step((), None, [job_a, job_p, job_b], [job_a, job_p, job_b])
         step((), None, [job_a, job_u, job_d], [job_a, job_u, job_d])
-        step((), None, [job_u, job_a], [job_a])
+        step((), None, [job_a, job_u], [job_a, job_u])
+        step((), None, [job_a, job_u], [job_a])
         biases = job_b.value
 
         bufs, plan = pieces_a.part(every)
@@ -725,8 +764,8 @@
                 4 * unit,
                 3 * moved,
             ),
-            [],
-            [job_u],
+            [job_d, job_p],
+            [job_u, job_d, job_p],
         )
         normed, inv, middle, mid_slope, mid_low, mid_t, tops_m = step(
             (act_ranges, ctx_low, tokens, out_bias, first_gain, first_shift, weight_a),
@@ -747,8 +786,8 @@
                 2 * unit,
                 2 * moved,
             ),
-            [job_u, job_d],
-            [job_u, job_d],
+            [job_u, job_p],
+            [job_u],
         )
 
         def up_part(lanes, start, finish):
@@ -774,9 +813,9 @@
             )
 
         act0, slope0, top0, weight_u0 = up_part(every[:half], [job_u, job_d], [job_u])
-        act1, slope1, top1, weight_u1 = up_part(every[half:], [], [job_d])
+        act1, slope1, top1, weight_u1 = up_part(every[half:], [], [job_d, job_p])
         step((), None, [job_d], [job_d])
-        step((), None, [job_d], [job_d])
+        step((), None, [job_d, job_p], [job_d, job_p])
         bufs_d, plan_d = pieces_d.part(every)
         layer_out, grad_second, ffn_t, sums_b, grad_up, up_sums = step(
             (act0, act1, slope0, slope1, middle, cotangent, down_bias, second_gain, second_shift, *bufs_d),
@@ -874,19 +913,19 @@
                 unit,
                 2 * moved,
             ),
-            [sum_a],
-            [sum_a, sum_d],
+            [sum_a, line_u, sum_s],
+            [sum_a, sum_d, sum_s],
         )[0]
-        step((), None, [sum_a, line_u, sum_s], [line_u, sum_s])
-        step((), None, [line_u, sum_s], [sum_a, sum_s])
+        step((), None, [sum_a, sum_s], [line_u])
+        step((), None, [line_u], [sum_a, sum_s])
         line_a = Job(net.scatter_line(*sum_a.value))
+        step((), None, [line_a, sum_d, sum_s], [line_a, sum_d, line_u, sum_s])
         step((), None, [line_a, sum_d, sum_s], [line_a, sum_d, sum_s])
-        step((), None, [line_a, sum_d, sum_s], [line_a, sum_d, line_u, sum_s])
-
-        down_grad, up_grad, a_grad, packed = sum_d.value, line_u.value, line_a.value, sum_s.value
+
+        packed = sum_s.value
+        down_grad, up_grad = (kept + last.astype(f32) for kept, last in (sum_d.value, line_u.value))
         down_grad = down_grad.T
-        qkv_grad = jnp.stack([a_grad[:, j * cols : (j + 1) * cols] for j in range(3)])
-        out_grad = a_grad[:, 3 * cols :].T
+        qkv_grad, out_grad = attn_grads(*line_a.value)
         own = lax.dynamic_slice_in_dim(packed, blocks + lane, 1)
         shared = packed[2 * blocks : 2 * blocks + 6]
         qv_bias_grad = jnp.concatenate([own[:, :cols], own[:, 2 * cols : 3 * cols]], 0)

time: 228 us -> 223 us (0.978)
  waiting for transfers between devices: 87.2 us -> 67.1 us
  Pallas kernels: 65.7 us -> 70.6 us
  other arithmetic: 4.41 us -> 8.61 us
  local copies, waits for them, and re-layouts: 5.28 us -> 8.74 us
    ppermute x62 -> x69, waiting for transfers between devices: 87.2 us -> 67.1 us  [step(): lax.ppermute(v, ALL, perm)]
    pallas_call x13 -> x14, Pallas kernels: 2.66 us -> 7.71 us  [glue(): return call(kernel, kernel.__name__, [VM] * len(ins), outs)(*ins)]
    unnamed x39 -> x54, local copies, waits for them, and re-layouts: 2.69 us -> 6.24 us
    ppermute x62 -> x69, starting transfers between devices: 63.5 us -> 65.2 us  [step(): lax.ppermute(v, ALL, perm)]
  transfers between devices with their start and end apart: 62 -> 69, of which waited for: 33 -> 24; matrix products, arithmetic and copies ran while one was open for 1% -> 2% of each run, Pallas kernels for 23% -> 25%
where the time goes in v7:
time: 223 us; the launch traced here: 222 us
  Pallas kernels  70.6 us (32%)
  waiting for transfers between devices  67.1 us (30%)
  starting transfers between devices  65.2 us (29%)
  local copies, waits for them, and re-layouts  8.74 us (4%)
  other arithmetic  8.61 us (4%)
    ppermute x69, waiting for transfers between devices, step(): lax.ppermute(v, ALL, perm)  67.1 us
    ppermute x69, starting transfers between devices, step(): lax.ppermute(v, ALL, perm)  65.2 us
    pallas_call x10, Pallas kernels, step(): outs = run(*ins) if run else ins  62.9 us
    pallas_call x14, Pallas kernels, glue(): return call(kernel, kernel.__name__, [VM] * len(ins), outs)(*ins)  7.71 us
    unnamed x54, local copies, waits for them, and re-layouts  6.24 us
  transfers between devices with their start and end apart: 69, of which 24 were waited for; matrix products, arithmetic and copies ran while one was open for 2% of the time, Pallas kernels for 25%

profile of v7, /device:TPU:0, one launch (start us, length us, event | category | flops | bytes accessed | tf_op | source)
XLA Modules:
  0.0 222.2 jit_solution(3976879415906898970)
XLA Ops:
  5.2 4.1 %collective-permute-start = (bf16[1,96,768]{2,1,0:T(8,128)(2,1)S(1)}, bf16[1,96,768]{2,1,0:T(8,128)(2,1)S(1)}, u32[]{:S(2)}, u32[]{:S(2)}) collective-permute-start(bf16[1,96,768]{2,1,0:T(8,128)(2,1)S(1)} %bitcast.24), channel_id=1, source_target_pairs={{0,16},{1,17},{2,18},{3,19},{4,20},{5,21},{6,22},{7,23},{8,24},{9,... | collective-permute-start | bytes 442376 | tf_op jit(solution)/shard_map/ppermute | solution.py:78
  9.3 1.5 collective-permute-start.1
  10.8 1.5 collective-permute-start.2
  12.9 3.1 %collective-permute-done.3 = f32[1,1408]{1,0:T(1,128)S(1)} collective-permute-done((f32[1,1408]{1,0:T(1,128)S(1)}, f32[1,1408]{1,0:T(1,128)S(1)}, u32[]{:S(2)}, u32[]{:S(2)}) %collective-permute-start.3) | collective-permute-done | bytes 5664 | tf_op jit(solution)/shard_map/ppermute | solution.py:78
  19.9 2.2 collective-permute-done.5
  22.0 2.6 %collective-permute-done.4 = bf16[2,96,768]{2,1,0:T(8,128)(2,1)S(1)} collective-permute-done((bf16[2,96,768]{2,1,0:T(8,128)(2,1)S(1)}, bf16[2,96,768]{2,1,0:T(8,128)(2,1)S(1)}, u32[]{:S(2)}, u32[]{:S(2)}) %collective-permute-start.4) | collective-permute-done | bytes 294944 | tf_op jit(solution)/shard_map/ppermute | solution.py:78
  24.7 1.3 collective-permute-start.7
  26.1 1.5 collective-permute-start.8
  27.6 3.3 %collective-permute-start.10 = (bf16[1,96,768]{2,1,0:T(8,128)(2,1)S(1)}, bf16[1,96,768]{2,1,0:T(8,128)(2,1)S(1)}, u32[]{:S(2)}, u32[]{:S(2)}) collective-permute-start(bf16[1,96,768]{2,1,0:T(8,128)(2,1)S(1)} %convert_bitcast_fusion), channel_id=1, source_target_pairs={{0,16},{1,17},{2,18},{3,19},{4,20},{5,21},{6,22},{7,23},{8,24},{9,... | collective-permute-start | bytes 442376 | tf_op jit(solution)/shard_map/ppermute | solution.py:78
  31.6 10.2 %collective-permute-done.11 = bf16[1,96,384]{2,1,0:T(8,128)(2,1)S(1)} collective-permute-done((bf16[1,96,384]{2,1,0:T(8,128)(2,1)S(1)}, bf16[1,96,384]{2,1,0:T(8,128)(2,1)S(1)}, u32[]{:S(2)}, u32[]{:S(2)}) %collective-permute-start.11) | collective-permute-done | bytes 73760 | tf_op jit(solution)/shard_map/ppermute | solution.py:78
  44.8 6.8 %collective-permute-done.12.rest_3_ = bf16[2,96,768]{2,1,0:T(8,128)(2,1)S(1)} collective-permute-done((bf16[2,96,768]{2,1,0:T(8,128)(2,1)S(1)}, bf16[2,96,768]{2,1,0:T(8,128)(2,1)S(1)}, u32[]{:S(2)}, u32[]{:S(2)}) %collective-permute-start.12) | collective-permute-done | bytes 294944 | tf_op jit(solution)/shard_map/ppermute | solution.py:78
  52.7 1.6 collective-permute-start.19
  54.3 1.5 collective-permute-start.20
  55.8 2.4 %collective-permute-start.23 = (bf16[4,96,384]{2,1,0:T(8,128)(2,1)S(1)}, bf16[4,96,384]{2,1,0:T(8,128)(2,1)S(1)}, u32[]{:S(2)}, u32[]{:S(2)}) collective-permute-start(bf16[4,96,384]{2,1,0:T(8,128)(2,1)S(1)} %pad_maximum_fusion.4), channel_id=1, source_target_pairs={{0,16},{1,17},{2,18},{3,19},{4,20},{5,21},{6,22},{7,23},{8,24},{9,... | collective-permute-start | bytes 884744 | tf_op jit(solution)/shard_map/ppermute | solution.py:78
  58.3 1.7 collective-permute-start.22
  60.0 11.3 %attn_forward.1 = (bf16[4,512,640]{2,1,0:T(8,128)(2,1)S(1)}, f32[4,8,512]{2,1,0:T(8,128)S(1)}, bf16[768,512]{1,0:T(8,128)(2,1)S(1)}, bf16[4,512,256]{2,1,0:T(8,1...) custom-call(f32[4]{0:T(128)S(1)} %copy-done.9, ...), custom_call_target="tpu_custom_call" | custom-call | flops 9663676416 | bytes 14155776 | tf_op jit(solution)/shard_map/attn_forward/pallas_call | solution.py:79
  71.3 1.5 copy-done.21
  75.6 3.2 %attn_finish.1 = (f32[512,768]{1,0:T(8,128)S(1)}, f32[512,1]{1,0:T(8,128)S(1)}, f32[512,768]{1,0:T(8,128)S(1)}, f32[512,768]{1,0:T(8,128)S(1)}, bf16[512,768]{1,...) custom-call(f32[4]{0:T(128)S(1)} %copy-done.9, ...), custom_call_target="tpu_custom_call" | custom-call | flops 4831838208 | bytes 9437184 | tf_op jit(solution)/shard_map/attn_finish/pallas_call | solution.py:79
  78.8 3.7 %collective-permute-done.24.rest_1_ = bf16[2,96,768]{2,1,0:T(8,128)(2,1)S(1)} collective-permute-done((bf16[2,96,768]{2,1,0:T(8,128)(2,1)S(1)}, bf16[2,96,768]{2,1,0:T(8,128)(2,1)S(1)}, u32[]{:S(2)}, u32[]{:S(2)}) %collective-permute-start.24) | collective-permute-done | bytes 294944 | tf_op jit(solution)/shard_map/ppermute | solution.py:78
  83.4 1.5 collective-permute-start.30
  85.7 3.9 %up_forward_0.1 = (bf16[2,512,768]{2,1,0:T(8,128)(2,1)S(1)}, f32[2,512,768]{2,1,0:T(8,128)S(1)}, f32[8,128]{1,0:T(8,128)S(1)}, bf16[2,768,768]{2,1,0:T(8,128)(2,1)S(1)}) custom-call(f32[4]{0:T(128)S(1)} %copy-done.9, bf16[512,768]{1,0:T(8,128)(2,1)S(1)} %get-tuple-element.458.mid_low, f32[4,1,1408]{2,1,0:T(1,128)S(1)} %bitcast.28, ...), custom_call_target="tpu_custom_call" | custom-call | flops 4831838208 | bytes 9437184 | tf_op jit(solution)/shard_map/up_forward_0/pallas_call | solution.py:79
  89.8 3.9 %up_forward_2.1 = (bf16[2,512,768]{2,1,0:T(8,128)(2,1)S(1)}, f32[2,512,768]{2,1,0:T(8,128)S(1)}, f32[8,128]{1,0:T(8,128)S(1)}, bf16[2,768,768]{2,1,0:T(8,128)(2,1)S(1)}) custom-call(f32[4]{0:T(128)S(1)} %copy-done.9, bf16[512,768]{1,0:T(8,128)(2,1)S(1)} %get-tuple-element.458.mid_low, f32[4,1,1408]{2,1,0:T(1,128)S(1)} %bitcast.29, ...), custom_call_target="tpu_custom_call" | custom-call | flops 4831838208 | bytes 9437184 | tf_op jit(solution)/shard_map/up_forward_2/pallas_call | solution.py:79
  96.0 4.5 %collective-permute-done.34.rest_3_ = bf16[2,96,384]{2,1,0:T(8,128)(2,1)S(1)} collective-permute-done((bf16[2,96,384]{2,1,0:T(8,128)(2,1)S(1)}, bf16[2,96,384]{2,1,0:T(8,128)(2,1)S(1)}, u32[]{:S(2)}, u32[]{:S(2)}) %collective-permute-start.34) | collective-permute-done | bytes 147488 | tf_op jit(solution)/shard_map/ppermute | solution.py:78
  101.8 2.0 collective-permute-done.38.rest_8_
  104.1 8.8 %down_both.1 = (bf16[512,768]{1,0:T(8,128)(2,1)}, f32[512,768]{1,0:T(8,128)S(1)}, bf16[768,512]{1,0:T(8,128)(2,1)S(1)}, f32[8,768]{1,0:T(8,128)S(1)}, bf16[4,512...) custom-call(bf16[2,512,768]{2,1,0:T(8,128)(2,1)S(1)} %get-tuple-element.538.act0.rest_0_, ...), custom_call_target="tpu_custom_call" | custom-call | flops 4831838208 | bytes 18874368 | tf_op jit(solution)/shard_map/down_both/pallas_call | solution.py:79
  112.9 2.7 %up_grad.1 = (bf16[2,8,96,768]{3,2,1,0:T(8,128)(2,1)S(1)}, bf16[2,8,96,768]{3,2,1,0:T(8,128)(2,1)S(1)}) custom-call(bf16[768,512]{1,0:T(8,128)(2,1)S(1)} %get-tuple-element.534.left_t, bf16[4,512,768]{2,1,0:T(8,128)(2,1)S(1)} %get-tuple-element.548.rest_0_.grad_up), custom_call_target="tpu_custom_call" | custom-call | flops 2415919104 | bytes 4718592 | tf_op jit(solution)/shard_map/up_grad/pallas_call | solution.py:79
  115.8 2.7 %down_grad.1 = (bf16[2,8,96,768]{3,2,1,0:T(8,128)(2,1)S(1)}, bf16[2,8,96,768]{3,2,1,0:T(8,128)(2,1)S(1)}) custom-call(bf16[768,512]{1,0:T(8,128)(2,1)S(1)} %get-tuple-element.537.left_t, bf16[2,512,768]{2,1,0:T(8,128)(2,1)S(1)} %copy-done.18, bf16[2,512,768]{2,1,0:T(8,128)(2,1)S(1)} %get-tuple-element.539.act1.rest_1_), custom_call_target="tpu_custom_call" | custom-call | flops 2415919104 | bytes 4718592 | tf_op jit(solution)/shard_map/down_grad/pallas_call | solution.py:79
  118.5 1.7 collective-permute-done.42.got
  120.6 1.5 collective-permute-start.44
  123.2 6.2 %mid_backward.1 = (f32[512,768]{1,0:T(8,128)S(1)}, bf16[768,512]{1,0:T(8,128)(2,1)S(1)}, bf16[4,512,256]{2,1,0:T(8,128)(2,1)S(1)}, f32[8,768]{1,0:T(8,128)S(1)}) custom-call(bf16[4,512,768]{2,1,0:T(8,128)(2,1)S(1)} %get-tuple-element.548.rest_0_.grad_up, f32[512,768]{1,0:T(8,128)S(1)} %get-tuple-element.549.grad_second, ...), custom_call_target="tpu_custom_call" | custom-call | flops 3221225472 | bytes 14155776 | tf_op jit(solution)/shard_map/mid_backward/pallas_call | solution.py:79
  134.2 15.1 %attn_backward.1 = (bf16[4,512,640]{2,1,0:T(8,128)(2,1)S(1)}, bf16[2,8,96,768]{3,2,1,0:T(8,128)(2,1)S(1)}, bf16[2,8,96,768]{3,2,1,0:T(8,128)(2,1)S(1)}, f32[16,768]{1,0:T(8,128)S(1)}) custom-call(s32[1]{0:T(128)S(6)} %copy.37.longs, s32[12]{0:T(128)S(1)} %copy-done.16, bf16[4,512,640]{2,1,0:T(8,128)(2,1)S(1)} %copy-done.22, ...), custom_call_target="tpu_custom_call" | custom-call | flops 9663676416 | bytes 9437184 | tf_op jit(solution)/shard_map/attn_backward/pallas_call | solution.py:79
  149.9 1.4 collective-permute-start.55
  151.3 1.5 collective-permute-start.53
  158.5 5.1 %token_backward.1 = bf16[512,768]{1,0:T(8,128)(2,1)} custom-call(f32[4]{0:T(128)S(1)} %copy-done.9, bf16[4,512,640]{2,1,0:T(8,128)(2,1)S(1)} %get-tuple-element.623.grad_qkv, f32[512,768]{1,0:T(8,128)S(1)} %get-tuple-element.624.grad_first, bf16[512,768]{1,0:T(8,128)(2,1)S(1)} %copy-done.2, bf16[4,768,768]{2,1,0:T(8,128)(2,1)S(1)} %get-tuple-element.626.weight.out_weight), custom_call_target="tpu_custom_call" | custom-call | flops 2415919104 | bytes 9437184 | tf_op jit(solution)/shard_map/token_backward/pallas_call | solution.py:79
  163.6 3.8 %collective-permute-done.54.from_y = bf16[96,768]{1,0:T(8,128)(2,1)S(1)} collective-permute-done((bf16[96,768]{1,0:T(8,128)(2,1)S(1)}, bf16[96,768]{1,0:T(8,128)(2,1)S(1)}, u32[]{:S(2)}, u32[]{:S(2)}) %collective-permute-start.54) | collective-permute-done | bytes 147488 | tf_op jit(solution)/shard_map/ppermute | solution.py:78
  170.8 1.4 collective-permute-start.63
  173.2 10.6 %collective-permute-done.59 = f32[16,768]{1,0:T(8,128)S(1)} collective-permute-done((f32[16,768]{1,0:T(8,128)S(1)}, f32[16,768]{1,0:T(8,128)S(1)}, u32[]{:S(2)}, u32[]{:S(2)}) %collective-permute-start.59) | collective-permute-done | bytes 49184 | tf_op jit(solution)/shard_map/ppermute | solution.py:78
  185.4 1.4 collective-permute-start.60
  186.8 1.5 collective-permute-start.61
  190.6 1.7 collective-permute-start.64
  192.3 2.0 collective-permute-start.65
  194.3 2.7 %collective-permute-done.64 = bf16[96,768]{1,0:T(8,128)(2,1)} collective-permute-done((bf16[96,768]{1,0:T(8,128)(2,1)}, bf16[96,768]{1,0:T(8,128)(2,1)}, u32[]{:S(2)}, u32[]{:S(2)}) %collective-permute-start.64) | collective-permute-done | bytes 147488 | tf_op jit(solution)/shard_map/ppermute | solution.py:78
  198.4 1.7 copy-done.1
  202.5 2.2 collective-permute-start.66
  205.5 2.1 collective-permute-start.68
  207.6 1.6 convert_add_fusion
  209.2 8.4 %collective-permute-done.68 = f32[16,768]{1,0:T(8,128)S(1)} collective-permute-done((f32[16,768]{1,0:T(8,128)S(1)}, f32[16,768]{1,0:T(8,128)S(1)}, u32[]{:S(2)}, u32[]{:S(2)}) %collective-permute-start.68) | collective-permute-done | bytes 49184 | tf_op jit(solution)/shard_map/ppermute | solution.py:78
  219.0 1.7 add_bitcast_fusion
  (206 shorter events, 50.1 us)
Async XLA Ops:
  5.2 11.1 %collective-permute-start = (bf16[1,96,768]{2,1,0:T(8,128)(2,1)S(1)}, bf16[1,96,768]{2,1,0:T(8,128)(2,1)S(1)}, u32[]{:S(2)}, u32[]{:S(2)}) collective-permute-start(bf16[1,96,768]{2,1,0:T(8,128)(2,1)S(1)} %bitcast.24), channel_id=1, source_target_pairs={{0,16},{1,17},{2,18},{3,19},{4,20},{5,21},{6,22},{7,23},{8,24},{9,... | collective-permute-start | bytes 442376 | tf_op jit(solution)/shard_map/ppermute | solution.py:78
  16.4 8.2 %collective-permute-start.4 = (bf16[2,96,768]{2,1,0:T(8,128)(2,1)S(1)}, bf16[2,96,768]{2,1,0:T(8,128)(2,1)S(1)}, u32[]{:S(2)}, u32[]{:S(2)}) collective-permute-start(bf16[2,96,768]{2,1,0:T(8,128)(2,1)S(1)} %pad_maximum_fusion.2), channel_id=1, source_target_pairs={{0,8},{1,9},{2,10},{3,11},{4,12},{5,13},{6,14},{7,15},{8,0},{9,1},... | collective-permute-start | bytes 884744 | tf_op jit(solution)/shard_map/ppermute | solution.py:78
  24.7 17.0 %collective-permute-start.7 = (bf16[4,96,768]{2,1,0:T(8,128)(2,1)S(1)}, bf16[4,96,768]{2,1,0:T(8,128)(2,1)S(1)}, u32[]{:S(2)}, u32[]{:S(2)}) collective-permute-start(bf16[4,96,768]{2,1,0:T(8,128)(2,1)S(1)} %pad_maximum_fusion.rest_0_), channel_id=1, source_target_pairs={{0,2},{1,3},{2,0},{3,1},{4,6},{5,7},{6,4},{7,5},{8,10},{9,11},{10,... | collective-permute-start | bytes 1769480 | tf_op jit(solution)/shard_map/ppermute | solution.py:78
  26.1 15.7 %collective-permute-start.8 = (bf16[4,96,768]{2,1,0:T(8,128)(2,1)S(1)}, bf16[4,96,768]{2,1,0:T(8,128)(2,1)S(1)}, u32[]{:S(2)}, u32[]{:S(2)}) collective-permute-start(bf16[4,96,768]{2,1,0:T(8,128)(2,1)S(1)} %pad_maximum_fusion.rest_0_), channel_id=1, source_target_pairs={{0,4},{1,5},{2,6},{3,7},{4,0},{5,1},{6,2},{7,3},{8,12},{9,13},{10,... | collective-permute-start | bytes 1769480 | tf_op jit(solution)/shard_map/ppermute | solution.py:78
  27.6 14.2 %collective-permute-start.9 = (bf16[4,96,768]{2,1,0:T(8,128)(2,1)S(1)}, bf16[4,96,768]{2,1,0:T(8,128)(2,1)S(1)}, u32[]{:S(2)}, u32[]{:S(2)}) collective-permute-start(bf16[4,96,768]{2,1,0:T(8,128)(2,1)S(1)} %pad_maximum_fusion.rest_0_), channel_id=1, source_target_pairs={{0,1},{1,0},{2,3},{3,2},{4,5},{5,4},{6,7},{7,6},{8,9},{9,8},{10,11... | collective-permute-start | bytes 1769480 | tf_op jit(solution)/shard_map/ppermute | solution.py:78
  27.6 14.2 %collective-permute-start.10 = (bf16[1,96,768]{2,1,0:T(8,128)(2,1)S(1)}, bf16[1,96,768]{2,1,0:T(8,128)(2,1)S(1)}, u32[]{:S(2)}, u32[]{:S(2)}) collective-permute-start(bf16[1,96,768]{2,1,0:T(8,128)(2,1)S(1)} %convert_bitcast_fusion), channel_id=1, source_target_pairs={{0,16},{1,17},{2,18},{3,19},{4,20},{5,21},{6,22},{7,23},{8,24},{9,... | collective-permute-start | bytes 442376 | tf_op jit(solution)/shard_map/ppermute | solution.py:78
  30.9 10.8 %collective-permute-start.11 = (bf16[1,96,384]{2,1,0:T(8,128)(2,1)S(1)}, bf16[1,96,384]{2,1,0:T(8,128)(2,1)S(1)}, u32[]{:S(2)}, u32[]{:S(2)}) collective-permute-start(bf16[1,96,384]{2,1,0:T(8,128)(2,1)S(1)} %get-tuple-element.362), channel_id=1, source_target_pairs={{0,16},{1,17},{2,18},{3,19},{4,20},{5,21},{6,22},{7,23},{8,24},{9,... | collective-permute-start | bytes 221192 | tf_op jit(solution)/shard_map/ppermute | solution.py:78
  41.9 10.2 %collective-permute-start.14 = (bf16[4,96,768]{2,1,0:T(8,128)(2,1)S(1)}, bf16[4,96,768]{2,1,0:T(8,128)(2,1)S(1)}, u32[]{:S(2)}, u32[]{:S(2)}) collective-permute-start(bf16[4,96,768]{2,1,0:T(8,128)(2,1)S(1)} %collective-permute-done.8.rest_1_), channel_id=1, source_target_pairs={{0,1},{1,0},{2,3},{3,2},{4,5},{5,4},{6,7},{7,6},{8,9},{9,8},{10,11... | collective-permute-start | bytes 1769480 | tf_op jit(solution)/shard_map/ppermute | solution.py:78
  42.0 10.1 %collective-permute-start.15 = (bf16[4,96,768]{2,1,0:T(8,128)(2,1)S(1)}, bf16[4,96,768]{2,1,0:T(8,128)(2,1)S(1)}, u32[]{:S(2)}, u32[]{:S(2)}) collective-permute-start(bf16[4,96,768]{2,1,0:T(8,128)(2,1)S(1)} %collective-permute-done.7.rest_2_), channel_id=1, source_target_pairs={{0,1},{1,0},{2,3},{3,2},{4,5},{5,4},{6,7},{7,6},{8,9},{9,8},{10,11... | collective-permute-start | bytes 1769480 | tf_op jit(solution)/shard_map/ppermute | solution.py:78
  42.5 9.1 %collective-permute-start.12 = (bf16[2,96,768]{2,1,0:T(8,128)(2,1)S(1)}, bf16[2,96,768]{2,1,0:T(8,128)(2,1)S(1)}, u32[]{:S(2)}, u32[]{:S(2)}) collective-permute-start(bf16[2,96,768]{2,1,0:T(8,128)(2,1)S(1)} %slice.68), channel_id=1, source_target_pairs={{0,2},{1,3},{2,0},{3,1},{4,6},{5,7},{6,4},{7,5},{8,10},{9,11},{10,... | collective-permute-start | bytes 884744 | tf_op jit(solution)/shard_map/ppermute | solution.py:78
  43.1 8.7 %collective-permute-start.13 = (bf16[2,96,768]{2,1,0:T(8,128)(2,1)S(1)}, bf16[2,96,768]{2,1,0:T(8,128)(2,1)S(1)}, u32[]{:S(2)}, u32[]{:S(2)}) collective-permute-start(bf16[2,96,768]{2,1,0:T(8,128)(2,1)S(1)} %slice.69), channel_id=1, source_target_pairs={{0,4},{1,5},{2,6},{3,7},{4,0},{5,1},{6,2},{7,3},{8,12},{9,13},{10,... | collective-permute-start | bytes 884744 | tf_op jit(solution)/shard_map/ppermute | solution.py:78
  43.6 8.4 %collective-permute-start.16 = (bf16[2,96,768]{2,1,0:T(8,128)(2,1)S(1)}, bf16[2,96,768]{2,1,0:T(8,128)(2,1)S(1)}, u32[]{:S(2)}, u32[]{:S(2)}) collective-permute-start(bf16[2,96,768]{2,1,0:T(8,128)(2,1)S(1)} %pad_maximum_fusion.3), channel_id=1, source_target_pairs={{0,8},{1,9},{2,10},{3,11},{4,12},{5,13},{6,14},{7,15},{8,0},{9,1},... | collective-permute-start | bytes 884744 | tf_op jit(solution)/shard_map/ppermute | solution.py:78
  52.7 20.1 %collective-permute-start.19 = (bf16[4,96,768]{2,1,0:T(8,128)(2,1)S(1)}, bf16[4,96,768]{2,1,0:T(8,128)(2,1)S(1)}, u32[]{:S(2)}, u32[]{:S(2)}) collective-permute-start(bf16[4,96,768]{2,1,0:T(8,128)(2,1)S(1)} %pad_maximum_fusion.1.rest_0_), channel_id=1, source_target_pairs={{0,2},{1,3},{2,0},{3,1},{4,6},{5,7},{6,4},{7,5},{8,10},{9,11},{10,... | collective-permute-start | bytes 1769480 | tf_op jit(solution)/shard_map/ppermute | solution.py:78
  54.3 18.5 %collective-permute-start.20 = (bf16[4,96,768]{2,1,0:T(8,128)(2,1)S(1)}, bf16[4,96,768]{2,1,0:T(8,128)(2,1)S(1)}, u32[]{:S(2)}, u32[]{:S(2)}) collective-permute-start(bf16[4,96,768]{2,1,0:T(8,128)(2,1)S(1)} %pad_maximum_fusion.1.rest_0_), channel_id=1, source_target_pairs={{0,4},{1,5},{2,6},{3,7},{4,0},{5,1},{6,2},{7,3},{8,12},{9,13},{10,... | collective-permute-start | bytes 1769480 | tf_op jit(solution)/shard_map/ppermute | solution.py:78
  55.8 17.0 %collective-permute-start.21 = (bf16[4,96,768]{2,1,0:T(8,128)(2,1)S(1)}, bf16[4,96,768]{2,1,0:T(8,128)(2,1)S(1)}, u32[]{:S(2)}, u32[]{:S(2)}) collective-permute-start(bf16[4,96,768]{2,1,0:T(8,128)(2,1)S(1)} %pad_maximum_fusion.1.rest_0_), channel_id=1, source_target_pairs={{0,1},{1,0},{2,3},{3,2},{4,5},{5,4},{6,7},{7,6},{8,9},{9,8},{10,11... | collective-permute-start | bytes 1769480 | tf_op jit(solution)/shard_map/ppermute | solution.py:78
  55.8 17.0 %collective-permute-start.23 = (bf16[4,96,384]{2,1,0:T(8,128)(2,1)S(1)}, bf16[4,96,384]{2,1,0:T(8,128)(2,1)S(1)}, u32[]{:S(2)}, u32[]{:S(2)}) collective-permute-start(bf16[4,96,384]{2,1,0:T(8,128)(2,1)S(1)} %pad_maximum_fusion.4), channel_id=1, source_target_pairs={{0,16},{1,17},{2,18},{3,19},{4,20},{5,21},{6,22},{7,23},{8,24},{9,... | collective-permute-start | bytes 884744 | tf_op jit(solution)/shard_map/ppermute | solution.py:78
  58.3 14.6 %collective-permute-start.22 = (bf16[2,96,384]{2,1,0:T(8,128)(2,1)S(1)}, bf16[2,96,384]{2,1,0:T(8,128)(2,1)S(1)}, u32[]{:S(2)}, u32[]{:S(2)}) collective-permute-start(bf16[2,96,384]{2,1,0:T(8,128)(2,1)S(1)} %pad_maximum_fusion.6), channel_id=1, source_target_pairs={{0,8},{1,9},{2,10},{3,11},{4,12},{5,13},{6,14},{7,15},{8,0},{9,1},... | collective-permute-start | bytes 442376 | tf_op jit(solution)/shard_map/ppermute | solution.py:78
  73.0 9.8 %collective-permute-start.26 = (bf16[4,96,768]{2,1,0:T(8,128)(2,1)S(1)}, bf16[4,96,768]{2,1,0:T(8,128)(2,1)S(1)}, u32[]{:S(2)}, u32[]{:S(2)}) collective-permute-start(bf16[4,96,768]{2,1,0:T(8,128)(2,1)S(1)} %collective-permute-done.20.rest_1_), channel_id=1, source_target_pairs={{0,1},{1,0},{2,3},{3,2},{4,5},{5,4},{6,7},{7,6},{8,9},{9,8},{10,11... | collective-permute-start | bytes 1769480 | tf_op jit(solution)/shard_map/ppermute | solution.py:78
  73.1 9.7 %collective-permute-start.27 = (bf16[4,96,768]{2,1,0:T(8,128)(2,1)S(1)}, bf16[4,96,768]{2,1,0:T(8,128)(2,1)S(1)}, u32[]{:S(2)}, u32[]{:S(2)}) collective-permute-start(bf16[4,96,768]{2,1,0:T(8,128)(2,1)S(1)} %collective-permute-done.19.rest_0_), channel_id=1, source_target_pairs={{0,1},{1,0},{2,3},{3,2},{4,5},{5,4},{6,7},{7,6},{8,9},{9,8},{10,11... | collective-permute-start | bytes 1769480 | tf_op jit(solution)/shard_map/ppermute | solution.py:78
  73.6 9.0 %collective-permute-start.24 = (bf16[2,96,768]{2,1,0:T(8,128)(2,1)S(1)}, bf16[2,96,768]{2,1,0:T(8,128)(2,1)S(1)}, u32[]{:S(2)}, u32[]{:S(2)}) collective-permute-start(bf16[2,96,768]{2,1,0:T(8,128)(2,1)S(1)} %slice.70), channel_id=1, source_target_pairs={{0,2},{1,3},{2,0},{3,1},{4,6},{5,7},{6,4},{7,5},{8,10},{9,11},{10,... | collective-permute-start | bytes 884744 | tf_op jit(solution)/shard_map/ppermute | solution.py:78
  74.1 8.7 %collective-permute-start.25 = (bf16[2,96,768]{2,1,0:T(8,128)(2,1)S(1)}, bf16[2,96,768]{2,1,0:T(8,128)(2,1)S(1)}, u32[]{:S(2)}, u32[]{:S(2)}) collective-permute-start(bf16[2,96,768]{2,1,0:T(8,128)(2,1)S(1)} %slice.71), channel_id=1, source_target_pairs={{0,4},{1,5},{2,6},{3,7},{4,0},{5,1},{6,2},{7,3},{8,12},{9,13},{10,... | collective-permute-start | bytes 884744 | tf_op jit(solution)/shard_map/ppermute | solution.py:78
  75.0 18.6 %collective-permute-start.33 = (bf16[8,96,384]{2,1,0:T(8,128)(2,1)S(1)}, bf16[8,96,384]{2,1,0:T(8,128)(2,1)S(1)}, u32[]{:S(2)}, u32[]{:S(2)}) collective-permute-start(bf16[8,96,384]{2,1,0:T(8,128)(2,1)S(1)} %get-tuple-element.517.rest_10_), channel_id=1, source_target_pairs={{0,8},{1,9},{2,10},{3,11},{4,12},{5,13},{6,14},{7,15},{8,0},{9,1},... | collective-permute-start | bytes 1769480 | tf_op jit(solution)/shard_map/ppermute | solution.py:78
  82.8 6.8 %collective-permute-start.28 = (bf16[2,96,768]{2,1,0:T(8,128)(2,1)S(1)}, bf16[2,96,768]{2,1,0:T(8,128)(2,1)S(1)}, u32[]{:S(2)}, u32[]{:S(2)}) collective-permute-start(bf16[2,96,768]{2,1,0:T(8,128)(2,1)S(1)} %collective-permute-done.24.rest_1_), channel_id=1, source_target_pairs={{0,1},{1,0},{2,3},{3,2},{4,5},{5,4},{6,7},{7,6},{8,9},{9,8},{10,11... | collective-permute-start | bytes 884744 | tf_op jit(solution)/shard_map/ppermute | solution.py:78
  82.9 6.9 %collective-permute-start.29 = (bf16[2,96,768]{2,1,0:T(8,128)(2,1)S(1)}, bf16[2,96,768]{2,1,0:T(8,128)(2,1)S(1)}, u32[]{:S(2)}, u32[]{:S(2)}) collective-permute-start(bf16[2,96,768]{2,1,0:T(8,128)(2,1)S(1)} %collective-permute-done.25.rest_2_), channel_id=1, source_target_pairs={{0,1},{1,0},{2,3},{3,2},{4,5},{5,4},{6,7},{7,6},{8,9},{9,8},{10,11... | collective-permute-start | bytes 884744 | tf_op jit(solution)/shard_map/ppermute | solution.py:78
  83.4 10.3 %collective-permute-start.30 = (bf16[4,96,384]{2,1,0:T(8,128)(2,1)S(1)}, bf16[4,96,384]{2,1,0:T(8,128)(2,1)S(1)}, u32[]{:S(2)}, u32[]{:S(2)}) collective-permute-start(bf16[4,96,384]{2,1,0:T(8,128)(2,1)S(1)} %get-tuple-element.507.rest_0_), channel_id=1, source_target_pairs={{0,2},{1,3},{2,0},{3,1},{4,6},{5,7},{6,4},{7,5},{8,10},{9,11},{10,... | collective-permute-start | bytes 884744 | tf_op jit(solution)/shard_map/ppermute | solution.py:78
  84.9 8.8 %collective-permute-start.31 = (bf16[4,96,384]{2,1,0:T(8,128)(2,1)S(1)}, bf16[4,96,384]{2,1,0:T(8,128)(2,1)S(1)}, u32[]{:S(2)}, u32[]{:S(2)}) collective-permute-start(bf16[4,96,384]{2,1,0:T(8,128)(2,1)S(1)} %get-tuple-element.507.rest_0_), channel_id=1, source_target_pairs={{0,4},{1,5},{2,6},{3,7},{4,0},{5,1},{6,2},{7,3},{8,12},{9,13},{10,... | collective-permute-start | bytes 884744 | tf_op jit(solution)/shard_map/ppermute | solution.py:78
  93.7 7.1 %collective-permute-start.36 = (bf16[4,96,384]{2,1,0:T(8,128)(2,1)S(1)}, bf16[4,96,384]{2,1,0:T(8,128)(2,1)S(1)}, u32[]{:S(2)}, u32[]{:S(2)}) collective-permute-start(bf16[4,96,384]{2,1,0:T(8,128)(2,1)S(1)} %collective-permute-done.31.rest_1_), channel_id=1, source_target_pairs={{0,1},{1,0},{2,3},{3,2},{4,5},{5,4},{6,7},{7,6},{8,9},{9,8},{10,11... | collective-permute-start | bytes 884744 | tf_op jit(solution)/shard_map/ppermute | solution.py:78
  120.4 10.7 %collective-permute-start.43 = (bf16[2,8,96,768]{3,2,1,0:T(8,128)(2,1)S(1)}, bf16[2,8,96,768]{3,2,1,0:T(8,128)(2,1)S(1)}, u32[]{:S(2)}, u32[]{:S(2)}) collective-permute-start(bf16[2,8,96,768]{3,2,1,0:T(8,128)(2,1)S(1)} %get-tuple-element.562), channel_id=1, source_target_pairs={{0,1},{1,0},{2,3},{3,2},{4,5},{5,4},{6,7},{7,6},{8,9},{9,8},{10,11... | collective-permute-start | bytes 7077896 | tf_op jit(solution)/shard_map/ppermute | solution.py:78
  120.6 9.3 %collective-permute-start.44 = (bf16[2,96,768]{2,1,0:T(8,128)(2,1)S(1)}, bf16[2,96,768]{2,1,0:T(8,128)(2,1)S(1)}, u32[]{:S(2)}, u32[]{:S(2)}) collective-permute-start(bf16[2,96,768]{2,1,0:T(8,128)(2,1)S(1)} %get-tuple-element.563), channel_id=1, source_target_pairs={{0,2},{1,3},{2,0},{3,1},{4,6},{5,7},{6,4},{7,5},{8,10},{9,11},{10,... | collective-permute-start | bytes 884744 | tf_op jit(solution)/shard_map/ppermute | solution.py:78
  122.1 9.0 %collective-permute-start.45 = (bf16[2,96,768]{2,1,0:T(8,128)(2,1)S(1)}, bf16[2,96,768]{2,1,0:T(8,128)(2,1)S(1)}, u32[]{:S(2)}, u32[]{:S(2)}) collective-permute-start(bf16[2,96,768]{2,1,0:T(8,128)(2,1)S(1)} %get-tuple-element.564), channel_id=1, source_target_pairs={{0,4},{1,5},{2,6},{3,7},{4,0},{5,1},{6,2},{7,3},{8,12},{9,13},{10,... | collective-permute-start | bytes 884744 | tf_op jit(solution)/shard_map/ppermute | solution.py:78
  131.7 17.5 %collective-permute-start.46 = (bf16[4,96,768]{2,1,0:T(8,128)(2,1)S(1)}, bf16[4,96,768]{2,1,0:T(8,128)(2,1)S(1)}, u32[]{:S(2)}, u32[]{:S(2)}) collective-permute-start(bf16[4,96,768]{2,1,0:T(8,128)(2,1)S(1)} %get-tuple-element.601), channel_id=1, source_target_pairs={{0,2},{1,3},{2,0},{3,1},{4,6},{5,7},{6,4},{7,5},{8,10},{9,11},{10,... | collective-permute-start | bytes 1769480 | tf_op jit(solution)/shard_map/ppermute | solution.py:78
  132.4 16.9 %collective-permute-start.47 = (bf16[4,96,768]{2,1,0:T(8,128)(2,1)S(1)}, bf16[4,96,768]{2,1,0:T(8,128)(2,1)S(1)}, u32[]{:S(2)}, u32[]{:S(2)}) collective-permute-start(bf16[4,96,768]{2,1,0:T(8,128)(2,1)S(1)} %get-tuple-element.602), channel_id=1, source_target_pairs={{0,4},{1,5},{2,6},{3,7},{4,0},{5,1},{6,2},{7,3},{8,12},{9,13},{10,... | collective-permute-start | bytes 1769480 | tf_op jit(solution)/shard_map/ppermute | solution.py:78
  133.5 15.8 %collective-permute-start.48 = (bf16[4,96,768]{2,1,0:T(8,128)(2,1)S(1)}, bf16[4,96,768]{2,1,0:T(8,128)(2,1)S(1)}, u32[]{:S(2)}, u32[]{:S(2)}) collective-permute-start(bf16[4,96,768]{2,1,0:T(8,128)(2,1)S(1)} %get-tuple-element.603), channel_id=1, source_target_pairs={{0,8},{1,9},{2,10},{3,11},{4,12},{5,13},{6,14},{7,15},{8,0},{9,1},... | collective-permute-start | bytes 1769480 | tf_op jit(solution)/shard_map/ppermute | solution.py:78
  149.9 17.4 %collective-permute-start.55 = (bf16[4,96,768]{2,1,0:T(8,128)(2,1)S(1)}, bf16[4,96,768]{2,1,0:T(8,128)(2,1)S(1)}, u32[]{:S(2)}, u32[]{:S(2)}) collective-permute-start(bf16[4,96,768]{2,1,0:T(8,128)(2,1)S(1)} %get-tuple-element.631), channel_id=1, source_target_pairs={{0,8},{1,9},{2,10},{3,11},{4,12},{5,13},{6,14},{7,15},{8,0},{9,1},... | collective-permute-start | bytes 1769480 | tf_op jit(solution)/shard_map/ppermute | solution.py:78
  154.3 13.1 %collective-permute-start.51 = (bf16[2,96,768]{2,1,0:T(8,128)(2,1)S(1)}, bf16[2,96,768]{2,1,0:T(8,128)(2,1)S(1)}, u32[]{:S(2)}, u32[]{:S(2)}) collective-permute-start(bf16[2,96,768]{2,1,0:T(8,128)(2,1)S(1)} %get-tuple-element.627), channel_id=1, source_target_pairs={{0,2},{1,3},{2,0},{3,1},{4,6},{5,7},{6,4},{7,5},{8,10},{9,11},{10,... | collective-permute-start | bytes 884744 | tf_op jit(solution)/shard_map/ppermute | solution.py:78
  155.5 11.9 %collective-permute-start.52 = (bf16[2,96,768]{2,1,0:T(8,128)(2,1)S(1)}, bf16[2,96,768]{2,1,0:T(8,128)(2,1)S(1)}, u32[]{:S(2)}, u32[]{:S(2)}) collective-permute-start(bf16[2,96,768]{2,1,0:T(8,128)(2,1)S(1)} %get-tuple-element.628), channel_id=1, source_target_pairs={{0,4},{1,5},{2,6},{3,7},{4,0},{5,1},{6,2},{7,3},{8,12},{9,13},{10,... | collective-permute-start | bytes 884744 | tf_op jit(solution)/shard_map/ppermute | solution.py:78
  156.6 10.8 %collective-permute-start.54 = (bf16[96,768]{1,0:T(8,128)(2,1)S(1)}, bf16[96,768]{1,0:T(8,128)(2,1)S(1)}, u32[]{:S(2)}, u32[]{:S(2)}) collective-permute-start(bf16[96,768]{1,0:T(8,128)(2,1)S(1)} %get-tuple-element.630), channel_id=1, source_target_pairs={{0,4},{1,5},{2,6},{3,7},{4,0},{5,1},{6,2},{7,3},{8,12},{9,13},{10,... | collective-permute-start | bytes 442376 | tf_op jit(solution)/shard_map/ppermute | solution.py:78
  157.5 9.9 %collective-permute-start.56 = (f32[16,768]{1,0:T(8,128)S(1)}, f32[16,768]{1,0:T(8,128)S(1)}, u32[]{:S(2)}, u32[]{:S(2)}) collective-permute-start(f32[16,768]{1,0:T(8,128)S(1)} %add_select_fusion.4), channel_id=1, source_target_pairs={{0,2},{1,3},{2,0},{3,1},{4,6},{5,7},{6,4},{7,5},{8,10},{9,11},{10,... | collective-permute-start | bytes 147464 | tf_op jit(solution)/shard_map/ppermute | solution.py:78
  167.8 16.0 %collective-permute-start.57 = (bf16[4,96,768]{2,1,0:T(8,128)(2,1)S(1)}, bf16[4,96,768]{2,1,0:T(8,128)(2,1)S(1)}, u32[]{:S(2)}, u32[]{:S(2)}) collective-permute-start(bf16[4,96,768]{2,1,0:T(8,128)(2,1)S(1)} %get-tuple-element.639), channel_id=1, source_target_pairs={{0,2},{1,3},{2,0},{3,1},{4,6},{5,7},{6,4},{7,5},{8,10},{9,11},{10,... | collective-permute-start | bytes 1769480 | tf_op jit(solution)/shard_map/ppermute | solution.py:78
  168.8 15.0 %collective-permute-start.58 = (bf16[4,96,768]{2,1,0:T(8,128)(2,1)S(1)}, bf16[4,96,768]{2,1,0:T(8,128)(2,1)S(1)}, u32[]{:S(2)}, u32[]{:S(2)}) collective-permute-start(bf16[4,96,768]{2,1,0:T(8,128)(2,1)S(1)} %get-tuple-element.640), channel_id=1, source_target_pairs={{0,4},{1,5},{2,6},{3,7},{4,0},{5,1},{6,2},{7,3},{8,12},{9,13},{10,... | collective-permute-start | bytes 1769480 | tf_op jit(solution)/shard_map/ppermute | solution.py:78
  169.9 13.9 %collective-permute-start.59 = (f32[16,768]{1,0:T(8,128)S(1)}, f32[16,768]{1,0:T(8,128)S(1)}, u32[]{:S(2)}, u32[]{:S(2)}) collective-permute-start(f32[16,768]{1,0:T(8,128)S(1)} %add_select_fusion.3), channel_id=1, source_target_pairs={{0,4},{1,5},{2,6},{3,7},{4,0},{5,1},{6,2},{7,3},{8,12},{9,13},{10,... | collective-permute-start | bytes 147464 | tf_op jit(solution)/shard_map/ppermute | solution.py:78
  170.8 18.4 %collective-permute-start.63 = (bf16[2,96,768]{2,1,0:T(8,128)(2,1)S(1)}, bf16[2,96,768]{2,1,0:T(8,128)(2,1)S(1)}, u32[]{:S(2)}, u32[]{:S(2)}) collective-permute-start(bf16[2,96,768]{2,1,0:T(8,128)(2,1)S(1)} %get-tuple-element.656), channel_id=1, source_target_pairs={{0,8},{1,9},{2,10},{3,11},{4,12},{5,13},{6,14},{7,15},{8,0},{9,1},... | collective-permute-start | bytes 884744 | tf_op jit(solution)/shard_map/ppermute | solution.py:78
  185.4 12.1 %collective-permute-start.60 = (bf16[2,96,768]{2,1,0:T(8,128)(2,1)}, bf16[2,96,768]{2,1,0:T(8,128)(2,1)}, u32[]{:S(2)}, u32[]{:S(2)}) collective-permute-start(bf16[2,96,768]{2,1,0:T(8,128)(2,1)} %get-tuple-element.652), channel_id=1, source_target_pairs={{0,8},{1,9},{2,10},{3,11},{4,12},{5,13},{6,14},{7,15},{8,0},{9,1},... | collective-permute-start | bytes 884744 | tf_op jit(solution)/shard_map/ppermute | solution.py:78
  186.8 10.7 %collective-permute-start.61 = (bf16[2,96,768]{2,1,0:T(8,128)(2,1)}, bf16[2,96,768]{2,1,0:T(8,128)(2,1)}, u32[]{:S(2)}, u32[]{:S(2)}) collective-permute-start(bf16[2,96,768]{2,1,0:T(8,128)(2,1)} %get-tuple-element.653), channel_id=1, source_target_pairs={{0,2},{1,3},{2,0},{3,1},{4,6},{5,7},{6,4},{7,5},{8,10},{9,11},{10,... | collective-permute-start | bytes 884744 | tf_op jit(solution)/shard_map/ppermute | solution.py:78
  188.3 9.2 %collective-permute-start.62 = (bf16[2,96,768]{2,1,0:T(8,128)(2,1)}, bf16[2,96,768]{2,1,0:T(8,128)(2,1)}, u32[]{:S(2)}, u32[]{:S(2)}) collective-permute-start(bf16[2,96,768]{2,1,0:T(8,128)(2,1)} %get-tuple-element.654), channel_id=1, source_target_pairs={{0,4},{1,5},{2,6},{3,7},{4,0},{5,1},{6,2},{7,3},{8,12},{9,13},{10,... | collective-permute-start | bytes 884744 | tf_op jit(solution)/shard_map/ppermute | solution.py:78
  202.5 15.1 %collective-permute-start.66 = (bf16[96,768]{1,0:T(8,128)(2,1)S(1)}, bf16[96,768]{1,0:T(8,128)(2,1)S(1)}, u32[]{:S(2)}, u32[]{:S(2)}) collective-permute-start(bf16[96,768]{1,0:T(8,128)(2,1)S(1)} %get-tuple-element.666), channel_id=1, source_target_pairs={{0,16},{1,17},{2,18},{3,19},{4,20},{5,21},{6,22},{7,23},{8,24},{9,... | collective-permute-start | bytes 442376 | tf_op jit(solution)/shard_map/ppermute | solution.py:78
  204.7 13.0 %collective-permute-start.67 = (bf16[96,768]{1,0:T(8,128)(2,1)S(1)}, bf16[96,768]{1,0:T(8,128)(2,1)S(1)}, u32[]{:S(2)}, u32[]{:S(2)}) collective-permute-start(bf16[96,768]{1,0:T(8,128)(2,1)S(1)} %get-tuple-element.667), channel_id=1, source_target_pairs={{0,16},{1,17},{2,18},{3,19},{4,20},{5,21},{6,22},{7,23},{8,24},{9,... | collective-permute-start | bytes 442376 | tf_op jit(solution)/shard_map/ppermute | solution.py:78
  205.5 12.1 %collective-permute-start.68 = (f32[16,768]{1,0:T(8,128)S(1)}, f32[16,768]{1,0:T(8,128)S(1)}, u32[]{:S(2)}, u32[]{:S(2)}) collective-permute-start(f32[16,768]{1,0:T(8,128)S(1)} %add_select_fusion.1), channel_id=1, source_target_pairs={{0,16},{1,17},{2,18},{3,19},{4,20},{5,21},{6,22},{7,23},{8,24},{9,... | collective-permute-start | bytes 147464 | tf_op jit(solution)/shard_map/ppermute | solution.py:78
  (46 other events, 361.8 us)

commit v8 on v7

--- a/solution.py
+++ b/solution.py
@@ -101,11 +101,11 @@
     def gather(shard, pieces):
         own = shard[None]
         for base, lane in ((0, 0), (5, 1)):
-            pieces.plan.append((base, lane, (0, 4, 2, 6), 0))
-            pieces.plan.append((base + 1, lane, (1, 5, 3, 7), 0))
-            pieces.plan.append((base + 2, lane + 2, (0, 4, 2, 6), 0))
-            pieces.plan.append((base + 3, lane + 2, (1, 5), 0))
-            pieces.plan.append((base + 4, lane + 2, (3, 7), 0))
+            pieces.plan.append((base, lane, (4, 4, 2, 0, 0), 0))
+            pieces.plan.append((base + 1, lane, (4, 4, 2, 1, 0), 0))
+            pieces.plan.append((base + 2, lane + 2, (4, 4, 2, 0, 0), 0))
+            pieces.plan.append((base + 3, lane + 2, (2, 4, 0, 1, 0), 0))
+            pieces.plan.append((base + 4, lane + 2, (2, 4, 0, 3, 0), 0))
         (far_z,) = yield [(own, PZ2)]
         pair = jnp.concatenate([own, far_z], 0)
         (near_z,) = yield [(pair, PZ1)]
@@ -137,8 +137,7 @@
             name = 20 + n
             pieces.bufs[name] = buf
             for x in range(2):
-                places = tuple(4 * far + near + y for far in range(2) for y in range(2))
-                pieces.plan.append((name, 2 * x + core, (x, places), first_col))
+                pieces.plan.append((name, 2 * x + core, (4, 1, 4, near, 2), first_col + x))
 
     @staticmethod
     def slot(block, dp):
@@ -184,7 +183,7 @@
 
     @staticmethod
     def sum_max(both, is_top):
-        for perm in (PC, PX, PY, PZ1, PZ2):
+        for perm in (PC, PZ1, PZ2, PX, PY):
             (other,) = yield [(both, perm)]
             both = jnp.where(is_top, jnp.maximum(both, other), both + other)
         return both
@@ -393,16 +392,20 @@
     for buf, lane, places, col in plan:
         src = bufs[buf]
         _, rows, width = src.shape
+        x, col = (col & 1, col - (col & 1))
         cols = pl.ds(col, width)
         if places is None:
             dst[lane, :, cols] = src[0]
             continue
-        index = list(range(len(places)))
-        if isinstance(places[1], tuple):
-            x, places = places
-            index = [4 * (n // 2) + 2 * x + n % 2 for n in range(len(places))]
-        for n, place in zip(index, places):
-            dst[lane, pl.ds(pl.multiple_of((dp ^ place) * rows, rows), rows), cols] = src[n]
+        count, a, b, c, skip = places
+
+        def move(i, carry):
+            place = a * (i & 1) + b * (i >> 1) + c
+            at = pl.multiple_of((dp ^ place) * rows, rows)
+            dst[lane, pl.ds(at, rows), cols] = src[i + skip * ((i >> 1) + x)]
+            return carry
+
+        lax.fori_loop(0, count, move, 0)
 
 
 def row(vec):
@@ -522,17 +525,21 @@
     top_hid[...] = jnp.zeros_like(top_hid)
     inv_limit = 1.0 / jnp.full((1, 1), lim[3], f32)
 
-    def each(lane, carry):
-        up = mm(mid_low[...], weight[lane]) + bias[first + lane, :, low_q:]
+    rows = mid_low.shape[0] // 2
+
+    def each(n, carry):
+        lane = n // 2
+        part = pl.ds(pl.multiple_of((n % 2) * rows, rows), rows)
+        up = mm(mid_low[part, :], weight[lane]) + bias[first + lane, :, low_q:]
         half = 0.5 * (1.0 + lax.erf(up * root_half))
         hidden = up * half
         top_hid[...] = jnp.maximum(top_hid[...], jnp.max(jnp.abs(hidden).reshape(-1, 8, hidden.shape[1]), axis=0))
         bent = jnp.tanh(hidden * inv_limit)
-        act_out[lane] = (lim[3] * bent).astype(bf16)
-        slope_out[lane] = (1.0 - bent * bent) * (half + up * jnp.exp(-0.5 * up * up) * density_scale)
+        act_out[lane, part] = (lim[3] * bent).astype(bf16)
+        slope_out[lane, part] = (1.0 - bent * bent) * (half + up * jnp.exp(-0.5 * up * up) * density_scale)
         return carry
 
-    lax.fori_loop(0, weight.shape[0], each, 0)
+    lax.fori_loop(0, 2 * weight.shape[0], each, 0)
     top_out[...] = jnp.broadcast_to(top_of(top_hid[...]), top_out.shape)
 
 
@@ -585,10 +592,7 @@
                 out[x, net.slot(block, dp)] = grad[block * rows : (block + 1) * rows]
 
 
-def mid_backward(dims, grad_up, grad_second, mid_slope, normed, inv, gain, ctx_slope, weight0, weight1, out_weight, *outs):
-    blocks, cols, width = dims
-    grad_out, attn_t, grad_ctx, sums, acc, attn_low = outs
-    at = 3 * cols - HEAD_DIM
+def mid_backward(grad_up, grad_second, mid_slope, normed, inv, gain, weight0, weight1, grad_out, attn_low, attn_t, sums, acc):
     acc[...] = jnp.zeros_like(acc)
     half = weight0.shape[0]
     for weight, first in ((weight0, 0), (weight1, half)):
@@ -608,30 +612,21 @@
     sums[1:2, :] = col_sum(incoming * normed[...])
     sums[2:3, :] = col_sum(incoming)
 
-    def spread(lane, carry):
-        grad_ctx[lane] = (mm(attn_low[...], out_weight[lane, :, at:]) * ctx_slope[lane]).astype(bf16)
-        return carry
-
-    lax.fori_loop(0, blocks, spread, 0)
-
-
-def attn_backward(net, dims, longs, shorts, qkv, lse, grad_ctx, in_t, attn_t, ctx_low, *rest):
+
+def heads_backward(first, dims, lane_me, qkv, lse, attn_low, weight, ctx_slope, mask, grad_ctx, out, sums):
     blocks, cols, width = dims
-    up_sums, sums_a, sums_b, tops_a, tops_m, top0, top1, out, far, near, packed, sums, mask = rest
     heads = cols // HEAD_DIM
-    rows = in_t.shape[0] // net.parts
-    start = 3 * cols - HEAD_DIM
-    end = 3 * cols + HEAD_DIM
-    fill_mask(mask, longs, shorts)
-    dp, lane_me = net.me()
-
-    def each(lane, carry):
+
+    def each(i, carry):
+        lane = first + i
+        part = mm(attn_low[...], weight[lane, :, 3 * cols - HEAD_DIM :])
+        grad_ctx[...] = (part * ctx_slope[lane]).astype(bf16)
         for h in range(heads):
             at = h * HEAD_DIM
             q = qkv[lane, :, at : at + HEAD_DIM]
             k = qkv[lane, :, cols + at : cols + at + HEAD_DIM]
             v = qkv[lane, :, 2 * cols + at : 2 * cols + at + HEAD_DIM]
-            grad = grad_ctx[lane, :, HEAD_DIM + at : 2 * HEAD_DIM + at]
+            grad = grad_ctx[:, HEAD_DIM + at : 2 * HEAD_DIM + at]
             shares = jnp.exp(mm_nt(k, q) * score_scale + mask[...] - lse[lane, h : h + 1, :])
             grad_shares = mm_nt(v, grad)
             inner = jnp.sum(shares * grad_shares, axis=0, keepdims=True)
@@ -639,29 +634,66 @@
             grad_v = mm(shares.astype(bf16), grad)
             grad_k = mm(grad_scores, q) * score_scale
             grad_q = (mm_tn(k, grad_scores) * score_scale).T
-            out[lane, :, at : at + HEAD_DIM] = grad_q.astype(bf16)
-            out[lane, :, cols + at : cols + at + HEAD_DIM] = grad_k.astype(bf16)
-            out[lane, :, 2 * cols + at : 2 * cols + at + HEAD_DIM] = grad_v.astype(bf16)
-        out[lane, :, 3 * cols :] = jnp.zeros((out.shape[1], HEAD_DIM), bf16)
-        sums[lane ^ lane_me] = col_sum(out[lane].astype(f32))
+            out[i, :, at : at + HEAD_DIM] = grad_q.astype(bf16)
+            out[i, :, cols + at : cols + at + HEAD_DIM] = grad_k.astype(bf16)
+            out[i, :, 2 * cols + at : 2 * cols + at + HEAD_DIM] = grad_v.astype(bf16)
+        out[i, :, 3 * cols :] = jnp.zeros((out.shape[1], HEAD_DIM), bf16)
+        sums[lane ^ lane_me] = col_sum(out[i].astype(f32))
         return carry
 
-    lax.fori_loop(0, blocks, each, 0)
-
-    def weights(x, carry):
-        for core, to in ((1, far), (0, near)):
-            left = mm(in_t[...], out[2 * x + core])
+    lax.fori_loop(0, out.shape[0], each, 0)
+
+
+def attn_backward(net, first, dims, longs, shorts, qkv, lse, attn_low, weight, ctx_slope, out, sums, mask, grad_ctx):
+    fill_mask(mask, longs, shorts)
+    sums[...] = jnp.zeros_like(sums)
+    heads_backward(first, dims, net.me()[1], qkv, lse, attn_low, weight, ctx_slope, mask, grad_ctx, out, sums)
+
+
+def attn_backward_last(net, dims, longs, shorts, lim, qkv, lse, attn_low, weight, ctx_slope, *rest):
+    blocks, cols, width = dims
+    in_t, attn_t, ctx_low, grad_first, tokens, more_out, more, *rest = rest
+    up_sums, sums_a, sums_b, tops_a, tops_m, top0, top1, *rest = rest
+    far, near, packed, tokens_out, out, sums, mask, grad_ctx, acc = rest
+    rows = in_t.shape[0] // net.parts
+    half = far.shape[0]
+    wide = 3 * cols + HEAD_DIM
+    start = 3 * cols - HEAD_DIM
+    dp, lane_me = net.me()
+    fill_mask(mask, longs, shorts)
+    sums[...] = more[...]
+    heads_backward(0, dims, lane_me, qkv, lse, attn_low, weight, ctx_slope, mask, grad_ctx, out, sums)
+    for x, grads in enumerate((out, more_out)):
+
+        def weights(core, carry):
+            left = mm(in_t[...], grads[core])
             right = mm(attn_t[...], ctx_low[2 * x + core])
-            mixed = (left[:, start:] + right[:, : end - start]).astype(bf16)
-            for block in range(net.parts):
-                rs = slice(block * rows, (block + 1) * rows)
-                place = net.slot(block, dp)
-                to[x, place, :, :start] = left[rs, :start].astype(bf16)
-                to[x, place, :, start:end] = mixed[rs]
-                to[x, place, :, end:] = right[rs, end - start :].astype(bf16)
-        return carry
-
-    lax.fori_loop(0, far.shape[0], weights, 0)
+            mixed = (left[:, start:] + right[:, : wide - start]).astype(bf16)
+            left, right = left[:, :start].astype(bf16), right[:, wide - start :].astype(bf16)
+            for to, wanted in ((near, 0), (far, 1)):
+
+                @pl.when(core == wanted)
+                def _():
+                    for block in range(net.parts):
+                        rs = slice(block * rows, (block + 1) * rows)
+                        place = net.slot(block, dp)
+                        to[x, place, :, :start] = left[rs]
+                        to[x, place, :, start:wide] = mixed[rs]
+                        to[x, place, :, wide:] = right[rs]
+
+            return carry
+
+        lax.fori_loop(0, 2, weights, 0)
+    acc[...] = jnp.zeros_like(acc)
+    for grads, first in ((out, 0), (more_out, half)):
+
+        def back(i, carry):
+            acc[...] += mm_nt(grads[i], weight[first + i, :, :wide])
+            return carry
+
+        lax.fori_loop(0, half, back, 0)
+    inputs = tokens[...].astype(f32)
+    tokens_out[...] = (grad_first[...] + jnp.where(jnp.abs(inputs) <= lim[0], acc[...], 0.0)).astype(bf16)
     packed[...] = jnp.zeros_like(packed)
     for j in range(blocks):
         packed[j : j + 1, :] = up_sums[j]
@@ -671,19 +703,6 @@
     tops = (tops_a[0:1, :], tops_a[1:2, :], tops_m[0:1, :], jnp.maximum(top0[0:1, :], top1[0:1, :]))
     for j, top in enumerate(tops):
         packed[2 * blocks + 6 : 2 * blocks + 7, 128 * j : 128 * j + 128] = top
-
-
-def token_backward(dims, lim, grad_qkv, grad_first, tokens, weight, out, acc):
-    blocks, cols, width = dims
-    acc[...] = jnp.zeros_like(acc)
-
-    def each(lane, carry):
-        acc[...] += mm_nt(grad_qkv[lane], weight[lane, :, : 3 * cols + HEAD_DIM])
-        return carry
-
-    lax.fori_loop(0, blocks, each, 0)
-    inputs = tokens[...].astype(f32)
-    out[...] = (grad_first[...] + jnp.where(jnp.abs(inputs) <= lim[0], acc[...], 0.0)).astype(bf16)
 
 
 def make_body(net):
@@ -720,6 +739,7 @@
 
         pieces_a, pieces_u, pieces_d = Pieces([]), Pieces([]), Pieces([])
         shard_a = attn_shard(qkv_weight, out_weight)
+        shard_a, up_bias, down_weight = tie(shard_a, up_bias, down_weight)
         job_a = Job(net.gather(shard_a, pieces_a))
         bias_row = jnp.concatenate(
             [qv_bias[0], jnp.zeros((cols,), f32), qv_bias[1], jnp.zeros((HEAD_DIM,), f32), up_bias]
@@ -860,37 +880,52 @@
                 finish,
             )
 
-        sum_u = Job(net.scatter_sum(*grad_of("up_grad", mid_t, (grad_up,))))
-        sum_d = Job(net.scatter_z_first(*grad_of("down_grad", ffn_t, (act0, act1), [sum_u], [sum_u])))
-        grad_first, attn_t, grad_ctx, sums_a = step(
-            (grad_up, grad_second, mid_slope, normed, inv, first_gain, ctx_slope, weight_u0, weight_u1, weight_a),
+        sum_d = Job(net.scatter_z_first(*grad_of("down_grad", ffn_t, (act0, act1))))
+        sum_u = Job(net.scatter_sum(*grad_of("up_grad", mid_t, (grad_up,), [sum_d], [sum_d])))
+        grad_first, attn_low, attn_t, sums_a = step(
+            (grad_up, grad_second, mid_slope, normed, inv, first_gain, weight_u0, weight_u1),
             call(
-                functools.partial(mid_backward, dims),
+                mid_backward,
                 "mid_backward",
-                [VM] * 10,
-                [
-                    like((rows, width)),
-                    like((width, rows), bf16),
-                    like((blocks, rows, out_cols), bf16),
-                    like((8, width)),
-                ],
-                [vmem(rows, width), vmem(rows, width, dtype=bf16)],
+                [VM] * 8,
+                [like((rows, width)), like((rows, width), bf16), like((width, rows), bf16), like((8, width))],
+                [vmem(rows, width)],
                 unit + unit // 3,
                 3 * moved,
             ),
-            [sum_d, sum_u],
-            [sum_d, sum_u],
+            [sum_u, sum_d],
+            [sum_u],
         )
-
-        grad_qkv, far, near, packed = step(
-            (long_lengths, short_lengths, qkv, lse, grad_ctx, in_t, attn_t, ctx_low)
+        grads_1, more = step(
+            (long_lengths, short_lengths, qkv, lse, attn_low, weight_a, ctx_slope),
+            call(
+                functools.partial(attn_backward, net, half, dims),
+                "attn_backward",
+                [SM] * 2 + [VM] * 5,
+                [like((half, rows, wide), bf16), like((blocks, 1, wide))],
+                [vmem(rows, rows), vmem(rows, out_cols, dtype=bf16)],
+                2 * unit,
+                2 * moved,
+            ),
+            [sum_u],
+            [sum_u, sum_d],
+        )
+        far, near, packed, tokens_grad = step(
+            (long_lengths, short_lengths, act_ranges, qkv, lse, attn_low, weight_a, ctx_slope)
+            + (in_t, attn_t, ctx_low, grad_first, tokens, grads_1, more)
             + (up_sums, sums_a, sums_b, tops_a, tops_m, top0, top1),
             call(
-                functools.partial(attn_backward, net, dims),
-                "attn_backward",
-                [SM] * 2 + [VM] * 13,
-                [like((blocks, rows, wide), bf16), both_shape, both_shape, like((16, width))],
-                [vmem(blocks, 1, wide), vmem(rows, rows)],
+                functools.partial(attn_backward_last, net, dims),
+                "attn_backward_last",
+                [SM] * 3 + [VM] * 19,
+                [both_shape, both_shape, like((16, width)), like((rows, width), bf16)],
+                [
+                    vmem(half, rows, wide, dtype=bf16),
+                    vmem(blocks, 1, wide),
+                    vmem(rows, rows),
+                    vmem(rows, out_cols, dtype=bf16),
+                    vmem(rows, width),
+                ],
                 4 * unit,
                 2 * moved,
             ),
@@ -901,26 +936,13 @@
         is_top = (jnp.arange(packed.shape[0]) == 2 * blocks + 6)[:, None]
         sum_s = Job(net.sum_max(packed, is_top))
         line_u = Job(net.scatter_line(*sum_u.value))
-        step((), None, [sum_a, sum_d, sum_s], [sum_a, sum_s])
-        tokens_grad = step(
-            (act_ranges, grad_qkv, grad_first, tokens, weight_a),
-            call(
-                functools.partial(token_backward, dims),
-                "token_backward",
-                [SM] + [VM] * 4,
-                [like((rows, width), bf16)],
-                [vmem(rows, width)],
-                unit,
-                2 * moved,
-            ),
-            [sum_a, line_u, sum_s],
-            [sum_a, sum_d, sum_s],
-        )[0]
-        step((), None, [sum_a, sum_s], [line_u])
-        step((), None, [line_u], [sum_a, sum_s])
+        step((), None, [sum_a, sum_d, line_u, sum_s], [sum_a, sum_s])
+        step((), None, [sum_a], [sum_a, sum_d, line_u])
+        step((), None, [sum_a, sum_d, line_u, sum_s], [sum_a, sum_d, line_u, sum_s])
         line_a = Job(net.scatter_line(*sum_a.value))
-        step((), None, [line_a, sum_d, sum_s], [line_a, sum_d, line_u, sum_s])
-        step((), None, [line_a, sum_d, sum_s], [line_a, sum_d, sum_s])
+        step((), None, [line_a, sum_s], [line_a, sum_s])
+        step((), None, [line_a, sum_s], [sum_s])
+        step((), None, [sum_s], [line_a, sum_s])
 
         packed = sum_s.value
         down_grad, up_grad = (kept + last.astype(f32) for kept, last in (sum_d.value, line_u.value))

time: 223 us -> 219 us (0.982)
  waiting for transfers between devices: 67.1 us -> 75 us
  starting transfers between devices: 65.2 us -> 59.3 us
  other arithmetic: 8.61 us -> 5.33 us
    ppermute x69, waiting for transfers between devices: 67.1 us -> 75 us  [step(): lax.ppermute(v, ALL, perm)]
    ppermute x69, starting transfers between devices: 65.2 us -> 59.3 us  [step(): lax.ppermute(v, ALL, perm)]
    pallas_call x14, Pallas kernels: 7.71 us -> 3.46 us  [glue(): return call(kernel, kernel.__name__, [VM] * len(ins), outs)(*ins)]
    pallas_call x10, Pallas kernels: 62.9 us -> 65.6 us  [step(): outs = run(*ins) if run else ins]
    unnamed x54 -> x46, local copies, waits for them, and re-layouts: 6.24 us -> 5.77 us
  transfers between devices with their start and end apart: 69 -> 69, of which waited for: 24 -> 30; matrix products, arithmetic and copies ran while one was open for 2% -> 1% of each run, Pallas kernels for 25% -> 25%
where the time goes in v8:
time: 219 us
  waiting for transfers between devices  75 us (34%)
  Pallas kernels  69.1 us (32%)
  starting transfers between devices  59.3 us (27%)
  local copies, waits for them, and re-layouts  8.27 us (4%)
  other arithmetic  5.33 us (2%)
    ppermute x69, waiting for transfers between devices, step(): lax.ppermute(v, ALL, perm)  75 us
    pallas_call x10, Pallas kernels, step(): outs = run(*ins) if run else ins  65.6 us
    ppermute x69, starting transfers between devices, step(): lax.ppermute(v, ALL, perm)  59.3 us
    unnamed x46, local copies, waits for them, and re-layouts  5.77 us
  transfers between devices with their start and end apart: 69, of which 30 were waited for; matrix products, arithmetic and copies ran while one was open for 1% of the time, Pallas kernels for 25%

profile of v8, /device:TPU:0, one launch (start us, length us, event | category | flops | bytes accessed | tf_op | source)
XLA Modules:
  0.0 218.9 jit_solution(682277835077779119)
XLA Ops:
  5.2 4.1 %collective-permute-start = (bf16[1,96,768]{2,1,0:T(8,128)(2,1)S(1)}, bf16[1,96,768]{2,1,0:T(8,128)(2,1)S(1)}, u32[]{:S(2)}, u32[]{:S(2)}) collective-permute-start(bf16[1,96,768]{2,1,0:T(8,128)(2,1)S(1)} %bitcast.24), channel_id=1, source_target_pairs={{0,16},{1,17},{2,18},{3,19},{4,20},{5,21},{6,22},{7,23},{8,24},{9,... | collective-permute-start | bytes 442376 | tf_op jit(solution)/shard_map/ppermute | solution.py:78
  9.3 1.5 collective-permute-start.1
  10.8 1.5 collective-permute-start.2
  12.9 3.1 %collective-permute-done.3 = f32[1,1408]{1,0:T(1,128)S(1)} collective-permute-done((f32[1,1408]{1,0:T(1,128)S(1)}, f32[1,1408]{1,0:T(1,128)S(1)}, u32[]{:S(2)}, u32[]{:S(2)}) %collective-permute-start.3) | collective-permute-done | bytes 5664 | tf_op jit(solution)/shard_map/ppermute | solution.py:78
  16.4 1.3 collective-permute-start.4
  19.8 2.2 collective-permute-done.5
  22.0 2.6 %collective-permute-done.4 = bf16[2,96,768]{2,1,0:T(8,128)(2,1)S(1)} collective-permute-done((bf16[2,96,768]{2,1,0:T(8,128)(2,1)S(1)}, bf16[2,96,768]{2,1,0:T(8,128)(2,1)S(1)}, u32[]{:S(2)}, u32[]{:S(2)}) %collective-permute-start.4) | collective-permute-done | bytes 294944 | tf_op jit(solution)/shard_map/ppermute | solution.py:78
  24.7 1.3 collective-permute-start.7
  26.1 1.5 collective-permute-start.8
  27.6 3.3 %collective-permute-start.10 = (bf16[1,96,768]{2,1,0:T(8,128)(2,1)S(1)}, bf16[1,96,768]{2,1,0:T(8,128)(2,1)S(1)}, u32[]{:S(2)}, u32[]{:S(2)}) collective-permute-start(bf16[1,96,768]{2,1,0:T(8,128)(2,1)S(1)} %convert_bitcast_fusion), channel_id=1, source_target_pairs={{0,16},{1,17},{2,18},{3,19},{4,20},{5,21},{6,22},{7,23},{8,24},{9,... | collective-permute-start | bytes 442376 | tf_op jit(solution)/shard_map/ppermute | solution.py:78
  31.6 10.2 %collective-permute-done.11 = bf16[1,96,384]{2,1,0:T(8,128)(2,1)S(1)} collective-permute-done((bf16[1,96,384]{2,1,0:T(8,128)(2,1)S(1)}, bf16[1,96,384]{2,1,0:T(8,128)(2,1)S(1)}, u32[]{:S(2)}, u32[]{:S(2)}) %collective-permute-start.11) | collective-permute-done | bytes 73760 | tf_op jit(solution)/shard_map/ppermute | solution.py:78
  44.8 6.8 %collective-permute-done.12.rest_3_ = bf16[2,96,768]{2,1,0:T(8,128)(2,1)S(1)} collective-permute-done((bf16[2,96,768]{2,1,0:T(8,128)(2,1)S(1)}, bf16[2,96,768]{2,1,0:T(8,128)(2,1)S(1)}, u32[]{:S(2)}, u32[]{:S(2)}) %collective-permute-start.12) | collective-permute-done | bytes 294944 | tf_op jit(solution)/shard_map/ppermute | solution.py:78
  52.7 1.6 collective-permute-start.19
  54.3 1.5 collective-permute-start.20
  55.8 2.4 %collective-permute-start.23 = (bf16[4,96,384]{2,1,0:T(8,128)(2,1)S(1)}, bf16[4,96,384]{2,1,0:T(8,128)(2,1)S(1)}, u32[]{:S(2)}, u32[]{:S(2)}) collective-permute-start(bf16[4,96,384]{2,1,0:T(8,128)(2,1)S(1)} %pad_maximum_fusion.4), channel_id=1, source_target_pairs={{0,16},{1,17},{2,18},{3,19},{4,20},{5,21},{6,22},{7,23},{8,24},{9,... | collective-permute-start | bytes 884744 | tf_op jit(solution)/shard_map/ppermute | solution.py:78
  58.2 1.7 collective-permute-start.22
  60.0 11.5 %attn_forward.1 = (bf16[4,512,640]{2,1,0:T(8,128)(2,1)S(1)}, f32[4,8,512]{2,1,0:T(8,128)S(1)}, bf16[768,512]{1,0:T(8,128)(2,1)S(1)}, bf16[4,512,256]{2,1,0:T(8,1...) custom-call(f32[4]{0:T(128)S(1)} %copy-done.11, ...), custom_call_target="tpu_custom_call" | custom-call | flops 9663676416 | bytes 14155776 | tf_op jit(solution)/shard_map/attn_forward/pallas_call | solution.py:79
  71.5 1.5 copy-done.13
  73.0 1.4 copy-done.15
  78.1 3.3 %attn_finish.1 = (f32[512,768]{1,0:T(8,128)S(1)}, f32[512,1]{1,0:T(8,128)S(1)}, f32[512,768]{1,0:T(8,128)S(1)}, f32[512,768]{1,0:T(8,128)S(1)}, bf16[512,768]{1,...) custom-call(f32[4]{0:T(128)S(1)} %copy-done.11, ...), custom_call_target="tpu_custom_call" | custom-call | flops 4831838208 | bytes 9437184 | tf_op jit(solution)/shard_map/attn_finish/pallas_call | solution.py:79
  81.3 3.7 %collective-permute-done.24.rest_1_ = bf16[2,96,768]{2,1,0:T(8,128)(2,1)S(1)} collective-permute-done((bf16[2,96,768]{2,1,0:T(8,128)(2,1)S(1)}, bf16[2,96,768]{2,1,0:T(8,128)(2,1)S(1)}, u32[]{:S(2)}, u32[]{:S(2)}) %collective-permute-start.24) | collective-permute-done | bytes 294944 | tf_op jit(solution)/shard_map/ppermute | solution.py:78
  85.8 1.5 collective-permute-start.30
  88.2 4.2 %up_forward_0.1 = (bf16[2,512,768]{2,1,0:T(8,128)(2,1)S(1)}, f32[2,512,768]{2,1,0:T(8,128)S(1)}, f32[8,128]{1,0:T(8,128)S(1)}, bf16[2,768,768]{2,1,0:T(8,128)(2,1)S(1)}) custom-call(f32[4]{0:T(128)S(1)} %copy-done.11, bf16[512,768]{1,0:T(8,128)(2,1)S(1)} %get-tuple-element.472.mid_low, f32[4,1,1408]{2,1,0:T(1,128)S(1)} %bitcast.28, ...), custom_call_target="tpu_custom_call" | custom-call | flops 4831838208 | bytes 9437184 | tf_op jit(solution)/shard_map/up_forward_0/pallas_call | solution.py:79
  92.5 4.2 %up_forward_2.1 = (bf16[2,512,768]{2,1,0:T(8,128)(2,1)S(1)}, f32[2,512,768]{2,1,0:T(8,128)S(1)}, f32[8,128]{1,0:T(8,128)S(1)}, bf16[2,768,768]{2,1,0:T(8,128)(2,1)S(1)}) custom-call(f32[4]{0:T(128)S(1)} %copy-done.11, bf16[512,768]{1,0:T(8,128)(2,1)S(1)} %get-tuple-element.472.mid_low, f32[4,1,1408]{2,1,0:T(1,128)S(1)} %bitcast.29, ...), custom_call_target="tpu_custom_call" | custom-call | flops 4831838208 | bytes 9437184 | tf_op jit(solution)/shard_map/up_forward_2/pallas_call | solution.py:79
  99.1 4.5 %collective-permute-done.34.rest_3_ = bf16[2,96,384]{2,1,0:T(8,128)(2,1)S(1)} collective-permute-done((bf16[2,96,384]{2,1,0:T(8,128)(2,1)S(1)}, bf16[2,96,384]{2,1,0:T(8,128)(2,1)S(1)}, u32[]{:S(2)}, u32[]{:S(2)}) %collective-permute-start.34) | collective-permute-done | bytes 147488 | tf_op jit(solution)/shard_map/ppermute | solution.py:78
  104.9 2.0 collective-permute-done.38.rest_8_
  107.2 9.1 %down_both.1 = (bf16[512,768]{1,0:T(8,128)(2,1)}, f32[512,768]{1,0:T(8,128)S(1)}, bf16[768,512]{1,0:T(8,128)(2,1)S(1)}, f32[8,768]{1,0:T(8,128)S(1)}, bf16[4,512...) custom-call(bf16[2,512,768]{2,1,0:T(8,128)(2,1)S(1)} %get-tuple-element.548.act0.rest_0_, ...), custom_call_target="tpu_custom_call" | custom-call | flops 4831838208 | bytes 18874368 | tf_op jit(solution)/shard_map/down_both/pallas_call | solution.py:79
  116.3 2.7 %down_grad.1 = (bf16[2,8,96,768]{3,2,1,0:T(8,128)(2,1)S(1)}, bf16[2,8,96,768]{3,2,1,0:T(8,128)(2,1)S(1)}) custom-call(bf16[768,512]{1,0:T(8,128)(2,1)S(1)} %get-tuple-element.547.left_t, bf16[2,512,768]{2,1,0:T(8,128)(2,1)S(1)} %get-tuple-element.548.act0.rest_0_, bf16[2,512,768]{2,1,0:T(8,128)(2,1)S(1)} %get-tuple-element.549.act1.rest_1_), custom_call_target="tpu_custom_call" | custom-call | flops 2415919104 | bytes 4718592 | tf_op jit(solution)/shard_map/down_grad/pallas_call | solution.py:79
  119.2 2.7 %up_grad.1 = (bf16[2,8,96,768]{3,2,1,0:T(8,128)(2,1)S(1)}, bf16[2,8,96,768]{3,2,1,0:T(8,128)(2,1)S(1)}) custom-call(bf16[768,512]{1,0:T(8,128)(2,1)S(1)} %get-tuple-element.551.left_t, bf16[4,512,768]{2,1,0:T(8,128)(2,1)S(1)} %get-tuple-element.560.rest_0_.grad_up), custom_call_target="tpu_custom_call" | custom-call | flops 2415919104 | bytes 4718592 | tf_op jit(solution)/shard_map/up_grad/pallas_call | solution.py:79
  121.9 1.7 collective-permute-done.42.got
  124.6 4.6 %mid_backward.1 = (f32[512,768]{1,0:T(8,128)S(1)}, bf16[512,768]{1,0:T(8,128)(2,1)S(1)}, bf16[768,512]{1,0:T(8,128)(2,1)S(1)}, f32[8,768]{1,0:T(8,128)S(1)}) custom-call(bf16[4,512,768]{2,1,0:T(8,128)(2,1)S(1)} %get-tuple-element.560.rest_0_.grad_up, f32[512,768]{1,0:T(8,128)S(1)} %get-tuple-element.561.grad_second, ...), custom_call_target="tpu_custom_call" | custom-call | flops 3221225472 | bytes 14155776 | tf_op jit(solution)/shard_map/mid_backward/pallas_call | solution.py:79
  129.4 1.6 collective-permute-start.44
  131.9 7.0 %attn_backward.1 = (bf16[2,512,640]{2,1,0:T(8,128)(2,1)S(1)}, f32[4,1,640]{2,1,0:T(1,128)S(1)}) custom-call(s32[1]{0:T(128)S(6)} %copy.37.longs, s32[12]{0:T(128)S(1)} %copy-done.10, bf16[4,512,640]{2,1,0:T(8,128)(2,1)S(1)} %copy-done.14, f32[4,8,512]{2,1,0:T(8,128)S(1)} %get-tuple-element.615.lse, bf16[512,768]{1,0:T(8,128)(2,1)S(1)} %get-tuple-element.616.attn_low, ...), custom_call_target="tpu_custom_call" | custom-call | flops 4831838208 | bytes 9437184 | tf_op jit(solution)/shard_map/attn_backward/pallas_call | solution.py:79
  140.2 1.5 collective-permute-start.47
  143.4 1.5 collective-permute-start.49
  145.8 16.4 %attn_backward_last.1 = (bf16[2,8,96,768]{3,2,1,0:T(8,128)(2,1)S(1)}, bf16[2,8,96,768]{3,2,1,0:T(8,128)(2,1)S(1)}, f32[16,768]{1,0:T(8,128)S(1)}, bf16[512,768]{1,0:T(8,128)(2,1)}) custom-call(s32[1]{0:T(128)S(6)} %copy.37.longs, s32[12]{0:T(128)S(1)} %copy-done.10, f32[4]{0:T(128)S(1)} %copy-done.11, bf16[4,512,640]{2,1,0:T(8,128)(2,1)S(1)} %copy-done.14, ...), custom_call_target="tpu_custom_call" | custom-call | flops 9663676416 | bytes 9437184 | tf_op jit(solution)/shard_map/attn_backward_last/pallas_call | solution.py:79
  165.0 1.5 collective-permute-start.58
  169.4 3.8 %collective-permute-done.56.in_x = bf16[2,96,768]{2,1,0:T(8,128)(2,1)S(1)} collective-permute-done((bf16[2,96,768]{2,1,0:T(8,128)(2,1)S(1)}, bf16[2,96,768]{2,1,0:T(8,128)(2,1)S(1)}, u32[]{:S(2)}, u32[]{:S(2)}) %collective-permute-start.56) | collective-permute-done | bytes 294944 | tf_op jit(solution)/shard_map/ppermute | solution.py:78
  173.8 4.9 %collective-permute-done.54.from_x = bf16[2,96,768]{2,1,0:T(8,128)(2,1)S(1)} collective-permute-done((bf16[2,96,768]{2,1,0:T(8,128)(2,1)S(1)}, bf16[2,96,768]{2,1,0:T(8,128)(2,1)S(1)}, u32[]{:S(2)}, u32[]{:S(2)}) %collective-permute-start.54) | collective-permute-done | bytes 294944 | tf_op jit(solution)/shard_map/ppermute | solution.py:78
  179.6 1.5 collective-permute-start.59
  182.4 2.8 %collective-permute-start.62 = (bf16[96,768]{1,0:T(8,128)(2,1)S(1)}, bf16[96,768]{1,0:T(8,128)(2,1)S(1)}, u32[]{:S(2)}, u32[]{:S(2)}) collective-permute-start(bf16[96,768]{1,0:T(8,128)(2,1)S(1)} %get-tuple-element.676), channel_id=1, source_target_pairs={{0,16},{1,17},{2,18},{3,19},{4,20},{5,21},{6,22},{7,23},{8,24},{9,... | collective-permute-start | bytes 442376 | tf_op jit(solution)/shard_map/ppermute | solution.py:78
  185.7 3.7 %collective-permute-done.63 = f32[16,768]{1,0:T(8,128)S(1)} collective-permute-done((f32[16,768]{1,0:T(8,128)S(1)}, f32[16,768]{1,0:T(8,128)S(1)}, u32[]{:S(2)}, u32[]{:S(2)}) %collective-permute-start.63) | collective-permute-done | bytes 49184 | tf_op jit(solution)/shard_map/ppermute | solution.py:78
  189.4 4.3 %collective-permute-done.61 = bf16[96,768]{1,0:T(8,128)(2,1)S(1)} collective-permute-done((bf16[96,768]{1,0:T(8,128)(2,1)S(1)}, bf16[96,768]{1,0:T(8,128)(2,1)S(1)}, u32[]{:S(2)}, u32[]{:S(2)}) %collective-permute-start.61) | collective-permute-done | bytes 147488 | tf_op jit(solution)/shard_map/ppermute | solution.py:78
  193.7 3.1 %collective-permute-done.62 = bf16[96,768]{1,0:T(8,128)(2,1)S(1)} collective-permute-done((bf16[96,768]{1,0:T(8,128)(2,1)S(1)}, bf16[96,768]{1,0:T(8,128)(2,1)S(1)}, u32[]{:S(2)}, u32[]{:S(2)}) %collective-permute-start.62) | collective-permute-done | bytes 147488 | tf_op jit(solution)/shard_map/ppermute | solution.py:78
  198.1 6.8 %collective-permute-done.65 = f32[16,768]{1,0:T(8,128)S(1)} collective-permute-done((f32[16,768]{1,0:T(8,128)S(1)}, f32[16,768]{1,0:T(8,128)S(1)}, u32[]{:S(2)}, u32[]{:S(2)}) %collective-permute-start.65) | collective-permute-done | bytes 49184 | tf_op jit(solution)/shard_map/ppermute | solution.py:78
  205.0 2.2 %collective-permute-done.64.from_z = bf16[2,96,768]{2,1,0:T(8,128)(2,1)S(1)} collective-permute-done((bf16[2,96,768]{2,1,0:T(8,128)(2,1)S(1)}, bf16[2,96,768]{2,1,0:T(8,128)(2,1)S(1)}, u32[]{:S(2)}, u32[]{:S(2)}) %collective-permute-start.64) | collective-permute-done | bytes 294944 | tf_op jit(solution)/shard_map/ppermute | solution.py:78
  209.3 2.1 collective-permute-done.67
  213.1 2.5 %collective-permute-done.68 = f32[16,768]{1,0:T(8,128)S(1)} collective-permute-done((f32[16,768]{1,0:T(8,128)S(1)}, f32[16,768]{1,0:T(8,128)S(1)}, u32[]{:S(2)}, u32[]{:S(2)}) %collective-permute-start.68) | collective-permute-done | bytes 49184 | tf_op jit(solution)/shard_map/ppermute | solution.py:78
  (199 shorter events, 44.7 us)
Async XLA Ops:
  5.2 11.1 %collective-permute-start = (bf16[1,96,768]{2,1,0:T(8,128)(2,1)S(1)}, bf16[1,96,768]{2,1,0:T(8,128)(2,1)S(1)}, u32[]{:S(2)}, u32[]{:S(2)}) collective-permute-start(bf16[1,96,768]{2,1,0:T(8,128)(2,1)S(1)} %bitcast.24), channel_id=1, source_target_pairs={{0,16},{1,17},{2,18},{3,19},{4,20},{5,21},{6,22},{7,23},{8,24},{9,... | collective-permute-start | bytes 442376 | tf_op jit(solution)/shard_map/ppermute | solution.py:78
  9.3 6.6 %collective-permute-start.1 = (bf16[1,96,384]{2,1,0:T(8,128)(2,1)S(1)}, bf16[1,96,384]{2,1,0:T(8,128)(2,1)S(1)}, u32[]{:S(2)}, u32[]{:S(2)}) collective-permute-start(bf16[1,96,384]{2,1,0:T(8,128)(2,1)S(1)} %get-tuple-element.362), channel_id=1, source_target_pairs={{0,2},{1,3},{2,0},{3,1},{4,6},{5,7},{6,4},{7,5},{8,10},{9,11},{10,... | collective-permute-start | bytes 221192 | tf_op jit(solution)/shard_map/ppermute | solution.py:78
  16.4 8.2 %collective-permute-start.4 = (bf16[2,96,768]{2,1,0:T(8,128)(2,1)S(1)}, bf16[2,96,768]{2,1,0:T(8,128)(2,1)S(1)}, u32[]{:S(2)}, u32[]{:S(2)}) collective-permute-start(bf16[2,96,768]{2,1,0:T(8,128)(2,1)S(1)} %pad_maximum_fusion.2), channel_id=1, source_target_pairs={{0,8},{1,9},{2,10},{3,11},{4,12},{5,13},{6,14},{7,15},{8,0},{9,1},... | collective-permute-start | bytes 884744 | tf_op jit(solution)/shard_map/ppermute | solution.py:78
  24.7 17.0 %collective-permute-start.7 = (bf16[4,96,768]{2,1,0:T(8,128)(2,1)S(1)}, bf16[4,96,768]{2,1,0:T(8,128)(2,1)S(1)}, u32[]{:S(2)}, u32[]{:S(2)}) collective-permute-start(bf16[4,96,768]{2,1,0:T(8,128)(2,1)S(1)} %pad_maximum_fusion.rest_0_), channel_id=1, source_target_pairs={{0,2},{1,3},{2,0},{3,1},{4,6},{5,7},{6,4},{7,5},{8,10},{9,11},{10,... | collective-permute-start | bytes 1769480 | tf_op jit(solution)/shard_map/ppermute | solution.py:78
  26.1 15.7 %collective-permute-start.8 = (bf16[4,96,768]{2,1,0:T(8,128)(2,1)S(1)}, bf16[4,96,768]{2,1,0:T(8,128)(2,1)S(1)}, u32[]{:S(2)}, u32[]{:S(2)}) collective-permute-start(bf16[4,96,768]{2,1,0:T(8,128)(2,1)S(1)} %pad_maximum_fusion.rest_0_), channel_id=1, source_target_pairs={{0,4},{1,5},{2,6},{3,7},{4,0},{5,1},{6,2},{7,3},{8,12},{9,13},{10,... | collective-permute-start | bytes 1769480 | tf_op jit(solution)/shard_map/ppermute | solution.py:78
  27.6 14.2 %collective-permute-start.9 = (bf16[4,96,768]{2,1,0:T(8,128)(2,1)S(1)}, bf16[4,96,768]{2,1,0:T(8,128)(2,1)S(1)}, u32[]{:S(2)}, u32[]{:S(2)}) collective-permute-start(bf16[4,96,768]{2,1,0:T(8,128)(2,1)S(1)} %pad_maximum_fusion.rest_0_), channel_id=1, source_target_pairs={{0,1},{1,0},{2,3},{3,2},{4,5},{5,4},{6,7},{7,6},{8,9},{9,8},{10,11... | collective-permute-start | bytes 1769480 | tf_op jit(solution)/shard_map/ppermute | solution.py:78
  27.6 14.2 %collective-permute-start.10 = (bf16[1,96,768]{2,1,0:T(8,128)(2,1)S(1)}, bf16[1,96,768]{2,1,0:T(8,128)(2,1)S(1)}, u32[]{:S(2)}, u32[]{:S(2)}) collective-permute-start(bf16[1,96,768]{2,1,0:T(8,128)(2,1)S(1)} %convert_bitcast_fusion), channel_id=1, source_target_pairs={{0,16},{1,17},{2,18},{3,19},{4,20},{5,21},{6,22},{7,23},{8,24},{9,... | collective-permute-start | bytes 442376 | tf_op jit(solution)/shard_map/ppermute | solution.py:78
  30.9 10.8 %collective-permute-start.11 = (bf16[1,96,384]{2,1,0:T(8,128)(2,1)S(1)}, bf16[1,96,384]{2,1,0:T(8,128)(2,1)S(1)}, u32[]{:S(2)}, u32[]{:S(2)}) collective-permute-start(bf16[1,96,384]{2,1,0:T(8,128)(2,1)S(1)} %get-tuple-element.376), channel_id=1, source_target_pairs={{0,16},{1,17},{2,18},{3,19},{4,20},{5,21},{6,22},{7,23},{8,24},{9,... | collective-permute-start | bytes 221192 | tf_op jit(solution)/shard_map/ppermute | solution.py:78
  41.9 10.2 %collective-permute-start.14 = (bf16[4,96,768]{2,1,0:T(8,128)(2,1)S(1)}, bf16[4,96,768]{2,1,0:T(8,128)(2,1)S(1)}, u32[]{:S(2)}, u32[]{:S(2)}) collective-permute-start(bf16[4,96,768]{2,1,0:T(8,128)(2,1)S(1)} %collective-permute-done.8.rest_1_), channel_id=1, source_target_pairs={{0,1},{1,0},{2,3},{3,2},{4,5},{5,4},{6,7},{7,6},{8,9},{9,8},{10,11... | collective-permute-start | bytes 1769480 | tf_op jit(solution)/shard_map/ppermute | solution.py:78
  41.9 10.1 %collective-permute-start.15 = (bf16[4,96,768]{2,1,0:T(8,128)(2,1)S(1)}, bf16[4,96,768]{2,1,0:T(8,128)(2,1)S(1)}, u32[]{:S(2)}, u32[]{:S(2)}) collective-permute-start(bf16[4,96,768]{2,1,0:T(8,128)(2,1)S(1)} %collective-permute-done.7.rest_2_), channel_id=1, source_target_pairs={{0,1},{1,0},{2,3},{3,2},{4,5},{5,4},{6,7},{7,6},{8,9},{9,8},{10,11... | collective-permute-start | bytes 1769480 | tf_op jit(solution)/shard_map/ppermute | solution.py:78
  42.5 9.1 %collective-permute-start.12 = (bf16[2,96,768]{2,1,0:T(8,128)(2,1)S(1)}, bf16[2,96,768]{2,1,0:T(8,128)(2,1)S(1)}, u32[]{:S(2)}, u32[]{:S(2)}) collective-permute-start(bf16[2,96,768]{2,1,0:T(8,128)(2,1)S(1)} %slice.68), channel_id=1, source_target_pairs={{0,2},{1,3},{2,0},{3,1},{4,6},{5,7},{6,4},{7,5},{8,10},{9,11},{10,... | collective-permute-start | bytes 884744 | tf_op jit(solution)/shard_map/ppermute | solution.py:78
  43.1 8.7 %collective-permute-start.13 = (bf16[2,96,768]{2,1,0:T(8,128)(2,1)S(1)}, bf16[2,96,768]{2,1,0:T(8,128)(2,1)S(1)}, u32[]{:S(2)}, u32[]{:S(2)}) collective-permute-start(bf16[2,96,768]{2,1,0:T(8,128)(2,1)S(1)} %slice.69), channel_id=1, source_target_pairs={{0,4},{1,5},{2,6},{3,7},{4,0},{5,1},{6,2},{7,3},{8,12},{9,13},{10,... | collective-permute-start | bytes 884744 | tf_op jit(solution)/shard_map/ppermute | solution.py:78
  43.6 8.4 %collective-permute-start.16 = (bf16[2,96,768]{2,1,0:T(8,128)(2,1)S(1)}, bf16[2,96,768]{2,1,0:T(8,128)(2,1)S(1)}, u32[]{:S(2)}, u32[]{:S(2)}) collective-permute-start(bf16[2,96,768]{2,1,0:T(8,128)(2,1)S(1)} %pad_maximum_fusion.3), channel_id=1, source_target_pairs={{0,8},{1,9},{2,10},{3,11},{4,12},{5,13},{6,14},{7,15},{8,0},{9,1},... | collective-permute-start | bytes 884744 | tf_op jit(solution)/shard_map/ppermute | solution.py:78
  52.7 22.6 %collective-permute-start.19 = (bf16[4,96,768]{2,1,0:T(8,128)(2,1)S(1)}, bf16[4,96,768]{2,1,0:T(8,128)(2,1)S(1)}, u32[]{:S(2)}, u32[]{:S(2)}) collective-permute-start(bf16[4,96,768]{2,1,0:T(8,128)(2,1)S(1)} %pad_maximum_fusion.1.rest_0_), channel_id=1, source_target_pairs={{0,2},{1,3},{2,0},{3,1},{4,6},{5,7},{6,4},{7,5},{8,10},{9,11},{10,... | collective-permute-start | bytes 1769480 | tf_op jit(solution)/shard_map/ppermute | solution.py:78
  54.3 21.0 %collective-permute-start.20 = (bf16[4,96,768]{2,1,0:T(8,128)(2,1)S(1)}, bf16[4,96,768]{2,1,0:T(8,128)(2,1)S(1)}, u32[]{:S(2)}, u32[]{:S(2)}) collective-permute-start(bf16[4,96,768]{2,1,0:T(8,128)(2,1)S(1)} %pad_maximum_fusion.1.rest_0_), channel_id=1, source_target_pairs={{0,4},{1,5},{2,6},{3,7},{4,0},{5,1},{6,2},{7,3},{8,12},{9,13},{10,... | collective-permute-start | bytes 1769480 | tf_op jit(solution)/shard_map/ppermute | solution.py:78
  55.8 19.5 %collective-permute-start.21 = (bf16[4,96,768]{2,1,0:T(8,128)(2,1)S(1)}, bf16[4,96,768]{2,1,0:T(8,128)(2,1)S(1)}, u32[]{:S(2)}, u32[]{:S(2)}) collective-permute-start(bf16[4,96,768]{2,1,0:T(8,128)(2,1)S(1)} %pad_maximum_fusion.1.rest_0_), channel_id=1, source_target_pairs={{0,1},{1,0},{2,3},{3,2},{4,5},{5,4},{6,7},{7,6},{8,9},{9,8},{10,11... | collective-permute-start | bytes 1769480 | tf_op jit(solution)/shard_map/ppermute | solution.py:78
  55.8 19.5 %collective-permute-start.23 = (bf16[4,96,384]{2,1,0:T(8,128)(2,1)S(1)}, bf16[4,96,384]{2,1,0:T(8,128)(2,1)S(1)}, u32[]{:S(2)}, u32[]{:S(2)}) collective-permute-start(bf16[4,96,384]{2,1,0:T(8,128)(2,1)S(1)} %pad_maximum_fusion.4), channel_id=1, source_target_pairs={{0,16},{1,17},{2,18},{3,19},{4,20},{5,21},{6,22},{7,23},{8,24},{9,... | collective-permute-start | bytes 884744 | tf_op jit(solution)/shard_map/ppermute | solution.py:78
  58.2 17.0 %collective-permute-start.22 = (bf16[2,96,384]{2,1,0:T(8,128)(2,1)S(1)}, bf16[2,96,384]{2,1,0:T(8,128)(2,1)S(1)}, u32[]{:S(2)}, u32[]{:S(2)}) collective-permute-start(bf16[2,96,384]{2,1,0:T(8,128)(2,1)S(1)} %pad_maximum_fusion.6), channel_id=1, source_target_pairs={{0,8},{1,9},{2,10},{3,11},{4,12},{5,13},{6,14},{7,15},{8,0},{9,1},... | collective-permute-start | bytes 442376 | tf_op jit(solution)/shard_map/ppermute | solution.py:78
  75.5 9.8 %collective-permute-start.26 = (bf16[4,96,768]{2,1,0:T(8,128)(2,1)S(1)}, bf16[4,96,768]{2,1,0:T(8,128)(2,1)S(1)}, u32[]{:S(2)}, u32[]{:S(2)}) collective-permute-start(bf16[4,96,768]{2,1,0:T(8,128)(2,1)S(1)} %collective-permute-done.20.rest_1_), channel_id=1, source_target_pairs={{0,1},{1,0},{2,3},{3,2},{4,5},{5,4},{6,7},{7,6},{8,9},{9,8},{10,11... | collective-permute-start | bytes 1769480 | tf_op jit(solution)/shard_map/ppermute | solution.py:78
  75.6 9.8 %collective-permute-start.27 = (bf16[4,96,768]{2,1,0:T(8,128)(2,1)S(1)}, bf16[4,96,768]{2,1,0:T(8,128)(2,1)S(1)}, u32[]{:S(2)}, u32[]{:S(2)}) collective-permute-start(bf16[4,96,768]{2,1,0:T(8,128)(2,1)S(1)} %collective-permute-done.19.rest_0_), channel_id=1, source_target_pairs={{0,1},{1,0},{2,3},{3,2},{4,5},{5,4},{6,7},{7,6},{8,9},{9,8},{10,11... | collective-permute-start | bytes 1769480 | tf_op jit(solution)/shard_map/ppermute | solution.py:78
  76.1 9.0 %collective-permute-start.24 = (bf16[2,96,768]{2,1,0:T(8,128)(2,1)S(1)}, bf16[2,96,768]{2,1,0:T(8,128)(2,1)S(1)}, u32[]{:S(2)}, u32[]{:S(2)}) collective-permute-start(bf16[2,96,768]{2,1,0:T(8,128)(2,1)S(1)} %slice.70), channel_id=1, source_target_pairs={{0,2},{1,3},{2,0},{3,1},{4,6},{5,7},{6,4},{7,5},{8,10},{9,11},{10,... | collective-permute-start | bytes 884744 | tf_op jit(solution)/shard_map/ppermute | solution.py:78
  76.6 8.7 %collective-permute-start.25 = (bf16[2,96,768]{2,1,0:T(8,128)(2,1)S(1)}, bf16[2,96,768]{2,1,0:T(8,128)(2,1)S(1)}, u32[]{:S(2)}, u32[]{:S(2)}) collective-permute-start(bf16[2,96,768]{2,1,0:T(8,128)(2,1)S(1)} %slice.71), channel_id=1, source_target_pairs={{0,4},{1,5},{2,6},{3,7},{4,0},{5,1},{6,2},{7,3},{8,12},{9,13},{10,... | collective-permute-start | bytes 884744 | tf_op jit(solution)/shard_map/ppermute | solution.py:78
  77.5 19.2 %collective-permute-start.33 = (bf16[8,96,384]{2,1,0:T(8,128)(2,1)S(1)}, bf16[8,96,384]{2,1,0:T(8,128)(2,1)S(1)}, u32[]{:S(2)}, u32[]{:S(2)}) collective-permute-start(bf16[8,96,384]{2,1,0:T(8,128)(2,1)S(1)} %get-tuple-element.531.rest_10_), channel_id=1, source_target_pairs={{0,8},{1,9},{2,10},{3,11},{4,12},{5,13},{6,14},{7,15},{8,0},{9,1},... | collective-permute-start | bytes 1769480 | tf_op jit(solution)/shard_map/ppermute | solution.py:78
  85.3 7.1 %collective-permute-start.28 = (bf16[2,96,768]{2,1,0:T(8,128)(2,1)S(1)}, bf16[2,96,768]{2,1,0:T(8,128)(2,1)S(1)}, u32[]{:S(2)}, u32[]{:S(2)}) collective-permute-start(bf16[2,96,768]{2,1,0:T(8,128)(2,1)S(1)} %collective-permute-done.24.rest_1_), channel_id=1, source_target_pairs={{0,1},{1,0},{2,3},{3,2},{4,5},{5,4},{6,7},{7,6},{8,9},{9,8},{10,11... | collective-permute-start | bytes 884744 | tf_op jit(solution)/shard_map/ppermute | solution.py:78
  85.3 7.1 %collective-permute-start.29 = (bf16[2,96,768]{2,1,0:T(8,128)(2,1)S(1)}, bf16[2,96,768]{2,1,0:T(8,128)(2,1)S(1)}, u32[]{:S(2)}, u32[]{:S(2)}) collective-permute-start(bf16[2,96,768]{2,1,0:T(8,128)(2,1)S(1)} %collective-permute-done.25.rest_2_), channel_id=1, source_target_pairs={{0,1},{1,0},{2,3},{3,2},{4,5},{5,4},{6,7},{7,6},{8,9},{9,8},{10,11... | collective-permute-start | bytes 884744 | tf_op jit(solution)/shard_map/ppermute | solution.py:78
  85.8 10.9 %collective-permute-start.30 = (bf16[4,96,384]{2,1,0:T(8,128)(2,1)S(1)}, bf16[4,96,384]{2,1,0:T(8,128)(2,1)S(1)}, u32[]{:S(2)}, u32[]{:S(2)}) collective-permute-start(bf16[4,96,384]{2,1,0:T(8,128)(2,1)S(1)} %get-tuple-element.521.rest_0_), channel_id=1, source_target_pairs={{0,2},{1,3},{2,0},{3,1},{4,6},{5,7},{6,4},{7,5},{8,10},{9,11},{10,... | collective-permute-start | bytes 884744 | tf_op jit(solution)/shard_map/ppermute | solution.py:78
  87.3 9.4 %collective-permute-start.31 = (bf16[4,96,384]{2,1,0:T(8,128)(2,1)S(1)}, bf16[4,96,384]{2,1,0:T(8,128)(2,1)S(1)}, u32[]{:S(2)}, u32[]{:S(2)}) collective-permute-start(bf16[4,96,384]{2,1,0:T(8,128)(2,1)S(1)} %get-tuple-element.521.rest_0_), channel_id=1, source_target_pairs={{0,4},{1,5},{2,6},{3,7},{4,0},{5,1},{6,2},{7,3},{8,12},{9,13},{10,... | collective-permute-start | bytes 884744 | tf_op jit(solution)/shard_map/ppermute | solution.py:78
  96.8 7.0 %collective-permute-start.36 = (bf16[4,96,384]{2,1,0:T(8,128)(2,1)S(1)}, bf16[4,96,384]{2,1,0:T(8,128)(2,1)S(1)}, u32[]{:S(2)}, u32[]{:S(2)}) collective-permute-start(bf16[4,96,384]{2,1,0:T(8,128)(2,1)S(1)} %collective-permute-done.31.rest_1_), channel_id=1, source_target_pairs={{0,1},{1,0},{2,3},{3,2},{4,5},{5,4},{6,7},{7,6},{8,9},{9,8},{10,11... | collective-permute-start | bytes 884744 | tf_op jit(solution)/shard_map/ppermute | solution.py:78
  124.1 15.6 %collective-permute-start.46 = (bf16[4,96,768]{2,1,0:T(8,128)(2,1)S(1)}, bf16[4,96,768]{2,1,0:T(8,128)(2,1)S(1)}, u32[]{:S(2)}, u32[]{:S(2)}) collective-permute-start(bf16[4,96,768]{2,1,0:T(8,128)(2,1)S(1)} %get-tuple-element.593), channel_id=1, source_target_pairs={{0,8},{1,9},{2,10},{3,11},{4,12},{5,13},{6,14},{7,15},{8,0},{9,1},... | collective-permute-start | bytes 1769480 | tf_op jit(solution)/shard_map/ppermute | solution.py:78
  129.4 10.2 %collective-permute-start.44 = (bf16[2,96,768]{2,1,0:T(8,128)(2,1)S(1)}, bf16[2,96,768]{2,1,0:T(8,128)(2,1)S(1)}, u32[]{:S(2)}, u32[]{:S(2)}) collective-permute-start(bf16[2,96,768]{2,1,0:T(8,128)(2,1)S(1)} %get-tuple-element.591), channel_id=1, source_target_pairs={{0,2},{1,3},{2,0},{3,1},{4,6},{5,7},{6,4},{7,5},{8,10},{9,11},{10,... | collective-permute-start | bytes 884744 | tf_op jit(solution)/shard_map/ppermute | solution.py:78
  131.0 8.7 %collective-permute-start.45 = (bf16[2,96,768]{2,1,0:T(8,128)(2,1)S(1)}, bf16[2,96,768]{2,1,0:T(8,128)(2,1)S(1)}, u32[]{:S(2)}, u32[]{:S(2)}) collective-permute-start(bf16[2,96,768]{2,1,0:T(8,128)(2,1)S(1)} %get-tuple-element.592), channel_id=1, source_target_pairs={{0,4},{1,5},{2,6},{3,7},{4,0},{5,1},{6,2},{7,3},{8,12},{9,13},{10,... | collective-permute-start | bytes 884744 | tf_op jit(solution)/shard_map/ppermute | solution.py:78
  140.2 22.0 %collective-permute-start.47 = (bf16[4,96,768]{2,1,0:T(8,128)(2,1)S(1)}, bf16[4,96,768]{2,1,0:T(8,128)(2,1)S(1)}, u32[]{:S(2)}, u32[]{:S(2)}) collective-permute-start(bf16[4,96,768]{2,1,0:T(8,128)(2,1)S(1)} %get-tuple-element.637), channel_id=1, source_target_pairs={{0,2},{1,3},{2,0},{3,1},{4,6},{5,7},{6,4},{7,5},{8,10},{9,11},{10,... | collective-permute-start | bytes 1769480 | tf_op jit(solution)/shard_map/ppermute | solution.py:78
  141.7 20.5 %collective-permute-start.48 = (bf16[4,96,768]{2,1,0:T(8,128)(2,1)S(1)}, bf16[4,96,768]{2,1,0:T(8,128)(2,1)S(1)}, u32[]{:S(2)}, u32[]{:S(2)}) collective-permute-start(bf16[4,96,768]{2,1,0:T(8,128)(2,1)S(1)} %get-tuple-element.638), channel_id=1, source_target_pairs={{0,4},{1,5},{2,6},{3,7},{4,0},{5,1},{6,2},{7,3},{8,12},{9,13},{10,... | collective-permute-start | bytes 1769480 | tf_op jit(solution)/shard_map/ppermute | solution.py:78
  142.9 19.4 %collective-permute-start.51 = (bf16[4,96,768]{2,1,0:T(8,128)(2,1)S(1)}, bf16[4,96,768]{2,1,0:T(8,128)(2,1)S(1)}, u32[]{:S(2)}, u32[]{:S(2)}) collective-permute-start(bf16[4,96,768]{2,1,0:T(8,128)(2,1)S(1)} %get-tuple-element.641), channel_id=1, source_target_pairs={{0,8},{1,9},{2,10},{3,11},{4,12},{5,13},{6,14},{7,15},{8,0},{9,1},... | collective-permute-start | bytes 1769480 | tf_op jit(solution)/shard_map/ppermute | solution.py:78
  143.4 18.8 %collective-permute-start.49 = (bf16[96,768]{1,0:T(8,128)(2,1)S(1)}, bf16[96,768]{1,0:T(8,128)(2,1)S(1)}, u32[]{:S(2)}, u32[]{:S(2)}) collective-permute-start(bf16[96,768]{1,0:T(8,128)(2,1)S(1)} %get-tuple-element.639), channel_id=1, source_target_pairs={{0,2},{1,3},{2,0},{3,1},{4,6},{5,7},{6,4},{7,5},{8,10},{9,11},{10,... | collective-permute-start | bytes 442376 | tf_op jit(solution)/shard_map/ppermute | solution.py:78
  144.9 17.3 %collective-permute-start.50 = (bf16[96,768]{1,0:T(8,128)(2,1)S(1)}, bf16[96,768]{1,0:T(8,128)(2,1)S(1)}, u32[]{:S(2)}, u32[]{:S(2)}) collective-permute-start(bf16[96,768]{1,0:T(8,128)(2,1)S(1)} %get-tuple-element.640), channel_id=1, source_target_pairs={{0,4},{1,5},{2,6},{3,7},{4,0},{5,1},{6,2},{7,3},{8,12},{9,13},{10,... | collective-permute-start | bytes 442376 | tf_op jit(solution)/shard_map/ppermute | solution.py:78
  163.4 9.9 %collective-permute-start.56 = (bf16[2,96,768]{2,1,0:T(8,128)(2,1)S(1)}, bf16[2,96,768]{2,1,0:T(8,128)(2,1)S(1)}, u32[]{:S(2)}, u32[]{:S(2)}) collective-permute-start(bf16[2,96,768]{2,1,0:T(8,128)(2,1)S(1)} %get-tuple-element.659), channel_id=1, source_target_pairs={{0,2},{1,3},{2,0},{3,1},{4,6},{5,7},{6,4},{7,5},{8,10},{9,11},{10,... | collective-permute-start | bytes 884744 | tf_op jit(solution)/shard_map/ppermute | solution.py:78
  163.9 9.9 %collective-permute-start.57 = (bf16[2,96,768]{2,1,0:T(8,128)(2,1)S(1)}, bf16[2,96,768]{2,1,0:T(8,128)(2,1)S(1)}, u32[]{:S(2)}, u32[]{:S(2)}) collective-permute-start(bf16[2,96,768]{2,1,0:T(8,128)(2,1)S(1)} %get-tuple-element.660), channel_id=1, source_target_pairs={{0,4},{1,5},{2,6},{3,7},{4,0},{5,1},{6,2},{7,3},{8,12},{9,13},{10,... | collective-permute-start | bytes 884744 | tf_op jit(solution)/shard_map/ppermute | solution.py:78
  165.0 8.8 %collective-permute-start.58 = (bf16[2,96,768]{2,1,0:T(8,128)(2,1)S(1)}, bf16[2,96,768]{2,1,0:T(8,128)(2,1)S(1)}, u32[]{:S(2)}, u32[]{:S(2)}) collective-permute-start(bf16[2,96,768]{2,1,0:T(8,128)(2,1)S(1)} %get-tuple-element.661), channel_id=1, source_target_pairs={{0,8},{1,9},{2,10},{3,11},{4,12},{5,13},{6,14},{7,15},{8,0},{9,1},... | collective-permute-start | bytes 884744 | tf_op jit(solution)/shard_map/ppermute | solution.py:78
  167.6 11.1 %collective-permute-start.54 = (bf16[2,96,768]{2,1,0:T(8,128)(2,1)S(1)}, bf16[2,96,768]{2,1,0:T(8,128)(2,1)S(1)}, u32[]{:S(2)}, u32[]{:S(2)}) collective-permute-start(bf16[2,96,768]{2,1,0:T(8,128)(2,1)S(1)} %get-tuple-element.657), channel_id=1, source_target_pairs={{0,2},{1,3},{2,0},{3,1},{4,6},{5,7},{6,4},{7,5},{8,10},{9,11},{10,... | collective-permute-start | bytes 884744 | tf_op jit(solution)/shard_map/ppermute | solution.py:78
  168.2 10.7 %collective-permute-start.55 = (bf16[2,96,768]{2,1,0:T(8,128)(2,1)S(1)}, bf16[2,96,768]{2,1,0:T(8,128)(2,1)S(1)}, u32[]{:S(2)}, u32[]{:S(2)}) collective-permute-start(bf16[2,96,768]{2,1,0:T(8,128)(2,1)S(1)} %get-tuple-element.658), channel_id=1, source_target_pairs={{0,4},{1,5},{2,6},{3,7},{4,0},{5,1},{6,2},{7,3},{8,12},{9,13},{10,... | collective-permute-start | bytes 884744 | tf_op jit(solution)/shard_map/ppermute | solution.py:78
  179.6 17.2 %collective-permute-start.59 = (bf16[4,96,768]{2,1,0:T(8,128)(2,1)S(1)}, bf16[4,96,768]{2,1,0:T(8,128)(2,1)S(1)}, u32[]{:S(2)}, u32[]{:S(2)}) collective-permute-start(bf16[4,96,768]{2,1,0:T(8,128)(2,1)S(1)} %get-tuple-element.673), channel_id=1, source_target_pairs={{0,2},{1,3},{2,0},{3,1},{4,6},{5,7},{6,4},{7,5},{8,10},{9,11},{10,... | collective-permute-start | bytes 1769480 | tf_op jit(solution)/shard_map/ppermute | solution.py:78
  181.1 15.7 %collective-permute-start.60 = (bf16[4,96,768]{2,1,0:T(8,128)(2,1)S(1)}, bf16[4,96,768]{2,1,0:T(8,128)(2,1)S(1)}, u32[]{:S(2)}, u32[]{:S(2)}) collective-permute-start(bf16[4,96,768]{2,1,0:T(8,128)(2,1)S(1)} %get-tuple-element.674), channel_id=1, source_target_pairs={{0,4},{1,5},{2,6},{3,7},{4,0},{5,1},{6,2},{7,3},{8,12},{9,13},{10,... | collective-permute-start | bytes 1769480 | tf_op jit(solution)/shard_map/ppermute | solution.py:78
  182.2 11.4 %collective-permute-start.61 = (bf16[96,768]{1,0:T(8,128)(2,1)S(1)}, bf16[96,768]{1,0:T(8,128)(2,1)S(1)}, u32[]{:S(2)}, u32[]{:S(2)}) collective-permute-start(bf16[96,768]{1,0:T(8,128)(2,1)S(1)} %get-tuple-element.675), channel_id=1, source_target_pairs={{0,16},{1,17},{2,18},{3,19},{4,20},{5,21},{6,22},{7,23},{8,24},{9,... | collective-permute-start | bytes 442376 | tf_op jit(solution)/shard_map/ppermute | solution.py:78
  182.4 14.4 %collective-permute-start.62 = (bf16[96,768]{1,0:T(8,128)(2,1)S(1)}, bf16[96,768]{1,0:T(8,128)(2,1)S(1)}, u32[]{:S(2)}, u32[]{:S(2)}) collective-permute-start(bf16[96,768]{1,0:T(8,128)(2,1)S(1)} %get-tuple-element.676), channel_id=1, source_target_pairs={{0,16},{1,17},{2,18},{3,19},{4,20},{5,21},{6,22},{7,23},{8,24},{9,... | collective-permute-start | bytes 442376 | tf_op jit(solution)/shard_map/ppermute | solution.py:78
  197.1 10.0 %collective-permute-start.64 = (bf16[2,96,768]{2,1,0:T(8,128)(2,1)S(1)}, bf16[2,96,768]{2,1,0:T(8,128)(2,1)S(1)}, u32[]{:S(2)}, u32[]{:S(2)}) collective-permute-start(bf16[2,96,768]{2,1,0:T(8,128)(2,1)S(1)} %get-tuple-element.683), channel_id=1, source_target_pairs={{0,8},{1,9},{2,10},{3,11},{4,12},{5,13},{6,14},{7,15},{8,0},{9,1},... | collective-permute-start | bytes 884744 | tf_op jit(solution)/shard_map/ppermute | solution.py:78
  197.2 7.8 %collective-permute-start.65 = (f32[16,768]{1,0:T(8,128)S(1)}, f32[16,768]{1,0:T(8,128)S(1)}, u32[]{:S(2)}, u32[]{:S(2)}) collective-permute-start(f32[16,768]{1,0:T(8,128)S(1)} %add_select_fusion.3), channel_id=1, source_target_pairs={{0,16},{1,17},{2,18},{3,19},{4,20},{5,21},{6,22},{7,23},{8,24},{9,... | collective-permute-start | bytes 147464 | tf_op jit(solution)/shard_map/ppermute | solution.py:78
  208.1 8.0 %collective-permute-start.66 = (bf16[96,768]{1,0:T(8,128)(2,1)S(1)}, bf16[96,768]{1,0:T(8,128)(2,1)S(1)}, u32[]{:S(2)}, u32[]{:S(2)}) collective-permute-start(bf16[96,768]{1,0:T(8,128)(2,1)S(1)} %get-tuple-element.689), channel_id=1, source_target_pairs={{0,16},{1,17},{2,18},{3,19},{4,20},{5,21},{6,22},{7,23},{8,24},{9,... | collective-permute-start | bytes 442376 | tf_op jit(solution)/shard_map/ppermute | solution.py:78
  (42 other events, 300.1 us)

commit v9 on v8

--- a/solution.py
+++ b/solution.py
@@ -247,7 +247,8 @@
 
 VM = pl.BlockSpec(memory_space=pltpu.VMEM)
 SM = pl.BlockSpec(memory_space=pltpu.SMEM)
-VMEM_MIB = 14
+VMEM_MIB = 8
+ROOMY = ("down_both",)
 
 
 def like(shape, dtype=f32):
@@ -262,7 +263,7 @@
         in_specs=specs,
         out_specs=[VM] * len(outs),
         scratch_shapes=list(scratch),
-        compiler_params=pltpu.CompilerParams(vmem_limit_bytes=VMEM_MIB * 2**20),
+        compiler_params=pltpu.CompilerParams(vmem_limit_bytes=(14 if name in ROOMY else VMEM_MIB) * 2**20),
         cost_estimate=pl.CostEstimate(flops=flops, bytes_accessed=moved, transcendentals=0),
     )
 
@@ -377,15 +378,25 @@
     return glue(attn_sums, [like((3, rows, cols)), like((cols, rows))], kept, last)
 
 
-def attn_shard(qkv_weight, out_weight):
+def shards(qkv_weight, out_weight, qv_bias, up_bias, down_weight_t):
     _, rows, cols = qkv_weight.shape
-
-    def attn_weights(qkv, out_weight, out):
+    wide = 3 * cols + HEAD_DIM
+    width = down_weight_t.shape[1]
+
+    def first_shards(qkv, out_weight, qv_bias, up_bias, down, attn, down_0, down_1, biases):
         for j in range(3):
-            out[:, j * cols : (j + 1) * cols] = qkv[j].astype(bf16)
-        out[:, 3 * cols :] = out_weight[...].T.astype(bf16)
-
-    return glue(attn_weights, [like((rows, 4 * cols), bf16)], qkv_weight, out_weight)[0]
+            attn[:, j * cols : (j + 1) * cols] = qkv[j].astype(bf16)
+        attn[:, 3 * cols :] = out_weight[...].T.astype(bf16)
+        down_0[...] = down[:, : width // 2].astype(bf16)
+        down_1[...] = down[:, width // 2 :].astype(bf16)
+        biases[...] = jnp.zeros_like(biases)
+        biases[:, :cols] = qv_bias[0:1, :]
+        biases[:, 2 * cols : 3 * cols] = qv_bias[1:2, :]
+        biases[:, wide:] = row(up_bias)
+
+    part = like((rows, width // 2), bf16)
+    outs = [like((rows, 4 * cols), bf16), part, part, like((1, wide + width))]
+    return glue(first_shards, outs, qkv_weight, out_weight, qv_bias, up_bias, down_weight_t)
 
 
 def assemble(plan, bufs, dst, dp):
@@ -650,13 +661,12 @@
     heads_backward(first, dims, net.me()[1], qkv, lse, attn_low, weight, ctx_slope, mask, grad_ctx, out, sums)
 
 
-def attn_backward_last(net, dims, longs, shorts, lim, qkv, lse, attn_low, weight, ctx_slope, *rest):
+def attn_backward_last(net, dims, longs, shorts, qkv, lse, attn_low, weight, ctx_slope, *rest):
     blocks, cols, width = dims
-    in_t, attn_t, ctx_low, grad_first, tokens, more_out, more, *rest = rest
+    in_t, attn_t, ctx_low, more_out, more, *rest = rest
     up_sums, sums_a, sums_b, tops_a, tops_m, top0, top1, *rest = rest
-    far, near, packed, tokens_out, out, sums, mask, grad_ctx, acc = rest
+    out, far, near, packed, sums, mask, grad_ctx = rest
     rows = in_t.shape[0] // net.parts
-    half = far.shape[0]
     wide = 3 * cols + HEAD_DIM
     start = 3 * cols - HEAD_DIM
     dp, lane_me = net.me()
@@ -684,16 +694,6 @@
             return carry
 
         lax.fori_loop(0, 2, weights, 0)
-    acc[...] = jnp.zeros_like(acc)
-    for grads, first in ((out, 0), (more_out, half)):
-
-        def back(i, carry):
-            acc[...] += mm_nt(grads[i], weight[first + i, :, :wide])
-            return carry
-
-        lax.fori_loop(0, half, back, 0)
-    inputs = tokens[...].astype(f32)
-    tokens_out[...] = (grad_first[...] + jnp.where(jnp.abs(inputs) <= lim[0], acc[...], 0.0)).astype(bf16)
     packed[...] = jnp.zeros_like(packed)
     for j in range(blocks):
         packed[j : j + 1, :] = up_sums[j]
@@ -703,6 +703,21 @@
     tops = (tops_a[0:1, :], tops_a[1:2, :], tops_m[0:1, :], jnp.maximum(top0[0:1, :], top1[0:1, :]))
     for j, top in enumerate(tops):
         packed[2 * blocks + 6 : 2 * blocks + 7, 128 * j : 128 * j + 128] = top
+
+
+def token_backward(dims, lim, grads_0, grads_1, grad_first, tokens, weight, out, acc):
+    blocks, cols, width = dims
+    acc[...] = jnp.zeros_like(acc)
+    half = grads_0.shape[0]
+    for grads, first in ((grads_0, 0), (grads_1, half)):
+
+        def back(i, carry):
+            acc[...] += mm_nt(grads[i], weight[first + i, :, : 3 * cols + HEAD_DIM])
+            return carry
+
+        lax.fori_loop(0, half, back, 0)
+    inputs = tokens[...].astype(f32)
+    out[...] = (grad_first[...] + jnp.where(jnp.abs(inputs) <= lim[0], acc[...], 0.0)).astype(bf16)
 
 
 def make_body(net):
@@ -738,18 +753,12 @@
         every = tuple(range(blocks))
 
         pieces_a, pieces_u, pieces_d = Pieces([]), Pieces([]), Pieces([])
-        shard_a = attn_shard(qkv_weight, out_weight)
-        shard_a, up_bias, down_weight = tie(shard_a, up_bias, down_weight)
+        shard_a, shard_d, shard_p, bias_row = shards(qkv_weight, out_weight, qv_bias, up_bias, down_weight.T)
         job_a = Job(net.gather(shard_a, pieces_a))
-        bias_row = jnp.concatenate(
-            [qv_bias[0], jnp.zeros((cols,), f32), qv_bias[1], jnp.zeros((HEAD_DIM,), f32), up_bias]
-        )
-        job_b = Job(net.gather_lane(bias_row[None]))
+        job_b = Job(net.gather_lane(bias_row))
         job_u = Job(net.gather(up_weight.astype(bf16), pieces_u))
-        shard_d = down_weight.T.astype(bf16)
-        col = up_cols // 2
-        job_d = Job(net.gather(shard_d[:, :col], pieces_d))
-        job_p = Job(net.gather_plane_first(shard_d[:, col:], pieces_d, col))
+        job_d = Job(net.gather(shard_d, pieces_d))
+        job_p = Job(net.gather_plane_first(shard_p, pieces_d, up_cols // 2))
 
         def vmem(*shape, dtype=f32):
             return pltpu.VMEM(shape, dtype)
@@ -758,8 +767,8 @@
         moved = 2 * width * width * blocks
 
         step((), None, [job_a, job_p, job_b], [job_a, job_p, job_b])
-        step((), None, [job_a, job_p, job_b], [job_a, job_p, job_b])
-        step((), None, [job_a, job_u, job_d], [job_a, job_u, job_d])
+        step((), None, [job_a, job_p, job_b, job_d], [job_a, job_p, job_b])
+        step((), None, [job_a, job_u], [job_a, job_u, job_d])
         step((), None, [job_a, job_u], [job_a, job_u])
         step((), None, [job_a, job_u], [job_a])
         biases = job_b.value
@@ -910,22 +919,16 @@
             [sum_u],
             [sum_u, sum_d],
         )
-        far, near, packed, tokens_grad = step(
-            (long_lengths, short_lengths, act_ranges, qkv, lse, attn_low, weight_a, ctx_slope)
-            + (in_t, attn_t, ctx_low, grad_first, tokens, grads_1, more)
+        grads_0, far, near, packed = step(
+            (long_lengths, short_lengths, qkv, lse, attn_low, weight_a, ctx_slope)
+            + (in_t, attn_t, ctx_low, grads_1, more)
             + (up_sums, sums_a, sums_b, tops_a, tops_m, top0, top1),
             call(
                 functools.partial(attn_backward_last, net, dims),
                 "attn_backward_last",
-                [SM] * 3 + [VM] * 19,
-                [both_shape, both_shape, like((16, width)), like((rows, width), bf16)],
-                [
-                    vmem(half, rows, wide, dtype=bf16),
-                    vmem(blocks, 1, wide),
-                    vmem(rows, rows),
-                    vmem(rows, out_cols, dtype=bf16),
-                    vmem(rows, width),
-                ],
+                [SM] * 2 + [VM] * 17,
+                [like((half, rows, wide), bf16), both_shape, both_shape, like((16, width))],
+                [vmem(blocks, 1, wide), vmem(rows, rows), vmem(rows, out_cols, dtype=bf16)],
                 4 * unit,
                 2 * moved,
             ),
@@ -936,9 +939,22 @@
         is_top = (jnp.arange(packed.shape[0]) == 2 * blocks + 6)[:, None]
         sum_s = Job(net.sum_max(packed, is_top))
         line_u = Job(net.scatter_line(*sum_u.value))
-        step((), None, [sum_a, sum_d, line_u, sum_s], [sum_a, sum_s])
-        step((), None, [sum_a], [sum_a, sum_d, line_u])
-        step((), None, [sum_a, sum_d, line_u, sum_s], [sum_a, sum_d, line_u, sum_s])
+        tokens_grad = step(
+            (act_ranges, grads_0, grads_1, grad_first, tokens, weight_a),
+            call(
+                functools.partial(token_backward, dims),
+                "token_backward",
+                [SM] + [VM] * 5,
+                [like((rows, width), bf16)],
+                [vmem(rows, width)],
+                unit,
+                2 * moved,
+            ),
+            [sum_a, sum_d, line_u, sum_s],
+            [sum_a, sum_d, line_u, sum_s],
+        )[0]
+        step((), None, [sum_a, sum_d], [sum_a, sum_d])
+        step((), None, [sum_a, line_u, sum_s], [sum_a, line_u, sum_s])
         line_a = Job(net.scatter_line(*sum_a.value))
         step((), None, [line_a, sum_s], [line_a, sum_s])
         step((), None, [line_a, sum_s], [sum_s])

time: 219 us -> 215 us (0.982)
  waiting for transfers between devices: 75 us -> 68.7 us
  starting transfers between devices: 59.3 us -> 64.7 us
  local copies, waits for them, and re-layouts: 8.27 us -> 5.24 us
    ppermute x69, waiting for transfers between devices: 75 us -> 68.7 us  [step(): lax.ppermute(v, ALL, perm)]
    ppermute x69, starting transfers between devices: 59.3 us -> 64.7 us  [step(): lax.ppermute(v, ALL, perm)]
    unnamed x46 -> x34, local copies, waits for them, and re-layouts: 5.77 us -> 4.3 us
    pallas_call x10 -> x11, Pallas kernels: 65.6 us -> 66 us  [step(): outs = run(*ins) if run else ins]
  transfers between devices with their start and end apart: 69 -> 69, of which waited for: 30 -> 34; matrix products, arithmetic and copies ran while one was open for 1% -> 1% of each run, Pallas kernels for 25% -> 25%
where the time goes in v9:
time: 215 us; the launch traced here: 214 us
  Pallas kernels  69.5 us (32%)
  waiting for transfers between devices  68.7 us (32%)
  starting transfers between devices  64.7 us (30%)
  local copies, waits for them, and re-layouts  5.24 us (2%)
  other arithmetic  4.32 us (2%)
    ppermute x69, waiting for transfers between devices, step(): lax.ppermute(v, ALL, perm)  68.7 us
    pallas_call x11, Pallas kernels, step(): outs = run(*ins) if run else ins  66 us
    ppermute x69, starting transfers between devices, step(): lax.ppermute(v, ALL, perm)  64.7 us
  transfers between devices with their start and end apart: 69, of which 34 were waited for; matrix products, arithmetic and copies ran while one was open for 1% of the time, Pallas kernels for 25%

profile of v9, /device:TPU:0, one launch (start us, length us, event | category | flops | bytes accessed | tf_op | source)
XLA Modules:
  0.0 214.3 jit_solution(16994074514138616680)
XLA Ops:
  5.0 4.1 %collective-permute-start = (bf16[1,96,768]{2,1,0:T(8,128)(2,1)S(1)}, bf16[1,96,768]{2,1,0:T(8,128)(2,1)S(1)}, u32[]{:S(2)}, u32[]{:S(2)}) collective-permute-start(bf16[1,96,768]{2,1,0:T(8,128)(2,1)S(1)} %bitcast.19), channel_id=1, source_target_pairs={{0,16},{1,17},{2,18},{3,19},{4,20},{5,21},{6,22},{7,23},{8,24},{9,... | collective-permute-start | bytes 442376 | tf_op jit(solution)/shard_map/ppermute | solution.py:78
  9.1 1.5 collective-permute-start.1
  10.6 1.5 collective-permute-start.2
  12.7 3.1 %collective-permute-done.3 = f32[1,1408]{1,0:T(1,128)S(1)} collective-permute-done((f32[1,1408]{1,0:T(1,128)S(1)}, f32[1,1408]{1,0:T(1,128)S(1)}, u32[]{:S(2)}, u32[]{:S(2)}) %collective-permute-start.3) | collective-permute-done | bytes 5664 | tf_op jit(solution)/shard_map/ppermute | solution.py:78
  16.2 1.3 collective-permute-start.4
  19.6 2.2 %collective-permute-done.5 = bf16[1,96,384]{2,1,0:T(8,128)(2,1)S(1)} collective-permute-done((bf16[1,96,384]{2,1,0:T(8,128)(2,1)S(1)}, bf16[1,96,384]{2,1,0:T(8,128)(2,1)S(1)}, u32[]{:S(2)}, u32[]{:S(2)}) %collective-permute-start.5) | collective-permute-done | bytes 73760 | tf_op jit(solution)/shard_map/ppermute | solution.py:78
  21.8 2.6 %collective-permute-done.4 = bf16[2,96,768]{2,1,0:T(8,128)(2,1)S(1)} collective-permute-done((bf16[2,96,768]{2,1,0:T(8,128)(2,1)S(1)}, bf16[2,96,768]{2,1,0:T(8,128)(2,1)S(1)}, u32[]{:S(2)}, u32[]{:S(2)}) %collective-permute-start.4) | collective-permute-done | bytes 294944 | tf_op jit(solution)/shard_map/ppermute | solution.py:78
  24.5 1.3 collective-permute-start.7
  25.9 1.5 collective-permute-start.8
  27.4 3.3 %collective-permute-start.11 = (bf16[1,96,384]{2,1,0:T(8,128)(2,1)S(1)}, bf16[1,96,384]{2,1,0:T(8,128)(2,1)S(1)}, u32[]{:S(2)}, u32[]{:S(2)}) collective-permute-start(bf16[1,96,384]{2,1,0:T(8,128)(2,1)S(1)} %bitcast.25), channel_id=1, source_target_pairs={{0,16},{1,17},{2,18},{3,19},{4,20},{5,21},{6,22},{7,23},{8,24},{9,... | collective-permute-start | bytes 221192 | tf_op jit(solution)/shard_map/ppermute | solution.py:78
  31.4 4.0 %collective-permute-done.11 = bf16[1,96,384]{2,1,0:T(8,128)(2,1)S(1)} collective-permute-done((bf16[1,96,384]{2,1,0:T(8,128)(2,1)S(1)}, bf16[1,96,384]{2,1,0:T(8,128)(2,1)S(1)}, u32[]{:S(2)}, u32[]{:S(2)}) %collective-permute-start.11) | collective-permute-done | bytes 73760 | tf_op jit(solution)/shard_map/ppermute | solution.py:78
  35.4 6.1 %collective-permute-done.10 = bf16[1,96,768]{2,1,0:T(8,128)(2,1)S(1)} collective-permute-done((bf16[1,96,768]{2,1,0:T(8,128)(2,1)S(1)}, bf16[1,96,768]{2,1,0:T(8,128)(2,1)S(1)}, u32[]{:S(2)}, u32[]{:S(2)}) %collective-permute-start.10) | collective-permute-done | bytes 147488 | tf_op jit(solution)/shard_map/ppermute | solution.py:78
  44.6 6.7 %collective-permute-done.12.rest_3_ = bf16[2,96,768]{2,1,0:T(8,128)(2,1)S(1)} collective-permute-done((bf16[2,96,768]{2,1,0:T(8,128)(2,1)S(1)}, bf16[2,96,768]{2,1,0:T(8,128)(2,1)S(1)}, u32[]{:S(2)}, u32[]{:S(2)}) %collective-permute-start.12) | collective-permute-done | bytes 294944 | tf_op jit(solution)/shard_map/ppermute | solution.py:78
  52.5 1.6 collective-permute-start.19
  54.1 1.5 collective-permute-start.20
  55.6 2.4 %collective-permute-start.23 = (bf16[4,96,384]{2,1,0:T(8,128)(2,1)S(1)}, bf16[4,96,384]{2,1,0:T(8,128)(2,1)S(1)}, u32[]{:S(2)}, u32[]{:S(2)}) collective-permute-start(bf16[4,96,384]{2,1,0:T(8,128)(2,1)S(1)} %pad_maximum_fusion.4), channel_id=1, source_target_pairs={{0,16},{1,17},{2,18},{3,19},{4,20},{5,21},{6,22},{7,23},{8,24},{9,... | collective-permute-start | bytes 884744 | tf_op jit(solution)/shard_map/ppermute | solution.py:78
  58.0 1.7 collective-permute-start.22
  59.8 11.5 %attn_forward.1 = (bf16[4,512,640]{2,1,0:T(8,128)(2,1)S(1)}, f32[4,8,512]{2,1,0:T(8,128)S(1)}, bf16[768,512]{1,0:T(8,128)(2,1)S(1)}, bf16[4,512,256]{2,1,0:T(8,1...) custom-call(f32[4]{0:T(128)S(1)} %copy-done.7, ...), custom_call_target="tpu_custom_call" | custom-call | flops 9663676416 | bytes 14155776 | tf_op jit(solution)/shard_map/attn_forward/pallas_call | solution.py:79
  75.2 3.3 %attn_finish.1 = (f32[512,768]{1,0:T(8,128)S(1)}, f32[512,1]{1,0:T(8,128)S(1)}, f32[512,768]{1,0:T(8,128)S(1)}, f32[512,768]{1,0:T(8,128)S(1)}, bf16[512,768]{1,...) custom-call(f32[4]{0:T(128)S(1)} %copy-done.7, ...), custom_call_target="tpu_custom_call" | custom-call | flops 4831838208 | bytes 9437184 | tf_op jit(solution)/shard_map/attn_finish/pallas_call | solution.py:79
  78.4 3.5 %collective-permute-done.24.rest_1_ = bf16[2,96,768]{2,1,0:T(8,128)(2,1)S(1)} collective-permute-done((bf16[2,96,768]{2,1,0:T(8,128)(2,1)S(1)}, bf16[2,96,768]{2,1,0:T(8,128)(2,1)S(1)}, u32[]{:S(2)}, u32[]{:S(2)}) %collective-permute-start.24) | collective-permute-done | bytes 294944 | tf_op jit(solution)/shard_map/ppermute | solution.py:78
  82.8 1.5 collective-permute-start.30
  85.1 4.2 %up_forward_0.1 = (bf16[2,512,768]{2,1,0:T(8,128)(2,1)S(1)}, f32[2,512,768]{2,1,0:T(8,128)S(1)}, f32[8,128]{1,0:T(8,128)S(1)}, bf16[2,768,768]{2,1,0:T(8,128)(2,1)S(1)}) custom-call(f32[4]{0:T(128)S(1)} %copy-done.7, bf16[512,768]{1,0:T(8,128)(2,1)S(1)} %get-tuple-element.480.mid_low, f32[4,1,1408]{2,1,0:T(1,128)S(1)} %bitcast.30, ...), custom_call_target="tpu_custom_call" | custom-call | flops 4831838208 | bytes 9437184 | tf_op jit(solution)/shard_map/up_forward_0/pallas_call | solution.py:79
  89.5 4.2 %up_forward_2.1 = (bf16[2,512,768]{2,1,0:T(8,128)(2,1)S(1)}, f32[2,512,768]{2,1,0:T(8,128)S(1)}, f32[8,128]{1,0:T(8,128)S(1)}, bf16[2,768,768]{2,1,0:T(8,128)(2,1)S(1)}) custom-call(f32[4]{0:T(128)S(1)} %copy-done.7, bf16[512,768]{1,0:T(8,128)(2,1)S(1)} %get-tuple-element.480.mid_low, f32[4,1,1408]{2,1,0:T(1,128)S(1)} %bitcast.31, ...), custom_call_target="tpu_custom_call" | custom-call | flops 4831838208 | bytes 9437184 | tf_op jit(solution)/shard_map/up_forward_2/pallas_call | solution.py:79
  96.0 4.5 %collective-permute-done.34.rest_3_ = bf16[2,96,384]{2,1,0:T(8,128)(2,1)S(1)} collective-permute-done((bf16[2,96,384]{2,1,0:T(8,128)(2,1)S(1)}, bf16[2,96,384]{2,1,0:T(8,128)(2,1)S(1)}, u32[]{:S(2)}, u32[]{:S(2)}) %collective-permute-start.34) | collective-permute-done | bytes 147488 | tf_op jit(solution)/shard_map/ppermute | solution.py:78
  101.8 2.0 collective-permute-done.38.rest_8_
  104.1 9.1 %down_both.1 = (bf16[512,768]{1,0:T(8,128)(2,1)}, f32[512,768]{1,0:T(8,128)S(1)}, bf16[768,512]{1,0:T(8,128)(2,1)S(1)}, f32[8,768]{1,0:T(8,128)S(1)}, bf16[4,512...) custom-call(bf16[2,512,768]{2,1,0:T(8,128)(2,1)S(1)} %get-tuple-element.556.act0.rest_0_, ...), custom_call_target="tpu_custom_call" | custom-call | flops 4831838208 | bytes 18874368 | tf_op jit(solution)/shard_map/down_both/pallas_call | solution.py:79
  113.2 2.7 %down_grad.1 = (bf16[2,8,96,768]{3,2,1,0:T(8,128)(2,1)S(1)}, bf16[2,8,96,768]{3,2,1,0:T(8,128)(2,1)S(1)}) custom-call(bf16[768,512]{1,0:T(8,128)(2,1)S(1)} %get-tuple-element.555.left_t, bf16[2,512,768]{2,1,0:T(8,128)(2,1)S(1)} %get-tuple-element.556.act0.rest_0_, bf16[2,512,768]{2,1,0:T(8,128)(2,1)S(1)} %get-tuple-element.557.act1.rest_1_), custom_call_target="tpu_custom_call" | custom-call | flops 2415919104 | bytes 4718592 | tf_op jit(solution)/shard_map/down_grad/pallas_call | solution.py:79
  116.1 2.7 %up_grad.1 = (bf16[2,8,96,768]{3,2,1,0:T(8,128)(2,1)S(1)}, bf16[2,8,96,768]{3,2,1,0:T(8,128)(2,1)S(1)}) custom-call(bf16[768,512]{1,0:T(8,128)(2,1)S(1)} %get-tuple-element.559.left_t, bf16[4,512,768]{2,1,0:T(8,128)(2,1)S(1)} %get-tuple-element.568.rest_0_.grad_up), custom_call_target="tpu_custom_call" | custom-call | flops 2415919104 | bytes 4718592 | tf_op jit(solution)/shard_map/up_grad/pallas_call | solution.py:79
  118.8 1.7 collective-permute-done.42.got
  121.7 4.7 %mid_backward.1 = (f32[512,768]{1,0:T(8,128)S(1)}, bf16[512,768]{1,0:T(8,128)(2,1)S(1)}, bf16[768,512]{1,0:T(8,128)(2,1)S(1)}, f32[8,768]{1,0:T(8,128)S(1)}) custom-call(bf16[4,512,768]{2,1,0:T(8,128)(2,1)S(1)} %get-tuple-element.568.rest_0_.grad_up, f32[512,768]{1,0:T(8,128)S(1)} %get-tuple-element.569.grad_second, ...), custom_call_target="tpu_custom_call" | custom-call | flops 3221225472 | bytes 14155776 | tf_op jit(solution)/shard_map/mid_backward/pallas_call | solution.py:79
  126.6 1.6 collective-permute-start.44
  129.0 6.9 %attn_backward.1 = (bf16[2,512,640]{2,1,0:T(8,128)(2,1)S(1)}, f32[4,1,640]{2,1,0:T(1,128)S(1)}) custom-call(s32[1]{0:T(128)S(6)} %copy.37.longs, s32[12]{0:T(128)S(1)} %copy-done.14, bf16[4,512,640]{2,1,0:T(8,128)(2,1)S(1)} %get-tuple-element.620.qkv, f32[4,8,512]{2,1,0:T(8,128)S(1)} %get-tuple-element.621.lse, ...), custom_call_target="tpu_custom_call" | custom-call | flops 4831838208 | bytes 9437184 | tf_op jit(solution)/shard_map/attn_backward/pallas_call | solution.py:79
  140.4 1.5 collective-permute-start.49
  142.8 11.7 %attn_backward_last.1 = (bf16[2,512,640]{2,1,0:T(8,128)(2,1)S(1)}, bf16[2,8,96,768]{3,2,1,0:T(8,128)(2,1)S(1)}, bf16[2,8,96,768]{3,2,1,0:T(8,128)(2,1)S(1)}, f32[16,768]{1,0:T(8,128)S(1)}) custom-call(s32[1]{0:T(128)S(6)} %copy.37.longs, s32[12]{0:T(128)S(1)} %copy-done.14, bf16[4,512,640]{2,1,0:T(8,128)(2,1)S(1)} %get-tuple-element.620.qkv, ...), custom_call_target="tpu_custom_call" | custom-call | flops 9663676416 | bytes 9437184 | tf_op jit(solution)/shard_map/attn_backward_last/pallas_call | solution.py:79
  159.6 5.1 %token_backward.1 = bf16[512,768]{1,0:T(8,128)(2,1)} custom-call(f32[4]{0:T(128)S(1)} %copy-done.7, bf16[2,512,640]{2,1,0:T(8,128)(2,1)S(1)} %get-tuple-element.659.grads_0, bf16[2,512,640]{2,1,0:T(8,128)(2,1)S(1)} %get-tuple-element.660.rest_3_.grads_1, f32[512,768]{1,0:T(8,128)S(1)} %get-tuple-element.661.grad_first, bf16[512,768]{1,0:T(8,128)(2,1)S(1)} %copy-done, ...), custom_call_target="tpu_custom_call" | custom-call | flops 2415919104 | bytes 9437184 | tf_op jit(solution)/shard_map/token_backward/pallas_call | solution.py:79
  164.7 1.5 collective-permute-done.53.in_x
  167.7 1.6 collective-permute-start.57
  170.2 2.6 %collective-permute-start.59 = (bf16[96,768]{1,0:T(8,128)(2,1)S(1)}, bf16[96,768]{1,0:T(8,128)(2,1)S(1)}, u32[]{:S(2)}, u32[]{:S(2)}) collective-permute-start(bf16[96,768]{1,0:T(8,128)(2,1)S(1)} %get-tuple-element.679), channel_id=1, source_target_pairs={{0,16},{1,17},{2,18},{3,19},{4,20},{5,21},{6,22},{7,23},{8,24},{9,... | collective-permute-start | bytes 442376 | tf_op jit(solution)/shard_map/ppermute | solution.py:78
  173.0 5.5 %collective-permute-done.59 = bf16[96,768]{1,0:T(8,128)(2,1)S(1)} collective-permute-done((bf16[96,768]{1,0:T(8,128)(2,1)S(1)}, bf16[96,768]{1,0:T(8,128)(2,1)S(1)}, u32[]{:S(2)}, u32[]{:S(2)}) %collective-permute-start.59) | collective-permute-done | bytes 147488 | tf_op jit(solution)/shard_map/ppermute | solution.py:78
  181.9 2.5 %collective-permute-start.63 = (f32[16,768]{1,0:T(8,128)S(1)}, f32[16,768]{1,0:T(8,128)S(1)}, u32[]{:S(2)}, u32[]{:S(2)}) collective-permute-start(f32[16,768]{1,0:T(8,128)S(1)} %add_select_fusion.4), channel_id=1, source_target_pairs={{0,8},{1,9},{2,10},{3,11},{4,12},{5,13},{6,14},{7,15},{8,0},{9,1},... | collective-permute-start | bytes 147464 | tf_op jit(solution)/shard_map/ppermute | solution.py:78
  184.3 2.1 collective-permute-done.63
  186.4 3.0 %collective-permute-done.62 = bf16[96,768]{1,0:T(8,128)(2,1)S(1)} collective-permute-done((bf16[96,768]{1,0:T(8,128)(2,1)S(1)}, bf16[96,768]{1,0:T(8,128)(2,1)S(1)}, u32[]{:S(2)}, u32[]{:S(2)}) %collective-permute-start.62) | collective-permute-done | bytes 147488 | tf_op jit(solution)/shard_map/ppermute | solution.py:78
  189.4 3.8 %collective-permute-done.60.in_x = bf16[4,96,768]{2,1,0:T(8,128)(2,1)S(1)} collective-permute-done((bf16[4,96,768]{2,1,0:T(8,128)(2,1)S(1)}, bf16[4,96,768]{2,1,0:T(8,128)(2,1)S(1)}, u32[]{:S(2)}, u32[]{:S(2)}) %collective-permute-start.60) | collective-permute-done | bytes 589856 | tf_op jit(solution)/shard_map/ppermute | solution.py:78
  194.7 3.3 %collective-permute-start.65 = (f32[16,768]{1,0:T(8,128)S(1)}, f32[16,768]{1,0:T(8,128)S(1)}, u32[]{:S(2)}, u32[]{:S(2)}) collective-permute-start(f32[16,768]{1,0:T(8,128)S(1)} %add_select_fusion.3), channel_id=1, source_target_pairs={{0,16},{1,17},{2,18},{3,19},{4,20},{5,21},{6,22},{7,23},{8,24},{9,... | collective-permute-start | bytes 147464 | tf_op jit(solution)/shard_map/ppermute | solution.py:78
  198.0 2.7 %collective-permute-done.65 = f32[16,768]{1,0:T(8,128)S(1)} collective-permute-done((f32[16,768]{1,0:T(8,128)S(1)}, f32[16,768]{1,0:T(8,128)S(1)}, u32[]{:S(2)}, u32[]{:S(2)}) %collective-permute-start.65) | collective-permute-done | bytes 49184 | tf_op jit(solution)/shard_map/ppermute | solution.py:78
  200.8 2.2 %collective-permute-done.64.from_z = bf16[2,96,768]{2,1,0:T(8,128)(2,1)S(1)} collective-permute-done((bf16[2,96,768]{2,1,0:T(8,128)(2,1)S(1)}, bf16[2,96,768]{2,1,0:T(8,128)(2,1)S(1)}, u32[]{:S(2)}, u32[]{:S(2)}) %collective-permute-start.64) | collective-permute-done | bytes 294944 | tf_op jit(solution)/shard_map/ppermute | solution.py:78
  204.5 1.7 collective-permute-start.66
  208.8 2.6 %collective-permute-done.68 = f32[16,768]{1,0:T(8,128)S(1)} collective-permute-done((f32[16,768]{1,0:T(8,128)S(1)}, f32[16,768]{1,0:T(8,128)S(1)}, u32[]{:S(2)}, u32[]{:S(2)}) %collective-permute-start.68) | collective-permute-done | bytes 49184 | tf_op jit(solution)/shard_map/ppermute | solution.py:78
  (179 shorter events, 48.4 us)
Async XLA Ops:
  5.0 11.1 %collective-permute-start = (bf16[1,96,768]{2,1,0:T(8,128)(2,1)S(1)}, bf16[1,96,768]{2,1,0:T(8,128)(2,1)S(1)}, u32[]{:S(2)}, u32[]{:S(2)}) collective-permute-start(bf16[1,96,768]{2,1,0:T(8,128)(2,1)S(1)} %bitcast.19), channel_id=1, source_target_pairs={{0,16},{1,17},{2,18},{3,19},{4,20},{5,21},{6,22},{7,23},{8,24},{9,... | collective-permute-start | bytes 442376 | tf_op jit(solution)/shard_map/ppermute | solution.py:78
  9.1 6.6 %collective-permute-start.1 = (bf16[1,96,384]{2,1,0:T(8,128)(2,1)S(1)}, bf16[1,96,384]{2,1,0:T(8,128)(2,1)S(1)}, u32[]{:S(2)}, u32[]{:S(2)}) collective-permute-start(bf16[1,96,384]{2,1,0:T(8,128)(2,1)S(1)} %bitcast.22), channel_id=1, source_target_pairs={{0,2},{1,3},{2,0},{3,1},{4,6},{5,7},{6,4},{7,5},{8,10},{9,11},{10,... | collective-permute-start | bytes 221192 | tf_op jit(solution)/shard_map/ppermute | solution.py:78
  16.2 8.2 %collective-permute-start.4 = (bf16[2,96,768]{2,1,0:T(8,128)(2,1)S(1)}, bf16[2,96,768]{2,1,0:T(8,128)(2,1)S(1)}, u32[]{:S(2)}, u32[]{:S(2)}) collective-permute-start(bf16[2,96,768]{2,1,0:T(8,128)(2,1)S(1)} %pad_maximum_fusion.2), channel_id=1, source_target_pairs={{0,8},{1,9},{2,10},{3,11},{4,12},{5,13},{6,14},{7,15},{8,0},{9,1},... | collective-permute-start | bytes 884744 | tf_op jit(solution)/shard_map/ppermute | solution.py:78
  24.5 17.0 %collective-permute-start.7 = (bf16[4,96,768]{2,1,0:T(8,128)(2,1)S(1)}, bf16[4,96,768]{2,1,0:T(8,128)(2,1)S(1)}, u32[]{:S(2)}, u32[]{:S(2)}) collective-permute-start(bf16[4,96,768]{2,1,0:T(8,128)(2,1)S(1)} %pad_maximum_fusion.rest_0_), channel_id=1, source_target_pairs={{0,2},{1,3},{2,0},{3,1},{4,6},{5,7},{6,4},{7,5},{8,10},{9,11},{10,... | collective-permute-start | bytes 1769480 | tf_op jit(solution)/shard_map/ppermute | solution.py:78
  25.9 15.7 %collective-permute-start.8 = (bf16[4,96,768]{2,1,0:T(8,128)(2,1)S(1)}, bf16[4,96,768]{2,1,0:T(8,128)(2,1)S(1)}, u32[]{:S(2)}, u32[]{:S(2)}) collective-permute-start(bf16[4,96,768]{2,1,0:T(8,128)(2,1)S(1)} %pad_maximum_fusion.rest_0_), channel_id=1, source_target_pairs={{0,4},{1,5},{2,6},{3,7},{4,0},{5,1},{6,2},{7,3},{8,12},{9,13},{10,... | collective-permute-start | bytes 1769480 | tf_op jit(solution)/shard_map/ppermute | solution.py:78
  27.4 14.2 %collective-permute-start.9 = (bf16[4,96,768]{2,1,0:T(8,128)(2,1)S(1)}, bf16[4,96,768]{2,1,0:T(8,128)(2,1)S(1)}, u32[]{:S(2)}, u32[]{:S(2)}) collective-permute-start(bf16[4,96,768]{2,1,0:T(8,128)(2,1)S(1)} %pad_maximum_fusion.rest_0_), channel_id=1, source_target_pairs={{0,1},{1,0},{2,3},{3,2},{4,5},{5,4},{6,7},{7,6},{8,9},{9,8},{10,11... | collective-permute-start | bytes 1769480 | tf_op jit(solution)/shard_map/ppermute | solution.py:78
  27.4 8.0 %collective-permute-start.11 = (bf16[1,96,384]{2,1,0:T(8,128)(2,1)S(1)}, bf16[1,96,384]{2,1,0:T(8,128)(2,1)S(1)}, u32[]{:S(2)}, u32[]{:S(2)}) collective-permute-start(bf16[1,96,384]{2,1,0:T(8,128)(2,1)S(1)} %bitcast.25), channel_id=1, source_target_pairs={{0,16},{1,17},{2,18},{3,19},{4,20},{5,21},{6,22},{7,23},{8,24},{9,... | collective-permute-start | bytes 221192 | tf_op jit(solution)/shard_map/ppermute | solution.py:78
  30.7 10.8 %collective-permute-start.10 = (bf16[1,96,768]{2,1,0:T(8,128)(2,1)S(1)}, bf16[1,96,768]{2,1,0:T(8,128)(2,1)S(1)}, u32[]{:S(2)}, u32[]{:S(2)}) collective-permute-start(bf16[1,96,768]{2,1,0:T(8,128)(2,1)S(1)} %convert_bitcast_fusion), channel_id=1, source_target_pairs={{0,16},{1,17},{2,18},{3,19},{4,20},{5,21},{6,22},{7,23},{8,24},{9,... | collective-permute-start | bytes 442376 | tf_op jit(solution)/shard_map/ppermute | solution.py:78
  41.7 10.2 %collective-permute-start.14 = (bf16[4,96,768]{2,1,0:T(8,128)(2,1)S(1)}, bf16[4,96,768]{2,1,0:T(8,128)(2,1)S(1)}, u32[]{:S(2)}, u32[]{:S(2)}) collective-permute-start(bf16[4,96,768]{2,1,0:T(8,128)(2,1)S(1)} %collective-permute-done.8.rest_1_), channel_id=1, source_target_pairs={{0,1},{1,0},{2,3},{3,2},{4,5},{5,4},{6,7},{7,6},{8,9},{9,8},{10,11... | collective-permute-start | bytes 1769480 | tf_op jit(solution)/shard_map/ppermute | solution.py:78
  41.8 10.1 %collective-permute-start.15 = (bf16[4,96,768]{2,1,0:T(8,128)(2,1)S(1)}, bf16[4,96,768]{2,1,0:T(8,128)(2,1)S(1)}, u32[]{:S(2)}, u32[]{:S(2)}) collective-permute-start(bf16[4,96,768]{2,1,0:T(8,128)(2,1)S(1)} %collective-permute-done.7.rest_2_), channel_id=1, source_target_pairs={{0,1},{1,0},{2,3},{3,2},{4,5},{5,4},{6,7},{7,6},{8,9},{9,8},{10,11... | collective-permute-start | bytes 1769480 | tf_op jit(solution)/shard_map/ppermute | solution.py:78
  42.3 9.1 %collective-permute-start.12 = (bf16[2,96,768]{2,1,0:T(8,128)(2,1)S(1)}, bf16[2,96,768]{2,1,0:T(8,128)(2,1)S(1)}, u32[]{:S(2)}, u32[]{:S(2)}) collective-permute-start(bf16[2,96,768]{2,1,0:T(8,128)(2,1)S(1)} %slice.52), channel_id=1, source_target_pairs={{0,2},{1,3},{2,0},{3,1},{4,6},{5,7},{6,4},{7,5},{8,10},{9,11},{10,... | collective-permute-start | bytes 884744 | tf_op jit(solution)/shard_map/ppermute | solution.py:78
  42.9 8.7 %collective-permute-start.13 = (bf16[2,96,768]{2,1,0:T(8,128)(2,1)S(1)}, bf16[2,96,768]{2,1,0:T(8,128)(2,1)S(1)}, u32[]{:S(2)}, u32[]{:S(2)}) collective-permute-start(bf16[2,96,768]{2,1,0:T(8,128)(2,1)S(1)} %slice.53), channel_id=1, source_target_pairs={{0,4},{1,5},{2,6},{3,7},{4,0},{5,1},{6,2},{7,3},{8,12},{9,13},{10,... | collective-permute-start | bytes 884744 | tf_op jit(solution)/shard_map/ppermute | solution.py:78
  43.4 8.4 %collective-permute-start.16 = (bf16[2,96,768]{2,1,0:T(8,128)(2,1)S(1)}, bf16[2,96,768]{2,1,0:T(8,128)(2,1)S(1)}, u32[]{:S(2)}, u32[]{:S(2)}) collective-permute-start(bf16[2,96,768]{2,1,0:T(8,128)(2,1)S(1)} %pad_maximum_fusion.3), channel_id=1, source_target_pairs={{0,8},{1,9},{2,10},{3,11},{4,12},{5,13},{6,14},{7,15},{8,0},{9,1},... | collective-permute-start | bytes 884744 | tf_op jit(solution)/shard_map/ppermute | solution.py:78
  52.5 19.7 %collective-permute-start.19 = (bf16[4,96,768]{2,1,0:T(8,128)(2,1)S(1)}, bf16[4,96,768]{2,1,0:T(8,128)(2,1)S(1)}, u32[]{:S(2)}, u32[]{:S(2)}) collective-permute-start(bf16[4,96,768]{2,1,0:T(8,128)(2,1)S(1)} %pad_maximum_fusion.1.rest_0_), channel_id=1, source_target_pairs={{0,2},{1,3},{2,0},{3,1},{4,6},{5,7},{6,4},{7,5},{8,10},{9,11},{10,... | collective-permute-start | bytes 1769480 | tf_op jit(solution)/shard_map/ppermute | solution.py:78
  54.1 18.2 %collective-permute-start.20 = (bf16[4,96,768]{2,1,0:T(8,128)(2,1)S(1)}, bf16[4,96,768]{2,1,0:T(8,128)(2,1)S(1)}, u32[]{:S(2)}, u32[]{:S(2)}) collective-permute-start(bf16[4,96,768]{2,1,0:T(8,128)(2,1)S(1)} %pad_maximum_fusion.1.rest_0_), channel_id=1, source_target_pairs={{0,4},{1,5},{2,6},{3,7},{4,0},{5,1},{6,2},{7,3},{8,12},{9,13},{10,... | collective-permute-start | bytes 1769480 | tf_op jit(solution)/shard_map/ppermute | solution.py:78
  55.6 16.7 %collective-permute-start.21 = (bf16[4,96,768]{2,1,0:T(8,128)(2,1)S(1)}, bf16[4,96,768]{2,1,0:T(8,128)(2,1)S(1)}, u32[]{:S(2)}, u32[]{:S(2)}) collective-permute-start(bf16[4,96,768]{2,1,0:T(8,128)(2,1)S(1)} %pad_maximum_fusion.1.rest_0_), channel_id=1, source_target_pairs={{0,1},{1,0},{2,3},{3,2},{4,5},{5,4},{6,7},{7,6},{8,9},{9,8},{10,11... | collective-permute-start | bytes 1769480 | tf_op jit(solution)/shard_map/ppermute | solution.py:78
  55.6 16.6 %collective-permute-start.23 = (bf16[4,96,384]{2,1,0:T(8,128)(2,1)S(1)}, bf16[4,96,384]{2,1,0:T(8,128)(2,1)S(1)}, u32[]{:S(2)}, u32[]{:S(2)}) collective-permute-start(bf16[4,96,384]{2,1,0:T(8,128)(2,1)S(1)} %pad_maximum_fusion.4), channel_id=1, source_target_pairs={{0,16},{1,17},{2,18},{3,19},{4,20},{5,21},{6,22},{7,23},{8,24},{9,... | collective-permute-start | bytes 884744 | tf_op jit(solution)/shard_map/ppermute | solution.py:78
  58.0 13.3 %collective-permute-start.22 = (bf16[2,96,384]{2,1,0:T(8,128)(2,1)S(1)}, bf16[2,96,384]{2,1,0:T(8,128)(2,1)S(1)}, u32[]{:S(2)}, u32[]{:S(2)}) collective-permute-start(bf16[2,96,384]{2,1,0:T(8,128)(2,1)S(1)} %pad_maximum_fusion.6), channel_id=1, source_target_pairs={{0,8},{1,9},{2,10},{3,11},{4,12},{5,13},{6,14},{7,15},{8,0},{9,1},... | collective-permute-start | bytes 442376 | tf_op jit(solution)/shard_map/ppermute | solution.py:78
  72.4 9.8 %collective-permute-start.26 = (bf16[4,96,768]{2,1,0:T(8,128)(2,1)S(1)}, bf16[4,96,768]{2,1,0:T(8,128)(2,1)S(1)}, u32[]{:S(2)}, u32[]{:S(2)}) collective-permute-start(bf16[4,96,768]{2,1,0:T(8,128)(2,1)S(1)} %collective-permute-done.20.rest_1_), channel_id=1, source_target_pairs={{0,1},{1,0},{2,3},{3,2},{4,5},{5,4},{6,7},{7,6},{8,9},{9,8},{10,11... | collective-permute-start | bytes 1769480 | tf_op jit(solution)/shard_map/ppermute | solution.py:78
  72.5 9.8 %collective-permute-start.27 = (bf16[4,96,768]{2,1,0:T(8,128)(2,1)S(1)}, bf16[4,96,768]{2,1,0:T(8,128)(2,1)S(1)}, u32[]{:S(2)}, u32[]{:S(2)}) collective-permute-start(bf16[4,96,768]{2,1,0:T(8,128)(2,1)S(1)} %collective-permute-done.19.rest_0_), channel_id=1, source_target_pairs={{0,1},{1,0},{2,3},{3,2},{4,5},{5,4},{6,7},{7,6},{8,9},{9,8},{10,11... | collective-permute-start | bytes 1769480 | tf_op jit(solution)/shard_map/ppermute | solution.py:78
  73.0 9.0 %collective-permute-start.24 = (bf16[2,96,768]{2,1,0:T(8,128)(2,1)S(1)}, bf16[2,96,768]{2,1,0:T(8,128)(2,1)S(1)}, u32[]{:S(2)}, u32[]{:S(2)}) collective-permute-start(bf16[2,96,768]{2,1,0:T(8,128)(2,1)S(1)} %slice.54), channel_id=1, source_target_pairs={{0,2},{1,3},{2,0},{3,1},{4,6},{5,7},{6,4},{7,5},{8,10},{9,11},{10,... | collective-permute-start | bytes 884744 | tf_op jit(solution)/shard_map/ppermute | solution.py:78
  73.5 8.7 %collective-permute-start.25 = (bf16[2,96,768]{2,1,0:T(8,128)(2,1)S(1)}, bf16[2,96,768]{2,1,0:T(8,128)(2,1)S(1)}, u32[]{:S(2)}, u32[]{:S(2)}) collective-permute-start(bf16[2,96,768]{2,1,0:T(8,128)(2,1)S(1)} %slice.55), channel_id=1, source_target_pairs={{0,4},{1,5},{2,6},{3,7},{4,0},{5,1},{6,2},{7,3},{8,12},{9,13},{10,... | collective-permute-start | bytes 884744 | tf_op jit(solution)/shard_map/ppermute | solution.py:78
  74.4 19.2 %collective-permute-start.33 = (bf16[8,96,384]{2,1,0:T(8,128)(2,1)S(1)}, bf16[8,96,384]{2,1,0:T(8,128)(2,1)S(1)}, u32[]{:S(2)}, u32[]{:S(2)}) collective-permute-start(bf16[8,96,384]{2,1,0:T(8,128)(2,1)S(1)} %get-tuple-element.539.rest_10_), channel_id=1, source_target_pairs={{0,8},{1,9},{2,10},{3,11},{4,12},{5,13},{6,14},{7,15},{8,0},{9,1},... | collective-permute-start | bytes 1769480 | tf_op jit(solution)/shard_map/ppermute | solution.py:78
  82.2 7.1 %collective-permute-start.28 = (bf16[2,96,768]{2,1,0:T(8,128)(2,1)S(1)}, bf16[2,96,768]{2,1,0:T(8,128)(2,1)S(1)}, u32[]{:S(2)}, u32[]{:S(2)}) collective-permute-start(bf16[2,96,768]{2,1,0:T(8,128)(2,1)S(1)} %collective-permute-done.24.rest_1_), channel_id=1, source_target_pairs={{0,1},{1,0},{2,3},{3,2},{4,5},{5,4},{6,7},{7,6},{8,9},{9,8},{10,11... | collective-permute-start | bytes 884744 | tf_op jit(solution)/shard_map/ppermute | solution.py:78
  82.3 7.2 %collective-permute-start.29 = (bf16[2,96,768]{2,1,0:T(8,128)(2,1)S(1)}, bf16[2,96,768]{2,1,0:T(8,128)(2,1)S(1)}, u32[]{:S(2)}, u32[]{:S(2)}) collective-permute-start(bf16[2,96,768]{2,1,0:T(8,128)(2,1)S(1)} %collective-permute-done.25.rest_2_), channel_id=1, source_target_pairs={{0,1},{1,0},{2,3},{3,2},{4,5},{5,4},{6,7},{7,6},{8,9},{9,8},{10,11... | collective-permute-start | bytes 884744 | tf_op jit(solution)/shard_map/ppermute | solution.py:78
  82.8 10.9 %collective-permute-start.30 = (bf16[4,96,384]{2,1,0:T(8,128)(2,1)S(1)}, bf16[4,96,384]{2,1,0:T(8,128)(2,1)S(1)}, u32[]{:S(2)}, u32[]{:S(2)}) collective-permute-start(bf16[4,96,384]{2,1,0:T(8,128)(2,1)S(1)} %get-tuple-element.529.rest_0_), channel_id=1, source_target_pairs={{0,2},{1,3},{2,0},{3,1},{4,6},{5,7},{6,4},{7,5},{8,10},{9,11},{10,... | collective-permute-start | bytes 884744 | tf_op jit(solution)/shard_map/ppermute | solution.py:78
  84.2 9.4 %collective-permute-start.31 = (bf16[4,96,384]{2,1,0:T(8,128)(2,1)S(1)}, bf16[4,96,384]{2,1,0:T(8,128)(2,1)S(1)}, u32[]{:S(2)}, u32[]{:S(2)}) collective-permute-start(bf16[4,96,384]{2,1,0:T(8,128)(2,1)S(1)} %get-tuple-element.529.rest_0_), channel_id=1, source_target_pairs={{0,4},{1,5},{2,6},{3,7},{4,0},{5,1},{6,2},{7,3},{8,12},{9,13},{10,... | collective-permute-start | bytes 884744 | tf_op jit(solution)/shard_map/ppermute | solution.py:78
  93.7 7.0 %collective-permute-start.36 = (bf16[4,96,384]{2,1,0:T(8,128)(2,1)S(1)}, bf16[4,96,384]{2,1,0:T(8,128)(2,1)S(1)}, u32[]{:S(2)}, u32[]{:S(2)}) collective-permute-start(bf16[4,96,384]{2,1,0:T(8,128)(2,1)S(1)} %collective-permute-done.31.rest_1_), channel_id=1, source_target_pairs={{0,1},{1,0},{2,3},{3,2},{4,5},{5,4},{6,7},{7,6},{8,9},{9,8},{10,11... | collective-permute-start | bytes 884744 | tf_op jit(solution)/shard_map/ppermute | solution.py:78
  121.0 15.6 %collective-permute-start.46 = (bf16[4,96,768]{2,1,0:T(8,128)(2,1)S(1)}, bf16[4,96,768]{2,1,0:T(8,128)(2,1)S(1)}, u32[]{:S(2)}, u32[]{:S(2)}) collective-permute-start(bf16[4,96,768]{2,1,0:T(8,128)(2,1)S(1)} %get-tuple-element.600), channel_id=1, source_target_pairs={{0,8},{1,9},{2,10},{3,11},{4,12},{5,13},{6,14},{7,15},{8,0},{9,1},... | collective-permute-start | bytes 1769480 | tf_op jit(solution)/shard_map/ppermute | solution.py:78
  126.6 10.0 %collective-permute-start.44 = (bf16[2,96,768]{2,1,0:T(8,128)(2,1)S(1)}, bf16[2,96,768]{2,1,0:T(8,128)(2,1)S(1)}, u32[]{:S(2)}, u32[]{:S(2)}) collective-permute-start(bf16[2,96,768]{2,1,0:T(8,128)(2,1)S(1)} %get-tuple-element.598), channel_id=1, source_target_pairs={{0,2},{1,3},{2,0},{3,1},{4,6},{5,7},{6,4},{7,5},{8,10},{9,11},{10,... | collective-permute-start | bytes 884744 | tf_op jit(solution)/shard_map/ppermute | solution.py:78
  128.1 8.7 %collective-permute-start.45 = (bf16[2,96,768]{2,1,0:T(8,128)(2,1)S(1)}, bf16[2,96,768]{2,1,0:T(8,128)(2,1)S(1)}, u32[]{:S(2)}, u32[]{:S(2)}) collective-permute-start(bf16[2,96,768]{2,1,0:T(8,128)(2,1)S(1)} %get-tuple-element.599), channel_id=1, source_target_pairs={{0,4},{1,5},{2,6},{3,7},{4,0},{5,1},{6,2},{7,3},{8,12},{9,13},{10,... | collective-permute-start | bytes 884744 | tf_op jit(solution)/shard_map/ppermute | solution.py:78
  137.3 18.9 %collective-permute-start.47 = (bf16[4,96,768]{2,1,0:T(8,128)(2,1)S(1)}, bf16[4,96,768]{2,1,0:T(8,128)(2,1)S(1)}, u32[]{:S(2)}, u32[]{:S(2)}) collective-permute-start(bf16[4,96,768]{2,1,0:T(8,128)(2,1)S(1)} %get-tuple-element.641), channel_id=1, source_target_pairs={{0,2},{1,3},{2,0},{3,1},{4,6},{5,7},{6,4},{7,5},{8,10},{9,11},{10,... | collective-permute-start | bytes 1769480 | tf_op jit(solution)/shard_map/ppermute | solution.py:78
  138.6 17.6 %collective-permute-start.48 = (bf16[4,96,768]{2,1,0:T(8,128)(2,1)S(1)}, bf16[4,96,768]{2,1,0:T(8,128)(2,1)S(1)}, u32[]{:S(2)}, u32[]{:S(2)}) collective-permute-start(bf16[4,96,768]{2,1,0:T(8,128)(2,1)S(1)} %get-tuple-element.642), channel_id=1, source_target_pairs={{0,4},{1,5},{2,6},{3,7},{4,0},{5,1},{6,2},{7,3},{8,12},{9,13},{10,... | collective-permute-start | bytes 1769480 | tf_op jit(solution)/shard_map/ppermute | solution.py:78
  139.7 16.5 %collective-permute-start.51 = (bf16[4,96,768]{2,1,0:T(8,128)(2,1)S(1)}, bf16[4,96,768]{2,1,0:T(8,128)(2,1)S(1)}, u32[]{:S(2)}, u32[]{:S(2)}) collective-permute-start(bf16[4,96,768]{2,1,0:T(8,128)(2,1)S(1)} %get-tuple-element.645), channel_id=1, source_target_pairs={{0,8},{1,9},{2,10},{3,11},{4,12},{5,13},{6,14},{7,15},{8,0},{9,1},... | collective-permute-start | bytes 1769480 | tf_op jit(solution)/shard_map/ppermute | solution.py:78
  140.4 14.6 %collective-permute-start.49 = (bf16[96,768]{1,0:T(8,128)(2,1)S(1)}, bf16[96,768]{1,0:T(8,128)(2,1)S(1)}, u32[]{:S(2)}, u32[]{:S(2)}) collective-permute-start(bf16[96,768]{1,0:T(8,128)(2,1)S(1)} %get-tuple-element.643), channel_id=1, source_target_pairs={{0,2},{1,3},{2,0},{3,1},{4,6},{5,7},{6,4},{7,5},{8,10},{9,11},{10,... | collective-permute-start | bytes 442376 | tf_op jit(solution)/shard_map/ppermute | solution.py:78
  141.9 14.4 %collective-permute-start.50 = (bf16[96,768]{1,0:T(8,128)(2,1)S(1)}, bf16[96,768]{1,0:T(8,128)(2,1)S(1)}, u32[]{:S(2)}, u32[]{:S(2)}) collective-permute-start(bf16[96,768]{1,0:T(8,128)(2,1)S(1)} %get-tuple-element.644), channel_id=1, source_target_pairs={{0,4},{1,5},{2,6},{3,7},{4,0},{5,1},{6,2},{7,3},{8,12},{9,13},{10,... | collective-permute-start | bytes 442376 | tf_op jit(solution)/shard_map/ppermute | solution.py:78
  156.8 10.6 %collective-permute-start.52 = (bf16[2,8,96,768]{3,2,1,0:T(8,128)(2,1)S(1)}, bf16[2,8,96,768]{3,2,1,0:T(8,128)(2,1)S(1)}, u32[]{:S(2)}, u32[]{:S(2)}) collective-permute-start(bf16[2,8,96,768]{3,2,1,0:T(8,128)(2,1)S(1)} %get-tuple-element.664), channel_id=1, source_target_pairs={{0,1},{1,0},{2,3},{3,2},{4,5},{5,4},{6,7},{7,6},{8,9},{9,8},{10,11... | collective-permute-start | bytes 7077896 | tf_op jit(solution)/shard_map/ppermute | solution.py:78
  156.9 9.4 %collective-permute-start.53 = (bf16[2,96,768]{2,1,0:T(8,128)(2,1)S(1)}, bf16[2,96,768]{2,1,0:T(8,128)(2,1)S(1)}, u32[]{:S(2)}, u32[]{:S(2)}) collective-permute-start(bf16[2,96,768]{2,1,0:T(8,128)(2,1)S(1)} %get-tuple-element.665), channel_id=1, source_target_pairs={{0,2},{1,3},{2,0},{3,1},{4,6},{5,7},{6,4},{7,5},{8,10},{9,11},{10,... | collective-permute-start | bytes 884744 | tf_op jit(solution)/shard_map/ppermute | solution.py:78
  157.5 9.1 %collective-permute-start.54 = (bf16[2,96,768]{2,1,0:T(8,128)(2,1)S(1)}, bf16[2,96,768]{2,1,0:T(8,128)(2,1)S(1)}, u32[]{:S(2)}, u32[]{:S(2)}) collective-permute-start(bf16[2,96,768]{2,1,0:T(8,128)(2,1)S(1)} %get-tuple-element.666), channel_id=1, source_target_pairs={{0,4},{1,5},{2,6},{3,7},{4,0},{5,1},{6,2},{7,3},{8,12},{9,13},{10,... | collective-permute-start | bytes 884744 | tf_op jit(solution)/shard_map/ppermute | solution.py:78
  158.6 8.8 %collective-permute-start.55 = (bf16[2,96,768]{2,1,0:T(8,128)(2,1)S(1)}, bf16[2,96,768]{2,1,0:T(8,128)(2,1)S(1)}, u32[]{:S(2)}, u32[]{:S(2)}) collective-permute-start(bf16[2,96,768]{2,1,0:T(8,128)(2,1)S(1)} %get-tuple-element.667), channel_id=1, source_target_pairs={{0,8},{1,9},{2,10},{3,11},{4,12},{5,13},{6,14},{7,15},{8,0},{9,1},... | collective-permute-start | bytes 884744 | tf_op jit(solution)/shard_map/ppermute | solution.py:78
  167.7 10.7 %collective-permute-start.57 = (bf16[2,96,768]{2,1,0:T(8,128)(2,1)S(1)}, bf16[2,96,768]{2,1,0:T(8,128)(2,1)S(1)}, u32[]{:S(2)}, u32[]{:S(2)}) collective-permute-start(bf16[2,96,768]{2,1,0:T(8,128)(2,1)S(1)} %get-tuple-element.677), channel_id=1, source_target_pairs={{0,2},{1,3},{2,0},{3,1},{4,6},{5,7},{6,4},{7,5},{8,10},{9,11},{10,... | collective-permute-start | bytes 884744 | tf_op jit(solution)/shard_map/ppermute | solution.py:78
  169.3 9.2 %collective-permute-start.58 = (bf16[2,96,768]{2,1,0:T(8,128)(2,1)S(1)}, bf16[2,96,768]{2,1,0:T(8,128)(2,1)S(1)}, u32[]{:S(2)}, u32[]{:S(2)}) collective-permute-start(bf16[2,96,768]{2,1,0:T(8,128)(2,1)S(1)} %get-tuple-element.678), channel_id=1, source_target_pairs={{0,4},{1,5},{2,6},{3,7},{4,0},{5,1},{6,2},{7,3},{8,12},{9,13},{10,... | collective-permute-start | bytes 884744 | tf_op jit(solution)/shard_map/ppermute | solution.py:78
  170.2 8.3 %collective-permute-start.59 = (bf16[96,768]{1,0:T(8,128)(2,1)S(1)}, bf16[96,768]{1,0:T(8,128)(2,1)S(1)}, u32[]{:S(2)}, u32[]{:S(2)}) collective-permute-start(bf16[96,768]{1,0:T(8,128)(2,1)S(1)} %get-tuple-element.679), channel_id=1, source_target_pairs={{0,16},{1,17},{2,18},{3,19},{4,20},{5,21},{6,22},{7,23},{8,24},{9,... | collective-permute-start | bytes 442376 | tf_op jit(solution)/shard_map/ppermute | solution.py:78
  178.8 14.4 %collective-permute-start.60 = (bf16[4,96,768]{2,1,0:T(8,128)(2,1)S(1)}, bf16[4,96,768]{2,1,0:T(8,128)(2,1)S(1)}, u32[]{:S(2)}, u32[]{:S(2)}) collective-permute-start(bf16[4,96,768]{2,1,0:T(8,128)(2,1)S(1)} %get-tuple-element.688), channel_id=1, source_target_pairs={{0,2},{1,3},{2,0},{3,1},{4,6},{5,7},{6,4},{7,5},{8,10},{9,11},{10,... | collective-permute-start | bytes 1769480 | tf_op jit(solution)/shard_map/ppermute | solution.py:78
  179.9 14.4 %collective-permute-start.61 = (bf16[4,96,768]{2,1,0:T(8,128)(2,1)S(1)}, bf16[4,96,768]{2,1,0:T(8,128)(2,1)S(1)}, u32[]{:S(2)}, u32[]{:S(2)}) collective-permute-start(bf16[4,96,768]{2,1,0:T(8,128)(2,1)S(1)} %get-tuple-element.689), channel_id=1, source_target_pairs={{0,4},{1,5},{2,6},{3,7},{4,0},{5,1},{6,2},{7,3},{8,12},{9,13},{10,... | collective-permute-start | bytes 1769480 | tf_op jit(solution)/shard_map/ppermute | solution.py:78
  180.7 8.6 %collective-permute-start.62 = (bf16[96,768]{1,0:T(8,128)(2,1)S(1)}, bf16[96,768]{1,0:T(8,128)(2,1)S(1)}, u32[]{:S(2)}, u32[]{:S(2)}) collective-permute-start(bf16[96,768]{1,0:T(8,128)(2,1)S(1)} %get-tuple-element.690), channel_id=1, source_target_pairs={{0,16},{1,17},{2,18},{3,19},{4,20},{5,21},{6,22},{7,23},{8,24},{9,... | collective-permute-start | bytes 442376 | tf_op jit(solution)/shard_map/ppermute | solution.py:78
  194.6 8.4 %collective-permute-start.64 = (bf16[2,96,768]{2,1,0:T(8,128)(2,1)S(1)}, bf16[2,96,768]{2,1,0:T(8,128)(2,1)S(1)}, u32[]{:S(2)}, u32[]{:S(2)}) collective-permute-start(bf16[2,96,768]{2,1,0:T(8,128)(2,1)S(1)} %get-tuple-element.697), channel_id=1, source_target_pairs={{0,8},{1,9},{2,10},{3,11},{4,12},{5,13},{6,14},{7,15},{8,0},{9,1},... | collective-permute-start | bytes 884744 | tf_op jit(solution)/shard_map/ppermute | solution.py:78
  204.5 7.0 %collective-permute-start.66 = (bf16[96,768]{1,0:T(8,128)(2,1)S(1)}, bf16[96,768]{1,0:T(8,128)(2,1)S(1)}, u32[]{:S(2)}, u32[]{:S(2)}) collective-permute-start(bf16[96,768]{1,0:T(8,128)(2,1)S(1)} %get-tuple-element.703), channel_id=1, source_target_pairs={{0,16},{1,17},{2,18},{3,19},{4,20},{5,21},{6,22},{7,23},{8,24},{9,... | collective-permute-start | bytes 442376 | tf_op jit(solution)/shard_map/ppermute | solution.py:78
  (36 other events, 270.8 us)

commit v10 on v9

--- a/solution.py
+++ b/solution.py
@@ -953,22 +953,29 @@
             [sum_a, sum_d, line_u, sum_s],
             [sum_a, sum_d, line_u, sum_s],
         )[0]
-        step((), None, [sum_a, sum_d], [sum_a, sum_d])
-        step((), None, [sum_a, line_u, sum_s], [sum_a, line_u, sum_s])
+        step((), None, [sum_a, sum_d, sum_s], [sum_a, sum_s])
+        step((), None, [sum_a, line_u, sum_s], [sum_a, sum_d, line_u, sum_s])
         line_a = Job(net.scatter_line(*sum_a.value))
-        step((), None, [line_a, sum_s], [line_a, sum_s])
         step((), None, [line_a, sum_s], [sum_s])
         step((), None, [sum_s], [line_a, sum_s])
 
-        packed = sum_s.value
-        down_grad, up_grad = (kept + last.astype(f32) for kept, last in (sum_d.value, line_u.value))
+        def finish(packed, down, up, ranges):
+            own = lax.dynamic_slice_in_dim(packed, blocks + lane, 1)
+            shared = packed[2 * blocks : 2 * blocks + 6]
+            return (
+                down[0] + down[1].astype(f32),
+                up[0] + up[1].astype(f32),
+                jnp.concatenate([own[:, :cols], own[:, 2 * cols : 3 * cols]], 0),
+                lax.dynamic_slice_in_dim(packed, lane, 1)[0],
+                [shared[n] for n in range(6)],
+                ema_decay * ranges + (1.0 - ema_decay) * packed[2 * blocks + 6, 0:512:128],
+            )
+
+        down_grad, up_grad, qv_bias_grad, up_bias_grad, shared, new_ranges = step(
+            (sum_s.value, sum_d.value, line_u.value, act_ranges), finish, [line_a], [line_a]
+        )
         down_grad = down_grad.T
         qkv_grad, out_grad = attn_grads(*line_a.value)
-        own = lax.dynamic_slice_in_dim(packed, blocks + lane, 1)
-        shared = packed[2 * blocks : 2 * blocks + 6]
-        qv_bias_grad = jnp.concatenate([own[:, :cols], own[:, 2 * cols : 3 * cols]], 0)
-        up_bias_grad = lax.dynamic_slice_in_dim(packed, lane, 1)[0]
-        new_ranges = ema_decay * act_ranges + (1.0 - ema_decay) * packed[2 * blocks + 6, 0:512:128]
         return (
             layer_out,
             tokens_grad,

time: 215 us -> 215 us (level)
  transfers between devices with their start and end apart: 69 -> 69, of which waited for: 34 -> 34; matrix products, arithmetic and copies ran while one was open for 1% -> 2% of each run, Pallas kernels for 25% -> 25%
where the time goes in v10:
time: 215 us
  waiting for transfers between devices  69.6 us (32%)
  Pallas kernels  69.5 us (32%)
  starting transfers between devices  64.3 us (30%)
  local copies, waits for them, and re-layouts  5.23 us (2%)
  other arithmetic  4.32 us (2%)
    ppermute x69, waiting for transfers between devices, step(): lax.ppermute(v, ALL, perm)  69.6 us
    pallas_call x11, Pallas kernels, step(): outs = run(*ins) if run else ins  66 us
    ppermute x69, starting transfers between devices, step(): lax.ppermute(v, ALL, perm)  64.3 us
  transfers between devices with their start and end apart: 69, of which 34 were waited for; matrix products, arithmetic and copies ran while one was open for 2% of the time, Pallas kernels for 25%

profile of v10, /device:TPU:0, one launch (start us, length us, event | category | flops | bytes accessed | tf_op | source)
XLA Modules:
  0.0 214.8 jit_solution(10500266277494838711)
XLA Ops:
  5.0 4.1 %collective-permute-start = (bf16[1,96,768]{2,1,0:T(8,128)(2,1)S(1)}, bf16[1,96,768]{2,1,0:T(8,128)(2,1)S(1)}, u32[]{:S(2)}, u32[]{:S(2)}) collective-permute-start(bf16[1,96,768]{2,1,0:T(8,128)(2,1)S(1)} %bitcast.18), channel_id=1, source_target_pairs={{0,16},{1,17},{2,18},{3,19},{4,20},{5,21},{6,22},{7,23},{8,24},{9,... | collective-permute-start | bytes 442376 | tf_op jit(solution)/shard_map/ppermute | solution.py:78
  9.1 1.5 collective-permute-start.1
  10.6 1.5 collective-permute-start.2
  12.7 3.1 %collective-permute-done.3 = f32[1,1408]{1,0:T(1,128)S(1)} collective-permute-done((f32[1,1408]{1,0:T(1,128)S(1)}, f32[1,1408]{1,0:T(1,128)S(1)}, u32[]{:S(2)}, u32[]{:S(2)}) %collective-permute-start.3) | collective-permute-done | bytes 5664 | tf_op jit(solution)/shard_map/ppermute | solution.py:78
  16.2 1.3 collective-permute-start.4
  19.6 2.2 %collective-permute-done.5 = bf16[1,96,384]{2,1,0:T(8,128)(2,1)S(1)} collective-permute-done((bf16[1,96,384]{2,1,0:T(8,128)(2,1)S(1)}, bf16[1,96,384]{2,1,0:T(8,128)(2,1)S(1)}, u32[]{:S(2)}, u32[]{:S(2)}) %collective-permute-start.5) | collective-permute-done | bytes 73760 | tf_op jit(solution)/shard_map/ppermute | solution.py:78
  21.8 2.6 %collective-permute-done.4 = bf16[2,96,768]{2,1,0:T(8,128)(2,1)S(1)} collective-permute-done((bf16[2,96,768]{2,1,0:T(8,128)(2,1)S(1)}, bf16[2,96,768]{2,1,0:T(8,128)(2,1)S(1)}, u32[]{:S(2)}, u32[]{:S(2)}) %collective-permute-start.4) | collective-permute-done | bytes 294944 | tf_op jit(solution)/shard_map/ppermute | solution.py:78
  24.5 1.3 collective-permute-start.7
  25.9 1.5 collective-permute-start.8
  27.4 3.3 %collective-permute-start.11 = (bf16[1,96,384]{2,1,0:T(8,128)(2,1)S(1)}, bf16[1,96,384]{2,1,0:T(8,128)(2,1)S(1)}, u32[]{:S(2)}, u32[]{:S(2)}) collective-permute-start(bf16[1,96,384]{2,1,0:T(8,128)(2,1)S(1)} %bitcast.24), channel_id=1, source_target_pairs={{0,16},{1,17},{2,18},{3,19},{4,20},{5,21},{6,22},{7,23},{8,24},{9,... | collective-permute-start | bytes 221192 | tf_op jit(solution)/shard_map/ppermute | solution.py:78
  31.4 4.0 %collective-permute-done.11 = bf16[1,96,384]{2,1,0:T(8,128)(2,1)S(1)} collective-permute-done((bf16[1,96,384]{2,1,0:T(8,128)(2,1)S(1)}, bf16[1,96,384]{2,1,0:T(8,128)(2,1)S(1)}, u32[]{:S(2)}, u32[]{:S(2)}) %collective-permute-start.11) | collective-permute-done | bytes 73760 | tf_op jit(solution)/shard_map/ppermute | solution.py:78
  35.4 6.1 %collective-permute-done.10 = bf16[1,96,768]{2,1,0:T(8,128)(2,1)S(1)} collective-permute-done((bf16[1,96,768]{2,1,0:T(8,128)(2,1)S(1)}, bf16[1,96,768]{2,1,0:T(8,128)(2,1)S(1)}, u32[]{:S(2)}, u32[]{:S(2)}) %collective-permute-start.10) | collective-permute-done | bytes 147488 | tf_op jit(solution)/shard_map/ppermute | solution.py:78
  44.6 6.7 %collective-permute-done.12.rest_3_ = bf16[2,96,768]{2,1,0:T(8,128)(2,1)S(1)} collective-permute-done((bf16[2,96,768]{2,1,0:T(8,128)(2,1)S(1)}, bf16[2,96,768]{2,1,0:T(8,128)(2,1)S(1)}, u32[]{:S(2)}, u32[]{:S(2)}) %collective-permute-start.12) | collective-permute-done | bytes 294944 | tf_op jit(solution)/shard_map/ppermute | solution.py:78
  52.5 1.6 collective-permute-start.19
  54.1 1.5 collective-permute-start.20
  55.6 2.4 %collective-permute-start.23 = (bf16[4,96,384]{2,1,0:T(8,128)(2,1)S(1)}, bf16[4,96,384]{2,1,0:T(8,128)(2,1)S(1)}, u32[]{:S(2)}, u32[]{:S(2)}) collective-permute-start(bf16[4,96,384]{2,1,0:T(8,128)(2,1)S(1)} %pad_maximum_fusion.4), channel_id=1, source_target_pairs={{0,16},{1,17},{2,18},{3,19},{4,20},{5,21},{6,22},{7,23},{8,24},{9,... | collective-permute-start | bytes 884744 | tf_op jit(solution)/shard_map/ppermute | solution.py:78
  58.0 1.7 collective-permute-start.22
  59.8 11.5 %attn_forward.1 = (bf16[4,512,640]{2,1,0:T(8,128)(2,1)S(1)}, f32[4,8,512]{2,1,0:T(8,128)S(1)}, bf16[768,512]{1,0:T(8,128)(2,1)S(1)}, bf16[4,512,256]{2,1,0:T(8,1...) custom-call(f32[4]{0:T(128)S(1)} %copy-done.7, ...), custom_call_target="tpu_custom_call" | custom-call | flops 9663676416 | bytes 14155776 | tf_op jit(solution)/shard_map/attn_forward/pallas_call | solution.py:79
  75.2 3.3 %attn_finish.1 = (f32[512,768]{1,0:T(8,128)S(1)}, f32[512,1]{1,0:T(8,128)S(1)}, f32[512,768]{1,0:T(8,128)S(1)}, f32[512,768]{1,0:T(8,128)S(1)}, bf16[512,768]{1,...) custom-call(f32[4]{0:T(128)S(1)} %copy-done.7, ...), custom_call_target="tpu_custom_call" | custom-call | flops 4831838208 | bytes 9437184 | tf_op jit(solution)/shard_map/attn_finish/pallas_call | solution.py:79
  78.4 3.5 %collective-permute-done.24.rest_1_ = bf16[2,96,768]{2,1,0:T(8,128)(2,1)S(1)} collective-permute-done((bf16[2,96,768]{2,1,0:T(8,128)(2,1)S(1)}, bf16[2,96,768]{2,1,0:T(8,128)(2,1)S(1)}, u32[]{:S(2)}, u32[]{:S(2)}) %collective-permute-start.24) | collective-permute-done | bytes 294944 | tf_op jit(solution)/shard_map/ppermute | solution.py:78
  82.8 1.5 collective-permute-start.30
  85.1 4.2 %up_forward_0.1 = (bf16[2,512,768]{2,1,0:T(8,128)(2,1)S(1)}, f32[2,512,768]{2,1,0:T(8,128)S(1)}, f32[8,128]{1,0:T(8,128)S(1)}, bf16[2,768,768]{2,1,0:T(8,128)(2,1)S(1)}) custom-call(f32[4]{0:T(128)S(1)} %copy-done.7, bf16[512,768]{1,0:T(8,128)(2,1)S(1)} %get-tuple-element.497.mid_low, f32[4,1,1408]{2,1,0:T(1,128)S(1)} %bitcast.29, ...), custom_call_target="tpu_custom_call" | custom-call | flops 4831838208 | bytes 9437184 | tf_op jit(solution)/shard_map/up_forward_0/pallas_call | solution.py:79
  89.5 4.2 %up_forward_2.1 = (bf16[2,512,768]{2,1,0:T(8,128)(2,1)S(1)}, f32[2,512,768]{2,1,0:T(8,128)S(1)}, f32[8,128]{1,0:T(8,128)S(1)}, bf16[2,768,768]{2,1,0:T(8,128)(2,1)S(1)}) custom-call(f32[4]{0:T(128)S(1)} %copy-done.7, bf16[512,768]{1,0:T(8,128)(2,1)S(1)} %get-tuple-element.497.mid_low, f32[4,1,1408]{2,1,0:T(1,128)S(1)} %bitcast.30, ...), custom_call_target="tpu_custom_call" | custom-call | flops 4831838208 | bytes 9437184 | tf_op jit(solution)/shard_map/up_forward_2/pallas_call | solution.py:79
  96.0 4.5 %collective-permute-done.34.rest_3_ = bf16[2,96,384]{2,1,0:T(8,128)(2,1)S(1)} collective-permute-done((bf16[2,96,384]{2,1,0:T(8,128)(2,1)S(1)}, bf16[2,96,384]{2,1,0:T(8,128)(2,1)S(1)}, u32[]{:S(2)}, u32[]{:S(2)}) %collective-permute-start.34) | collective-permute-done | bytes 147488 | tf_op jit(solution)/shard_map/ppermute | solution.py:78
  101.8 2.0 collective-permute-done.38.rest_8_
  104.1 9.1 %down_both.1 = (bf16[512,768]{1,0:T(8,128)(2,1)}, f32[512,768]{1,0:T(8,128)S(1)}, bf16[768,512]{1,0:T(8,128)(2,1)S(1)}, f32[8,768]{1,0:T(8,128)S(1)}, bf16[4,512...) custom-call(bf16[2,512,768]{2,1,0:T(8,128)(2,1)S(1)} %get-tuple-element.573.act0.rest_0_, ...), custom_call_target="tpu_custom_call" | custom-call | flops 4831838208 | bytes 18874368 | tf_op jit(solution)/shard_map/down_both/pallas_call | solution.py:79
  113.2 2.7 %down_grad.1 = (bf16[2,8,96,768]{3,2,1,0:T(8,128)(2,1)S(1)}, bf16[2,8,96,768]{3,2,1,0:T(8,128)(2,1)S(1)}) custom-call(bf16[768,512]{1,0:T(8,128)(2,1)S(1)} %get-tuple-element.572.left_t, bf16[2,512,768]{2,1,0:T(8,128)(2,1)S(1)} %get-tuple-element.573.act0.rest_0_, bf16[2,512,768]{2,1,0:T(8,128)(2,1)S(1)} %get-tuple-element.574.act1.rest_1_), custom_call_target="tpu_custom_call" | custom-call | flops 2415919104 | bytes 4718592 | tf_op jit(solution)/shard_map/down_grad/pallas_call | solution.py:79
  116.1 2.7 %up_grad.1 = (bf16[2,8,96,768]{3,2,1,0:T(8,128)(2,1)S(1)}, bf16[2,8,96,768]{3,2,1,0:T(8,128)(2,1)S(1)}) custom-call(bf16[768,512]{1,0:T(8,128)(2,1)S(1)} %get-tuple-element.576.left_t, bf16[4,512,768]{2,1,0:T(8,128)(2,1)S(1)} %get-tuple-element.585.rest_0_.grad_up), custom_call_target="tpu_custom_call" | custom-call | flops 2415919104 | bytes 4718592 | tf_op jit(solution)/shard_map/up_grad/pallas_call | solution.py:79
  118.8 1.7 collective-permute-done.42.got
  121.7 4.7 %mid_backward.1 = (f32[512,768]{1,0:T(8,128)S(1)}, bf16[512,768]{1,0:T(8,128)(2,1)S(1)}, bf16[768,512]{1,0:T(8,128)(2,1)S(1)}, f32[8,768]{1,0:T(8,128)S(1)}) custom-call(bf16[4,512,768]{2,1,0:T(8,128)(2,1)S(1)} %get-tuple-element.585.rest_0_.grad_up, f32[512,768]{1,0:T(8,128)S(1)} %get-tuple-element.586.grad_second, ...), custom_call_target="tpu_custom_call" | custom-call | flops 3221225472 | bytes 14155776 | tf_op jit(solution)/shard_map/mid_backward/pallas_call | solution.py:79
  126.6 1.6 collective-permute-start.44
  129.0 6.9 %attn_backward.1 = (bf16[2,512,640]{2,1,0:T(8,128)(2,1)S(1)}, f32[4,1,640]{2,1,0:T(1,128)S(1)}) custom-call(s32[1]{0:T(128)S(6)} %copy.37.longs, s32[12]{0:T(128)S(1)} %copy-done.14, bf16[4,512,640]{2,1,0:T(8,128)(2,1)S(1)} %get-tuple-element.637.qkv, f32[4,8,512]{2,1,0:T(8,128)S(1)} %get-tuple-element.638.lse, ...), custom_call_target="tpu_custom_call" | custom-call | flops 4831838208 | bytes 9437184 | tf_op jit(solution)/shard_map/attn_backward/pallas_call | solution.py:79
  137.3 1.3 collective-permute-start.47
  140.4 1.5 collective-permute-start.49
  142.8 11.7 %attn_backward_last.1 = (bf16[2,512,640]{2,1,0:T(8,128)(2,1)S(1)}, bf16[2,8,96,768]{3,2,1,0:T(8,128)(2,1)S(1)}, bf16[2,8,96,768]{3,2,1,0:T(8,128)(2,1)S(1)}, f32[16,768]{1,0:T(8,128)S(1)}) custom-call(s32[1]{0:T(128)S(6)} %copy.37.longs, s32[12]{0:T(128)S(1)} %copy-done.14, bf16[4,512,640]{2,1,0:T(8,128)(2,1)S(1)} %get-tuple-element.637.qkv, ...), custom_call_target="tpu_custom_call" | custom-call | flops 9663676416 | bytes 9437184 | tf_op jit(solution)/shard_map/attn_backward_last/pallas_call | solution.py:79
  159.6 5.1 %token_backward.1 = bf16[512,768]{1,0:T(8,128)(2,1)} custom-call(f32[4]{0:T(128)S(1)} %copy-done.7, bf16[2,512,640]{2,1,0:T(8,128)(2,1)S(1)} %get-tuple-element.676.grads_0, bf16[2,512,640]{2,1,0:T(8,128)(2,1)S(1)} %get-tuple-element.677.rest_3_.grads_1, f32[512,768]{1,0:T(8,128)S(1)} %get-tuple-element.678.grad_first, bf16[512,768]{1,0:T(8,128)(2,1)S(1)} %copy-done, ...), custom_call_target="tpu_custom_call" | custom-call | flops 2415919104 | bytes 9437184 | tf_op jit(solution)/shard_map/token_backward/pallas_call | solution.py:79
  164.7 1.5 collective-permute-done.53.in_x
  167.8 1.6 collective-permute-start.57
  171.0 3.3 %collective-permute-done.59 = f32[16,768]{1,0:T(8,128)S(1)} collective-permute-done((f32[16,768]{1,0:T(8,128)S(1)}, f32[16,768]{1,0:T(8,128)S(1)}, u32[]{:S(2)}, u32[]{:S(2)}) %collective-permute-start.59) | collective-permute-done | bytes 49184 | tf_op jit(solution)/shard_map/ppermute | solution.py:78
  174.3 1.4 collective-permute-done.57.from_x
  178.9 3.1 %collective-permute-start.62 = (bf16[96,768]{1,0:T(8,128)(2,1)S(1)}, bf16[96,768]{1,0:T(8,128)(2,1)S(1)}, u32[]{:S(2)}, u32[]{:S(2)}) collective-permute-start(bf16[96,768]{1,0:T(8,128)(2,1)S(1)} %get-tuple-element.708), channel_id=1, source_target_pairs={{0,16},{1,17},{2,18},{3,19},{4,20},{5,21},{6,22},{7,23},{8,24},{9,... | collective-permute-start | bytes 442376 | tf_op jit(solution)/shard_map/ppermute | solution.py:78
  182.1 2.9 %collective-permute-start.64 = (f32[16,768]{1,0:T(8,128)S(1)}, f32[16,768]{1,0:T(8,128)S(1)}, u32[]{:S(2)}, u32[]{:S(2)}) collective-permute-start(f32[16,768]{1,0:T(8,128)S(1)} %add_select_fusion.3), channel_id=1, source_target_pairs={{0,16},{1,17},{2,18},{3,19},{4,20},{5,21},{6,22},{7,23},{8,24},{9,... | collective-permute-start | bytes 147464 | tf_op jit(solution)/shard_map/ppermute | solution.py:78
  185.0 7.1 %collective-permute-done.62 = bf16[96,768]{1,0:T(8,128)(2,1)S(1)} collective-permute-done((bf16[96,768]{1,0:T(8,128)(2,1)S(1)}, bf16[96,768]{1,0:T(8,128)(2,1)S(1)}, u32[]{:S(2)}, u32[]{:S(2)}) %collective-permute-start.62) | collective-permute-done | bytes 147488 | tf_op jit(solution)/shard_map/ppermute | solution.py:78
  192.1 2.9 %collective-permute-done.64 = f32[16,768]{1,0:T(8,128)S(1)} collective-permute-done((f32[16,768]{1,0:T(8,128)S(1)}, f32[16,768]{1,0:T(8,128)S(1)}, u32[]{:S(2)}, u32[]{:S(2)}) %collective-permute-start.64) | collective-permute-done | bytes 49184 | tf_op jit(solution)/shard_map/ppermute | solution.py:78
  197.1 2.4 %collective-permute-done.66 = f32[16,768]{1,0:T(8,128)S(1)} collective-permute-done((f32[16,768]{1,0:T(8,128)S(1)}, f32[16,768]{1,0:T(8,128)S(1)}, u32[]{:S(2)}, u32[]{:S(2)}) %collective-permute-start.66) | collective-permute-done | bytes 49184 | tf_op jit(solution)/shard_map/ppermute | solution.py:78
  200.4 3.2 %collective-permute-done.67 = f32[16,768]{1,0:T(8,128)S(1)} collective-permute-done((f32[16,768]{1,0:T(8,128)S(1)}, f32[16,768]{1,0:T(8,128)S(1)}, u32[]{:S(2)}, u32[]{:S(2)}) %collective-permute-start.67) | collective-permute-done | bytes 49184 | tf_op jit(solution)/shard_map/ppermute | solution.py:78
  204.2 3.4 %collective-permute-start.68 = (bf16[96,768]{1,0:T(8,128)(2,1)S(1)}, bf16[96,768]{1,0:T(8,128)(2,1)S(1)}, u32[]{:S(2)}, u32[]{:S(2)}) collective-permute-start(bf16[96,768]{1,0:T(8,128)(2,1)S(1)} %get-tuple-element.732), channel_id=1, source_target_pairs={{0,16},{1,17},{2,18},{3,19},{4,20},{5,21},{6,22},{7,23},{8,24},{9,... | collective-permute-start | bytes 442376 | tf_op jit(solution)/shard_map/ppermute | solution.py:78
  210.9 3.0 %collective-permute-done.68.last = bf16[96,768]{1,0:T(8,128)(2,1)S(1)} collective-permute-done((bf16[96,768]{1,0:T(8,128)(2,1)S(1)}, bf16[96,768]{1,0:T(8,128)(2,1)S(1)}, u32[]{:S(2)}, u32[]{:S(2)}) %collective-permute-start.68) | collective-permute-done | bytes 147488 | tf_op jit(solution)/shard_map/ppermute | solution.py:78
  (179 shorter events, 47.0 us)
Async XLA Ops:
  5.0 11.1 %collective-permute-start = (bf16[1,96,768]{2,1,0:T(8,128)(2,1)S(1)}, bf16[1,96,768]{2,1,0:T(8,128)(2,1)S(1)}, u32[]{:S(2)}, u32[]{:S(2)}) collective-permute-start(bf16[1,96,768]{2,1,0:T(8,128)(2,1)S(1)} %bitcast.18), channel_id=1, source_target_pairs={{0,16},{1,17},{2,18},{3,19},{4,20},{5,21},{6,22},{7,23},{8,24},{9,... | collective-permute-start | bytes 442376 | tf_op jit(solution)/shard_map/ppermute | solution.py:78
  16.2 8.2 %collective-permute-start.4 = (bf16[2,96,768]{2,1,0:T(8,128)(2,1)S(1)}, bf16[2,96,768]{2,1,0:T(8,128)(2,1)S(1)}, u32[]{:S(2)}, u32[]{:S(2)}) collective-permute-start(bf16[2,96,768]{2,1,0:T(8,128)(2,1)S(1)} %pad_maximum_fusion.2), channel_id=1, source_target_pairs={{0,8},{1,9},{2,10},{3,11},{4,12},{5,13},{6,14},{7,15},{8,0},{9,1},... | collective-permute-start | bytes 884744 | tf_op jit(solution)/shard_map/ppermute | solution.py:78
  24.5 17.0 %collective-permute-start.7 = (bf16[4,96,768]{2,1,0:T(8,128)(2,1)S(1)}, bf16[4,96,768]{2,1,0:T(8,128)(2,1)S(1)}, u32[]{:S(2)}, u32[]{:S(2)}) collective-permute-start(bf16[4,96,768]{2,1,0:T(8,128)(2,1)S(1)} %pad_maximum_fusion.rest_0_), channel_id=1, source_target_pairs={{0,2},{1,3},{2,0},{3,1},{4,6},{5,7},{6,4},{7,5},{8,10},{9,11},{10,... | collective-permute-start | bytes 1769480 | tf_op jit(solution)/shard_map/ppermute | solution.py:78
  25.9 15.7 %collective-permute-start.8 = (bf16[4,96,768]{2,1,0:T(8,128)(2,1)S(1)}, bf16[4,96,768]{2,1,0:T(8,128)(2,1)S(1)}, u32[]{:S(2)}, u32[]{:S(2)}) collective-permute-start(bf16[4,96,768]{2,1,0:T(8,128)(2,1)S(1)} %pad_maximum_fusion.rest_0_), channel_id=1, source_target_pairs={{0,4},{1,5},{2,6},{3,7},{4,0},{5,1},{6,2},{7,3},{8,12},{9,13},{10,... | collective-permute-start | bytes 1769480 | tf_op jit(solution)/shard_map/ppermute | solution.py:78
  27.4 14.2 %collective-permute-start.9 = (bf16[4,96,768]{2,1,0:T(8,128)(2,1)S(1)}, bf16[4,96,768]{2,1,0:T(8,128)(2,1)S(1)}, u32[]{:S(2)}, u32[]{:S(2)}) collective-permute-start(bf16[4,96,768]{2,1,0:T(8,128)(2,1)S(1)} %pad_maximum_fusion.rest_0_), channel_id=1, source_target_pairs={{0,1},{1,0},{2,3},{3,2},{4,5},{5,4},{6,7},{7,6},{8,9},{9,8},{10,11... | collective-permute-start | bytes 1769480 | tf_op jit(solution)/shard_map/ppermute | solution.py:78
  27.4 8.0 %collective-permute-start.11 = (bf16[1,96,384]{2,1,0:T(8,128)(2,1)S(1)}, bf16[1,96,384]{2,1,0:T(8,128)(2,1)S(1)}, u32[]{:S(2)}, u32[]{:S(2)}) collective-permute-start(bf16[1,96,384]{2,1,0:T(8,128)(2,1)S(1)} %bitcast.24), channel_id=1, source_target_pairs={{0,16},{1,17},{2,18},{3,19},{4,20},{5,21},{6,22},{7,23},{8,24},{9,... | collective-permute-start | bytes 221192 | tf_op jit(solution)/shard_map/ppermute | solution.py:78
  30.7 10.8 %collective-permute-start.10 = (bf16[1,96,768]{2,1,0:T(8,128)(2,1)S(1)}, bf16[1,96,768]{2,1,0:T(8,128)(2,1)S(1)}, u32[]{:S(2)}, u32[]{:S(2)}) collective-permute-start(bf16[1,96,768]{2,1,0:T(8,128)(2,1)S(1)} %convert_bitcast_fusion), channel_id=1, source_target_pairs={{0,16},{1,17},{2,18},{3,19},{4,20},{5,21},{6,22},{7,23},{8,24},{9,... | collective-permute-start | bytes 442376 | tf_op jit(solution)/shard_map/ppermute | solution.py:78
  41.7 10.2 %collective-permute-start.14 = (bf16[4,96,768]{2,1,0:T(8,128)(2,1)S(1)}, bf16[4,96,768]{2,1,0:T(8,128)(2,1)S(1)}, u32[]{:S(2)}, u32[]{:S(2)}) collective-permute-start(bf16[4,96,768]{2,1,0:T(8,128)(2,1)S(1)} %collective-permute-done.8.rest_1_), channel_id=1, source_target_pairs={{0,1},{1,0},{2,3},{3,2},{4,5},{5,4},{6,7},{7,6},{8,9},{9,8},{10,11... | collective-permute-start | bytes 1769480 | tf_op jit(solution)/shard_map/ppermute | solution.py:78
  41.8 10.1 %collective-permute-start.15 = (bf16[4,96,768]{2,1,0:T(8,128)(2,1)S(1)}, bf16[4,96,768]{2,1,0:T(8,128)(2,1)S(1)}, u32[]{:S(2)}, u32[]{:S(2)}) collective-permute-start(bf16[4,96,768]{2,1,0:T(8,128)(2,1)S(1)} %collective-permute-done.7.rest_2_), channel_id=1, source_target_pairs={{0,1},{1,0},{2,3},{3,2},{4,5},{5,4},{6,7},{7,6},{8,9},{9,8},{10,11... | collective-permute-start | bytes 1769480 | tf_op jit(solution)/shard_map/ppermute | solution.py:78
  42.3 9.1 %collective-permute-start.12 = (bf16[2,96,768]{2,1,0:T(8,128)(2,1)S(1)}, bf16[2,96,768]{2,1,0:T(8,128)(2,1)S(1)}, u32[]{:S(2)}, u32[]{:S(2)}) collective-permute-start(bf16[2,96,768]{2,1,0:T(8,128)(2,1)S(1)} %slice.52), channel_id=1, source_target_pairs={{0,2},{1,3},{2,0},{3,1},{4,6},{5,7},{6,4},{7,5},{8,10},{9,11},{10,... | collective-permute-start | bytes 884744 | tf_op jit(solution)/shard_map/ppermute | solution.py:78
  42.9 8.7 %collective-permute-start.13 = (bf16[2,96,768]{2,1,0:T(8,128)(2,1)S(1)}, bf16[2,96,768]{2,1,0:T(8,128)(2,1)S(1)}, u32[]{:S(2)}, u32[]{:S(2)}) collective-permute-start(bf16[2,96,768]{2,1,0:T(8,128)(2,1)S(1)} %slice.53), channel_id=1, source_target_pairs={{0,4},{1,5},{2,6},{3,7},{4,0},{5,1},{6,2},{7,3},{8,12},{9,13},{10,... | collective-permute-start | bytes 884744 | tf_op jit(solution)/shard_map/ppermute | solution.py:78
  43.4 8.4 %collective-permute-start.16 = (bf16[2,96,768]{2,1,0:T(8,128)(2,1)S(1)}, bf16[2,96,768]{2,1,0:T(8,128)(2,1)S(1)}, u32[]{:S(2)}, u32[]{:S(2)}) collective-permute-start(bf16[2,96,768]{2,1,0:T(8,128)(2,1)S(1)} %pad_maximum_fusion.3), channel_id=1, source_target_pairs={{0,8},{1,9},{2,10},{3,11},{4,12},{5,13},{6,14},{7,15},{8,0},{9,1},... | collective-permute-start | bytes 884744 | tf_op jit(solution)/shard_map/ppermute | solution.py:78
  52.5 19.7 %collective-permute-start.19 = (bf16[4,96,768]{2,1,0:T(8,128)(2,1)S(1)}, bf16[4,96,768]{2,1,0:T(8,128)(2,1)S(1)}, u32[]{:S(2)}, u32[]{:S(2)}) collective-permute-start(bf16[4,96,768]{2,1,0:T(8,128)(2,1)S(1)} %pad_maximum_fusion.1.rest_0_), channel_id=1, source_target_pairs={{0,2},{1,3},{2,0},{3,1},{4,6},{5,7},{6,4},{7,5},{8,10},{9,11},{10,... | collective-permute-start | bytes 1769480 | tf_op jit(solution)/shard_map/ppermute | solution.py:78
  54.1 18.2 %collective-permute-start.20 = (bf16[4,96,768]{2,1,0:T(8,128)(2,1)S(1)}, bf16[4,96,768]{2,1,0:T(8,128)(2,1)S(1)}, u32[]{:S(2)}, u32[]{:S(2)}) collective-permute-start(bf16[4,96,768]{2,1,0:T(8,128)(2,1)S(1)} %pad_maximum_fusion.1.rest_0_), channel_id=1, source_target_pairs={{0,4},{1,5},{2,6},{3,7},{4,0},{5,1},{6,2},{7,3},{8,12},{9,13},{10,... | collective-permute-start | bytes 1769480 | tf_op jit(solution)/shard_map/ppermute | solution.py:78
  55.6 16.7 %collective-permute-start.21 = (bf16[4,96,768]{2,1,0:T(8,128)(2,1)S(1)}, bf16[4,96,768]{2,1,0:T(8,128)(2,1)S(1)}, u32[]{:S(2)}, u32[]{:S(2)}) collective-permute-start(bf16[4,96,768]{2,1,0:T(8,128)(2,1)S(1)} %pad_maximum_fusion.1.rest_0_), channel_id=1, source_target_pairs={{0,1},{1,0},{2,3},{3,2},{4,5},{5,4},{6,7},{7,6},{8,9},{9,8},{10,11... | collective-permute-start | bytes 1769480 | tf_op jit(solution)/shard_map/ppermute | solution.py:78
  55.6 16.6 %collective-permute-start.23 = (bf16[4,96,384]{2,1,0:T(8,128)(2,1)S(1)}, bf16[4,96,384]{2,1,0:T(8,128)(2,1)S(1)}, u32[]{:S(2)}, u32[]{:S(2)}) collective-permute-start(bf16[4,96,384]{2,1,0:T(8,128)(2,1)S(1)} %pad_maximum_fusion.4), channel_id=1, source_target_pairs={{0,16},{1,17},{2,18},{3,19},{4,20},{5,21},{6,22},{7,23},{8,24},{9,... | collective-permute-start | bytes 884744 | tf_op jit(solution)/shard_map/ppermute | solution.py:78
  58.0 13.3 %collective-permute-start.22 = (bf16[2,96,384]{2,1,0:T(8,128)(2,1)S(1)}, bf16[2,96,384]{2,1,0:T(8,128)(2,1)S(1)}, u32[]{:S(2)}, u32[]{:S(2)}) collective-permute-start(bf16[2,96,384]{2,1,0:T(8,128)(2,1)S(1)} %pad_maximum_fusion.6), channel_id=1, source_target_pairs={{0,8},{1,9},{2,10},{3,11},{4,12},{5,13},{6,14},{7,15},{8,0},{9,1},... | collective-permute-start | bytes 442376 | tf_op jit(solution)/shard_map/ppermute | solution.py:78
  72.4 9.8 %collective-permute-start.26 = (bf16[4,96,768]{2,1,0:T(8,128)(2,1)S(1)}, bf16[4,96,768]{2,1,0:T(8,128)(2,1)S(1)}, u32[]{:S(2)}, u32[]{:S(2)}) collective-permute-start(bf16[4,96,768]{2,1,0:T(8,128)(2,1)S(1)} %collective-permute-done.20.rest_1_), channel_id=1, source_target_pairs={{0,1},{1,0},{2,3},{3,2},{4,5},{5,4},{6,7},{7,6},{8,9},{9,8},{10,11... | collective-permute-start | bytes 1769480 | tf_op jit(solution)/shard_map/ppermute | solution.py:78
  72.5 9.8 %collective-permute-start.27 = (bf16[4,96,768]{2,1,0:T(8,128)(2,1)S(1)}, bf16[4,96,768]{2,1,0:T(8,128)(2,1)S(1)}, u32[]{:S(2)}, u32[]{:S(2)}) collective-permute-start(bf16[4,96,768]{2,1,0:T(8,128)(2,1)S(1)} %collective-permute-done.19.rest_0_), channel_id=1, source_target_pairs={{0,1},{1,0},{2,3},{3,2},{4,5},{5,4},{6,7},{7,6},{8,9},{9,8},{10,11... | collective-permute-start | bytes 1769480 | tf_op jit(solution)/shard_map/ppermute | solution.py:78
  73.0 9.0 %collective-permute-start.24 = (bf16[2,96,768]{2,1,0:T(8,128)(2,1)S(1)}, bf16[2,96,768]{2,1,0:T(8,128)(2,1)S(1)}, u32[]{:S(2)}, u32[]{:S(2)}) collective-permute-start(bf16[2,96,768]{2,1,0:T(8,128)(2,1)S(1)} %slice.54), channel_id=1, source_target_pairs={{0,2},{1,3},{2,0},{3,1},{4,6},{5,7},{6,4},{7,5},{8,10},{9,11},{10,... | collective-permute-start | bytes 884744 | tf_op jit(solution)/shard_map/ppermute | solution.py:78
  73.5 8.7 %collective-permute-start.25 = (bf16[2,96,768]{2,1,0:T(8,128)(2,1)S(1)}, bf16[2,96,768]{2,1,0:T(8,128)(2,1)S(1)}, u32[]{:S(2)}, u32[]{:S(2)}) collective-permute-start(bf16[2,96,768]{2,1,0:T(8,128)(2,1)S(1)} %slice.55), channel_id=1, source_target_pairs={{0,4},{1,5},{2,6},{3,7},{4,0},{5,1},{6,2},{7,3},{8,12},{9,13},{10,... | collective-permute-start | bytes 884744 | tf_op jit(solution)/shard_map/ppermute | solution.py:78
  74.4 19.2 %collective-permute-start.33 = (bf16[8,96,384]{2,1,0:T(8,128)(2,1)S(1)}, bf16[8,96,384]{2,1,0:T(8,128)(2,1)S(1)}, u32[]{:S(2)}, u32[]{:S(2)}) collective-permute-start(bf16[8,96,384]{2,1,0:T(8,128)(2,1)S(1)} %get-tuple-element.556.rest_10_), channel_id=1, source_target_pairs={{0,8},{1,9},{2,10},{3,11},{4,12},{5,13},{6,14},{7,15},{8,0},{9,1},... | collective-permute-start | bytes 1769480 | tf_op jit(solution)/shard_map/ppermute | solution.py:78
  82.2 7.1 %collective-permute-start.28 = (bf16[2,96,768]{2,1,0:T(8,128)(2,1)S(1)}, bf16[2,96,768]{2,1,0:T(8,128)(2,1)S(1)}, u32[]{:S(2)}, u32[]{:S(2)}) collective-permute-start(bf16[2,96,768]{2,1,0:T(8,128)(2,1)S(1)} %collective-permute-done.24.rest_1_), channel_id=1, source_target_pairs={{0,1},{1,0},{2,3},{3,2},{4,5},{5,4},{6,7},{7,6},{8,9},{9,8},{10,11... | collective-permute-start | bytes 884744 | tf_op jit(solution)/shard_map/ppermute | solution.py:78
  82.3 7.2 %collective-permute-start.29 = (bf16[2,96,768]{2,1,0:T(8,128)(2,1)S(1)}, bf16[2,96,768]{2,1,0:T(8,128)(2,1)S(1)}, u32[]{:S(2)}, u32[]{:S(2)}) collective-permute-start(bf16[2,96,768]{2,1,0:T(8,128)(2,1)S(1)} %collective-permute-done.25.rest_2_), channel_id=1, source_target_pairs={{0,1},{1,0},{2,3},{3,2},{4,5},{5,4},{6,7},{7,6},{8,9},{9,8},{10,11... | collective-permute-start | bytes 884744 | tf_op jit(solution)/shard_map/ppermute | solution.py:78
  82.8 10.9 %collective-permute-start.30 = (bf16[4,96,384]{2,1,0:T(8,128)(2,1)S(1)}, bf16[4,96,384]{2,1,0:T(8,128)(2,1)S(1)}, u32[]{:S(2)}, u32[]{:S(2)}) collective-permute-start(bf16[4,96,384]{2,1,0:T(8,128)(2,1)S(1)} %get-tuple-element.546.rest_0_), channel_id=1, source_target_pairs={{0,2},{1,3},{2,0},{3,1},{4,6},{5,7},{6,4},{7,5},{8,10},{9,11},{10,... | collective-permute-start | bytes 884744 | tf_op jit(solution)/shard_map/ppermute | solution.py:78
  84.2 9.4 %collective-permute-start.31 = (bf16[4,96,384]{2,1,0:T(8,128)(2,1)S(1)}, bf16[4,96,384]{2,1,0:T(8,128)(2,1)S(1)}, u32[]{:S(2)}, u32[]{:S(2)}) collective-permute-start(bf16[4,96,384]{2,1,0:T(8,128)(2,1)S(1)} %get-tuple-element.546.rest_0_), channel_id=1, source_target_pairs={{0,4},{1,5},{2,6},{3,7},{4,0},{5,1},{6,2},{7,3},{8,12},{9,13},{10,... | collective-permute-start | bytes 884744 | tf_op jit(solution)/shard_map/ppermute | solution.py:78
  93.7 7.0 %collective-permute-start.36 = (bf16[4,96,384]{2,1,0:T(8,128)(2,1)S(1)}, bf16[4,96,384]{2,1,0:T(8,128)(2,1)S(1)}, u32[]{:S(2)}, u32[]{:S(2)}) collective-permute-start(bf16[4,96,384]{2,1,0:T(8,128)(2,1)S(1)} %collective-permute-done.31.rest_1_), channel_id=1, source_target_pairs={{0,1},{1,0},{2,3},{3,2},{4,5},{5,4},{6,7},{7,6},{8,9},{9,8},{10,11... | collective-permute-start | bytes 884744 | tf_op jit(solution)/shard_map/ppermute | solution.py:78
  121.0 15.6 %collective-permute-start.46 = (bf16[4,96,768]{2,1,0:T(8,128)(2,1)S(1)}, bf16[4,96,768]{2,1,0:T(8,128)(2,1)S(1)}, u32[]{:S(2)}, u32[]{:S(2)}) collective-permute-start(bf16[4,96,768]{2,1,0:T(8,128)(2,1)S(1)} %get-tuple-element.617), channel_id=1, source_target_pairs={{0,8},{1,9},{2,10},{3,11},{4,12},{5,13},{6,14},{7,15},{8,0},{9,1},... | collective-permute-start | bytes 1769480 | tf_op jit(solution)/shard_map/ppermute | solution.py:78
  126.6 10.0 %collective-permute-start.44 = (bf16[2,96,768]{2,1,0:T(8,128)(2,1)S(1)}, bf16[2,96,768]{2,1,0:T(8,128)(2,1)S(1)}, u32[]{:S(2)}, u32[]{:S(2)}) collective-permute-start(bf16[2,96,768]{2,1,0:T(8,128)(2,1)S(1)} %get-tuple-element.615), channel_id=1, source_target_pairs={{0,2},{1,3},{2,0},{3,1},{4,6},{5,7},{6,4},{7,5},{8,10},{9,11},{10,... | collective-permute-start | bytes 884744 | tf_op jit(solution)/shard_map/ppermute | solution.py:78
  128.1 8.7 %collective-permute-start.45 = (bf16[2,96,768]{2,1,0:T(8,128)(2,1)S(1)}, bf16[2,96,768]{2,1,0:T(8,128)(2,1)S(1)}, u32[]{:S(2)}, u32[]{:S(2)}) collective-permute-start(bf16[2,96,768]{2,1,0:T(8,128)(2,1)S(1)} %get-tuple-element.616), channel_id=1, source_target_pairs={{0,4},{1,5},{2,6},{3,7},{4,0},{5,1},{6,2},{7,3},{8,12},{9,13},{10,... | collective-permute-start | bytes 884744 | tf_op jit(solution)/shard_map/ppermute | solution.py:78
  137.3 18.9 %collective-permute-start.47 = (bf16[4,96,768]{2,1,0:T(8,128)(2,1)S(1)}, bf16[4,96,768]{2,1,0:T(8,128)(2,1)S(1)}, u32[]{:S(2)}, u32[]{:S(2)}) collective-permute-start(bf16[4,96,768]{2,1,0:T(8,128)(2,1)S(1)} %get-tuple-element.658), channel_id=1, source_target_pairs={{0,2},{1,3},{2,0},{3,1},{4,6},{5,7},{6,4},{7,5},{8,10},{9,11},{10,... | collective-permute-start | bytes 1769480 | tf_op jit(solution)/shard_map/ppermute | solution.py:78
  138.6 17.6 %collective-permute-start.48 = (bf16[4,96,768]{2,1,0:T(8,128)(2,1)S(1)}, bf16[4,96,768]{2,1,0:T(8,128)(2,1)S(1)}, u32[]{:S(2)}, u32[]{:S(2)}) collective-permute-start(bf16[4,96,768]{2,1,0:T(8,128)(2,1)S(1)} %get-tuple-element.659), channel_id=1, source_target_pairs={{0,4},{1,5},{2,6},{3,7},{4,0},{5,1},{6,2},{7,3},{8,12},{9,13},{10,... | collective-permute-start | bytes 1769480 | tf_op jit(solution)/shard_map/ppermute | solution.py:78
  139.7 16.5 %collective-permute-start.51 = (bf16[4,96,768]{2,1,0:T(8,128)(2,1)S(1)}, bf16[4,96,768]{2,1,0:T(8,128)(2,1)S(1)}, u32[]{:S(2)}, u32[]{:S(2)}) collective-permute-start(bf16[4,96,768]{2,1,0:T(8,128)(2,1)S(1)} %get-tuple-element.662), channel_id=1, source_target_pairs={{0,8},{1,9},{2,10},{3,11},{4,12},{5,13},{6,14},{7,15},{8,0},{9,1},... | collective-permute-start | bytes 1769480 | tf_op jit(solution)/shard_map/ppermute | solution.py:78
  140.4 14.6 %collective-permute-start.49 = (bf16[96,768]{1,0:T(8,128)(2,1)S(1)}, bf16[96,768]{1,0:T(8,128)(2,1)S(1)}, u32[]{:S(2)}, u32[]{:S(2)}) collective-permute-start(bf16[96,768]{1,0:T(8,128)(2,1)S(1)} %get-tuple-element.660), channel_id=1, source_target_pairs={{0,2},{1,3},{2,0},{3,1},{4,6},{5,7},{6,4},{7,5},{8,10},{9,11},{10,... | collective-permute-start | bytes 442376 | tf_op jit(solution)/shard_map/ppermute | solution.py:78
  141.9 14.4 %collective-permute-start.50 = (bf16[96,768]{1,0:T(8,128)(2,1)S(1)}, bf16[96,768]{1,0:T(8,128)(2,1)S(1)}, u32[]{:S(2)}, u32[]{:S(2)}) collective-permute-start(bf16[96,768]{1,0:T(8,128)(2,1)S(1)} %get-tuple-element.661), channel_id=1, source_target_pairs={{0,4},{1,5},{2,6},{3,7},{4,0},{5,1},{6,2},{7,3},{8,12},{9,13},{10,... | collective-permute-start | bytes 442376 | tf_op jit(solution)/shard_map/ppermute | solution.py:78
  156.8 10.6 %collective-permute-start.52 = (bf16[2,8,96,768]{3,2,1,0:T(8,128)(2,1)S(1)}, bf16[2,8,96,768]{3,2,1,0:T(8,128)(2,1)S(1)}, u32[]{:S(2)}, u32[]{:S(2)}) collective-permute-start(bf16[2,8,96,768]{3,2,1,0:T(8,128)(2,1)S(1)} %get-tuple-element.681), channel_id=1, source_target_pairs={{0,1},{1,0},{2,3},{3,2},{4,5},{5,4},{6,7},{7,6},{8,9},{9,8},{10,11... | collective-permute-start | bytes 7077896 | tf_op jit(solution)/shard_map/ppermute | solution.py:78
  156.9 9.4 %collective-permute-start.53 = (bf16[2,96,768]{2,1,0:T(8,128)(2,1)S(1)}, bf16[2,96,768]{2,1,0:T(8,128)(2,1)S(1)}, u32[]{:S(2)}, u32[]{:S(2)}) collective-permute-start(bf16[2,96,768]{2,1,0:T(8,128)(2,1)S(1)} %get-tuple-element.682), channel_id=1, source_target_pairs={{0,2},{1,3},{2,0},{3,1},{4,6},{5,7},{6,4},{7,5},{8,10},{9,11},{10,... | collective-permute-start | bytes 884744 | tf_op jit(solution)/shard_map/ppermute | solution.py:78
  157.5 9.1 %collective-permute-start.54 = (bf16[2,96,768]{2,1,0:T(8,128)(2,1)S(1)}, bf16[2,96,768]{2,1,0:T(8,128)(2,1)S(1)}, u32[]{:S(2)}, u32[]{:S(2)}) collective-permute-start(bf16[2,96,768]{2,1,0:T(8,128)(2,1)S(1)} %get-tuple-element.683), channel_id=1, source_target_pairs={{0,4},{1,5},{2,6},{3,7},{4,0},{5,1},{6,2},{7,3},{8,12},{9,13},{10,... | collective-permute-start | bytes 884744 | tf_op jit(solution)/shard_map/ppermute | solution.py:78
  158.6 8.8 %collective-permute-start.55 = (bf16[2,96,768]{2,1,0:T(8,128)(2,1)S(1)}, bf16[2,96,768]{2,1,0:T(8,128)(2,1)S(1)}, u32[]{:S(2)}, u32[]{:S(2)}) collective-permute-start(bf16[2,96,768]{2,1,0:T(8,128)(2,1)S(1)} %get-tuple-element.684), channel_id=1, source_target_pairs={{0,8},{1,9},{2,10},{3,11},{4,12},{5,13},{6,14},{7,15},{8,0},{9,1},... | collective-permute-start | bytes 884744 | tf_op jit(solution)/shard_map/ppermute | solution.py:78
  167.8 8.0 %collective-permute-start.57 = (bf16[2,96,768]{2,1,0:T(8,128)(2,1)S(1)}, bf16[2,96,768]{2,1,0:T(8,128)(2,1)S(1)}, u32[]{:S(2)}, u32[]{:S(2)}) collective-permute-start(bf16[2,96,768]{2,1,0:T(8,128)(2,1)S(1)} %get-tuple-element.695), channel_id=1, source_target_pairs={{0,2},{1,3},{2,0},{3,1},{4,6},{5,7},{6,4},{7,5},{8,10},{9,11},{10,... | collective-permute-start | bytes 884744 | tf_op jit(solution)/shard_map/ppermute | solution.py:78
  169.3 7.6 %collective-permute-start.58 = (bf16[2,96,768]{2,1,0:T(8,128)(2,1)S(1)}, bf16[2,96,768]{2,1,0:T(8,128)(2,1)S(1)}, u32[]{:S(2)}, u32[]{:S(2)}) collective-permute-start(bf16[2,96,768]{2,1,0:T(8,128)(2,1)S(1)} %get-tuple-element.696), channel_id=1, source_target_pairs={{0,4},{1,5},{2,6},{3,7},{4,0},{5,1},{6,2},{7,3},{8,12},{9,13},{10,... | collective-permute-start | bytes 884744 | tf_op jit(solution)/shard_map/ppermute | solution.py:78
  177.4 17.5 %collective-permute-start.60 = (bf16[4,96,768]{2,1,0:T(8,128)(2,1)S(1)}, bf16[4,96,768]{2,1,0:T(8,128)(2,1)S(1)}, u32[]{:S(2)}, u32[]{:S(2)}) collective-permute-start(bf16[4,96,768]{2,1,0:T(8,128)(2,1)S(1)} %get-tuple-element.706), channel_id=1, source_target_pairs={{0,2},{1,3},{2,0},{3,1},{4,6},{5,7},{6,4},{7,5},{8,10},{9,11},{10,... | collective-permute-start | bytes 1769480 | tf_op jit(solution)/shard_map/ppermute | solution.py:78
  178.0 16.9 %collective-permute-start.61 = (bf16[4,96,768]{2,1,0:T(8,128)(2,1)S(1)}, bf16[4,96,768]{2,1,0:T(8,128)(2,1)S(1)}, u32[]{:S(2)}, u32[]{:S(2)}) collective-permute-start(bf16[4,96,768]{2,1,0:T(8,128)(2,1)S(1)} %get-tuple-element.707), channel_id=1, source_target_pairs={{0,4},{1,5},{2,6},{3,7},{4,0},{5,1},{6,2},{7,3},{8,12},{9,13},{10,... | collective-permute-start | bytes 1769480 | tf_op jit(solution)/shard_map/ppermute | solution.py:78
  178.9 13.1 %collective-permute-start.62 = (bf16[96,768]{1,0:T(8,128)(2,1)S(1)}, bf16[96,768]{1,0:T(8,128)(2,1)S(1)}, u32[]{:S(2)}, u32[]{:S(2)}) collective-permute-start(bf16[96,768]{1,0:T(8,128)(2,1)S(1)} %get-tuple-element.708), channel_id=1, source_target_pairs={{0,16},{1,17},{2,18},{3,19},{4,20},{5,21},{6,22},{7,23},{8,24},{9,... | collective-permute-start | bytes 442376 | tf_op jit(solution)/shard_map/ppermute | solution.py:78
  182.0 12.9 %collective-permute-start.63 = (bf16[96,768]{1,0:T(8,128)(2,1)S(1)}, bf16[96,768]{1,0:T(8,128)(2,1)S(1)}, u32[]{:S(2)}, u32[]{:S(2)}) collective-permute-start(bf16[96,768]{1,0:T(8,128)(2,1)S(1)} %get-tuple-element.709), channel_id=1, source_target_pairs={{0,16},{1,17},{2,18},{3,19},{4,20},{5,21},{6,22},{7,23},{8,24},{9,... | collective-permute-start | bytes 442376 | tf_op jit(solution)/shard_map/ppermute | solution.py:78
  182.1 12.9 %collective-permute-start.64 = (f32[16,768]{1,0:T(8,128)S(1)}, f32[16,768]{1,0:T(8,128)S(1)}, u32[]{:S(2)}, u32[]{:S(2)}) collective-permute-start(f32[16,768]{1,0:T(8,128)S(1)} %add_select_fusion.3), channel_id=1, source_target_pairs={{0,16},{1,17},{2,18},{3,19},{4,20},{5,21},{6,22},{7,23},{8,24},{9,... | collective-permute-start | bytes 147464 | tf_op jit(solution)/shard_map/ppermute | solution.py:78
  196.4 7.6 %collective-permute-start.65 = (bf16[2,96,768]{2,1,0:T(8,128)(2,1)S(1)}, bf16[2,96,768]{2,1,0:T(8,128)(2,1)S(1)}, u32[]{:S(2)}, u32[]{:S(2)}) collective-permute-start(bf16[2,96,768]{2,1,0:T(8,128)(2,1)S(1)} %get-tuple-element.716), channel_id=1, source_target_pairs={{0,8},{1,9},{2,10},{3,11},{4,12},{5,13},{6,14},{7,15},{8,0},{9,1},... | collective-permute-start | bytes 884744 | tf_op jit(solution)/shard_map/ppermute | solution.py:78
  204.2 9.7 %collective-permute-start.68 = (bf16[96,768]{1,0:T(8,128)(2,1)S(1)}, bf16[96,768]{1,0:T(8,128)(2,1)S(1)}, u32[]{:S(2)}, u32[]{:S(2)}) collective-permute-start(bf16[96,768]{1,0:T(8,128)(2,1)S(1)} %get-tuple-element.732), channel_id=1, source_target_pairs={{0,16},{1,17},{2,18},{3,19},{4,20},{5,21},{6,22},{7,23},{8,24},{9,... | collective-permute-start | bytes 442376 | tf_op jit(solution)/shard_map/ppermute | solution.py:78
  (36 other events, 270.9 us)

commit v11 on v9

--- a/solution.py
+++ b/solution.py
@@ -149,7 +149,17 @@
         (got,) = yield [(far, PC)]
         out_x, out_y = add_first(near, got)
         from_x, from_y = yield [(out_x, PX), (out_y, PY)]
-        out_x, out_y = add_second(near, got, from_x, from_y)
+        out_x, out_y = add_second(near, got, near, got, from_x, from_y)
+        in_x, in_y = yield [(out_x, PX), (out_y, PY)]
+        return near, got, in_x, in_y
+
+    @staticmethod
+    def scatter_halves(far_1, near_1, late):
+        (got_1,) = yield [(far_1, PC)]
+        out_x, out_y = add_first(near_1, got_1)
+        from_x, from_y, got = yield [(out_x, PX), (out_y, PY), (late["far"], PC)]
+        near = late["near"]
+        out_x, out_y = add_second(near_1, got_1, near, got, from_x, from_y)
         in_x, in_y = yield [(out_x, PX), (out_y, PY)]
         return near, got, in_x, in_y
 
@@ -219,6 +229,13 @@
         yield
 
     @staticmethod
+    def scatter_halves(far_1, near_1, late):
+        while not late:
+            yield []
+        far = jnp.concatenate([late["far"], far_1], 0)
+        return (yield from Plain.scatter_sum(far, jnp.concatenate([late["near"], near_1], 0)))
+
+    @staticmethod
     def scatter_line(grads):
         own = lax.psum_scatter(grads, "tensor", scatter_dimension=0, tiled=False)
         own = lax.psum_scatter(own, "dp", scatter_dimension=0, tiled=True)
@@ -273,19 +290,23 @@
 
 
 def add_first(near, got):
+    top = near.shape[0] - 1
+
     def first_sums(near, got, out_x, out_y):
         for k in range(2):
-            out_x[k] = (near[1, 4 + k].astype(f32) + got[1, 4 + k].astype(f32)).astype(bf16)
-            out_y[k] = (near[1, 6 + k].astype(f32) + got[1, 6 + k].astype(f32)).astype(bf16)
+            out_x[k] = (near[top, 4 + k].astype(f32) + got[top, 4 + k].astype(f32)).astype(bf16)
+            out_y[k] = (near[top, 6 + k].astype(f32) + got[top, 6 + k].astype(f32)).astype(bf16)
 
     part = like((2,) + near.shape[2:], bf16)
     return glue(first_sums, [part, part], near, got)
 
 
-def add_second(near, got, from_x, from_y):
-    def second_sums(near, got, from_x, from_y, out_x, out_y):
+def add_second(near_1, got_1, near, got, from_x, from_y):
+    top = near_1.shape[0] - 1
+
+    def second_sums(near_1, got_1, near, got, from_x, from_y, out_x, out_y):
         for k in range(4):
-            over_x = near[1, k].astype(f32) + got[1, k].astype(f32)
+            over_x = near_1[top, k].astype(f32) + got_1[top, k].astype(f32)
             over_y = near[0, 4 + k].astype(f32) + got[0, 4 + k].astype(f32)
             if k < 2:
                 over_y = over_y + from_x[k].astype(f32)
@@ -295,7 +316,7 @@
             out_y[k] = over_y.astype(bf16)
 
     part = like((4,) + near.shape[2:], bf16)
-    return glue(second_sums, [part, part], near, got, from_x, from_y)
+    return glue(second_sums, [part, part], near_1, got_1, near, got, from_x, from_y)
 
 
 def add_third(near, got, in_x, in_y):
@@ -655,45 +676,49 @@
     lax.fori_loop(0, out.shape[0], each, 0)
 
 
-def attn_backward(net, first, dims, longs, shorts, qkv, lse, attn_low, weight, ctx_slope, out, sums, mask, grad_ctx):
+def in_weight_grads(net, first, dims, in_t, attn_t, ctx_low, grads, far, near):
+    blocks, cols, width = dims
+    rows = in_t.shape[0] // net.parts
+    wide = 3 * cols + HEAD_DIM
+    start = 3 * cols - HEAD_DIM
+    dp = net.me()[0]
+
+    def weights(core, carry):
+        left = mm(in_t[...], grads[core])
+        right = mm(attn_t[...], ctx_low[first + core])
+        mixed = (left[:, start:] + right[:, : wide - start]).astype(bf16)
+        left, right = left[:, :start].astype(bf16), right[:, wide - start :].astype(bf16)
+        for to, wanted in ((near, 0), (far, 1)):
+
+            @pl.when(core == wanted)
+            def _():
+                for block in range(net.parts):
+                    rs = slice(block * rows, (block + 1) * rows)
+                    place = net.slot(block, dp)
+                    to[0, place, :, :start] = left[rs]
+                    to[0, place, :, start:wide] = mixed[rs]
+                    to[0, place, :, wide:] = right[rs]
+
+        return carry
+
+    lax.fori_loop(0, 2, weights, 0)
+
+
+def attn_backward(net, first, dims, longs, shorts, qkv, lse, attn_low, weight, ctx_slope, in_t, attn_t, ctx_low, *rest):
+    out, far, near, sums, mask, grad_ctx = rest
     fill_mask(mask, longs, shorts)
     sums[...] = jnp.zeros_like(sums)
     heads_backward(first, dims, net.me()[1], qkv, lse, attn_low, weight, ctx_slope, mask, grad_ctx, out, sums)
-
-
-def attn_backward_last(net, dims, longs, shorts, qkv, lse, attn_low, weight, ctx_slope, *rest):
+    in_weight_grads(net, first, dims, in_t, attn_t, ctx_low, out, far, near)
+
+
+def attn_backward_last(net, dims, longs, shorts, qkv, lse, attn_low, weight, ctx_slope, in_t, attn_t, ctx_low, *rest):
     blocks, cols, width = dims
-    in_t, attn_t, ctx_low, more_out, more, *rest = rest
-    up_sums, sums_a, sums_b, tops_a, tops_m, top0, top1, *rest = rest
-    out, far, near, packed, sums, mask, grad_ctx = rest
-    rows = in_t.shape[0] // net.parts
-    wide = 3 * cols + HEAD_DIM
-    start = 3 * cols - HEAD_DIM
-    dp, lane_me = net.me()
+    more, up_sums, sums_a, sums_b, tops_a, tops_m, top0, top1, out, far, near, packed, sums, mask, grad_ctx = rest
     fill_mask(mask, longs, shorts)
     sums[...] = more[...]
-    heads_backward(0, dims, lane_me, qkv, lse, attn_low, weight, ctx_slope, mask, grad_ctx, out, sums)
-    for x, grads in enumerate((out, more_out)):
-
-        def weights(core, carry):
-            left = mm(in_t[...], grads[core])
-            right = mm(attn_t[...], ctx_low[2 * x + core])
-            mixed = (left[:, start:] + right[:, : wide - start]).astype(bf16)
-            left, right = left[:, :start].astype(bf16), right[:, wide - start :].astype(bf16)
-            for to, wanted in ((near, 0), (far, 1)):
-
-                @pl.when(core == wanted)
-                def _():
-                    for block in range(net.parts):
-                        rs = slice(block * rows, (block + 1) * rows)
-                        place = net.slot(block, dp)
-                        to[x, place, :, :start] = left[rs]
-                        to[x, place, :, start:wide] = mixed[rs]
-                        to[x, place, :, wide:] = right[rs]
-
-            return carry
-
-        lax.fori_loop(0, 2, weights, 0)
+    heads_backward(0, dims, net.me()[1], qkv, lse, attn_low, weight, ctx_slope, mask, grad_ctx, out, sums)
+    in_weight_grads(net, 0, dims, in_t, attn_t, ctx_low, out, far, near)
     packed[...] = jnp.zeros_like(packed)
     for j in range(blocks):
         packed[j : j + 1, :] = up_sums[j]
@@ -905,13 +930,14 @@
             [sum_u, sum_d],
             [sum_u],
         )
-        grads_1, more = step(
-            (long_lengths, short_lengths, qkv, lse, attn_low, weight_a, ctx_slope),
+        half_shape = like((1,) + grad_shape.shape, bf16)
+        grads_1, far, near, more = step(
+            (long_lengths, short_lengths, qkv, lse, attn_low, weight_a, ctx_slope, in_t, attn_t, ctx_low),
             call(
                 functools.partial(attn_backward, net, half, dims),
                 "attn_backward",
-                [SM] * 2 + [VM] * 5,
-                [like((half, rows, wide), bf16), like((blocks, 1, wide))],
+                [SM] * 2 + [VM] * 8,
+                [like((half, rows, wide), bf16), half_shape, half_shape, like((blocks, 1, wide))],
                 [vmem(rows, rows), vmem(rows, out_cols, dtype=bf16)],
                 2 * unit,
                 2 * moved,
@@ -919,23 +945,25 @@
             [sum_u],
             [sum_u, sum_d],
         )
+        late = {}
+        sum_a = Job(net.scatter_halves(far, near, late))
         grads_0, far, near, packed = step(
-            (long_lengths, short_lengths, qkv, lse, attn_low, weight_a, ctx_slope)
-            + (in_t, attn_t, ctx_low, grads_1, more)
-            + (up_sums, sums_a, sums_b, tops_a, tops_m, top0, top1),
+            (long_lengths, short_lengths, qkv, lse, attn_low, weight_a, ctx_slope, in_t, attn_t, ctx_low)
+            + (more, up_sums, sums_a, sums_b, tops_a, tops_m, top0, top1),
             call(
                 functools.partial(attn_backward_last, net, dims),
                 "attn_backward_last",
-                [SM] * 2 + [VM] * 17,
-                [like((half, rows, wide), bf16), both_shape, both_shape, like((16, width))],
+                [SM] * 2 + [VM] * 16,
+                [like((half, rows, wide), bf16), half_shape, half_shape, like((16, width))],
                 [vmem(blocks, 1, wide), vmem(rows, rows), vmem(rows, out_cols, dtype=bf16)],
                 4 * unit,
                 2 * moved,
             ),
-            [sum_u, sum_d],
+            [sum_u, sum_a, sum_d],
             [sum_u, sum_d],
         )
-        sum_a = Job(net.scatter_sum(far, near))
+        late.update(far=far, near=near)
+        step((), None, [], [sum_a])
         is_top = (jnp.arange(packed.shape[0]) == 2 * blocks + 6)[:, None]
         sum_s = Job(net.sum_max(packed, is_top))
         line_u = Job(net.scatter_line(*sum_u.value))
@@ -950,25 +978,27 @@
                 unit,
                 2 * moved,
             ),
-            [sum_a, sum_d, line_u, sum_s],
-            [sum_a, sum_d, line_u, sum_s],
+            [sum_a, sum_d],
+            [sum_a, sum_d],
         )[0]
-        step((), None, [sum_a, sum_d], [sum_a, sum_d])
-        step((), None, [sum_a, line_u, sum_s], [sum_a, line_u, sum_s])
+        step((), None, [sum_a, line_u, sum_d, sum_s], [line_u, sum_d, sum_s])
+        step((), None, [line_u, sum_s], [sum_a, line_u, sum_s])
         line_a = Job(net.scatter_line(*sum_a.value))
         step((), None, [line_a, sum_s], [line_a, sum_s])
-        step((), None, [line_a, sum_s], [sum_s])
+
+        def finish(down, up):
+            return down[0] + down[1].astype(f32), up[0] + up[1].astype(f32)
+
+        down_grad, up_grad = step((sum_d.value, line_u.value), finish, [line_a, sum_s], [sum_s])
         step((), None, [sum_s], [line_a, sum_s])
-
         packed = sum_s.value
-        down_grad, up_grad = (kept + last.astype(f32) for kept, last in (sum_d.value, line_u.value))
-        down_grad = down_grad.T
-        qkv_grad, out_grad = attn_grads(*line_a.value)
         own = lax.dynamic_slice_in_dim(packed, blocks + lane, 1)
         shared = packed[2 * blocks : 2 * blocks + 6]
         qv_bias_grad = jnp.concatenate([own[:, :cols], own[:, 2 * cols : 3 * cols]], 0)
         up_bias_grad = lax.dynamic_slice_in_dim(packed, lane, 1)[0]
         new_ranges = ema_decay * act_ranges + (1.0 - ema_decay) * packed[2 * blocks + 6, 0:512:128]
+        down_grad = down_grad.T
+        qkv_grad, out_grad = attn_grads(*line_a.value)
         return (
             layer_out,
             tokens_grad,

time: 215 us -> 218 us (1.014)
  starting transfers between devices: 64.7 us -> 67 us
    ppermute x69 -> x70, starting transfers between devices: 64.7 us -> 67 us  [step(): lax.ppermute(v, ALL, perm)]
    ppermute x69 -> x70, waiting for transfers between devices: 68.7 us -> 69.5 us  [step(): lax.ppermute(v, ALL, perm)]
  transfers between devices with their start and end apart: 69 -> 70, of which waited for: 34 -> 34; matrix products, arithmetic and copies ran while one was open for 1% -> 1% of each run, Pallas kernels for 25% -> 25%
where the time goes in v11:
time: 218 us; the launch traced here: 217 us
  Pallas kernels  69.5 us (32%)
  waiting for transfers between devices  69.5 us (32%)
  starting transfers between devices  67 us (31%)
  local copies, waits for them, and re-layouts  5.23 us (2%)
  other arithmetic  4.33 us (2%)
    ppermute x70, waiting for transfers between devices, step(): lax.ppermute(v, ALL, perm)  69.5 us
    ppermute x70, starting transfers between devices, step(): lax.ppermute(v, ALL, perm)  67 us
    pallas_call x11, Pallas kernels, step(): outs = run(*ins) if run else ins  66 us
  transfers between devices with their start and end apart: 70, of which 34 were waited for; matrix products, arithmetic and copies ran while one was open for 1% of the time, Pallas kernels for 25%

profile of v11, /device:TPU:0, one launch (start us, length us, event | category | flops | bytes accessed | tf_op | source)
XLA Modules:
  0.0 217.4 jit_solution(2830458186745910856)
XLA Ops:
  5.0 4.1 %collective-permute-start = (bf16[1,96,768]{2,1,0:T(8,128)(2,1)S(1)}, bf16[1,96,768]{2,1,0:T(8,128)(2,1)S(1)}, u32[]{:S(2)}, u32[]{:S(2)}) collective-permute-start(bf16[1,96,768]{2,1,0:T(8,128)(2,1)S(1)} %bitcast.18), channel_id=1, source_target_pairs={{0,16},{1,17},{2,18},{3,19},{4,20},{5,21},{6,22},{7,23},{8,24},{9,... | collective-permute-start | bytes 442376 | tf_op jit(solution)/shard_map/ppermute | solution.py:78
  9.1 1.5 collective-permute-start.1
  10.6 1.5 collective-permute-start.2
  12.7 3.1 %collective-permute-done.3 = f32[1,1408]{1,0:T(1,128)S(1)} collective-permute-done((f32[1,1408]{1,0:T(1,128)S(1)}, f32[1,1408]{1,0:T(1,128)S(1)}, u32[]{:S(2)}, u32[]{:S(2)}) %collective-permute-start.3) | collective-permute-done | bytes 5664 | tf_op jit(solution)/shard_map/ppermute | solution.py:78
  19.6 2.2 %collective-permute-done.5 = bf16[1,96,384]{2,1,0:T(8,128)(2,1)S(1)} collective-permute-done((bf16[1,96,384]{2,1,0:T(8,128)(2,1)S(1)}, bf16[1,96,384]{2,1,0:T(8,128)(2,1)S(1)}, u32[]{:S(2)}, u32[]{:S(2)}) %collective-permute-start.5) | collective-permute-done | bytes 73760 | tf_op jit(solution)/shard_map/ppermute | solution.py:78
  21.8 2.6 %collective-permute-done.4 = bf16[2,96,768]{2,1,0:T(8,128)(2,1)S(1)} collective-permute-done((bf16[2,96,768]{2,1,0:T(8,128)(2,1)S(1)}, bf16[2,96,768]{2,1,0:T(8,128)(2,1)S(1)}, u32[]{:S(2)}, u32[]{:S(2)}) %collective-permute-start.4) | collective-permute-done | bytes 294944 | tf_op jit(solution)/shard_map/ppermute | solution.py:78
  25.8 1.5 collective-permute-start.8
  27.4 3.3 %collective-permute-start.11 = (bf16[1,96,384]{2,1,0:T(8,128)(2,1)S(1)}, bf16[1,96,384]{2,1,0:T(8,128)(2,1)S(1)}, u32[]{:S(2)}, u32[]{:S(2)}) collective-permute-start(bf16[1,96,384]{2,1,0:T(8,128)(2,1)S(1)} %bitcast.24), channel_id=1, source_target_pairs={{0,16},{1,17},{2,18},{3,19},{4,20},{5,21},{6,22},{7,23},{8,24},{9,... | collective-permute-start | bytes 221192 | tf_op jit(solution)/shard_map/ppermute | solution.py:78
  31.4 4.0 %collective-permute-done.11 = bf16[1,96,384]{2,1,0:T(8,128)(2,1)S(1)} collective-permute-done((bf16[1,96,384]{2,1,0:T(8,128)(2,1)S(1)}, bf16[1,96,384]{2,1,0:T(8,128)(2,1)S(1)}, u32[]{:S(2)}, u32[]{:S(2)}) %collective-permute-start.11) | collective-permute-done | bytes 73760 | tf_op jit(solution)/shard_map/ppermute | solution.py:78
  35.4 6.1 %collective-permute-done.10 = bf16[1,96,768]{2,1,0:T(8,128)(2,1)S(1)} collective-permute-done((bf16[1,96,768]{2,1,0:T(8,128)(2,1)S(1)}, bf16[1,96,768]{2,1,0:T(8,128)(2,1)S(1)}, u32[]{:S(2)}, u32[]{:S(2)}) %collective-permute-start.10) | collective-permute-done | bytes 147488 | tf_op jit(solution)/shard_map/ppermute | solution.py:78
  44.6 6.7 %collective-permute-done.12.rest_3_ = bf16[2,96,768]{2,1,0:T(8,128)(2,1)S(1)} collective-permute-done((bf16[2,96,768]{2,1,0:T(8,128)(2,1)S(1)}, bf16[2,96,768]{2,1,0:T(8,128)(2,1)S(1)}, u32[]{:S(2)}, u32[]{:S(2)}) %collective-permute-start.12) | collective-permute-done | bytes 294944 | tf_op jit(solution)/shard_map/ppermute | solution.py:78
  52.5 1.6 collective-permute-start.19
  54.1 1.5 collective-permute-start.20
  55.6 2.4 %collective-permute-start.23 = (bf16[4,96,384]{2,1,0:T(8,128)(2,1)S(1)}, bf16[4,96,384]{2,1,0:T(8,128)(2,1)S(1)}, u32[]{:S(2)}, u32[]{:S(2)}) collective-permute-start(bf16[4,96,384]{2,1,0:T(8,128)(2,1)S(1)} %pad_maximum_fusion.4), channel_id=1, source_target_pairs={{0,16},{1,17},{2,18},{3,19},{4,20},{5,21},{6,22},{7,23},{8,24},{9,... | collective-permute-start | bytes 884744 | tf_op jit(solution)/shard_map/ppermute | solution.py:78
  58.0 1.7 collective-permute-start.22
  59.8 11.5 %attn_forward.1 = (bf16[4,512,640]{2,1,0:T(8,128)(2,1)S(1)}, f32[4,8,512]{2,1,0:T(8,128)S(1)}, bf16[768,512]{1,0:T(8,128)(2,1)S(1)}, bf16[4,512,256]{2,1,0:T(8,1...) custom-call(f32[4]{0:T(128)S(1)} %copy-done.7, ...), custom_call_target="tpu_custom_call" | custom-call | flops 9663676416 | bytes 14155776 | tf_op jit(solution)/shard_map/attn_forward/pallas_call | solution.py:79
  75.2 3.3 %attn_finish.1 = (f32[512,768]{1,0:T(8,128)S(1)}, f32[512,1]{1,0:T(8,128)S(1)}, f32[512,768]{1,0:T(8,128)S(1)}, f32[512,768]{1,0:T(8,128)S(1)}, bf16[512,768]{1,...) custom-call(f32[4]{0:T(128)S(1)} %copy-done.7, ...), custom_call_target="tpu_custom_call" | custom-call | flops 4831838208 | bytes 9437184 | tf_op jit(solution)/shard_map/attn_finish/pallas_call | solution.py:79
  78.4 3.5 %collective-permute-done.24.rest_1_ = bf16[2,96,768]{2,1,0:T(8,128)(2,1)S(1)} collective-permute-done((bf16[2,96,768]{2,1,0:T(8,128)(2,1)S(1)}, bf16[2,96,768]{2,1,0:T(8,128)(2,1)S(1)}, u32[]{:S(2)}, u32[]{:S(2)}) %collective-permute-start.24) | collective-permute-done | bytes 294944 | tf_op jit(solution)/shard_map/ppermute | solution.py:78
  82.8 1.5 collective-permute-start.30
  85.1 4.2 %up_forward_0.1 = (bf16[2,512,768]{2,1,0:T(8,128)(2,1)S(1)}, f32[2,512,768]{2,1,0:T(8,128)S(1)}, f32[8,128]{1,0:T(8,128)S(1)}, bf16[2,768,768]{2,1,0:T(8,128)(2,1)S(1)}) custom-call(f32[4]{0:T(128)S(1)} %copy-done.7, bf16[512,768]{1,0:T(8,128)(2,1)S(1)} %get-tuple-element.494.mid_low, f32[4,1,1408]{2,1,0:T(1,128)S(1)} %bitcast.29, ...), custom_call_target="tpu_custom_call" | custom-call | flops 4831838208 | bytes 9437184 | tf_op jit(solution)/shard_map/up_forward_0/pallas_call | solution.py:79
  89.5 4.2 %up_forward_2.1 = (bf16[2,512,768]{2,1,0:T(8,128)(2,1)S(1)}, f32[2,512,768]{2,1,0:T(8,128)S(1)}, f32[8,128]{1,0:T(8,128)S(1)}, bf16[2,768,768]{2,1,0:T(8,128)(2,1)S(1)}) custom-call(f32[4]{0:T(128)S(1)} %copy-done.7, bf16[512,768]{1,0:T(8,128)(2,1)S(1)} %get-tuple-element.494.mid_low, f32[4,1,1408]{2,1,0:T(1,128)S(1)} %bitcast.30, ...), custom_call_target="tpu_custom_call" | custom-call | flops 4831838208 | bytes 9437184 | tf_op jit(solution)/shard_map/up_forward_2/pallas_call | solution.py:79
  96.0 4.5 %collective-permute-done.34.rest_3_ = bf16[2,96,384]{2,1,0:T(8,128)(2,1)S(1)} collective-permute-done((bf16[2,96,384]{2,1,0:T(8,128)(2,1)S(1)}, bf16[2,96,384]{2,1,0:T(8,128)(2,1)S(1)}, u32[]{:S(2)}, u32[]{:S(2)}) %collective-permute-start.34) | collective-permute-done | bytes 147488 | tf_op jit(solution)/shard_map/ppermute | solution.py:78
  101.8 2.0 collective-permute-done.38.rest_8_
  104.1 9.0 %down_both.1 = (bf16[512,768]{1,0:T(8,128)(2,1)}, f32[512,768]{1,0:T(8,128)S(1)}, bf16[768,512]{1,0:T(8,128)(2,1)S(1)}, f32[8,768]{1,0:T(8,128)S(1)}, bf16[4,512...) custom-call(bf16[2,512,768]{2,1,0:T(8,128)(2,1)S(1)} %get-tuple-element.570.act0.rest_0_, ...), custom_call_target="tpu_custom_call" | custom-call | flops 4831838208 | bytes 18874368 | tf_op jit(solution)/shard_map/down_both/pallas_call | solution.py:79
  113.2 2.7 %down_grad.1 = (bf16[2,8,96,768]{3,2,1,0:T(8,128)(2,1)S(1)}, bf16[2,8,96,768]{3,2,1,0:T(8,128)(2,1)S(1)}) custom-call(bf16[768,512]{1,0:T(8,128)(2,1)S(1)} %get-tuple-element.569.left_t, bf16[2,512,768]{2,1,0:T(8,128)(2,1)S(1)} %get-tuple-element.570.act0.rest_0_, bf16[2,512,768]{2,1,0:T(8,128)(2,1)S(1)} %get-tuple-element.571.act1.rest_1_), custom_call_target="tpu_custom_call" | custom-call | flops 2415919104 | bytes 4718592 | tf_op jit(solution)/shard_map/down_grad/pallas_call | solution.py:79
  116.1 2.7 %up_grad.1 = (bf16[2,8,96,768]{3,2,1,0:T(8,128)(2,1)S(1)}, bf16[2,8,96,768]{3,2,1,0:T(8,128)(2,1)S(1)}) custom-call(bf16[768,512]{1,0:T(8,128)(2,1)S(1)} %get-tuple-element.573.left_t, bf16[4,512,768]{2,1,0:T(8,128)(2,1)S(1)} %get-tuple-element.582.rest_0_.grad_up), custom_call_target="tpu_custom_call" | custom-call | flops 2415919104 | bytes 4718592 | tf_op jit(solution)/shard_map/up_grad/pallas_call | solution.py:79
  118.8 1.7 collective-permute-done.42.got
  121.7 4.7 %mid_backward.1 = (f32[512,768]{1,0:T(8,128)S(1)}, bf16[512,768]{1,0:T(8,128)(2,1)S(1)}, bf16[768,512]{1,0:T(8,128)(2,1)S(1)}, f32[8,768]{1,0:T(8,128)S(1)}) custom-call(bf16[4,512,768]{2,1,0:T(8,128)(2,1)S(1)} %get-tuple-element.582.rest_0_.grad_up, f32[512,768]{1,0:T(8,128)S(1)} %get-tuple-element.583.grad_second, ...), custom_call_target="tpu_custom_call" | custom-call | flops 3221225472 | bytes 14155776 | tf_op jit(solution)/shard_map/mid_backward/pallas_call | solution.py:79
  126.5 1.6 collective-permute-start.44
  128.9 9.4 %attn_backward.1 = (bf16[2,512,640]{2,1,0:T(8,128)(2,1)S(1)}, bf16[1,8,96,768]{3,2,1,0:T(8,128)(2,1)S(1)}, bf16[1,8,96,768]{3,2,1,0:T(8,128)(2,1)S(1)}, f32[4,1,640]{2,1,0:T(1,128)S(1)}) custom-call(s32[1]{0:T(128)S(6)} %copy.37.longs, s32[12]{0:T(128)S(1)} %copy-done.14, bf16[4,512,640]{2,1,0:T(8,128)(2,1)S(1)} %get-tuple-element.639.qkv, ...), custom_call_target="tpu_custom_call" | custom-call | flops 4831838208 | bytes 9437184 | tf_op jit(solution)/shard_map/attn_backward/pallas_call | solution.py:79
  143.5 2.2 %collective-permute-done.49.from_x = bf16[96,768]{1,0:T(8,128)(2,1)S(1)} collective-permute-done((bf16[96,768]{1,0:T(8,128)(2,1)S(1)}, bf16[96,768]{1,0:T(8,128)(2,1)S(1)}, u32[]{:S(2)}, u32[]{:S(2)}) %collective-permute-start.49) | collective-permute-done | bytes 147488 | tf_op jit(solution)/shard_map/ppermute | solution.py:78
  146.9 9.3 %attn_backward_last.1 = (bf16[2,512,640]{2,1,0:T(8,128)(2,1)S(1)}, bf16[1,8,96,768]{3,2,1,0:T(8,128)(2,1)S(1)}, bf16[1,8,96,768]{3,2,1,0:T(8,128)(2,1)S(1)}, f32[16,768]{1,0:T(8,128)S(1)}) custom-call(s32[1]{0:T(128)S(6)} %copy.37.longs, s32[12]{0:T(128)S(1)} %copy-done.14, bf16[4,512,640]{2,1,0:T(8,128)(2,1)S(1)} %get-tuple-element.639.qkv, ...), custom_call_target="tpu_custom_call" | custom-call | flops 9663676416 | bytes 9437184 | tf_op jit(solution)/shard_map/attn_backward_last/pallas_call | solution.py:79
  156.2 3.1 %collective-permute-done.50.from_y = bf16[96,768]{1,0:T(8,128)(2,1)S(1)} collective-permute-done((bf16[96,768]{1,0:T(8,128)(2,1)S(1)}, bf16[96,768]{1,0:T(8,128)(2,1)S(1)}, u32[]{:S(2)}, u32[]{:S(2)}) %collective-permute-start.50) | collective-permute-done | bytes 147488 | tf_op jit(solution)/shard_map/ppermute | solution.py:78
  161.6 1.5 collective-permute-start.56
  164.3 5.1 %token_backward.1 = bf16[512,768]{1,0:T(8,128)(2,1)} custom-call(f32[4]{0:T(128)S(1)} %copy-done.7, bf16[2,512,640]{2,1,0:T(8,128)(2,1)S(1)} %get-tuple-element.678.grads_0, bf16[2,512,640]{2,1,0:T(8,128)(2,1)S(1)} %get-tuple-element.679.grads_1, f32[512,768]{1,0:T(8,128)S(1)} %get-tuple-element.680.grad_first, bf16[512,768]{1,0:T(8,128)(2,1)S(1)} %copy-done, ...), custom_call_target="tpu_custom_call" | custom-call | flops 2415919104 | bytes 9437184 | tf_op jit(solution)/shard_map/token_backward/pallas_call | solution.py:79
  170.3 5.2 %collective-permute-done.56.in_x = bf16[2,96,768]{2,1,0:T(8,128)(2,1)S(1)} collective-permute-done((bf16[2,96,768]{2,1,0:T(8,128)(2,1)S(1)}, bf16[2,96,768]{2,1,0:T(8,128)(2,1)S(1)}, u32[]{:S(2)}, u32[]{:S(2)}) %collective-permute-start.56) | collective-permute-done | bytes 294944 | tf_op jit(solution)/shard_map/ppermute | solution.py:78
  176.4 1.6 collective-permute-start.60
  178.0 1.5 collective-permute-start.58
  180.4 2.1 collective-permute-start.61
  183.8 3.3 %collective-permute-done.61 = bf16[96,768]{1,0:T(8,128)(2,1)S(1)} collective-permute-done((bf16[96,768]{1,0:T(8,128)(2,1)S(1)}, bf16[96,768]{1,0:T(8,128)(2,1)S(1)}, u32[]{:S(2)}, u32[]{:S(2)}) %collective-permute-start.61) | collective-permute-done | bytes 147488 | tf_op jit(solution)/shard_map/ppermute | solution.py:78
  188.0 2.6 %collective-permute-start.63 = (bf16[96,768]{1,0:T(8,128)(2,1)S(1)}, bf16[96,768]{1,0:T(8,128)(2,1)S(1)}, u32[]{:S(2)}, u32[]{:S(2)}) collective-permute-start(bf16[96,768]{1,0:T(8,128)(2,1)S(1)} %get-tuple-element.711), channel_id=1, source_target_pairs={{0,16},{1,17},{2,18},{3,19},{4,20},{5,21},{6,22},{7,23},{8,24},{9,... | collective-permute-start | bytes 442376 | tf_op jit(solution)/shard_map/ppermute | solution.py:78
  190.5 2.4 %collective-permute-start.64 = (f32[16,768]{1,0:T(8,128)S(1)}, f32[16,768]{1,0:T(8,128)S(1)}, u32[]{:S(2)}, u32[]{:S(2)}) collective-permute-start(f32[16,768]{1,0:T(8,128)S(1)} %add_select_fusion.4), channel_id=1, source_target_pairs={{0,8},{1,9},{2,10},{3,11},{4,12},{5,13},{6,14},{7,15},{8,0},{9,1},... | collective-permute-start | bytes 147464 | tf_op jit(solution)/shard_map/ppermute | solution.py:78
  192.9 3.0 %collective-permute-done.64 = f32[16,768]{1,0:T(8,128)S(1)} collective-permute-done((f32[16,768]{1,0:T(8,128)S(1)}, f32[16,768]{1,0:T(8,128)S(1)}, u32[]{:S(2)}, u32[]{:S(2)}) %collective-permute-start.64) | collective-permute-done | bytes 49184 | tf_op jit(solution)/shard_map/ppermute | solution.py:78
  197.9 2.6 %collective-permute-start.66 = (f32[16,768]{1,0:T(8,128)S(1)}, f32[16,768]{1,0:T(8,128)S(1)}, u32[]{:S(2)}, u32[]{:S(2)}) collective-permute-start(f32[16,768]{1,0:T(8,128)S(1)} %add_select_fusion.3), channel_id=1, source_target_pairs={{0,16},{1,17},{2,18},{3,19},{4,20},{5,21},{6,22},{7,23},{8,24},{9,... | collective-permute-start | bytes 147464 | tf_op jit(solution)/shard_map/ppermute | solution.py:78
  200.5 2.5 %collective-permute-done.66 = f32[16,768]{1,0:T(8,128)S(1)} collective-permute-done((f32[16,768]{1,0:T(8,128)S(1)}, f32[16,768]{1,0:T(8,128)S(1)}, u32[]{:S(2)}, u32[]{:S(2)}) %collective-permute-start.66) | collective-permute-done | bytes 49184 | tf_op jit(solution)/shard_map/ppermute | solution.py:78
  203.0 2.2 %collective-permute-done.65.from_z = bf16[2,96,768]{2,1,0:T(8,128)(2,1)S(1)} collective-permute-done((bf16[2,96,768]{2,1,0:T(8,128)(2,1)S(1)}, bf16[2,96,768]{2,1,0:T(8,128)(2,1)S(1)}, u32[]{:S(2)}, u32[]{:S(2)}) %collective-permute-start.65) | collective-permute-done | bytes 294944 | tf_op jit(solution)/shard_map/ppermute | solution.py:78
  205.3 2.3 %collective-permute-start.68 = (f32[16,768]{1,0:T(8,128)S(1)}, f32[16,768]{1,0:T(8,128)S(1)}, u32[]{:S(2)}, u32[]{:S(2)}) collective-permute-start(f32[16,768]{1,0:T(8,128)S(1)} %add_select_fusion.2), channel_id=1, source_target_pairs={{0,2},{1,3},{2,0},{3,1},{4,6},{5,7},{6,4},{7,5},{8,10},{9,11},{10,... | collective-permute-start | bytes 147464 | tf_op jit(solution)/shard_map/ppermute | solution.py:78
  210.9 3.0 %collective-permute-done.69 = f32[16,768]{1,0:T(8,128)S(1)} collective-permute-done((f32[16,768]{1,0:T(8,128)S(1)}, f32[16,768]{1,0:T(8,128)S(1)}, u32[]{:S(2)}, u32[]{:S(2)}) %collective-permute-start.69) | collective-permute-done | bytes 49184 | tf_op jit(solution)/shard_map/ppermute | solution.py:78
  (181 shorter events, 49.5 us)
Async XLA Ops:
  5.0 11.1 %collective-permute-start = (bf16[1,96,768]{2,1,0:T(8,128)(2,1)S(1)}, bf16[1,96,768]{2,1,0:T(8,128)(2,1)S(1)}, u32[]{:S(2)}, u32[]{:S(2)}) collective-permute-start(bf16[1,96,768]{2,1,0:T(8,128)(2,1)S(1)} %bitcast.18), channel_id=1, source_target_pairs={{0,16},{1,17},{2,18},{3,19},{4,20},{5,21},{6,22},{7,23},{8,24},{9,... | collective-permute-start | bytes 442376 | tf_op jit(solution)/shard_map/ppermute | solution.py:78
  16.2 8.2 %collective-permute-start.4 = (bf16[2,96,768]{2,1,0:T(8,128)(2,1)S(1)}, bf16[2,96,768]{2,1,0:T(8,128)(2,1)S(1)}, u32[]{:S(2)}, u32[]{:S(2)}) collective-permute-start(bf16[2,96,768]{2,1,0:T(8,128)(2,1)S(1)} %pad_maximum_fusion.2), channel_id=1, source_target_pairs={{0,8},{1,9},{2,10},{3,11},{4,12},{5,13},{6,14},{7,15},{8,0},{9,1},... | collective-permute-start | bytes 884744 | tf_op jit(solution)/shard_map/ppermute | solution.py:78
  24.5 17.0 %collective-permute-start.7 = (bf16[4,96,768]{2,1,0:T(8,128)(2,1)S(1)}, bf16[4,96,768]{2,1,0:T(8,128)(2,1)S(1)}, u32[]{:S(2)}, u32[]{:S(2)}) collective-permute-start(bf16[4,96,768]{2,1,0:T(8,128)(2,1)S(1)} %pad_maximum_fusion.rest_0_), channel_id=1, source_target_pairs={{0,2},{1,3},{2,0},{3,1},{4,6},{5,7},{6,4},{7,5},{8,10},{9,11},{10,... | collective-permute-start | bytes 1769480 | tf_op jit(solution)/shard_map/ppermute | solution.py:78
  25.8 15.7 %collective-permute-start.8 = (bf16[4,96,768]{2,1,0:T(8,128)(2,1)S(1)}, bf16[4,96,768]{2,1,0:T(8,128)(2,1)S(1)}, u32[]{:S(2)}, u32[]{:S(2)}) collective-permute-start(bf16[4,96,768]{2,1,0:T(8,128)(2,1)S(1)} %pad_maximum_fusion.rest_0_), channel_id=1, source_target_pairs={{0,4},{1,5},{2,6},{3,7},{4,0},{5,1},{6,2},{7,3},{8,12},{9,13},{10,... | collective-permute-start | bytes 1769480 | tf_op jit(solution)/shard_map/ppermute | solution.py:78
  27.4 14.2 %collective-permute-start.9 = (bf16[4,96,768]{2,1,0:T(8,128)(2,1)S(1)}, bf16[4,96,768]{2,1,0:T(8,128)(2,1)S(1)}, u32[]{:S(2)}, u32[]{:S(2)}) collective-permute-start(bf16[4,96,768]{2,1,0:T(8,128)(2,1)S(1)} %pad_maximum_fusion.rest_0_), channel_id=1, source_target_pairs={{0,1},{1,0},{2,3},{3,2},{4,5},{5,4},{6,7},{7,6},{8,9},{9,8},{10,11... | collective-permute-start | bytes 1769480 | tf_op jit(solution)/shard_map/ppermute | solution.py:78
  27.4 8.0 %collective-permute-start.11 = (bf16[1,96,384]{2,1,0:T(8,128)(2,1)S(1)}, bf16[1,96,384]{2,1,0:T(8,128)(2,1)S(1)}, u32[]{:S(2)}, u32[]{:S(2)}) collective-permute-start(bf16[1,96,384]{2,1,0:T(8,128)(2,1)S(1)} %bitcast.24), channel_id=1, source_target_pairs={{0,16},{1,17},{2,18},{3,19},{4,20},{5,21},{6,22},{7,23},{8,24},{9,... | collective-permute-start | bytes 221192 | tf_op jit(solution)/shard_map/ppermute | solution.py:78
  30.7 10.8 %collective-permute-start.10 = (bf16[1,96,768]{2,1,0:T(8,128)(2,1)S(1)}, bf16[1,96,768]{2,1,0:T(8,128)(2,1)S(1)}, u32[]{:S(2)}, u32[]{:S(2)}) collective-permute-start(bf16[1,96,768]{2,1,0:T(8,128)(2,1)S(1)} %convert_bitcast_fusion), channel_id=1, source_target_pairs={{0,16},{1,17},{2,18},{3,19},{4,20},{5,21},{6,22},{7,23},{8,24},{9,... | collective-permute-start | bytes 442376 | tf_op jit(solution)/shard_map/ppermute | solution.py:78
  41.7 10.2 %collective-permute-start.14 = (bf16[4,96,768]{2,1,0:T(8,128)(2,1)S(1)}, bf16[4,96,768]{2,1,0:T(8,128)(2,1)S(1)}, u32[]{:S(2)}, u32[]{:S(2)}) collective-permute-start(bf16[4,96,768]{2,1,0:T(8,128)(2,1)S(1)} %collective-permute-done.8.rest_1_), channel_id=1, source_target_pairs={{0,1},{1,0},{2,3},{3,2},{4,5},{5,4},{6,7},{7,6},{8,9},{9,8},{10,11... | collective-permute-start | bytes 1769480 | tf_op jit(solution)/shard_map/ppermute | solution.py:78
  41.8 10.1 %collective-permute-start.15 = (bf16[4,96,768]{2,1,0:T(8,128)(2,1)S(1)}, bf16[4,96,768]{2,1,0:T(8,128)(2,1)S(1)}, u32[]{:S(2)}, u32[]{:S(2)}) collective-permute-start(bf16[4,96,768]{2,1,0:T(8,128)(2,1)S(1)} %collective-permute-done.7.rest_2_), channel_id=1, source_target_pairs={{0,1},{1,0},{2,3},{3,2},{4,5},{5,4},{6,7},{7,6},{8,9},{9,8},{10,11... | collective-permute-start | bytes 1769480 | tf_op jit(solution)/shard_map/ppermute | solution.py:78
  42.3 9.1 %collective-permute-start.12 = (bf16[2,96,768]{2,1,0:T(8,128)(2,1)S(1)}, bf16[2,96,768]{2,1,0:T(8,128)(2,1)S(1)}, u32[]{:S(2)}, u32[]{:S(2)}) collective-permute-start(bf16[2,96,768]{2,1,0:T(8,128)(2,1)S(1)} %slice.52), channel_id=1, source_target_pairs={{0,2},{1,3},{2,0},{3,1},{4,6},{5,7},{6,4},{7,5},{8,10},{9,11},{10,... | collective-permute-start | bytes 884744 | tf_op jit(solution)/shard_map/ppermute | solution.py:78
  42.9 8.7 %collective-permute-start.13 = (bf16[2,96,768]{2,1,0:T(8,128)(2,1)S(1)}, bf16[2,96,768]{2,1,0:T(8,128)(2,1)S(1)}, u32[]{:S(2)}, u32[]{:S(2)}) collective-permute-start(bf16[2,96,768]{2,1,0:T(8,128)(2,1)S(1)} %slice.53), channel_id=1, source_target_pairs={{0,4},{1,5},{2,6},{3,7},{4,0},{5,1},{6,2},{7,3},{8,12},{9,13},{10,... | collective-permute-start | bytes 884744 | tf_op jit(solution)/shard_map/ppermute | solution.py:78
  43.4 8.4 %collective-permute-start.16 = (bf16[2,96,768]{2,1,0:T(8,128)(2,1)S(1)}, bf16[2,96,768]{2,1,0:T(8,128)(2,1)S(1)}, u32[]{:S(2)}, u32[]{:S(2)}) collective-permute-start(bf16[2,96,768]{2,1,0:T(8,128)(2,1)S(1)} %pad_maximum_fusion.3), channel_id=1, source_target_pairs={{0,8},{1,9},{2,10},{3,11},{4,12},{5,13},{6,14},{7,15},{8,0},{9,1},... | collective-permute-start | bytes 884744 | tf_op jit(solution)/shard_map/ppermute | solution.py:78
  52.5 19.7 %collective-permute-start.19 = (bf16[4,96,768]{2,1,0:T(8,128)(2,1)S(1)}, bf16[4,96,768]{2,1,0:T(8,128)(2,1)S(1)}, u32[]{:S(2)}, u32[]{:S(2)}) collective-permute-start(bf16[4,96,768]{2,1,0:T(8,128)(2,1)S(1)} %pad_maximum_fusion.1.rest_0_), channel_id=1, source_target_pairs={{0,2},{1,3},{2,0},{3,1},{4,6},{5,7},{6,4},{7,5},{8,10},{9,11},{10,... | collective-permute-start | bytes 1769480 | tf_op jit(solution)/shard_map/ppermute | solution.py:78
  54.1 18.2 %collective-permute-start.20 = (bf16[4,96,768]{2,1,0:T(8,128)(2,1)S(1)}, bf16[4,96,768]{2,1,0:T(8,128)(2,1)S(1)}, u32[]{:S(2)}, u32[]{:S(2)}) collective-permute-start(bf16[4,96,768]{2,1,0:T(8,128)(2,1)S(1)} %pad_maximum_fusion.1.rest_0_), channel_id=1, source_target_pairs={{0,4},{1,5},{2,6},{3,7},{4,0},{5,1},{6,2},{7,3},{8,12},{9,13},{10,... | collective-permute-start | bytes 1769480 | tf_op jit(solution)/shard_map/ppermute | solution.py:78
  55.6 16.7 %collective-permute-start.21 = (bf16[4,96,768]{2,1,0:T(8,128)(2,1)S(1)}, bf16[4,96,768]{2,1,0:T(8,128)(2,1)S(1)}, u32[]{:S(2)}, u32[]{:S(2)}) collective-permute-start(bf16[4,96,768]{2,1,0:T(8,128)(2,1)S(1)} %pad_maximum_fusion.1.rest_0_), channel_id=1, source_target_pairs={{0,1},{1,0},{2,3},{3,2},{4,5},{5,4},{6,7},{7,6},{8,9},{9,8},{10,11... | collective-permute-start | bytes 1769480 | tf_op jit(solution)/shard_map/ppermute | solution.py:78
  55.6 16.6 %collective-permute-start.23 = (bf16[4,96,384]{2,1,0:T(8,128)(2,1)S(1)}, bf16[4,96,384]{2,1,0:T(8,128)(2,1)S(1)}, u32[]{:S(2)}, u32[]{:S(2)}) collective-permute-start(bf16[4,96,384]{2,1,0:T(8,128)(2,1)S(1)} %pad_maximum_fusion.4), channel_id=1, source_target_pairs={{0,16},{1,17},{2,18},{3,19},{4,20},{5,21},{6,22},{7,23},{8,24},{9,... | collective-permute-start | bytes 884744 | tf_op jit(solution)/shard_map/ppermute | solution.py:78
  58.0 13.3 %collective-permute-start.22 = (bf16[2,96,384]{2,1,0:T(8,128)(2,1)S(1)}, bf16[2,96,384]{2,1,0:T(8,128)(2,1)S(1)}, u32[]{:S(2)}, u32[]{:S(2)}) collective-permute-start(bf16[2,96,384]{2,1,0:T(8,128)(2,1)S(1)} %pad_maximum_fusion.6), channel_id=1, source_target_pairs={{0,8},{1,9},{2,10},{3,11},{4,12},{5,13},{6,14},{7,15},{8,0},{9,1},... | collective-permute-start | bytes 442376 | tf_op jit(solution)/shard_map/ppermute | solution.py:78
  72.4 9.8 %collective-permute-start.26 = (bf16[4,96,768]{2,1,0:T(8,128)(2,1)S(1)}, bf16[4,96,768]{2,1,0:T(8,128)(2,1)S(1)}, u32[]{:S(2)}, u32[]{:S(2)}) collective-permute-start(bf16[4,96,768]{2,1,0:T(8,128)(2,1)S(1)} %collective-permute-done.20.rest_1_), channel_id=1, source_target_pairs={{0,1},{1,0},{2,3},{3,2},{4,5},{5,4},{6,7},{7,6},{8,9},{9,8},{10,11... | collective-permute-start | bytes 1769480 | tf_op jit(solution)/shard_map/ppermute | solution.py:78
  72.5 9.8 %collective-permute-start.27 = (bf16[4,96,768]{2,1,0:T(8,128)(2,1)S(1)}, bf16[4,96,768]{2,1,0:T(8,128)(2,1)S(1)}, u32[]{:S(2)}, u32[]{:S(2)}) collective-permute-start(bf16[4,96,768]{2,1,0:T(8,128)(2,1)S(1)} %collective-permute-done.19.rest_0_), channel_id=1, source_target_pairs={{0,1},{1,0},{2,3},{3,2},{4,5},{5,4},{6,7},{7,6},{8,9},{9,8},{10,11... | collective-permute-start | bytes 1769480 | tf_op jit(solution)/shard_map/ppermute | solution.py:78
  73.0 9.0 %collective-permute-start.24 = (bf16[2,96,768]{2,1,0:T(8,128)(2,1)S(1)}, bf16[2,96,768]{2,1,0:T(8,128)(2,1)S(1)}, u32[]{:S(2)}, u32[]{:S(2)}) collective-permute-start(bf16[2,96,768]{2,1,0:T(8,128)(2,1)S(1)} %slice.54), channel_id=1, source_target_pairs={{0,2},{1,3},{2,0},{3,1},{4,6},{5,7},{6,4},{7,5},{8,10},{9,11},{10,... | collective-permute-start | bytes 884744 | tf_op jit(solution)/shard_map/ppermute | solution.py:78
  73.5 8.7 %collective-permute-start.25 = (bf16[2,96,768]{2,1,0:T(8,128)(2,1)S(1)}, bf16[2,96,768]{2,1,0:T(8,128)(2,1)S(1)}, u32[]{:S(2)}, u32[]{:S(2)}) collective-permute-start(bf16[2,96,768]{2,1,0:T(8,128)(2,1)S(1)} %slice.55), channel_id=1, source_target_pairs={{0,4},{1,5},{2,6},{3,7},{4,0},{5,1},{6,2},{7,3},{8,12},{9,13},{10,... | collective-permute-start | bytes 884744 | tf_op jit(solution)/shard_map/ppermute | solution.py:78
  74.4 19.2 %collective-permute-start.33 = (bf16[8,96,384]{2,1,0:T(8,128)(2,1)S(1)}, bf16[8,96,384]{2,1,0:T(8,128)(2,1)S(1)}, u32[]{:S(2)}, u32[]{:S(2)}) collective-permute-start(bf16[8,96,384]{2,1,0:T(8,128)(2,1)S(1)} %get-tuple-element.553.rest_10_), channel_id=1, source_target_pairs={{0,8},{1,9},{2,10},{3,11},{4,12},{5,13},{6,14},{7,15},{8,0},{9,1},... | collective-permute-start | bytes 1769480 | tf_op jit(solution)/shard_map/ppermute | solution.py:78
  82.2 7.1 %collective-permute-start.28 = (bf16[2,96,768]{2,1,0:T(8,128)(2,1)S(1)}, bf16[2,96,768]{2,1,0:T(8,128)(2,1)S(1)}, u32[]{:S(2)}, u32[]{:S(2)}) collective-permute-start(bf16[2,96,768]{2,1,0:T(8,128)(2,1)S(1)} %collective-permute-done.24.rest_1_), channel_id=1, source_target_pairs={{0,1},{1,0},{2,3},{3,2},{4,5},{5,4},{6,7},{7,6},{8,9},{9,8},{10,11... | collective-permute-start | bytes 884744 | tf_op jit(solution)/shard_map/ppermute | solution.py:78
  82.3 7.2 %collective-permute-start.29 = (bf16[2,96,768]{2,1,0:T(8,128)(2,1)S(1)}, bf16[2,96,768]{2,1,0:T(8,128)(2,1)S(1)}, u32[]{:S(2)}, u32[]{:S(2)}) collective-permute-start(bf16[2,96,768]{2,1,0:T(8,128)(2,1)S(1)} %collective-permute-done.25.rest_2_), channel_id=1, source_target_pairs={{0,1},{1,0},{2,3},{3,2},{4,5},{5,4},{6,7},{7,6},{8,9},{9,8},{10,11... | collective-permute-start | bytes 884744 | tf_op jit(solution)/shard_map/ppermute | solution.py:78
  82.8 10.9 %collective-permute-start.30 = (bf16[4,96,384]{2,1,0:T(8,128)(2,1)S(1)}, bf16[4,96,384]{2,1,0:T(8,128)(2,1)S(1)}, u32[]{:S(2)}, u32[]{:S(2)}) collective-permute-start(bf16[4,96,384]{2,1,0:T(8,128)(2,1)S(1)} %get-tuple-element.543.rest_0_), channel_id=1, source_target_pairs={{0,2},{1,3},{2,0},{3,1},{4,6},{5,7},{6,4},{7,5},{8,10},{9,11},{10,... | collective-permute-start | bytes 884744 | tf_op jit(solution)/shard_map/ppermute | solution.py:78
  84.3 9.4 %collective-permute-start.31 = (bf16[4,96,384]{2,1,0:T(8,128)(2,1)S(1)}, bf16[4,96,384]{2,1,0:T(8,128)(2,1)S(1)}, u32[]{:S(2)}, u32[]{:S(2)}) collective-permute-start(bf16[4,96,384]{2,1,0:T(8,128)(2,1)S(1)} %get-tuple-element.543.rest_0_), channel_id=1, source_target_pairs={{0,4},{1,5},{2,6},{3,7},{4,0},{5,1},{6,2},{7,3},{8,12},{9,13},{10,... | collective-permute-start | bytes 884744 | tf_op jit(solution)/shard_map/ppermute | solution.py:78
  93.7 7.1 %collective-permute-start.36 = (bf16[4,96,384]{2,1,0:T(8,128)(2,1)S(1)}, bf16[4,96,384]{2,1,0:T(8,128)(2,1)S(1)}, u32[]{:S(2)}, u32[]{:S(2)}) collective-permute-start(bf16[4,96,384]{2,1,0:T(8,128)(2,1)S(1)} %collective-permute-done.31.rest_1_), channel_id=1, source_target_pairs={{0,1},{1,0},{2,3},{3,2},{4,5},{5,4},{6,7},{7,6},{8,9},{9,8},{10,11... | collective-permute-start | bytes 884744 | tf_op jit(solution)/shard_map/ppermute | solution.py:78
  121.0 17.4 %collective-permute-start.46 = (bf16[4,96,768]{2,1,0:T(8,128)(2,1)S(1)}, bf16[4,96,768]{2,1,0:T(8,128)(2,1)S(1)}, u32[]{:S(2)}, u32[]{:S(2)}) collective-permute-start(bf16[4,96,768]{2,1,0:T(8,128)(2,1)S(1)} %get-tuple-element.619), channel_id=1, source_target_pairs={{0,8},{1,9},{2,10},{3,11},{4,12},{5,13},{6,14},{7,15},{8,0},{9,1},... | collective-permute-start | bytes 1769480 | tf_op jit(solution)/shard_map/ppermute | solution.py:78
  126.5 11.9 %collective-permute-start.44 = (bf16[2,96,768]{2,1,0:T(8,128)(2,1)S(1)}, bf16[2,96,768]{2,1,0:T(8,128)(2,1)S(1)}, u32[]{:S(2)}, u32[]{:S(2)}) collective-permute-start(bf16[2,96,768]{2,1,0:T(8,128)(2,1)S(1)} %get-tuple-element.617), channel_id=1, source_target_pairs={{0,2},{1,3},{2,0},{3,1},{4,6},{5,7},{6,4},{7,5},{8,10},{9,11},{10,... | collective-permute-start | bytes 884744 | tf_op jit(solution)/shard_map/ppermute | solution.py:78
  128.1 10.3 %collective-permute-start.45 = (bf16[2,96,768]{2,1,0:T(8,128)(2,1)S(1)}, bf16[2,96,768]{2,1,0:T(8,128)(2,1)S(1)}, u32[]{:S(2)}, u32[]{:S(2)}) collective-permute-start(bf16[2,96,768]{2,1,0:T(8,128)(2,1)S(1)} %get-tuple-element.618), channel_id=1, source_target_pairs={{0,4},{1,5},{2,6},{3,7},{4,0},{5,1},{6,2},{7,3},{8,12},{9,13},{10,... | collective-permute-start | bytes 884744 | tf_op jit(solution)/shard_map/ppermute | solution.py:78
  138.9 20.7 %collective-permute-start.52 = (bf16[1,8,96,768]{3,2,1,0:T(8,128)(2,1)S(1)}, bf16[1,8,96,768]{3,2,1,0:T(8,128)(2,1)S(1)}, u32[]{:S(2)}, u32[]{:S(2)}) collective-permute-start(bf16[1,8,96,768]{3,2,1,0:T(8,128)(2,1)S(1)} %get-tuple-element.668), channel_id=1, source_target_pairs={{0,1},{1,0},{2,3},{3,2},{4,5},{5,4},{6,7},{7,6},{8,9},{9,8},{10,11... | collective-permute-start | bytes 3538952 | tf_op jit(solution)/shard_map/ppermute | solution.py:78
  139.0 6.8 %collective-permute-start.49 = (bf16[96,768]{1,0:T(8,128)(2,1)S(1)}, bf16[96,768]{1,0:T(8,128)(2,1)S(1)}, u32[]{:S(2)}, u32[]{:S(2)}) collective-permute-start(bf16[96,768]{1,0:T(8,128)(2,1)S(1)} %get-tuple-element.661), channel_id=1, source_target_pairs={{0,2},{1,3},{2,0},{3,1},{4,6},{5,7},{6,4},{7,5},{8,10},{9,11},{10,... | collective-permute-start | bytes 442376 | tf_op jit(solution)/shard_map/ppermute | solution.py:78
  139.6 19.8 %collective-permute-start.47 = (bf16[4,96,768]{2,1,0:T(8,128)(2,1)S(1)}, bf16[4,96,768]{2,1,0:T(8,128)(2,1)S(1)}, u32[]{:S(2)}, u32[]{:S(2)}) collective-permute-start(bf16[4,96,768]{2,1,0:T(8,128)(2,1)S(1)} %get-tuple-element.659), channel_id=1, source_target_pairs={{0,2},{1,3},{2,0},{3,1},{4,6},{5,7},{6,4},{7,5},{8,10},{9,11},{10,... | collective-permute-start | bytes 1769480 | tf_op jit(solution)/shard_map/ppermute | solution.py:78
  141.1 18.3 %collective-permute-start.48 = (bf16[4,96,768]{2,1,0:T(8,128)(2,1)S(1)}, bf16[4,96,768]{2,1,0:T(8,128)(2,1)S(1)}, u32[]{:S(2)}, u32[]{:S(2)}) collective-permute-start(bf16[4,96,768]{2,1,0:T(8,128)(2,1)S(1)} %get-tuple-element.660), channel_id=1, source_target_pairs={{0,4},{1,5},{2,6},{3,7},{4,0},{5,1},{6,2},{7,3},{8,12},{9,13},{10,... | collective-permute-start | bytes 1769480 | tf_op jit(solution)/shard_map/ppermute | solution.py:78
  142.2 17.1 %collective-permute-start.51 = (bf16[4,96,768]{2,1,0:T(8,128)(2,1)S(1)}, bf16[4,96,768]{2,1,0:T(8,128)(2,1)S(1)}, u32[]{:S(2)}, u32[]{:S(2)}) collective-permute-start(bf16[4,96,768]{2,1,0:T(8,128)(2,1)S(1)} %get-tuple-element.663), channel_id=1, source_target_pairs={{0,8},{1,9},{2,10},{3,11},{4,12},{5,13},{6,14},{7,15},{8,0},{9,1},... | collective-permute-start | bytes 1769480 | tf_op jit(solution)/shard_map/ppermute | solution.py:78
  145.7 13.6 %collective-permute-start.50 = (bf16[96,768]{1,0:T(8,128)(2,1)S(1)}, bf16[96,768]{1,0:T(8,128)(2,1)S(1)}, u32[]{:S(2)}, u32[]{:S(2)}) collective-permute-start(bf16[96,768]{1,0:T(8,128)(2,1)S(1)} %get-tuple-element.662), channel_id=1, source_target_pairs={{0,4},{1,5},{2,6},{3,7},{4,0},{5,1},{6,2},{7,3},{8,12},{9,13},{10,... | collective-permute-start | bytes 442376 | tf_op jit(solution)/shard_map/ppermute | solution.py:78
  159.8 16.1 %collective-permute-start.55 = (bf16[1,8,96,768]{3,2,1,0:T(8,128)(2,1)S(1)}, bf16[1,8,96,768]{3,2,1,0:T(8,128)(2,1)S(1)}, u32[]{:S(2)}, u32[]{:S(2)}) collective-permute-start(bf16[1,8,96,768]{3,2,1,0:T(8,128)(2,1)S(1)} %get-tuple-element.685), channel_id=1, source_target_pairs={{0,1},{1,0},{2,3},{3,2},{4,5},{5,4},{6,7},{7,6},{8,9},{9,8},{10,11... | collective-permute-start | bytes 3538952 | tf_op jit(solution)/shard_map/ppermute | solution.py:78
  159.8 9.9 %collective-permute-start.53 = (bf16[2,96,768]{2,1,0:T(8,128)(2,1)S(1)}, bf16[2,96,768]{2,1,0:T(8,128)(2,1)S(1)}, u32[]{:S(2)}, u32[]{:S(2)}) collective-permute-start(bf16[2,96,768]{2,1,0:T(8,128)(2,1)S(1)} %get-tuple-element.683), channel_id=1, source_target_pairs={{0,2},{1,3},{2,0},{3,1},{4,6},{5,7},{6,4},{7,5},{8,10},{9,11},{10,... | collective-permute-start | bytes 884744 | tf_op jit(solution)/shard_map/ppermute | solution.py:78
  160.4 9.9 %collective-permute-start.54 = (bf16[2,96,768]{2,1,0:T(8,128)(2,1)S(1)}, bf16[2,96,768]{2,1,0:T(8,128)(2,1)S(1)}, u32[]{:S(2)}, u32[]{:S(2)}) collective-permute-start(bf16[2,96,768]{2,1,0:T(8,128)(2,1)S(1)} %get-tuple-element.684), channel_id=1, source_target_pairs={{0,4},{1,5},{2,6},{3,7},{4,0},{5,1},{6,2},{7,3},{8,12},{9,13},{10,... | collective-permute-start | bytes 884744 | tf_op jit(solution)/shard_map/ppermute | solution.py:78
  161.6 14.0 %collective-permute-start.56 = (bf16[2,96,768]{2,1,0:T(8,128)(2,1)S(1)}, bf16[2,96,768]{2,1,0:T(8,128)(2,1)S(1)}, u32[]{:S(2)}, u32[]{:S(2)}) collective-permute-start(bf16[2,96,768]{2,1,0:T(8,128)(2,1)S(1)} %get-tuple-element.686), channel_id=1, source_target_pairs={{0,2},{1,3},{2,0},{3,1},{4,6},{5,7},{6,4},{7,5},{8,10},{9,11},{10,... | collective-permute-start | bytes 884744 | tf_op jit(solution)/shard_map/ppermute | solution.py:78
  163.1 12.7 %collective-permute-start.57 = (bf16[2,96,768]{2,1,0:T(8,128)(2,1)S(1)}, bf16[2,96,768]{2,1,0:T(8,128)(2,1)S(1)}, u32[]{:S(2)}, u32[]{:S(2)}) collective-permute-start(bf16[2,96,768]{2,1,0:T(8,128)(2,1)S(1)} %get-tuple-element.687), channel_id=1, source_target_pairs={{0,4},{1,5},{2,6},{3,7},{4,0},{5,1},{6,2},{7,3},{8,12},{9,13},{10,... | collective-permute-start | bytes 884744 | tf_op jit(solution)/shard_map/ppermute | solution.py:78
  176.4 11.5 %collective-permute-start.60 = (bf16[2,96,768]{2,1,0:T(8,128)(2,1)S(1)}, bf16[2,96,768]{2,1,0:T(8,128)(2,1)S(1)}, u32[]{:S(2)}, u32[]{:S(2)}) collective-permute-start(bf16[2,96,768]{2,1,0:T(8,128)(2,1)S(1)} %get-tuple-element.705), channel_id=1, source_target_pairs={{0,8},{1,9},{2,10},{3,11},{4,12},{5,13},{6,14},{7,15},{8,0},{9,1},... | collective-permute-start | bytes 884744 | tf_op jit(solution)/shard_map/ppermute | solution.py:78
  178.0 19.3 %collective-permute-start.58 = (bf16[4,96,768]{2,1,0:T(8,128)(2,1)S(1)}, bf16[4,96,768]{2,1,0:T(8,128)(2,1)S(1)}, u32[]{:S(2)}, u32[]{:S(2)}) collective-permute-start(bf16[4,96,768]{2,1,0:T(8,128)(2,1)S(1)} %get-tuple-element.702), channel_id=1, source_target_pairs={{0,2},{1,3},{2,0},{3,1},{4,6},{5,7},{6,4},{7,5},{8,10},{9,11},{10,... | collective-permute-start | bytes 1769480 | tf_op jit(solution)/shard_map/ppermute | solution.py:78
  179.5 17.8 %collective-permute-start.59 = (bf16[4,96,768]{2,1,0:T(8,128)(2,1)S(1)}, bf16[4,96,768]{2,1,0:T(8,128)(2,1)S(1)}, u32[]{:S(2)}, u32[]{:S(2)}) collective-permute-start(bf16[4,96,768]{2,1,0:T(8,128)(2,1)S(1)} %get-tuple-element.703), channel_id=1, source_target_pairs={{0,4},{1,5},{2,6},{3,7},{4,0},{5,1},{6,2},{7,3},{8,12},{9,13},{10,... | collective-permute-start | bytes 1769480 | tf_op jit(solution)/shard_map/ppermute | solution.py:78
  180.4 6.7 %collective-permute-start.61 = (bf16[96,768]{1,0:T(8,128)(2,1)S(1)}, bf16[96,768]{1,0:T(8,128)(2,1)S(1)}, u32[]{:S(2)}, u32[]{:S(2)}) collective-permute-start(bf16[96,768]{1,0:T(8,128)(2,1)S(1)} %get-tuple-element.706), channel_id=1, source_target_pairs={{0,16},{1,17},{2,18},{3,19},{4,20},{5,21},{6,22},{7,23},{8,24},{9,... | collective-permute-start | bytes 442376 | tf_op jit(solution)/shard_map/ppermute | solution.py:78
  188.0 9.3 %collective-permute-start.63 = (bf16[96,768]{1,0:T(8,128)(2,1)S(1)}, bf16[96,768]{1,0:T(8,128)(2,1)S(1)}, u32[]{:S(2)}, u32[]{:S(2)}) collective-permute-start(bf16[96,768]{1,0:T(8,128)(2,1)S(1)} %get-tuple-element.711), channel_id=1, source_target_pairs={{0,16},{1,17},{2,18},{3,19},{4,20},{5,21},{6,22},{7,23},{8,24},{9,... | collective-permute-start | bytes 442376 | tf_op jit(solution)/shard_map/ppermute | solution.py:78
  197.6 7.6 %collective-permute-start.65 = (bf16[2,96,768]{2,1,0:T(8,128)(2,1)S(1)}, bf16[2,96,768]{2,1,0:T(8,128)(2,1)S(1)}, u32[]{:S(2)}, u32[]{:S(2)}) collective-permute-start(bf16[2,96,768]{2,1,0:T(8,128)(2,1)S(1)} %get-tuple-element.718), channel_id=1, source_target_pairs={{0,8},{1,9},{2,10},{3,11},{4,12},{5,13},{6,14},{7,15},{8,0},{9,1},... | collective-permute-start | bytes 884744 | tf_op jit(solution)/shard_map/ppermute | solution.py:78
  207.7 6.9 %collective-permute-start.67 = (bf16[96,768]{1,0:T(8,128)(2,1)S(1)}, bf16[96,768]{1,0:T(8,128)(2,1)S(1)}, u32[]{:S(2)}, u32[]{:S(2)}) collective-permute-start(bf16[96,768]{1,0:T(8,128)(2,1)S(1)} %get-tuple-element.728), channel_id=1, source_target_pairs={{0,16},{1,17},{2,18},{3,19},{4,20},{5,21},{6,22},{7,23},{8,24},{9,... | collective-permute-start | bytes 442376 | tf_op jit(solution)/shard_map/ppermute | solution.py:78
  (37 other events, 222.2 us)

commit v12 on v9

--- a/solution.py
+++ b/solution.py
@@ -247,8 +247,7 @@
 
 VM = pl.BlockSpec(memory_space=pltpu.VMEM)
 SM = pl.BlockSpec(memory_space=pltpu.SMEM)
-VMEM_MIB = 8
-ROOMY = ("down_both",)
+VMEM_MIB = {"down_both": 14, "first_shards": 60}
 
 
 def like(shape, dtype=f32):
@@ -263,7 +262,7 @@
         in_specs=specs,
         out_specs=[VM] * len(outs),
         scratch_shapes=list(scratch),
-        compiler_params=pltpu.CompilerParams(vmem_limit_bytes=(14 if name in ROOMY else VMEM_MIB) * 2**20),
+        compiler_params=pltpu.CompilerParams(vmem_limit_bytes=VMEM_MIB.get(name, 8) * 2**20),
         cost_estimate=pl.CostEstimate(flops=flops, bytes_accessed=moved, transcendentals=0),
     )
 
@@ -383,7 +382,14 @@
     wide = 3 * cols + HEAD_DIM
     width = down_weight_t.shape[1]
 
-    def first_shards(qkv, out_weight, qv_bias, up_bias, down, attn, down_0, down_1, biases):
+    def first_shards(*refs):
+        sources, (attn, down_0, down_1, biases), locals_, sems = refs[:5], refs[5:9], refs[9:14], refs[14]
+        copies = [pltpu.make_async_copy(src, dst, sems.at[n]) for n, (src, dst) in enumerate(zip(sources, locals_))]
+        for copy in copies:
+            copy.start()
+        for copy in copies:
+            copy.wait()
+        qkv, out_weight, qv_bias, up_bias, down = locals_
         for j in range(3):
             attn[:, j * cols : (j + 1) * cols] = qkv[j].astype(bf16)
         attn[:, 3 * cols :] = out_weight[...].T.astype(bf16)
@@ -396,7 +402,9 @@
 
     part = like((rows, width // 2), bf16)
     outs = [like((rows, 4 * cols), bf16), part, part, like((1, wide + width))]
-    return glue(first_shards, outs, qkv_weight, out_weight, qv_bias, up_bias, down_weight_t)
+    ins = (qkv_weight, out_weight, qv_bias, up_bias, down_weight_t)
+    scratch = [pltpu.VMEM(value.shape, f32) for value in ins] + [pltpu.SemaphoreType.DMA((len(ins),))]
+    return call(first_shards, "first_shards", [pl.BlockSpec(memory_space=pltpu.HBM)] * len(ins), outs, scratch)(*ins)
 
 
 def assemble(plan, bufs, dst, dp):
@@ -957,11 +965,14 @@
         step((), None, [sum_a, line_u, sum_s], [sum_a, line_u, sum_s])
         line_a = Job(net.scatter_line(*sum_a.value))
         step((), None, [line_a, sum_s], [line_a, sum_s])
-        step((), None, [line_a, sum_s], [sum_s])
+
+        def finish(down, up):
+            return down[0] + down[1].astype(f32), up[0] + up[1].astype(f32)
+
+        down_grad, up_grad = step((sum_d.value, line_u.value), finish, [line_a, sum_s], [sum_s])
         step((), None, [sum_s], [line_a, sum_s])
 
         packed = sum_s.value
-        down_grad, up_grad = (kept + last.astype(f32) for kept, last in (sum_d.value, line_u.value))
         down_grad = down_grad.T
         qkv_grad, out_grad = attn_grads(*line_a.value)
         own = lax.dynamic_slice_in_dim(packed, blocks + lane, 1)

time: 215 us -> 215 us (level)
  local copies, waits for them, and re-layouts: 5.24 us -> 1.96 us
  other arithmetic: 4.32 us -> 6.83 us
    unnamed x34 -> x30, local copies, waits for them, and re-layouts: 4.3 us -> 1.02 us
  transfers between devices with their start and end apart: 69 -> 69, of which waited for: 34 -> 34; matrix products, arithmetic and copies ran while one was open for 1% -> 2% of each run, Pallas kernels for 25% -> 25%
where the time goes in v12:
time: 215 us
  Pallas kernels  71.3 us (33%)
  waiting for transfers between devices  67.7 us (31%)
  starting transfers between devices  65.1 us (30%)
  other arithmetic  6.83 us (3%)
    ppermute x69, waiting for transfers between devices, step(): lax.ppermute(v, ALL, perm)  67.7 us
    pallas_call x11, Pallas kernels, step(): outs = run(*ins) if run else ins  66 us
    ppermute x69, starting transfers between devices, step(): lax.ppermute(v, ALL, perm)  65.1 us
  transfers between devices with their start and end apart: 69, of which 34 were waited for; matrix products, arithmetic and copies ran while one was open for 2% of the time, Pallas kernels for 25%

profile of v12, /device:TPU:0, one launch (start us, length us, event | category | flops | bytes accessed | tf_op | source)
XLA Modules:
  0.0 214.7 jit_solution(12126740110701037890)
XLA Ops:
  0.6 2.0 first_shards.1
  2.7 4.1 %collective-permute-start = (bf16[1,96,768]{2,1,0:T(8,128)(2,1)}, bf16[1,96,768]{2,1,0:T(8,128)(2,1)S(1)}, u32[]{:S(2)}, u32[]{:S(2)}) collective-permute-start(bf16[1,96,768]{2,1,0:T(8,128)(2,1)} %bitcast.21), channel_id=1, source_target_pairs={{0,16},{1,17},{2,18},{3,19},{4,20},{5,21},{6,22},{7,23},{8,24},{9,... | collective-permute-start | bytes 442376 | tf_op jit(solution)/shard_map/ppermute | solution.py:78
  6.8 1.5 collective-permute-start.1
  8.3 1.5 collective-permute-start.2
  10.4 3.3 %collective-permute-done.3 = f32[1,1408]{1,0:T(1,128)S(1)} collective-permute-done((f32[1,1408]{1,0:T(1,128)}, f32[1,1408]{1,0:T(1,128)S(1)}, u32[]{:S(2)}, u32[]{:S(2)}) %collective-permute-start.3) | collective-permute-done | bytes 5664 | tf_op jit(solution)/shard_map/ppermute | solution.py:78
  19.2 2.1 collective-permute-done.5
  21.3 2.6 %collective-permute-done.4 = bf16[2,96,768]{2,1,0:T(8,128)(2,1)S(1)} collective-permute-done((bf16[2,96,768]{2,1,0:T(8,128)(2,1)S(1)}, bf16[2,96,768]{2,1,0:T(8,128)(2,1)S(1)}, u32[]{:S(2)}, u32[]{:S(2)}) %collective-permute-start.4) | collective-permute-done | bytes 294944 | tf_op jit(solution)/shard_map/ppermute | solution.py:78
  24.9 1.4 collective-permute-start.7
  26.3 1.5 collective-permute-start.8
  27.9 3.3 %collective-permute-start.11 = (bf16[1,96,384]{2,1,0:T(8,128)(2,1)}, bf16[1,96,384]{2,1,0:T(8,128)(2,1)S(1)}, u32[]{:S(2)}, u32[]{:S(2)}) collective-permute-start(bf16[1,96,384]{2,1,0:T(8,128)(2,1)} %bitcast.27), channel_id=1, source_target_pairs={{0,16},{1,17},{2,18},{3,19},{4,20},{5,21},{6,22},{7,23},{8,24},{9,... | collective-permute-start | bytes 221192 | tf_op jit(solution)/shard_map/ppermute | solution.py:78
  32.7 3.4 %collective-permute-done.11 = bf16[1,96,384]{2,1,0:T(8,128)(2,1)S(1)} collective-permute-done((bf16[1,96,384]{2,1,0:T(8,128)(2,1)}, bf16[1,96,384]{2,1,0:T(8,128)(2,1)S(1)}, u32[]{:S(2)}, u32[]{:S(2)}) %collective-permute-start.11) | collective-permute-done | bytes 73760 | tf_op jit(solution)/shard_map/ppermute | solution.py:78
  36.1 6.1 %collective-permute-done.10 = bf16[1,96,768]{2,1,0:T(8,128)(2,1)S(1)} collective-permute-done((bf16[1,96,768]{2,1,0:T(8,128)(2,1)S(1)}, bf16[1,96,768]{2,1,0:T(8,128)(2,1)S(1)}, u32[]{:S(2)}, u32[]{:S(2)}) %collective-permute-start.10) | collective-permute-done | bytes 147488 | tf_op jit(solution)/shard_map/ppermute | solution.py:78
  45.1 6.8 %collective-permute-done.12.rest_3_ = bf16[2,96,768]{2,1,0:T(8,128)(2,1)S(1)} collective-permute-done((bf16[2,96,768]{2,1,0:T(8,128)(2,1)S(1)}, bf16[2,96,768]{2,1,0:T(8,128)(2,1)S(1)}, u32[]{:S(2)}, u32[]{:S(2)}) %collective-permute-start.12) | collective-permute-done | bytes 294944 | tf_op jit(solution)/shard_map/ppermute | solution.py:78
  53.2 1.6 collective-permute-start.19
  54.7 1.5 collective-permute-start.20
  56.3 2.4 %collective-permute-start.23 = (bf16[4,96,384]{2,1,0:T(8,128)(2,1)S(1)}, bf16[4,96,384]{2,1,0:T(8,128)(2,1)S(1)}, u32[]{:S(2)}, u32[]{:S(2)}) collective-permute-start(bf16[4,96,384]{2,1,0:T(8,128)(2,1)S(1)} %pad_maximum_fusion.4), channel_id=1, source_target_pairs={{0,16},{1,17},{2,18},{3,19},{4,20},{5,21},{6,22},{7,23},{8,24},{9,... | collective-permute-start | bytes 884744 | tf_op jit(solution)/shard_map/ppermute | solution.py:78
  58.7 1.7 collective-permute-start.22
  60.4 11.5 %attn_forward.1 = (bf16[4,512,640]{2,1,0:T(8,128)(2,1)S(1)}, f32[4,8,512]{2,1,0:T(8,128)S(1)}, bf16[768,512]{1,0:T(8,128)(2,1)S(1)}, bf16[4,512,256]{2,1,0:T(8,1...) custom-call(f32[4]{0:T(128)S(1)} %copy-done.2, ...), custom_call_target="tpu_custom_call" | custom-call | flops 9663676416 | bytes 14155776 | tf_op jit(solution)/shard_map/attn_forward/pallas_call | solution.py:79
  75.6 3.3 %attn_finish.1 = (f32[512,768]{1,0:T(8,128)S(1)}, f32[512,1]{1,0:T(8,128)S(1)}, f32[512,768]{1,0:T(8,128)S(1)}, f32[512,768]{1,0:T(8,128)S(1)}, bf16[512,768]{1,...) custom-call(f32[4]{0:T(128)S(1)} %copy-done.2, ...), custom_call_target="tpu_custom_call" | custom-call | flops 4831838208 | bytes 9437184 | tf_op jit(solution)/shard_map/attn_finish/pallas_call | solution.py:79
  78.9 3.8 %collective-permute-done.24.rest_1_ = bf16[2,96,768]{2,1,0:T(8,128)(2,1)S(1)} collective-permute-done((bf16[2,96,768]{2,1,0:T(8,128)(2,1)S(1)}, bf16[2,96,768]{2,1,0:T(8,128)(2,1)S(1)}, u32[]{:S(2)}, u32[]{:S(2)}) %collective-permute-start.24) | collective-permute-done | bytes 294944 | tf_op jit(solution)/shard_map/ppermute | solution.py:78
  83.4 1.5 collective-permute-start.30
  85.6 4.2 %up_forward_0.1 = (bf16[2,512,768]{2,1,0:T(8,128)(2,1)S(1)}, f32[2,512,768]{2,1,0:T(8,128)S(1)}, f32[8,128]{1,0:T(8,128)S(1)}, bf16[2,768,768]{2,1,0:T(8,128)(2,1)S(1)}) custom-call(f32[4]{0:T(128)S(1)} %copy-done.2, bf16[512,768]{1,0:T(8,128)(2,1)S(1)} %get-tuple-element.487.mid_low, f32[4,1,1408]{2,1,0:T(1,128)S(1)} %bitcast.19, ...), custom_call_target="tpu_custom_call" | custom-call | flops 4831838208 | bytes 9437184 | tf_op jit(solution)/shard_map/up_forward_0/pallas_call | solution.py:79
  89.9 4.2 %up_forward_2.1 = (bf16[2,512,768]{2,1,0:T(8,128)(2,1)S(1)}, f32[2,512,768]{2,1,0:T(8,128)S(1)}, f32[8,128]{1,0:T(8,128)S(1)}, bf16[2,768,768]{2,1,0:T(8,128)(2,1)S(1)}) custom-call(f32[4]{0:T(128)S(1)} %copy-done.2, bf16[512,768]{1,0:T(8,128)(2,1)S(1)} %get-tuple-element.487.mid_low, f32[4,1,1408]{2,1,0:T(1,128)S(1)} %bitcast.20, ...), custom_call_target="tpu_custom_call" | custom-call | flops 4831838208 | bytes 9437184 | tf_op jit(solution)/shard_map/up_forward_2/pallas_call | solution.py:79
  96.6 4.3 %collective-permute-done.34.rest_3_ = bf16[2,96,384]{2,1,0:T(8,128)(2,1)S(1)} collective-permute-done((bf16[2,96,384]{2,1,0:T(8,128)(2,1)S(1)}, bf16[2,96,384]{2,1,0:T(8,128)(2,1)S(1)}, u32[]{:S(2)}, u32[]{:S(2)}) %collective-permute-start.34) | collective-permute-done | bytes 147488 | tf_op jit(solution)/shard_map/ppermute | solution.py:78
  102.2 2.0 collective-permute-done.38.rest_8_
  104.5 9.1 %down_both.1 = (bf16[512,768]{1,0:T(8,128)(2,1)}, f32[512,768]{1,0:T(8,128)S(1)}, bf16[768,512]{1,0:T(8,128)(2,1)S(1)}, f32[8,768]{1,0:T(8,128)S(1)}, bf16[4,512...) custom-call(bf16[2,512,768]{2,1,0:T(8,128)(2,1)S(1)} %get-tuple-element.563.act0.rest_0_, ...), custom_call_target="tpu_custom_call" | custom-call | flops 4831838208 | bytes 18874368 | tf_op jit(solution)/shard_map/down_both/pallas_call | solution.py:79
  113.6 2.7 %down_grad.1 = (bf16[2,8,96,768]{3,2,1,0:T(8,128)(2,1)S(1)}, bf16[2,8,96,768]{3,2,1,0:T(8,128)(2,1)S(1)}) custom-call(bf16[768,512]{1,0:T(8,128)(2,1)S(1)} %get-tuple-element.562.left_t, bf16[2,512,768]{2,1,0:T(8,128)(2,1)S(1)} %get-tuple-element.563.act0.rest_0_, bf16[2,512,768]{2,1,0:T(8,128)(2,1)S(1)} %get-tuple-element.564.act1.rest_1_), custom_call_target="tpu_custom_call" | custom-call | flops 2415919104 | bytes 4718592 | tf_op jit(solution)/shard_map/down_grad/pallas_call | solution.py:79
  116.5 2.7 %up_grad.1 = (bf16[2,8,96,768]{3,2,1,0:T(8,128)(2,1)S(1)}, bf16[2,8,96,768]{3,2,1,0:T(8,128)(2,1)S(1)}) custom-call(bf16[768,512]{1,0:T(8,128)(2,1)S(1)} %get-tuple-element.566.left_t, bf16[4,512,768]{2,1,0:T(8,128)(2,1)S(1)} %get-tuple-element.575.rest_0_.grad_up), custom_call_target="tpu_custom_call" | custom-call | flops 2415919104 | bytes 4718592 | tf_op jit(solution)/shard_map/up_grad/pallas_call | solution.py:79
  119.2 1.7 collective-permute-done.42.got
  122.1 4.7 %mid_backward.1 = (f32[512,768]{1,0:T(8,128)S(1)}, bf16[512,768]{1,0:T(8,128)(2,1)S(1)}, bf16[768,512]{1,0:T(8,128)(2,1)S(1)}, f32[8,768]{1,0:T(8,128)S(1)}) custom-call(bf16[4,512,768]{2,1,0:T(8,128)(2,1)S(1)} %get-tuple-element.575.rest_0_.grad_up, f32[512,768]{1,0:T(8,128)S(1)} %get-tuple-element.576.grad_second, ...), custom_call_target="tpu_custom_call" | custom-call | flops 3221225472 | bytes 14155776 | tf_op jit(solution)/shard_map/mid_backward/pallas_call | solution.py:79
  127.0 1.6 collective-permute-start.44
  129.6 6.9 %attn_backward.1 = (bf16[2,512,640]{2,1,0:T(8,128)(2,1)S(1)}, f32[4,1,640]{2,1,0:T(1,128)S(1)}) custom-call(s32[1]{0:T(128)S(6)} %copy.37.longs, s32[12]{0:T(128)S(1)} %copy-done.9, bf16[4,512,640]{2,1,0:T(8,128)(2,1)S(1)} %get-tuple-element.627.qkv, f32[4,8,512]{2,1,0:T(8,128)S(1)} %get-tuple-element.628.lse, ...), custom_call_target="tpu_custom_call" | custom-call | flops 4831838208 | bytes 9437184 | tf_op jit(solution)/shard_map/attn_backward/pallas_call | solution.py:79
  139.0 1.3 collective-permute-start.48
  141.0 1.5 collective-permute-start.49
  143.2 11.6 %attn_backward_last.1 = (bf16[2,512,640]{2,1,0:T(8,128)(2,1)S(1)}, bf16[2,8,96,768]{3,2,1,0:T(8,128)(2,1)S(1)}, bf16[2,8,96,768]{3,2,1,0:T(8,128)(2,1)S(1)}, f32[16,768]{1,0:T(8,128)S(1)}) custom-call(s32[1]{0:T(128)S(6)} %copy.37.longs, s32[12]{0:T(128)S(1)} %copy-done.9, bf16[4,512,640]{2,1,0:T(8,128)(2,1)S(1)} %get-tuple-element.627.qkv, ...), custom_call_target="tpu_custom_call" | custom-call | flops 9663676416 | bytes 9437184 | tf_op jit(solution)/shard_map/attn_backward_last/pallas_call | solution.py:79
  160.3 5.1 %token_backward.1 = bf16[512,768]{1,0:T(8,128)(2,1)} custom-call(f32[4]{0:T(128)S(1)} %copy-done.2, bf16[2,512,640]{2,1,0:T(8,128)(2,1)S(1)} %get-tuple-element.666.grads_0, bf16[2,512,640]{2,1,0:T(8,128)(2,1)S(1)} %get-tuple-element.667.rest_3_.grads_1, f32[512,768]{1,0:T(8,128)S(1)} %get-tuple-element.668.grad_first, bf16[512,768]{1,0:T(8,128)(2,1)S(1)} %copy-done, ...), custom_call_target="tpu_custom_call" | custom-call | flops 2415919104 | bytes 9437184 | tf_op jit(solution)/shard_map/token_backward/pallas_call | solution.py:79
  168.3 1.6 collective-permute-start.57
  170.6 2.6 %collective-permute-start.59 = (bf16[96,768]{1,0:T(8,128)(2,1)S(1)}, bf16[96,768]{1,0:T(8,128)(2,1)S(1)}, u32[]{:S(2)}, u32[]{:S(2)}) collective-permute-start(bf16[96,768]{1,0:T(8,128)(2,1)S(1)} %get-tuple-element.686), channel_id=1, source_target_pairs={{0,16},{1,17},{2,18},{3,19},{4,20},{5,21},{6,22},{7,23},{8,24},{9,... | collective-permute-start | bytes 442376 | tf_op jit(solution)/shard_map/ppermute | solution.py:78
  173.4 5.5 %collective-permute-done.59 = bf16[96,768]{1,0:T(8,128)(2,1)S(1)} collective-permute-done((bf16[96,768]{1,0:T(8,128)(2,1)S(1)}, bf16[96,768]{1,0:T(8,128)(2,1)S(1)}, u32[]{:S(2)}, u32[]{:S(2)}) %collective-permute-start.59) | collective-permute-done | bytes 147488 | tf_op jit(solution)/shard_map/ppermute | solution.py:78
  182.3 2.7 %collective-permute-start.63 = (f32[16,768]{1,0:T(8,128)S(1)}, f32[16,768]{1,0:T(8,128)S(1)}, u32[]{:S(2)}, u32[]{:S(2)}) collective-permute-start(f32[16,768]{1,0:T(8,128)S(1)} %add_select_fusion.4), channel_id=1, source_target_pairs={{0,8},{1,9},{2,10},{3,11},{4,12},{5,13},{6,14},{7,15},{8,0},{9,1},... | collective-permute-start | bytes 147464 | tf_op jit(solution)/shard_map/ppermute | solution.py:78
  185.0 2.1 collective-permute-done.63
  187.1 2.9 %collective-permute-done.62 = bf16[96,768]{1,0:T(8,128)(2,1)S(1)} collective-permute-done((bf16[96,768]{1,0:T(8,128)(2,1)S(1)}, bf16[96,768]{1,0:T(8,128)(2,1)S(1)}, u32[]{:S(2)}, u32[]{:S(2)}) %collective-permute-start.62) | collective-permute-done | bytes 147488 | tf_op jit(solution)/shard_map/ppermute | solution.py:78
  190.0 3.7 %collective-permute-done.60.in_x = bf16[4,96,768]{2,1,0:T(8,128)(2,1)S(1)} collective-permute-done((bf16[4,96,768]{2,1,0:T(8,128)(2,1)S(1)}, bf16[4,96,768]{2,1,0:T(8,128)(2,1)S(1)}, u32[]{:S(2)}, u32[]{:S(2)}) %collective-permute-start.60) | collective-permute-done | bytes 589856 | tf_op jit(solution)/shard_map/ppermute | solution.py:78
  195.1 3.3 %collective-permute-start.65 = (f32[16,768]{1,0:T(8,128)S(1)}, f32[16,768]{1,0:T(8,128)S(1)}, u32[]{:S(2)}, u32[]{:S(2)}) collective-permute-start(f32[16,768]{1,0:T(8,128)S(1)} %add_select_fusion.3), channel_id=1, source_target_pairs={{0,16},{1,17},{2,18},{3,19},{4,20},{5,21},{6,22},{7,23},{8,24},{9,... | collective-permute-start | bytes 147464 | tf_op jit(solution)/shard_map/ppermute | solution.py:78
  198.5 2.7 %collective-permute-done.65 = f32[16,768]{1,0:T(8,128)S(1)} collective-permute-done((f32[16,768]{1,0:T(8,128)S(1)}, f32[16,768]{1,0:T(8,128)S(1)}, u32[]{:S(2)}, u32[]{:S(2)}) %collective-permute-start.65) | collective-permute-done | bytes 49184 | tf_op jit(solution)/shard_map/ppermute | solution.py:78
  201.2 2.2 %collective-permute-done.64.from_z = bf16[2,96,768]{2,1,0:T(8,128)(2,1)S(1)} collective-permute-done((bf16[2,96,768]{2,1,0:T(8,128)(2,1)S(1)}, bf16[2,96,768]{2,1,0:T(8,128)(2,1)S(1)}, u32[]{:S(2)}, u32[]{:S(2)}) %collective-permute-start.64) | collective-permute-done | bytes 294944 | tf_op jit(solution)/shard_map/ppermute | solution.py:78
  204.2 1.7 collective-permute-start.66
  208.7 3.2 %collective-permute-done.68 = f32[16,768]{1,0:T(8,128)S(1)} collective-permute-done((f32[16,768]{1,0:T(8,128)S(1)}, f32[16,768]{1,0:T(8,128)S(1)}, u32[]{:S(2)}, u32[]{:S(2)}) %collective-permute-start.68) | collective-permute-done | bytes 49184 | tf_op jit(solution)/shard_map/ppermute | solution.py:78
  (175 shorter events, 48.1 us)
Async XLA Ops:
  2.7 11.3 %collective-permute-start = (bf16[1,96,768]{2,1,0:T(8,128)(2,1)}, bf16[1,96,768]{2,1,0:T(8,128)(2,1)S(1)}, u32[]{:S(2)}, u32[]{:S(2)}) collective-permute-start(bf16[1,96,768]{2,1,0:T(8,128)(2,1)} %bitcast.21), channel_id=1, source_target_pairs={{0,16},{1,17},{2,18},{3,19},{4,20},{5,21},{6,22},{7,23},{8,24},{9,... | collective-permute-start | bytes 442376 | tf_op jit(solution)/shard_map/ppermute | solution.py:78
  6.8 6.8 %collective-permute-start.1 = (bf16[1,96,384]{2,1,0:T(8,128)(2,1)}, bf16[1,96,384]{2,1,0:T(8,128)(2,1)S(1)}, u32[]{:S(2)}, u32[]{:S(2)}) collective-permute-start(bf16[1,96,384]{2,1,0:T(8,128)(2,1)} %bitcast.24), channel_id=1, source_target_pairs={{0,2},{1,3},{2,0},{3,1},{4,6},{5,7},{6,4},{7,5},{8,10},{9,11},{10,... | collective-permute-start | bytes 221192 | tf_op jit(solution)/shard_map/ppermute | solution.py:78
  15.7 8.2 %collective-permute-start.4 = (bf16[2,96,768]{2,1,0:T(8,128)(2,1)S(1)}, bf16[2,96,768]{2,1,0:T(8,128)(2,1)S(1)}, u32[]{:S(2)}, u32[]{:S(2)}) collective-permute-start(bf16[2,96,768]{2,1,0:T(8,128)(2,1)S(1)} %pad_maximum_fusion.2), channel_id=1, source_target_pairs={{0,8},{1,9},{2,10},{3,11},{4,12},{5,13},{6,14},{7,15},{8,0},{9,1},... | collective-permute-start | bytes 884744 | tf_op jit(solution)/shard_map/ppermute | solution.py:78
  24.9 17.3 %collective-permute-start.7 = (bf16[4,96,768]{2,1,0:T(8,128)(2,1)S(1)}, bf16[4,96,768]{2,1,0:T(8,128)(2,1)S(1)}, u32[]{:S(2)}, u32[]{:S(2)}) collective-permute-start(bf16[4,96,768]{2,1,0:T(8,128)(2,1)S(1)} %pad_maximum_fusion.rest_0_), channel_id=1, source_target_pairs={{0,2},{1,3},{2,0},{3,1},{4,6},{5,7},{6,4},{7,5},{8,10},{9,11},{10,... | collective-permute-start | bytes 1769480 | tf_op jit(solution)/shard_map/ppermute | solution.py:78
  26.3 15.9 %collective-permute-start.8 = (bf16[4,96,768]{2,1,0:T(8,128)(2,1)S(1)}, bf16[4,96,768]{2,1,0:T(8,128)(2,1)S(1)}, u32[]{:S(2)}, u32[]{:S(2)}) collective-permute-start(bf16[4,96,768]{2,1,0:T(8,128)(2,1)S(1)} %pad_maximum_fusion.rest_0_), channel_id=1, source_target_pairs={{0,4},{1,5},{2,6},{3,7},{4,0},{5,1},{6,2},{7,3},{8,12},{9,13},{10,... | collective-permute-start | bytes 1769480 | tf_op jit(solution)/shard_map/ppermute | solution.py:78
  27.9 14.3 %collective-permute-start.9 = (bf16[4,96,768]{2,1,0:T(8,128)(2,1)S(1)}, bf16[4,96,768]{2,1,0:T(8,128)(2,1)S(1)}, u32[]{:S(2)}, u32[]{:S(2)}) collective-permute-start(bf16[4,96,768]{2,1,0:T(8,128)(2,1)S(1)} %pad_maximum_fusion.rest_0_), channel_id=1, source_target_pairs={{0,1},{1,0},{2,3},{3,2},{4,5},{5,4},{6,7},{7,6},{8,9},{9,8},{10,11... | collective-permute-start | bytes 1769480 | tf_op jit(solution)/shard_map/ppermute | solution.py:78
  27.9 8.2 %collective-permute-start.11 = (bf16[1,96,384]{2,1,0:T(8,128)(2,1)}, bf16[1,96,384]{2,1,0:T(8,128)(2,1)S(1)}, u32[]{:S(2)}, u32[]{:S(2)}) collective-permute-start(bf16[1,96,384]{2,1,0:T(8,128)(2,1)} %bitcast.27), channel_id=1, source_target_pairs={{0,16},{1,17},{2,18},{3,19},{4,20},{5,21},{6,22},{7,23},{8,24},{9,... | collective-permute-start | bytes 221192 | tf_op jit(solution)/shard_map/ppermute | solution.py:78
  31.1 11.0 %collective-permute-start.10 = (bf16[1,96,768]{2,1,0:T(8,128)(2,1)S(1)}, bf16[1,96,768]{2,1,0:T(8,128)(2,1)S(1)}, u32[]{:S(2)}, u32[]{:S(2)}) collective-permute-start(bf16[1,96,768]{2,1,0:T(8,128)(2,1)S(1)} %convert_bitcast_fusion), channel_id=1, source_target_pairs={{0,16},{1,17},{2,18},{3,19},{4,20},{5,21},{6,22},{7,23},{8,24},{9,... | collective-permute-start | bytes 442376 | tf_op jit(solution)/shard_map/ppermute | solution.py:78
  42.3 10.2 %collective-permute-start.14 = (bf16[4,96,768]{2,1,0:T(8,128)(2,1)S(1)}, bf16[4,96,768]{2,1,0:T(8,128)(2,1)S(1)}, u32[]{:S(2)}, u32[]{:S(2)}) collective-permute-start(bf16[4,96,768]{2,1,0:T(8,128)(2,1)S(1)} %collective-permute-done.8.rest_1_), channel_id=1, source_target_pairs={{0,1},{1,0},{2,3},{3,2},{4,5},{5,4},{6,7},{7,6},{8,9},{9,8},{10,11... | collective-permute-start | bytes 1769480 | tf_op jit(solution)/shard_map/ppermute | solution.py:78
  42.4 10.1 %collective-permute-start.15 = (bf16[4,96,768]{2,1,0:T(8,128)(2,1)S(1)}, bf16[4,96,768]{2,1,0:T(8,128)(2,1)S(1)}, u32[]{:S(2)}, u32[]{:S(2)}) collective-permute-start(bf16[4,96,768]{2,1,0:T(8,128)(2,1)S(1)} %collective-permute-done.7.rest_2_), channel_id=1, source_target_pairs={{0,1},{1,0},{2,3},{3,2},{4,5},{5,4},{6,7},{7,6},{8,9},{9,8},{10,11... | collective-permute-start | bytes 1769480 | tf_op jit(solution)/shard_map/ppermute | solution.py:78
  42.9 9.1 %collective-permute-start.12 = (bf16[2,96,768]{2,1,0:T(8,128)(2,1)S(1)}, bf16[2,96,768]{2,1,0:T(8,128)(2,1)S(1)}, u32[]{:S(2)}, u32[]{:S(2)}) collective-permute-start(bf16[2,96,768]{2,1,0:T(8,128)(2,1)S(1)} %slice.52), channel_id=1, source_target_pairs={{0,2},{1,3},{2,0},{3,1},{4,6},{5,7},{6,4},{7,5},{8,10},{9,11},{10,... | collective-permute-start | bytes 884744 | tf_op jit(solution)/shard_map/ppermute | solution.py:78
  43.5 8.7 %collective-permute-start.13 = (bf16[2,96,768]{2,1,0:T(8,128)(2,1)S(1)}, bf16[2,96,768]{2,1,0:T(8,128)(2,1)S(1)}, u32[]{:S(2)}, u32[]{:S(2)}) collective-permute-start(bf16[2,96,768]{2,1,0:T(8,128)(2,1)S(1)} %slice.53), channel_id=1, source_target_pairs={{0,4},{1,5},{2,6},{3,7},{4,0},{5,1},{6,2},{7,3},{8,12},{9,13},{10,... | collective-permute-start | bytes 884744 | tf_op jit(solution)/shard_map/ppermute | solution.py:78
  44.0 8.4 %collective-permute-start.16 = (bf16[2,96,768]{2,1,0:T(8,128)(2,1)S(1)}, bf16[2,96,768]{2,1,0:T(8,128)(2,1)S(1)}, u32[]{:S(2)}, u32[]{:S(2)}) collective-permute-start(bf16[2,96,768]{2,1,0:T(8,128)(2,1)S(1)} %pad_maximum_fusion.3), channel_id=1, source_target_pairs={{0,8},{1,9},{2,10},{3,11},{4,12},{5,13},{6,14},{7,15},{8,0},{9,1},... | collective-permute-start | bytes 884744 | tf_op jit(solution)/shard_map/ppermute | solution.py:78
  53.2 19.7 %collective-permute-start.19 = (bf16[4,96,768]{2,1,0:T(8,128)(2,1)S(1)}, bf16[4,96,768]{2,1,0:T(8,128)(2,1)S(1)}, u32[]{:S(2)}, u32[]{:S(2)}) collective-permute-start(bf16[4,96,768]{2,1,0:T(8,128)(2,1)S(1)} %pad_maximum_fusion.1.rest_0_), channel_id=1, source_target_pairs={{0,2},{1,3},{2,0},{3,1},{4,6},{5,7},{6,4},{7,5},{8,10},{9,11},{10,... | collective-permute-start | bytes 1769480 | tf_op jit(solution)/shard_map/ppermute | solution.py:78
  54.7 18.2 %collective-permute-start.20 = (bf16[4,96,768]{2,1,0:T(8,128)(2,1)S(1)}, bf16[4,96,768]{2,1,0:T(8,128)(2,1)S(1)}, u32[]{:S(2)}, u32[]{:S(2)}) collective-permute-start(bf16[4,96,768]{2,1,0:T(8,128)(2,1)S(1)} %pad_maximum_fusion.1.rest_0_), channel_id=1, source_target_pairs={{0,4},{1,5},{2,6},{3,7},{4,0},{5,1},{6,2},{7,3},{8,12},{9,13},{10,... | collective-permute-start | bytes 1769480 | tf_op jit(solution)/shard_map/ppermute | solution.py:78
  56.2 16.7 %collective-permute-start.21 = (bf16[4,96,768]{2,1,0:T(8,128)(2,1)S(1)}, bf16[4,96,768]{2,1,0:T(8,128)(2,1)S(1)}, u32[]{:S(2)}, u32[]{:S(2)}) collective-permute-start(bf16[4,96,768]{2,1,0:T(8,128)(2,1)S(1)} %pad_maximum_fusion.1.rest_0_), channel_id=1, source_target_pairs={{0,1},{1,0},{2,3},{3,2},{4,5},{5,4},{6,7},{7,6},{8,9},{9,8},{10,11... | collective-permute-start | bytes 1769480 | tf_op jit(solution)/shard_map/ppermute | solution.py:78
  56.3 16.6 %collective-permute-start.23 = (bf16[4,96,384]{2,1,0:T(8,128)(2,1)S(1)}, bf16[4,96,384]{2,1,0:T(8,128)(2,1)S(1)}, u32[]{:S(2)}, u32[]{:S(2)}) collective-permute-start(bf16[4,96,384]{2,1,0:T(8,128)(2,1)S(1)} %pad_maximum_fusion.4), channel_id=1, source_target_pairs={{0,16},{1,17},{2,18},{3,19},{4,20},{5,21},{6,22},{7,23},{8,24},{9,... | collective-permute-start | bytes 884744 | tf_op jit(solution)/shard_map/ppermute | solution.py:78
  58.7 13.3 %collective-permute-start.22 = (bf16[2,96,384]{2,1,0:T(8,128)(2,1)S(1)}, bf16[2,96,384]{2,1,0:T(8,128)(2,1)S(1)}, u32[]{:S(2)}, u32[]{:S(2)}) collective-permute-start(bf16[2,96,384]{2,1,0:T(8,128)(2,1)S(1)} %pad_maximum_fusion.6), channel_id=1, source_target_pairs={{0,8},{1,9},{2,10},{3,11},{4,12},{5,13},{6,14},{7,15},{8,0},{9,1},... | collective-permute-start | bytes 442376 | tf_op jit(solution)/shard_map/ppermute | solution.py:78
  73.1 9.8 %collective-permute-start.26 = (bf16[4,96,768]{2,1,0:T(8,128)(2,1)S(1)}, bf16[4,96,768]{2,1,0:T(8,128)(2,1)S(1)}, u32[]{:S(2)}, u32[]{:S(2)}) collective-permute-start(bf16[4,96,768]{2,1,0:T(8,128)(2,1)S(1)} %collective-permute-done.20.rest_1_), channel_id=1, source_target_pairs={{0,1},{1,0},{2,3},{3,2},{4,5},{5,4},{6,7},{7,6},{8,9},{9,8},{10,11... | collective-permute-start | bytes 1769480 | tf_op jit(solution)/shard_map/ppermute | solution.py:78
  73.1 9.8 %collective-permute-start.27 = (bf16[4,96,768]{2,1,0:T(8,128)(2,1)S(1)}, bf16[4,96,768]{2,1,0:T(8,128)(2,1)S(1)}, u32[]{:S(2)}, u32[]{:S(2)}) collective-permute-start(bf16[4,96,768]{2,1,0:T(8,128)(2,1)S(1)} %collective-permute-done.19.rest_0_), channel_id=1, source_target_pairs={{0,1},{1,0},{2,3},{3,2},{4,5},{5,4},{6,7},{7,6},{8,9},{9,8},{10,11... | collective-permute-start | bytes 1769480 | tf_op jit(solution)/shard_map/ppermute | solution.py:78
  73.6 9.0 %collective-permute-start.24 = (bf16[2,96,768]{2,1,0:T(8,128)(2,1)S(1)}, bf16[2,96,768]{2,1,0:T(8,128)(2,1)S(1)}, u32[]{:S(2)}, u32[]{:S(2)}) collective-permute-start(bf16[2,96,768]{2,1,0:T(8,128)(2,1)S(1)} %slice.54), channel_id=1, source_target_pairs={{0,2},{1,3},{2,0},{3,1},{4,6},{5,7},{6,4},{7,5},{8,10},{9,11},{10,... | collective-permute-start | bytes 884744 | tf_op jit(solution)/shard_map/ppermute | solution.py:78
  74.2 8.7 %collective-permute-start.25 = (bf16[2,96,768]{2,1,0:T(8,128)(2,1)S(1)}, bf16[2,96,768]{2,1,0:T(8,128)(2,1)S(1)}, u32[]{:S(2)}, u32[]{:S(2)}) collective-permute-start(bf16[2,96,768]{2,1,0:T(8,128)(2,1)S(1)} %slice.55), channel_id=1, source_target_pairs={{0,4},{1,5},{2,6},{3,7},{4,0},{5,1},{6,2},{7,3},{8,12},{9,13},{10,... | collective-permute-start | bytes 884744 | tf_op jit(solution)/shard_map/ppermute | solution.py:78
  74.8 19.2 %collective-permute-start.33 = (bf16[8,96,384]{2,1,0:T(8,128)(2,1)S(1)}, bf16[8,96,384]{2,1,0:T(8,128)(2,1)S(1)}, u32[]{:S(2)}, u32[]{:S(2)}) collective-permute-start(bf16[8,96,384]{2,1,0:T(8,128)(2,1)S(1)} %get-tuple-element.546.rest_10_), channel_id=1, source_target_pairs={{0,8},{1,9},{2,10},{3,11},{4,12},{5,13},{6,14},{7,15},{8,0},{9,1},... | collective-permute-start | bytes 1769480 | tf_op jit(solution)/shard_map/ppermute | solution.py:78
  82.9 6.9 %collective-permute-start.28 = (bf16[2,96,768]{2,1,0:T(8,128)(2,1)S(1)}, bf16[2,96,768]{2,1,0:T(8,128)(2,1)S(1)}, u32[]{:S(2)}, u32[]{:S(2)}) collective-permute-start(bf16[2,96,768]{2,1,0:T(8,128)(2,1)S(1)} %collective-permute-done.24.rest_1_), channel_id=1, source_target_pairs={{0,1},{1,0},{2,3},{3,2},{4,5},{5,4},{6,7},{7,6},{8,9},{9,8},{10,11... | collective-permute-start | bytes 884744 | tf_op jit(solution)/shard_map/ppermute | solution.py:78
  82.9 6.9 %collective-permute-start.29 = (bf16[2,96,768]{2,1,0:T(8,128)(2,1)S(1)}, bf16[2,96,768]{2,1,0:T(8,128)(2,1)S(1)}, u32[]{:S(2)}, u32[]{:S(2)}) collective-permute-start(bf16[2,96,768]{2,1,0:T(8,128)(2,1)S(1)} %collective-permute-done.25.rest_2_), channel_id=1, source_target_pairs={{0,1},{1,0},{2,3},{3,2},{4,5},{5,4},{6,7},{7,6},{8,9},{9,8},{10,11... | collective-permute-start | bytes 884744 | tf_op jit(solution)/shard_map/ppermute | solution.py:78
  83.4 10.7 %collective-permute-start.30 = (bf16[4,96,384]{2,1,0:T(8,128)(2,1)S(1)}, bf16[4,96,384]{2,1,0:T(8,128)(2,1)S(1)}, u32[]{:S(2)}, u32[]{:S(2)}) collective-permute-start(bf16[4,96,384]{2,1,0:T(8,128)(2,1)S(1)} %get-tuple-element.536.rest_0_), channel_id=1, source_target_pairs={{0,2},{1,3},{2,0},{3,1},{4,6},{5,7},{6,4},{7,5},{8,10},{9,11},{10,... | collective-permute-start | bytes 884744 | tf_op jit(solution)/shard_map/ppermute | solution.py:78
  84.9 9.2 %collective-permute-start.31 = (bf16[4,96,384]{2,1,0:T(8,128)(2,1)S(1)}, bf16[4,96,384]{2,1,0:T(8,128)(2,1)S(1)}, u32[]{:S(2)}, u32[]{:S(2)}) collective-permute-start(bf16[4,96,384]{2,1,0:T(8,128)(2,1)S(1)} %get-tuple-element.536.rest_0_), channel_id=1, source_target_pairs={{0,4},{1,5},{2,6},{3,7},{4,0},{5,1},{6,2},{7,3},{8,12},{9,13},{10,... | collective-permute-start | bytes 884744 | tf_op jit(solution)/shard_map/ppermute | solution.py:78
  94.2 7.1 %collective-permute-start.36 = (bf16[4,96,384]{2,1,0:T(8,128)(2,1)S(1)}, bf16[4,96,384]{2,1,0:T(8,128)(2,1)S(1)}, u32[]{:S(2)}, u32[]{:S(2)}) collective-permute-start(bf16[4,96,384]{2,1,0:T(8,128)(2,1)S(1)} %collective-permute-done.31.rest_1_), channel_id=1, source_target_pairs={{0,1},{1,0},{2,3},{3,2},{4,5},{5,4},{6,7},{7,6},{8,9},{9,8},{10,11... | collective-permute-start | bytes 884744 | tf_op jit(solution)/shard_map/ppermute | solution.py:78
  121.4 15.6 %collective-permute-start.46 = (bf16[4,96,768]{2,1,0:T(8,128)(2,1)S(1)}, bf16[4,96,768]{2,1,0:T(8,128)(2,1)S(1)}, u32[]{:S(2)}, u32[]{:S(2)}) collective-permute-start(bf16[4,96,768]{2,1,0:T(8,128)(2,1)S(1)} %get-tuple-element.607), channel_id=1, source_target_pairs={{0,8},{1,9},{2,10},{3,11},{4,12},{5,13},{6,14},{7,15},{8,0},{9,1},... | collective-permute-start | bytes 1769480 | tf_op jit(solution)/shard_map/ppermute | solution.py:78
  127.0 10.0 %collective-permute-start.44 = (bf16[2,96,768]{2,1,0:T(8,128)(2,1)S(1)}, bf16[2,96,768]{2,1,0:T(8,128)(2,1)S(1)}, u32[]{:S(2)}, u32[]{:S(2)}) collective-permute-start(bf16[2,96,768]{2,1,0:T(8,128)(2,1)S(1)} %get-tuple-element.605), channel_id=1, source_target_pairs={{0,2},{1,3},{2,0},{3,1},{4,6},{5,7},{6,4},{7,5},{8,10},{9,11},{10,... | collective-permute-start | bytes 884744 | tf_op jit(solution)/shard_map/ppermute | solution.py:78
  128.6 8.7 %collective-permute-start.45 = (bf16[2,96,768]{2,1,0:T(8,128)(2,1)S(1)}, bf16[2,96,768]{2,1,0:T(8,128)(2,1)S(1)}, u32[]{:S(2)}, u32[]{:S(2)}) collective-permute-start(bf16[2,96,768]{2,1,0:T(8,128)(2,1)S(1)} %get-tuple-element.606), channel_id=1, source_target_pairs={{0,4},{1,5},{2,6},{3,7},{4,0},{5,1},{6,2},{7,3},{8,12},{9,13},{10,... | collective-permute-start | bytes 884744 | tf_op jit(solution)/shard_map/ppermute | solution.py:78
  137.8 18.9 %collective-permute-start.47 = (bf16[4,96,768]{2,1,0:T(8,128)(2,1)S(1)}, bf16[4,96,768]{2,1,0:T(8,128)(2,1)S(1)}, u32[]{:S(2)}, u32[]{:S(2)}) collective-permute-start(bf16[4,96,768]{2,1,0:T(8,128)(2,1)S(1)} %get-tuple-element.648), channel_id=1, source_target_pairs={{0,2},{1,3},{2,0},{3,1},{4,6},{5,7},{6,4},{7,5},{8,10},{9,11},{10,... | collective-permute-start | bytes 1769480 | tf_op jit(solution)/shard_map/ppermute | solution.py:78
  139.0 17.6 %collective-permute-start.48 = (bf16[4,96,768]{2,1,0:T(8,128)(2,1)S(1)}, bf16[4,96,768]{2,1,0:T(8,128)(2,1)S(1)}, u32[]{:S(2)}, u32[]{:S(2)}) collective-permute-start(bf16[4,96,768]{2,1,0:T(8,128)(2,1)S(1)} %get-tuple-element.649), channel_id=1, source_target_pairs={{0,4},{1,5},{2,6},{3,7},{4,0},{5,1},{6,2},{7,3},{8,12},{9,13},{10,... | collective-permute-start | bytes 1769480 | tf_op jit(solution)/shard_map/ppermute | solution.py:78
  140.4 16.3 %collective-permute-start.51 = (bf16[4,96,768]{2,1,0:T(8,128)(2,1)S(1)}, bf16[4,96,768]{2,1,0:T(8,128)(2,1)S(1)}, u32[]{:S(2)}, u32[]{:S(2)}) collective-permute-start(bf16[4,96,768]{2,1,0:T(8,128)(2,1)S(1)} %get-tuple-element.652), channel_id=1, source_target_pairs={{0,8},{1,9},{2,10},{3,11},{4,12},{5,13},{6,14},{7,15},{8,0},{9,1},... | collective-permute-start | bytes 1769480 | tf_op jit(solution)/shard_map/ppermute | solution.py:78
  141.0 14.4 %collective-permute-start.49 = (bf16[96,768]{1,0:T(8,128)(2,1)S(1)}, bf16[96,768]{1,0:T(8,128)(2,1)S(1)}, u32[]{:S(2)}, u32[]{:S(2)}) collective-permute-start(bf16[96,768]{1,0:T(8,128)(2,1)S(1)} %get-tuple-element.650), channel_id=1, source_target_pairs={{0,2},{1,3},{2,0},{3,1},{4,6},{5,7},{6,4},{7,5},{8,10},{9,11},{10,... | collective-permute-start | bytes 442376 | tf_op jit(solution)/shard_map/ppermute | solution.py:78
  142.5 14.2 %collective-permute-start.50 = (bf16[96,768]{1,0:T(8,128)(2,1)S(1)}, bf16[96,768]{1,0:T(8,128)(2,1)S(1)}, u32[]{:S(2)}, u32[]{:S(2)}) collective-permute-start(bf16[96,768]{1,0:T(8,128)(2,1)S(1)} %get-tuple-element.651), channel_id=1, source_target_pairs={{0,4},{1,5},{2,6},{3,7},{4,0},{5,1},{6,2},{7,3},{8,12},{9,13},{10,... | collective-permute-start | bytes 442376 | tf_op jit(solution)/shard_map/ppermute | solution.py:78
  157.2 10.8 %collective-permute-start.52 = (bf16[2,8,96,768]{3,2,1,0:T(8,128)(2,1)S(1)}, bf16[2,8,96,768]{3,2,1,0:T(8,128)(2,1)S(1)}, u32[]{:S(2)}, u32[]{:S(2)}) collective-permute-start(bf16[2,8,96,768]{3,2,1,0:T(8,128)(2,1)S(1)} %get-tuple-element.671), channel_id=1, source_target_pairs={{0,1},{1,0},{2,3},{3,2},{4,5},{5,4},{6,7},{7,6},{8,9},{9,8},{10,11... | collective-permute-start | bytes 7077896 | tf_op jit(solution)/shard_map/ppermute | solution.py:78
  157.3 9.4 %collective-permute-start.53 = (bf16[2,96,768]{2,1,0:T(8,128)(2,1)S(1)}, bf16[2,96,768]{2,1,0:T(8,128)(2,1)S(1)}, u32[]{:S(2)}, u32[]{:S(2)}) collective-permute-start(bf16[2,96,768]{2,1,0:T(8,128)(2,1)S(1)} %get-tuple-element.672), channel_id=1, source_target_pairs={{0,2},{1,3},{2,0},{3,1},{4,6},{5,7},{6,4},{7,5},{8,10},{9,11},{10,... | collective-permute-start | bytes 884744 | tf_op jit(solution)/shard_map/ppermute | solution.py:78
  157.9 9.1 %collective-permute-start.54 = (bf16[2,96,768]{2,1,0:T(8,128)(2,1)S(1)}, bf16[2,96,768]{2,1,0:T(8,128)(2,1)S(1)}, u32[]{:S(2)}, u32[]{:S(2)}) collective-permute-start(bf16[2,96,768]{2,1,0:T(8,128)(2,1)S(1)} %get-tuple-element.673), channel_id=1, source_target_pairs={{0,4},{1,5},{2,6},{3,7},{4,0},{5,1},{6,2},{7,3},{8,12},{9,13},{10,... | collective-permute-start | bytes 884744 | tf_op jit(solution)/shard_map/ppermute | solution.py:78
  159.2 8.8 %collective-permute-start.55 = (bf16[2,96,768]{2,1,0:T(8,128)(2,1)S(1)}, bf16[2,96,768]{2,1,0:T(8,128)(2,1)S(1)}, u32[]{:S(2)}, u32[]{:S(2)}) collective-permute-start(bf16[2,96,768]{2,1,0:T(8,128)(2,1)S(1)} %get-tuple-element.674), channel_id=1, source_target_pairs={{0,8},{1,9},{2,10},{3,11},{4,12},{5,13},{6,14},{7,15},{8,0},{9,1},... | collective-permute-start | bytes 884744 | tf_op jit(solution)/shard_map/ppermute | solution.py:78
  168.3 10.5 %collective-permute-start.57 = (bf16[2,96,768]{2,1,0:T(8,128)(2,1)S(1)}, bf16[2,96,768]{2,1,0:T(8,128)(2,1)S(1)}, u32[]{:S(2)}, u32[]{:S(2)}) collective-permute-start(bf16[2,96,768]{2,1,0:T(8,128)(2,1)S(1)} %get-tuple-element.684), channel_id=1, source_target_pairs={{0,2},{1,3},{2,0},{3,1},{4,6},{5,7},{6,4},{7,5},{8,10},{9,11},{10,... | collective-permute-start | bytes 884744 | tf_op jit(solution)/shard_map/ppermute | solution.py:78
  169.9 9.0 %collective-permute-start.58 = (bf16[2,96,768]{2,1,0:T(8,128)(2,1)S(1)}, bf16[2,96,768]{2,1,0:T(8,128)(2,1)S(1)}, u32[]{:S(2)}, u32[]{:S(2)}) collective-permute-start(bf16[2,96,768]{2,1,0:T(8,128)(2,1)S(1)} %get-tuple-element.685), channel_id=1, source_target_pairs={{0,4},{1,5},{2,6},{3,7},{4,0},{5,1},{6,2},{7,3},{8,12},{9,13},{10,... | collective-permute-start | bytes 884744 | tf_op jit(solution)/shard_map/ppermute | solution.py:78
  170.6 8.3 %collective-permute-start.59 = (bf16[96,768]{1,0:T(8,128)(2,1)S(1)}, bf16[96,768]{1,0:T(8,128)(2,1)S(1)}, u32[]{:S(2)}, u32[]{:S(2)}) collective-permute-start(bf16[96,768]{1,0:T(8,128)(2,1)S(1)} %get-tuple-element.686), channel_id=1, source_target_pairs={{0,16},{1,17},{2,18},{3,19},{4,20},{5,21},{6,22},{7,23},{8,24},{9,... | collective-permute-start | bytes 442376 | tf_op jit(solution)/shard_map/ppermute | solution.py:78
  179.2 14.4 %collective-permute-start.60 = (bf16[4,96,768]{2,1,0:T(8,128)(2,1)S(1)}, bf16[4,96,768]{2,1,0:T(8,128)(2,1)S(1)}, u32[]{:S(2)}, u32[]{:S(2)}) collective-permute-start(bf16[4,96,768]{2,1,0:T(8,128)(2,1)S(1)} %get-tuple-element.695), channel_id=1, source_target_pairs={{0,2},{1,3},{2,0},{3,1},{4,6},{5,7},{6,4},{7,5},{8,10},{9,11},{10,... | collective-permute-start | bytes 1769480 | tf_op jit(solution)/shard_map/ppermute | solution.py:78
  180.3 14.4 %collective-permute-start.61 = (bf16[4,96,768]{2,1,0:T(8,128)(2,1)S(1)}, bf16[4,96,768]{2,1,0:T(8,128)(2,1)S(1)}, u32[]{:S(2)}, u32[]{:S(2)}) collective-permute-start(bf16[4,96,768]{2,1,0:T(8,128)(2,1)S(1)} %get-tuple-element.696), channel_id=1, source_target_pairs={{0,4},{1,5},{2,6},{3,7},{4,0},{5,1},{6,2},{7,3},{8,12},{9,13},{10,... | collective-permute-start | bytes 1769480 | tf_op jit(solution)/shard_map/ppermute | solution.py:78
  181.4 8.6 %collective-permute-start.62 = (bf16[96,768]{1,0:T(8,128)(2,1)S(1)}, bf16[96,768]{1,0:T(8,128)(2,1)S(1)}, u32[]{:S(2)}, u32[]{:S(2)}) collective-permute-start(bf16[96,768]{1,0:T(8,128)(2,1)S(1)} %get-tuple-element.697), channel_id=1, source_target_pairs={{0,16},{1,17},{2,18},{3,19},{4,20},{5,21},{6,22},{7,23},{8,24},{9,... | collective-permute-start | bytes 442376 | tf_op jit(solution)/shard_map/ppermute | solution.py:78
  195.1 8.4 %collective-permute-start.64 = (bf16[2,96,768]{2,1,0:T(8,128)(2,1)S(1)}, bf16[2,96,768]{2,1,0:T(8,128)(2,1)S(1)}, u32[]{:S(2)}, u32[]{:S(2)}) collective-permute-start(bf16[2,96,768]{2,1,0:T(8,128)(2,1)S(1)} %get-tuple-element.704), channel_id=1, source_target_pairs={{0,8},{1,9},{2,10},{3,11},{4,12},{5,13},{6,14},{7,15},{8,0},{9,1},... | collective-permute-start | bytes 884744 | tf_op jit(solution)/shard_map/ppermute | solution.py:78
  204.2 7.7 %collective-permute-start.66 = (bf16[96,768]{1,0:T(8,128)(2,1)S(1)}, bf16[96,768]{1,0:T(8,128)(2,1)S(1)}, u32[]{:S(2)}, u32[]{:S(2)}) collective-permute-start(bf16[96,768]{1,0:T(8,128)(2,1)S(1)} %get-tuple-element.714), channel_id=1, source_target_pairs={{0,16},{1,17},{2,18},{3,19},{4,20},{5,21},{6,22},{7,23},{8,24},{9,... | collective-permute-start | bytes 442376 | tf_op jit(solution)/shard_map/ppermute | solution.py:78
  (34 other events, 378.2 us)

commit v13 on v9

--- a/solution.py
+++ b/solution.py
@@ -953,8 +953,8 @@
             [sum_a, sum_d, line_u, sum_s],
             [sum_a, sum_d, line_u, sum_s],
         )[0]
-        step((), None, [sum_a, sum_d], [sum_a, sum_d])
-        step((), None, [sum_a, line_u, sum_s], [sum_a, line_u, sum_s])
+        step((), None, [sum_a, sum_d], [sum_a])
+        step((), None, [sum_a, line_u, sum_s], [sum_a, sum_d, line_u, sum_s])
         line_a = Job(net.scatter_line(*sum_a.value))
         step((), None, [line_a, sum_s], [line_a, sum_s])
         step((), None, [line_a, sum_s], [sum_s])

time: 215 us -> 216 us (level)
  transfers between devices with their start and end apart: 69 -> 69, of which waited for: 34 -> 33; matrix products, arithmetic and copies ran while one was open for 1% -> 1% of each run, Pallas kernels for 25% -> 25%
where the time goes in v13:
time: 216 us
  waiting for transfers between devices  70.8 us (33%)
  Pallas kernels  69.5 us (32%)
  starting transfers between devices  64 us (30%)
  local copies, waits for them, and re-layouts  5.23 us (2%)
  other arithmetic  4.32 us (2%)
    ppermute x69, waiting for transfers between devices, step(): lax.ppermute(v, ALL, perm)  70.8 us
    pallas_call x11, Pallas kernels, step(): outs = run(*ins) if run else ins  66 us
    ppermute x69, starting transfers between devices, step(): lax.ppermute(v, ALL, perm)  64 us
  transfers between devices with their start and end apart: 69, of which 33 were waited for; matrix products, arithmetic and copies ran while one was open for 1% of the time, Pallas kernels for 25%

profile of v13, /device:TPU:0, one launch (start us, length us, event | category | flops | bytes accessed | tf_op | source)
XLA Modules:
  0.0 215.7 jit_solution(18075301898515363585)
XLA Ops:
  5.0 4.1 %collective-permute-start = (bf16[1,96,768]{2,1,0:T(8,128)(2,1)S(1)}, bf16[1,96,768]{2,1,0:T(8,128)(2,1)S(1)}, u32[]{:S(2)}, u32[]{:S(2)}) collective-permute-start(bf16[1,96,768]{2,1,0:T(8,128)(2,1)S(1)} %bitcast.19), channel_id=1, source_target_pairs={{0,16},{1,17},{2,18},{3,19},{4,20},{5,21},{6,22},{7,23},{8,24},{9,... | collective-permute-start | bytes 442376 | tf_op jit(solution)/shard_map/ppermute | solution.py:78
  9.1 1.5 collective-permute-start.1
  10.6 1.5 collective-permute-start.2
  12.7 3.1 %collective-permute-done.3 = f32[1,1408]{1,0:T(1,128)S(1)} collective-permute-done((f32[1,1408]{1,0:T(1,128)S(1)}, f32[1,1408]{1,0:T(1,128)S(1)}, u32[]{:S(2)}, u32[]{:S(2)}) %collective-permute-start.3) | collective-permute-done | bytes 5664 | tf_op jit(solution)/shard_map/ppermute | solution.py:78
  16.2 1.3 collective-permute-start.4
  19.6 2.2 %collective-permute-done.5 = bf16[1,96,384]{2,1,0:T(8,128)(2,1)S(1)} collective-permute-done((bf16[1,96,384]{2,1,0:T(8,128)(2,1)S(1)}, bf16[1,96,384]{2,1,0:T(8,128)(2,1)S(1)}, u32[]{:S(2)}, u32[]{:S(2)}) %collective-permute-start.5) | collective-permute-done | bytes 73760 | tf_op jit(solution)/shard_map/ppermute | solution.py:78
  21.8 2.6 %collective-permute-done.4 = bf16[2,96,768]{2,1,0:T(8,128)(2,1)S(1)} collective-permute-done((bf16[2,96,768]{2,1,0:T(8,128)(2,1)S(1)}, bf16[2,96,768]{2,1,0:T(8,128)(2,1)S(1)}, u32[]{:S(2)}, u32[]{:S(2)}) %collective-permute-start.4) | collective-permute-done | bytes 294944 | tf_op jit(solution)/shard_map/ppermute | solution.py:78
  24.5 1.3 collective-permute-start.7
  25.9 1.5 collective-permute-start.8
  27.4 3.3 %collective-permute-start.11 = (bf16[1,96,384]{2,1,0:T(8,128)(2,1)S(1)}, bf16[1,96,384]{2,1,0:T(8,128)(2,1)S(1)}, u32[]{:S(2)}, u32[]{:S(2)}) collective-permute-start(bf16[1,96,384]{2,1,0:T(8,128)(2,1)S(1)} %bitcast.25), channel_id=1, source_target_pairs={{0,16},{1,17},{2,18},{3,19},{4,20},{5,21},{6,22},{7,23},{8,24},{9,... | collective-permute-start | bytes 221192 | tf_op jit(solution)/shard_map/ppermute | solution.py:78
  31.4 4.0 %collective-permute-done.11 = bf16[1,96,384]{2,1,0:T(8,128)(2,1)S(1)} collective-permute-done((bf16[1,96,384]{2,1,0:T(8,128)(2,1)S(1)}, bf16[1,96,384]{2,1,0:T(8,128)(2,1)S(1)}, u32[]{:S(2)}, u32[]{:S(2)}) %collective-permute-start.11) | collective-permute-done | bytes 73760 | tf_op jit(solution)/shard_map/ppermute | solution.py:78
  35.4 6.1 %collective-permute-done.10 = bf16[1,96,768]{2,1,0:T(8,128)(2,1)S(1)} collective-permute-done((bf16[1,96,768]{2,1,0:T(8,128)(2,1)S(1)}, bf16[1,96,768]{2,1,0:T(8,128)(2,1)S(1)}, u32[]{:S(2)}, u32[]{:S(2)}) %collective-permute-start.10) | collective-permute-done | bytes 147488 | tf_op jit(solution)/shard_map/ppermute | solution.py:78
  44.6 6.7 %collective-permute-done.12.rest_3_ = bf16[2,96,768]{2,1,0:T(8,128)(2,1)S(1)} collective-permute-done((bf16[2,96,768]{2,1,0:T(8,128)(2,1)S(1)}, bf16[2,96,768]{2,1,0:T(8,128)(2,1)S(1)}, u32[]{:S(2)}, u32[]{:S(2)}) %collective-permute-start.12) | collective-permute-done | bytes 294944 | tf_op jit(solution)/shard_map/ppermute | solution.py:78
  52.5 1.6 collective-permute-start.19
  54.1 1.5 collective-permute-start.20
  55.6 2.4 %collective-permute-start.23 = (bf16[4,96,384]{2,1,0:T(8,128)(2,1)S(1)}, bf16[4,96,384]{2,1,0:T(8,128)(2,1)S(1)}, u32[]{:S(2)}, u32[]{:S(2)}) collective-permute-start(bf16[4,96,384]{2,1,0:T(8,128)(2,1)S(1)} %pad_maximum_fusion.4), channel_id=1, source_target_pairs={{0,16},{1,17},{2,18},{3,19},{4,20},{5,21},{6,22},{7,23},{8,24},{9,... | collective-permute-start | bytes 884744 | tf_op jit(solution)/shard_map/ppermute | solution.py:78
  58.0 1.7 collective-permute-start.22
  59.8 11.5 %attn_forward.1 = (bf16[4,512,640]{2,1,0:T(8,128)(2,1)S(1)}, f32[4,8,512]{2,1,0:T(8,128)S(1)}, bf16[768,512]{1,0:T(8,128)(2,1)S(1)}, bf16[4,512,256]{2,1,0:T(8,1...) custom-call(f32[4]{0:T(128)S(1)} %copy-done.7, ...), custom_call_target="tpu_custom_call" | custom-call | flops 9663676416 | bytes 14155776 | tf_op jit(solution)/shard_map/attn_forward/pallas_call | solution.py:79
  75.2 3.3 %attn_finish.1 = (f32[512,768]{1,0:T(8,128)S(1)}, f32[512,1]{1,0:T(8,128)S(1)}, f32[512,768]{1,0:T(8,128)S(1)}, f32[512,768]{1,0:T(8,128)S(1)}, bf16[512,768]{1,...) custom-call(f32[4]{0:T(128)S(1)} %copy-done.7, ...), custom_call_target="tpu_custom_call" | custom-call | flops 4831838208 | bytes 9437184 | tf_op jit(solution)/shard_map/attn_finish/pallas_call | solution.py:79
  78.4 3.5 %collective-permute-done.24.rest_1_ = bf16[2,96,768]{2,1,0:T(8,128)(2,1)S(1)} collective-permute-done((bf16[2,96,768]{2,1,0:T(8,128)(2,1)S(1)}, bf16[2,96,768]{2,1,0:T(8,128)(2,1)S(1)}, u32[]{:S(2)}, u32[]{:S(2)}) %collective-permute-start.24) | collective-permute-done | bytes 294944 | tf_op jit(solution)/shard_map/ppermute | solution.py:78
  82.8 1.5 collective-permute-start.30
  85.1 4.2 %up_forward_0.1 = (bf16[2,512,768]{2,1,0:T(8,128)(2,1)S(1)}, f32[2,512,768]{2,1,0:T(8,128)S(1)}, f32[8,128]{1,0:T(8,128)S(1)}, bf16[2,768,768]{2,1,0:T(8,128)(2,1)S(1)}) custom-call(f32[4]{0:T(128)S(1)} %copy-done.7, bf16[512,768]{1,0:T(8,128)(2,1)S(1)} %get-tuple-element.480.mid_low, f32[4,1,1408]{2,1,0:T(1,128)S(1)} %bitcast.30, ...), custom_call_target="tpu_custom_call" | custom-call | flops 4831838208 | bytes 9437184 | tf_op jit(solution)/shard_map/up_forward_0/pallas_call | solution.py:79
  89.5 4.2 %up_forward_2.1 = (bf16[2,512,768]{2,1,0:T(8,128)(2,1)S(1)}, f32[2,512,768]{2,1,0:T(8,128)S(1)}, f32[8,128]{1,0:T(8,128)S(1)}, bf16[2,768,768]{2,1,0:T(8,128)(2,1)S(1)}) custom-call(f32[4]{0:T(128)S(1)} %copy-done.7, bf16[512,768]{1,0:T(8,128)(2,1)S(1)} %get-tuple-element.480.mid_low, f32[4,1,1408]{2,1,0:T(1,128)S(1)} %bitcast.31, ...), custom_call_target="tpu_custom_call" | custom-call | flops 4831838208 | bytes 9437184 | tf_op jit(solution)/shard_map/up_forward_2/pallas_call | solution.py:79
  96.0 4.5 %collective-permute-done.34.rest_3_ = bf16[2,96,384]{2,1,0:T(8,128)(2,1)S(1)} collective-permute-done((bf16[2,96,384]{2,1,0:T(8,128)(2,1)S(1)}, bf16[2,96,384]{2,1,0:T(8,128)(2,1)S(1)}, u32[]{:S(2)}, u32[]{:S(2)}) %collective-permute-start.34) | collective-permute-done | bytes 147488 | tf_op jit(solution)/shard_map/ppermute | solution.py:78
  101.8 2.0 collective-permute-done.38.rest_8_
  104.1 9.1 %down_both.1 = (bf16[512,768]{1,0:T(8,128)(2,1)}, f32[512,768]{1,0:T(8,128)S(1)}, bf16[768,512]{1,0:T(8,128)(2,1)S(1)}, f32[8,768]{1,0:T(8,128)S(1)}, bf16[4,512...) custom-call(bf16[2,512,768]{2,1,0:T(8,128)(2,1)S(1)} %get-tuple-element.556.act0.rest_0_, ...), custom_call_target="tpu_custom_call" | custom-call | flops 4831838208 | bytes 18874368 | tf_op jit(solution)/shard_map/down_both/pallas_call | solution.py:79
  113.2 2.7 %down_grad.1 = (bf16[2,8,96,768]{3,2,1,0:T(8,128)(2,1)S(1)}, bf16[2,8,96,768]{3,2,1,0:T(8,128)(2,1)S(1)}) custom-call(bf16[768,512]{1,0:T(8,128)(2,1)S(1)} %get-tuple-element.555.left_t, bf16[2,512,768]{2,1,0:T(8,128)(2,1)S(1)} %get-tuple-element.556.act0.rest_0_, bf16[2,512,768]{2,1,0:T(8,128)(2,1)S(1)} %get-tuple-element.557.act1.rest_1_), custom_call_target="tpu_custom_call" | custom-call | flops 2415919104 | bytes 4718592 | tf_op jit(solution)/shard_map/down_grad/pallas_call | solution.py:79
  116.1 2.7 %up_grad.1 = (bf16[2,8,96,768]{3,2,1,0:T(8,128)(2,1)S(1)}, bf16[2,8,96,768]{3,2,1,0:T(8,128)(2,1)S(1)}) custom-call(bf16[768,512]{1,0:T(8,128)(2,1)S(1)} %get-tuple-element.559.left_t, bf16[4,512,768]{2,1,0:T(8,128)(2,1)S(1)} %get-tuple-element.568.rest_0_.grad_up), custom_call_target="tpu_custom_call" | custom-call | flops 2415919104 | bytes 4718592 | tf_op jit(solution)/shard_map/up_grad/pallas_call | solution.py:79
  118.8 1.7 collective-permute-done.42.got
  121.7 4.7 %mid_backward.1 = (f32[512,768]{1,0:T(8,128)S(1)}, bf16[512,768]{1,0:T(8,128)(2,1)S(1)}, bf16[768,512]{1,0:T(8,128)(2,1)S(1)}, f32[8,768]{1,0:T(8,128)S(1)}) custom-call(bf16[4,512,768]{2,1,0:T(8,128)(2,1)S(1)} %get-tuple-element.568.rest_0_.grad_up, f32[512,768]{1,0:T(8,128)S(1)} %get-tuple-element.569.grad_second, ...), custom_call_target="tpu_custom_call" | custom-call | flops 3221225472 | bytes 14155776 | tf_op jit(solution)/shard_map/mid_backward/pallas_call | solution.py:79
  126.6 1.6 collective-permute-start.44
  129.0 6.9 %attn_backward.1 = (bf16[2,512,640]{2,1,0:T(8,128)(2,1)S(1)}, f32[4,1,640]{2,1,0:T(1,128)S(1)}) custom-call(s32[1]{0:T(128)S(6)} %copy.37.longs, s32[12]{0:T(128)S(1)} %copy-done.14, bf16[4,512,640]{2,1,0:T(8,128)(2,1)S(1)} %get-tuple-element.620.qkv, f32[4,8,512]{2,1,0:T(8,128)S(1)} %get-tuple-element.621.lse, ...), custom_call_target="tpu_custom_call" | custom-call | flops 4831838208 | bytes 9437184 | tf_op jit(solution)/shard_map/attn_backward/pallas_call | solution.py:79
  137.3 1.3 collective-permute-start.47
  140.4 1.5 collective-permute-start.49
  142.8 11.7 %attn_backward_last.1 = (bf16[2,512,640]{2,1,0:T(8,128)(2,1)S(1)}, bf16[2,8,96,768]{3,2,1,0:T(8,128)(2,1)S(1)}, bf16[2,8,96,768]{3,2,1,0:T(8,128)(2,1)S(1)}, f32[16,768]{1,0:T(8,128)S(1)}) custom-call(s32[1]{0:T(128)S(6)} %copy.37.longs, s32[12]{0:T(128)S(1)} %copy-done.14, bf16[4,512,640]{2,1,0:T(8,128)(2,1)S(1)} %get-tuple-element.620.qkv, ...), custom_call_target="tpu_custom_call" | custom-call | flops 9663676416 | bytes 9437184 | tf_op jit(solution)/shard_map/attn_backward_last/pallas_call | solution.py:79
  159.6 5.1 %token_backward.1 = bf16[512,768]{1,0:T(8,128)(2,1)} custom-call(f32[4]{0:T(128)S(1)} %copy-done.7, bf16[2,512,640]{2,1,0:T(8,128)(2,1)S(1)} %get-tuple-element.659.grads_0, bf16[2,512,640]{2,1,0:T(8,128)(2,1)S(1)} %get-tuple-element.660.rest_3_.grads_1, f32[512,768]{1,0:T(8,128)S(1)} %get-tuple-element.661.grad_first, bf16[512,768]{1,0:T(8,128)(2,1)S(1)} %copy-done, ...), custom_call_target="tpu_custom_call" | custom-call | flops 2415919104 | bytes 9437184 | tf_op jit(solution)/shard_map/token_backward/pallas_call | solution.py:79
  164.7 1.5 collective-permute-done.53.in_x
  167.7 1.6 collective-permute-start.57
  170.3 5.4 %collective-permute-done.57.from_x = bf16[2,96,768]{2,1,0:T(8,128)(2,1)S(1)} collective-permute-done((bf16[2,96,768]{2,1,0:T(8,128)(2,1)S(1)}, bf16[2,96,768]{2,1,0:T(8,128)(2,1)S(1)}, u32[]{:S(2)}, u32[]{:S(2)}) %collective-permute-start.57) | collective-permute-done | bytes 294944 | tf_op jit(solution)/shard_map/ppermute | solution.py:78
  178.8 3.1 %collective-permute-start.61 = (bf16[96,768]{1,0:T(8,128)(2,1)S(1)}, bf16[96,768]{1,0:T(8,128)(2,1)S(1)}, u32[]{:S(2)}, u32[]{:S(2)}) collective-permute-start(bf16[96,768]{1,0:T(8,128)(2,1)S(1)} %get-tuple-element.689), channel_id=1, source_target_pairs={{0,16},{1,17},{2,18},{3,19},{4,20},{5,21},{6,22},{7,23},{8,24},{9,... | collective-permute-start | bytes 442376 | tf_op jit(solution)/shard_map/ppermute | solution.py:78
  182.9 8.0 %collective-permute-done.61 = bf16[96,768]{1,0:T(8,128)(2,1)S(1)} collective-permute-done((bf16[96,768]{1,0:T(8,128)(2,1)S(1)}, bf16[96,768]{1,0:T(8,128)(2,1)S(1)}, u32[]{:S(2)}, u32[]{:S(2)}) %collective-permute-start.61) | collective-permute-done | bytes 147488 | tf_op jit(solution)/shard_map/ppermute | solution.py:78
  190.9 1.8 collective-permute-done.62
  193.4 3.4 %collective-permute-start.65 = (f32[16,768]{1,0:T(8,128)S(1)}, f32[16,768]{1,0:T(8,128)S(1)}, u32[]{:S(2)}, u32[]{:S(2)}) collective-permute-start(f32[16,768]{1,0:T(8,128)S(1)} %add_select_fusion.3), channel_id=1, source_target_pairs={{0,16},{1,17},{2,18},{3,19},{4,20},{5,21},{6,22},{7,23},{8,24},{9,... | collective-permute-start | bytes 147464 | tf_op jit(solution)/shard_map/ppermute | solution.py:78
  196.8 3.7 %collective-permute-done.65 = f32[16,768]{1,0:T(8,128)S(1)} collective-permute-done((f32[16,768]{1,0:T(8,128)S(1)}, f32[16,768]{1,0:T(8,128)S(1)}, u32[]{:S(2)}, u32[]{:S(2)}) %collective-permute-start.65) | collective-permute-done | bytes 49184 | tf_op jit(solution)/shard_map/ppermute | solution.py:78
  200.4 1.4 collective-permute-done.64.from_z
  203.6 2.9 %collective-permute-start.66 = (bf16[96,768]{1,0:T(8,128)(2,1)S(1)}, bf16[96,768]{1,0:T(8,128)(2,1)S(1)}, u32[]{:S(2)}, u32[]{:S(2)}) collective-permute-start(bf16[96,768]{1,0:T(8,128)(2,1)S(1)} %get-tuple-element.703), channel_id=1, source_target_pairs={{0,16},{1,17},{2,18},{3,19},{4,20},{5,21},{6,22},{7,23},{8,24},{9,... | collective-permute-start | bytes 442376 | tf_op jit(solution)/shard_map/ppermute | solution.py:78
  208.2 2.5 %collective-permute-done.68 = f32[16,768]{1,0:T(8,128)S(1)} collective-permute-done((f32[16,768]{1,0:T(8,128)S(1)}, f32[16,768]{1,0:T(8,128)S(1)}, u32[]{:S(2)}, u32[]{:S(2)}) %collective-permute-start.68) | collective-permute-done | bytes 49184 | tf_op jit(solution)/shard_map/ppermute | solution.py:78
  210.7 2.2 %collective-permute-done.66.last = bf16[96,768]{1,0:T(8,128)(2,1)S(1)} collective-permute-done((bf16[96,768]{1,0:T(8,128)(2,1)S(1)}, bf16[96,768]{1,0:T(8,128)(2,1)S(1)}, u32[]{:S(2)}, u32[]{:S(2)}) %collective-permute-start.66) | collective-permute-done | bytes 147488 | tf_op jit(solution)/shard_map/ppermute | solution.py:78
  (179 shorter events, 46.3 us)
Async XLA Ops:
  5.0 11.1 %collective-permute-start = (bf16[1,96,768]{2,1,0:T(8,128)(2,1)S(1)}, bf16[1,96,768]{2,1,0:T(8,128)(2,1)S(1)}, u32[]{:S(2)}, u32[]{:S(2)}) collective-permute-start(bf16[1,96,768]{2,1,0:T(8,128)(2,1)S(1)} %bitcast.19), channel_id=1, source_target_pairs={{0,16},{1,17},{2,18},{3,19},{4,20},{5,21},{6,22},{7,23},{8,24},{9,... | collective-permute-start | bytes 442376 | tf_op jit(solution)/shard_map/ppermute | solution.py:78
  16.2 8.2 %collective-permute-start.4 = (bf16[2,96,768]{2,1,0:T(8,128)(2,1)S(1)}, bf16[2,96,768]{2,1,0:T(8,128)(2,1)S(1)}, u32[]{:S(2)}, u32[]{:S(2)}) collective-permute-start(bf16[2,96,768]{2,1,0:T(8,128)(2,1)S(1)} %pad_maximum_fusion.2), channel_id=1, source_target_pairs={{0,8},{1,9},{2,10},{3,11},{4,12},{5,13},{6,14},{7,15},{8,0},{9,1},... | collective-permute-start | bytes 884744 | tf_op jit(solution)/shard_map/ppermute | solution.py:78
  24.5 17.0 %collective-permute-start.7 = (bf16[4,96,768]{2,1,0:T(8,128)(2,1)S(1)}, bf16[4,96,768]{2,1,0:T(8,128)(2,1)S(1)}, u32[]{:S(2)}, u32[]{:S(2)}) collective-permute-start(bf16[4,96,768]{2,1,0:T(8,128)(2,1)S(1)} %pad_maximum_fusion.rest_0_), channel_id=1, source_target_pairs={{0,2},{1,3},{2,0},{3,1},{4,6},{5,7},{6,4},{7,5},{8,10},{9,11},{10,... | collective-permute-start | bytes 1769480 | tf_op jit(solution)/shard_map/ppermute | solution.py:78
  25.9 15.7 %collective-permute-start.8 = (bf16[4,96,768]{2,1,0:T(8,128)(2,1)S(1)}, bf16[4,96,768]{2,1,0:T(8,128)(2,1)S(1)}, u32[]{:S(2)}, u32[]{:S(2)}) collective-permute-start(bf16[4,96,768]{2,1,0:T(8,128)(2,1)S(1)} %pad_maximum_fusion.rest_0_), channel_id=1, source_target_pairs={{0,4},{1,5},{2,6},{3,7},{4,0},{5,1},{6,2},{7,3},{8,12},{9,13},{10,... | collective-permute-start | bytes 1769480 | tf_op jit(solution)/shard_map/ppermute | solution.py:78
  27.4 14.2 %collective-permute-start.9 = (bf16[4,96,768]{2,1,0:T(8,128)(2,1)S(1)}, bf16[4,96,768]{2,1,0:T(8,128)(2,1)S(1)}, u32[]{:S(2)}, u32[]{:S(2)}) collective-permute-start(bf16[4,96,768]{2,1,0:T(8,128)(2,1)S(1)} %pad_maximum_fusion.rest_0_), channel_id=1, source_target_pairs={{0,1},{1,0},{2,3},{3,2},{4,5},{5,4},{6,7},{7,6},{8,9},{9,8},{10,11... | collective-permute-start | bytes 1769480 | tf_op jit(solution)/shard_map/ppermute | solution.py:78
  27.4 8.0 %collective-permute-start.11 = (bf16[1,96,384]{2,1,0:T(8,128)(2,1)S(1)}, bf16[1,96,384]{2,1,0:T(8,128)(2,1)S(1)}, u32[]{:S(2)}, u32[]{:S(2)}) collective-permute-start(bf16[1,96,384]{2,1,0:T(8,128)(2,1)S(1)} %bitcast.25), channel_id=1, source_target_pairs={{0,16},{1,17},{2,18},{3,19},{4,20},{5,21},{6,22},{7,23},{8,24},{9,... | collective-permute-start | bytes 221192 | tf_op jit(solution)/shard_map/ppermute | solution.py:78
  30.7 10.8 %collective-permute-start.10 = (bf16[1,96,768]{2,1,0:T(8,128)(2,1)S(1)}, bf16[1,96,768]{2,1,0:T(8,128)(2,1)S(1)}, u32[]{:S(2)}, u32[]{:S(2)}) collective-permute-start(bf16[1,96,768]{2,1,0:T(8,128)(2,1)S(1)} %convert_bitcast_fusion), channel_id=1, source_target_pairs={{0,16},{1,17},{2,18},{3,19},{4,20},{5,21},{6,22},{7,23},{8,24},{9,... | collective-permute-start | bytes 442376 | tf_op jit(solution)/shard_map/ppermute | solution.py:78
  41.7 10.2 %collective-permute-start.14 = (bf16[4,96,768]{2,1,0:T(8,128)(2,1)S(1)}, bf16[4,96,768]{2,1,0:T(8,128)(2,1)S(1)}, u32[]{:S(2)}, u32[]{:S(2)}) collective-permute-start(bf16[4,96,768]{2,1,0:T(8,128)(2,1)S(1)} %collective-permute-done.8.rest_1_), channel_id=1, source_target_pairs={{0,1},{1,0},{2,3},{3,2},{4,5},{5,4},{6,7},{7,6},{8,9},{9,8},{10,11... | collective-permute-start | bytes 1769480 | tf_op jit(solution)/shard_map/ppermute | solution.py:78
  41.8 10.1 %collective-permute-start.15 = (bf16[4,96,768]{2,1,0:T(8,128)(2,1)S(1)}, bf16[4,96,768]{2,1,0:T(8,128)(2,1)S(1)}, u32[]{:S(2)}, u32[]{:S(2)}) collective-permute-start(bf16[4,96,768]{2,1,0:T(8,128)(2,1)S(1)} %collective-permute-done.7.rest_2_), channel_id=1, source_target_pairs={{0,1},{1,0},{2,3},{3,2},{4,5},{5,4},{6,7},{7,6},{8,9},{9,8},{10,11... | collective-permute-start | bytes 1769480 | tf_op jit(solution)/shard_map/ppermute | solution.py:78
  42.3 9.1 %collective-permute-start.12 = (bf16[2,96,768]{2,1,0:T(8,128)(2,1)S(1)}, bf16[2,96,768]{2,1,0:T(8,128)(2,1)S(1)}, u32[]{:S(2)}, u32[]{:S(2)}) collective-permute-start(bf16[2,96,768]{2,1,0:T(8,128)(2,1)S(1)} %slice.52), channel_id=1, source_target_pairs={{0,2},{1,3},{2,0},{3,1},{4,6},{5,7},{6,4},{7,5},{8,10},{9,11},{10,... | collective-permute-start | bytes 884744 | tf_op jit(solution)/shard_map/ppermute | solution.py:78
  42.9 8.7 %collective-permute-start.13 = (bf16[2,96,768]{2,1,0:T(8,128)(2,1)S(1)}, bf16[2,96,768]{2,1,0:T(8,128)(2,1)S(1)}, u32[]{:S(2)}, u32[]{:S(2)}) collective-permute-start(bf16[2,96,768]{2,1,0:T(8,128)(2,1)S(1)} %slice.53), channel_id=1, source_target_pairs={{0,4},{1,5},{2,6},{3,7},{4,0},{5,1},{6,2},{7,3},{8,12},{9,13},{10,... | collective-permute-start | bytes 884744 | tf_op jit(solution)/shard_map/ppermute | solution.py:78
  43.4 8.4 %collective-permute-start.16 = (bf16[2,96,768]{2,1,0:T(8,128)(2,1)S(1)}, bf16[2,96,768]{2,1,0:T(8,128)(2,1)S(1)}, u32[]{:S(2)}, u32[]{:S(2)}) collective-permute-start(bf16[2,96,768]{2,1,0:T(8,128)(2,1)S(1)} %pad_maximum_fusion.3), channel_id=1, source_target_pairs={{0,8},{1,9},{2,10},{3,11},{4,12},{5,13},{6,14},{7,15},{8,0},{9,1},... | collective-permute-start | bytes 884744 | tf_op jit(solution)/shard_map/ppermute | solution.py:78
  52.5 19.7 %collective-permute-start.19 = (bf16[4,96,768]{2,1,0:T(8,128)(2,1)S(1)}, bf16[4,96,768]{2,1,0:T(8,128)(2,1)S(1)}, u32[]{:S(2)}, u32[]{:S(2)}) collective-permute-start(bf16[4,96,768]{2,1,0:T(8,128)(2,1)S(1)} %pad_maximum_fusion.1.rest_0_), channel_id=1, source_target_pairs={{0,2},{1,3},{2,0},{3,1},{4,6},{5,7},{6,4},{7,5},{8,10},{9,11},{10,... | collective-permute-start | bytes 1769480 | tf_op jit(solution)/shard_map/ppermute | solution.py:78
  54.1 18.2 %collective-permute-start.20 = (bf16[4,96,768]{2,1,0:T(8,128)(2,1)S(1)}, bf16[4,96,768]{2,1,0:T(8,128)(2,1)S(1)}, u32[]{:S(2)}, u32[]{:S(2)}) collective-permute-start(bf16[4,96,768]{2,1,0:T(8,128)(2,1)S(1)} %pad_maximum_fusion.1.rest_0_), channel_id=1, source_target_pairs={{0,4},{1,5},{2,6},{3,7},{4,0},{5,1},{6,2},{7,3},{8,12},{9,13},{10,... | collective-permute-start | bytes 1769480 | tf_op jit(solution)/shard_map/ppermute | solution.py:78
  55.6 16.7 %collective-permute-start.21 = (bf16[4,96,768]{2,1,0:T(8,128)(2,1)S(1)}, bf16[4,96,768]{2,1,0:T(8,128)(2,1)S(1)}, u32[]{:S(2)}, u32[]{:S(2)}) collective-permute-start(bf16[4,96,768]{2,1,0:T(8,128)(2,1)S(1)} %pad_maximum_fusion.1.rest_0_), channel_id=1, source_target_pairs={{0,1},{1,0},{2,3},{3,2},{4,5},{5,4},{6,7},{7,6},{8,9},{9,8},{10,11... | collective-permute-start | bytes 1769480 | tf_op jit(solution)/shard_map/ppermute | solution.py:78
  55.6 16.6 %collective-permute-start.23 = (bf16[4,96,384]{2,1,0:T(8,128)(2,1)S(1)}, bf16[4,96,384]{2,1,0:T(8,128)(2,1)S(1)}, u32[]{:S(2)}, u32[]{:S(2)}) collective-permute-start(bf16[4,96,384]{2,1,0:T(8,128)(2,1)S(1)} %pad_maximum_fusion.4), channel_id=1, source_target_pairs={{0,16},{1,17},{2,18},{3,19},{4,20},{5,21},{6,22},{7,23},{8,24},{9,... | collective-permute-start | bytes 884744 | tf_op jit(solution)/shard_map/ppermute | solution.py:78
  58.0 13.3 %collective-permute-start.22 = (bf16[2,96,384]{2,1,0:T(8,128)(2,1)S(1)}, bf16[2,96,384]{2,1,0:T(8,128)(2,1)S(1)}, u32[]{:S(2)}, u32[]{:S(2)}) collective-permute-start(bf16[2,96,384]{2,1,0:T(8,128)(2,1)S(1)} %pad_maximum_fusion.6), channel_id=1, source_target_pairs={{0,8},{1,9},{2,10},{3,11},{4,12},{5,13},{6,14},{7,15},{8,0},{9,1},... | collective-permute-start | bytes 442376 | tf_op jit(solution)/shard_map/ppermute | solution.py:78
  72.4 9.8 %collective-permute-start.26 = (bf16[4,96,768]{2,1,0:T(8,128)(2,1)S(1)}, bf16[4,96,768]{2,1,0:T(8,128)(2,1)S(1)}, u32[]{:S(2)}, u32[]{:S(2)}) collective-permute-start(bf16[4,96,768]{2,1,0:T(8,128)(2,1)S(1)} %collective-permute-done.20.rest_1_), channel_id=1, source_target_pairs={{0,1},{1,0},{2,3},{3,2},{4,5},{5,4},{6,7},{7,6},{8,9},{9,8},{10,11... | collective-permute-start | bytes 1769480 | tf_op jit(solution)/shard_map/ppermute | solution.py:78
  72.5 9.8 %collective-permute-start.27 = (bf16[4,96,768]{2,1,0:T(8,128)(2,1)S(1)}, bf16[4,96,768]{2,1,0:T(8,128)(2,1)S(1)}, u32[]{:S(2)}, u32[]{:S(2)}) collective-permute-start(bf16[4,96,768]{2,1,0:T(8,128)(2,1)S(1)} %collective-permute-done.19.rest_0_), channel_id=1, source_target_pairs={{0,1},{1,0},{2,3},{3,2},{4,5},{5,4},{6,7},{7,6},{8,9},{9,8},{10,11... | collective-permute-start | bytes 1769480 | tf_op jit(solution)/shard_map/ppermute | solution.py:78
  73.0 9.0 %collective-permute-start.24 = (bf16[2,96,768]{2,1,0:T(8,128)(2,1)S(1)}, bf16[2,96,768]{2,1,0:T(8,128)(2,1)S(1)}, u32[]{:S(2)}, u32[]{:S(2)}) collective-permute-start(bf16[2,96,768]{2,1,0:T(8,128)(2,1)S(1)} %slice.54), channel_id=1, source_target_pairs={{0,2},{1,3},{2,0},{3,1},{4,6},{5,7},{6,4},{7,5},{8,10},{9,11},{10,... | collective-permute-start | bytes 884744 | tf_op jit(solution)/shard_map/ppermute | solution.py:78
  73.5 8.7 %collective-permute-start.25 = (bf16[2,96,768]{2,1,0:T(8,128)(2,1)S(1)}, bf16[2,96,768]{2,1,0:T(8,128)(2,1)S(1)}, u32[]{:S(2)}, u32[]{:S(2)}) collective-permute-start(bf16[2,96,768]{2,1,0:T(8,128)(2,1)S(1)} %slice.55), channel_id=1, source_target_pairs={{0,4},{1,5},{2,6},{3,7},{4,0},{5,1},{6,2},{7,3},{8,12},{9,13},{10,... | collective-permute-start | bytes 884744 | tf_op jit(solution)/shard_map/ppermute | solution.py:78
  74.4 19.2 %collective-permute-start.33 = (bf16[8,96,384]{2,1,0:T(8,128)(2,1)S(1)}, bf16[8,96,384]{2,1,0:T(8,128)(2,1)S(1)}, u32[]{:S(2)}, u32[]{:S(2)}) collective-permute-start(bf16[8,96,384]{2,1,0:T(8,128)(2,1)S(1)} %get-tuple-element.539.rest_10_), channel_id=1, source_target_pairs={{0,8},{1,9},{2,10},{3,11},{4,12},{5,13},{6,14},{7,15},{8,0},{9,1},... | collective-permute-start | bytes 1769480 | tf_op jit(solution)/shard_map/ppermute | solution.py:78
  82.2 7.1 %collective-permute-start.28 = (bf16[2,96,768]{2,1,0:T(8,128)(2,1)S(1)}, bf16[2,96,768]{2,1,0:T(8,128)(2,1)S(1)}, u32[]{:S(2)}, u32[]{:S(2)}) collective-permute-start(bf16[2,96,768]{2,1,0:T(8,128)(2,1)S(1)} %collective-permute-done.24.rest_1_), channel_id=1, source_target_pairs={{0,1},{1,0},{2,3},{3,2},{4,5},{5,4},{6,7},{7,6},{8,9},{9,8},{10,11... | collective-permute-start | bytes 884744 | tf_op jit(solution)/shard_map/ppermute | solution.py:78
  82.3 7.2 %collective-permute-start.29 = (bf16[2,96,768]{2,1,0:T(8,128)(2,1)S(1)}, bf16[2,96,768]{2,1,0:T(8,128)(2,1)S(1)}, u32[]{:S(2)}, u32[]{:S(2)}) collective-permute-start(bf16[2,96,768]{2,1,0:T(8,128)(2,1)S(1)} %collective-permute-done.25.rest_2_), channel_id=1, source_target_pairs={{0,1},{1,0},{2,3},{3,2},{4,5},{5,4},{6,7},{7,6},{8,9},{9,8},{10,11... | collective-permute-start | bytes 884744 | tf_op jit(solution)/shard_map/ppermute | solution.py:78
  82.8 10.9 %collective-permute-start.30 = (bf16[4,96,384]{2,1,0:T(8,128)(2,1)S(1)}, bf16[4,96,384]{2,1,0:T(8,128)(2,1)S(1)}, u32[]{:S(2)}, u32[]{:S(2)}) collective-permute-start(bf16[4,96,384]{2,1,0:T(8,128)(2,1)S(1)} %get-tuple-element.529.rest_0_), channel_id=1, source_target_pairs={{0,2},{1,3},{2,0},{3,1},{4,6},{5,7},{6,4},{7,5},{8,10},{9,11},{10,... | collective-permute-start | bytes 884744 | tf_op jit(solution)/shard_map/ppermute | solution.py:78
  84.2 9.4 %collective-permute-start.31 = (bf16[4,96,384]{2,1,0:T(8,128)(2,1)S(1)}, bf16[4,96,384]{2,1,0:T(8,128)(2,1)S(1)}, u32[]{:S(2)}, u32[]{:S(2)}) collective-permute-start(bf16[4,96,384]{2,1,0:T(8,128)(2,1)S(1)} %get-tuple-element.529.rest_0_), channel_id=1, source_target_pairs={{0,4},{1,5},{2,6},{3,7},{4,0},{5,1},{6,2},{7,3},{8,12},{9,13},{10,... | collective-permute-start | bytes 884744 | tf_op jit(solution)/shard_map/ppermute | solution.py:78
  121.0 15.6 %collective-permute-start.46 = (bf16[4,96,768]{2,1,0:T(8,128)(2,1)S(1)}, bf16[4,96,768]{2,1,0:T(8,128)(2,1)S(1)}, u32[]{:S(2)}, u32[]{:S(2)}) collective-permute-start(bf16[4,96,768]{2,1,0:T(8,128)(2,1)S(1)} %get-tuple-element.600), channel_id=1, source_target_pairs={{0,8},{1,9},{2,10},{3,11},{4,12},{5,13},{6,14},{7,15},{8,0},{9,1},... | collective-permute-start | bytes 1769480 | tf_op jit(solution)/shard_map/ppermute | solution.py:78
  126.6 10.0 %collective-permute-start.44 = (bf16[2,96,768]{2,1,0:T(8,128)(2,1)S(1)}, bf16[2,96,768]{2,1,0:T(8,128)(2,1)S(1)}, u32[]{:S(2)}, u32[]{:S(2)}) collective-permute-start(bf16[2,96,768]{2,1,0:T(8,128)(2,1)S(1)} %get-tuple-element.598), channel_id=1, source_target_pairs={{0,2},{1,3},{2,0},{3,1},{4,6},{5,7},{6,4},{7,5},{8,10},{9,11},{10,... | collective-permute-start | bytes 884744 | tf_op jit(solution)/shard_map/ppermute | solution.py:78
  128.1 8.7 %collective-permute-start.45 = (bf16[2,96,768]{2,1,0:T(8,128)(2,1)S(1)}, bf16[2,96,768]{2,1,0:T(8,128)(2,1)S(1)}, u32[]{:S(2)}, u32[]{:S(2)}) collective-permute-start(bf16[2,96,768]{2,1,0:T(8,128)(2,1)S(1)} %get-tuple-element.599), channel_id=1, source_target_pairs={{0,4},{1,5},{2,6},{3,7},{4,0},{5,1},{6,2},{7,3},{8,12},{9,13},{10,... | collective-permute-start | bytes 884744 | tf_op jit(solution)/shard_map/ppermute | solution.py:78
  137.3 18.9 %collective-permute-start.47 = (bf16[4,96,768]{2,1,0:T(8,128)(2,1)S(1)}, bf16[4,96,768]{2,1,0:T(8,128)(2,1)S(1)}, u32[]{:S(2)}, u32[]{:S(2)}) collective-permute-start(bf16[4,96,768]{2,1,0:T(8,128)(2,1)S(1)} %get-tuple-element.641), channel_id=1, source_target_pairs={{0,2},{1,3},{2,0},{3,1},{4,6},{5,7},{6,4},{7,5},{8,10},{9,11},{10,... | collective-permute-start | bytes 1769480 | tf_op jit(solution)/shard_map/ppermute | solution.py:78
  138.6 17.6 %collective-permute-start.48 = (bf16[4,96,768]{2,1,0:T(8,128)(2,1)S(1)}, bf16[4,96,768]{2,1,0:T(8,128)(2,1)S(1)}, u32[]{:S(2)}, u32[]{:S(2)}) collective-permute-start(bf16[4,96,768]{2,1,0:T(8,128)(2,1)S(1)} %get-tuple-element.642), channel_id=1, source_target_pairs={{0,4},{1,5},{2,6},{3,7},{4,0},{5,1},{6,2},{7,3},{8,12},{9,13},{10,... | collective-permute-start | bytes 1769480 | tf_op jit(solution)/shard_map/ppermute | solution.py:78
  139.7 16.5 %collective-permute-start.51 = (bf16[4,96,768]{2,1,0:T(8,128)(2,1)S(1)}, bf16[4,96,768]{2,1,0:T(8,128)(2,1)S(1)}, u32[]{:S(2)}, u32[]{:S(2)}) collective-permute-start(bf16[4,96,768]{2,1,0:T(8,128)(2,1)S(1)} %get-tuple-element.645), channel_id=1, source_target_pairs={{0,8},{1,9},{2,10},{3,11},{4,12},{5,13},{6,14},{7,15},{8,0},{9,1},... | collective-permute-start | bytes 1769480 | tf_op jit(solution)/shard_map/ppermute | solution.py:78
  140.4 14.6 %collective-permute-start.49 = (bf16[96,768]{1,0:T(8,128)(2,1)S(1)}, bf16[96,768]{1,0:T(8,128)(2,1)S(1)}, u32[]{:S(2)}, u32[]{:S(2)}) collective-permute-start(bf16[96,768]{1,0:T(8,128)(2,1)S(1)} %get-tuple-element.643), channel_id=1, source_target_pairs={{0,2},{1,3},{2,0},{3,1},{4,6},{5,7},{6,4},{7,5},{8,10},{9,11},{10,... | collective-permute-start | bytes 442376 | tf_op jit(solution)/shard_map/ppermute | solution.py:78
  141.9 14.4 %collective-permute-start.50 = (bf16[96,768]{1,0:T(8,128)(2,1)S(1)}, bf16[96,768]{1,0:T(8,128)(2,1)S(1)}, u32[]{:S(2)}, u32[]{:S(2)}) collective-permute-start(bf16[96,768]{1,0:T(8,128)(2,1)S(1)} %get-tuple-element.644), channel_id=1, source_target_pairs={{0,4},{1,5},{2,6},{3,7},{4,0},{5,1},{6,2},{7,3},{8,12},{9,13},{10,... | collective-permute-start | bytes 442376 | tf_op jit(solution)/shard_map/ppermute | solution.py:78
  156.8 10.6 %collective-permute-start.52 = (bf16[2,8,96,768]{3,2,1,0:T(8,128)(2,1)S(1)}, bf16[2,8,96,768]{3,2,1,0:T(8,128)(2,1)S(1)}, u32[]{:S(2)}, u32[]{:S(2)}) collective-permute-start(bf16[2,8,96,768]{3,2,1,0:T(8,128)(2,1)S(1)} %get-tuple-element.664), channel_id=1, source_target_pairs={{0,1},{1,0},{2,3},{3,2},{4,5},{5,4},{6,7},{7,6},{8,9},{9,8},{10,11... | collective-permute-start | bytes 7077896 | tf_op jit(solution)/shard_map/ppermute | solution.py:78
  156.9 9.4 %collective-permute-start.53 = (bf16[2,96,768]{2,1,0:T(8,128)(2,1)S(1)}, bf16[2,96,768]{2,1,0:T(8,128)(2,1)S(1)}, u32[]{:S(2)}, u32[]{:S(2)}) collective-permute-start(bf16[2,96,768]{2,1,0:T(8,128)(2,1)S(1)} %get-tuple-element.665), channel_id=1, source_target_pairs={{0,2},{1,3},{2,0},{3,1},{4,6},{5,7},{6,4},{7,5},{8,10},{9,11},{10,... | collective-permute-start | bytes 884744 | tf_op jit(solution)/shard_map/ppermute | solution.py:78
  157.5 9.1 %collective-permute-start.54 = (bf16[2,96,768]{2,1,0:T(8,128)(2,1)S(1)}, bf16[2,96,768]{2,1,0:T(8,128)(2,1)S(1)}, u32[]{:S(2)}, u32[]{:S(2)}) collective-permute-start(bf16[2,96,768]{2,1,0:T(8,128)(2,1)S(1)} %get-tuple-element.666), channel_id=1, source_target_pairs={{0,4},{1,5},{2,6},{3,7},{4,0},{5,1},{6,2},{7,3},{8,12},{9,13},{10,... | collective-permute-start | bytes 884744 | tf_op jit(solution)/shard_map/ppermute | solution.py:78
  158.6 8.8 %collective-permute-start.55 = (bf16[2,96,768]{2,1,0:T(8,128)(2,1)S(1)}, bf16[2,96,768]{2,1,0:T(8,128)(2,1)S(1)}, u32[]{:S(2)}, u32[]{:S(2)}) collective-permute-start(bf16[2,96,768]{2,1,0:T(8,128)(2,1)S(1)} %get-tuple-element.667), channel_id=1, source_target_pairs={{0,8},{1,9},{2,10},{3,11},{4,12},{5,13},{6,14},{7,15},{8,0},{9,1},... | collective-permute-start | bytes 884744 | tf_op jit(solution)/shard_map/ppermute | solution.py:78
  167.7 8.0 %collective-permute-start.57 = (bf16[2,96,768]{2,1,0:T(8,128)(2,1)S(1)}, bf16[2,96,768]{2,1,0:T(8,128)(2,1)S(1)}, u32[]{:S(2)}, u32[]{:S(2)}) collective-permute-start(bf16[2,96,768]{2,1,0:T(8,128)(2,1)S(1)} %get-tuple-element.677), channel_id=1, source_target_pairs={{0,2},{1,3},{2,0},{3,1},{4,6},{5,7},{6,4},{7,5},{8,10},{9,11},{10,... | collective-permute-start | bytes 884744 | tf_op jit(solution)/shard_map/ppermute | solution.py:78
  169.3 7.6 %collective-permute-start.58 = (bf16[2,96,768]{2,1,0:T(8,128)(2,1)S(1)}, bf16[2,96,768]{2,1,0:T(8,128)(2,1)S(1)}, u32[]{:S(2)}, u32[]{:S(2)}) collective-permute-start(bf16[2,96,768]{2,1,0:T(8,128)(2,1)S(1)} %get-tuple-element.678), channel_id=1, source_target_pairs={{0,4},{1,5},{2,6},{3,7},{4,0},{5,1},{6,2},{7,3},{8,12},{9,13},{10,... | collective-permute-start | bytes 884744 | tf_op jit(solution)/shard_map/ppermute | solution.py:78
  177.3 15.4 %collective-permute-start.59 = (bf16[4,96,768]{2,1,0:T(8,128)(2,1)S(1)}, bf16[4,96,768]{2,1,0:T(8,128)(2,1)S(1)}, u32[]{:S(2)}, u32[]{:S(2)}) collective-permute-start(bf16[4,96,768]{2,1,0:T(8,128)(2,1)S(1)} %get-tuple-element.687), channel_id=1, source_target_pairs={{0,2},{1,3},{2,0},{3,1},{4,6},{5,7},{6,4},{7,5},{8,10},{9,11},{10,... | collective-permute-start | bytes 1769480 | tf_op jit(solution)/shard_map/ppermute | solution.py:78
  177.9 14.8 %collective-permute-start.60 = (bf16[4,96,768]{2,1,0:T(8,128)(2,1)S(1)}, bf16[4,96,768]{2,1,0:T(8,128)(2,1)S(1)}, u32[]{:S(2)}, u32[]{:S(2)}) collective-permute-start(bf16[4,96,768]{2,1,0:T(8,128)(2,1)S(1)} %get-tuple-element.688), channel_id=1, source_target_pairs={{0,4},{1,5},{2,6},{3,7},{4,0},{5,1},{6,2},{7,3},{8,12},{9,13},{10,... | collective-permute-start | bytes 1769480 | tf_op jit(solution)/shard_map/ppermute | solution.py:78
  178.8 12.1 %collective-permute-start.61 = (bf16[96,768]{1,0:T(8,128)(2,1)S(1)}, bf16[96,768]{1,0:T(8,128)(2,1)S(1)}, u32[]{:S(2)}, u32[]{:S(2)}) collective-permute-start(bf16[96,768]{1,0:T(8,128)(2,1)S(1)} %get-tuple-element.689), channel_id=1, source_target_pairs={{0,16},{1,17},{2,18},{3,19},{4,20},{5,21},{6,22},{7,23},{8,24},{9,... | collective-permute-start | bytes 442376 | tf_op jit(solution)/shard_map/ppermute | solution.py:78
  181.9 10.8 %collective-permute-start.62 = (bf16[96,768]{1,0:T(8,128)(2,1)S(1)}, bf16[96,768]{1,0:T(8,128)(2,1)S(1)}, u32[]{:S(2)}, u32[]{:S(2)}) collective-permute-start(bf16[96,768]{1,0:T(8,128)(2,1)S(1)} %get-tuple-element.690), channel_id=1, source_target_pairs={{0,16},{1,17},{2,18},{3,19},{4,20},{5,21},{6,22},{7,23},{8,24},{9,... | collective-permute-start | bytes 442376 | tf_op jit(solution)/shard_map/ppermute | solution.py:78
  181.9 9.0 %collective-permute-start.63 = (f32[16,768]{1,0:T(8,128)S(1)}, f32[16,768]{1,0:T(8,128)S(1)}, u32[]{:S(2)}, u32[]{:S(2)}) collective-permute-start(f32[16,768]{1,0:T(8,128)S(1)} %add_select_fusion.4), channel_id=1, source_target_pairs={{0,8},{1,9},{2,10},{3,11},{4,12},{5,13},{6,14},{7,15},{8,0},{9,1},... | collective-permute-start | bytes 147464 | tf_op jit(solution)/shard_map/ppermute | solution.py:78
  193.0 8.8 %collective-permute-start.64 = (bf16[2,96,768]{2,1,0:T(8,128)(2,1)S(1)}, bf16[2,96,768]{2,1,0:T(8,128)(2,1)S(1)}, u32[]{:S(2)}, u32[]{:S(2)}) collective-permute-start(bf16[2,96,768]{2,1,0:T(8,128)(2,1)S(1)} %get-tuple-element.697), channel_id=1, source_target_pairs={{0,8},{1,9},{2,10},{3,11},{4,12},{5,13},{6,14},{7,15},{8,0},{9,1},... | collective-permute-start | bytes 884744 | tf_op jit(solution)/shard_map/ppermute | solution.py:78
  193.4 7.1 %collective-permute-start.65 = (f32[16,768]{1,0:T(8,128)S(1)}, f32[16,768]{1,0:T(8,128)S(1)}, u32[]{:S(2)}, u32[]{:S(2)}) collective-permute-start(f32[16,768]{1,0:T(8,128)S(1)} %add_select_fusion.3), channel_id=1, source_target_pairs={{0,16},{1,17},{2,18},{3,19},{4,20},{5,21},{6,22},{7,23},{8,24},{9,... | collective-permute-start | bytes 147464 | tf_op jit(solution)/shard_map/ppermute | solution.py:78
  203.6 9.2 %collective-permute-start.66 = (bf16[96,768]{1,0:T(8,128)(2,1)S(1)}, bf16[96,768]{1,0:T(8,128)(2,1)S(1)}, u32[]{:S(2)}, u32[]{:S(2)}) collective-permute-start(bf16[96,768]{1,0:T(8,128)(2,1)S(1)} %get-tuple-element.703), channel_id=1, source_target_pairs={{0,16},{1,17},{2,18},{3,19},{4,20},{5,21},{6,22},{7,23},{8,24},{9,... | collective-permute-start | bytes 442376 | tf_op jit(solution)/shard_map/ppermute | solution.py:78
  (36 other events, 274.2 us)
